TPU v7x, 32 devices: a whole 2x2x4 slice. The times are simulated.
32 devices in a mesh: groups: 2 (over y), fsdp: 8 (over z, x), seq: 2 (over core).
Axes of the slice: x: 2, y: 2, z: 4, core: 2. Of those that a mesh axis runs over, the one named last changes fastest.
Arguments:
- tokens: bfloat16 [2048, 8192], P(('groups', 'fsdp', 'seq')), parts along dimension 0, may hold values from -6 to 6
- gate_blocks: bfloat16 [1280, 4096], P('fsdp'), may hold values from -0.09375 to 0.09375
- gate_slot: int32 [1280], P('fsdp'), may hold values from 0 to 256, as said below
- up_blocks: bfloat16 [1280, 4096], P('fsdp'), may hold values from -0.09375 to 0.09375
- up_slot: int32 [1280], P('fsdp'), may hold values from 0 to 256, as said below
- down_blocks: bfloat16 [1280, 4096], P('fsdp'), may hold values from -0.25 to 0.25
- down_slot: int32 [1280], P('fsdp'), may hold values from 0 to 256, as said below
- sketch: bfloat16 [32, 8192], P(None, 'fsdp'), may hold values from -0.0625 to 0.0625
- probe_index: int32 [16, 256], replicated, may hold values from 0 to 8191
- probe_value: float32 [16, 256], replicated, may hold values from -32 to 32
Outputs:
- products: float32 [32, 8192], P('groups', 'fsdp'), parts along dimension 0
There are 2 independent parts, one for each index of `groups`. A program takes and returns all parts, laid end to end along the dimension named above; an argument that names none is the same for every part. Nothing has to cross between parts.
Inputs may be any that keep to these rules, and one draw needn't show every extreme that they name: `gate_slot`: slots j * 160 to (j + 1) * 160 - 1 belong to fsdp owner j; they hold distinct block numbers below 256, filled slots first, then the value 256 for empty slots. Every owner fills 3 * 32 slots or more, and in every draw some owner fills all 160. `up_slot`: as for gate_slot, drawn independently. `down_slot`: as for gate_slot, drawn independently.
All inputs are finite; a program needn't handle non-finite values.
Results may differ from a plain program's by a relative error of at most 0.0038.
Values may be sent and summed in bfloat16 or wider, within the bound.
No kernel may reach another device: no remote copies, remote signals or barrier semaphores. Data moves between devices by JAX's collectives and lax.ppermute only.
A program may use at most 128 MiB of HBM per device.

v0:
```python
import jax
import jax.numpy as jnp
from jax import lax
from jax.sharding import PartitionSpec as P

HID_DEV = 128
BLK = 64
P_SIZE = 16
K = 32


def unpack(blocks, slot_ids, cell_total):
    holder = jnp.zeros((cell_total + 1, blocks.shape[1]), blocks.dtype)
    return holder.at[slot_ids].set(blocks)[:cell_total]


def contract_last(first_mat, second_mat):
    return lax.dot_general(
        first_mat, second_mat, (((1,), (1,)), ((), ())), preferred_element_type=jnp.float32
    )


def per_device(
    tokens,
    gate_blocks,
    gate_slot,
    up_blocks,
    up_slot,
    down_blocks,
    down_slot,
    sketch,
    probe_index,
    probe_value,
):
    owners = lax.axis_size("fsdp")
    model_width = tokens.shape[1]
    local_width = model_width // owners
    block_rows = local_width // BLK
    hidden = HID_DEV
    col_blocks = hidden * owners // BLK
    cell_total = block_rows * col_blocks
    gate_dense = unpack(gate_blocks, gate_slot, cell_total).reshape(
        block_rows, col_blocks, BLK, BLK
    )
    up_dense = unpack(up_blocks, up_slot, cell_total).reshape(block_rows, col_blocks, BLK, BLK)
    stacked = jnp.stack([gate_dense, up_dense], axis=1)
    stacked = stacked.reshape(block_rows, 2, owners, hidden // BLK, BLK, BLK)
    stacked = stacked.transpose(0, 4, 2, 1, 3, 5).reshape(local_width, owners * 2 * hidden)
    both_weights = lax.all_to_all(stacked, "fsdp", split_axis=1, concat_axis=0, tiled=True)
    picked = both_weights[probe_index].astype(jnp.float32)
    probe_both = jnp.sum(picked * probe_value[:, :, None], axis=1)
    preact = jnp.dot(
        lax.all_gather(tokens, "fsdp", axis=0, tiled=True),
        both_weights,
        preferred_element_type=jnp.float32,
    )
    row_count = preact.shape[0]
    gate_pre = preact[:, :hidden]
    up_pre = preact[:, hidden:]
    down_dense = unpack(down_blocks, down_slot, cell_total).reshape(
        col_blocks, block_rows, BLK, BLK
    )
    down_dense = down_dense.transpose(0, 2, 1, 3).reshape(col_blocks * BLK, local_width)
    down_rows = lax.all_to_all(down_dense, "fsdp", split_axis=0, concat_axis=1, tiled=True)
    full_sketch = lax.all_gather(sketch, "fsdp", axis=1, tiled=True)
    projected = contract_last(down_rows, full_sketch)
    projected = projected.astype(jnp.bfloat16)
    sigmoid_g = jax.nn.sigmoid(gate_pre)
    activated = gate_pre * sigmoid_g
    slope_g = sigmoid_g * (1.0 + gate_pre * (1.0 - sigmoid_g))
    lead_term = slope_g * up_pre
    tangent = (
        lead_term[:, None, :] * probe_both[None, :, :hidden]
        + activated[:, None, :] * probe_both[None, :, hidden:]
    )
    tangent = tangent.astype(jnp.bfloat16)
    partial_sketch = jnp.dot(
        tangent.reshape(row_count * P_SIZE, hidden), projected, preferred_element_type=jnp.float32
    )
    partial_sketch = partial_sketch.reshape(row_count, P_SIZE * K)
    sketch_rows = lax.psum(partial_sketch, "fsdp").astype(jnp.bfloat16)
    backward = contract_last(sketch_rows.reshape(row_count * P_SIZE, K), projected).reshape(
        row_count, P_SIZE, hidden
    )
    summed = jnp.concatenate(
        [
            jnp.sum(backward * lead_term[:, None, :], axis=0),
            jnp.sum(backward * activated[:, None, :], axis=0),
        ],
        axis=1,
    )
    summed = lax.psum(summed, "seq").astype(jnp.bfloat16)
    products = contract_last(summed, both_weights)
    return lax.psum_scatter(products, "fsdp", scatter_dimension=1, tiled=True)


def solution(mesh):
    in_specs = (
        P(("groups", "fsdp", "seq"), None),
        P("fsdp", None),
        P("fsdp"),
        P("fsdp", None),
        P("fsdp"),
        P("fsdp", None),
        P("fsdp"),
        P(None, "fsdp"),
        P(),
        P(),
    )
    out_specs = P("groups", "fsdp")
    return jax.shard_map(
        per_device, mesh=mesh, in_specs=in_specs, out_specs=out_specs, check_vma=False
    )
```

profile of v0, /device:TPU:0, one launch (start us, length us, event | category | flops | bytes accessed | tf_op | source)
XLA Modules:
  0.0 471.8 jit_solution(3671803869858965092)
XLA Ops:
  6.5 0.7 all-gather.2.cloned.1.call-update
  7.9 3.9 scatter_custom_fusion.2
  11.8 1.5 slice.36
  13.3 6.9 %reshape.39 = bf16[16,16,64,64]{3,2,1,0:T(8,128)(2,1)} reshape(bf16[256,4096]{1,0:T(8,128)(2,1)} %slice.36) | data formatting | bytes 4194304 | tf_op jit(solution)/shard_map/reshape | solution.py:60
  20.2 8.0 %copy.32 = bf16[16,16,64,64]{3,1,2,0:T(8,128)(2,1)} copy(bf16[16,16,64,64]{3,2,1,0:T(8,128)(2,1)} %reshape.39) | data formatting | bytes 4194304 | tf_op jit(solution)/shard_map/reshape | solution.py:60
  28.2 6.5 %all_to_all.32 = bf16[8,128,1024]{2,1,0:T(8,128)(2,1)} reshape(bf16[16,64,16,64]{3,2,1,0:T(8,128)(2,1)} %bitcast.42) | data formatting | bytes 4194304 | tf_op jit(solution)/shard_map/all_to_all | solution.py:64
  34.8 7.3 %all-to-all-start.1 = ((bf16[8,128,1024]{2,1,0:T(8,128)(2,1)}), bf16[8,128,1024]{2,1,0:T(8,128)(2,1)}, u32[]{:S(2)}, u32[]{:S(2)}) async-start(bf16[8,128,1024]{2,1,0:T(8,128)(2,1)} %all_to_all.32), calls=%async_computation.1 | async-start | bytes 4194304 | tf_op jit(solution)/shard_map/all_to_all | solution.py:64
  42.0 4.0 scatter_custom_fusion
  46.1 1.5 slice.30
  47.6 6.9 %stack.7 = bf16[16,1,8,2,64,64]{5,4,3,2,0,1:T(8,128)(2,1)} reshape(bf16[256,4096]{1,0:T(8,128)(2,1)} %slice.30) | data formatting | bytes 4194304 | tf_op jit(solution)/shard_map/stack | solution.py:46
  54.5 3.9 scatter_custom_fusion.1
  58.3 1.5 slice.31
  59.9 6.9 %stack.8 = bf16[16,1,8,2,64,64]{5,4,3,2,0,1:T(8,128)(2,1)} reshape(bf16[256,4096]{1,0:T(8,128)(2,1)} %slice.31) | data formatting | bytes 4194304 | tf_op jit(solution)/shard_map/stack | solution.py:46
  66.7 8.6 %maximum_bitcast_fusion = bf16[16,64,8,2,2,64]{5,1,4,2,0,3:T(8,128)(2,1)} fusion(bf16[16,1,8,2,64,64]{5,4,3,2,0,1:T(8,128)(2,1)} %stack.8, bf16[16,1,8,2,64,64]{5,4,3,2,0,1:T(8,128)(2,1)} %stack.7), kind=kLoop, calls=%fused_computation.4 | loop fusion | flops 2097152 | bytes 8388608 | tf_op jit(solution)/shard_map/transpose | solution.py:48
  75.3 13.1 %copy.20 = bf16[16,64,8,2,2,64]{1,0,5,4,3,2:T(8,128)(2,1)} copy(bf16[16,64,8,2,2,64]{5,1,4,2,0,3:T(8,128)(2,1)} %maximum_bitcast_fusion) | data formatting | bytes 8388608 | tf_op jit(solution)/shard_map/transpose | solution.py:48
  88.4 12.0 %all_to_all.28 = bf16[1024,8,256]{0,2,1:T(8,128)(2,1)} reshape(bf16[16,64,8,2,2,64]{1,0,5,4,3,2:T(8,128)(2,1)} %copy.20) | data formatting | bytes 8388608 | tf_op jit(solution)/shard_map/all_to_all | solution.py:49
  100.4 34.2 %all-to-all-done.1 = bf16[8,128,1024]{2,1,0:T(8,128)(2,1)} async-done(((bf16[8,128,1024]{2,1,0:T(8,128)(2,1)}), bf16[8,128,1024]{2,1,0:T(8,128)(2,1)}, u32[]{:S(2)}, u32[]{:S(2)}) %all-to-all-start.1) | async-done | bytes 2097184 | tf_op jit(solution)/shard_map/all_to_all | solution.py:64
  134.5 5.9 %all-to-all-start = ((bf16[1024,8,256]{0,2,1:T(8,128)(2,1)}), bf16[1024,8,256]{0,2,1:T(8,128)(2,1)}, u32[]{:S(2)}, u32[]{:S(2)}) async-start(bf16[1024,8,256]{0,2,1:T(8,128)(2,1)} %all_to_all.28), calls=%async_computation | async-start | bytes 8388608 | tf_op jit(solution)/shard_map/all_to_all | solution.py:49
  140.5 141.7 %all_gather.7 = bf16[32,8192]{1,0:T(8,128)(2,1)S(1)} all-gather(bf16[32,1024]{1,0:T(8,128)(2,1)S(1)} %copy-done), channel_id=1, replica_groups=mesh['groups'=2,'fsdp'=8,'seq'=2] {'fsdp'}, dimensions={1}, use_global_device_ids=true | all-gather | bytes 589824 | tf_op jit(solution)/shard_map/all_gather | solution.py:65
  282.2 3.0 copy.26
  285.7 6.5 %copy.21 = bf16[8,1024,256]{2,1,0:T(8,128)(2,1)} copy(bf16[8,1024,256]{1,2,0:T(8,128)(2,1)} %bitcast.1) | data formatting | bytes 8388608 | tf_op jit(solution)/shard_map/all_to_all | solution.py:49
  292.2 15.7 %gather_fusion = bf16[4096,256]{1,0:T(8,128)(2,1)S(1)} fusion(bf16[8192,256]{1,0:T(8,128)(2,1)} %bitcast.39, s32[4096]{0:T(1024)S(1)} %broadcast_clamp_fusion), kind=kCustom, calls=%fused_computation | custom fusion | bytes 4210688 | tf_op jit(solution)/shard_map/gather | solution.py:50
  308.0 0.7 fusion
  308.7 7.0 %convolution_bitcast_fusion = f32[512,256]{0,1:T(8,128)S(1)} fusion(bf16[8192,256]{1,0:T(8,128)(2,1)} %bitcast.40, bf16[512,8192]{1,0:T(8,128)(2,1)} %all-gather.2.cloned.1.call-done), kind=kOutput, calls=%fused_computation.11 | convolution fusion | flops 2147483648 | bytes 13107200 | tf_op jit(solution)/shard_map/dot_general | solution.py:52
  316.7 1.4 copy.24
  318.1 2.6 fusion.14
  320.7 3.5 reshape.40
  324.2 70.7 %all-reduce.1 = bf16[512,512]{1,0:T(8,128)(2,1)S(1)} all-reduce(f32[512,512]{1,0:T(8,128)S(1)} %reshape.40), channel_id=1, replica_groups=mesh['groups'=2,'fsdp'=8,'seq'=2] {'fsdp'}, use_global_device_ids=true, to_apply=%region_4.0 | all-reduce | flops 262144 | bytes 1572864 | tf_op jit(solution)/shard_map/psum | solution.py:81
  395.2 1.0 multiply_reduce_fusion.1
  396.2 3.4 psum.15
  399.6 4.2 fusion.15
  403.8 61.1 %reduce-scatter.2.cloned.1.call-done = f32[16,1024]{1,0:T(8,128)} async-done(((f32[16,8192]{1,0:T(8,128)}), f32[16,1024]{1,0:T(8,128)}) %reduce-scatter.2.cloned.1.call-update) | async-done | bytes 65552 | tf_op jit(solution)/shard_map/reduce_scatter | solution.py:94
  (29 shorter events, 2.4 us)
Async XLA Ops:
  6.5 302.2 %all-gather.2.cloned.1.call-start = ((), (), s32[]{:S(2)}) async-start(), calls=%async_computation.3 | async-start | bytes 9437184 | tf_op jit(solution)/shard_map/all_gather | solution.py:53
  34.8 7.3 %copy-start.3 = (s32[160]{0:T(256)S(1)}, s32[160]{0:T(256)}, u32[]{:S(2)}) copy-start(s32[160]{0:T(256)} %param.12) | copy-start | bytes 1924
  34.8 99.8 %all-to-all-start.1 = ((bf16[8,128,1024]{2,1,0:T(8,128)(2,1)}), bf16[8,128,1024]{2,1,0:T(8,128)(2,1)}, u32[]{:S(2)}, u32[]{:S(2)}) async-start(bf16[8,128,1024]{2,1,0:T(8,128)(2,1)} %all_to_all.32), calls=%async_computation.1 | async-start | bytes 4194304 | tf_op jit(solution)/shard_map/all_to_all | solution.py:64
  47.6 6.9 %copy-start.4 = (s32[160]{0:T(256)S(1)}, s32[160]{0:T(256)}, u32[]{:S(2)}) copy-start(s32[160]{0:T(256)} %param.14) | copy-start | bytes 1924
  100.4 40.1 %copy-start.2 = (s32[16,256]{1,0:T(8,128)S(1)}, s32[16,256]{1,0:T(8,128)}, u32[]{:S(2)}) copy-start(s32[16,256]{1,0:T(8,128)} %param.18) | copy-start | bytes 49156
  100.4 40.2 %copy-start = (bf16[32,1024]{1,0:T(8,128)(2,1)S(1)}, bf16[32,1024]{1,0:T(8,128)(2,1)}, u32[]{:S(2)}) copy-start(bf16[32,1024]{1,0:T(8,128)(2,1)} %param.17) | copy-start | bytes 196612
  134.5 151.2 %all-to-all-start = ((bf16[1024,8,256]{0,2,1:T(8,128)(2,1)}), bf16[1024,8,256]{0,2,1:T(8,128)(2,1)}, u32[]{:S(2)}, u32[]{:S(2)}) async-start(bf16[1024,8,256]{0,2,1:T(8,128)(2,1)} %all_to_all.28), calls=%async_computation | async-start | bytes 8388608 | tf_op jit(solution)/shard_map/all_to_all | solution.py:49
  140.4 324.5 %reduce-scatter.2.cloned.1.call-start = ((), (), s32[]{:S(2)}) async-start(), calls=%async_computation.4 | async-start | bytes 589824 | tf_op jit(solution)/shard_map/reduce_scatter | solution.py:94
  292.2 15.7 %copy-start.1 = (f32[16,256]{1,0:T(8,128)S(1)}, f32[16,256]{1,0:T(8,128)}, u32[]{:S(2)}) copy-start(f32[16,256]{1,0:T(8,128)} %param.19) | copy-start | bytes 49156
Sparse Core Ops, SparseCore 0:
  9.5 226.6 all-gather.1
  403.9 60.9 reduce-scatter.1
where the time goes:
time: 474 us; the launch traced here: 472 us
  blocking collectives  216 us (46%)
  local copies, waits for them, and re-layouts  107 us (23%)
  waiting for transfers between devices  96 us (20%)
  matrix products  15.2 us (3%)
  between operations  13.6 us (3%)
  starting transfers between devices  13.2 us (3%)
  other arithmetic  10.7 us (2%)
    all_gather x1, blocking collectives, per_device(): full_sketch = lax.all_gather(sketch, 'fsdp', axis=1, tiled=True)  142 us
    psum x1, blocking collectives, per_device(): sketch_rows = lax.psum(partial_sketch, 'fsdp').astype(jnp.bfloat16)  70.7 us
    reduce_scatter x1, waiting for transfers between devices, per_device(): return lax.psum_scatter(products, 'fsdp', scatter_dimension=1, tiled=True)  61.1 us
    all_to_all x1, waiting for transfers between devices, per_device(): lax.all_to_all(down_dense, 'fsdp', split_axis=0, concat_axis=1, tiled=True)  34.2 us
    all_to_all x2, local copies, waits for them, and re-layouts, per_device(): lax.all_to_all(stacked, 'fsdp', split_axis=1, concat_axis=0, tiled=True)  18.5 us
    gather x1, local copies, waits for them, and re-layouts, per_device(): picked = both_weights[probe_index].astype(jnp.float32)  15.7 us
    reshape x2, local copies, waits for them, and re-layouts, per_device(): unpack(down_blocks, down_slot, cell_total)  14.9 us
    another operation x2, local copies, waits for them, and re-layouts, per_device(): stacked = jnp.stack([gate_dense, up_dense], axis=1)  13.8 us
  transfers between devices with their start and end apart: 4, of which 2 were waited for; matrix products, arithmetic and copies ran while one was open for 20% of the time, Pallas kernels for 0%

commit v1 on v0

--- a/solution.py
+++ b/solution.py
@@ -1,6 +1,10 @@
+import functools
+
 import jax
 import jax.numpy as jnp
 from jax import lax
+from jax.experimental import pallas as pl
+from jax.experimental.pallas import tpu as pltpu
 from jax.sharding import PartitionSpec as P
 
 HID_DEV = 128
@@ -8,6 +12,12 @@
 P_SIZE = 16
 K = 32
 
+BF = jnp.bfloat16
+F32 = jnp.float32
+VMEM = pl.BlockSpec(memory_space=pltpu.VMEM)
+SMEM = pl.BlockSpec(memory_space=pltpu.SMEM)
+PARAMS = pltpu.CompilerParams(vmem_limit_bytes=56 * 1024 * 1024)
+
 
 def unpack(blocks, slot_ids, cell_total):
     holder = jnp.zeros((cell_total + 1, blocks.shape[1]), blocks.dtype)
@@ -20,7 +30,7 @@
     )
 
 
-def per_device(
+def hidden_split(
     tokens,
     gate_blocks,
     gate_slot,
@@ -94,6 +104,394 @@
     return lax.psum_scatter(products, "fsdp", scatter_dimension=1, tiled=True)
 
 
+def dot(a, b):
+    return jnp.dot(a, b, preferred_element_type=F32)
+
+
+def split3(value):
+    high = value.astype(BF)
+    rest = value - high.astype(F32)
+    mid = rest.astype(BF)
+    low = (rest - mid.astype(F32)).astype(BF)
+    return high, mid, low
+
+
+def shuffled(natural):
+    return (natural // BLK) * BLK + (natural % 2) * (BLK // 2) + (natural % BLK) // 2
+
+
+def shuffle_matrix(size):
+    rows = lax.broadcasted_iota(jnp.int32, (size, size), 0)
+    cols = lax.broadcasted_iota(jnp.int32, (size, size), 1)
+    return jnp.where(shuffled(rows) == cols, 1.0, 0.0).astype(BF)
+
+
+def unshuffle_matrix(size):
+    rows = lax.broadcasted_iota(jnp.int32, (size, size), 0)
+    cols = lax.broadcasted_iota(jnp.int32, (size, size), 1)
+    return jnp.where(shuffled(cols) == rows, 1.0, 0.0).astype(BF)
+
+
+def stage_blocks(blocks_ref, tiles_ref, first_slot):
+    @pl.loop(0, blocks_ref.shape[0] // 16)
+    def _(step):
+        row = pl.multiple_of(step * 16, 16)
+        target = (first_slot + row) * 32
+        for chunk in range(32):
+            piece = blocks_ref[pl.ds(row, 16), 128 * chunk : 128 * (chunk + 1)].astype(F32)
+            tiles_ref[pl.ds(target + chunk, 16, stride=32), :] = piece
+
+
+def assembled_pair(tiles_ref, left_slot, right_slot):
+    left = tiles_ref[pl.ds(pl.multiple_of(left_slot * 32, 32), 32), :]
+    right = tiles_ref[pl.ds(pl.multiple_of(right_slot * 32, 32), 32), :]
+    low_half = lax.broadcasted_iota(jnp.int32, (32, 128), 1) < BLK
+    even = jnp.where(low_half, left, pltpu.roll(right, BLK, 1))
+    odd = jnp.where(low_half, pltpu.roll(left, BLK, 1), right)
+    return even.astype(BF), odd.astype(BF)
+
+
+def assemble_columns(inv_ref, inv_row, tiles_ref, put):
+    @pl.loop(0, 16)
+    def _(block_row):
+        for pair in range(8):
+            cell = block_row * 16 + 2 * pair
+            even, odd = assembled_pair(
+                tiles_ref, inv_ref[inv_row, cell], inv_ref[inv_row, cell + 1]
+            )
+            row = pl.multiple_of(block_row * BLK, BLK)
+            put(pair, row, even)
+            put(pair, row + BLK // 2, odd)
+
+
+def own_kernel(
+    place_ref,
+    inv_ref,
+    gate_ref,
+    up_ref,
+    down_ref,
+    sketch_ref,
+    index_ref,
+    value_ref,
+    weight_ref,
+    payload_ref,
+    tiles_ref,
+    omega_ref,
+    split_ref,
+    down_dense_ref,
+):
+    owner = place_ref[0]
+    quarter = place_ref[1]
+    tiles_ref[pl.ds(160 * 32, 32), :] = jnp.zeros((32, 128), F32)
+
+    for which, blocks_ref in enumerate((gate_ref, up_ref)):
+        stage_blocks(blocks_ref, tiles_ref, 0)
+
+        def put(pair, row, piece):
+            lane = (pair % 2) * 128
+            weight_ref[4 * which + pair // 2, pl.ds(row, 32), lane : lane + 128] = piece
+
+        assemble_columns(inv_ref, which, tiles_ref, put)
+
+    stage_blocks(down_ref, tiles_ref, 0)
+    for local_row in range(4):
+        for pair in range(8):
+            cell = (quarter * 4 + local_row) * 16 + 2 * pair
+            even, odd = assembled_pair(tiles_ref, inv_ref[2, cell], inv_ref[2, cell + 1])
+            row = local_row * BLK
+            down_dense_ref[row : row + 32, 128 * pair : 128 * (pair + 1)] = even
+            down_dense_ref[row + 32 : row + 64, 128 * pair : 128 * (pair + 1)] = odd
+    payload_ref[32:64, :] = contract_last(sketch_ref[...], down_dense_ref[...])
+
+    local = index_ref[...] - owner * 1024
+    inside = (local >= 0) & (local < 1024)
+    safe = jnp.where(inside, local, 0)
+    spot = shuffled(safe)
+    high_part = jnp.where(inside, spot // 128, -1)
+    low_part = spot % 128
+    values = value_ref[...]
+    high_iota = lax.broadcasted_iota(jnp.int32, (8, 256), 0)
+    low_iota = lax.broadcasted_iota(jnp.int32, (128, 256), 0)
+    for probe in range(P_SIZE):
+        picked = jnp.where(
+            high_iota == high_part[probe : probe + 1, :], values[probe : probe + 1, :], 0.0
+        )
+        one_hot = jnp.where(low_iota == low_part[probe : probe + 1, :], 1.0, 0.0).astype(BF)
+        total = None
+        for part in split3(picked):
+            term = contract_last(part, one_hot)
+            total = term if total is None else total + term
+        omega_ref[8 * probe : 8 * (probe + 1), :] = total
+    for high in range(8):
+        piece = omega_ref[pl.ds(high, 16, stride=8), :]
+        for part_index, part in enumerate(split3(piece)):
+            split_ref[
+                16 * part_index : 16 * (part_index + 1), 128 * high : 128 * (high + 1)
+            ] = part
+    for which in range(2):
+        triple = dot(split_ref[...], weight_ref[4 * which + quarter])
+        payload_ref[16 * which : 16 * (which + 1), :] = triple[:16] + triple[16:32] + triple[32:]
+
+
+def partial_kernel(
+    inv_row,
+    place_ref,
+    inv_ref,
+    first_ref,
+    second_ref,
+    own_weight_ref,
+    tok0_ref,
+    tok1_ref,
+    tok2_ref,
+    tok3_ref,
+    keep_ref,
+    out1_ref,
+    out2_ref,
+    out3_ref,
+    tiles_ref,
+    weight_ref,
+    tokens_ref,
+):
+    side = place_ref[2]
+    core = place_ref[3]
+    tiles_ref[pl.ds(160 * 32, 32), :] = jnp.zeros((32, 128), F32)
+    stage_blocks(first_ref, tiles_ref, core * 80)
+    stage_blocks(second_ref, tiles_ref, (1 - core) * 80)
+
+    def put(pair, row, piece):
+        lane = (pair % 2) * 128
+        weight_ref[pair // 2, pl.ds(row, 32), lane : lane + 128] = piece
+
+    assemble_columns(inv_ref, inv_row, tiles_ref, put)
+    shuffle = shuffle_matrix(256)
+    for source, tok_ref in enumerate((tok0_ref, tok1_ref, tok2_ref, tok3_ref)):
+        for group in range(8):
+            moved = dot(tok_ref[:, 256 * group : 256 * (group + 1)], shuffle).astype(BF)
+            half = lax.rem(group // 4 + side, 2)
+            tokens_ref[
+                half, 64 * source : 64 * (source + 1), 256 * (group % 4) : 256 * (group % 4 + 1)
+            ] = moved
+    for chunk in range(4):
+        total = dot(tokens_ref[0], own_weight_ref[chunk]) + dot(tokens_ref[1], weight_ref[chunk])
+        cols = slice(256 * chunk, 256 * (chunk + 1))
+        keep_ref[:, cols] = total[:64]
+        out1_ref[:, cols] = total[64:128].astype(BF)
+        out2_ref[:, cols] = total[128:192].astype(BF)
+        out3_ref[:, cols] = total[192:].astype(BF)
+
+
+def middle_kernel(
+    place_ref,
+    gate0_ref,
+    gate1_ref,
+    gate2_ref,
+    gate3_ref,
+    up0_ref,
+    up1_ref,
+    up2_ref,
+    up3_ref,
+    pay0_ref,
+    pay1_ref,
+    pay2_ref,
+    pay3_ref,
+    out_ref,
+    lead_ref,
+    act_ref,
+    pay_ref,
+    proj_ref,
+    tangent_ref,
+):
+    quarter = place_ref[1]
+    low_bit = quarter % 2
+    high_bit = quarter // 2
+    unshuffle = unshuffle_matrix(256)
+    for flip, ref in enumerate((pay0_ref, pay1_ref, pay2_ref, pay3_ref)):
+        spot = lax.rem(low_bit + flip % 2, 2) + 2 * lax.rem(high_bit + flip // 2, 2)
+        pay_ref[spot] = ref[...]
+    for chunk in range(4):
+        cols = slice(256 * chunk, 256 * (chunk + 1))
+        proj_ref[:, cols] = dot(pay_ref[chunk, 32:64, :].astype(BF), unshuffle).astype(BF)
+        gate_pre = (
+            gate0_ref[:, cols]
+            + gate1_ref[:, cols].astype(F32)
+            + gate2_ref[:, cols].astype(F32)
+            + gate3_ref[:, cols].astype(F32)
+        )
+        up_pre = (
+            up0_ref[:, cols]
+            + up1_ref[:, cols].astype(F32)
+            + up2_ref[:, cols].astype(F32)
+            + up3_ref[:, cols].astype(F32)
+        )
+        sigmoid_g = jax.nn.sigmoid(gate_pre)
+        activated = gate_pre * sigmoid_g
+        slope_g = sigmoid_g * (1.0 + gate_pre * (1.0 - sigmoid_g))
+        lead = slope_g * up_pre
+        lead_ref[:, cols] = lead
+        act_ref[:, cols] = activated
+        for probe in range(P_SIZE):
+            probe_gate = pay_ref[chunk, probe : probe + 1, :]
+            probe_up = pay_ref[chunk, 16 + probe : 17 + probe, :]
+            tangent_ref[64 * probe : 64 * (probe + 1), cols] = (
+                lead * probe_gate + activated * probe_up
+            ).astype(BF)
+    sketch_rows = contract_last(tangent_ref[...], proj_ref[...]).astype(BF)
+    for probe in range(P_SIZE):
+        rows = sketch_rows[64 * probe : 64 * (probe + 1), :]
+        backward = dot(rows, proj_ref[...])
+        out_ref[probe : probe + 1, :1024] = jnp.sum(backward * lead_ref[...], axis=0, keepdims=True)
+        out_ref[probe : probe + 1, 1024:] = jnp.sum(backward * act_ref[...], axis=0, keepdims=True)
+
+
+def product_kernel(sum_ref, weight_ref, out_ref):
+    sums = sum_ref[...].astype(BF)
+    total = None
+    for chunk in range(8):
+        term = contract_last(sums[:, 256 * chunk : 256 * (chunk + 1)], weight_ref[chunk])
+        total = term if total is None else total + term
+    unshuffle = unshuffle_matrix(256)
+    for group in range(4):
+        cols = slice(256 * group, 256 * (group + 1))
+        high, mid, low = split3(total[:, cols])
+        out_ref[:, cols] = dot(high, unshuffle) + dot(mid, unshuffle) + dot(low, unshuffle)
+
+
+def pair_split(
+    tokens,
+    gate_blocks,
+    gate_slot,
+    up_blocks,
+    up_slot,
+    down_blocks,
+    down_slot,
+    sketch,
+    probe_index,
+    probe_value,
+):
+    owner = lax.axis_index("fsdp")
+    core = lax.axis_index("seq")
+    group = lax.axis_index("groups")
+    zone = owner // 2
+    side = owner % 2
+    place = jnp.stack([owner, 2 * group + core, side, core]).astype(jnp.int32)
+
+    def owner_flip(value, bits):
+        return lax.ppermute(value, "fsdp", [(i, i ^ bits) for i in range(8)])
+
+    def core_flip(value):
+        return lax.ppermute(value, "seq", [(0, 1), (1, 0)])
+
+    def token_slice(target_zone):
+        return lax.dynamic_slice(tokens, (0, target_zone * 2048), (64, 2048))
+
+    slots = jnp.stack([gate_slot, up_slot, down_slot])
+    cells = lax.broadcasted_iota(jnp.int32, (3, 160, 256), 2)
+    slot_numbers = lax.broadcasted_iota(jnp.int32, (3, 160, 256), 1)
+    inv = jnp.min(jnp.where(slots[:, :, None] == cells, slot_numbers, 160), axis=1)
+
+    tok_parts = [token_slice(zone)]
+    for flip in (1, 2, 3):
+        tok_parts.append(owner_flip(token_slice(zone ^ flip), 2 * flip))
+
+    near_inv = owner_flip(inv, 1)
+    near_gate = owner_flip(lax.dynamic_slice(gate_blocks, (core * 80, 0), (80, 4096)), 1)
+    near_up = owner_flip(lax.dynamic_slice(up_blocks, (core * 80, 0), (80, 4096)), 1)
+
+    weights, payload = pl.pallas_call(
+        own_kernel,
+        out_shape=(
+            jax.ShapeDtypeStruct((8, 1024, 256), BF),
+            jax.ShapeDtypeStruct((64, 256), F32),
+        ),
+        in_specs=[SMEM, SMEM] + [VMEM] * 6,
+        out_specs=(VMEM, VMEM),
+        scratch_shapes=[
+            pltpu.VMEM((161 * 32, 128), F32),
+            pltpu.VMEM((128, 128), F32),
+            pltpu.VMEM((48, 1024), BF),
+            pltpu.VMEM((256, 1024), BF),
+        ],
+        compiler_params=PARAMS,
+        name="own_blocks",
+    )(place, inv, gate_blocks, up_blocks, down_blocks, sketch, probe_index, probe_value)
+
+    for bits in (1, 2, 4):
+        payload = payload + owner_flip(payload, bits)
+    pay_parts = [
+        payload,
+        core_flip(payload),
+        lax.ppermute(payload, "groups", [(0, 1), (1, 0)]),
+        lax.ppermute(payload, ("groups", "seq"), [(i, i ^ 3) for i in range(4)]),
+    ]
+
+    def partial_sums(which, near):
+        return pl.pallas_call(
+            functools.partial(partial_kernel, which),
+            out_shape=(jax.ShapeDtypeStruct((64, 1024), F32),)
+            + (jax.ShapeDtypeStruct((64, 1024), BF),) * 3,
+            grid=(1,),
+            in_specs=[SMEM, SMEM, VMEM, VMEM]
+            + [pl.BlockSpec((4, 1024, 256), lambda i: (which, 0, 0))]
+            + [VMEM] * 4,
+            out_specs=(VMEM,) * 4,
+            scratch_shapes=[
+                pltpu.VMEM((161 * 32, 128), F32),
+                pltpu.VMEM((4, 1024, 256), BF),
+                pltpu.VMEM((2, 256, 1024), BF),
+            ],
+            compiler_params=PARAMS,
+            name="partial_sums",
+        )(place, near_inv, near, core_flip(near), weights, *tok_parts)
+
+    middle_args = []
+    for which, near in enumerate((near_gate, near_up)):
+        keep, *sent = partial_sums(which, near)
+        middle_args.append(keep)
+        for flip in (1, 2, 3):
+            middle_args.append(owner_flip(sent[flip - 1], 2 * flip))
+
+    sums = pl.pallas_call(
+        middle_kernel,
+        out_shape=jax.ShapeDtypeStruct((P_SIZE, 2048), F32),
+        in_specs=[SMEM] + [VMEM] * 12,
+        out_specs=VMEM,
+        scratch_shapes=[
+            pltpu.VMEM((64, 1024), F32),
+            pltpu.VMEM((64, 1024), F32),
+            pltpu.VMEM((4, 64, 256), F32),
+            pltpu.VMEM((K, 1024), BF),
+            pltpu.VMEM((64 * P_SIZE, 1024), BF),
+        ],
+        compiler_params=PARAMS,
+        name="token_sums",
+    )(place, *middle_args, *pay_parts)
+
+    sums = sums + core_flip(sums)
+    for bits in (1, 2, 4):
+        sums = sums + owner_flip(sums, bits)
+
+    return pl.pallas_call(
+        product_kernel,
+        out_shape=jax.ShapeDtypeStruct((P_SIZE, 1024), F32),
+        in_specs=[VMEM, VMEM],
+        out_specs=VMEM,
+        compiler_params=PARAMS,
+        name="products",
+    )(sums, weights)
+
+
+def per_device(tokens, gate_blocks, *rest):
+    fits = (
+        lax.axis_size("fsdp") == 8
+        and lax.axis_size("seq") == 2
+        and lax.axis_size("groups") == 2
+        and tokens.shape == (64, 8192)
+        and gate_blocks.shape == (160, 4096)
+        and rest[-2].shape == (P_SIZE, 256)
+    )
+    return (pair_split if fits else hidden_split)(tokens, gate_blocks, *rest)
+
+
 def solution(mesh):
     in_specs = (
         P(("groups", "fsdp", "seq"), None),

time: 474 us -> 146 us (0.31)
  blocking collectives: 216 us -> 0 us
  local copies, waits for them, and re-layouts: 107 us -> 4.37 us
  Pallas kernels: 0 us -> 40.7 us
  waiting for transfers between devices: 96 us -> 60.3 us
  starting transfers between devices: 13.2 us -> 35.9 us
  matrix products: 15.2 us -> 0 us
  between operations: 13.6 us -> 0.25 us
  other arithmetic: 10.7 us -> 3.86 us
    all_gather x1 -> x0, blocking collectives: 142 us -> none  [per_device(): full_sketch = lax.all_gather(sketch, 'fsdp', axis=1, tiled=True)]
    psum x2 -> x0, blocking collectives: 74.1 us -> none  [the longest x1 70.7 us: per_device(): sketch_rows = lax.psum(partial_sketch, 'fsdp').astype(jnp.bfloat16)]
    reduce_scatter x1 -> x0, waiting for transfers between devices: 61.1 us -> none  [per_device(): return lax.psum_scatter(products, 'fsdp', scatter_dimension=1, tiled=True)]
    ppermute x0 -> x24, waiting for transfers between devices: none -> 60.3 us  [the longest x18 58.8 us: owner_flip(): return lax.ppermute(value, 'fsdp', [(i, i ^ bits) for i in range(8)])]
    pallas_call x0 -> x5, Pallas kernels: none -> 40.7 us  [the longest x2 17.8 us: partial_sums(): pl.pallas_call(functools.partial(partial_kernel, which), out_shape=(jax.S...]
    ppermute x0 -> x24, starting transfers between devices: none -> 35.9 us  [the longest x18 33.8 us: owner_flip(): return lax.ppermute(value, 'fsdp', [(i, i ^ bits) for i in range(8)])]
    all_to_all x2 -> x0, waiting for transfers between devices: 34.2 us -> none  [the longest x1 34.2 us: per_device(): lax.all_to_all(down_dense, 'fsdp', split_axis=0, concat_axis=1, tiled=True)]
    all_to_all x4 -> x0, local copies, waits for them, and re-layouts: 28 us -> none  [the longest x2 18.5 us: per_device(): lax.all_to_all(stacked, 'fsdp', split_axis=1, concat_axis=0, tiled=True)]
  transfers between devices with their start and end apart: 4 -> 24, of which waited for: 2 -> 11; matrix products, arithmetic and copies ran while one was open for 20% -> 2% of each run, Pallas kernels for 0% -> 22%
where the time goes in v1:
time: 146 us; the launch traced here: 145 us
  waiting for transfers between devices  60.3 us (41%)
  Pallas kernels  40.7 us (28%)
  starting transfers between devices  35.9 us (25%)
  local copies, waits for them, and re-layouts  4.37 us (3%)
  other arithmetic  3.86 us (3%)
    ppermute x18, waiting for transfers between devices, owner_flip(): return lax.ppermute(value, 'fsdp', [(i, i ^ bits) for i in range(8)])  58.8 us
    ppermute x18, starting transfers between devices, owner_flip(): return lax.ppermute(value, 'fsdp', [(i, i ^ bits) for i in range(8)])  33.8 us
    pallas_call x2, Pallas kernels, partial_sums(): pl.pallas_call(functools.partial(partial_kernel, which), out_shape=(jax.S...  17.8 us
    pallas_call x1, Pallas kernels, pair_split(): pl.pallas_call(own_kernel, out_shape=(jax.ShapeDtypeStruct((8, 1024, 256)...  14.2 us
    pallas_call x1, Pallas kernels, pair_split(): pl.pallas_call(middle_kernel, out_shape=jax.ShapeDtypeStruct((P_SIZE, 204...  4.38 us
    pallas_call x1, Pallas kernels, pair_split(): pl.pallas_call(product_kernel, out_shape=jax.ShapeDtypeStruct((P_SIZE, 10...  4.31 us
  transfers between devices with their start and end apart: 24, of which 11 were waited for; matrix products, arithmetic and copies ran while one was open for 2% of the time, Pallas kernels for 22%

profile of v1, /device:TPU:0, one launch (start us, length us, event | category | flops | bytes accessed | tf_op | source)
XLA Modules:
  0.0 145.5 jit_solution(12853108363023239373)
XLA Ops:
  0.0 2.1 %constant_dynamic-slice_fusion.5 = bf16[80,4096]{1,0:T(8,128)(2,1)} fusion(bf16[160,4096]{1,0:T(8,128)(2,1)} %gate_ref.1, s32[]{:T(128)S(6)} %select_n.33), kind=kLoop, calls=%fused_computation.8 | loop fusion | bytes 1310724 | tf_op jit(solution)/shard_map/dynamic_slice | solution.py:397
  2.1 3.0 %collective-permute-start.1 = (bf16[80,4096]{1,0:T(8,128)(2,1)}, bf16[80,4096]{1,0:T(8,128)(2,1)S(1)}, u32[]{:S(2)}, u32[]{:S(2)}) collective-permute-start(bf16[80,4096]{1,0:T(8,128)(2,1)} %constant_dynamic-slice_fusion.5), channel_id=1, source_target_pairs={{0,2},{2,0},{4,6},{6,4},{8,10},{10,8},{12,14},{14,12},{1,3},{3,1},... | collective-permute-start | bytes 1966088 | tf_op jit(solution)/shard_map/ppermute | solution.py:379
  6.0 14.8 %collective-permute-done.1.first_ref = bf16[80,4096]{1,0:T(8,128)(2,1)S(1)} collective-permute-done((bf16[80,4096]{1,0:T(8,128)(2,1)}, bf16[80,4096]{1,0:T(8,128)(2,1)S(1)}, u32[]{:S(2)}, u32[]{:S(2)}) %collective-permute-start.1) | collective-permute-done | bytes 655392 | tf_op jit(solution)/shard_map/ppermute | solution.py:379
  21.4 14.2 %own_blocks.1 = (bf16[8,1024,256]{2,1,0:T(8,128)(2,1)}, f32[64,256]{1,0:T(8,128)}) custom-call(s32[4]{0:T(128)} %pad_add_fusion.1.place_ref, s32[3,256]{1,0:T(4,128)} %select_reduce_fusion.inv_ref, bf16[160,4096]{1,0:T(8,128)(2,1)} %gate_ref.1, bf16[160,4096]{1,0:T(8,128)(2,1)} %up_ref.1, bf16[160,4096]{1,0:T(8,128)(2,1)} %down_ref.1, ...), custom_call_target="tpu_custom_call" | custom-call | tf_op jit(solution)/shard_map/own_blocks/pallas_call | solution.py:400
  35.7 2.1 %collective-permute-start.14 = (f32[64,256]{1,0:T(8,128)}, f32[64,256]{1,0:T(8,128)S(1)}, u32[]{:S(2)}, u32[]{:S(2)}) collective-permute-start(f32[64,256]{1,0:T(8,128)} %get-tuple-element.24), channel_id=1, source_target_pairs={{0,2},{2,0},{4,6},{6,4},{8,10},{10,8},{12,14},{14,12},{1,3},{3,1},... | collective-permute-start | bytes 196616 | tf_op jit(solution)/shard_map/ppermute | solution.py:379
  38.3 2.4 %collective-permute-done.14 = f32[64,256]{1,0:T(8,128)S(1)} collective-permute-done((f32[64,256]{1,0:T(8,128)}, f32[64,256]{1,0:T(8,128)S(1)}, u32[]{:S(2)}, u32[]{:S(2)}) %collective-permute-start.14) | collective-permute-done | bytes 65568 | tf_op jit(solution)/shard_map/ppermute | solution.py:379
  41.5 1.9 %collective-permute-start.15 = (f32[64,256]{1,0:T(8,128)S(1)}, f32[64,256]{1,0:T(8,128)S(1)}, u32[]{:S(2)}, u32[]{:S(2)}) collective-permute-start(f32[64,256]{1,0:T(8,128)S(1)} %add.52), channel_id=1, source_target_pairs={{0,4},{2,6},{4,0},{6,2},{8,12},{10,14},{12,8},{14,10},{1,5},{3,7},... | collective-permute-start | bytes 196616 | tf_op jit(solution)/shard_map/ppermute | solution.py:379
  44.4 2.9 %collective-permute-start.4 = (bf16[64,2048]{1,0:T(8,128)(2,1)S(1)}, bf16[64,2048]{1,0:T(8,128)(2,1)S(1)}, u32[]{:S(2)}, u32[]{:S(2)}) collective-permute-start(bf16[64,2048]{1,0:T(8,128)(2,1)S(1)} %get-tuple-element.28), channel_id=1, source_target_pairs={{0,8},{2,10},{4,12},{6,14},{8,0},{10,2},{12,4},{14,6},{1,9},{3,11}... | collective-permute-start | bytes 786440 | tf_op jit(solution)/shard_map/ppermute | solution.py:379
  47.3 3.1 %collective-permute-start.5 = (bf16[64,2048]{1,0:T(8,128)(2,1)S(1)}, bf16[64,2048]{1,0:T(8,128)(2,1)S(1)}, u32[]{:S(2)}, u32[]{:S(2)}) collective-permute-start(bf16[64,2048]{1,0:T(8,128)(2,1)S(1)} %get-tuple-element.25), channel_id=1, source_target_pairs={{0,12},{2,14},{4,8},{6,10},{8,4},{10,6},{12,0},{14,2},{1,13},{3,15... | collective-permute-start | bytes 786440 | tf_op jit(solution)/shard_map/ppermute | solution.py:379
  50.4 6.7 %collective-permute-done.3.tok1_ref = bf16[64,2048]{1,0:T(8,128)(2,1)S(1)} collective-permute-done((bf16[64,2048]{1,0:T(8,128)(2,1)S(1)}, bf16[64,2048]{1,0:T(8,128)(2,1)S(1)}, u32[]{:S(2)}, u32[]{:S(2)}) %collective-permute-start.3) | collective-permute-done | bytes 262176 | tf_op jit(solution)/shard_map/ppermute | solution.py:379
  57.1 10.1 %collective-permute-done.4.tok2_ref = bf16[64,2048]{1,0:T(8,128)(2,1)S(1)} collective-permute-done((bf16[64,2048]{1,0:T(8,128)(2,1)S(1)}, bf16[64,2048]{1,0:T(8,128)(2,1)S(1)}, u32[]{:S(2)}, u32[]{:S(2)}) %collective-permute-start.4) | collective-permute-done | bytes 262176 | tf_op jit(solution)/shard_map/ppermute | solution.py:379
  68.0 8.9 %partial_sums.2 = (f32[64,1024]{1,0:T(8,128)}, bf16[64,1024]{1,0:T(8,128)(2,1)}, bf16[64,1024]{1,0:T(8,128)(2,1)}, bf16[64,1024]{1,0:T(8,128)(2,1)}) custom-call(s32[4]{0:T(128)} %pad_add_fusion.1.place_ref, s32[3,256]{1,0:T(4,128)} %copy-done.18, bf16[80,4096]{1,0:T(8,128)(2,1)} %copy-done.6, bf16[80,4096]{1,0:T(8,128)(2,1)} %collective-permute-done.2.second_ref, ...), custom_call_target="tpu_custom_call" | custom-call | tf_op jit(solution)/shard_map/partial_sums/pallas_call | solution.py:428
  76.9 5.4 %collective-permute-start.6 = (bf16[64,1024]{1,0:T(8,128)(2,1)}, bf16[64,1024]{1,0:T(8,128)(2,1)S(1)}, u32[]{:S(2)}, u32[]{:S(2)}) collective-permute-start(bf16[64,1024]{1,0:T(8,128)(2,1)} %get-tuple-element.17), channel_id=1, source_target_pairs={{0,4},{2,6},{4,0},{6,2},{8,12},{10,14},{12,8},{14,10},{1,5},{3,7},... | collective-permute-start | bytes 393224 | tf_op jit(solution)/shard_map/ppermute | solution.py:379
  82.4 1.6 %collective-permute-start.18 = (f32[64,256]{1,0:T(8,128)S(1)}, f32[64,256]{1,0:T(8,128)S(1)}, u32[]{:S(2)}, u32[]{:S(2)}) collective-permute-start(f32[64,256]{1,0:T(8,128)S(1)} %add.54.pay0_ref), channel_id=1, source_target_pairs={{0,16},{16,0},{1,17},{17,1},{2,18},{18,2},{3,19},{19,3},{4,20},{20... | collective-permute-start | bytes 196616 | tf_op jit(solution)/shard_map/ppermute | solution.py:423
  84.2 1.9 %collective-permute-start.7 = (bf16[64,1024]{1,0:T(8,128)(2,1)}, bf16[64,1024]{1,0:T(8,128)(2,1)S(1)}, u32[]{:S(2)}, u32[]{:S(2)}) collective-permute-start(bf16[64,1024]{1,0:T(8,128)(2,1)} %get-tuple-element.18), channel_id=1, source_target_pairs={{0,8},{2,10},{4,12},{6,14},{8,0},{10,2},{12,4},{14,6},{1,9},{3,11}... | collective-permute-start | bytes 393224 | tf_op jit(solution)/shard_map/ppermute | solution.py:379
  86.2 8.9 %partial_sums.3 = (f32[64,1024]{1,0:T(8,128)}, bf16[64,1024]{1,0:T(8,128)(2,1)}, bf16[64,1024]{1,0:T(8,128)(2,1)}, bf16[64,1024]{1,0:T(8,128)(2,1)}) custom-call(s32[4]{0:T(128)} %pad_add_fusion.1.place_ref, s32[3,256]{1,0:T(4,128)} %copy-done.18, bf16[80,4096]{1,0:T(8,128)(2,1)} %copy-done.5, bf16[80,4096]{1,0:T(8,128)(2,1)} %copy-done.7, ...), custom_call_target="tpu_custom_call" | custom-call | tf_op jit(solution)/shard_map/partial_sums/pallas_call | solution.py:428
  95.1 2.3 %collective-permute-start.8 = (bf16[64,1024]{1,0:T(8,128)(2,1)S(1)}, bf16[64,1024]{1,0:T(8,128)(2,1)S(1)}, u32[]{:S(2)}, u32[]{:S(2)}) collective-permute-start(bf16[64,1024]{1,0:T(8,128)(2,1)S(1)} %copy-done.23), channel_id=1, source_target_pairs={{0,12},{2,14},{4,8},{6,10},{8,4},{10,6},{12,0},{14,2},{1,13},{3,15... | collective-permute-start | bytes 393224 | tf_op jit(solution)/shard_map/ppermute | solution.py:379
  97.5 2.1 %collective-permute-start.12 = (bf16[64,1024]{1,0:T(8,128)(2,1)}, bf16[64,1024]{1,0:T(8,128)(2,1)S(1)}, u32[]{:S(2)}, u32[]{:S(2)}) collective-permute-start(bf16[64,1024]{1,0:T(8,128)(2,1)} %get-tuple-element.22), channel_id=1, source_target_pairs={{0,8},{2,10},{4,12},{6,14},{8,0},{10,2},{12,4},{14,6},{1,9},{3,11}... | collective-permute-start | bytes 393224 | tf_op jit(solution)/shard_map/ppermute | solution.py:379
  99.6 2.3 %collective-permute-start.13 = (bf16[64,1024]{1,0:T(8,128)(2,1)}, bf16[64,1024]{1,0:T(8,128)(2,1)S(1)}, u32[]{:S(2)}, u32[]{:S(2)}) collective-permute-start(bf16[64,1024]{1,0:T(8,128)(2,1)} %get-tuple-element.23), channel_id=1, source_target_pairs={{0,12},{2,14},{4,8},{6,10},{8,4},{10,6},{12,0},{14,2},{1,13},{3,15... | collective-permute-start | bytes 393224 | tf_op jit(solution)/shard_map/ppermute | solution.py:379
  101.9 1.5 %collective-permute-done.8.gate3_ref = bf16[64,1024]{1,0:T(8,128)(2,1)S(1)} collective-permute-done((bf16[64,1024]{1,0:T(8,128)(2,1)S(1)}, bf16[64,1024]{1,0:T(8,128)(2,1)S(1)}, u32[]{:S(2)}, u32[]{:S(2)}) %collective-permute-start.8) | collective-permute-done | bytes 131104 | tf_op jit(solution)/shard_map/ppermute | solution.py:379
  103.4 2.3 %collective-permute-done.11.up1_ref = bf16[64,1024]{1,0:T(8,128)(2,1)S(1)} collective-permute-done((bf16[64,1024]{1,0:T(8,128)(2,1)}, bf16[64,1024]{1,0:T(8,128)(2,1)S(1)}, u32[]{:S(2)}, u32[]{:S(2)}) %collective-permute-start.11) | collective-permute-done | bytes 131104 | tf_op jit(solution)/shard_map/ppermute | solution.py:379
  105.6 8.1 %collective-permute-done.12.up2_ref = bf16[64,1024]{1,0:T(8,128)(2,1)S(1)} collective-permute-done((bf16[64,1024]{1,0:T(8,128)(2,1)}, bf16[64,1024]{1,0:T(8,128)(2,1)S(1)}, u32[]{:S(2)}, u32[]{:S(2)}) %collective-permute-start.12) | collective-permute-done | bytes 131104 | tf_op jit(solution)/shard_map/ppermute | solution.py:379
  114.5 4.4 %token_sums.1 = f32[16,2048]{1,0:T(8,128)} custom-call(s32[4]{0:T(128)} %pad_add_fusion.1.place_ref, f32[64,1024]{1,0:T(8,128)} %get-tuple-element.16.gate0_ref, bf16[64,1024]{1,0:T(8,128)(2,1)} %copy-done.9, bf16[64,1024]{1,0:T(8,128)(2,1)} %copy-done.10, bf16[64,1024]{1,0:T(8,128)(2,1)} %copy-done.11, f32[64,1024]{1,0:T(8,128)} %get-tuple-element.20.up0_ref, ...), custom_call_target="tpu_custom_call" | custom-call | tf_op jit(solution)/shard_map/token_sums/pallas_call | solution.py:453
  118.8 1.6 %collective-permute-done.20 = f32[16,2048]{1,0:T(8,128)S(1)} collective-permute-done((f32[16,2048]{1,0:T(8,128)}, f32[16,2048]{1,0:T(8,128)S(1)}, u32[]{:S(2)}, u32[]{:S(2)}) %collective-permute-start.20) | collective-permute-done | bytes 131104 | tf_op jit(solution)/shard_map/ppermute | solution.py:382
  120.4 0.9 add.55
  121.3 1.6 %collective-permute-start.21 = (f32[16,2048]{1,0:T(8,128)S(1)}, f32[16,2048]{1,0:T(8,128)S(1)}, u32[]{:S(2)}, u32[]{:S(2)}) collective-permute-start(f32[16,2048]{1,0:T(8,128)S(1)} %add.55), channel_id=1, source_target_pairs={{0,2},{2,0},{4,6},{6,4},{8,10},{10,8},{12,14},{14,12},{1,3},{3,1},... | collective-permute-start | bytes 393224 | tf_op jit(solution)/shard_map/ppermute | solution.py:379
  122.9 4.0 %collective-permute-done.21 = f32[16,2048]{1,0:T(8,128)S(1)} collective-permute-done((f32[16,2048]{1,0:T(8,128)S(1)}, f32[16,2048]{1,0:T(8,128)S(1)}, u32[]{:S(2)}, u32[]{:S(2)}) %collective-permute-start.21) | collective-permute-done | bytes 131104 | tf_op jit(solution)/shard_map/ppermute | solution.py:379
  127.0 2.9 %collective-permute-start.22 = (f32[16,2048]{1,0:T(8,128)S(1)}, f32[16,2048]{1,0:T(8,128)S(1)}, u32[]{:S(2)}, u32[]{:S(2)}) collective-permute-start(f32[16,2048]{1,0:T(8,128)S(1)} %add.56), channel_id=1, source_target_pairs={{0,4},{2,6},{4,0},{6,2},{8,12},{10,14},{12,8},{14,10},{1,5},{3,7},... | collective-permute-start | bytes 393224 | tf_op jit(solution)/shard_map/ppermute | solution.py:379
  129.9 3.0 %collective-permute-done.22 = f32[16,2048]{1,0:T(8,128)S(1)} collective-permute-done((f32[16,2048]{1,0:T(8,128)S(1)}, f32[16,2048]{1,0:T(8,128)S(1)}, u32[]{:S(2)}, u32[]{:S(2)}) %collective-permute-start.22) | collective-permute-done | bytes 131104 | tf_op jit(solution)/shard_map/ppermute | solution.py:379
  132.9 1.8 %collective-permute-start.23 = (f32[16,2048]{1,0:T(8,128)S(1)}, f32[16,2048]{1,0:T(8,128)S(1)}, u32[]{:S(2)}, u32[]{:S(2)}) collective-permute-start(f32[16,2048]{1,0:T(8,128)S(1)} %add.57), channel_id=1, source_target_pairs={{0,8},{2,10},{4,12},{6,14},{8,0},{10,2},{12,4},{14,6},{1,9},{3,11}... | collective-permute-start | bytes 393224 | tf_op jit(solution)/shard_map/ppermute | solution.py:379
  134.7 5.8 %collective-permute-done.23 = f32[16,2048]{1,0:T(8,128)S(1)} collective-permute-done((f32[16,2048]{1,0:T(8,128)S(1)}, f32[16,2048]{1,0:T(8,128)S(1)}, u32[]{:S(2)}, u32[]{:S(2)}) %collective-permute-start.23) | collective-permute-done | bytes 131104 | tf_op jit(solution)/shard_map/ppermute | solution.py:379
  141.1 4.3 %products.1 = f32[16,1024]{1,0:T(8,128)} custom-call(f32[16,2048]{1,0:T(8,128)} %add.58.sum_ref, bf16[8,1024,256]{2,1,0:T(8,128)(2,1)} %get-tuple-element.15.own_weight_ref.weight_ref), custom_call_target="tpu_custom_call" | custom-call | tf_op jit(solution)/shard_map/products/pallas_call | solution.py:473
  (82 shorter events, 6.4 us)
Async XLA Ops:
  2.1 18.7 %collective-permute-start.1 = (bf16[80,4096]{1,0:T(8,128)(2,1)}, bf16[80,4096]{1,0:T(8,128)(2,1)S(1)}, u32[]{:S(2)}, u32[]{:S(2)}) collective-permute-start(bf16[80,4096]{1,0:T(8,128)(2,1)} %constant_dynamic-slice_fusion.5), channel_id=1, source_target_pairs={{0,2},{2,0},{4,6},{6,4},{8,10},{10,8},{12,14},{14,12},{1,3},{3,1},... | collective-permute-start | bytes 1966088 | tf_op jit(solution)/shard_map/ppermute | solution.py:379
  5.1 32.7 %collective-permute-start.9 = (bf16[80,4096]{1,0:T(8,128)(2,1)S(1)}, bf16[80,4096]{1,0:T(8,128)(2,1)S(1)}, u32[]{:S(2)}, u32[]{:S(2)}) collective-permute-start(bf16[80,4096]{1,0:T(8,128)(2,1)S(1)} %constant_dynamic-slice_fusion), channel_id=1, source_target_pairs={{0,2},{2,0},{4,6},{6,4},{8,10},{10,8},{12,14},{14,12},{1,3},{3,1},... | collective-permute-start | bytes 1966088 | tf_op jit(solution)/shard_map/ppermute | solution.py:379
  20.8 46.4 %collective-permute-start.2 = (bf16[80,4096]{1,0:T(8,128)(2,1)S(1)}, bf16[80,4096]{1,0:T(8,128)(2,1)}, u32[]{:S(2)}, u32[]{:S(2)}) collective-permute-start(bf16[80,4096]{1,0:T(8,128)(2,1)S(1)} %collective-permute-done.1.first_ref), channel_id=1, source_target_pairs={{0,1},{1,0},{2,3},{3,2},{4,5},{5,4},{6,7},{7,6},{8,9},{9,8},{10,11... | collective-permute-start | bytes 1966088 | tf_op jit(solution)/shard_map/ppermute | solution.py:382
  21.4 16.5 %copy-start.19 = (s32[3,256]{1,0:T(4,128)S(1)}, s32[3,256]{1,0:T(4,128)}, u32[]{:S(2)}) copy-start(s32[3,256]{1,0:T(4,128)} %select_reduce_fusion.inv_ref) | copy-start | bytes 9220
  21.4 22.0 %copy-start.4 = (bf16[64,8192]{1,0:T(8,128)(2,1)S(1)}, bf16[64,8192]{1,0:T(8,128)(2,1)}, u32[]{:S(2)}) copy-start(bf16[64,8192]{1,0:T(8,128)(2,1)} %param.10) | copy-start | bytes 3145732
  35.7 5.0 %collective-permute-start.14 = (f32[64,256]{1,0:T(8,128)}, f32[64,256]{1,0:T(8,128)S(1)}, u32[]{:S(2)}, u32[]{:S(2)}) collective-permute-start(f32[64,256]{1,0:T(8,128)} %get-tuple-element.24), channel_id=1, source_target_pairs={{0,2},{2,0},{4,6},{6,4},{8,10},{10,8},{12,14},{14,12},{1,3},{3,1},... | collective-permute-start | bytes 196616 | tf_op jit(solution)/shard_map/ppermute | solution.py:379
  37.8 39.1 %copy-start.5 = (bf16[80,4096]{1,0:T(8,128)(2,1)}, bf16[80,4096]{1,0:T(8,128)(2,1)S(1)}, u32[]{:S(2)}) copy-start(bf16[80,4096]{1,0:T(8,128)(2,1)S(1)} %collective-permute-done.9.first_ref) | copy-start | bytes 1966084
  37.8 46.5 %collective-permute-start.10 = (bf16[80,4096]{1,0:T(8,128)(2,1)S(1)}, bf16[80,4096]{1,0:T(8,128)(2,1)S(1)}, u32[]{:S(2)}, u32[]{:S(2)}) collective-permute-start(bf16[80,4096]{1,0:T(8,128)(2,1)S(1)} %collective-permute-done.9.first_ref), channel_id=1, source_target_pairs={{0,1},{1,0},{2,3},{3,2},{4,5},{5,4},{6,7},{7,6},{8,9},{9,8},{10,11... | collective-permute-start | bytes 1966088 | tf_op jit(solution)/shard_map/ppermute | solution.py:382
  37.9 6.5 %collective-permute-start = (s32[3,256]{1,0:T(4,128)S(1)}, s32[3,256]{1,0:T(4,128)S(1)}, u32[]{:S(2)}, u32[]{:S(2)}) collective-permute-start(s32[3,256]{1,0:T(4,128)S(1)} %copy-done.19), channel_id=1, source_target_pairs={{0,2},{2,0},{4,6},{6,4},{8,10},{10,8},{12,14},{14,12},{1,3},{3,1},... | collective-permute-start | bytes 9224 | tf_op jit(solution)/shard_map/ppermute | solution.py:379
  41.5 5.8 %collective-permute-start.15 = (f32[64,256]{1,0:T(8,128)S(1)}, f32[64,256]{1,0:T(8,128)S(1)}, u32[]{:S(2)}, u32[]{:S(2)}) collective-permute-start(f32[64,256]{1,0:T(8,128)S(1)} %add.52), channel_id=1, source_target_pairs={{0,4},{2,6},{4,0},{6,2},{8,12},{10,14},{12,8},{14,10},{1,5},{3,7},... | collective-permute-start | bytes 196616 | tf_op jit(solution)/shard_map/ppermute | solution.py:379
  44.2 12.8 %collective-permute-start.3 = (bf16[64,2048]{1,0:T(8,128)(2,1)S(1)}, bf16[64,2048]{1,0:T(8,128)(2,1)S(1)}, u32[]{:S(2)}, u32[]{:S(2)}) collective-permute-start(bf16[64,2048]{1,0:T(8,128)(2,1)S(1)} %get-tuple-element.26), channel_id=1, source_target_pairs={{0,4},{2,6},{4,0},{6,2},{8,12},{10,14},{12,8},{14,10},{1,5},{3,7},... | collective-permute-start | bytes 786440 | tf_op jit(solution)/shard_map/ppermute | solution.py:379
  44.4 22.8 %copy-start.18 = (s32[3,256]{1,0:T(4,128)}, s32[3,256]{1,0:T(4,128)S(1)}, u32[]{:S(2)}) copy-start(s32[3,256]{1,0:T(4,128)S(1)} %collective-permute-done.inv_ref) | copy-start | bytes 9220
  44.4 22.8 %collective-permute-start.4 = (bf16[64,2048]{1,0:T(8,128)(2,1)S(1)}, bf16[64,2048]{1,0:T(8,128)(2,1)S(1)}, u32[]{:S(2)}, u32[]{:S(2)}) collective-permute-start(bf16[64,2048]{1,0:T(8,128)(2,1)S(1)} %get-tuple-element.28), channel_id=1, source_target_pairs={{0,8},{2,10},{4,12},{6,14},{8,0},{10,2},{12,4},{14,6},{1,9},{3,11}... | collective-permute-start | bytes 786440 | tf_op jit(solution)/shard_map/ppermute | solution.py:379
  47.3 19.9 %collective-permute-start.5 = (bf16[64,2048]{1,0:T(8,128)(2,1)S(1)}, bf16[64,2048]{1,0:T(8,128)(2,1)S(1)}, u32[]{:S(2)}, u32[]{:S(2)}) collective-permute-start(bf16[64,2048]{1,0:T(8,128)(2,1)S(1)} %get-tuple-element.25), channel_id=1, source_target_pairs={{0,12},{2,14},{4,8},{6,10},{8,4},{10,6},{12,0},{14,2},{1,13},{3,15... | collective-permute-start | bytes 786440 | tf_op jit(solution)/shard_map/ppermute | solution.py:379
  57.1 25.2 %collective-permute-start.16 = (f32[64,256]{1,0:T(8,128)S(1)}, f32[64,256]{1,0:T(8,128)S(1)}, u32[]{:S(2)}, u32[]{:S(2)}) collective-permute-start(f32[64,256]{1,0:T(8,128)S(1)} %add.53), channel_id=1, source_target_pairs={{0,8},{2,10},{4,12},{6,14},{8,0},{10,2},{12,4},{14,6},{1,9},{3,11}... | collective-permute-start | bytes 196616 | tf_op jit(solution)/shard_map/ppermute | solution.py:379
  76.9 22.7 %collective-permute-start.6 = (bf16[64,1024]{1,0:T(8,128)(2,1)}, bf16[64,1024]{1,0:T(8,128)(2,1)S(1)}, u32[]{:S(2)}, u32[]{:S(2)}) collective-permute-start(bf16[64,1024]{1,0:T(8,128)(2,1)} %get-tuple-element.17), channel_id=1, source_target_pairs={{0,4},{2,6},{4,0},{6,2},{8,12},{10,14},{12,8},{14,10},{1,5},{3,7},... | collective-permute-start | bytes 393224 | tf_op jit(solution)/shard_map/ppermute | solution.py:379
  82.3 31.5 %copy-start.8 = (f32[64,256]{1,0:T(8,128)}, f32[64,256]{1,0:T(8,128)S(1)}, u32[]{:S(2)}) copy-start(f32[64,256]{1,0:T(8,128)S(1)} %add.54.pay0_ref) | copy-start | bytes 196612
  82.3 12.8 %collective-permute-start.17 = (f32[64,256]{1,0:T(8,128)S(1)}, f32[64,256]{1,0:T(8,128)S(1)}, u32[]{:S(2)}, u32[]{:S(2)}) collective-permute-start(f32[64,256]{1,0:T(8,128)S(1)} %add.54.pay0_ref), channel_id=1, source_target_pairs={{0,1},{1,0},{2,3},{3,2},{4,5},{5,4},{6,7},{7,6},{8,9},{9,8},{10,11... | collective-permute-start | bytes 196616 | tf_op jit(solution)/shard_map/ppermute | solution.py:382
  82.4 15.1 %collective-permute-start.18 = (f32[64,256]{1,0:T(8,128)S(1)}, f32[64,256]{1,0:T(8,128)S(1)}, u32[]{:S(2)}, u32[]{:S(2)}) collective-permute-start(f32[64,256]{1,0:T(8,128)S(1)} %add.54.pay0_ref), channel_id=1, source_target_pairs={{0,16},{16,0},{1,17},{17,1},{2,18},{18,2},{3,19},{19,3},{4,20},{20... | collective-permute-start | bytes 196616 | tf_op jit(solution)/shard_map/ppermute | solution.py:423
  83.9 13.5 %collective-permute-start.19 = (f32[64,256]{1,0:T(8,128)S(1)}, f32[64,256]{1,0:T(8,128)S(1)}, u32[]{:S(2)}, u32[]{:S(2)}) collective-permute-start(f32[64,256]{1,0:T(8,128)S(1)} %add.54.pay0_ref), channel_id=1, source_target_pairs={{0,17},{1,16},{16,1},{17,0},{2,19},{3,18},{18,3},{19,2},{4,21},{5,... | collective-permute-start | bytes 196616 | tf_op jit(solution)/shard_map/ppermute | solution.py:424
  84.2 17.6 %collective-permute-start.7 = (bf16[64,1024]{1,0:T(8,128)(2,1)}, bf16[64,1024]{1,0:T(8,128)(2,1)S(1)}, u32[]{:S(2)}, u32[]{:S(2)}) collective-permute-start(bf16[64,1024]{1,0:T(8,128)(2,1)} %get-tuple-element.18), channel_id=1, source_target_pairs={{0,8},{2,10},{4,12},{6,14},{8,0},{10,2},{12,4},{14,6},{1,9},{3,11}... | collective-permute-start | bytes 393224 | tf_op jit(solution)/shard_map/ppermute | solution.py:379
  95.1 18.7 %copy-start.15 = (f32[64,256]{1,0:T(8,128)}, f32[64,256]{1,0:T(8,128)S(1)}, u32[]{:S(2)}) copy-start(f32[64,256]{1,0:T(8,128)S(1)} %collective-permute-done.17.pay1_ref) | copy-start | bytes 196612
  95.1 8.3 %collective-permute-start.8 = (bf16[64,1024]{1,0:T(8,128)(2,1)S(1)}, bf16[64,1024]{1,0:T(8,128)(2,1)S(1)}, u32[]{:S(2)}, u32[]{:S(2)}) collective-permute-start(bf16[64,1024]{1,0:T(8,128)(2,1)S(1)} %copy-done.23), channel_id=1, source_target_pairs={{0,12},{2,14},{4,8},{6,10},{8,4},{10,6},{12,0},{14,2},{1,13},{3,15... | collective-permute-start | bytes 393224 | tf_op jit(solution)/shard_map/ppermute | solution.py:379
  97.4 16.3 %copy-start.16 = (f32[64,256]{1,0:T(8,128)}, f32[64,256]{1,0:T(8,128)S(1)}, u32[]{:S(2)}) copy-start(f32[64,256]{1,0:T(8,128)S(1)} %collective-permute-done.18.pay2_ref) | copy-start | bytes 196612
  97.4 8.2 %collective-permute-start.11 = (bf16[64,1024]{1,0:T(8,128)(2,1)}, bf16[64,1024]{1,0:T(8,128)(2,1)S(1)}, u32[]{:S(2)}, u32[]{:S(2)}) collective-permute-start(bf16[64,1024]{1,0:T(8,128)(2,1)} %get-tuple-element.21), channel_id=1, source_target_pairs={{0,4},{2,6},{4,0},{6,2},{8,12},{10,14},{12,8},{14,10},{1,5},{3,7},... | collective-permute-start | bytes 393224 | tf_op jit(solution)/shard_map/ppermute | solution.py:379
  97.5 16.3 %copy-start.17 = (f32[64,256]{1,0:T(8,128)}, f32[64,256]{1,0:T(8,128)S(1)}, u32[]{:S(2)}) copy-start(f32[64,256]{1,0:T(8,128)S(1)} %collective-permute-done.19.pay3_ref) | copy-start | bytes 196612
  97.5 16.3 %collective-permute-start.12 = (bf16[64,1024]{1,0:T(8,128)(2,1)}, bf16[64,1024]{1,0:T(8,128)(2,1)S(1)}, u32[]{:S(2)}, u32[]{:S(2)}) collective-permute-start(bf16[64,1024]{1,0:T(8,128)(2,1)} %get-tuple-element.22), channel_id=1, source_target_pairs={{0,8},{2,10},{4,12},{6,14},{8,0},{10,2},{12,4},{14,6},{1,9},{3,11}... | collective-permute-start | bytes 393224 | tf_op jit(solution)/shard_map/ppermute | solution.py:379
  99.6 14.2 %collective-permute-start.13 = (bf16[64,1024]{1,0:T(8,128)(2,1)}, bf16[64,1024]{1,0:T(8,128)(2,1)S(1)}, u32[]{:S(2)}, u32[]{:S(2)}) collective-permute-start(bf16[64,1024]{1,0:T(8,128)(2,1)} %get-tuple-element.23), channel_id=1, source_target_pairs={{0,12},{2,14},{4,8},{6,10},{8,4},{10,6},{12,0},{14,2},{1,13},{3,15... | collective-permute-start | bytes 393224 | tf_op jit(solution)/shard_map/ppermute | solution.py:379
  118.8 1.6 %collective-permute-start.20 = (f32[16,2048]{1,0:T(8,128)}, f32[16,2048]{1,0:T(8,128)S(1)}, u32[]{:S(2)}, u32[]{:S(2)}) collective-permute-start(f32[16,2048]{1,0:T(8,128)} %token_sums.1), channel_id=1, source_target_pairs={{0,1},{1,0},{2,3},{3,2},{4,5},{5,4},{6,7},{7,6},{8,9},{9,8},{10,11... | collective-permute-start | bytes 393224 | tf_op jit(solution)/shard_map/ppermute | solution.py:382
  121.3 5.6 %collective-permute-start.21 = (f32[16,2048]{1,0:T(8,128)S(1)}, f32[16,2048]{1,0:T(8,128)S(1)}, u32[]{:S(2)}, u32[]{:S(2)}) collective-permute-start(f32[16,2048]{1,0:T(8,128)S(1)} %add.55), channel_id=1, source_target_pairs={{0,2},{2,0},{4,6},{6,4},{8,10},{10,8},{12,14},{14,12},{1,3},{3,1},... | collective-permute-start | bytes 393224 | tf_op jit(solution)/shard_map/ppermute | solution.py:379
  127.0 5.9 %collective-permute-start.22 = (f32[16,2048]{1,0:T(8,128)S(1)}, f32[16,2048]{1,0:T(8,128)S(1)}, u32[]{:S(2)}, u32[]{:S(2)}) collective-permute-start(f32[16,2048]{1,0:T(8,128)S(1)} %add.56), channel_id=1, source_target_pairs={{0,4},{2,6},{4,0},{6,2},{8,12},{10,14},{12,8},{14,10},{1,5},{3,7},... | collective-permute-start | bytes 393224 | tf_op jit(solution)/shard_map/ppermute | solution.py:379
  132.9 7.6 %collective-permute-start.23 = (f32[16,2048]{1,0:T(8,128)S(1)}, f32[16,2048]{1,0:T(8,128)S(1)}, u32[]{:S(2)}, u32[]{:S(2)}) collective-permute-start(f32[16,2048]{1,0:T(8,128)S(1)} %add.57), channel_id=1, source_target_pairs={{0,8},{2,10},{4,12},{6,14},{8,0},{10,2},{12,4},{14,6},{1,9},{3,11}... | collective-permute-start | bytes 393224 | tf_op jit(solution)/shard_map/ppermute | solution.py:379
  (16 other events, 106.1 us)

commit v2 on v1

--- a/solution.py
+++ b/solution.py
@@ -16,6 +16,7 @@
 F32 = jnp.float32
 VMEM = pl.BlockSpec(memory_space=pltpu.VMEM)
 SMEM = pl.BlockSpec(memory_space=pltpu.SMEM)
+
 PARAMS = pltpu.CompilerParams(vmem_limit_bytes=56 * 1024 * 1024)
 
 
@@ -233,40 +234,40 @@
         payload_ref[16 * which : 16 * (which + 1), :] = triple[:16] + triple[16:32] + triple[32:]
 
 
+def near_kernel(inv_row, place_ref, inv_ref, first_ref, second_ref, weight_ref, tiles_ref):
+    core = place_ref[3]
+    tiles_ref[pl.ds(160 * 32, 32), :] = jnp.zeros((32, 128), F32)
+    stage_blocks(first_ref, tiles_ref, core * 80)
+    stage_blocks(second_ref, tiles_ref, (1 - core) * 80)
+
+    def put(pair, row, piece):
+        lane = (pair % 2) * 128
+        weight_ref[pair // 2, pl.ds(row, 32), lane : lane + 128] = piece
+
+    assemble_columns(inv_ref, inv_row, tiles_ref, put)
+
+
 def partial_kernel(
-    inv_row,
     place_ref,
-    inv_ref,
-    first_ref,
-    second_ref,
     own_weight_ref,
-    tok0_ref,
-    tok1_ref,
-    tok2_ref,
-    tok3_ref,
+    weight_ref,
+    tok_ref,
     keep_ref,
     out1_ref,
     out2_ref,
     out3_ref,
-    tiles_ref,
-    weight_ref,
     tokens_ref,
 ):
     side = place_ref[2]
-    core = place_ref[3]
-    tiles_ref[pl.ds(160 * 32, 32), :] = jnp.zeros((32, 128), F32)
-    stage_blocks(first_ref, tiles_ref, core * 80)
-    stage_blocks(second_ref, tiles_ref, (1 - core) * 80)
-
-    def put(pair, row, piece):
-        lane = (pair % 2) * 128
-        weight_ref[pair // 2, pl.ds(row, 32), lane : lane + 128] = piece
-
-    assemble_columns(inv_ref, inv_row, tiles_ref, put)
+    zone = place_ref[0] // 2
     shuffle = shuffle_matrix(256)
-    for source, tok_ref in enumerate((tok0_ref, tok1_ref, tok2_ref, tok3_ref)):
+    low_bit = lax.rem(zone, 2)
+    high_bit = zone // 2
+    for source in range(4):
+        spot = lax.rem(low_bit + source % 2, 2) + 2 * lax.rem(high_bit + source // 2, 2)
         for group in range(8):
-            moved = dot(tok_ref[:, 256 * group : 256 * (group + 1)], shuffle).astype(BF)
+            piece = tok_ref[spot, :, 256 * group : 256 * (group + 1)]
+            moved = dot(piece, shuffle).astype(BF)
             half = lax.rem(group // 4 + side, 2)
             tokens_ref[
                 half, 64 * source : 64 * (source + 1), 256 * (group % 4) : 256 * (group % 4 + 1)
@@ -381,17 +382,20 @@
     def core_flip(value):
         return lax.ppermute(value, "seq", [(0, 1), (1, 0)])
 
-    def token_slice(target_zone):
-        return lax.dynamic_slice(tokens, (0, target_zone * 2048), (64, 2048))
-
     slots = jnp.stack([gate_slot, up_slot, down_slot])
     cells = lax.broadcasted_iota(jnp.int32, (3, 160, 256), 2)
     slot_numbers = lax.broadcasted_iota(jnp.int32, (3, 160, 256), 1)
     inv = jnp.min(jnp.where(slots[:, :, None] == cells, slot_numbers, 160), axis=1)
 
-    tok_parts = [token_slice(zone)]
-    for flip in (1, 2, 3):
-        tok_parts.append(owner_flip(token_slice(zone ^ flip), 2 * flip))
+    by_zone = tokens.reshape(64, 4, 2048).transpose(1, 0, 2)
+    gathered = lax.all_to_all(
+        by_zone,
+        "fsdp",
+        split_axis=0,
+        concat_axis=0,
+        tiled=True,
+        axis_index_groups=[[0, 2, 4, 6], [1, 3, 5, 7]],
+    )
 
     near_inv = owner_flip(inv, 1)
     near_gate = owner_flip(lax.dynamic_slice(gate_blocks, (core * 80, 0), (80, 4096)), 1)
@@ -424,24 +428,32 @@
         lax.ppermute(payload, ("groups", "seq"), [(i, i ^ 3) for i in range(4)]),
     ]
 
+    def near_weights(which, near):
+        return pl.pallas_call(
+            functools.partial(near_kernel, which),
+            out_shape=jax.ShapeDtypeStruct((4, 1024, 256), BF),
+            in_specs=[SMEM, SMEM, VMEM, VMEM],
+            out_specs=VMEM,
+            scratch_shapes=[pltpu.VMEM((161 * 32, 128), F32)],
+            compiler_params=PARAMS,
+            name="near_blocks",
+        )(place, near_inv, near, core_flip(near))
+
     def partial_sums(which, near):
+        near_dense = near_weights(which, near)
         return pl.pallas_call(
-            functools.partial(partial_kernel, which),
+            partial_kernel,
             out_shape=(jax.ShapeDtypeStruct((64, 1024), F32),)
             + (jax.ShapeDtypeStruct((64, 1024), BF),) * 3,
             grid=(1,),
-            in_specs=[SMEM, SMEM, VMEM, VMEM]
+            in_specs=[SMEM]
             + [pl.BlockSpec((4, 1024, 256), lambda i: (which, 0, 0))]
-            + [VMEM] * 4,
+            + [VMEM] * 2,
             out_specs=(VMEM,) * 4,
-            scratch_shapes=[
-                pltpu.VMEM((161 * 32, 128), F32),
-                pltpu.VMEM((4, 1024, 256), BF),
-                pltpu.VMEM((2, 256, 1024), BF),
-            ],
+            scratch_shapes=[pltpu.VMEM((2, 256, 1024), BF)],
             compiler_params=PARAMS,
             name="partial_sums",
-        )(place, near_inv, near, core_flip(near), weights, *tok_parts)
+        )(place, weights, near_dense, gathered)
 
     middle_args = []
     for which, near in enumerate((near_gate, near_up)):

time: 146 us -> 143 us (0.979)
  waiting for transfers between devices: 60.3 us -> 50.5 us
  Pallas kernels: 40.7 us -> 46.5 us
  local copies, waits for them, and re-layouts: 4.37 us -> 6.33 us
    ppermute x18 -> x15, waiting for transfers between devices: 58.8 us -> 48.9 us  [owner_flip(): return lax.ppermute(value, 'fsdp', [(i, i ^ bits) for i in range(8)])]
    ppermute x18 -> x15, starting transfers between devices: 33.8 us -> 27.9 us  [owner_flip(): return lax.ppermute(value, 'fsdp', [(i, i ^ bits) for i in range(8)])]
    pallas_call x2 -> x4, Pallas kernels: 17.8 us -> 23.6 us  [the longest x2 13 us: near_weights(): pl.pallas_call(functools.partial(near_kernel, which), out_shape=jax.Shape...]
    all_to_all x0 -> x1, starting transfers between devices: none -> 5.01 us  [pair_split(): lax.all_to_all(by_zone, 'fsdp', split_axis=0, concat_axis=0, tiled=True,...]
    unnamed x48 -> x46, local copies, waits for them, and re-layouts: 1.47 us -> 4.03 us
  transfers between devices with their start and end apart: 24 -> 22, of which waited for: 11 -> 11; matrix products, arithmetic and copies ran while one was open for 2% -> 2% of each run, Pallas kernels for 22% -> 27%
where the time goes in v2:
time: 143 us; the launch traced here: 142 us
  waiting for transfers between devices  50.5 us (35%)
  Pallas kernels  46.5 us (33%)
  starting transfers between devices  34.9 us (24%)
  local copies, waits for them, and re-layouts  6.33 us (4%)
  other arithmetic  3.93 us (3%)
    ppermute x15, waiting for transfers between devices, owner_flip(): return lax.ppermute(value, 'fsdp', [(i, i ^ bits) for i in range(8)])  48.9 us
    ppermute x15, starting transfers between devices, owner_flip(): return lax.ppermute(value, 'fsdp', [(i, i ^ bits) for i in range(8)])  27.9 us
    pallas_call x1, Pallas kernels, pair_split(): pl.pallas_call(own_kernel, out_shape=(jax.ShapeDtypeStruct((8, 1024, 256)...  14.2 us
    pallas_call x2, Pallas kernels, near_weights(): pl.pallas_call(functools.partial(near_kernel, which), out_shape=jax.Shape...  13 us
    pallas_call x2, Pallas kernels, partial_sums(): pl.pallas_call(partial_kernel, out_shape=(jax.ShapeDtypeStruct((64, 1024)...  10.6 us
    all_to_all x1, starting transfers between devices, pair_split(): lax.all_to_all(by_zone, 'fsdp', split_axis=0, concat_axis=0, tiled=True,...  5.01 us
    pallas_call x1, Pallas kernels, pair_split(): pl.pallas_call(middle_kernel, out_shape=jax.ShapeDtypeStruct((P_SIZE, 204...  4.4 us
    pallas_call x1, Pallas kernels, pair_split(): pl.pallas_call(product_kernel, out_shape=jax.ShapeDtypeStruct((P_SIZE, 10...  4.31 us
  transfers between devices with their start and end apart: 22, of which 11 were waited for; matrix products, arithmetic and copies ran while one was open for 2% of the time, Pallas kernels for 27%

profile of v2, /device:TPU:0, one launch (start us, length us, event | category | flops | bytes accessed | tf_op | source)
XLA Modules:
  0.0 142.3 jit_solution(7957243051607503139)
XLA Ops:
  0.0 1.2 constant_dynamic-slice_fusion.1
  1.2 3.0 %collective-permute-start.1 = (bf16[80,4096]{1,0:T(8,128)(2,1)S(1)}, bf16[80,4096]{1,0:T(8,128)(2,1)}, u32[]{:S(2)}, u32[]{:S(2)}) collective-permute-start(bf16[80,4096]{1,0:T(8,128)(2,1)S(1)} %constant_dynamic-slice_fusion.1), channel_id=1, source_target_pairs={{0,2},{2,0},{4,6},{6,4},{8,10},{10,8},{12,14},{14,12},{1,3},{3,1},... | collective-permute-start | bytes 1966088 | tf_op jit(solution)/shard_map/ppermute | solution.py:380
  5.3 5.0 %all-to-all-start = ((bf16[4,64,2048]{2,1,0:T(8,128)(2,1)}), bf16[4,64,2048]{2,1,0:T(8,128)(2,1)S(1)}, u32[]{:S(2)}, u32[]{:S(2)}) async-start(bf16[4,64,2048]{2,1,0:T(8,128)(2,1)} %bitcast.13), calls=%async_computation | async-start | bytes 2097152 | tf_op jit(solution)/shard_map/all_to_all | solution.py:391
  10.9 8.9 %collective-permute-done.1.first_ref = bf16[80,4096]{1,0:T(8,128)(2,1)} collective-permute-done((bf16[80,4096]{1,0:T(8,128)(2,1)S(1)}, bf16[80,4096]{1,0:T(8,128)(2,1)}, u32[]{:S(2)}, u32[]{:S(2)}) %collective-permute-start.1) | collective-permute-done | bytes 655392 | tf_op jit(solution)/shard_map/ppermute | solution.py:380
  19.9 13.1 %collective-permute-done.6.first_ref = bf16[80,4096]{1,0:T(8,128)(2,1)S(1)} collective-permute-done((bf16[80,4096]{1,0:T(8,128)(2,1)S(1)}, bf16[80,4096]{1,0:T(8,128)(2,1)S(1)}, u32[]{:S(2)}, u32[]{:S(2)}) %collective-permute-start.6) | collective-permute-done | bytes 655392 | tf_op jit(solution)/shard_map/ppermute | solution.py:380
  34.4 14.2 %own_blocks.1 = (bf16[8,1024,256]{2,1,0:T(8,128)(2,1)}, f32[64,256]{1,0:T(8,128)}) custom-call(s32[4]{0:T(128)} %pad_add_fusion.1.place_ref, s32[3,256]{1,0:T(4,128)} %select_reduce_fusion.inv_ref, bf16[160,4096]{1,0:T(8,128)(2,1)} %gate_ref.1, bf16[160,4096]{1,0:T(8,128)(2,1)} %up_ref.1, bf16[160,4096]{1,0:T(8,128)(2,1)} %down_ref.1, ...), custom_call_target="tpu_custom_call" | custom-call | tf_op jit(solution)/shard_map/own_blocks/pallas_call | solution.py:404
  48.6 1.7 %collective-permute-start.11 = (f32[64,256]{1,0:T(8,128)}, f32[64,256]{1,0:T(8,128)S(1)}, u32[]{:S(2)}, u32[]{:S(2)}) collective-permute-start(f32[64,256]{1,0:T(8,128)} %get-tuple-element.24), channel_id=1, source_target_pairs={{0,2},{2,0},{4,6},{6,4},{8,10},{10,8},{12,14},{14,12},{1,3},{3,1},... | collective-permute-start | bytes 196616 | tf_op jit(solution)/shard_map/ppermute | solution.py:380
  50.3 2.9 %collective-permute-done.11 = f32[64,256]{1,0:T(8,128)S(1)} collective-permute-done((f32[64,256]{1,0:T(8,128)}, f32[64,256]{1,0:T(8,128)S(1)}, u32[]{:S(2)}, u32[]{:S(2)}) %collective-permute-start.11) | collective-permute-done | bytes 65568 | tf_op jit(solution)/shard_map/ppermute | solution.py:380
  54.1 1.9 %collective-permute-start.12 = (f32[64,256]{1,0:T(8,128)S(1)}, f32[64,256]{1,0:T(8,128)S(1)}, u32[]{:S(2)}, u32[]{:S(2)}) collective-permute-start(f32[64,256]{1,0:T(8,128)S(1)} %add.35), channel_id=1, source_target_pairs={{0,4},{2,6},{4,0},{6,2},{8,12},{10,14},{12,8},{14,10},{1,5},{3,7},... | collective-permute-start | bytes 196616 | tf_op jit(solution)/shard_map/ppermute | solution.py:380
  56.0 1.5 %collective-permute-start = (s32[3,256]{1,0:T(4,128)S(1)}, s32[3,256]{1,0:T(4,128)S(1)}, u32[]{:S(2)}, u32[]{:S(2)}) collective-permute-start(s32[3,256]{1,0:T(4,128)S(1)} %copy-done.17), channel_id=1, source_target_pairs={{0,2},{2,0},{4,6},{6,4},{8,10},{10,8},{12,14},{14,12},{1,3},{3,1},... | collective-permute-start | bytes 9224 | tf_op jit(solution)/shard_map/ppermute | solution.py:380
  58.4 2.9 %collective-permute-start.13 = (f32[64,256]{1,0:T(8,128)S(1)}, f32[64,256]{1,0:T(8,128)S(1)}, u32[]{:S(2)}, u32[]{:S(2)}) collective-permute-start(f32[64,256]{1,0:T(8,128)S(1)} %add.36), channel_id=1, source_target_pairs={{0,8},{2,10},{4,12},{6,14},{8,0},{10,2},{12,4},{14,6},{1,9},{3,11}... | collective-permute-start | bytes 196616 | tf_op jit(solution)/shard_map/ppermute | solution.py:380
  62.8 6.5 %near_blocks.2.weight_ref = bf16[4,1024,256]{2,1,0:T(8,128)(2,1)} custom-call(s32[4]{0:T(128)} %pad_add_fusion.1.place_ref, s32[3,256]{1,0:T(4,128)} %copy-done.16, bf16[80,4096]{1,0:T(8,128)(2,1)} %collective-permute-done.1.first_ref, bf16[80,4096]{1,0:T(8,128)(2,1)} %copy-done.5), custom_call_target="tpu_custom_call" | custom-call | tf_op jit(solution)/shard_map/near_blocks/pallas_call | solution.py:432
  70.2 5.3 %partial_sums.2 = (f32[64,1024]{1,0:T(8,128)}, bf16[64,1024]{1,0:T(8,128)(2,1)}, bf16[64,1024]{1,0:T(8,128)(2,1)}, bf16[64,1024]{1,0:T(8,128)(2,1)}) custom-call(s32[4]{0:T(128)} %pad_add_fusion.1.place_ref, bf16[8,1024,256]{2,1,0:T(8,128)(2,1)} %get-tuple-element.15.own_weight_ref.weight_ref, bf16[4,1024,256]{2,1,0:T(8,128)(2,1)} %near_blocks.2.weight_ref, ...), custom_call_target="tpu_custom_call" | custom-call | tf_op jit(solution)/shard_map/partial_sums/pallas_call | solution.py:444
  75.5 1.6 %collective-permute-start.3 = (bf16[64,1024]{1,0:T(8,128)(2,1)}, bf16[64,1024]{1,0:T(8,128)(2,1)S(1)}, u32[]{:S(2)}, u32[]{:S(2)}) collective-permute-start(bf16[64,1024]{1,0:T(8,128)(2,1)} %get-tuple-element.17), channel_id=1, source_target_pairs={{0,4},{2,6},{4,0},{6,2},{8,12},{10,14},{12,8},{14,10},{1,5},{3,7},... | collective-permute-start | bytes 393224 | tf_op jit(solution)/shard_map/ppermute | solution.py:380
  77.2 1.6 %collective-permute-start.15 = (f32[64,256]{1,0:T(8,128)S(1)}, f32[64,256]{1,0:T(8,128)S(1)}, u32[]{:S(2)}, u32[]{:S(2)}) collective-permute-start(f32[64,256]{1,0:T(8,128)S(1)} %add.37.pay0_ref), channel_id=1, source_target_pairs={{0,16},{16,0},{1,17},{17,1},{2,18},{18,2},{3,19},{19,3},{4,20},{20... | collective-permute-start | bytes 196616 | tf_op jit(solution)/shard_map/ppermute | solution.py:427
  80.0 6.5 %near_blocks.3.weight_ref = bf16[4,1024,256]{2,1,0:T(8,128)(2,1)} custom-call(s32[4]{0:T(128)} %pad_add_fusion.1.place_ref, s32[3,256]{1,0:T(4,128)} %copy-done.16, bf16[80,4096]{1,0:T(8,128)(2,1)} %copy-done.3, bf16[80,4096]{1,0:T(8,128)(2,1)} %copy-done.4), custom_call_target="tpu_custom_call" | custom-call | tf_op jit(solution)/shard_map/near_blocks/pallas_call | solution.py:432
  86.9 5.3 %partial_sums.3 = (f32[64,1024]{1,0:T(8,128)}, bf16[64,1024]{1,0:T(8,128)(2,1)}, bf16[64,1024]{1,0:T(8,128)(2,1)}, bf16[64,1024]{1,0:T(8,128)(2,1)}) custom-call(s32[4]{0:T(128)} %pad_add_fusion.1.place_ref, bf16[8,1024,256]{2,1,0:T(8,128)(2,1)} %get-tuple-element.15.own_weight_ref.weight_ref, bf16[4,1024,256]{2,1,0:T(8,128)(2,1)} %near_blocks.3.weight_ref, ...), custom_call_target="tpu_custom_call" | custom-call | tf_op jit(solution)/shard_map/partial_sums/pallas_call | solution.py:444
  92.2 2.5 %collective-permute-start.5 = (bf16[64,1024]{1,0:T(8,128)(2,1)S(1)}, bf16[64,1024]{1,0:T(8,128)(2,1)S(1)}, u32[]{:S(2)}, u32[]{:S(2)}) collective-permute-start(bf16[64,1024]{1,0:T(8,128)(2,1)S(1)} %copy-done.21), channel_id=1, source_target_pairs={{0,12},{2,14},{4,8},{6,10},{8,4},{10,6},{12,0},{14,2},{1,13},{3,15... | collective-permute-start | bytes 393224 | tf_op jit(solution)/shard_map/ppermute | solution.py:380
  95.5 1.2 collective-permute-start.9
  96.7 2.5 %collective-permute-start.10 = (bf16[64,1024]{1,0:T(8,128)(2,1)}, bf16[64,1024]{1,0:T(8,128)(2,1)S(1)}, u32[]{:S(2)}, u32[]{:S(2)}) collective-permute-start(bf16[64,1024]{1,0:T(8,128)(2,1)} %get-tuple-element.23), channel_id=1, source_target_pairs={{0,12},{2,14},{4,8},{6,10},{8,4},{10,6},{12,0},{14,2},{1,13},{3,15... | collective-permute-start | bytes 393224 | tf_op jit(solution)/shard_map/ppermute | solution.py:380
  99.2 1.3 collective-permute-done.5.gate3_ref
  100.5 3.1 %collective-permute-done.8.up1_ref = bf16[64,1024]{1,0:T(8,128)(2,1)S(1)} collective-permute-done((bf16[64,1024]{1,0:T(8,128)(2,1)}, bf16[64,1024]{1,0:T(8,128)(2,1)S(1)}, u32[]{:S(2)}, u32[]{:S(2)}) %collective-permute-start.8) | collective-permute-done | bytes 131104 | tf_op jit(solution)/shard_map/ppermute | solution.py:380
  103.5 7.0 %collective-permute-done.9.up2_ref = bf16[64,1024]{1,0:T(8,128)(2,1)S(1)} collective-permute-done((bf16[64,1024]{1,0:T(8,128)(2,1)}, bf16[64,1024]{1,0:T(8,128)(2,1)S(1)}, u32[]{:S(2)}, u32[]{:S(2)}) %collective-permute-start.9) | collective-permute-done | bytes 131104 | tf_op jit(solution)/shard_map/ppermute | solution.py:380
  111.2 4.4 %token_sums.1 = f32[16,2048]{1,0:T(8,128)} custom-call(s32[4]{0:T(128)} %pad_add_fusion.1.place_ref, f32[64,1024]{1,0:T(8,128)} %get-tuple-element.16.gate0_ref, bf16[64,1024]{1,0:T(8,128)(2,1)} %copy-done.7, bf16[64,1024]{1,0:T(8,128)(2,1)} %copy-done.8, bf16[64,1024]{1,0:T(8,128)(2,1)} %copy-done.9, f32[64,1024]{1,0:T(8,128)} %get-tuple-element.20.up0_ref, ...), custom_call_target="tpu_custom_call" | custom-call | tf_op jit(solution)/shard_map/token_sums/pallas_call | solution.py:465
  115.7 1.6 %collective-permute-done.17 = f32[16,2048]{1,0:T(8,128)S(1)} collective-permute-done((f32[16,2048]{1,0:T(8,128)}, f32[16,2048]{1,0:T(8,128)S(1)}, u32[]{:S(2)}, u32[]{:S(2)}) %collective-permute-start.17) | collective-permute-done | bytes 131104 | tf_op jit(solution)/shard_map/ppermute | solution.py:383
  118.1 1.6 %collective-permute-start.18 = (f32[16,2048]{1,0:T(8,128)S(1)}, f32[16,2048]{1,0:T(8,128)S(1)}, u32[]{:S(2)}, u32[]{:S(2)}) collective-permute-start(f32[16,2048]{1,0:T(8,128)S(1)} %add.38), channel_id=1, source_target_pairs={{0,2},{2,0},{4,6},{6,4},{8,10},{10,8},{12,14},{14,12},{1,3},{3,1},... | collective-permute-start | bytes 393224 | tf_op jit(solution)/shard_map/ppermute | solution.py:380
  119.7 4.0 %collective-permute-done.18 = f32[16,2048]{1,0:T(8,128)S(1)} collective-permute-done((f32[16,2048]{1,0:T(8,128)S(1)}, f32[16,2048]{1,0:T(8,128)S(1)}, u32[]{:S(2)}, u32[]{:S(2)}) %collective-permute-start.18) | collective-permute-done | bytes 131104 | tf_op jit(solution)/shard_map/ppermute | solution.py:380
  123.8 2.8 %collective-permute-start.19 = (f32[16,2048]{1,0:T(8,128)S(1)}, f32[16,2048]{1,0:T(8,128)S(1)}, u32[]{:S(2)}, u32[]{:S(2)}) collective-permute-start(f32[16,2048]{1,0:T(8,128)S(1)} %add.39), channel_id=1, source_target_pairs={{0,4},{2,6},{4,0},{6,2},{8,12},{10,14},{12,8},{14,10},{1,5},{3,7},... | collective-permute-start | bytes 393224 | tf_op jit(solution)/shard_map/ppermute | solution.py:380
  126.5 3.0 %collective-permute-done.19 = f32[16,2048]{1,0:T(8,128)S(1)} collective-permute-done((f32[16,2048]{1,0:T(8,128)S(1)}, f32[16,2048]{1,0:T(8,128)S(1)}, u32[]{:S(2)}, u32[]{:S(2)}) %collective-permute-start.19) | collective-permute-done | bytes 131104 | tf_op jit(solution)/shard_map/ppermute | solution.py:380
  129.5 3.2 %collective-permute-start.20 = (f32[16,2048]{1,0:T(8,128)S(1)}, f32[16,2048]{1,0:T(8,128)S(1)}, u32[]{:S(2)}, u32[]{:S(2)}) collective-permute-start(f32[16,2048]{1,0:T(8,128)S(1)} %add.40), channel_id=1, source_target_pairs={{0,8},{2,10},{4,12},{6,14},{8,0},{10,2},{12,4},{14,6},{1,9},{3,11}... | collective-permute-start | bytes 393224 | tf_op jit(solution)/shard_map/ppermute | solution.py:380
  132.7 4.6 %collective-permute-done.20 = f32[16,2048]{1,0:T(8,128)S(1)} collective-permute-done((f32[16,2048]{1,0:T(8,128)S(1)}, f32[16,2048]{1,0:T(8,128)S(1)}, u32[]{:S(2)}, u32[]{:S(2)}) %collective-permute-start.20) | collective-permute-done | bytes 131104 | tf_op jit(solution)/shard_map/ppermute | solution.py:380
  138.0 4.3 %products.1 = f32[16,1024]{1,0:T(8,128)} custom-call(f32[16,2048]{1,0:T(8,128)} %add.41.sum_ref, bf16[8,1024,256]{2,1,0:T(8,128)(2,1)} %get-tuple-element.15.own_weight_ref.weight_ref), custom_call_target="tpu_custom_call" | custom-call | tf_op jit(solution)/shard_map/products/pallas_call | solution.py:485
  (78 shorter events, 12.0 us)
Async XLA Ops:
  1.2 18.7 %collective-permute-start.1 = (bf16[80,4096]{1,0:T(8,128)(2,1)S(1)}, bf16[80,4096]{1,0:T(8,128)(2,1)}, u32[]{:S(2)}, u32[]{:S(2)}) collective-permute-start(bf16[80,4096]{1,0:T(8,128)(2,1)S(1)} %constant_dynamic-slice_fusion.1), channel_id=1, source_target_pairs={{0,2},{2,0},{4,6},{6,4},{8,10},{10,8},{12,14},{14,12},{1,3},{3,1},... | collective-permute-start | bytes 1966088 | tf_op jit(solution)/shard_map/ppermute | solution.py:380
  5.3 28.4 %copy-start.18 = (s32[160]{0:T(256)S(1)}, s32[160]{0:T(256)}, u32[]{:S(2)}) copy-start(s32[160]{0:T(256)} %param.16) | copy-start | bytes 1924
  5.3 28.4 %copy-start.19 = (s32[160]{0:T(256)S(1)}, s32[160]{0:T(256)}, u32[]{:S(2)}) copy-start(s32[160]{0:T(256)} %param.14) | copy-start | bytes 1924
  5.3 28.4 %copy-start.20 = (s32[160]{0:T(256)S(1)}, s32[160]{0:T(256)}, u32[]{:S(2)}) copy-start(s32[160]{0:T(256)} %param.12) | copy-start | bytes 1924
  5.3 64.0 %all-to-all-start = ((bf16[4,64,2048]{2,1,0:T(8,128)(2,1)}), bf16[4,64,2048]{2,1,0:T(8,128)(2,1)S(1)}, u32[]{:S(2)}, u32[]{:S(2)}) async-start(bf16[4,64,2048]{2,1,0:T(8,128)(2,1)} %bitcast.13), calls=%async_computation | async-start | bytes 2097152 | tf_op jit(solution)/shard_map/all_to_all | solution.py:391
  10.3 22.7 %collective-permute-start.6 = (bf16[80,4096]{1,0:T(8,128)(2,1)S(1)}, bf16[80,4096]{1,0:T(8,128)(2,1)S(1)}, u32[]{:S(2)}, u32[]{:S(2)}) collective-permute-start(bf16[80,4096]{1,0:T(8,128)(2,1)S(1)} %constant_dynamic-slice_fusion), channel_id=1, source_target_pairs={{0,2},{2,0},{4,6},{6,4},{8,10},{10,8},{12,14},{14,12},{1,3},{3,1},... | collective-permute-start | bytes 1966088 | tf_op jit(solution)/shard_map/ppermute | solution.py:380
  19.9 41.4 %collective-permute-start.2 = (bf16[80,4096]{1,0:T(8,128)(2,1)}, bf16[80,4096]{1,0:T(8,128)(2,1)S(1)}, u32[]{:S(2)}, u32[]{:S(2)}) collective-permute-start(bf16[80,4096]{1,0:T(8,128)(2,1)} %collective-permute-done.1.first_ref), channel_id=1, source_target_pairs={{0,1},{1,0},{2,3},{3,2},{4,5},{5,4},{6,7},{7,6},{8,9},{9,8},{10,11... | collective-permute-start | bytes 1966088 | tf_op jit(solution)/shard_map/ppermute | solution.py:383
  33.0 15.6 %copy-start.3 = (bf16[80,4096]{1,0:T(8,128)(2,1)}, bf16[80,4096]{1,0:T(8,128)(2,1)S(1)}, u32[]{:S(2)}) copy-start(bf16[80,4096]{1,0:T(8,128)(2,1)S(1)} %collective-permute-done.6.first_ref) | copy-start | bytes 1966084
  33.0 46.1 %collective-permute-start.7 = (bf16[80,4096]{1,0:T(8,128)(2,1)S(1)}, bf16[80,4096]{1,0:T(8,128)(2,1)S(1)}, u32[]{:S(2)}, u32[]{:S(2)}) collective-permute-start(bf16[80,4096]{1,0:T(8,128)(2,1)S(1)} %collective-permute-done.6.first_ref), channel_id=1, source_target_pairs={{0,1},{1,0},{2,3},{3,2},{4,5},{5,4},{6,7},{7,6},{8,9},{9,8},{10,11... | collective-permute-start | bytes 1966088 | tf_op jit(solution)/shard_map/ppermute | solution.py:383
  34.4 21.5 %copy-start.17 = (s32[3,256]{1,0:T(4,128)S(1)}, s32[3,256]{1,0:T(4,128)}, u32[]{:S(2)}) copy-start(s32[3,256]{1,0:T(4,128)} %select_reduce_fusion.inv_ref) | copy-start | bytes 9220
  48.6 4.6 %collective-permute-start.11 = (f32[64,256]{1,0:T(8,128)}, f32[64,256]{1,0:T(8,128)S(1)}, u32[]{:S(2)}, u32[]{:S(2)}) collective-permute-start(f32[64,256]{1,0:T(8,128)} %get-tuple-element.24), channel_id=1, source_target_pairs={{0,2},{2,0},{4,6},{6,4},{8,10},{10,8},{12,14},{14,12},{1,3},{3,1},... | collective-permute-start | bytes 196616 | tf_op jit(solution)/shard_map/ppermute | solution.py:380
  54.1 4.3 %collective-permute-start.12 = (f32[64,256]{1,0:T(8,128)S(1)}, f32[64,256]{1,0:T(8,128)S(1)}, u32[]{:S(2)}, u32[]{:S(2)}) collective-permute-start(f32[64,256]{1,0:T(8,128)S(1)} %add.35), channel_id=1, source_target_pairs={{0,4},{2,6},{4,0},{6,2},{8,12},{10,14},{12,8},{14,10},{1,5},{3,7},... | collective-permute-start | bytes 196616 | tf_op jit(solution)/shard_map/ppermute | solution.py:380
  56.0 5.4 %collective-permute-start = (s32[3,256]{1,0:T(4,128)S(1)}, s32[3,256]{1,0:T(4,128)S(1)}, u32[]{:S(2)}, u32[]{:S(2)}) collective-permute-start(s32[3,256]{1,0:T(4,128)S(1)} %copy-done.17), channel_id=1, source_target_pairs={{0,2},{2,0},{4,6},{6,4},{8,10},{10,8},{12,14},{14,12},{1,3},{3,1},... | collective-permute-start | bytes 9224 | tf_op jit(solution)/shard_map/ppermute | solution.py:380
  58.4 18.7 %collective-permute-start.13 = (f32[64,256]{1,0:T(8,128)S(1)}, f32[64,256]{1,0:T(8,128)S(1)}, u32[]{:S(2)}, u32[]{:S(2)}) collective-permute-start(f32[64,256]{1,0:T(8,128)S(1)} %add.36), channel_id=1, source_target_pairs={{0,8},{2,10},{4,12},{6,14},{8,0},{10,2},{12,4},{14,6},{1,9},{3,11}... | collective-permute-start | bytes 196616 | tf_op jit(solution)/shard_map/ppermute | solution.py:380
  75.5 21.2 %collective-permute-start.3 = (bf16[64,1024]{1,0:T(8,128)(2,1)}, bf16[64,1024]{1,0:T(8,128)(2,1)S(1)}, u32[]{:S(2)}, u32[]{:S(2)}) collective-permute-start(bf16[64,1024]{1,0:T(8,128)(2,1)} %get-tuple-element.17), channel_id=1, source_target_pairs={{0,4},{2,6},{4,0},{6,2},{8,12},{10,14},{12,8},{14,10},{1,5},{3,7},... | collective-permute-start | bytes 393224 | tf_op jit(solution)/shard_map/ppermute | solution.py:380
  77.1 15.1 %copy-start.6 = (f32[64,256]{1,0:T(8,128)}, f32[64,256]{1,0:T(8,128)S(1)}, u32[]{:S(2)}) copy-start(f32[64,256]{1,0:T(8,128)S(1)} %add.37.pay0_ref) | copy-start | bytes 196612
  77.1 15.1 %collective-permute-start.14 = (f32[64,256]{1,0:T(8,128)S(1)}, f32[64,256]{1,0:T(8,128)S(1)}, u32[]{:S(2)}, u32[]{:S(2)}) collective-permute-start(f32[64,256]{1,0:T(8,128)S(1)} %add.37.pay0_ref), channel_id=1, source_target_pairs={{0,1},{1,0},{2,3},{3,2},{4,5},{5,4},{6,7},{7,6},{8,9},{9,8},{10,11... | collective-permute-start | bytes 196616 | tf_op jit(solution)/shard_map/ppermute | solution.py:383
  77.2 17.6 %collective-permute-start.15 = (f32[64,256]{1,0:T(8,128)S(1)}, f32[64,256]{1,0:T(8,128)S(1)}, u32[]{:S(2)}, u32[]{:S(2)}) collective-permute-start(f32[64,256]{1,0:T(8,128)S(1)} %add.37.pay0_ref), channel_id=1, source_target_pairs={{0,16},{16,0},{1,17},{17,1},{2,18},{18,2},{3,19},{19,3},{4,20},{20... | collective-permute-start | bytes 196616 | tf_op jit(solution)/shard_map/ppermute | solution.py:427
  78.8 16.7 %collective-permute-start.16 = (f32[64,256]{1,0:T(8,128)S(1)}, f32[64,256]{1,0:T(8,128)S(1)}, u32[]{:S(2)}, u32[]{:S(2)}) collective-permute-start(f32[64,256]{1,0:T(8,128)S(1)} %add.37.pay0_ref), channel_id=1, source_target_pairs={{0,17},{1,16},{16,1},{17,0},{2,19},{3,18},{18,3},{19,2},{4,21},{5,... | collective-permute-start | bytes 196616 | tf_op jit(solution)/shard_map/ppermute | solution.py:428
  86.5 12.6 %collective-permute-start.4 = (bf16[64,1024]{1,0:T(8,128)(2,1)S(1)}, bf16[64,1024]{1,0:T(8,128)(2,1)S(1)}, u32[]{:S(2)}, u32[]{:S(2)}) collective-permute-start(bf16[64,1024]{1,0:T(8,128)(2,1)S(1)} %copy-done.22), channel_id=1, source_target_pairs={{0,8},{2,10},{4,12},{6,14},{8,0},{10,2},{12,4},{14,6},{1,9},{3,11}... | collective-permute-start | bytes 393224 | tf_op jit(solution)/shard_map/ppermute | solution.py:380
  92.2 18.3 %copy-start.13 = (f32[64,256]{1,0:T(8,128)}, f32[64,256]{1,0:T(8,128)S(1)}, u32[]{:S(2)}) copy-start(f32[64,256]{1,0:T(8,128)S(1)} %collective-permute-done.14.pay1_ref) | copy-start | bytes 196612
  92.2 8.3 %collective-permute-start.5 = (bf16[64,1024]{1,0:T(8,128)(2,1)S(1)}, bf16[64,1024]{1,0:T(8,128)(2,1)S(1)}, u32[]{:S(2)}, u32[]{:S(2)}) collective-permute-start(bf16[64,1024]{1,0:T(8,128)(2,1)S(1)} %copy-done.21), channel_id=1, source_target_pairs={{0,12},{2,14},{4,8},{6,10},{8,4},{10,6},{12,0},{14,2},{1,13},{3,15... | collective-permute-start | bytes 393224 | tf_op jit(solution)/shard_map/ppermute | solution.py:380
  94.8 15.8 %copy-start.14 = (f32[64,256]{1,0:T(8,128)}, f32[64,256]{1,0:T(8,128)S(1)}, u32[]{:S(2)}) copy-start(f32[64,256]{1,0:T(8,128)S(1)} %collective-permute-done.15.pay2_ref) | copy-start | bytes 196612
  94.8 8.8 %collective-permute-start.8 = (bf16[64,1024]{1,0:T(8,128)(2,1)}, bf16[64,1024]{1,0:T(8,128)(2,1)S(1)}, u32[]{:S(2)}, u32[]{:S(2)}) collective-permute-start(bf16[64,1024]{1,0:T(8,128)(2,1)} %get-tuple-element.21), channel_id=1, source_target_pairs={{0,4},{2,6},{4,0},{6,2},{8,12},{10,14},{12,8},{14,10},{1,5},{3,7},... | collective-permute-start | bytes 393224 | tf_op jit(solution)/shard_map/ppermute | solution.py:380
  95.5 15.1 %copy-start.15 = (f32[64,256]{1,0:T(8,128)}, f32[64,256]{1,0:T(8,128)S(1)}, u32[]{:S(2)}) copy-start(f32[64,256]{1,0:T(8,128)S(1)} %collective-permute-done.16.pay3_ref) | copy-start | bytes 196612
  95.5 15.1 %collective-permute-start.9 = (bf16[64,1024]{1,0:T(8,128)(2,1)}, bf16[64,1024]{1,0:T(8,128)(2,1)S(1)}, u32[]{:S(2)}, u32[]{:S(2)}) collective-permute-start(bf16[64,1024]{1,0:T(8,128)(2,1)} %get-tuple-element.22), channel_id=1, source_target_pairs={{0,8},{2,10},{4,12},{6,14},{8,0},{10,2},{12,4},{14,6},{1,9},{3,11}... | collective-permute-start | bytes 393224 | tf_op jit(solution)/shard_map/ppermute | solution.py:380
  96.7 13.9 %copy-start.7 = (bf16[64,1024]{1,0:T(8,128)(2,1)}, bf16[64,1024]{1,0:T(8,128)(2,1)S(1)}, u32[]{:S(2)}) copy-start(bf16[64,1024]{1,0:T(8,128)(2,1)S(1)} %collective-permute-done.3.gate1_ref) | copy-start | bytes 393220
  96.7 13.8 %collective-permute-start.10 = (bf16[64,1024]{1,0:T(8,128)(2,1)}, bf16[64,1024]{1,0:T(8,128)(2,1)S(1)}, u32[]{:S(2)}, u32[]{:S(2)}) collective-permute-start(bf16[64,1024]{1,0:T(8,128)(2,1)} %get-tuple-element.23), channel_id=1, source_target_pairs={{0,12},{2,14},{4,8},{6,10},{8,4},{10,6},{12,0},{14,2},{1,13},{3,15... | collective-permute-start | bytes 393224 | tf_op jit(solution)/shard_map/ppermute | solution.py:380
  115.7 1.6 %collective-permute-start.17 = (f32[16,2048]{1,0:T(8,128)}, f32[16,2048]{1,0:T(8,128)S(1)}, u32[]{:S(2)}, u32[]{:S(2)}) collective-permute-start(f32[16,2048]{1,0:T(8,128)} %token_sums.1), channel_id=1, source_target_pairs={{0,1},{1,0},{2,3},{3,2},{4,5},{5,4},{6,7},{7,6},{8,9},{9,8},{10,11... | collective-permute-start | bytes 393224 | tf_op jit(solution)/shard_map/ppermute | solution.py:383
  118.1 5.6 %collective-permute-start.18 = (f32[16,2048]{1,0:T(8,128)S(1)}, f32[16,2048]{1,0:T(8,128)S(1)}, u32[]{:S(2)}, u32[]{:S(2)}) collective-permute-start(f32[16,2048]{1,0:T(8,128)S(1)} %add.38), channel_id=1, source_target_pairs={{0,2},{2,0},{4,6},{6,4},{8,10},{10,8},{12,14},{14,12},{1,3},{3,1},... | collective-permute-start | bytes 393224 | tf_op jit(solution)/shard_map/ppermute | solution.py:380
  123.8 5.7 %collective-permute-start.19 = (f32[16,2048]{1,0:T(8,128)S(1)}, f32[16,2048]{1,0:T(8,128)S(1)}, u32[]{:S(2)}, u32[]{:S(2)}) collective-permute-start(f32[16,2048]{1,0:T(8,128)S(1)} %add.39), channel_id=1, source_target_pairs={{0,4},{2,6},{4,0},{6,2},{8,12},{10,14},{12,8},{14,10},{1,5},{3,7},... | collective-permute-start | bytes 393224 | tf_op jit(solution)/shard_map/ppermute | solution.py:380
  129.5 7.8 %collective-permute-start.20 = (f32[16,2048]{1,0:T(8,128)S(1)}, f32[16,2048]{1,0:T(8,128)S(1)}, u32[]{:S(2)}, u32[]{:S(2)}) collective-permute-start(f32[16,2048]{1,0:T(8,128)S(1)} %add.40), channel_id=1, source_target_pairs={{0,8},{2,10},{4,12},{6,14},{8,0},{10,2},{12,4},{14,6},{1,9},{3,11}... | collective-permute-start | bytes 393224 | tf_op jit(solution)/shard_map/ppermute | solution.py:380
  (13 other events, 57.6 us)

commit v3 on v2

--- a/solution.py
+++ b/solution.py
@@ -17,7 +17,11 @@
 VMEM = pl.BlockSpec(memory_space=pltpu.VMEM)
 SMEM = pl.BlockSpec(memory_space=pltpu.SMEM)
 
-PARAMS = pltpu.CompilerParams(vmem_limit_bytes=56 * 1024 * 1024)
+STRIDE = 168
+
+
+def params(mebibytes):
+    return pltpu.CompilerParams(vmem_limit_bytes=mebibytes * 1024 * 1024)
 
 
 def unpack(blocks, slot_ids, cell_total):
@@ -137,18 +141,25 @@
     @pl.loop(0, blocks_ref.shape[0] // 16)
     def _(step):
         row = pl.multiple_of(step * 16, 16)
-        target = (first_slot + row) * 32
+        target = pl.multiple_of(first_slot + row, 16)
         for chunk in range(32):
             piece = blocks_ref[pl.ds(row, 16), 128 * chunk : 128 * (chunk + 1)].astype(F32)
-            tiles_ref[pl.ds(target + chunk, 16, stride=32), :] = piece
+            tiles_ref[pl.ds(target + chunk * STRIDE, 16), :] = piece
+
+
+def clear_empty_slot(tiles_ref):
+    for chunk in range(32):
+        tiles_ref[pl.ds(chunk * STRIDE + 160, 8), :] = jnp.zeros((8, 128), F32)
 
 
 def assembled_pair(tiles_ref, left_slot, right_slot):
-    left = tiles_ref[pl.ds(pl.multiple_of(left_slot * 32, 32), 32), :]
-    right = tiles_ref[pl.ds(pl.multiple_of(right_slot * 32, 32), 32), :]
+    left = tiles_ref[pl.ds(left_slot, 32, stride=STRIDE), :]
+    right = tiles_ref[pl.ds(right_slot, 32, stride=STRIDE), :]
     low_half = lax.broadcasted_iota(jnp.int32, (32, 128), 1) < BLK
-    even = jnp.where(low_half, left, pltpu.roll(right, BLK, 1))
-    odd = jnp.where(low_half, pltpu.roll(left, BLK, 1), right)
+    straight = jnp.where(low_half, left, right)
+    crossed = pltpu.roll(jnp.where(low_half, right, left), BLK, 1)
+    even = jnp.where(low_half, straight, crossed)
+    odd = jnp.where(low_half, crossed, straight)
     return even.astype(BF), odd.astype(BF)
 
 
@@ -183,7 +194,7 @@
 ):
     owner = place_ref[0]
     quarter = place_ref[1]
-    tiles_ref[pl.ds(160 * 32, 32), :] = jnp.zeros((32, 128), F32)
+    clear_empty_slot(tiles_ref)
 
     for which, blocks_ref in enumerate((gate_ref, up_ref)):
         stage_blocks(blocks_ref, tiles_ref, 0)
@@ -234,37 +245,29 @@
         payload_ref[16 * which : 16 * (which + 1), :] = triple[:16] + triple[16:32] + triple[32:]
 
 
-def near_kernel(inv_row, place_ref, inv_ref, first_ref, second_ref, weight_ref, tiles_ref):
-    core = place_ref[3]
-    tiles_ref[pl.ds(160 * 32, 32), :] = jnp.zeros((32, 128), F32)
-    stage_blocks(first_ref, tiles_ref, core * 80)
-    stage_blocks(second_ref, tiles_ref, (1 - core) * 80)
+def flipped(two_bits, flip):
+    low_bit = lax.rem(two_bits + flip % 2, 2)
+    return low_bit + 2 * lax.rem(two_bits // 2 + flip // 2, 2)
+
+
+def near_kernel(place_ref, inv_ref, blocks_ref, weight_ref, tiles_ref):
+    clear_empty_slot(tiles_ref)
+    stage_blocks(blocks_ref, tiles_ref, 0)
 
     def put(pair, row, piece):
         lane = (pair % 2) * 128
         weight_ref[pair // 2, pl.ds(row, 32), lane : lane + 128] = piece
 
-    assemble_columns(inv_ref, inv_row, tiles_ref, put)
-
-
-def partial_kernel(
-    place_ref,
-    own_weight_ref,
-    weight_ref,
-    tok_ref,
-    keep_ref,
-    out1_ref,
-    out2_ref,
-    out3_ref,
-    tokens_ref,
-):
+    assemble_columns(inv_ref, place_ref[3], tiles_ref, put)
+
+
+def partial_kernel(stacked, place_ref, own_ref, near_ref, tok_ref, keep_ref, *rest):
+    tokens_ref = rest[-1]
     side = place_ref[2]
     zone = place_ref[0] // 2
     shuffle = shuffle_matrix(256)
-    low_bit = lax.rem(zone, 2)
-    high_bit = zone // 2
     for source in range(4):
-        spot = lax.rem(low_bit + source % 2, 2) + 2 * lax.rem(high_bit + source // 2, 2)
+        spot = flipped(zone, source)
         for group in range(8):
             piece = tok_ref[spot, :, 256 * group : 256 * (group + 1)]
             moved = dot(piece, shuffle).astype(BF)
@@ -273,57 +276,55 @@
                 half, 64 * source : 64 * (source + 1), 256 * (group % 4) : 256 * (group % 4 + 1)
             ] = moved
     for chunk in range(4):
-        total = dot(tokens_ref[0], own_weight_ref[chunk]) + dot(tokens_ref[1], weight_ref[chunk])
+        total = dot(tokens_ref[0], own_ref[chunk]) + dot(tokens_ref[1], near_ref[chunk])
         cols = slice(256 * chunk, 256 * (chunk + 1))
         keep_ref[:, cols] = total[:64]
-        out1_ref[:, cols] = total[64:128].astype(BF)
-        out2_ref[:, cols] = total[128:192].astype(BF)
-        out3_ref[:, cols] = total[192:].astype(BF)
+        for flip in range(0 if stacked else 1, 4):
+            sent = total[64 * flip : 64 * (flip + 1)].astype(BF)
+            if stacked:
+                rest[0][flipped(zone, flip), :, cols] = sent
+            else:
+                rest[flip - 1][:, cols] = sent
 
 
 def middle_kernel(
     place_ref,
-    gate0_ref,
-    gate1_ref,
-    gate2_ref,
-    gate3_ref,
-    up0_ref,
-    up1_ref,
-    up2_ref,
-    up3_ref,
+    first_keep_ref,
+    first_ref,
+    second_keep_ref,
+    second1_ref,
+    second2_ref,
+    second3_ref,
     pay0_ref,
     pay1_ref,
     pay2_ref,
     pay3_ref,
-    out_ref,
+    mine_ref,
+    theirs_ref,
     lead_ref,
     act_ref,
     pay_ref,
     proj_ref,
     tangent_ref,
+    rows_ref,
 ):
+    zone = place_ref[0] // 2
     quarter = place_ref[1]
-    low_bit = quarter % 2
-    high_bit = quarter // 2
+    core = place_ref[3]
     unshuffle = unshuffle_matrix(256)
     for flip, ref in enumerate((pay0_ref, pay1_ref, pay2_ref, pay3_ref)):
-        spot = lax.rem(low_bit + flip % 2, 2) + 2 * lax.rem(high_bit + flip // 2, 2)
-        pay_ref[spot] = ref[...]
+        pay_ref[flipped(quarter, flip)] = ref[...]
     for chunk in range(4):
         cols = slice(256 * chunk, 256 * (chunk + 1))
         proj_ref[:, cols] = dot(pay_ref[chunk, 32:64, :].astype(BF), unshuffle).astype(BF)
-        gate_pre = (
-            gate0_ref[:, cols]
-            + gate1_ref[:, cols].astype(F32)
-            + gate2_ref[:, cols].astype(F32)
-            + gate3_ref[:, cols].astype(F32)
-        )
-        up_pre = (
-            up0_ref[:, cols]
-            + up1_ref[:, cols].astype(F32)
-            + up2_ref[:, cols].astype(F32)
-            + up3_ref[:, cols].astype(F32)
-        )
+        first = first_keep_ref[:, cols]
+        for flip in (1, 2, 3):
+            first = first + first_ref[flipped(zone, flip), :, cols].astype(F32)
+        second = second_keep_ref[:, cols]
+        for ref in (second1_ref, second2_ref, second3_ref):
+            second = second + ref[:, cols].astype(F32)
+        gate_pre = jnp.where(core == 0, first, second)
+        up_pre = jnp.where(core == 0, second, first)
         sigmoid_g = jax.nn.sigmoid(gate_pre)
         activated = gate_pre * sigmoid_g
         slope_g = sigmoid_g * (1.0 + gate_pre * (1.0 - sigmoid_g))
@@ -336,16 +337,21 @@
             tangent_ref[64 * probe : 64 * (probe + 1), cols] = (
                 lead * probe_gate + activated * probe_up
             ).astype(BF)
-    sketch_rows = contract_last(tangent_ref[...], proj_ref[...]).astype(BF)
-    for probe in range(P_SIZE):
-        rows = sketch_rows[64 * probe : 64 * (probe + 1), :]
-        backward = dot(rows, proj_ref[...])
-        out_ref[probe : probe + 1, :1024] = jnp.sum(backward * lead_ref[...], axis=0, keepdims=True)
-        out_ref[probe : probe + 1, 1024:] = jnp.sum(backward * act_ref[...], axis=0, keepdims=True)
-
-
-def product_kernel(sum_ref, weight_ref, out_ref):
-    sums = sum_ref[...].astype(BF)
+    rows_ref[...] = contract_last(tangent_ref[...], proj_ref[...]).astype(BF)
+    for step in range(P_SIZE):
+        probe = lax.rem(step + 8 * core, P_SIZE)
+        backward = dot(rows_ref[pl.ds(pl.multiple_of(probe * 64, 64), 64), :], proj_ref[...])
+        target = mine_ref if step < 8 else theirs_ref
+        row = slice(step % 8, step % 8 + 1)
+        target[row, :1024] = jnp.sum(backward * lead_ref[...], axis=0, keepdims=True)
+        target[row, 1024:] = jnp.sum(backward * act_ref[...], axis=0, keepdims=True)
+
+
+def product_kernel(place_ref, mine_ref, theirs_ref, weight_ref, out_ref, sum_ref):
+    core = place_ref[3]
+    sum_ref[core] = mine_ref[...]
+    sum_ref[1 - core] = theirs_ref[...]
+    sums = jnp.concatenate([sum_ref[0], sum_ref[1]], axis=0).astype(BF)
     total = None
     for chunk in range(8):
         term = contract_last(sums[:, 256 * chunk : 256 * (chunk + 1)], weight_ref[chunk])
@@ -372,34 +378,34 @@
     owner = lax.axis_index("fsdp")
     core = lax.axis_index("seq")
     group = lax.axis_index("groups")
-    zone = owner // 2
-    side = owner % 2
-    place = jnp.stack([owner, 2 * group + core, side, core]).astype(jnp.int32)
+    place = jnp.stack([owner, 2 * group + core, owner % 2, core]).astype(jnp.int32)
 
     def owner_flip(value, bits):
         return lax.ppermute(value, "fsdp", [(i, i ^ bits) for i in range(8)])
 
     def core_flip(value):
         return lax.ppermute(value, "seq", [(0, 1), (1, 0)])
+
+    def zone_exchange(value):
+        return lax.all_to_all(
+            value,
+            "fsdp",
+            split_axis=0,
+            concat_axis=0,
+            tiled=True,
+            axis_index_groups=[[0, 2, 4, 6], [1, 3, 5, 7]],
+        )
+
+    by_zone = tokens.reshape(64, 4, 2048).transpose(1, 0, 2)
+    by_zone, gate_source, up_source = lax.optimization_barrier((by_zone, gate_blocks, up_blocks))
+    gathered = core_flip(zone_exchange(by_zone))
+    near = owner_flip(jnp.where(core == 0, gate_source, up_source), 1)
 
     slots = jnp.stack([gate_slot, up_slot, down_slot])
     cells = lax.broadcasted_iota(jnp.int32, (3, 160, 256), 2)
     slot_numbers = lax.broadcasted_iota(jnp.int32, (3, 160, 256), 1)
     inv = jnp.min(jnp.where(slots[:, :, None] == cells, slot_numbers, 160), axis=1)
-
-    by_zone = tokens.reshape(64, 4, 2048).transpose(1, 0, 2)
-    gathered = lax.all_to_all(
-        by_zone,
-        "fsdp",
-        split_axis=0,
-        concat_axis=0,
-        tiled=True,
-        axis_index_groups=[[0, 2, 4, 6], [1, 3, 5, 7]],
-    )
-
     near_inv = owner_flip(inv, 1)
-    near_gate = owner_flip(lax.dynamic_slice(gate_blocks, (core * 80, 0), (80, 4096)), 1)
-    near_up = owner_flip(lax.dynamic_slice(up_blocks, (core * 80, 0), (80, 4096)), 1)
 
     weights, payload = pl.pallas_call(
         own_kernel,
@@ -410,17 +416,18 @@
         in_specs=[SMEM, SMEM] + [VMEM] * 6,
         out_specs=(VMEM, VMEM),
         scratch_shapes=[
-            pltpu.VMEM((161 * 32, 128), F32),
+            pltpu.VMEM((32 * STRIDE, 128), F32),
             pltpu.VMEM((128, 128), F32),
             pltpu.VMEM((48, 1024), BF),
             pltpu.VMEM((256, 1024), BF),
         ],
-        compiler_params=PARAMS,
+        compiler_params=params(20),
         name="own_blocks",
     )(place, inv, gate_blocks, up_blocks, down_blocks, sketch, probe_index, probe_value)
 
     for bits in (1, 2, 4):
         payload = payload + owner_flip(payload, bits)
+    near, near_inv, payload = lax.optimization_barrier((near, near_inv, payload))
     pay_parts = [
         payload,
         core_flip(payload),
@@ -428,68 +435,74 @@
         lax.ppermute(payload, ("groups", "seq"), [(i, i ^ 3) for i in range(4)]),
     ]
 
-    def near_weights(which, near):
+    near_weights = pl.pallas_call(
+        near_kernel,
+        out_shape=jax.ShapeDtypeStruct((4, 1024, 256), BF),
+        in_specs=[SMEM, SMEM, VMEM],
+        out_specs=VMEM,
+        scratch_shapes=[pltpu.VMEM((32 * STRIDE, 128), F32)],
+        compiler_params=params(12),
+        name="near_blocks",
+    )(place, near_inv, near)
+
+    def partial_sums(stacked, near_dense):
+        def own_index(i, place_ref):
+            return (place_ref[3] if stacked else 1 - place_ref[3], 0, 0)
+
+        sent_shapes = (
+            (jax.ShapeDtypeStruct((4, 64, 1024), BF),)
+            if stacked
+            else (jax.ShapeDtypeStruct((64, 1024), BF),) * 3
+        )
         return pl.pallas_call(
-            functools.partial(near_kernel, which),
-            out_shape=jax.ShapeDtypeStruct((4, 1024, 256), BF),
-            in_specs=[SMEM, SMEM, VMEM, VMEM],
-            out_specs=VMEM,
-            scratch_shapes=[pltpu.VMEM((161 * 32, 128), F32)],
-            compiler_params=PARAMS,
-            name="near_blocks",
-        )(place, near_inv, near, core_flip(near))
-
-    def partial_sums(which, near):
-        near_dense = near_weights(which, near)
-        return pl.pallas_call(
-            partial_kernel,
-            out_shape=(jax.ShapeDtypeStruct((64, 1024), F32),)
-            + (jax.ShapeDtypeStruct((64, 1024), BF),) * 3,
-            grid=(1,),
-            in_specs=[SMEM]
-            + [pl.BlockSpec((4, 1024, 256), lambda i: (which, 0, 0))]
-            + [VMEM] * 2,
-            out_specs=(VMEM,) * 4,
-            scratch_shapes=[pltpu.VMEM((2, 256, 1024), BF)],
-            compiler_params=PARAMS,
+            functools.partial(partial_kernel, stacked),
+            out_shape=(jax.ShapeDtypeStruct((64, 1024), F32),) + sent_shapes,
+            grid_spec=pltpu.PrefetchScalarGridSpec(
+                num_scalar_prefetch=1,
+                grid=(1,),
+                in_specs=[pl.BlockSpec((4, 1024, 256), own_index), VMEM, VMEM],
+                out_specs=(VMEM,) * (1 + len(sent_shapes)),
+                scratch_shapes=[pltpu.VMEM((2, 256, 1024), BF)],
+            ),
+            compiler_params=params(16),
             name="partial_sums",
         )(place, weights, near_dense, gathered)
 
-    middle_args = []
-    for which, near in enumerate((near_gate, near_up)):
-        keep, *sent = partial_sums(which, near)
-        middle_args.append(keep)
-        for flip in (1, 2, 3):
-            middle_args.append(owner_flip(sent[flip - 1], 2 * flip))
-
-    sums = pl.pallas_call(
+    first_keep, first_sent = partial_sums(True, near_weights)
+    first_back = zone_exchange(first_sent)
+    second_keep, *second_sent = partial_sums(False, core_flip(near_weights))
+    second_back = [owner_flip(second_sent[flip - 1], 2 * flip) for flip in (1, 2, 3)]
+
+    mine, theirs = pl.pallas_call(
         middle_kernel,
-        out_shape=jax.ShapeDtypeStruct((P_SIZE, 2048), F32),
-        in_specs=[SMEM] + [VMEM] * 12,
-        out_specs=VMEM,
+        out_shape=(jax.ShapeDtypeStruct((8, 2048), F32),) * 2,
+        in_specs=[SMEM] + [VMEM] * 10,
+        out_specs=(VMEM, VMEM),
         scratch_shapes=[
             pltpu.VMEM((64, 1024), F32),
             pltpu.VMEM((64, 1024), F32),
             pltpu.VMEM((4, 64, 256), F32),
             pltpu.VMEM((K, 1024), BF),
             pltpu.VMEM((64 * P_SIZE, 1024), BF),
+            pltpu.VMEM((64 * P_SIZE, K), BF),
         ],
-        compiler_params=PARAMS,
+        compiler_params=params(16),
         name="token_sums",
-    )(place, *middle_args, *pay_parts)
-
-    sums = sums + core_flip(sums)
+    )(place, first_keep, first_back, second_keep, *second_back, *pay_parts)
+
+    sums = mine + core_flip(theirs)
     for bits in (1, 2, 4):
         sums = sums + owner_flip(sums, bits)
 
     return pl.pallas_call(
         product_kernel,
         out_shape=jax.ShapeDtypeStruct((P_SIZE, 1024), F32),
-        in_specs=[VMEM, VMEM],
+        in_specs=[SMEM, VMEM, VMEM, VMEM],
         out_specs=VMEM,
-        compiler_params=PARAMS,
+        scratch_shapes=[pltpu.VMEM((2, 8, 2048), F32)],
+        compiler_params=params(12),
         name="products",
-    )(sums, weights)
+    )(place, sums, core_flip(sums), weights)
 
 
 def per_device(tokens, gate_blocks, *rest):

time: 143 us -> 119 us (0.83)
  Pallas kernels: 46.5 us -> 24.2 us
  local copies, waits for them, and re-layouts: 6.33 us -> 13.1 us
  waiting for transfers between devices: 50.5 us -> 46.4 us
  other arithmetic: 3.93 us -> 1.57 us
  starting transfers between devices: 34.9 us -> 32.8 us
    ppermute x15 -> x11, waiting for transfers between devices: 48.9 us -> 34.7 us  [owner_flip(): return lax.ppermute(value, 'fsdp', [(i, i ^ bits) for i in range(8)])]
    pallas_call x5 -> x4, Pallas kernels: 28 us -> 14.3 us  [the longest x2 6.75 us: partial_sums(): pl.pallas_call(functools.partial(partial_kernel, stacked), out_shape=(jax...]
    ppermute x15 -> x11, starting transfers between devices: 27.9 us -> 21.1 us  [owner_flip(): return lax.ppermute(value, 'fsdp', [(i, i ^ bits) for i in range(8)])]
    pallas_call x1, Pallas kernels: 14.2 us -> 7.33 us  [pair_split(): pl.pallas_call(own_kernel, out_shape=(jax.ShapeDtypeStruct((8, 1024, 256)...]
    unnamed x46 -> x28, local copies, waits for them, and re-layouts: 4.03 us -> 10.7 us
    ppermute x4 -> x5, waiting for transfers between devices: 1.56 us -> 7.48 us  [core_flip(): return lax.ppermute(value, 'seq', [(0, 1), (1, 0)])]
    all_to_all x1 -> x2, starting transfers between devices: 5.01 us -> 9.34 us  [zone_exchange(): lax.all_to_all(value, 'fsdp', split_axis=0, concat_axis=0, tiled=True, ax...]
    ppermute x1, waiting for transfers between devices: 0.01 us -> 2.74 us  [pair_split(): lax.ppermute(payload, 'groups', [(0, 1), (1, 0)])]
  transfers between devices with their start and end apart: 22 -> 20, of which waited for: 11 -> 14; matrix products, arithmetic and copies ran while one was open for 2% -> 0% of each run, Pallas kernels for 27% -> 15%
where the time goes in v3:
time: 119 us; the launch traced here: 118 us
  waiting for transfers between devices  46.4 us (39%)
  starting transfers between devices  32.8 us (28%)
  Pallas kernels  24.2 us (20%)
  local copies, waits for them, and re-layouts  13.1 us (11%)
  other arithmetic  1.57 us (1%)
    ppermute x11, waiting for transfers between devices, owner_flip(): return lax.ppermute(value, 'fsdp', [(i, i ^ bits) for i in range(8)])  34.7 us
    ppermute x11, starting transfers between devices, owner_flip(): return lax.ppermute(value, 'fsdp', [(i, i ^ bits) for i in range(8)])  21.1 us
    unnamed x28, local copies, waits for them, and re-layouts  10.7 us
    all_to_all x2, starting transfers between devices, zone_exchange(): lax.all_to_all(value, 'fsdp', split_axis=0, concat_axis=0, tiled=True, ax...  9.34 us
    ppermute x5, waiting for transfers between devices, core_flip(): return lax.ppermute(value, 'seq', [(0, 1), (1, 0)])  7.48 us
    pallas_call x1, Pallas kernels, pair_split(): pl.pallas_call(own_kernel, out_shape=(jax.ShapeDtypeStruct((8, 1024, 256)...  7.33 us
    pallas_call x2, Pallas kernels, partial_sums(): pl.pallas_call(functools.partial(partial_kernel, stacked), out_shape=(jax...  6.75 us
    pallas_call x1, Pallas kernels, pair_split(): pl.pallas_call(near_kernel, out_shape=jax.ShapeDtypeStruct((4, 1024, 256)...  3.86 us
  transfers between devices with their start and end apart: 20, of which 14 were waited for; matrix products, arithmetic and copies ran while one was open for 0% of the time, Pallas kernels for 15%

profile of v3, /device:TPU:0, one launch (start us, length us, event | category | flops | bytes accessed | tf_op | source)
XLA Modules:
  0.0 118.3 jit_solution(1104354264218415280)
XLA Ops:
  0.0 2.4 %copy.15 = bf16[8,4,8,2048]{3,2,0,1:T(8,128)(2,1)} copy(bf16[8,4,8,2048]{3,2,1,0:T(8,128)(2,1)} %bitcast.15) | data formatting | bytes 2097152 | tf_op jit(solution)/shard_map/reshape | solution.py:399
  3.8 3.0 %collective-permute-start = (bf16[160,4096]{1,0:T(8,128)(2,1)}, bf16[160,4096]{1,0:T(8,128)(2,1)}, u32[]{:S(2)}, u32[]{:S(2)}) collective-permute-start(bf16[160,4096]{1,0:T(8,128)(2,1)} %broadcast_select_fusion), channel_id=1, source_target_pairs={{0,2},{2,0},{4,6},{6,4},{8,10},{10,8},{12,14},{14,12},{1,3},{3,1},... | collective-permute-start | bytes 3932168 | tf_op jit(solution)/shard_map/ppermute | solution.py:384
  6.8 4.9 %all-to-all-start = ((bf16[4,64,2048]{2,1,0:T(8,128)(2,1)}), bf16[4,64,2048]{2,1,0:T(8,128)(2,1)}, u32[]{:S(2)}, u32[]{:S(2)}) async-start(bf16[4,64,2048]{2,1,0:T(8,128)(2,1)} %bitcast.14), calls=%async_computation | async-start | bytes 2097152 | tf_op jit(solution)/shard_map/all_to_all | solution.py:390
  13.3 7.3 %own_blocks.1 = (bf16[8,1024,256]{2,1,0:T(8,128)(2,1)S(1)}, f32[64,256]{1,0:T(8,128)S(1)}) custom-call(s32[4]{0:T(128)S(1)} %pad_add_fusion.1.place_ref, s32[3,256]{1,0:T(4,128)S(1)} %select_reduce_fusion.inv_ref, bf16[160,4096]{1,0:T(8,128)(2,1)S(1)} %copy-done.4, bf16[160,4096]{1,0:T(8,128)(2,1)S(1)} %copy-done.5, bf16[160,4096]{1,0:T(8,128)(2,1)S(1)} %copy-done.6, ...), custom_call_target="tpu_custom_call" | custom-call | tf_op jit(solution)/shard_map/own_blocks/pallas_call | solution.py:410
  20.6 2.0 %copy-done = bf16[8,1024,256]{2,1,0:T(8,128)(2,1)} copy-done((bf16[8,1024,256]{2,1,0:T(8,128)(2,1)}, bf16[8,1024,256]{2,1,0:T(8,128)(2,1)S(1)}, u32[]{:S(2)}) %copy-start) | copy-done | bytes 4194328
  23.1 14.5 %collective-permute-done.2 = f32[64,256]{1,0:T(8,128)S(1)} collective-permute-done((f32[64,256]{1,0:T(8,128)S(1)}, f32[64,256]{1,0:T(8,128)S(1)}, u32[]{:S(2)}, u32[]{:S(2)}) %collective-permute-start.2) | collective-permute-done | bytes 65568 | tf_op jit(solution)/shard_map/ppermute | solution.py:384
  37.7 2.4 %collective-permute-start.3 = (f32[64,256]{1,0:T(8,128)S(1)}, f32[64,256]{1,0:T(8,128)S(1)}, u32[]{:S(2)}, u32[]{:S(2)}) collective-permute-start(f32[64,256]{1,0:T(8,128)S(1)} %add.30), channel_id=1, source_target_pairs={{0,4},{2,6},{4,0},{6,2},{8,12},{10,14},{12,8},{14,10},{1,5},{3,7},... | collective-permute-start | bytes 196616 | tf_op jit(solution)/shard_map/ppermute | solution.py:384
  40.0 2.4 %collective-permute-done.3 = f32[64,256]{1,0:T(8,128)S(1)} collective-permute-done((f32[64,256]{1,0:T(8,128)S(1)}, f32[64,256]{1,0:T(8,128)S(1)}, u32[]{:S(2)}, u32[]{:S(2)}) %collective-permute-start.3) | collective-permute-done | bytes 65568 | tf_op jit(solution)/shard_map/ppermute | solution.py:384
  42.4 3.0 %collective-permute-start.4 = (f32[64,256]{1,0:T(8,128)S(1)}, f32[64,256]{1,0:T(8,128)S(1)}, u32[]{:S(2)}, u32[]{:S(2)}) collective-permute-start(f32[64,256]{1,0:T(8,128)S(1)} %add.31), channel_id=1, source_target_pairs={{0,8},{2,10},{4,12},{6,14},{8,0},{10,2},{12,4},{14,6},{1,9},{3,11}... | collective-permute-start | bytes 196616 | tf_op jit(solution)/shard_map/ppermute | solution.py:384
  45.4 1.5 %collective-permute-start.1 = (s32[3,256]{1,0:T(4,128)S(1)}, s32[3,256]{1,0:T(4,128)S(1)}, u32[]{:S(2)}, u32[]{:S(2)}) collective-permute-start(s32[3,256]{1,0:T(4,128)S(1)} %select_reduce_fusion.inv_ref), channel_id=1, source_target_pairs={{0,2},{2,0},{4,6},{6,4},{8,10},{10,8},{12,14},{14,12},{1,3},{3,1},... | collective-permute-start | bytes 9224 | tf_op jit(solution)/shard_map/ppermute | solution.py:384
  49.0 3.9 %near_blocks.1.near_ref = bf16[4,1024,256]{2,1,0:T(8,128)(2,1)S(1)} custom-call(s32[4]{0:T(128)S(1)} %pad_add_fusion.1.place_ref, s32[3,256]{1,0:T(4,128)S(1)} %collective-permute-done.1.inv_ref, bf16[160,4096]{1,0:T(8,128)(2,1)} %collective-permute-done.blocks_ref), custom_call_target="tpu_custom_call" | custom-call | tf_op jit(solution)/shard_map/near_blocks/pallas_call | solution.py:438
  53.4 5.0 %collective-permute-done.5.tok_ref = bf16[4,64,2048]{2,1,0:T(8,128)(2,1)S(1)} collective-permute-done((bf16[4,64,2048]{2,1,0:T(8,128)(2,1)}, bf16[4,64,2048]{2,1,0:T(8,128)(2,1)S(1)}, u32[]{:S(2)}, u32[]{:S(2)}) %collective-permute-start.5) | collective-permute-done | bytes 1048608 | tf_op jit(solution)/shard_map/ppermute | solution.py:387
  58.4 2.2 %copy-done.1 = bf16[8,1024,256]{2,1,0:T(8,128)(2,1)S(1)} copy-done((bf16[8,1024,256]{2,1,0:T(8,128)(2,1)S(1)}, bf16[8,1024,256]{2,1,0:T(8,128)(2,1)}, u32[]{:S(2)}) %copy-start.1) | copy-done | bytes 4194328
  60.6 2.6 %partial_sums.2 = (f32[64,1024]{1,0:T(8,128)S(1)}, bf16[4,64,1024]{2,1,0:T(8,128)(2,1)S(1)}) custom-call(s32[4]{0:T(128)S(1)} %pad_add_fusion.1.place_ref, bf16[8,1024,256]{2,1,0:T(8,128)(2,1)S(1)} %copy-done.1, bf16[4,1024,256]{2,1,0:T(8,128)(2,1)S(1)} %near_blocks.1.near_ref, bf16[4,64,2048]{2,1,0:T(8,128)(2,1)S(1)} %collective-permute-done.5.tok_ref), custom_call_target="tpu_custom_call" | custom-call | tf_op jit(solution)/shard_map/partial_sums/pallas_call | solution.py:457
  64.0 4.5 %all-to-all-start.1 = ((bf16[4,64,1024]{2,1,0:T(8,128)(2,1)}), bf16[4,64,1024]{2,1,0:T(8,128)(2,1)}, u32[]{:S(2)}, u32[]{:S(2)}) async-start(bf16[4,64,1024]{2,1,0:T(8,128)(2,1)} %copy-done.7), calls=%async_computation.1 | async-start | bytes 1048576 | tf_op jit(solution)/shard_map/all_to_all | solution.py:390
  68.6 2.2 %copy-done.2 = bf16[8,1024,256]{2,1,0:T(8,128)(2,1)S(1)} copy-done((bf16[8,1024,256]{2,1,0:T(8,128)(2,1)S(1)}, bf16[8,1024,256]{2,1,0:T(8,128)(2,1)}, u32[]{:S(2)}) %copy-start.2) | copy-done | bytes 4194328
  70.8 4.2 %partial_sums.3 = (f32[64,1024]{1,0:T(8,128)S(1)}, bf16[64,1024]{1,0:T(8,128)(2,1)S(1)}, bf16[64,1024]{1,0:T(8,128)(2,1)S(1)}, bf16[64,1024]{1,0:T(8,128)(2,1)S(1)}) custom-call(s32[4]{0:T(128)S(1)} %pad_add_fusion.1.place_ref, bf16[8,1024,256]{2,1,0:T(8,128)(2,1)S(1)} %copy-done.2, bf16[4,1024,256]{2,1,0:T(8,128)(2,1)} %collective-permute-done.6.near_ref, ...), custom_call_target="tpu_custom_call" | custom-call | tf_op jit(solution)/shard_map/partial_sums/pallas_call | solution.py:457
  74.9 2.0 %collective-permute-start.7 = (bf16[64,1024]{1,0:T(8,128)(2,1)S(1)}, bf16[64,1024]{1,0:T(8,128)(2,1)S(1)}, u32[]{:S(2)}, u32[]{:S(2)}) collective-permute-start(bf16[64,1024]{1,0:T(8,128)(2,1)S(1)} %get-tuple-element.31), channel_id=1, source_target_pairs={{0,4},{2,6},{4,0},{6,2},{8,12},{10,14},{12,8},{14,10},{1,5},{3,7},... | collective-permute-start | bytes 393224 | tf_op jit(solution)/shard_map/ppermute | solution.py:384
  76.9 2.4 %collective-permute-start.8 = (bf16[64,1024]{1,0:T(8,128)(2,1)S(1)}, bf16[64,1024]{1,0:T(8,128)(2,1)S(1)}, u32[]{:S(2)}, u32[]{:S(2)}) collective-permute-start(bf16[64,1024]{1,0:T(8,128)(2,1)S(1)} %get-tuple-element.32), channel_id=1, source_target_pairs={{0,8},{2,10},{4,12},{6,14},{8,0},{10,2},{12,4},{14,6},{1,9},{3,11}... | collective-permute-start | bytes 393224 | tf_op jit(solution)/shard_map/ppermute | solution.py:384
  79.4 1.5 %collective-permute-start.11 = (f32[64,256]{1,0:T(8,128)S(1)}, f32[64,256]{1,0:T(8,128)S(1)}, u32[]{:S(2)}, u32[]{:S(2)}) collective-permute-start(f32[64,256]{1,0:T(8,128)S(1)} %add.32.pay0_ref), channel_id=1, source_target_pairs={{0,16},{16,0},{1,17},{17,1},{2,18},{18,2},{3,19},{19,3},{4,20},{20... | collective-permute-start | bytes 196616 | tf_op jit(solution)/shard_map/ppermute | solution.py:434
  80.9 2.7 %collective-permute-done.11.pay2_ref = f32[64,256]{1,0:T(8,128)S(1)} collective-permute-done((f32[64,256]{1,0:T(8,128)S(1)}, f32[64,256]{1,0:T(8,128)S(1)}, u32[]{:S(2)}, u32[]{:S(2)}) %collective-permute-start.11) | collective-permute-done | bytes 65568 | tf_op jit(solution)/shard_map/ppermute | solution.py:434
  83.7 1.4 %collective-permute-done.12.pay3_ref = f32[64,256]{1,0:T(8,128)S(1)} collective-permute-done((f32[64,256]{1,0:T(8,128)S(1)}, f32[64,256]{1,0:T(8,128)S(1)}, u32[]{:S(2)}, u32[]{:S(2)}) %collective-permute-start.12) | collective-permute-done | bytes 65568 | tf_op jit(solution)/shard_map/ppermute | solution.py:435
  85.2 7.6 %collective-permute-done.8.second2_ref = bf16[64,1024]{1,0:T(8,128)(2,1)S(1)} collective-permute-done((bf16[64,1024]{1,0:T(8,128)(2,1)S(1)}, bf16[64,1024]{1,0:T(8,128)(2,1)S(1)}, u32[]{:S(2)}, u32[]{:S(2)}) %collective-permute-start.8) | collective-permute-done | bytes 131104 | tf_op jit(solution)/shard_map/ppermute | solution.py:384
  92.8 3.7 %token_sums.1 = (f32[8,2048]{1,0:T(8,128)S(1)}, f32[8,2048]{1,0:T(8,128)S(1)}) custom-call(s32[4]{0:T(128)S(1)} %pad_add_fusion.1.place_ref, f32[64,1024]{1,0:T(8,128)S(1)} %get-tuple-element.28.first_keep_ref, bf16[4,64,1024]{2,1,0:T(8,128)(2,1)} %all-to-all-done.1.first_ref, f32[64,1024]{1,0:T(8,128)S(1)} %get-tuple-element.30.second_keep_ref, ...), custom_call_target="tpu_custom_call" | custom-call | tf_op jit(solution)/shard_map/token_sums/pallas_call | solution.py:476
  97.8 1.6 %collective-permute-start.14 = (f32[8,2048]{1,0:T(8,128)S(1)}, f32[8,2048]{1,0:T(8,128)S(1)}, u32[]{:S(2)}, u32[]{:S(2)}) collective-permute-start(f32[8,2048]{1,0:T(8,128)S(1)} %add.33), channel_id=1, source_target_pairs={{0,2},{2,0},{4,6},{6,4},{8,10},{10,8},{12,14},{14,12},{1,3},{3,1},... | collective-permute-start | bytes 196616 | tf_op jit(solution)/shard_map/ppermute | solution.py:384
  99.3 2.8 %collective-permute-done.14 = f32[8,2048]{1,0:T(8,128)S(1)} collective-permute-done((f32[8,2048]{1,0:T(8,128)S(1)}, f32[8,2048]{1,0:T(8,128)S(1)}, u32[]{:S(2)}, u32[]{:S(2)}) %collective-permute-start.14) | collective-permute-done | bytes 65568 | tf_op jit(solution)/shard_map/ppermute | solution.py:384
  102.1 2.6 %collective-permute-start.15 = (f32[8,2048]{1,0:T(8,128)S(1)}, f32[8,2048]{1,0:T(8,128)S(1)}, u32[]{:S(2)}, u32[]{:S(2)}) collective-permute-start(f32[8,2048]{1,0:T(8,128)S(1)} %add.34), channel_id=1, source_target_pairs={{0,4},{2,6},{4,0},{6,2},{8,12},{10,14},{12,8},{14,10},{1,5},{3,7},... | collective-permute-start | bytes 196616 | tf_op jit(solution)/shard_map/ppermute | solution.py:384
  104.7 2.2 %collective-permute-done.15 = f32[8,2048]{1,0:T(8,128)S(1)} collective-permute-done((f32[8,2048]{1,0:T(8,128)S(1)}, f32[8,2048]{1,0:T(8,128)S(1)}, u32[]{:S(2)}, u32[]{:S(2)}) %collective-permute-start.15) | collective-permute-done | bytes 65568 | tf_op jit(solution)/shard_map/ppermute | solution.py:384
  106.9 2.1 %collective-permute-start.16 = (f32[8,2048]{1,0:T(8,128)S(1)}, f32[8,2048]{1,0:T(8,128)S(1)}, u32[]{:S(2)}, u32[]{:S(2)}) collective-permute-start(f32[8,2048]{1,0:T(8,128)S(1)} %add.35), channel_id=1, source_target_pairs={{0,8},{2,10},{4,12},{6,14},{8,0},{10,2},{12,4},{14,6},{1,9},{3,11}... | collective-permute-start | bytes 196616 | tf_op jit(solution)/shard_map/ppermute | solution.py:384
  109.1 3.1 %collective-permute-done.16 = f32[8,2048]{1,0:T(8,128)S(1)} collective-permute-done((f32[8,2048]{1,0:T(8,128)S(1)}, f32[8,2048]{1,0:T(8,128)S(1)}, u32[]{:S(2)}, u32[]{:S(2)}) %collective-permute-start.16) | collective-permute-done | bytes 65568 | tf_op jit(solution)/shard_map/ppermute | solution.py:384
  113.5 2.2 %copy-done.3 = bf16[8,1024,256]{2,1,0:T(8,128)(2,1)S(1)} copy-done((bf16[8,1024,256]{2,1,0:T(8,128)(2,1)S(1)}, bf16[8,1024,256]{2,1,0:T(8,128)(2,1)}, u32[]{:S(2)}) %copy-start.3) | copy-done | bytes 4194328
  115.7 2.6 %products.1 = f32[16,1024]{1,0:T(8,128)} custom-call(s32[4]{0:T(128)S(1)} %pad_add_fusion.1.place_ref, f32[8,2048]{1,0:T(8,128)S(1)} %add.36.mine_ref, f32[8,2048]{1,0:T(8,128)S(1)} %collective-permute-done.17.theirs_ref, bf16[8,1024,256]{2,1,0:T(8,128)(2,1)S(1)} %copy-done.3), custom_call_target="tpu_custom_call" | custom-call | tf_op jit(solution)/shard_map/products/pallas_call | solution.py:497
  (54 shorter events, 9.9 us)
Async XLA Ops:
  0.0 2.5 %copy-start.4 = (bf16[160,4096]{1,0:T(8,128)(2,1)S(1)}, bf16[160,4096]{1,0:T(8,128)(2,1)}, u32[]{:S(2)}) copy-start(bf16[160,4096]{1,0:T(8,128)(2,1)} %gate_ref.1) | copy-start | bytes 3932164
  3.7 8.0 %copy-start.11 = (s32[160]{0:T(256)S(1)}, s32[160]{0:T(256)}, u32[]{:S(2)}) copy-start(s32[160]{0:T(256)} %param.16) | copy-start | bytes 1924
  3.7 8.0 %copy-start.12 = (s32[160]{0:T(256)S(1)}, s32[160]{0:T(256)}, u32[]{:S(2)}) copy-start(s32[160]{0:T(256)} %param.14) | copy-start | bytes 1924
  3.7 8.0 %copy-start.13 = (s32[160]{0:T(256)S(1)}, s32[160]{0:T(256)}, u32[]{:S(2)}) copy-start(s32[160]{0:T(256)} %param.12) | copy-start | bytes 1924
  3.7 8.2 %copy-start.5 = (bf16[160,4096]{1,0:T(8,128)(2,1)S(1)}, bf16[160,4096]{1,0:T(8,128)(2,1)}, u32[]{:S(2)}) copy-start(bf16[160,4096]{1,0:T(8,128)(2,1)} %up_ref.1) | copy-start | bytes 3932164
  3.7 8.2 %copy-start.8 = (bf16[32,1024]{1,0:T(8,128)(2,1)S(1)}, bf16[32,1024]{1,0:T(8,128)(2,1)}, u32[]{:S(2)}) copy-start(bf16[32,1024]{1,0:T(8,128)(2,1)} %sketch_ref.1) | copy-start | bytes 196612
  3.7 8.2 %copy-start.9 = (s32[16,256]{1,0:T(8,128)S(1)}, s32[16,256]{1,0:T(8,128)}, u32[]{:S(2)}) copy-start(s32[16,256]{1,0:T(8,128)} %index_ref.1) | copy-start | bytes 49156
  3.8 8.2 %copy-start.10 = (f32[16,256]{1,0:T(8,128)S(1)}, f32[16,256]{1,0:T(8,128)}, u32[]{:S(2)}) copy-start(f32[16,256]{1,0:T(8,128)} %value_ref.1) | copy-start | bytes 49156
  3.8 45.2 %collective-permute-start = (bf16[160,4096]{1,0:T(8,128)(2,1)}, bf16[160,4096]{1,0:T(8,128)(2,1)}, u32[]{:S(2)}, u32[]{:S(2)}) collective-permute-start(bf16[160,4096]{1,0:T(8,128)(2,1)} %broadcast_select_fusion), channel_id=1, source_target_pairs={{0,2},{2,0},{4,6},{6,4},{8,10},{10,8},{12,14},{14,12},{1,3},{3,1},... | collective-permute-start | bytes 3932168 | tf_op jit(solution)/shard_map/ppermute | solution.py:384
  6.8 46.2 %all-to-all-start = ((bf16[4,64,2048]{2,1,0:T(8,128)(2,1)}), bf16[4,64,2048]{2,1,0:T(8,128)(2,1)}, u32[]{:S(2)}, u32[]{:S(2)}) async-start(bf16[4,64,2048]{2,1,0:T(8,128)(2,1)} %bitcast.14), calls=%async_computation | async-start | bytes 2097152 | tf_op jit(solution)/shard_map/all_to_all | solution.py:390
  20.6 2.0 %copy-start = (bf16[8,1024,256]{2,1,0:T(8,128)(2,1)}, bf16[8,1024,256]{2,1,0:T(8,128)(2,1)S(1)}, u32[]{:S(2)}) copy-start(bf16[8,1024,256]{2,1,0:T(8,128)(2,1)S(1)} %get-tuple-element.21.own_ref.weight_ref) | copy-start | bytes 12582916
  22.6 15.0 %collective-permute-start.2 = (f32[64,256]{1,0:T(8,128)S(1)}, f32[64,256]{1,0:T(8,128)S(1)}, u32[]{:S(2)}, u32[]{:S(2)}) collective-permute-start(f32[64,256]{1,0:T(8,128)S(1)} %get-tuple-element.24), channel_id=1, source_target_pairs={{0,2},{2,0},{4,6},{6,4},{8,10},{10,8},{12,14},{14,12},{1,3},{3,1},... | collective-permute-start | bytes 196616 | tf_op jit(solution)/shard_map/ppermute | solution.py:384
  37.7 4.7 %collective-permute-start.3 = (f32[64,256]{1,0:T(8,128)S(1)}, f32[64,256]{1,0:T(8,128)S(1)}, u32[]{:S(2)}, u32[]{:S(2)}) collective-permute-start(f32[64,256]{1,0:T(8,128)S(1)} %add.30), channel_id=1, source_target_pairs={{0,4},{2,6},{4,0},{6,2},{8,12},{10,14},{12,8},{14,10},{1,5},{3,7},... | collective-permute-start | bytes 196616 | tf_op jit(solution)/shard_map/ppermute | solution.py:384
  42.4 5.3 %collective-permute-start.4 = (f32[64,256]{1,0:T(8,128)S(1)}, f32[64,256]{1,0:T(8,128)S(1)}, u32[]{:S(2)}, u32[]{:S(2)}) collective-permute-start(f32[64,256]{1,0:T(8,128)S(1)} %add.31), channel_id=1, source_target_pairs={{0,8},{2,10},{4,12},{6,14},{8,0},{10,2},{12,4},{14,6},{1,9},{3,11}... | collective-permute-start | bytes 196616 | tf_op jit(solution)/shard_map/ppermute | solution.py:384
  45.4 3.6 %collective-permute-start.1 = (s32[3,256]{1,0:T(4,128)S(1)}, s32[3,256]{1,0:T(4,128)S(1)}, u32[]{:S(2)}, u32[]{:S(2)}) collective-permute-start(s32[3,256]{1,0:T(4,128)S(1)} %select_reduce_fusion.inv_ref), channel_id=1, source_target_pairs={{0,2},{2,0},{4,6},{6,4},{8,10},{10,8},{12,14},{14,12},{1,3},{3,1},... | collective-permute-start | bytes 9224 | tf_op jit(solution)/shard_map/ppermute | solution.py:384
  52.9 15.7 %collective-permute-start.6 = (bf16[4,1024,256]{2,1,0:T(8,128)(2,1)S(1)}, bf16[4,1024,256]{2,1,0:T(8,128)(2,1)}, u32[]{:S(2)}, u32[]{:S(2)}) collective-permute-start(bf16[4,1024,256]{2,1,0:T(8,128)(2,1)S(1)} %near_blocks.1.near_ref), channel_id=1, source_target_pairs={{0,1},{1,0},{2,3},{3,2},{4,5},{5,4},{6,7},{7,6},{8,9},{9,8},{10,11... | collective-permute-start | bytes 6291464 | tf_op jit(solution)/shard_map/ppermute | solution.py:387
  52.9 5.5 %collective-permute-start.5 = (bf16[4,64,2048]{2,1,0:T(8,128)(2,1)}, bf16[4,64,2048]{2,1,0:T(8,128)(2,1)S(1)}, u32[]{:S(2)}, u32[]{:S(2)}) collective-permute-start(bf16[4,64,2048]{2,1,0:T(8,128)(2,1)} %all-to-all-done), channel_id=1, source_target_pairs={{0,1},{1,0},{2,3},{3,2},{4,5},{5,4},{6,7},{7,6},{8,9},{9,8},{10,11... | collective-permute-start | bytes 3145736 | tf_op jit(solution)/shard_map/ppermute | solution.py:387
  58.4 2.2 %copy-start.1 = (bf16[8,1024,256]{2,1,0:T(8,128)(2,1)S(1)}, bf16[8,1024,256]{2,1,0:T(8,128)(2,1)}, u32[]{:S(2)}) copy-start(bf16[8,1024,256]{2,1,0:T(8,128)(2,1)} %copy-done) | copy-start | bytes 12582916
  64.0 21.2 %all-to-all-start.1 = ((bf16[4,64,1024]{2,1,0:T(8,128)(2,1)}), bf16[4,64,1024]{2,1,0:T(8,128)(2,1)}, u32[]{:S(2)}, u32[]{:S(2)}) async-start(bf16[4,64,1024]{2,1,0:T(8,128)(2,1)} %copy-done.7), calls=%async_computation.1 | async-start | bytes 1048576 | tf_op jit(solution)/shard_map/all_to_all | solution.py:390
  68.4 12.5 %collective-permute-start.10 = (f32[64,256]{1,0:T(8,128)S(1)}, f32[64,256]{1,0:T(8,128)S(1)}, u32[]{:S(2)}, u32[]{:S(2)}) collective-permute-start(f32[64,256]{1,0:T(8,128)S(1)} %add.32.pay0_ref), channel_id=1, source_target_pairs={{0,1},{1,0},{2,3},{3,2},{4,5},{5,4},{6,7},{7,6},{8,9},{9,8},{10,11... | collective-permute-start | bytes 196616 | tf_op jit(solution)/shard_map/ppermute | solution.py:387
  68.6 2.2 %copy-start.2 = (bf16[8,1024,256]{2,1,0:T(8,128)(2,1)S(1)}, bf16[8,1024,256]{2,1,0:T(8,128)(2,1)}, u32[]{:S(2)}) copy-start(bf16[8,1024,256]{2,1,0:T(8,128)(2,1)} %copy-done) | copy-start | bytes 12582916
  74.9 10.3 %collective-permute-start.7 = (bf16[64,1024]{1,0:T(8,128)(2,1)S(1)}, bf16[64,1024]{1,0:T(8,128)(2,1)S(1)}, u32[]{:S(2)}, u32[]{:S(2)}) collective-permute-start(bf16[64,1024]{1,0:T(8,128)(2,1)S(1)} %get-tuple-element.31), channel_id=1, source_target_pairs={{0,4},{2,6},{4,0},{6,2},{8,12},{10,14},{12,8},{14,10},{1,5},{3,7},... | collective-permute-start | bytes 393224 | tf_op jit(solution)/shard_map/ppermute | solution.py:384
  76.9 15.9 %collective-permute-start.8 = (bf16[64,1024]{1,0:T(8,128)(2,1)S(1)}, bf16[64,1024]{1,0:T(8,128)(2,1)S(1)}, u32[]{:S(2)}, u32[]{:S(2)}) collective-permute-start(bf16[64,1024]{1,0:T(8,128)(2,1)S(1)} %get-tuple-element.32), channel_id=1, source_target_pairs={{0,8},{2,10},{4,12},{6,14},{8,0},{10,2},{12,4},{14,6},{1,9},{3,11}... | collective-permute-start | bytes 393224 | tf_op jit(solution)/shard_map/ppermute | solution.py:384
  79.3 13.5 %collective-permute-start.9 = (bf16[64,1024]{1,0:T(8,128)(2,1)S(1)}, bf16[64,1024]{1,0:T(8,128)(2,1)S(1)}, u32[]{:S(2)}, u32[]{:S(2)}) collective-permute-start(bf16[64,1024]{1,0:T(8,128)(2,1)S(1)} %get-tuple-element.33), channel_id=1, source_target_pairs={{0,12},{2,14},{4,8},{6,10},{8,4},{10,6},{12,0},{14,2},{1,13},{3,15... | collective-permute-start | bytes 393224 | tf_op jit(solution)/shard_map/ppermute | solution.py:384
  79.4 4.3 %collective-permute-start.11 = (f32[64,256]{1,0:T(8,128)S(1)}, f32[64,256]{1,0:T(8,128)S(1)}, u32[]{:S(2)}, u32[]{:S(2)}) collective-permute-start(f32[64,256]{1,0:T(8,128)S(1)} %add.32.pay0_ref), channel_id=1, source_target_pairs={{0,16},{16,0},{1,17},{17,1},{2,18},{18,2},{3,19},{19,3},{4,20},{20... | collective-permute-start | bytes 196616 | tf_op jit(solution)/shard_map/ppermute | solution.py:434
  80.9 4.2 %collective-permute-start.12 = (f32[64,256]{1,0:T(8,128)S(1)}, f32[64,256]{1,0:T(8,128)S(1)}, u32[]{:S(2)}, u32[]{:S(2)}) collective-permute-start(f32[64,256]{1,0:T(8,128)S(1)} %add.32.pay0_ref), channel_id=1, source_target_pairs={{0,17},{1,16},{16,1},{17,0},{2,19},{3,18},{18,3},{19,2},{4,21},{5,... | collective-permute-start | bytes 196616 | tf_op jit(solution)/shard_map/ppermute | solution.py:435
  96.4 1.3 %collective-permute-start.13 = (f32[8,2048]{1,0:T(8,128)S(1)}, f32[8,2048]{1,0:T(8,128)S(1)}, u32[]{:S(2)}, u32[]{:S(2)}) collective-permute-start(f32[8,2048]{1,0:T(8,128)S(1)} %get-tuple-element.36), channel_id=1, source_target_pairs={{0,1},{1,0},{2,3},{3,2},{4,5},{5,4},{6,7},{7,6},{8,9},{9,8},{10,11... | collective-permute-start | bytes 196616 | tf_op jit(solution)/shard_map/ppermute | solution.py:387
  97.8 4.3 %collective-permute-start.14 = (f32[8,2048]{1,0:T(8,128)S(1)}, f32[8,2048]{1,0:T(8,128)S(1)}, u32[]{:S(2)}, u32[]{:S(2)}) collective-permute-start(f32[8,2048]{1,0:T(8,128)S(1)} %add.33), channel_id=1, source_target_pairs={{0,2},{2,0},{4,6},{6,4},{8,10},{10,8},{12,14},{14,12},{1,3},{3,1},... | collective-permute-start | bytes 196616 | tf_op jit(solution)/shard_map/ppermute | solution.py:384
  102.1 4.8 %collective-permute-start.15 = (f32[8,2048]{1,0:T(8,128)S(1)}, f32[8,2048]{1,0:T(8,128)S(1)}, u32[]{:S(2)}, u32[]{:S(2)}) collective-permute-start(f32[8,2048]{1,0:T(8,128)S(1)} %add.34), channel_id=1, source_target_pairs={{0,4},{2,6},{4,0},{6,2},{8,12},{10,14},{12,8},{14,10},{1,5},{3,7},... | collective-permute-start | bytes 196616 | tf_op jit(solution)/shard_map/ppermute | solution.py:384
  106.9 5.2 %collective-permute-start.16 = (f32[8,2048]{1,0:T(8,128)S(1)}, f32[8,2048]{1,0:T(8,128)S(1)}, u32[]{:S(2)}, u32[]{:S(2)}) collective-permute-start(f32[8,2048]{1,0:T(8,128)S(1)} %add.35), channel_id=1, source_target_pairs={{0,8},{2,10},{4,12},{6,14},{8,0},{10,2},{12,4},{14,6},{1,9},{3,11}... | collective-permute-start | bytes 196616 | tf_op jit(solution)/shard_map/ppermute | solution.py:384
  112.2 1.3 %collective-permute-start.17 = (f32[8,2048]{1,0:T(8,128)S(1)}, f32[8,2048]{1,0:T(8,128)S(1)}, u32[]{:S(2)}, u32[]{:S(2)}) collective-permute-start(f32[8,2048]{1,0:T(8,128)S(1)} %add.36.mine_ref), channel_id=1, source_target_pairs={{0,1},{1,0},{2,3},{3,2},{4,5},{5,4},{6,7},{7,6},{8,9},{9,8},{10,11... | collective-permute-start | bytes 196616 | tf_op jit(solution)/shard_map/ppermute | solution.py:387
  113.5 2.2 %copy-start.3 = (bf16[8,1024,256]{2,1,0:T(8,128)(2,1)S(1)}, bf16[8,1024,256]{2,1,0:T(8,128)(2,1)}, u32[]{:S(2)}) copy-start(bf16[8,1024,256]{2,1,0:T(8,128)(2,1)} %copy-done) | copy-start | bytes 12582916
  (2 other events, 2.1 us)

commit v4 on v3

--- a/solution.py
+++ b/solution.py
@@ -16,6 +16,7 @@
 F32 = jnp.float32
 VMEM = pl.BlockSpec(memory_space=pltpu.VMEM)
 SMEM = pl.BlockSpec(memory_space=pltpu.SMEM)
+HBM = pl.BlockSpec(memory_space=pltpu.HBM)
 
 STRIDE = 168
 
@@ -185,27 +186,46 @@
     sketch_ref,
     index_ref,
     value_ref,
-    weight_ref,
+    weight_out_ref,
     payload_ref,
     tiles_ref,
     omega_ref,
     split_ref,
     down_dense_ref,
+    blocks_ref,
+    weight_ref,
+    in_sem,
+    out_sem,
 ):
     owner = place_ref[0]
     quarter = place_ref[1]
+    loads = [
+        pltpu.make_async_copy(source, blocks_ref.at[i], in_sem.at[i])
+        for i, source in enumerate((gate_ref, up_ref, down_ref))
+    ]
+    stores = [
+        pltpu.make_async_copy(
+            weight_ref.at[pl.ds(4 * i, 4)], weight_out_ref.at[pl.ds(4 * i, 4)], out_sem.at[i]
+        )
+        for i in range(2)
+    ]
+    for load in loads:
+        load.start()
     clear_empty_slot(tiles_ref)
 
-    for which, blocks_ref in enumerate((gate_ref, up_ref)):
-        stage_blocks(blocks_ref, tiles_ref, 0)
+    for which in range(2):
+        loads[which].wait()
+        stage_blocks(blocks_ref.at[which], tiles_ref, 0)
 
         def put(pair, row, piece):
             lane = (pair % 2) * 128
             weight_ref[4 * which + pair // 2, pl.ds(row, 32), lane : lane + 128] = piece
 
         assemble_columns(inv_ref, which, tiles_ref, put)
-
-    stage_blocks(down_ref, tiles_ref, 0)
+        stores[which].start()
+
+    loads[2].wait()
+    stage_blocks(blocks_ref.at[2], tiles_ref, 0)
     for local_row in range(4):
         for pair in range(8):
             cell = (quarter * 4 + local_row) * 16 + 2 * pair
@@ -243,6 +263,8 @@
     for which in range(2):
         triple = dot(split_ref[...], weight_ref[4 * which + quarter])
         payload_ref[16 * which : 16 * (which + 1), :] = triple[:16] + triple[16:32] + triple[32:]
+    for store in stores:
+        store.wait()
 
 
 def flipped(two_bits, flip):
@@ -250,21 +272,7 @@
     return low_bit + 2 * lax.rem(two_bits // 2 + flip // 2, 2)
 
 
-def near_kernel(place_ref, inv_ref, blocks_ref, weight_ref, tiles_ref):
-    clear_empty_slot(tiles_ref)
-    stage_blocks(blocks_ref, tiles_ref, 0)
-
-    def put(pair, row, piece):
-        lane = (pair % 2) * 128
-        weight_ref[pair // 2, pl.ds(row, 32), lane : lane + 128] = piece
-
-    assemble_columns(inv_ref, place_ref[3], tiles_ref, put)
-
-
-def partial_kernel(stacked, place_ref, own_ref, near_ref, tok_ref, keep_ref, *rest):
-    tokens_ref = rest[-1]
-    side = place_ref[2]
-    zone = place_ref[0] // 2
+def shuffle_tokens(zone, side, tok_ref, tokens_ref):
     shuffle = shuffle_matrix(256)
     for source in range(4):
         spot = flipped(zone, source)
@@ -275,16 +283,105 @@
             tokens_ref[
                 half, 64 * source : 64 * (source + 1), 256 * (group % 4) : 256 * (group % 4 + 1)
             ] = moved
+
+
+def first_kernel(
+    place_ref,
+    inv_ref,
+    blocks_in_ref,
+    weight_in_ref,
+    tok_in_ref,
+    keep_ref,
+    sent_out_ref,
+    near_out_ref,
+    blocks_ref,
+    tiles_ref,
+    near_ref,
+    own_ref,
+    tok_ref,
+    tokens_ref,
+    sent_ref,
+    in_sem,
+    near_sem,
+    sent_sem,
+):
+    zone = place_ref[0] // 2
+    side = place_ref[2]
+    core = place_ref[3]
+    loads = [
+        pltpu.make_async_copy(blocks_in_ref, blocks_ref, in_sem.at[0]),
+        pltpu.make_async_copy(tok_in_ref, tok_ref, in_sem.at[1]),
+        pltpu.make_async_copy(weight_in_ref.at[pl.ds(4 * core, 4)], own_ref, in_sem.at[2]),
+    ]
+    for load in loads:
+        load.start()
+    clear_empty_slot(tiles_ref)
+    loads[0].wait()
+    stage_blocks(blocks_ref, tiles_ref, 0)
+
+    def put(pair, row, piece):
+        lane = (pair % 2) * 128
+        near_ref[pair // 2, pl.ds(row, 32), lane : lane + 128] = piece
+
+    assemble_columns(inv_ref, core, tiles_ref, put)
+    near_store = pltpu.make_async_copy(near_ref, near_out_ref, near_sem)
+    near_store.start()
+    loads[1].wait()
+    shuffle_tokens(zone, side, tok_ref, tokens_ref)
+    loads[2].wait()
+    stores = []
     for chunk in range(4):
         total = dot(tokens_ref[0], own_ref[chunk]) + dot(tokens_ref[1], near_ref[chunk])
         cols = slice(256 * chunk, 256 * (chunk + 1))
         keep_ref[:, cols] = total[:64]
-        for flip in range(0 if stacked else 1, 4):
-            sent = total[64 * flip : 64 * (flip + 1)].astype(BF)
-            if stacked:
-                rest[0][flipped(zone, flip), :, cols] = sent
-            else:
-                rest[flip - 1][:, cols] = sent
+        for flip in range(4):
+            sent_ref[flipped(zone, flip), :, cols] = total[64 * flip : 64 * (flip + 1)].astype(BF)
+        lanes = pl.ds(256 * chunk, 256)
+        store = pltpu.make_async_copy(
+            sent_ref.at[:, :, lanes], sent_out_ref.at[:, :, lanes], sent_sem.at[chunk]
+        )
+        store.start()
+        stores.append(store)
+    for store in stores:
+        store.wait()
+    near_store.wait()
+
+
+def second_kernel(
+    place_ref,
+    near_in_ref,
+    weight_in_ref,
+    tok_in_ref,
+    keep_ref,
+    out1_ref,
+    out2_ref,
+    out3_ref,
+    near_ref,
+    own_ref,
+    tok_ref,
+    tokens_ref,
+    in_sem,
+):
+    zone = place_ref[0] // 2
+    side = place_ref[2]
+    core = place_ref[3]
+    loads = [
+        pltpu.make_async_copy(tok_in_ref, tok_ref, in_sem.at[0]),
+        pltpu.make_async_copy(weight_in_ref.at[pl.ds(4 - 4 * core, 4)], own_ref, in_sem.at[1]),
+        pltpu.make_async_copy(near_in_ref, near_ref, in_sem.at[2]),
+    ]
+    for load in loads:
+        load.start()
+    loads[0].wait()
+    shuffle_tokens(zone, side, tok_ref, tokens_ref)
+    loads[1].wait()
+    loads[2].wait()
+    for chunk in range(4):
+        total = dot(tokens_ref[0], own_ref[chunk]) + dot(tokens_ref[1], near_ref[chunk])
+        cols = slice(256 * chunk, 256 * (chunk + 1))
+        keep_ref[:, cols] = total[:64]
+        for flip, ref in enumerate((out1_ref, out2_ref, out3_ref), 1):
+            ref[:, cols] = total[64 * flip : 64 * (flip + 1)].astype(BF)
 
 
 def middle_kernel(
@@ -347,14 +444,21 @@
         target[row, 1024:] = jnp.sum(backward * act_ref[...], axis=0, keepdims=True)
 
 
-def product_kernel(place_ref, mine_ref, theirs_ref, weight_ref, out_ref, sum_ref):
+def product_kernel(place_ref, mine_ref, theirs_ref, weight_ref, out_ref, sum_ref, held_ref, sem):
     core = place_ref[3]
+    loads = [
+        pltpu.make_async_copy(weight_ref.at[chunk], held_ref.at[chunk], sem.at[chunk])
+        for chunk in range(8)
+    ]
+    for load in loads:
+        load.start()
     sum_ref[core] = mine_ref[...]
     sum_ref[1 - core] = theirs_ref[...]
     sums = jnp.concatenate([sum_ref[0], sum_ref[1]], axis=0).astype(BF)
     total = None
     for chunk in range(8):
-        term = contract_last(sums[:, 256 * chunk : 256 * (chunk + 1)], weight_ref[chunk])
+        loads[chunk].wait()
+        term = contract_last(sums[:, 256 * chunk : 256 * (chunk + 1)], held_ref[chunk])
         total = term if total is None else total + term
     unshuffle = unshuffle_matrix(256)
     for group in range(4):
@@ -398,7 +502,7 @@
 
     by_zone = tokens.reshape(64, 4, 2048).transpose(1, 0, 2)
     by_zone, gate_source, up_source = lax.optimization_barrier((by_zone, gate_blocks, up_blocks))
-    gathered = core_flip(zone_exchange(by_zone))
+    gathered = zone_exchange(by_zone)
     near = owner_flip(jnp.where(core == 0, gate_source, up_source), 1)
 
     slots = jnp.stack([gate_slot, up_slot, down_slot])
@@ -413,21 +517,28 @@
             jax.ShapeDtypeStruct((8, 1024, 256), BF),
             jax.ShapeDtypeStruct((64, 256), F32),
         ),
-        in_specs=[SMEM, SMEM] + [VMEM] * 6,
-        out_specs=(VMEM, VMEM),
+        in_specs=[SMEM, SMEM] + [HBM] * 3 + [VMEM] * 3,
+        out_specs=(HBM, VMEM),
         scratch_shapes=[
             pltpu.VMEM((32 * STRIDE, 128), F32),
             pltpu.VMEM((128, 128), F32),
             pltpu.VMEM((48, 1024), BF),
             pltpu.VMEM((256, 1024), BF),
+            pltpu.VMEM((3, 160, 4096), BF),
+            pltpu.VMEM((8, 1024, 256), BF),
+            pltpu.SemaphoreType.DMA((3,)),
+            pltpu.SemaphoreType.DMA((2,)),
         ],
-        compiler_params=params(20),
+        compiler_params=params(60),
         name="own_blocks",
     )(place, inv, gate_blocks, up_blocks, down_blocks, sketch, probe_index, probe_value)
 
-    for bits in (1, 2, 4):
+    for bits in (2, 4):
         payload = payload + owner_flip(payload, bits)
-    near, near_inv, payload = lax.optimization_barrier((near, near_inv, payload))
+    near, near_inv, payload, gathered = lax.optimization_barrier(
+        (near, near_inv, payload, gathered)
+    )
+    payload = payload + owner_flip(payload, 1)
     pay_parts = [
         payload,
         core_flip(payload),
@@ -435,42 +546,48 @@
         lax.ppermute(payload, ("groups", "seq"), [(i, i ^ 3) for i in range(4)]),
     ]
 
-    near_weights = pl.pallas_call(
-        near_kernel,
-        out_shape=jax.ShapeDtypeStruct((4, 1024, 256), BF),
-        in_specs=[SMEM, SMEM, VMEM],
-        out_specs=VMEM,
-        scratch_shapes=[pltpu.VMEM((32 * STRIDE, 128), F32)],
-        compiler_params=params(12),
-        name="near_blocks",
-    )(place, near_inv, near)
-
-    def partial_sums(stacked, near_dense):
-        def own_index(i, place_ref):
-            return (place_ref[3] if stacked else 1 - place_ref[3], 0, 0)
-
-        sent_shapes = (
-            (jax.ShapeDtypeStruct((4, 64, 1024), BF),)
-            if stacked
-            else (jax.ShapeDtypeStruct((64, 1024), BF),) * 3
-        )
-        return pl.pallas_call(
-            functools.partial(partial_kernel, stacked),
-            out_shape=(jax.ShapeDtypeStruct((64, 1024), F32),) + sent_shapes,
-            grid_spec=pltpu.PrefetchScalarGridSpec(
-                num_scalar_prefetch=1,
-                grid=(1,),
-                in_specs=[pl.BlockSpec((4, 1024, 256), own_index), VMEM, VMEM],
-                out_specs=(VMEM,) * (1 + len(sent_shapes)),
-                scratch_shapes=[pltpu.VMEM((2, 256, 1024), BF)],
-            ),
-            compiler_params=params(16),
-            name="partial_sums",
-        )(place, weights, near_dense, gathered)
-
-    first_keep, first_sent = partial_sums(True, near_weights)
+    first_keep, first_sent, near_weights = pl.pallas_call(
+        first_kernel,
+        out_shape=(
+            jax.ShapeDtypeStruct((64, 1024), F32),
+            jax.ShapeDtypeStruct((4, 64, 1024), BF),
+            jax.ShapeDtypeStruct((4, 1024, 256), BF),
+        ),
+        in_specs=[SMEM, SMEM, HBM, HBM, HBM],
+        out_specs=(VMEM, HBM, HBM),
+        scratch_shapes=[
+            pltpu.VMEM((160, 4096), BF),
+            pltpu.VMEM((32 * STRIDE, 128), F32),
+            pltpu.VMEM((4, 1024, 256), BF),
+            pltpu.VMEM((4, 1024, 256), BF),
+            pltpu.VMEM((4, 64, 2048), BF),
+            pltpu.VMEM((2, 256, 1024), BF),
+            pltpu.VMEM((4, 64, 1024), BF),
+            pltpu.SemaphoreType.DMA((3,)),
+            pltpu.SemaphoreType.DMA,
+            pltpu.SemaphoreType.DMA((4,)),
+        ],
+        compiler_params=params(60),
+        name="first_partial",
+    )(place, near_inv, near, weights, gathered)
     first_back = zone_exchange(first_sent)
-    second_keep, *second_sent = partial_sums(False, core_flip(near_weights))
+
+    second_keep, *second_sent = pl.pallas_call(
+        second_kernel,
+        out_shape=(jax.ShapeDtypeStruct((64, 1024), F32),)
+        + (jax.ShapeDtypeStruct((64, 1024), BF),) * 3,
+        in_specs=[SMEM, HBM, HBM, HBM],
+        out_specs=(VMEM,) * 4,
+        scratch_shapes=[
+            pltpu.VMEM((4, 1024, 256), BF),
+            pltpu.VMEM((4, 1024, 256), BF),
+            pltpu.VMEM((4, 64, 2048), BF),
+            pltpu.VMEM((2, 256, 1024), BF),
+            pltpu.SemaphoreType.DMA((3,)),
+        ],
+        compiler_params=params(59),
+        name="second_partial",
+    )(place, core_flip(near_weights), weights, gathered)
     second_back = [owner_flip(second_sent[flip - 1], 2 * flip) for flip in (1, 2, 3)]
 
     mine, theirs = pl.pallas_call(
@@ -497,10 +614,14 @@
     return pl.pallas_call(
         product_kernel,
         out_shape=jax.ShapeDtypeStruct((P_SIZE, 1024), F32),
-        in_specs=[SMEM, VMEM, VMEM, VMEM],
+        in_specs=[SMEM, VMEM, VMEM, HBM],
         out_specs=VMEM,
-        scratch_shapes=[pltpu.VMEM((2, 8, 2048), F32)],
-        compiler_params=params(12),
+        scratch_shapes=[
+            pltpu.VMEM((2, 8, 2048), F32),
+            pltpu.VMEM((8, 1024, 256), BF),
+            pltpu.SemaphoreType.DMA((8,)),
+        ],
+        compiler_params=params(59),
         name="products",
     )(place, sums, core_flip(sums), weights)
 

time: 119 us -> 109 us (0.916)
  waiting for transfers between devices: 46.4 us -> 32.1 us
  local copies, waits for them, and re-layouts: 13.1 us -> 6.8 us
  Pallas kernels: 24.2 us -> 30.4 us
  starting transfers between devices: 32.8 us -> 35.9 us
  other arithmetic: 1.57 us -> 3.58 us
    ppermute x11, waiting for transfers between devices: 34.7 us -> 25.4 us  [owner_flip(): return lax.ppermute(value, 'fsdp', [(i, i ^ bits) for i in range(8)])]
    unnamed x28, local copies, waits for them, and re-layouts: 10.7 us -> 4.43 us
    ppermute x5 -> x4, waiting for transfers between devices: 7.48 us -> 2.49 us  [core_flip(): return lax.ppermute(value, 'seq', [(0, 1), (1, 0)])]
    pallas_call x3 -> x2, Pallas kernels: 10.6 us -> 13.5 us  [the longest x1 8.18 us: pair_split(): pl.pallas_call(first_kernel, out_shape=(jax.ShapeDtypeStruct((64, 1024),...]
    pallas_call x1, Pallas kernels: 7.33 us -> 9.58 us  [pair_split(): pl.pallas_call(own_kernel, out_shape=(jax.ShapeDtypeStruct((8, 1024, 256)...]
    all_to_all x2, starting transfers between devices: 9.34 us -> 11.3 us  [zone_exchange(): lax.all_to_all(value, 'fsdp', split_axis=0, concat_axis=0, tiled=True, ax...]
    ppermute x11, starting transfers between devices: 21.1 us -> 22.8 us  [owner_flip(): return lax.ppermute(value, 'fsdp', [(i, i ^ bits) for i in range(8)])]
    pallas_call x1, Pallas kernels: 2.59 us -> 4.21 us  [pair_split(): pl.pallas_call(product_kernel, out_shape=jax.ShapeDtypeStruct((P_SIZE, 10...]
  transfers between devices with their start and end apart: 20 -> 19, of which waited for: 14 -> 12; matrix products, arithmetic and copies ran while one was open for 0% -> 3% of each run, Pallas kernels for 15% -> 14%
where the time goes in v4:
time: 109 us
  starting transfers between devices  35.9 us (33%)
  waiting for transfers between devices  32.1 us (29%)
  Pallas kernels  30.4 us (28%)
  local copies, waits for them, and re-layouts  6.8 us (6%)
  other arithmetic  3.58 us (3%)
    ppermute x11, waiting for transfers between devices, owner_flip(): return lax.ppermute(value, 'fsdp', [(i, i ^ bits) for i in range(8)])  25.4 us
    ppermute x11, starting transfers between devices, owner_flip(): return lax.ppermute(value, 'fsdp', [(i, i ^ bits) for i in range(8)])  22.8 us
    all_to_all x2, starting transfers between devices, zone_exchange(): lax.all_to_all(value, 'fsdp', split_axis=0, concat_axis=0, tiled=True, ax...  11.3 us
    pallas_call x1, Pallas kernels, pair_split(): pl.pallas_call(own_kernel, out_shape=(jax.ShapeDtypeStruct((8, 1024, 256)...  9.58 us
    pallas_call x1, Pallas kernels, pair_split(): pl.pallas_call(first_kernel, out_shape=(jax.ShapeDtypeStruct((64, 1024),...  8.18 us
    pallas_call x1, Pallas kernels, pair_split(): pl.pallas_call(second_kernel, out_shape=(jax.ShapeDtypeStruct((64, 1024),...  5.28 us
    unnamed x28, local copies, waits for them, and re-layouts  4.43 us
    pallas_call x1, Pallas kernels, pair_split(): pl.pallas_call(product_kernel, out_shape=jax.ShapeDtypeStruct((P_SIZE, 10...  4.21 us
  transfers between devices with their start and end apart: 19, of which 12 were waited for; matrix products, arithmetic and copies ran while one was open for 3% of the time, Pallas kernels for 14%

profile of v4, /device:TPU:0, one launch (start us, length us, event | category | flops | bytes accessed | tf_op | source)
XLA Modules:
  0.0 109.0 jit_solution(17410851944933220025)
XLA Ops:
  0.0 2.4 %copy.15 = bf16[8,4,8,2048]{3,2,0,1:T(8,128)(2,1)} copy(bf16[8,4,8,2048]{3,2,1,0:T(8,128)(2,1)} %bitcast.14) | data formatting | bytes 2097152 | tf_op jit(solution)/shard_map/reshape | solution.py:503
  2.4 6.4 %all-to-all-start = ((bf16[4,64,2048]{2,1,0:T(8,128)(2,1)}), bf16[4,64,2048]{2,1,0:T(8,128)(2,1)S(1)}, u32[]{:S(2)}, u32[]{:S(2)}) async-start(bf16[4,64,2048]{2,1,0:T(8,128)(2,1)} %bitcast.13), calls=%async_computation | async-start | bytes 2097152 | tf_op jit(solution)/shard_map/all_to_all | solution.py:494
  8.8 1.3 %broadcast_select_fusion = bf16[160,4096]{1,0:T(8,128)(2,1)} fusion(bf16[160,4096]{1,0:T(8,128)(2,1)S(1)} %copy-done.4, bf16[160,4096]{1,0:T(8,128)(2,1)} %up_ref.1, pred[]{:T(512)S(6)} %eq.13), kind=kLoop, calls=%fused_computation | loop fusion | flops 655360 | bytes 3932161 | tf_op jit(solution)/shard_map/jit(_where)/select_n | solution.py:506
  10.1 1.5 %collective-permute-start = (bf16[160,4096]{1,0:T(8,128)(2,1)}, bf16[160,4096]{1,0:T(8,128)(2,1)S(1)}, u32[]{:S(2)}, u32[]{:S(2)}) collective-permute-start(bf16[160,4096]{1,0:T(8,128)(2,1)} %broadcast_select_fusion), channel_id=1, source_target_pairs={{0,2},{2,0},{4,6},{6,4},{8,10},{10,8},{12,14},{14,12},{1,3},{3,1},... | collective-permute-start | bytes 3932168 | tf_op jit(solution)/shard_map/ppermute | solution.py:488
  13.0 9.6 %own_blocks.1 = (bf16[8,1024,256]{2,1,0:T(8,128)(2,1)}, f32[64,256]{1,0:T(8,128)}) custom-call(s32[4]{0:T(128)} %pad_add_fusion.1.place_ref, s32[3,256]{1,0:T(4,128)} %select_reduce_fusion.inv_ref, bf16[160,4096]{1,0:T(8,128)(2,1)} %gate_ref.1, bf16[160,4096]{1,0:T(8,128)(2,1)} %up_ref.1, bf16[160,4096]{1,0:T(8,128)(2,1)} %down_ref.1, ...), custom_call_target="tpu_custom_call" | custom-call | tf_op jit(solution)/shard_map/own_blocks/pallas_call | solution.py:514
  22.6 2.1 %collective-permute-start.2 = (f32[64,256]{1,0:T(8,128)}, f32[64,256]{1,0:T(8,128)S(1)}, u32[]{:S(2)}, u32[]{:S(2)}) collective-permute-start(f32[64,256]{1,0:T(8,128)} %get-tuple-element.25), channel_id=1, source_target_pairs={{0,4},{2,6},{4,0},{6,2},{8,12},{10,14},{12,8},{14,10},{1,5},{3,7},... | collective-permute-start | bytes 196616 | tf_op jit(solution)/shard_map/ppermute | solution.py:488
  24.7 2.8 %collective-permute-done.2 = f32[64,256]{1,0:T(8,128)S(1)} collective-permute-done((f32[64,256]{1,0:T(8,128)}, f32[64,256]{1,0:T(8,128)S(1)}, u32[]{:S(2)}, u32[]{:S(2)}) %collective-permute-start.2) | collective-permute-done | bytes 65568 | tf_op jit(solution)/shard_map/ppermute | solution.py:488
  28.4 4.5 %collective-permute-start.3 = (f32[64,256]{1,0:T(8,128)S(1)}, f32[64,256]{1,0:T(8,128)S(1)}, u32[]{:S(2)}, u32[]{:S(2)}) collective-permute-start(f32[64,256]{1,0:T(8,128)S(1)} %add.30), channel_id=1, source_target_pairs={{0,8},{2,10},{4,12},{6,14},{8,0},{10,2},{12,4},{14,6},{1,9},{3,11}... | collective-permute-start | bytes 196616 | tf_op jit(solution)/shard_map/ppermute | solution.py:488
  32.8 1.5 %collective-permute-start.1 = (s32[3,256]{1,0:T(4,128)S(1)}, s32[3,256]{1,0:T(4,128)S(1)}, u32[]{:S(2)}, u32[]{:S(2)}) collective-permute-start(s32[3,256]{1,0:T(4,128)S(1)} %copy-done.9), channel_id=1, source_target_pairs={{0,2},{2,0},{4,6},{6,4},{8,10},{10,8},{12,14},{14,12},{1,3},{3,1},... | collective-permute-start | bytes 9224 | tf_op jit(solution)/shard_map/ppermute | solution.py:488
  34.3 3.1 %collective-permute-done.3 = f32[64,256]{1,0:T(8,128)S(1)} collective-permute-done((f32[64,256]{1,0:T(8,128)S(1)}, f32[64,256]{1,0:T(8,128)S(1)}, u32[]{:S(2)}, u32[]{:S(2)}) %collective-permute-start.3) | collective-permute-done | bytes 65568 | tf_op jit(solution)/shard_map/ppermute | solution.py:488
  37.4 4.6 %collective-permute-done.1.inv_ref = s32[3,256]{1,0:T(4,128)S(1)} collective-permute-done((s32[3,256]{1,0:T(4,128)S(1)}, s32[3,256]{1,0:T(4,128)S(1)}, u32[]{:S(2)}, u32[]{:S(2)}) %collective-permute-start.1) | collective-permute-done | bytes 3104 | tf_op jit(solution)/shard_map/ppermute | solution.py:488
  43.5 8.2 %first_partial.1 = (f32[64,1024]{1,0:T(8,128)}, bf16[4,64,1024]{2,1,0:T(8,128)(2,1)}, bf16[4,1024,256]{2,1,0:T(8,128)(2,1)}) custom-call(s32[4]{0:T(128)} %pad_add_fusion.1.place_ref, s32[3,256]{1,0:T(4,128)} %copy-done.10, bf16[160,4096]{1,0:T(8,128)(2,1)} %copy-done.6, bf16[8,1024,256]{2,1,0:T(8,128)(2,1)} %get-tuple-element.29.weight_in_ref.weight_ref, ...), custom_call_target="tpu_custom_call" | custom-call | tf_op jit(solution)/shard_map/first_partial/pallas_call | solution.py:549
  51.7 4.8 %all-to-all-start.1 = ((bf16[4,64,1024]{2,1,0:T(8,128)(2,1)}), bf16[4,64,1024]{2,1,0:T(8,128)(2,1)S(1)}, u32[]{:S(2)}, u32[]{:S(2)}) async-start(bf16[4,64,1024]{2,1,0:T(8,128)(2,1)} %get-tuple-element.32), calls=%async_computation.1 | async-start | bytes 1048576 | tf_op jit(solution)/shard_map/all_to_all | solution.py:494
  56.5 1.5 %collective-permute-start.8 = (f32[64,256]{1,0:T(8,128)S(1)}, f32[64,256]{1,0:T(8,128)S(1)}, u32[]{:S(2)}, u32[]{:S(2)}) collective-permute-start(f32[64,256]{1,0:T(8,128)S(1)} %add.31), channel_id=1, source_target_pairs={{0,2},{2,0},{4,6},{6,4},{8,10},{10,8},{12,14},{14,12},{1,3},{3,1},... | collective-permute-start | bytes 196616 | tf_op jit(solution)/shard_map/ppermute | solution.py:488
  58.0 2.8 %collective-permute-done.8 = f32[64,256]{1,0:T(8,128)S(1)} collective-permute-done((f32[64,256]{1,0:T(8,128)S(1)}, f32[64,256]{1,0:T(8,128)S(1)}, u32[]{:S(2)}, u32[]{:S(2)}) %collective-permute-start.8) | collective-permute-done | bytes 65568 | tf_op jit(solution)/shard_map/ppermute | solution.py:488
  60.9 1.4 %copy-done.5 = bf16[4,1024,256]{2,1,0:T(8,128)(2,1)} copy-done((bf16[4,1024,256]{2,1,0:T(8,128)(2,1)}, bf16[4,1024,256]{2,1,0:T(8,128)(2,1)S(1)}, u32[]{:S(2)}) %copy-start.5) | copy-done | bytes 2097176
  62.3 5.3 %second_partial.1 = (f32[64,1024]{1,0:T(8,128)}, bf16[64,1024]{1,0:T(8,128)(2,1)}, bf16[64,1024]{1,0:T(8,128)(2,1)}, bf16[64,1024]{1,0:T(8,128)(2,1)}) custom-call(s32[4]{0:T(128)} %pad_add_fusion.1.place_ref, bf16[4,1024,256]{2,1,0:T(8,128)(2,1)} %copy-done.5, bf16[8,1024,256]{2,1,0:T(8,128)(2,1)} %get-tuple-element.29.weight_in_ref.weight_ref, ...), custom_call_target="tpu_custom_call" | custom-call | tf_op jit(solution)/shard_map/second_partial/pallas_call | solution.py:575
  67.6 2.1 %collective-permute-start.5 = (bf16[64,1024]{1,0:T(8,128)(2,1)}, bf16[64,1024]{1,0:T(8,128)(2,1)S(1)}, u32[]{:S(2)}, u32[]{:S(2)}) collective-permute-start(bf16[64,1024]{1,0:T(8,128)(2,1)} %get-tuple-element.35), channel_id=1, source_target_pairs={{0,4},{2,6},{4,0},{6,2},{8,12},{10,14},{12,8},{14,10},{1,5},{3,7},... | collective-permute-start | bytes 393224 | tf_op jit(solution)/shard_map/ppermute | solution.py:488
  69.7 2.4 %collective-permute-start.6 = (bf16[64,1024]{1,0:T(8,128)(2,1)}, bf16[64,1024]{1,0:T(8,128)(2,1)S(1)}, u32[]{:S(2)}, u32[]{:S(2)}) collective-permute-start(bf16[64,1024]{1,0:T(8,128)(2,1)} %get-tuple-element.36), channel_id=1, source_target_pairs={{0,8},{2,10},{4,12},{6,14},{8,0},{10,2},{12,4},{14,6},{1,9},{3,11}... | collective-permute-start | bytes 393224 | tf_op jit(solution)/shard_map/ppermute | solution.py:488
  72.1 1.5 %collective-permute-start.10 = (f32[64,256]{1,0:T(8,128)S(1)}, f32[64,256]{1,0:T(8,128)S(1)}, u32[]{:S(2)}, u32[]{:S(2)}) collective-permute-start(f32[64,256]{1,0:T(8,128)S(1)} %add.32.pay0_ref), channel_id=1, source_target_pairs={{0,16},{16,0},{1,17},{17,1},{2,18},{18,2},{3,19},{19,3},{4,20},{20... | collective-permute-start | bytes 196616 | tf_op jit(solution)/shard_map/ppermute | solution.py:545
  73.7 2.7 %collective-permute-done.10.pay2_ref = f32[64,256]{1,0:T(8,128)S(1)} collective-permute-done((f32[64,256]{1,0:T(8,128)S(1)}, f32[64,256]{1,0:T(8,128)S(1)}, u32[]{:S(2)}, u32[]{:S(2)}) %collective-permute-start.10) | collective-permute-done | bytes 65568 | tf_op jit(solution)/shard_map/ppermute | solution.py:545
  76.4 1.5 %collective-permute-done.11.pay3_ref = f32[64,256]{1,0:T(8,128)S(1)} collective-permute-done((f32[64,256]{1,0:T(8,128)S(1)}, f32[64,256]{1,0:T(8,128)S(1)}, u32[]{:S(2)}, u32[]{:S(2)}) %collective-permute-start.11) | collective-permute-done | bytes 65568 | tf_op jit(solution)/shard_map/ppermute | solution.py:546
  77.9 4.9 %collective-permute-done.6.second2_ref = bf16[64,1024]{1,0:T(8,128)(2,1)S(1)} collective-permute-done((bf16[64,1024]{1,0:T(8,128)(2,1)}, bf16[64,1024]{1,0:T(8,128)(2,1)S(1)}, u32[]{:S(2)}, u32[]{:S(2)}) %collective-permute-start.6) | collective-permute-done | bytes 131104 | tf_op jit(solution)/shard_map/ppermute | solution.py:488
  83.8 3.2 %token_sums.1 = (f32[8,2048]{1,0:T(8,128)S(1)}, f32[8,2048]{1,0:T(8,128)S(1)}) custom-call(s32[4]{0:T(128)S(1)} %copy-done.2, f32[64,1024]{1,0:T(8,128)S(1)} %copy-done, bf16[4,64,1024]{2,1,0:T(8,128)(2,1)S(1)} %all-to-all-done.1.first_ref, f32[64,1024]{1,0:T(8,128)S(1)} %copy-done.1, bf16[64,1024]{1,0:T(8,128)(2,1)S(1)} %collective-permute-done.5.second1_ref, ...), custom_call_target="tpu_custom_call" | custom-call | tf_op jit(solution)/shard_map/token_sums/pallas_call | solution.py:593
  87.0 1.2 %collective-permute-done.12 = f32[8,2048]{1,0:T(8,128)S(1)} collective-permute-done((f32[8,2048]{1,0:T(8,128)S(1)}, f32[8,2048]{1,0:T(8,128)S(1)}, u32[]{:S(2)}, u32[]{:S(2)}) %collective-permute-start.12) | collective-permute-done | bytes 65568 | tf_op jit(solution)/shard_map/ppermute | solution.py:491
  88.3 1.6 %collective-permute-start.13 = (f32[8,2048]{1,0:T(8,128)S(1)}, f32[8,2048]{1,0:T(8,128)S(1)}, u32[]{:S(2)}, u32[]{:S(2)}) collective-permute-start(f32[8,2048]{1,0:T(8,128)S(1)} %add.33), channel_id=1, source_target_pairs={{0,2},{2,0},{4,6},{6,4},{8,10},{10,8},{12,14},{14,12},{1,3},{3,1},... | collective-permute-start | bytes 196616 | tf_op jit(solution)/shard_map/ppermute | solution.py:488
  89.8 2.8 %collective-permute-done.13 = f32[8,2048]{1,0:T(8,128)S(1)} collective-permute-done((f32[8,2048]{1,0:T(8,128)S(1)}, f32[8,2048]{1,0:T(8,128)S(1)}, u32[]{:S(2)}, u32[]{:S(2)}) %collective-permute-start.13) | collective-permute-done | bytes 65568 | tf_op jit(solution)/shard_map/ppermute | solution.py:488
  92.6 2.7 %collective-permute-start.14 = (f32[8,2048]{1,0:T(8,128)S(1)}, f32[8,2048]{1,0:T(8,128)S(1)}, u32[]{:S(2)}, u32[]{:S(2)}) collective-permute-start(f32[8,2048]{1,0:T(8,128)S(1)} %add.34), channel_id=1, source_target_pairs={{0,4},{2,6},{4,0},{6,2},{8,12},{10,14},{12,8},{14,10},{1,5},{3,7},... | collective-permute-start | bytes 196616 | tf_op jit(solution)/shard_map/ppermute | solution.py:488
  95.3 2.2 %collective-permute-done.14 = f32[8,2048]{1,0:T(8,128)S(1)} collective-permute-done((f32[8,2048]{1,0:T(8,128)S(1)}, f32[8,2048]{1,0:T(8,128)S(1)}, u32[]{:S(2)}, u32[]{:S(2)}) %collective-permute-start.14) | collective-permute-done | bytes 65568 | tf_op jit(solution)/shard_map/ppermute | solution.py:488
  97.6 3.0 %collective-permute-start.15 = (f32[8,2048]{1,0:T(8,128)S(1)}, f32[8,2048]{1,0:T(8,128)S(1)}, u32[]{:S(2)}, u32[]{:S(2)}) collective-permute-start(f32[8,2048]{1,0:T(8,128)S(1)} %add.35), channel_id=1, source_target_pairs={{0,8},{2,10},{4,12},{6,14},{8,0},{10,2},{12,4},{14,6},{1,9},{3,11}... | collective-permute-start | bytes 196616 | tf_op jit(solution)/shard_map/ppermute | solution.py:488
  100.6 2.2 %collective-permute-done.15 = f32[8,2048]{1,0:T(8,128)S(1)} collective-permute-done((f32[8,2048]{1,0:T(8,128)S(1)}, f32[8,2048]{1,0:T(8,128)S(1)}, u32[]{:S(2)}, u32[]{:S(2)}) %collective-permute-start.15) | collective-permute-done | bytes 65568 | tf_op jit(solution)/shard_map/ppermute | solution.py:488
  104.8 4.2 %products.1 = f32[16,1024]{1,0:T(8,128)} custom-call(s32[4]{0:T(128)} %pad_add_fusion.1.place_ref, f32[8,2048]{1,0:T(8,128)} %copy-done.7, f32[8,2048]{1,0:T(8,128)} %copy-done.8, bf16[8,1024,256]{2,1,0:T(8,128)(2,1)} %get-tuple-element.29.weight_in_ref.weight_ref), custom_call_target="tpu_custom_call" | custom-call | tf_op jit(solution)/shard_map/products/pallas_call | solution.py:614
  (51 shorter events, 7.0 us)
Async XLA Ops:
  2.4 6.5 %copy-start.4 = (bf16[160,4096]{1,0:T(8,128)(2,1)S(1)}, bf16[160,4096]{1,0:T(8,128)(2,1)}, u32[]{:S(2)}) copy-start(bf16[160,4096]{1,0:T(8,128)(2,1)} %gate_ref.1) | copy-start | bytes 3932164
  2.4 39.6 %all-to-all-start = ((bf16[4,64,2048]{2,1,0:T(8,128)(2,1)}), bf16[4,64,2048]{2,1,0:T(8,128)(2,1)S(1)}, u32[]{:S(2)}, u32[]{:S(2)}) async-start(bf16[4,64,2048]{2,1,0:T(8,128)(2,1)} %bitcast.13), calls=%async_computation | async-start | bytes 2097152 | tf_op jit(solution)/shard_map/all_to_all | solution.py:494
  8.8 3.4 %copy-start.11 = (s32[160]{0:T(256)S(1)}, s32[160]{0:T(256)}, u32[]{:S(2)}) copy-start(s32[160]{0:T(256)} %param.16) | copy-start | bytes 1924
  8.8 3.4 %copy-start.12 = (s32[160]{0:T(256)S(1)}, s32[160]{0:T(256)}, u32[]{:S(2)}) copy-start(s32[160]{0:T(256)} %param.14) | copy-start | bytes 1924
  8.8 3.4 %copy-start.13 = (s32[160]{0:T(256)S(1)}, s32[160]{0:T(256)}, u32[]{:S(2)}) copy-start(s32[160]{0:T(256)} %param.12) | copy-start | bytes 1924
  10.1 31.9 %collective-permute-start = (bf16[160,4096]{1,0:T(8,128)(2,1)}, bf16[160,4096]{1,0:T(8,128)(2,1)S(1)}, u32[]{:S(2)}, u32[]{:S(2)}) collective-permute-start(bf16[160,4096]{1,0:T(8,128)(2,1)} %broadcast_select_fusion), channel_id=1, source_target_pairs={{0,2},{2,0},{4,6},{6,4},{8,10},{10,8},{12,14},{14,12},{1,3},{3,1},... | collective-permute-start | bytes 3932168 | tf_op jit(solution)/shard_map/ppermute | solution.py:488
  13.0 19.8 %copy-start.9 = (s32[3,256]{1,0:T(4,128)S(1)}, s32[3,256]{1,0:T(4,128)}, u32[]{:S(2)}) copy-start(s32[3,256]{1,0:T(4,128)} %select_reduce_fusion.inv_ref) | copy-start | bytes 9220
  22.6 4.9 %collective-permute-start.2 = (f32[64,256]{1,0:T(8,128)}, f32[64,256]{1,0:T(8,128)S(1)}, u32[]{:S(2)}, u32[]{:S(2)}) collective-permute-start(f32[64,256]{1,0:T(8,128)} %get-tuple-element.25), channel_id=1, source_target_pairs={{0,4},{2,6},{4,0},{6,2},{8,12},{10,14},{12,8},{14,10},{1,5},{3,7},... | collective-permute-start | bytes 196616 | tf_op jit(solution)/shard_map/ppermute | solution.py:488
  28.4 9.0 %collective-permute-start.3 = (f32[64,256]{1,0:T(8,128)S(1)}, f32[64,256]{1,0:T(8,128)S(1)}, u32[]{:S(2)}, u32[]{:S(2)}) collective-permute-start(f32[64,256]{1,0:T(8,128)S(1)} %add.30), channel_id=1, source_target_pairs={{0,8},{2,10},{4,12},{6,14},{8,0},{10,2},{12,4},{14,6},{1,9},{3,11}... | collective-permute-start | bytes 196616 | tf_op jit(solution)/shard_map/ppermute | solution.py:488
  32.8 9.2 %collective-permute-start.1 = (s32[3,256]{1,0:T(4,128)S(1)}, s32[3,256]{1,0:T(4,128)S(1)}, u32[]{:S(2)}, u32[]{:S(2)}) collective-permute-start(s32[3,256]{1,0:T(4,128)S(1)} %copy-done.9), channel_id=1, source_target_pairs={{0,2},{2,0},{4,6},{6,4},{8,10},{10,8},{12,14},{14,12},{1,3},{3,1},... | collective-permute-start | bytes 9224 | tf_op jit(solution)/shard_map/ppermute | solution.py:488
  42.0 1.1 copy-start.6
  42.0 1.5 %copy-start.3 = (bf16[4,64,2048]{2,1,0:T(8,128)(2,1)}, bf16[4,64,2048]{2,1,0:T(8,128)(2,1)S(1)}, u32[]{:S(2)}) copy-start(bf16[4,64,2048]{2,1,0:T(8,128)(2,1)S(1)} %all-to-all-done.tok_in_ref) | copy-start | bytes 3145732
  51.6 9.3 %collective-permute-start.4 = (bf16[4,1024,256]{2,1,0:T(8,128)(2,1)}, bf16[4,1024,256]{2,1,0:T(8,128)(2,1)S(1)}, u32[]{:S(2)}, u32[]{:S(2)}) collective-permute-start(bf16[4,1024,256]{2,1,0:T(8,128)(2,1)} %get-tuple-element.33), channel_id=1, source_target_pairs={{0,1},{1,0},{2,3},{3,2},{4,5},{5,4},{6,7},{7,6},{8,9},{9,8},{10,11... | collective-permute-start | bytes 6291464 | tf_op jit(solution)/shard_map/ppermute | solution.py:491
  51.7 26.2 %all-to-all-start.1 = ((bf16[4,64,1024]{2,1,0:T(8,128)(2,1)}), bf16[4,64,1024]{2,1,0:T(8,128)(2,1)S(1)}, u32[]{:S(2)}, u32[]{:S(2)}) async-start(bf16[4,64,1024]{2,1,0:T(8,128)(2,1)} %get-tuple-element.32), calls=%async_computation.1 | async-start | bytes 1048576 | tf_op jit(solution)/shard_map/all_to_all | solution.py:494
  56.5 4.3 %collective-permute-start.8 = (f32[64,256]{1,0:T(8,128)S(1)}, f32[64,256]{1,0:T(8,128)S(1)}, u32[]{:S(2)}, u32[]{:S(2)}) collective-permute-start(f32[64,256]{1,0:T(8,128)S(1)} %add.31), channel_id=1, source_target_pairs={{0,2},{2,0},{4,6},{6,4},{8,10},{10,8},{12,14},{14,12},{1,3},{3,1},... | collective-permute-start | bytes 196616 | tf_op jit(solution)/shard_map/ppermute | solution.py:488
  60.8 22.0 %copy-start = (f32[64,1024]{1,0:T(8,128)S(1)}, f32[64,1024]{1,0:T(8,128)}, u32[]{:S(2)}) copy-start(f32[64,1024]{1,0:T(8,128)} %get-tuple-element.31.first_keep_ref) | copy-start | bytes 786436
  60.8 22.0 %copy-start.2 = (s32[4]{0:T(128)S(1)}, s32[4]{0:T(128)}, u32[]{:S(2)}) copy-start(s32[4]{0:T(128)} %pad_add_fusion.1.place_ref) | copy-start | bytes 52
  60.8 12.8 %collective-permute-start.9 = (f32[64,256]{1,0:T(8,128)S(1)}, f32[64,256]{1,0:T(8,128)S(1)}, u32[]{:S(2)}, u32[]{:S(2)}) collective-permute-start(f32[64,256]{1,0:T(8,128)S(1)} %add.32.pay0_ref), channel_id=1, source_target_pairs={{0,1},{1,0},{2,3},{3,2},{4,5},{5,4},{6,7},{7,6},{8,9},{9,8},{10,11... | collective-permute-start | bytes 196616 | tf_op jit(solution)/shard_map/ppermute | solution.py:491
  60.9 1.4 %copy-start.5 = (bf16[4,1024,256]{2,1,0:T(8,128)(2,1)}, bf16[4,1024,256]{2,1,0:T(8,128)(2,1)S(1)}, u32[]{:S(2)}) copy-start(bf16[4,1024,256]{2,1,0:T(8,128)(2,1)S(1)} %collective-permute-done.4.near_in_ref) | copy-start | bytes 6291460
  67.6 10.3 %collective-permute-start.5 = (bf16[64,1024]{1,0:T(8,128)(2,1)}, bf16[64,1024]{1,0:T(8,128)(2,1)S(1)}, u32[]{:S(2)}, u32[]{:S(2)}) collective-permute-start(bf16[64,1024]{1,0:T(8,128)(2,1)} %get-tuple-element.35), channel_id=1, source_target_pairs={{0,4},{2,6},{4,0},{6,2},{8,12},{10,14},{12,8},{14,10},{1,5},{3,7},... | collective-permute-start | bytes 393224 | tf_op jit(solution)/shard_map/ppermute | solution.py:488
  69.7 13.1 %collective-permute-start.6 = (bf16[64,1024]{1,0:T(8,128)(2,1)}, bf16[64,1024]{1,0:T(8,128)(2,1)S(1)}, u32[]{:S(2)}, u32[]{:S(2)}) collective-permute-start(bf16[64,1024]{1,0:T(8,128)(2,1)} %get-tuple-element.36), channel_id=1, source_target_pairs={{0,8},{2,10},{4,12},{6,14},{8,0},{10,2},{12,4},{14,6},{1,9},{3,11}... | collective-permute-start | bytes 393224 | tf_op jit(solution)/shard_map/ppermute | solution.py:488
  72.1 10.7 %collective-permute-start.7 = (bf16[64,1024]{1,0:T(8,128)(2,1)}, bf16[64,1024]{1,0:T(8,128)(2,1)S(1)}, u32[]{:S(2)}, u32[]{:S(2)}) collective-permute-start(bf16[64,1024]{1,0:T(8,128)(2,1)} %get-tuple-element.37), channel_id=1, source_target_pairs={{0,12},{2,14},{4,8},{6,10},{8,4},{10,6},{12,0},{14,2},{1,13},{3,15... | collective-permute-start | bytes 393224 | tf_op jit(solution)/shard_map/ppermute | solution.py:488
  72.1 4.3 %collective-permute-start.10 = (f32[64,256]{1,0:T(8,128)S(1)}, f32[64,256]{1,0:T(8,128)S(1)}, u32[]{:S(2)}, u32[]{:S(2)}) collective-permute-start(f32[64,256]{1,0:T(8,128)S(1)} %add.32.pay0_ref), channel_id=1, source_target_pairs={{0,16},{16,0},{1,17},{17,1},{2,18},{18,2},{3,19},{19,3},{4,20},{20... | collective-permute-start | bytes 196616 | tf_op jit(solution)/shard_map/ppermute | solution.py:545
  73.7 4.2 %collective-permute-start.11 = (f32[64,256]{1,0:T(8,128)S(1)}, f32[64,256]{1,0:T(8,128)S(1)}, u32[]{:S(2)}, u32[]{:S(2)}) collective-permute-start(f32[64,256]{1,0:T(8,128)S(1)} %add.32.pay0_ref), channel_id=1, source_target_pairs={{0,17},{1,16},{16,1},{17,0},{2,19},{3,18},{18,3},{19,2},{4,21},{5,... | collective-permute-start | bytes 196616 | tf_op jit(solution)/shard_map/ppermute | solution.py:546
  82.8 1.0 copy-start.1
  86.9 1.3 %collective-permute-start.12 = (f32[8,2048]{1,0:T(8,128)S(1)}, f32[8,2048]{1,0:T(8,128)S(1)}, u32[]{:S(2)}, u32[]{:S(2)}) collective-permute-start(f32[8,2048]{1,0:T(8,128)S(1)} %get-tuple-element.40), channel_id=1, source_target_pairs={{0,1},{1,0},{2,3},{3,2},{4,5},{5,4},{6,7},{7,6},{8,9},{9,8},{10,11... | collective-permute-start | bytes 196616 | tf_op jit(solution)/shard_map/ppermute | solution.py:491
  88.3 4.3 %collective-permute-start.13 = (f32[8,2048]{1,0:T(8,128)S(1)}, f32[8,2048]{1,0:T(8,128)S(1)}, u32[]{:S(2)}, u32[]{:S(2)}) collective-permute-start(f32[8,2048]{1,0:T(8,128)S(1)} %add.33), channel_id=1, source_target_pairs={{0,2},{2,0},{4,6},{6,4},{8,10},{10,8},{12,14},{14,12},{1,3},{3,1},... | collective-permute-start | bytes 196616 | tf_op jit(solution)/shard_map/ppermute | solution.py:488
  92.6 5.0 %collective-permute-start.14 = (f32[8,2048]{1,0:T(8,128)S(1)}, f32[8,2048]{1,0:T(8,128)S(1)}, u32[]{:S(2)}, u32[]{:S(2)}) collective-permute-start(f32[8,2048]{1,0:T(8,128)S(1)} %add.34), channel_id=1, source_target_pairs={{0,4},{2,6},{4,0},{6,2},{8,12},{10,14},{12,8},{14,10},{1,5},{3,7},... | collective-permute-start | bytes 196616 | tf_op jit(solution)/shard_map/ppermute | solution.py:488
  97.6 5.2 %collective-permute-start.15 = (f32[8,2048]{1,0:T(8,128)S(1)}, f32[8,2048]{1,0:T(8,128)S(1)}, u32[]{:S(2)}, u32[]{:S(2)}) collective-permute-start(f32[8,2048]{1,0:T(8,128)S(1)} %add.35), channel_id=1, source_target_pairs={{0,8},{2,10},{4,12},{6,14},{8,0},{10,2},{12,4},{14,6},{1,9},{3,11}... | collective-permute-start | bytes 196616 | tf_op jit(solution)/shard_map/ppermute | solution.py:488
  102.8 1.3 %copy-start.7 = (f32[8,2048]{1,0:T(8,128)}, f32[8,2048]{1,0:T(8,128)S(1)}, u32[]{:S(2)}) copy-start(f32[8,2048]{1,0:T(8,128)S(1)} %add.36.mine_ref) | copy-start | bytes 196612
  102.8 1.3 %collective-permute-start.16 = (f32[8,2048]{1,0:T(8,128)S(1)}, f32[8,2048]{1,0:T(8,128)S(1)}, u32[]{:S(2)}, u32[]{:S(2)}) collective-permute-start(f32[8,2048]{1,0:T(8,128)S(1)} %add.36.mine_ref), channel_id=1, source_target_pairs={{0,1},{1,0},{2,3},{3,2},{4,5},{5,4},{6,7},{7,6},{8,9},{9,8},{10,11... | collective-permute-start | bytes 196616 | tf_op jit(solution)/shard_map/ppermute | solution.py:491
  104.2 0.6 copy-start.8
  (1 other events, 0.6 us)

commit v5 on v4

--- a/solution.py
+++ b/solution.py
@@ -17,12 +17,13 @@
 VMEM = pl.BlockSpec(memory_space=pltpu.VMEM)
 SMEM = pl.BlockSpec(memory_space=pltpu.SMEM)
 HBM = pl.BlockSpec(memory_space=pltpu.HBM)
+ANY = pl.BlockSpec(memory_space=pl.ANY)
 
 STRIDE = 168
 
 
 def params(mebibytes):
-    return pltpu.CompilerParams(vmem_limit_bytes=mebibytes * 1024 * 1024)
+    return pltpu.CompilerParams(vmem_limit_bytes=int(mebibytes * 1024 * 1024))
 
 
 def unpack(blocks, slot_ids, cell_total):
@@ -175,6 +176,38 @@
             row = pl.multiple_of(block_row * BLK, BLK)
             put(pair, row, even)
             put(pair, row + BLK // 2, odd)
+
+
+def head_kernel(
+    place_ref, tok_in_ref, gate_ref, up_ref, zone_out_ref, kind_out_ref, tok_ref, blocks_ref, sem
+):
+    core = place_ref[3]
+
+    @pl.when(core == 0)
+    def _():
+        pltpu.make_async_copy(gate_ref, blocks_ref, sem.at[0]).start()
+
+    @pl.when(core != 0)
+    def _():
+        pltpu.make_async_copy(up_ref, blocks_ref, sem.at[0]).start()
+
+    loads, stores = [], []
+    for zone in range(4):
+        held = tok_ref.at[zone]
+        lanes = pl.ds(2048 * zone, 2048)
+        loads.append(pltpu.make_async_copy(tok_in_ref.at[:, lanes], held, sem.at[2 + zone]))
+        stores.append(pltpu.make_async_copy(held, zone_out_ref.at[zone], sem.at[6 + zone]))
+    for load in loads:
+        load.start()
+    pltpu.make_async_copy(gate_ref, blocks_ref, sem.at[0]).wait()
+    kind_store = pltpu.make_async_copy(blocks_ref, kind_out_ref, sem.at[1])
+    kind_store.start()
+    for load, store in zip(loads, stores):
+        load.wait()
+        store.start()
+    for store in stores:
+        store.wait()
+    kind_store.wait()
 
 
 def own_kernel(
@@ -272,17 +305,14 @@
     return low_bit + 2 * lax.rem(two_bits // 2 + flip // 2, 2)
 
 
-def shuffle_tokens(zone, side, tok_ref, tokens_ref):
+def shuffle_tokens(side, tok_ref, tokens_ref):
     shuffle = shuffle_matrix(256)
-    for source in range(4):
-        spot = flipped(zone, source)
-        for group in range(8):
-            piece = tok_ref[spot, :, 256 * group : 256 * (group + 1)]
-            moved = dot(piece, shuffle).astype(BF)
-            half = lax.rem(group // 4 + side, 2)
-            tokens_ref[
-                half, 64 * source : 64 * (source + 1), 256 * (group % 4) : 256 * (group % 4 + 1)
-            ] = moved
+    for group in range(8):
+        piece = tok_ref[:, :, 256 * group : 256 * (group + 1)].reshape(256, 256)
+        half = lax.rem(group // 4 + side, 2)
+        tokens_ref[half, :, 256 * (group % 4) : 256 * (group % 4 + 1)] = dot(piece, shuffle).astype(
+            BF
+        )
 
 
 def first_kernel(
@@ -301,6 +331,7 @@
     tok_ref,
     tokens_ref,
     sent_ref,
+    total_ref,
     in_sem,
     near_sem,
     sent_sem,
@@ -327,15 +358,15 @@
     near_store = pltpu.make_async_copy(near_ref, near_out_ref, near_sem)
     near_store.start()
     loads[1].wait()
-    shuffle_tokens(zone, side, tok_ref, tokens_ref)
+    shuffle_tokens(side, tok_ref, tokens_ref)
     loads[2].wait()
     stores = []
     for chunk in range(4):
         total = dot(tokens_ref[0], own_ref[chunk]) + dot(tokens_ref[1], near_ref[chunk])
         cols = slice(256 * chunk, 256 * (chunk + 1))
-        keep_ref[:, cols] = total[:64]
-        for flip in range(4):
-            sent_ref[flipped(zone, flip), :, cols] = total[64 * flip : 64 * (flip + 1)].astype(BF)
+        total_ref[...] = total
+        keep_ref[:, cols] = total_ref[pl.ds(pl.multiple_of(64 * zone, 64), 64), :]
+        sent_ref[:, :, cols] = total.astype(BF).reshape(4, 64, 256)
         lanes = pl.ds(256 * chunk, 256)
         store = pltpu.make_async_copy(
             sent_ref.at[:, :, lanes], sent_out_ref.at[:, :, lanes], sent_sem.at[chunk]
@@ -360,6 +391,7 @@
     own_ref,
     tok_ref,
     tokens_ref,
+    total_ref,
     in_sem,
 ):
     zone = place_ref[0] // 2
@@ -373,15 +405,17 @@
     for load in loads:
         load.start()
     loads[0].wait()
-    shuffle_tokens(zone, side, tok_ref, tokens_ref)
+    shuffle_tokens(side, tok_ref, tokens_ref)
     loads[1].wait()
     loads[2].wait()
     for chunk in range(4):
         total = dot(tokens_ref[0], own_ref[chunk]) + dot(tokens_ref[1], near_ref[chunk])
         cols = slice(256 * chunk, 256 * (chunk + 1))
-        keep_ref[:, cols] = total[:64]
+        total_ref[...] = total
+        keep_ref[:, cols] = total_ref[pl.ds(pl.multiple_of(64 * zone, 64), 64), :]
         for flip, ref in enumerate((out1_ref, out2_ref, out3_ref), 1):
-            ref[:, cols] = total[64 * flip : 64 * (flip + 1)].astype(BF)
+            row = pl.multiple_of(64 * flipped(zone, flip), 64)
+            ref[:, cols] = total_ref[pl.ds(row, 64), :].astype(BF)
 
 
 def middle_kernel(
@@ -396,15 +430,20 @@
     pay1_ref,
     pay2_ref,
     pay3_ref,
+    weight_in_ref,
     mine_ref,
     theirs_ref,
+    weight_out_ref,
     lead_ref,
     act_ref,
     pay_ref,
     proj_ref,
     tangent_ref,
     rows_ref,
+    weight_sem,
 ):
+    weight_copy = pltpu.make_async_copy(weight_in_ref, weight_out_ref, weight_sem)
+    weight_copy.start()
     zone = place_ref[0] // 2
     quarter = place_ref[1]
     core = place_ref[3]
@@ -442,23 +481,17 @@
         row = slice(step % 8, step % 8 + 1)
         target[row, :1024] = jnp.sum(backward * lead_ref[...], axis=0, keepdims=True)
         target[row, 1024:] = jnp.sum(backward * act_ref[...], axis=0, keepdims=True)
-
-
-def product_kernel(place_ref, mine_ref, theirs_ref, weight_ref, out_ref, sum_ref, held_ref, sem):
+    weight_copy.wait()
+
+
+def product_kernel(place_ref, mine_ref, theirs_ref, weight_ref, out_ref, sum_ref):
     core = place_ref[3]
-    loads = [
-        pltpu.make_async_copy(weight_ref.at[chunk], held_ref.at[chunk], sem.at[chunk])
-        for chunk in range(8)
-    ]
-    for load in loads:
-        load.start()
     sum_ref[core] = mine_ref[...]
     sum_ref[1 - core] = theirs_ref[...]
     sums = jnp.concatenate([sum_ref[0], sum_ref[1]], axis=0).astype(BF)
     total = None
     for chunk in range(8):
-        loads[chunk].wait()
-        term = contract_last(sums[:, 256 * chunk : 256 * (chunk + 1)], held_ref[chunk])
+        term = contract_last(sums[:, 256 * chunk : 256 * (chunk + 1)], weight_ref[chunk])
         total = term if total is None else total + term
     unshuffle = unshuffle_matrix(256)
     for group in range(4):
@@ -500,10 +533,24 @@
             axis_index_groups=[[0, 2, 4, 6], [1, 3, 5, 7]],
         )
 
-    by_zone = tokens.reshape(64, 4, 2048).transpose(1, 0, 2)
-    by_zone, gate_source, up_source = lax.optimization_barrier((by_zone, gate_blocks, up_blocks))
+    by_zone, kind = pl.pallas_call(
+        head_kernel,
+        out_shape=(
+            jax.ShapeDtypeStruct((4, 64, 2048), BF),
+            jax.ShapeDtypeStruct((160, 4096), BF),
+        ),
+        in_specs=[SMEM, HBM, HBM, HBM],
+        out_specs=(HBM, HBM),
+        scratch_shapes=[
+            pltpu.VMEM((4, 64, 2048), BF),
+            pltpu.VMEM((160, 4096), BF),
+            pltpu.SemaphoreType.DMA((10,)),
+        ],
+        compiler_params=params(60),
+        name="head",
+    )(place, tokens, gate_blocks, up_blocks)
+    near = owner_flip(kind, 1)
     gathered = zone_exchange(by_zone)
-    near = owner_flip(jnp.where(core == 0, gate_source, up_source), 1)
 
     slots = jnp.stack([gate_slot, up_slot, down_slot])
     cells = lax.broadcasted_iota(jnp.int32, (3, 160, 256), 2)
@@ -538,14 +585,6 @@
     near, near_inv, payload, gathered = lax.optimization_barrier(
         (near, near_inv, payload, gathered)
     )
-    payload = payload + owner_flip(payload, 1)
-    pay_parts = [
-        payload,
-        core_flip(payload),
-        lax.ppermute(payload, "groups", [(0, 1), (1, 0)]),
-        lax.ppermute(payload, ("groups", "seq"), [(i, i ^ 3) for i in range(4)]),
-    ]
-
     first_keep, first_sent, near_weights = pl.pallas_call(
         first_kernel,
         out_shape=(
@@ -553,7 +592,7 @@
             jax.ShapeDtypeStruct((4, 64, 1024), BF),
             jax.ShapeDtypeStruct((4, 1024, 256), BF),
         ),
-        in_specs=[SMEM, SMEM, HBM, HBM, HBM],
+        in_specs=[SMEM, SMEM, ANY, HBM, ANY],
         out_specs=(VMEM, HBM, HBM),
         scratch_shapes=[
             pltpu.VMEM((160, 4096), BF),
@@ -563,11 +602,12 @@
             pltpu.VMEM((4, 64, 2048), BF),
             pltpu.VMEM((2, 256, 1024), BF),
             pltpu.VMEM((4, 64, 1024), BF),
+            pltpu.VMEM((256, 256), F32),
             pltpu.SemaphoreType.DMA((3,)),
             pltpu.SemaphoreType.DMA,
             pltpu.SemaphoreType.DMA((4,)),
         ],
-        compiler_params=params(60),
+        compiler_params=params(50),
         name="first_partial",
     )(place, near_inv, near, weights, gathered)
     first_back = zone_exchange(first_sent)
@@ -576,25 +616,36 @@
         second_kernel,
         out_shape=(jax.ShapeDtypeStruct((64, 1024), F32),)
         + (jax.ShapeDtypeStruct((64, 1024), BF),) * 3,
-        in_specs=[SMEM, HBM, HBM, HBM],
+        in_specs=[SMEM, ANY, HBM, ANY],
         out_specs=(VMEM,) * 4,
         scratch_shapes=[
             pltpu.VMEM((4, 1024, 256), BF),
             pltpu.VMEM((4, 1024, 256), BF),
             pltpu.VMEM((4, 64, 2048), BF),
             pltpu.VMEM((2, 256, 1024), BF),
+            pltpu.VMEM((256, 256), F32),
             pltpu.SemaphoreType.DMA((3,)),
         ],
-        compiler_params=params(59),
+        compiler_params=params(50),
         name="second_partial",
     )(place, core_flip(near_weights), weights, gathered)
     second_back = [owner_flip(second_sent[flip - 1], 2 * flip) for flip in (1, 2, 3)]
 
-    mine, theirs = pl.pallas_call(
+    second_back[0], payload = lax.optimization_barrier((second_back[0], payload))
+    payload = payload + owner_flip(payload, 1)
+    pay_parts = [
+        payload,
+        core_flip(payload),
+        lax.ppermute(payload, "groups", [(0, 1), (1, 0)]),
+        lax.ppermute(payload, ("groups", "seq"), [(i, i ^ 3) for i in range(4)]),
+    ]
+
+    mine, theirs, weights_at_hand = pl.pallas_call(
         middle_kernel,
-        out_shape=(jax.ShapeDtypeStruct((8, 2048), F32),) * 2,
-        in_specs=[SMEM] + [VMEM] * 10,
-        out_specs=(VMEM, VMEM),
+        out_shape=(jax.ShapeDtypeStruct((8, 2048), F32),) * 2
+        + (jax.ShapeDtypeStruct((8, 1024, 256), BF),),
+        in_specs=[SMEM] + [VMEM] * 10 + [HBM],
+        out_specs=(VMEM,) * 3,
         scratch_shapes=[
             pltpu.VMEM((64, 1024), F32),
             pltpu.VMEM((64, 1024), F32),
@@ -602,10 +653,11 @@
             pltpu.VMEM((K, 1024), BF),
             pltpu.VMEM((64 * P_SIZE, 1024), BF),
             pltpu.VMEM((64 * P_SIZE, K), BF),
+            pltpu.SemaphoreType.DMA,
         ],
-        compiler_params=params(16),
+        compiler_params=params(48),
         name="token_sums",
-    )(place, first_keep, first_back, second_keep, *second_back, *pay_parts)
+    )(place, first_keep, first_back, second_keep, *second_back, *pay_parts, weights)
 
     sums = mine + core_flip(theirs)
     for bits in (1, 2, 4):
@@ -614,16 +666,12 @@
     return pl.pallas_call(
         product_kernel,
         out_shape=jax.ShapeDtypeStruct((P_SIZE, 1024), F32),
-        in_specs=[SMEM, VMEM, VMEM, HBM],
+        in_specs=[SMEM, VMEM, VMEM, VMEM],
         out_specs=VMEM,
-        scratch_shapes=[
-            pltpu.VMEM((2, 8, 2048), F32),
-            pltpu.VMEM((8, 1024, 256), BF),
-            pltpu.SemaphoreType.DMA((8,)),
-        ],
-        compiler_params=params(59),
+        scratch_shapes=[pltpu.VMEM((2, 8, 2048), F32)],
+        compiler_params=params(30),
         name="products",
-    )(place, sums, core_flip(sums), weights)
+    )(place, sums, core_flip(sums), weights_at_hand)
 
 
 def per_device(tokens, gate_blocks, *rest):

time: 109 us -> 102 us (0.936)
  local copies, waits for them, and re-layouts: 6.8 us -> 0.03 us
  waiting for transfers between devices: 32.1 us -> 28 us
  starting transfers between devices: 35.9 us -> 39.8 us
  other arithmetic: 3.58 us -> 2.3 us
    unnamed x28 -> x10, local copies, waits for them, and re-layouts: 4.43 us -> 0.03 us
    ppermute x11, starting transfers between devices: 22.8 us -> 26.4 us  [owner_flip(): return lax.ppermute(value, 'fsdp', [(i, i ^ bits) for i in range(8)])]
    pallas_call x0 -> x1, Pallas kernels: none -> 3.53 us  [pair_split(): pl.pallas_call(head_kernel, out_shape=(jax.ShapeDtypeStruct((4, 64, 2048)...]
    ppermute x1, waiting for transfers between devices: 2.74 us -> 0.01 us  [pair_split(): lax.ppermute(payload, 'groups', [(0, 1), (1, 0)])]
    reshape x1 -> x0, local copies, waits for them, and re-layouts: 2.37 us -> none  [pair_split(): by_zone = tokens.reshape(64, 4, 2048).transpose(1, 0, 2)]
    pallas_call x1, Pallas kernels: 8.18 us -> 5.87 us  [pair_split(): pl.pallas_call(first_kernel, out_shape=(jax.ShapeDtypeStruct((64, 1024),...]
    pallas_call x1, Pallas kernels: 3.15 us -> 5.13 us  [pair_split(): pl.pallas_call(middle_kernel, out_shape=(jax.ShapeDtypeStruct((8, 2048),...]
    pallas_call x1, Pallas kernels: 4.21 us -> 2.59 us  [pair_split(): pl.pallas_call(product_kernel, out_shape=jax.ShapeDtypeStruct((P_SIZE, 10...]
  transfers between devices with their start and end apart: 19 -> 19, of which waited for: 12 -> 10; matrix products, arithmetic and copies ran while one was open for 3% -> 2% of each run, Pallas kernels for 14% -> 14%
where the time goes in v5:
time: 102 us; the launch traced here: 101 us
  starting transfers between devices  39.8 us (39%)
  Pallas kernels  31 us (30%)
  waiting for transfers between devices  28 us (27%)
  other arithmetic  2.3 us (2%)
    ppermute x11, starting transfers between devices, owner_flip(): return lax.ppermute(value, 'fsdp', [(i, i ^ bits) for i in range(8)])  26.4 us
    ppermute x11, waiting for transfers between devices, owner_flip(): return lax.ppermute(value, 'fsdp', [(i, i ^ bits) for i in range(8)])  25.5 us
    all_to_all x2, starting transfers between devices, zone_exchange(): lax.all_to_all(value, 'fsdp', split_axis=0, concat_axis=0, tiled=True, ax...  11.3 us
    pallas_call x1, Pallas kernels, pair_split(): pl.pallas_call(own_kernel, out_shape=(jax.ShapeDtypeStruct((8, 1024, 256)...  9.59 us
    pallas_call x1, Pallas kernels, pair_split(): pl.pallas_call(first_kernel, out_shape=(jax.ShapeDtypeStruct((64, 1024),...  5.87 us
    pallas_call x1, Pallas kernels, pair_split(): pl.pallas_call(middle_kernel, out_shape=(jax.ShapeDtypeStruct((8, 2048),...  5.13 us
    pallas_call x1, Pallas kernels, pair_split(): pl.pallas_call(second_kernel, out_shape=(jax.ShapeDtypeStruct((64, 1024),...  4.25 us
    pallas_call x1, Pallas kernels, pair_split(): pl.pallas_call(head_kernel, out_shape=(jax.ShapeDtypeStruct((4, 64, 2048)...  3.53 us
  transfers between devices with their start and end apart: 19, of which 10 were waited for; matrix products, arithmetic and copies ran while one was open for 2% of the time, Pallas kernels for 14%

profile of v5, /device:TPU:0, one launch (start us, length us, event | category | flops | bytes accessed | tf_op | source)
XLA Modules:
  0.0 101.2 jit_solution(3178953371134486701)
XLA Ops:
  0.6 3.5 %head.1 = (bf16[4,64,2048]{2,1,0:T(8,128)(2,1)}, bf16[160,4096]{1,0:T(8,128)(2,1)}) custom-call(s32[4]{0:T(128)} %pad_add_fusion.1.place_ref, bf16[64,8192]{1,0:T(8,128)(2,1)} %tok_in_ref.1, bf16[160,4096]{1,0:T(8,128)(2,1)} %gate_ref.3, bf16[160,4096]{1,0:T(8,128)(2,1)} %up_ref.3), custom_call_target="tpu_custom_call" | custom-call | tf_op jit(solution)/shard_map/head/pallas_call | solution.py:536
  4.2 6.5 %all-to-all-start = ((bf16[4,64,2048]{2,1,0:T(8,128)(2,1)}), bf16[4,64,2048]{2,1,0:T(8,128)(2,1)S(1)}, u32[]{:S(2)}, u32[]{:S(2)}) async-start(bf16[4,64,2048]{2,1,0:T(8,128)(2,1)} %get-tuple-element.27), calls=%async_computation | async-start | bytes 2097152 | tf_op jit(solution)/shard_map/all_to_all | solution.py:527
  10.7 1.5 %collective-permute-start = (bf16[160,4096]{1,0:T(8,128)(2,1)}, bf16[160,4096]{1,0:T(8,128)(2,1)S(1)}, u32[]{:S(2)}, u32[]{:S(2)}) collective-permute-start(bf16[160,4096]{1,0:T(8,128)(2,1)} %get-tuple-element.25), channel_id=1, source_target_pairs={{0,2},{2,0},{4,6},{6,4},{8,10},{10,8},{12,14},{14,12},{1,3},{3,1},... | collective-permute-start | bytes 3932168 | tf_op jit(solution)/shard_map/ppermute | solution.py:521
  12.2 0.7 select_reduce_fusion.inv_ref
  12.9 9.6 %own_blocks.1 = (bf16[8,1024,256]{2,1,0:T(8,128)(2,1)}, f32[64,256]{1,0:T(8,128)}) custom-call(s32[4]{0:T(128)} %pad_add_fusion.1.place_ref, s32[3,256]{1,0:T(4,128)} %select_reduce_fusion.inv_ref, bf16[160,4096]{1,0:T(8,128)(2,1)} %gate_ref.3, bf16[160,4096]{1,0:T(8,128)(2,1)} %up_ref.3, bf16[160,4096]{1,0:T(8,128)(2,1)} %down_ref.1, ...), custom_call_target="tpu_custom_call" | custom-call | tf_op jit(solution)/shard_map/own_blocks/pallas_call | solution.py:561
  22.5 2.1 %collective-permute-start.2 = (f32[64,256]{1,0:T(8,128)}, f32[64,256]{1,0:T(8,128)S(1)}, u32[]{:S(2)}, u32[]{:S(2)}) collective-permute-start(f32[64,256]{1,0:T(8,128)} %get-tuple-element.26), channel_id=1, source_target_pairs={{0,4},{2,6},{4,0},{6,2},{8,12},{10,14},{12,8},{14,10},{1,5},{3,7},... | collective-permute-start | bytes 196616 | tf_op jit(solution)/shard_map/ppermute | solution.py:521
  24.6 4.6 %collective-permute-done.2 = f32[64,256]{1,0:T(8,128)S(1)} collective-permute-done((f32[64,256]{1,0:T(8,128)}, f32[64,256]{1,0:T(8,128)S(1)}, u32[]{:S(2)}, u32[]{:S(2)}) %collective-permute-start.2) | collective-permute-done | bytes 65568 | tf_op jit(solution)/shard_map/ppermute | solution.py:521
  29.2 0.9 add.30
  30.1 4.5 %collective-permute-start.3 = (f32[64,256]{1,0:T(8,128)S(1)}, f32[64,256]{1,0:T(8,128)S(1)}, u32[]{:S(2)}, u32[]{:S(2)}) collective-permute-start(f32[64,256]{1,0:T(8,128)S(1)} %add.30), channel_id=1, source_target_pairs={{0,8},{2,10},{4,12},{6,14},{8,0},{10,2},{12,4},{14,6},{1,9},{3,11}... | collective-permute-start | bytes 196616 | tf_op jit(solution)/shard_map/ppermute | solution.py:521
  34.6 1.5 %collective-permute-start.1 = (s32[3,256]{1,0:T(4,128)S(1)}, s32[3,256]{1,0:T(4,128)S(1)}, u32[]{:S(2)}, u32[]{:S(2)}) collective-permute-start(s32[3,256]{1,0:T(4,128)S(1)} %copy-done.1), channel_id=1, source_target_pairs={{0,2},{2,0},{4,6},{6,4},{8,10},{10,8},{12,14},{14,12},{1,3},{3,1},... | collective-permute-start | bytes 9224 | tf_op jit(solution)/shard_map/ppermute | solution.py:521
  36.1 3.1 %collective-permute-done.3 = f32[64,256]{1,0:T(8,128)S(1)} collective-permute-done((f32[64,256]{1,0:T(8,128)S(1)}, f32[64,256]{1,0:T(8,128)S(1)}, u32[]{:S(2)}, u32[]{:S(2)}) %collective-permute-start.3) | collective-permute-done | bytes 65568 | tf_op jit(solution)/shard_map/ppermute | solution.py:521
  39.2 2.0 %collective-permute-done.1.inv_ref = s32[3,256]{1,0:T(4,128)S(1)} collective-permute-done((s32[3,256]{1,0:T(4,128)S(1)}, s32[3,256]{1,0:T(4,128)S(1)}, u32[]{:S(2)}, u32[]{:S(2)}) %collective-permute-start.1) | collective-permute-done | bytes 3104 | tf_op jit(solution)/shard_map/ppermute | solution.py:521
  41.2 5.9 %first_partial.1 = (f32[64,1024]{1,0:T(8,128)S(1)}, bf16[4,64,1024]{2,1,0:T(8,128)(2,1)}, bf16[4,1024,256]{2,1,0:T(8,128)(2,1)}) custom-call(s32[4]{0:T(128)S(1)} %copy-done, s32[3,256]{1,0:T(4,128)S(1)} %collective-permute-done.1.inv_ref, bf16[160,4096]{1,0:T(8,128)(2,1)S(1)} %collective-permute-done.blocks_in_ref, ...), custom_call_target="tpu_custom_call" | custom-call | tf_op jit(solution)/shard_map/first_partial/pallas_call | solution.py:588
  47.2 4.8 %all-to-all-start.1 = ((bf16[4,64,1024]{2,1,0:T(8,128)(2,1)}), bf16[4,64,1024]{2,1,0:T(8,128)(2,1)S(1)}, u32[]{:S(2)}, u32[]{:S(2)}) async-start(bf16[4,64,1024]{2,1,0:T(8,128)(2,1)} %get-tuple-element.33), calls=%async_computation.1 | async-start | bytes 1048576 | tf_op jit(solution)/shard_map/all_to_all | solution.py:527
  52.0 4.2 %second_partial.1 = (f32[64,1024]{1,0:T(8,128)S(1)}, bf16[64,1024]{1,0:T(8,128)(2,1)S(1)}, bf16[64,1024]{1,0:T(8,128)(2,1)S(1)}, bf16[64,1024]{1,0:T(8,128)(2,1)S(1)}) custom-call(s32[4]{0:T(128)S(1)} %copy-done, bf16[4,1024,256]{2,1,0:T(8,128)(2,1)} %collective-permute-done.4.near_in_ref, bf16[8,1024,256]{2,1,0:T(8,128)(2,1)} %get-tuple-element.30.weight_in_ref, ...), custom_call_target="tpu_custom_call" | custom-call | tf_op jit(solution)/shard_map/second_partial/pallas_call | solution.py:615
  56.3 2.1 %collective-permute-start.5 = (bf16[64,1024]{1,0:T(8,128)(2,1)S(1)}, bf16[64,1024]{1,0:T(8,128)(2,1)S(1)}, u32[]{:S(2)}, u32[]{:S(2)}) collective-permute-start(bf16[64,1024]{1,0:T(8,128)(2,1)S(1)} %get-tuple-element.36), channel_id=1, source_target_pairs={{0,4},{2,6},{4,0},{6,2},{8,12},{10,14},{12,8},{14,10},{1,5},{3,7},... | collective-permute-start | bytes 393224 | tf_op jit(solution)/shard_map/ppermute | solution.py:521
  58.4 2.4 %collective-permute-start.6 = (bf16[64,1024]{1,0:T(8,128)(2,1)S(1)}, bf16[64,1024]{1,0:T(8,128)(2,1)S(1)}, u32[]{:S(2)}, u32[]{:S(2)}) collective-permute-start(bf16[64,1024]{1,0:T(8,128)(2,1)S(1)} %get-tuple-element.39), channel_id=1, source_target_pairs={{0,8},{2,10},{4,12},{6,14},{8,0},{10,2},{12,4},{14,6},{1,9},{3,11}... | collective-permute-start | bytes 393224 | tf_op jit(solution)/shard_map/ppermute | solution.py:521
  60.7 3.8 %collective-permute-done.5.second1_ref = bf16[64,1024]{1,0:T(8,128)(2,1)S(1)} collective-permute-done((bf16[64,1024]{1,0:T(8,128)(2,1)S(1)}, bf16[64,1024]{1,0:T(8,128)(2,1)S(1)}, u32[]{:S(2)}, u32[]{:S(2)}) %collective-permute-start.5) | collective-permute-done | bytes 131104 | tf_op jit(solution)/shard_map/ppermute | solution.py:521
  64.5 1.5 %collective-permute-start.8 = (f32[64,256]{1,0:T(8,128)S(1)}, f32[64,256]{1,0:T(8,128)S(1)}, u32[]{:S(2)}, u32[]{:S(2)}) collective-permute-start(f32[64,256]{1,0:T(8,128)S(1)} %add.31), channel_id=1, source_target_pairs={{0,2},{2,0},{4,6},{6,4},{8,10},{10,8},{12,14},{14,12},{1,3},{3,1},... | collective-permute-start | bytes 196616 | tf_op jit(solution)/shard_map/ppermute | solution.py:521
  66.0 3.9 %collective-permute-start.7 = (bf16[64,1024]{1,0:T(8,128)(2,1)S(1)}, bf16[64,1024]{1,0:T(8,128)(2,1)S(1)}, u32[]{:S(2)}, u32[]{:S(2)}) collective-permute-start(bf16[64,1024]{1,0:T(8,128)(2,1)S(1)} %get-tuple-element.40), channel_id=1, source_target_pairs={{0,12},{2,14},{4,8},{6,10},{8,4},{10,6},{12,0},{14,2},{1,13},{3,15... | collective-permute-start | bytes 393224 | tf_op jit(solution)/shard_map/ppermute | solution.py:521
  70.0 1.6 %collective-permute-start.10 = (f32[64,256]{1,0:T(8,128)S(1)}, f32[64,256]{1,0:T(8,128)S(1)}, u32[]{:S(2)}, u32[]{:S(2)}) collective-permute-start(f32[64,256]{1,0:T(8,128)S(1)} %add.32.pay0_ref), channel_id=1, source_target_pairs={{0,16},{16,0},{1,17},{17,1},{2,18},{18,2},{3,19},{19,3},{4,20},{20... | collective-permute-start | bytes 196616 | tf_op jit(solution)/shard_map/ppermute | solution.py:639
  71.8 4.5 %collective-permute-done.6.second2_ref = bf16[64,1024]{1,0:T(8,128)(2,1)S(1)} collective-permute-done((bf16[64,1024]{1,0:T(8,128)(2,1)S(1)}, bf16[64,1024]{1,0:T(8,128)(2,1)S(1)}, u32[]{:S(2)}, u32[]{:S(2)}) %collective-permute-start.6) | collective-permute-done | bytes 131104 | tf_op jit(solution)/shard_map/ppermute | solution.py:521
  76.3 5.1 %token_sums.1 = (f32[8,2048]{1,0:T(8,128)S(1)}, f32[8,2048]{1,0:T(8,128)S(1)}, bf16[8,1024,256]{2,1,0:T(8,128)(2,1)S(1)}) custom-call(s32[4]{0:T(128)S(1)} %copy-done, f32[64,1024]{1,0:T(8,128)S(1)} %get-tuple-element.32.first_keep_ref, bf16[4,64,1024]{2,1,0:T(8,128)(2,1)S(1)} %all-to-all-done.1.first_ref, f32[64,1024]{1,0:T(8,128)S(1)} %get-tuple-element.35.second_keep_ref, ...), custom_call_target="tpu_custom_call" | custom-call | tf_op jit(solution)/shard_map/token_sums/pallas_call | solution.py:643
  81.5 1.2 %collective-permute-done.12 = f32[8,2048]{1,0:T(8,128)S(1)} collective-permute-done((f32[8,2048]{1,0:T(8,128)S(1)}, f32[8,2048]{1,0:T(8,128)S(1)}, u32[]{:S(2)}, u32[]{:S(2)}) %collective-permute-start.12) | collective-permute-done | bytes 65568 | tf_op jit(solution)/shard_map/ppermute | solution.py:524
  82.8 1.6 %collective-permute-start.13 = (f32[8,2048]{1,0:T(8,128)S(1)}, f32[8,2048]{1,0:T(8,128)S(1)}, u32[]{:S(2)}, u32[]{:S(2)}) collective-permute-start(f32[8,2048]{1,0:T(8,128)S(1)} %add.33), channel_id=1, source_target_pairs={{0,2},{2,0},{4,6},{6,4},{8,10},{10,8},{12,14},{14,12},{1,3},{3,1},... | collective-permute-start | bytes 196616 | tf_op jit(solution)/shard_map/ppermute | solution.py:521
  84.4 2.8 %collective-permute-done.13 = f32[8,2048]{1,0:T(8,128)S(1)} collective-permute-done((f32[8,2048]{1,0:T(8,128)S(1)}, f32[8,2048]{1,0:T(8,128)S(1)}, u32[]{:S(2)}, u32[]{:S(2)}) %collective-permute-start.13) | collective-permute-done | bytes 65568 | tf_op jit(solution)/shard_map/ppermute | solution.py:521
  87.1 2.7 %collective-permute-start.14 = (f32[8,2048]{1,0:T(8,128)S(1)}, f32[8,2048]{1,0:T(8,128)S(1)}, u32[]{:S(2)}, u32[]{:S(2)}) collective-permute-start(f32[8,2048]{1,0:T(8,128)S(1)} %add.34), channel_id=1, source_target_pairs={{0,4},{2,6},{4,0},{6,2},{8,12},{10,14},{12,8},{14,10},{1,5},{3,7},... | collective-permute-start | bytes 196616 | tf_op jit(solution)/shard_map/ppermute | solution.py:521
  89.8 2.2 %collective-permute-done.14 = f32[8,2048]{1,0:T(8,128)S(1)} collective-permute-done((f32[8,2048]{1,0:T(8,128)S(1)}, f32[8,2048]{1,0:T(8,128)S(1)}, u32[]{:S(2)}, u32[]{:S(2)}) %collective-permute-start.14) | collective-permute-done | bytes 65568 | tf_op jit(solution)/shard_map/ppermute | solution.py:521
  92.1 2.7 %collective-permute-start.15 = (f32[8,2048]{1,0:T(8,128)S(1)}, f32[8,2048]{1,0:T(8,128)S(1)}, u32[]{:S(2)}, u32[]{:S(2)}) collective-permute-start(f32[8,2048]{1,0:T(8,128)S(1)} %add.35), channel_id=1, source_target_pairs={{0,8},{2,10},{4,12},{6,14},{8,0},{10,2},{12,4},{14,6},{1,9},{3,11}... | collective-permute-start | bytes 196616 | tf_op jit(solution)/shard_map/ppermute | solution.py:521
  94.8 2.5 %collective-permute-done.15 = f32[8,2048]{1,0:T(8,128)S(1)} collective-permute-done((f32[8,2048]{1,0:T(8,128)S(1)}, f32[8,2048]{1,0:T(8,128)S(1)}, u32[]{:S(2)}, u32[]{:S(2)}) %collective-permute-start.15) | collective-permute-done | bytes 65568 | tf_op jit(solution)/shard_map/ppermute | solution.py:521
  97.4 1.2 %collective-permute-done.16.theirs_ref = f32[8,2048]{1,0:T(8,128)S(1)} collective-permute-done((f32[8,2048]{1,0:T(8,128)S(1)}, f32[8,2048]{1,0:T(8,128)S(1)}, u32[]{:S(2)}, u32[]{:S(2)}) %collective-permute-start.16) | collective-permute-done | bytes 65568 | tf_op jit(solution)/shard_map/ppermute | solution.py:524
  98.7 2.6 %products.1 = f32[16,1024]{1,0:T(8,128)} custom-call(s32[4]{0:T(128)S(1)} %copy-done, f32[8,2048]{1,0:T(8,128)S(1)} %add.36.mine_ref, f32[8,2048]{1,0:T(8,128)S(1)} %collective-permute-done.16.theirs_ref, bf16[8,1024,256]{2,1,0:T(8,128)(2,1)S(1)} %get-tuple-element.44.weight_ref), custom_call_target="tpu_custom_call" | custom-call | tf_op jit(solution)/shard_map/products/pallas_call | solution.py:666
  (32 shorter events, 1.3 us)
Async XLA Ops:
  4.2 8.0 %copy-start.2 = (s32[160]{0:T(256)S(1)}, s32[160]{0:T(256)}, u32[]{:S(2)}) copy-start(s32[160]{0:T(256)} %param.16) | copy-start | bytes 1924
  4.2 8.0 %copy-start.3 = (s32[160]{0:T(256)S(1)}, s32[160]{0:T(256)}, u32[]{:S(2)}) copy-start(s32[160]{0:T(256)} %param.14) | copy-start | bytes 1924
  4.2 8.0 %copy-start.4 = (s32[160]{0:T(256)S(1)}, s32[160]{0:T(256)}, u32[]{:S(2)}) copy-start(s32[160]{0:T(256)} %param.12) | copy-start | bytes 1924
  4.2 37.0 %all-to-all-start = ((bf16[4,64,2048]{2,1,0:T(8,128)(2,1)}), bf16[4,64,2048]{2,1,0:T(8,128)(2,1)S(1)}, u32[]{:S(2)}, u32[]{:S(2)}) async-start(bf16[4,64,2048]{2,1,0:T(8,128)(2,1)} %get-tuple-element.27), calls=%async_computation | async-start | bytes 2097152 | tf_op jit(solution)/shard_map/all_to_all | solution.py:527
  10.7 30.5 %collective-permute-start = (bf16[160,4096]{1,0:T(8,128)(2,1)}, bf16[160,4096]{1,0:T(8,128)(2,1)S(1)}, u32[]{:S(2)}, u32[]{:S(2)}) collective-permute-start(bf16[160,4096]{1,0:T(8,128)(2,1)} %get-tuple-element.25), channel_id=1, source_target_pairs={{0,2},{2,0},{4,6},{6,4},{8,10},{10,8},{12,14},{14,12},{1,3},{3,1},... | collective-permute-start | bytes 3932168 | tf_op jit(solution)/shard_map/ppermute | solution.py:521
  12.9 21.7 %copy-start.1 = (s32[3,256]{1,0:T(4,128)S(1)}, s32[3,256]{1,0:T(4,128)}, u32[]{:S(2)}) copy-start(s32[3,256]{1,0:T(4,128)} %select_reduce_fusion.inv_ref) | copy-start | bytes 9220
  12.9 28.3 %copy-start = (s32[4]{0:T(128)S(1)}, s32[4]{0:T(128)}, u32[]{:S(2)}) copy-start(s32[4]{0:T(128)} %pad_add_fusion.1.place_ref) | copy-start | bytes 52
  22.5 6.7 %collective-permute-start.2 = (f32[64,256]{1,0:T(8,128)}, f32[64,256]{1,0:T(8,128)S(1)}, u32[]{:S(2)}, u32[]{:S(2)}) collective-permute-start(f32[64,256]{1,0:T(8,128)} %get-tuple-element.26), channel_id=1, source_target_pairs={{0,4},{2,6},{4,0},{6,2},{8,12},{10,14},{12,8},{14,10},{1,5},{3,7},... | collective-permute-start | bytes 196616 | tf_op jit(solution)/shard_map/ppermute | solution.py:521
  30.1 9.1 %collective-permute-start.3 = (f32[64,256]{1,0:T(8,128)S(1)}, f32[64,256]{1,0:T(8,128)S(1)}, u32[]{:S(2)}, u32[]{:S(2)}) collective-permute-start(f32[64,256]{1,0:T(8,128)S(1)} %add.30), channel_id=1, source_target_pairs={{0,8},{2,10},{4,12},{6,14},{8,0},{10,2},{12,4},{14,6},{1,9},{3,11}... | collective-permute-start | bytes 196616 | tf_op jit(solution)/shard_map/ppermute | solution.py:521
  34.6 6.6 %collective-permute-start.1 = (s32[3,256]{1,0:T(4,128)S(1)}, s32[3,256]{1,0:T(4,128)S(1)}, u32[]{:S(2)}, u32[]{:S(2)}) collective-permute-start(s32[3,256]{1,0:T(4,128)S(1)} %copy-done.1), channel_id=1, source_target_pairs={{0,2},{2,0},{4,6},{6,4},{8,10},{10,8},{12,14},{14,12},{1,3},{3,1},... | collective-permute-start | bytes 9224 | tf_op jit(solution)/shard_map/ppermute | solution.py:521
  47.1 4.9 %collective-permute-start.4 = (bf16[4,1024,256]{2,1,0:T(8,128)(2,1)}, bf16[4,1024,256]{2,1,0:T(8,128)(2,1)}, u32[]{:S(2)}, u32[]{:S(2)}) collective-permute-start(bf16[4,1024,256]{2,1,0:T(8,128)(2,1)} %get-tuple-element.34), channel_id=1, source_target_pairs={{0,1},{1,0},{2,3},{3,2},{4,5},{5,4},{6,7},{7,6},{8,9},{9,8},{10,11... | collective-permute-start | bytes 6291464 | tf_op jit(solution)/shard_map/ppermute | solution.py:524
  47.2 24.7 %all-to-all-start.1 = ((bf16[4,64,1024]{2,1,0:T(8,128)(2,1)}), bf16[4,64,1024]{2,1,0:T(8,128)(2,1)S(1)}, u32[]{:S(2)}, u32[]{:S(2)}) async-start(bf16[4,64,1024]{2,1,0:T(8,128)(2,1)} %get-tuple-element.33), calls=%async_computation.1 | async-start | bytes 1048576 | tf_op jit(solution)/shard_map/all_to_all | solution.py:527
  56.3 8.2 %collective-permute-start.5 = (bf16[64,1024]{1,0:T(8,128)(2,1)S(1)}, bf16[64,1024]{1,0:T(8,128)(2,1)S(1)}, u32[]{:S(2)}, u32[]{:S(2)}) collective-permute-start(bf16[64,1024]{1,0:T(8,128)(2,1)S(1)} %get-tuple-element.36), channel_id=1, source_target_pairs={{0,4},{2,6},{4,0},{6,2},{8,12},{10,14},{12,8},{14,10},{1,5},{3,7},... | collective-permute-start | bytes 393224 | tf_op jit(solution)/shard_map/ppermute | solution.py:521
  58.4 17.9 %collective-permute-start.6 = (bf16[64,1024]{1,0:T(8,128)(2,1)S(1)}, bf16[64,1024]{1,0:T(8,128)(2,1)S(1)}, u32[]{:S(2)}, u32[]{:S(2)}) collective-permute-start(bf16[64,1024]{1,0:T(8,128)(2,1)S(1)} %get-tuple-element.39), channel_id=1, source_target_pairs={{0,8},{2,10},{4,12},{6,14},{8,0},{10,2},{12,4},{14,6},{1,9},{3,11}... | collective-permute-start | bytes 393224 | tf_op jit(solution)/shard_map/ppermute | solution.py:521
  64.5 5.4 %collective-permute-start.8 = (f32[64,256]{1,0:T(8,128)S(1)}, f32[64,256]{1,0:T(8,128)S(1)}, u32[]{:S(2)}, u32[]{:S(2)}) collective-permute-start(f32[64,256]{1,0:T(8,128)S(1)} %add.31), channel_id=1, source_target_pairs={{0,2},{2,0},{4,6},{6,4},{8,10},{10,8},{12,14},{14,12},{1,3},{3,1},... | collective-permute-start | bytes 196616 | tf_op jit(solution)/shard_map/ppermute | solution.py:521
  66.0 10.3 %collective-permute-start.7 = (bf16[64,1024]{1,0:T(8,128)(2,1)S(1)}, bf16[64,1024]{1,0:T(8,128)(2,1)S(1)}, u32[]{:S(2)}, u32[]{:S(2)}) collective-permute-start(bf16[64,1024]{1,0:T(8,128)(2,1)S(1)} %get-tuple-element.40), channel_id=1, source_target_pairs={{0,12},{2,14},{4,8},{6,10},{8,4},{10,6},{12,0},{14,2},{1,13},{3,15... | collective-permute-start | bytes 393224 | tf_op jit(solution)/shard_map/ppermute | solution.py:521
  69.9 6.4 %collective-permute-start.11 = (f32[64,256]{1,0:T(8,128)S(1)}, f32[64,256]{1,0:T(8,128)S(1)}, u32[]{:S(2)}, u32[]{:S(2)}) collective-permute-start(f32[64,256]{1,0:T(8,128)S(1)} %add.32.pay0_ref), channel_id=1, source_target_pairs={{0,17},{1,16},{16,1},{17,0},{2,19},{3,18},{18,3},{19,2},{4,21},{5,... | collective-permute-start | bytes 196616 | tf_op jit(solution)/shard_map/ppermute | solution.py:640
  70.0 6.3 %collective-permute-start.10 = (f32[64,256]{1,0:T(8,128)S(1)}, f32[64,256]{1,0:T(8,128)S(1)}, u32[]{:S(2)}, u32[]{:S(2)}) collective-permute-start(f32[64,256]{1,0:T(8,128)S(1)} %add.32.pay0_ref), channel_id=1, source_target_pairs={{0,16},{16,0},{1,17},{17,1},{2,18},{18,2},{3,19},{19,3},{4,20},{20... | collective-permute-start | bytes 196616 | tf_op jit(solution)/shard_map/ppermute | solution.py:639
  71.6 4.7 %collective-permute-start.9 = (f32[64,256]{1,0:T(8,128)S(1)}, f32[64,256]{1,0:T(8,128)S(1)}, u32[]{:S(2)}, u32[]{:S(2)}) collective-permute-start(f32[64,256]{1,0:T(8,128)S(1)} %add.32.pay0_ref), channel_id=1, source_target_pairs={{0,1},{1,0},{2,3},{3,2},{4,5},{5,4},{6,7},{7,6},{8,9},{9,8},{10,11... | collective-permute-start | bytes 196616 | tf_op jit(solution)/shard_map/ppermute | solution.py:524
  81.5 1.3 %collective-permute-start.12 = (f32[8,2048]{1,0:T(8,128)S(1)}, f32[8,2048]{1,0:T(8,128)S(1)}, u32[]{:S(2)}, u32[]{:S(2)}) collective-permute-start(f32[8,2048]{1,0:T(8,128)S(1)} %get-tuple-element.43), channel_id=1, source_target_pairs={{0,1},{1,0},{2,3},{3,2},{4,5},{5,4},{6,7},{7,6},{8,9},{9,8},{10,11... | collective-permute-start | bytes 196616 | tf_op jit(solution)/shard_map/ppermute | solution.py:524
  82.8 4.3 %collective-permute-start.13 = (f32[8,2048]{1,0:T(8,128)S(1)}, f32[8,2048]{1,0:T(8,128)S(1)}, u32[]{:S(2)}, u32[]{:S(2)}) collective-permute-start(f32[8,2048]{1,0:T(8,128)S(1)} %add.33), channel_id=1, source_target_pairs={{0,2},{2,0},{4,6},{6,4},{8,10},{10,8},{12,14},{14,12},{1,3},{3,1},... | collective-permute-start | bytes 196616 | tf_op jit(solution)/shard_map/ppermute | solution.py:521
  87.1 4.9 %collective-permute-start.14 = (f32[8,2048]{1,0:T(8,128)S(1)}, f32[8,2048]{1,0:T(8,128)S(1)}, u32[]{:S(2)}, u32[]{:S(2)}) collective-permute-start(f32[8,2048]{1,0:T(8,128)S(1)} %add.34), channel_id=1, source_target_pairs={{0,4},{2,6},{4,0},{6,2},{8,12},{10,14},{12,8},{14,10},{1,5},{3,7},... | collective-permute-start | bytes 196616 | tf_op jit(solution)/shard_map/ppermute | solution.py:521
  92.1 5.2 %collective-permute-start.15 = (f32[8,2048]{1,0:T(8,128)S(1)}, f32[8,2048]{1,0:T(8,128)S(1)}, u32[]{:S(2)}, u32[]{:S(2)}) collective-permute-start(f32[8,2048]{1,0:T(8,128)S(1)} %add.35), channel_id=1, source_target_pairs={{0,8},{2,10},{4,12},{6,14},{8,0},{10,2},{12,4},{14,6},{1,9},{3,11}... | collective-permute-start | bytes 196616 | tf_op jit(solution)/shard_map/ppermute | solution.py:521
  97.3 1.3 %collective-permute-start.16 = (f32[8,2048]{1,0:T(8,128)S(1)}, f32[8,2048]{1,0:T(8,128)S(1)}, u32[]{:S(2)}, u32[]{:S(2)}) collective-permute-start(f32[8,2048]{1,0:T(8,128)S(1)} %add.36.mine_ref), channel_id=1, source_target_pairs={{0,1},{1,0},{2,3},{3,2},{4,5},{5,4},{6,7},{7,6},{8,9},{9,8},{10,11... | collective-permute-start | bytes 196616 | tf_op jit(solution)/shard_map/ppermute | solution.py:524

commit v6 on v5

--- a/solution.py
+++ b/solution.py
@@ -430,26 +430,27 @@
     pay1_ref,
     pay2_ref,
     pay3_ref,
-    weight_in_ref,
+    across0_ref,
+    across1_ref,
+    across2_ref,
+    across3_ref,
     mine_ref,
     theirs_ref,
-    weight_out_ref,
     lead_ref,
     act_ref,
     pay_ref,
     proj_ref,
     tangent_ref,
     rows_ref,
-    weight_sem,
 ):
-    weight_copy = pltpu.make_async_copy(weight_in_ref, weight_out_ref, weight_sem)
-    weight_copy.start()
     zone = place_ref[0] // 2
     quarter = place_ref[1]
     core = place_ref[3]
     unshuffle = unshuffle_matrix(256)
-    for flip, ref in enumerate((pay0_ref, pay1_ref, pay2_ref, pay3_ref)):
-        pay_ref[flipped(quarter, flip)] = ref[...]
+    near_parts = (pay0_ref, pay1_ref, pay2_ref, pay3_ref)
+    across_parts = (across0_ref, across1_ref, across2_ref, across3_ref)
+    for flip in range(4):
+        pay_ref[flipped(quarter, flip)] = near_parts[flip][...] + across_parts[flip][...]
     for chunk in range(4):
         cols = slice(256 * chunk, 256 * (chunk + 1))
         proj_ref[:, cols] = dot(pay_ref[chunk, 32:64, :].astype(BF), unshuffle).astype(BF)
@@ -481,7 +482,12 @@
         row = slice(step % 8, step % 8 + 1)
         target[row, :1024] = jnp.sum(backward * lead_ref[...], axis=0, keepdims=True)
         target[row, 1024:] = jnp.sum(backward * act_ref[...], axis=0, keepdims=True)
-    weight_copy.wait()
+
+
+def fetch_kernel(weight_in_ref, weight_out_ref, sem):
+    copy = pltpu.make_async_copy(weight_in_ref, weight_out_ref, sem)
+    copy.start()
+    copy.wait()
 
 
 def product_kernel(place_ref, mine_ref, theirs_ref, weight_ref, out_ref, sum_ref):
@@ -580,11 +586,18 @@
         name="own_blocks",
     )(place, inv, gate_blocks, up_blocks, down_blocks, sketch, probe_index, probe_value)
 
-    for bits in (2, 4):
-        payload = payload + owner_flip(payload, bits)
-    near, near_inv, payload, gathered = lax.optimization_barrier(
-        (near, near_inv, payload, gathered)
-    )
+    from_zones = [owner_flip(payload, bits) for bits in (4, 6, 2)]
+    payload = payload + from_zones[0] + from_zones[1] + from_zones[2]
+    pay_parts = [
+        payload,
+        core_flip(payload),
+        lax.ppermute(payload, "groups", [(0, 1), (1, 0)]),
+        lax.ppermute(payload, ("groups", "seq"), [(i, i ^ 3) for i in range(4)]),
+    ]
+    near, near_inv, gathered, pay_parts = lax.optimization_barrier(
+        (near, near_inv, gathered, pay_parts)
+    )
+
     first_keep, first_sent, near_weights = pl.pallas_call(
         first_kernel,
         out_shape=(
@@ -631,21 +644,25 @@
     )(place, core_flip(near_weights), weights, gathered)
     second_back = [owner_flip(second_sent[flip - 1], 2 * flip) for flip in (1, 2, 3)]
 
-    second_back[0], payload = lax.optimization_barrier((second_back[0], payload))
-    payload = payload + owner_flip(payload, 1)
-    pay_parts = [
-        payload,
-        core_flip(payload),
-        lax.ppermute(payload, "groups", [(0, 1), (1, 0)]),
-        lax.ppermute(payload, ("groups", "seq"), [(i, i ^ 3) for i in range(4)]),
-    ]
-
-    mine, theirs, weights_at_hand = pl.pallas_call(
+    pay_parts = pay_parts + [owner_flip(part, 1) for part in pay_parts]
+
+    first_back, weights = lax.optimization_barrier((first_back, weights))
+    weights_at_hand = pl.pallas_call(
+        fetch_kernel,
+        out_shape=jax.ShapeDtypeStruct((8, 1024, 256), BF),
+        in_specs=[HBM],
+        out_specs=VMEM,
+        scratch_shapes=[pltpu.SemaphoreType.DMA],
+        compiler_params=params(48),
+        name="fetch_weights",
+    )(weights)
+    pay_parts[0], weights_at_hand = lax.optimization_barrier((pay_parts[0], weights_at_hand))
+
+    mine, theirs = pl.pallas_call(
         middle_kernel,
-        out_shape=(jax.ShapeDtypeStruct((8, 2048), F32),) * 2
-        + (jax.ShapeDtypeStruct((8, 1024, 256), BF),),
-        in_specs=[SMEM] + [VMEM] * 10 + [HBM],
-        out_specs=(VMEM,) * 3,
+        out_shape=(jax.ShapeDtypeStruct((8, 2048), F32),) * 2,
+        in_specs=[SMEM] + [VMEM] * 14,
+        out_specs=(VMEM,) * 2,
         scratch_shapes=[
             pltpu.VMEM((64, 1024), F32),
             pltpu.VMEM((64, 1024), F32),
@@ -653,11 +670,10 @@
             pltpu.VMEM((K, 1024), BF),
             pltpu.VMEM((64 * P_SIZE, 1024), BF),
             pltpu.VMEM((64 * P_SIZE, K), BF),
-            pltpu.SemaphoreType.DMA,
         ],
         compiler_params=params(48),
         name="token_sums",
-    )(place, first_keep, first_back, second_keep, *second_back, *pay_parts, weights)
+    )(place, first_keep, first_back, second_keep, *second_back, *pay_parts)
 
     sums = mine + core_flip(theirs)
     for bits in (1, 2, 4):

time: 102 us -> 106 us (1.039)
  waiting for transfers between devices: 28 us -> 37.1 us
  starting transfers between devices: 39.8 us -> 34.8 us
    ppermute x11 -> x15, waiting for transfers between devices: 25.5 us -> 31.3 us  [owner_flip(): return lax.ppermute(value, 'fsdp', [(i, i ^ bits) for i in range(8)])]
    ppermute x11 -> x15, starting transfers between devices: 26.4 us -> 22.6 us  [owner_flip(): return lax.ppermute(value, 'fsdp', [(i, i ^ bits) for i in range(8)])]
    all_to_all x2, waiting for transfers between devices: 0.01 us -> 3.12 us  [zone_exchange(): lax.all_to_all(value, 'fsdp', split_axis=0, concat_axis=0, tiled=True, ax...]
    pallas_call x0 -> x1, Pallas kernels: none -> 2.2 us  [pair_split(): pl.pallas_call(fetch_kernel, out_shape=jax.ShapeDtypeStruct((8, 1024, 256...]
    pallas_call x1, Pallas kernels: 5.13 us -> 3.17 us  [pair_split(): pl.pallas_call(middle_kernel, out_shape=(jax.ShapeDtypeStruct((8, 2048),...]
    all_to_all x2, starting transfers between devices: 11.3 us -> 9.93 us  [zone_exchange(): lax.all_to_all(value, 'fsdp', split_axis=0, concat_axis=0, tiled=True, ax...]
  transfers between devices with their start and end apart: 19 -> 23, of which waited for: 10 -> 12; matrix products, arithmetic and copies ran while one was open for 2% -> 2% of each run, Pallas kernels for 14% -> 15%
where the time goes in v6:
time: 106 us
  waiting for transfers between devices  37.1 us (35%)
  starting transfers between devices  34.8 us (33%)
  Pallas kernels  31.2 us (29%)
  other arithmetic  2.24 us (2%)
    ppermute x15, waiting for transfers between devices, owner_flip(): return lax.ppermute(value, 'fsdp', [(i, i ^ bits) for i in range(8)])  31.3 us
    ppermute x15, starting transfers between devices, owner_flip(): return lax.ppermute(value, 'fsdp', [(i, i ^ bits) for i in range(8)])  22.6 us
    all_to_all x2, starting transfers between devices, zone_exchange(): lax.all_to_all(value, 'fsdp', split_axis=0, concat_axis=0, tiled=True, ax...  9.93 us
    pallas_call x1, Pallas kernels, pair_split(): pl.pallas_call(own_kernel, out_shape=(jax.ShapeDtypeStruct((8, 1024, 256)...  9.59 us
    pallas_call x1, Pallas kernels, pair_split(): pl.pallas_call(first_kernel, out_shape=(jax.ShapeDtypeStruct((64, 1024),...  5.88 us
    pallas_call x1, Pallas kernels, pair_split(): pl.pallas_call(second_kernel, out_shape=(jax.ShapeDtypeStruct((64, 1024),...  4.25 us
    pallas_call x1, Pallas kernels, pair_split(): pl.pallas_call(head_kernel, out_shape=(jax.ShapeDtypeStruct((4, 64, 2048)...  3.51 us
    pallas_call x1, Pallas kernels, pair_split(): pl.pallas_call(middle_kernel, out_shape=(jax.ShapeDtypeStruct((8, 2048),...  3.17 us
  transfers between devices with their start and end apart: 23, of which 12 were waited for; matrix products, arithmetic and copies ran while one was open for 2% of the time, Pallas kernels for 15%

profile of v6, /device:TPU:0, one launch (start us, length us, event | category | flops | bytes accessed | tf_op | source)
XLA Modules:
  0.0 105.5 jit_solution(4266501785167108609)
XLA Ops:
  0.6 3.5 %head.1 = (bf16[4,64,2048]{2,1,0:T(8,128)(2,1)}, bf16[160,4096]{1,0:T(8,128)(2,1)}) custom-call(s32[4]{0:T(128)} %pad_add_fusion.1.place_ref, bf16[64,8192]{1,0:T(8,128)(2,1)} %tok_in_ref.1, bf16[160,4096]{1,0:T(8,128)(2,1)} %gate_ref.3, bf16[160,4096]{1,0:T(8,128)(2,1)} %up_ref.3), custom_call_target="tpu_custom_call" | custom-call | tf_op jit(solution)/shard_map/head/pallas_call | solution.py:542
  4.1 6.5 %all-to-all-start = ((bf16[4,64,2048]{2,1,0:T(8,128)(2,1)}), bf16[4,64,2048]{2,1,0:T(8,128)(2,1)S(1)}, u32[]{:S(2)}, u32[]{:S(2)}) async-start(bf16[4,64,2048]{2,1,0:T(8,128)(2,1)} %get-tuple-element.30), calls=%async_computation | async-start | bytes 2097152 | tf_op jit(solution)/shard_map/all_to_all | solution.py:533
  10.6 1.5 %collective-permute-start = (bf16[160,4096]{1,0:T(8,128)(2,1)}, bf16[160,4096]{1,0:T(8,128)(2,1)S(1)}, u32[]{:S(2)}, u32[]{:S(2)}) collective-permute-start(bf16[160,4096]{1,0:T(8,128)(2,1)} %get-tuple-element.29), channel_id=1, source_target_pairs={{0,2},{2,0},{4,6},{6,4},{8,10},{10,8},{12,14},{14,12},{1,3},{3,1},... | collective-permute-start | bytes 3932168 | tf_op jit(solution)/shard_map/ppermute | solution.py:527
  12.9 9.6 %own_blocks.1 = (bf16[8,1024,256]{2,1,0:T(8,128)(2,1)}, f32[64,256]{1,0:T(8,128)}) custom-call(s32[4]{0:T(128)} %pad_add_fusion.1.place_ref, s32[3,256]{1,0:T(4,128)} %select_reduce_fusion.inv_ref, bf16[160,4096]{1,0:T(8,128)(2,1)} %gate_ref.3, bf16[160,4096]{1,0:T(8,128)(2,1)} %up_ref.3, bf16[160,4096]{1,0:T(8,128)(2,1)} %down_ref.1, ...), custom_call_target="tpu_custom_call" | custom-call | tf_op jit(solution)/shard_map/own_blocks/pallas_call | solution.py:567
  22.5 2.1 %collective-permute-start.4 = (f32[64,256]{1,0:T(8,128)}, f32[64,256]{1,0:T(8,128)S(1)}, u32[]{:S(2)}, u32[]{:S(2)}) collective-permute-start(f32[64,256]{1,0:T(8,128)} %get-tuple-element.31), channel_id=1, source_target_pairs={{0,4},{2,6},{4,0},{6,2},{8,12},{10,14},{12,8},{14,10},{1,5},{3,7},... | collective-permute-start | bytes 196616 | tf_op jit(solution)/shard_map/ppermute | solution.py:527
  24.6 2.4 %collective-permute-start.3 = (f32[64,256]{1,0:T(8,128)}, f32[64,256]{1,0:T(8,128)S(1)}, u32[]{:S(2)}, u32[]{:S(2)}) collective-permute-start(f32[64,256]{1,0:T(8,128)} %get-tuple-element.31), channel_id=1, source_target_pairs={{0,12},{2,14},{4,8},{6,10},{8,4},{10,6},{12,0},{14,2},{1,13},{3,15... | collective-permute-start | bytes 196616 | tf_op jit(solution)/shard_map/ppermute | solution.py:527
  26.9 3.4 %collective-permute-done.4 = f32[64,256]{1,0:T(8,128)S(1)} collective-permute-done((f32[64,256]{1,0:T(8,128)}, f32[64,256]{1,0:T(8,128)S(1)}, u32[]{:S(2)}, u32[]{:S(2)}) %collective-permute-start.4) | collective-permute-done | bytes 65568 | tf_op jit(solution)/shard_map/ppermute | solution.py:527
  30.3 4.9 %collective-permute-done.3 = f32[64,256]{1,0:T(8,128)S(1)} collective-permute-done((f32[64,256]{1,0:T(8,128)}, f32[64,256]{1,0:T(8,128)S(1)}, u32[]{:S(2)}, u32[]{:S(2)}) %collective-permute-start.3) | collective-permute-done | bytes 65568 | tf_op jit(solution)/shard_map/ppermute | solution.py:527
  35.2 6.7 %collective-permute-done.2 = f32[64,256]{1,0:T(8,128)S(1)} collective-permute-done((f32[64,256]{1,0:T(8,128)}, f32[64,256]{1,0:T(8,128)S(1)}, u32[]{:S(2)}, u32[]{:S(2)}) %collective-permute-start.2) | collective-permute-done | bytes 65568 | tf_op jit(solution)/shard_map/ppermute | solution.py:527
  42.9 1.6 %collective-permute-start.6 = (f32[64,256]{1,0:T(8,128)S(1)}, f32[64,256]{1,0:T(8,128)S(1)}, u32[]{:S(2)}, u32[]{:S(2)}) collective-permute-start(f32[64,256]{1,0:T(8,128)S(1)} %add_add_fusion.pay0_ref), channel_id=1, source_target_pairs={{0,16},{16,0},{1,17},{17,1},{2,18},{18,2},{3,19},{19,3},{4,20},{20... | collective-permute-start | bytes 196616 | tf_op jit(solution)/shard_map/ppermute | solution.py:594
  44.8 1.5 %collective-permute-start.1 = (s32[3,256]{1,0:T(4,128)S(1)}, s32[3,256]{1,0:T(4,128)S(1)}, u32[]{:S(2)}, u32[]{:S(2)}) collective-permute-start(s32[3,256]{1,0:T(4,128)S(1)} %copy-done.1), channel_id=1, source_target_pairs={{0,2},{2,0},{4,6},{6,4},{8,10},{10,8},{12,14},{14,12},{1,3},{3,1},... | collective-permute-start | bytes 9224 | tf_op jit(solution)/shard_map/ppermute | solution.py:527
  46.2 2.1 %collective-permute-done.1.inv_ref = s32[3,256]{1,0:T(4,128)S(1)} collective-permute-done((s32[3,256]{1,0:T(4,128)S(1)}, s32[3,256]{1,0:T(4,128)S(1)}, u32[]{:S(2)}, u32[]{:S(2)}) %collective-permute-start.1) | collective-permute-done | bytes 3104 | tf_op jit(solution)/shard_map/ppermute | solution.py:527
  48.5 5.9 %first_partial.1 = (f32[64,1024]{1,0:T(8,128)S(1)}, bf16[4,64,1024]{2,1,0:T(8,128)(2,1)}, bf16[4,1024,256]{2,1,0:T(8,128)(2,1)}) custom-call(s32[4]{0:T(128)S(1)} %copy-done, s32[3,256]{1,0:T(4,128)S(1)} %collective-permute-done.1.inv_ref, bf16[160,4096]{1,0:T(8,128)(2,1)S(1)} %collective-permute-done.blocks_in_ref, ...), custom_call_target="tpu_custom_call" | custom-call | tf_op jit(solution)/shard_map/first_partial/pallas_call | solution.py:601
  54.7 3.5 %all-to-all-start.1 = ((bf16[4,64,1024]{2,1,0:T(8,128)(2,1)}), bf16[4,64,1024]{2,1,0:T(8,128)(2,1)S(1)}, u32[]{:S(2)}, u32[]{:S(2)}) async-start(bf16[4,64,1024]{2,1,0:T(8,128)(2,1)} %get-tuple-element.37), calls=%async_computation.1 | async-start | bytes 1048576 | tf_op jit(solution)/shard_map/all_to_all | solution.py:533
  58.1 1.6 %collective-permute-start.12 = (f32[64,256]{1,0:T(8,128)S(1)}, f32[64,256]{1,0:T(8,128)S(1)}, u32[]{:S(2)}, u32[]{:S(2)}) collective-permute-start(f32[64,256]{1,0:T(8,128)S(1)} %add_add_fusion.pay0_ref), channel_id=1, source_target_pairs={{0,2},{2,0},{4,6},{6,4},{8,10},{10,8},{12,14},{14,12},{1,3},{3,1},... | collective-permute-start | bytes 196616 | tf_op jit(solution)/shard_map/ppermute | solution.py:527
  60.2 4.2 %second_partial.1 = (f32[64,1024]{1,0:T(8,128)S(1)}, bf16[64,1024]{1,0:T(8,128)(2,1)S(1)}, bf16[64,1024]{1,0:T(8,128)(2,1)S(1)}, bf16[64,1024]{1,0:T(8,128)(2,1)S(1)}) custom-call(s32[4]{0:T(128)S(1)} %copy-done, bf16[4,1024,256]{2,1,0:T(8,128)(2,1)} %collective-permute-done.8.near_in_ref, bf16[8,1024,256]{2,1,0:T(8,128)(2,1)} %get-tuple-element.45.weight_in_ref, ...), custom_call_target="tpu_custom_call" | custom-call | tf_op jit(solution)/shard_map/second_partial/pallas_call | solution.py:628
  64.5 2.0 %collective-permute-start.9 = (bf16[64,1024]{1,0:T(8,128)(2,1)S(1)}, bf16[64,1024]{1,0:T(8,128)(2,1)S(1)}, u32[]{:S(2)}, u32[]{:S(2)}) collective-permute-start(bf16[64,1024]{1,0:T(8,128)(2,1)S(1)} %get-tuple-element.41), channel_id=1, source_target_pairs={{0,4},{2,6},{4,0},{6,2},{8,12},{10,14},{12,8},{14,10},{1,5},{3,7},... | collective-permute-start | bytes 393224 | tf_op jit(solution)/shard_map/ppermute | solution.py:527
  66.5 2.4 %collective-permute-start.10 = (bf16[64,1024]{1,0:T(8,128)(2,1)S(1)}, bf16[64,1024]{1,0:T(8,128)(2,1)S(1)}, u32[]{:S(2)}, u32[]{:S(2)}) collective-permute-start(bf16[64,1024]{1,0:T(8,128)(2,1)S(1)} %get-tuple-element.42), channel_id=1, source_target_pairs={{0,8},{2,10},{4,12},{6,14},{8,0},{10,2},{12,4},{14,6},{1,9},{3,11}... | collective-permute-start | bytes 393224 | tf_op jit(solution)/shard_map/ppermute | solution.py:527
  68.9 1.5 %collective-permute-start.14 = (f32[64,256]{1,0:T(8,128)S(1)}, f32[64,256]{1,0:T(8,128)S(1)}, u32[]{:S(2)}, u32[]{:S(2)}) collective-permute-start(f32[64,256]{1,0:T(8,128)S(1)} %collective-permute-done.6.pay2_ref), channel_id=1, source_target_pairs={{0,2},{2,0},{4,6},{6,4},{8,10},{10,8},{12,14},{14,12},{1,3},{3,1},... | collective-permute-start | bytes 196616 | tf_op jit(solution)/shard_map/ppermute | solution.py:527
  71.0 3.1 %all-to-all-done.1.first_ref = bf16[4,64,1024]{2,1,0:T(8,128)(2,1)S(1)} async-done(((bf16[4,64,1024]{2,1,0:T(8,128)(2,1)}), bf16[4,64,1024]{2,1,0:T(8,128)(2,1)S(1)}, u32[]{:S(2)}, u32[]{:S(2)}) %all-to-all-start.1) | async-done | bytes 524320 | tf_op jit(solution)/shard_map/all_to_all | solution.py:533
  74.1 2.2 %fetch_weights.1.weight_ref = bf16[8,1024,256]{2,1,0:T(8,128)(2,1)S(1)} custom-call(bf16[8,1024,256]{2,1,0:T(8,128)(2,1)} %get-tuple-element.45.weight_in_ref), custom_call_target="tpu_custom_call" | custom-call | tf_op jit(solution)/shard_map/fetch_weights/pallas_call | solution.py:650
  76.3 6.0 %collective-permute-done.10.second2_ref = bf16[64,1024]{1,0:T(8,128)(2,1)S(1)} collective-permute-done((bf16[64,1024]{1,0:T(8,128)(2,1)S(1)}, bf16[64,1024]{1,0:T(8,128)(2,1)S(1)}, u32[]{:S(2)}, u32[]{:S(2)}) %collective-permute-start.10) | collective-permute-done | bytes 131104 | tf_op jit(solution)/shard_map/ppermute | solution.py:527
  82.4 3.2 %token_sums.1 = (f32[8,2048]{1,0:T(8,128)S(1)}, f32[8,2048]{1,0:T(8,128)S(1)}) custom-call(s32[4]{0:T(128)S(1)} %copy-done, f32[64,1024]{1,0:T(8,128)S(1)} %get-tuple-element.36.first_keep_ref, bf16[4,64,1024]{2,1,0:T(8,128)(2,1)S(1)} %all-to-all-done.1.first_ref, f32[64,1024]{1,0:T(8,128)S(1)} %get-tuple-element.40.second_keep_ref, ...), custom_call_target="tpu_custom_call" | custom-call | tf_op jit(solution)/shard_map/token_sums/pallas_call | solution.py:661
  85.6 1.2 %collective-permute-done.16 = f32[8,2048]{1,0:T(8,128)S(1)} collective-permute-done((f32[8,2048]{1,0:T(8,128)S(1)}, f32[8,2048]{1,0:T(8,128)S(1)}, u32[]{:S(2)}, u32[]{:S(2)}) %collective-permute-start.16) | collective-permute-done | bytes 65568 | tf_op jit(solution)/shard_map/ppermute | solution.py:530
  86.9 1.6 %collective-permute-start.17 = (f32[8,2048]{1,0:T(8,128)S(1)}, f32[8,2048]{1,0:T(8,128)S(1)}, u32[]{:S(2)}, u32[]{:S(2)}) collective-permute-start(f32[8,2048]{1,0:T(8,128)S(1)} %add.33), channel_id=1, source_target_pairs={{0,2},{2,0},{4,6},{6,4},{8,10},{10,8},{12,14},{14,12},{1,3},{3,1},... | collective-permute-start | bytes 196616 | tf_op jit(solution)/shard_map/ppermute | solution.py:527
  88.4 2.8 %collective-permute-done.17 = f32[8,2048]{1,0:T(8,128)S(1)} collective-permute-done((f32[8,2048]{1,0:T(8,128)S(1)}, f32[8,2048]{1,0:T(8,128)S(1)}, u32[]{:S(2)}, u32[]{:S(2)}) %collective-permute-start.17) | collective-permute-done | bytes 65568 | tf_op jit(solution)/shard_map/ppermute | solution.py:527
  91.2 2.9 %collective-permute-start.18 = (f32[8,2048]{1,0:T(8,128)S(1)}, f32[8,2048]{1,0:T(8,128)S(1)}, u32[]{:S(2)}, u32[]{:S(2)}) collective-permute-start(f32[8,2048]{1,0:T(8,128)S(1)} %add.34), channel_id=1, source_target_pairs={{0,4},{2,6},{4,0},{6,2},{8,12},{10,14},{12,8},{14,10},{1,5},{3,7},... | collective-permute-start | bytes 196616 | tf_op jit(solution)/shard_map/ppermute | solution.py:527
  94.1 2.2 %collective-permute-done.18 = f32[8,2048]{1,0:T(8,128)S(1)} collective-permute-done((f32[8,2048]{1,0:T(8,128)S(1)}, f32[8,2048]{1,0:T(8,128)S(1)}, u32[]{:S(2)}, u32[]{:S(2)}) %collective-permute-start.18) | collective-permute-done | bytes 65568 | tf_op jit(solution)/shard_map/ppermute | solution.py:527
  96.4 2.1 %collective-permute-start.19 = (f32[8,2048]{1,0:T(8,128)S(1)}, f32[8,2048]{1,0:T(8,128)S(1)}, u32[]{:S(2)}, u32[]{:S(2)}) collective-permute-start(f32[8,2048]{1,0:T(8,128)S(1)} %add.35), channel_id=1, source_target_pairs={{0,8},{2,10},{4,12},{6,14},{8,0},{10,2},{12,4},{14,6},{1,9},{3,11}... | collective-permute-start | bytes 196616 | tf_op jit(solution)/shard_map/ppermute | solution.py:527
  98.5 3.1 %collective-permute-done.19 = f32[8,2048]{1,0:T(8,128)S(1)} collective-permute-done((f32[8,2048]{1,0:T(8,128)S(1)}, f32[8,2048]{1,0:T(8,128)S(1)}, u32[]{:S(2)}, u32[]{:S(2)}) %collective-permute-start.19) | collective-permute-done | bytes 65568 | tf_op jit(solution)/shard_map/ppermute | solution.py:527
  101.7 1.2 %collective-permute-done.20.theirs_ref = f32[8,2048]{1,0:T(8,128)S(1)} collective-permute-done((f32[8,2048]{1,0:T(8,128)S(1)}, f32[8,2048]{1,0:T(8,128)S(1)}, u32[]{:S(2)}, u32[]{:S(2)}) %collective-permute-start.20) | collective-permute-done | bytes 65568 | tf_op jit(solution)/shard_map/ppermute | solution.py:530
  102.9 2.6 %products.1 = f32[16,1024]{1,0:T(8,128)} custom-call(s32[4]{0:T(128)S(1)} %copy-done, f32[8,2048]{1,0:T(8,128)S(1)} %add.36.mine_ref, f32[8,2048]{1,0:T(8,128)S(1)} %collective-permute-done.20.theirs_ref, bf16[8,1024,256]{2,1,0:T(8,128)(2,1)S(1)} %fetch_weights.1.weight_ref), custom_call_target="tpu_custom_call" | custom-call | tf_op jit(solution)/shard_map/products/pallas_call | solution.py:682
  (39 shorter events, 4.4 us)
Async XLA Ops:
  4.1 8.0 %copy-start.2 = (s32[160]{0:T(256)S(1)}, s32[160]{0:T(256)}, u32[]{:S(2)}) copy-start(s32[160]{0:T(256)} %param.16) | copy-start | bytes 1924
  4.1 8.0 %copy-start.3 = (s32[160]{0:T(256)S(1)}, s32[160]{0:T(256)}, u32[]{:S(2)}) copy-start(s32[160]{0:T(256)} %param.14) | copy-start | bytes 1924
  4.1 8.0 %copy-start.4 = (s32[160]{0:T(256)S(1)}, s32[160]{0:T(256)}, u32[]{:S(2)}) copy-start(s32[160]{0:T(256)} %param.12) | copy-start | bytes 1924
  4.1 44.4 %all-to-all-start = ((bf16[4,64,2048]{2,1,0:T(8,128)(2,1)}), bf16[4,64,2048]{2,1,0:T(8,128)(2,1)S(1)}, u32[]{:S(2)}, u32[]{:S(2)}) async-start(bf16[4,64,2048]{2,1,0:T(8,128)(2,1)} %get-tuple-element.30), calls=%async_computation | async-start | bytes 2097152 | tf_op jit(solution)/shard_map/all_to_all | solution.py:533
  10.6 37.9 %collective-permute-start = (bf16[160,4096]{1,0:T(8,128)(2,1)}, bf16[160,4096]{1,0:T(8,128)(2,1)S(1)}, u32[]{:S(2)}, u32[]{:S(2)}) collective-permute-start(bf16[160,4096]{1,0:T(8,128)(2,1)} %get-tuple-element.29), channel_id=1, source_target_pairs={{0,2},{2,0},{4,6},{6,4},{8,10},{10,8},{12,14},{14,12},{1,3},{3,1},... | collective-permute-start | bytes 3932168 | tf_op jit(solution)/shard_map/ppermute | solution.py:527
  12.9 31.9 %copy-start.1 = (s32[3,256]{1,0:T(4,128)S(1)}, s32[3,256]{1,0:T(4,128)}, u32[]{:S(2)}) copy-start(s32[3,256]{1,0:T(4,128)} %select_reduce_fusion.inv_ref) | copy-start | bytes 9220
  12.9 35.7 %copy-start = (s32[4]{0:T(128)S(1)}, s32[4]{0:T(128)}, u32[]{:S(2)}) copy-start(s32[4]{0:T(128)} %pad_add_fusion.1.place_ref) | copy-start | bytes 52
  22.5 7.9 %collective-permute-start.4 = (f32[64,256]{1,0:T(8,128)}, f32[64,256]{1,0:T(8,128)S(1)}, u32[]{:S(2)}, u32[]{:S(2)}) collective-permute-start(f32[64,256]{1,0:T(8,128)} %get-tuple-element.31), channel_id=1, source_target_pairs={{0,4},{2,6},{4,0},{6,2},{8,12},{10,14},{12,8},{14,10},{1,5},{3,7},... | collective-permute-start | bytes 196616 | tf_op jit(solution)/shard_map/ppermute | solution.py:527
  24.6 10.7 %collective-permute-start.3 = (f32[64,256]{1,0:T(8,128)}, f32[64,256]{1,0:T(8,128)S(1)}, u32[]{:S(2)}, u32[]{:S(2)}) collective-permute-start(f32[64,256]{1,0:T(8,128)} %get-tuple-element.31), channel_id=1, source_target_pairs={{0,12},{2,14},{4,8},{6,10},{8,4},{10,6},{12,0},{14,2},{1,13},{3,15... | collective-permute-start | bytes 196616 | tf_op jit(solution)/shard_map/ppermute | solution.py:527
  26.9 15.0 %collective-permute-start.2 = (f32[64,256]{1,0:T(8,128)}, f32[64,256]{1,0:T(8,128)S(1)}, u32[]{:S(2)}, u32[]{:S(2)}) collective-permute-start(f32[64,256]{1,0:T(8,128)} %get-tuple-element.31), channel_id=1, source_target_pairs={{0,8},{2,10},{4,12},{6,14},{8,0},{10,2},{12,4},{14,6},{1,9},{3,11}... | collective-permute-start | bytes 196616 | tf_op jit(solution)/shard_map/ppermute | solution.py:527
  42.8 5.6 %collective-permute-start.5 = (f32[64,256]{1,0:T(8,128)S(1)}, f32[64,256]{1,0:T(8,128)S(1)}, u32[]{:S(2)}, u32[]{:S(2)}) collective-permute-start(f32[64,256]{1,0:T(8,128)S(1)} %add_add_fusion.pay0_ref), channel_id=1, source_target_pairs={{0,1},{1,0},{2,3},{3,2},{4,5},{5,4},{6,7},{7,6},{8,9},{9,8},{10,11... | collective-permute-start | bytes 196616 | tf_op jit(solution)/shard_map/ppermute | solution.py:530
  42.9 5.5 %collective-permute-start.6 = (f32[64,256]{1,0:T(8,128)S(1)}, f32[64,256]{1,0:T(8,128)S(1)}, u32[]{:S(2)}, u32[]{:S(2)}) collective-permute-start(f32[64,256]{1,0:T(8,128)S(1)} %add_add_fusion.pay0_ref), channel_id=1, source_target_pairs={{0,16},{16,0},{1,17},{17,1},{2,18},{18,2},{3,19},{19,3},{4,20},{20... | collective-permute-start | bytes 196616 | tf_op jit(solution)/shard_map/ppermute | solution.py:594
  44.5 4.0 %collective-permute-start.7 = (f32[64,256]{1,0:T(8,128)S(1)}, f32[64,256]{1,0:T(8,128)S(1)}, u32[]{:S(2)}, u32[]{:S(2)}) collective-permute-start(f32[64,256]{1,0:T(8,128)S(1)} %add_add_fusion.pay0_ref), channel_id=1, source_target_pairs={{0,17},{1,16},{16,1},{17,0},{2,19},{3,18},{18,3},{19,2},{4,21},{5,... | collective-permute-start | bytes 196616 | tf_op jit(solution)/shard_map/ppermute | solution.py:595
  44.8 3.6 %collective-permute-start.1 = (s32[3,256]{1,0:T(4,128)S(1)}, s32[3,256]{1,0:T(4,128)S(1)}, u32[]{:S(2)}, u32[]{:S(2)}) collective-permute-start(s32[3,256]{1,0:T(4,128)S(1)} %copy-done.1), channel_id=1, source_target_pairs={{0,2},{2,0},{4,6},{6,4},{8,10},{10,8},{12,14},{14,12},{1,3},{3,1},... | collective-permute-start | bytes 9224 | tf_op jit(solution)/shard_map/ppermute | solution.py:527
  54.4 5.8 %collective-permute-start.8 = (bf16[4,1024,256]{2,1,0:T(8,128)(2,1)}, bf16[4,1024,256]{2,1,0:T(8,128)(2,1)}, u32[]{:S(2)}, u32[]{:S(2)}) collective-permute-start(bf16[4,1024,256]{2,1,0:T(8,128)(2,1)} %get-tuple-element.39), channel_id=1, source_target_pairs={{0,1},{1,0},{2,3},{3,2},{4,5},{5,4},{6,7},{7,6},{8,9},{9,8},{10,11... | collective-permute-start | bytes 6291464 | tf_op jit(solution)/shard_map/ppermute | solution.py:530
  54.7 19.4 %all-to-all-start.1 = ((bf16[4,64,1024]{2,1,0:T(8,128)(2,1)}), bf16[4,64,1024]{2,1,0:T(8,128)(2,1)S(1)}, u32[]{:S(2)}, u32[]{:S(2)}) async-start(bf16[4,64,1024]{2,1,0:T(8,128)(2,1)} %get-tuple-element.37), calls=%async_computation.1 | async-start | bytes 1048576 | tf_op jit(solution)/shard_map/all_to_all | solution.py:533
  58.1 10.8 %collective-permute-start.12 = (f32[64,256]{1,0:T(8,128)S(1)}, f32[64,256]{1,0:T(8,128)S(1)}, u32[]{:S(2)}, u32[]{:S(2)}) collective-permute-start(f32[64,256]{1,0:T(8,128)S(1)} %add_add_fusion.pay0_ref), channel_id=1, source_target_pairs={{0,2},{2,0},{4,6},{6,4},{8,10},{10,8},{12,14},{14,12},{1,3},{3,1},... | collective-permute-start | bytes 196616 | tf_op jit(solution)/shard_map/ppermute | solution.py:527
  59.7 10.7 %collective-permute-start.13 = (f32[64,256]{1,0:T(8,128)S(1)}, f32[64,256]{1,0:T(8,128)S(1)}, u32[]{:S(2)}, u32[]{:S(2)}) collective-permute-start(f32[64,256]{1,0:T(8,128)S(1)} %collective-permute-done.5.pay1_ref), channel_id=1, source_target_pairs={{0,2},{2,0},{4,6},{6,4},{8,10},{10,8},{12,14},{14,12},{1,3},{3,1},... | collective-permute-start | bytes 196616 | tf_op jit(solution)/shard_map/ppermute | solution.py:527
  64.5 11.8 %collective-permute-start.9 = (bf16[64,1024]{1,0:T(8,128)(2,1)S(1)}, bf16[64,1024]{1,0:T(8,128)(2,1)S(1)}, u32[]{:S(2)}, u32[]{:S(2)}) collective-permute-start(bf16[64,1024]{1,0:T(8,128)(2,1)S(1)} %get-tuple-element.41), channel_id=1, source_target_pairs={{0,4},{2,6},{4,0},{6,2},{8,12},{10,14},{12,8},{14,10},{1,5},{3,7},... | collective-permute-start | bytes 393224 | tf_op jit(solution)/shard_map/ppermute | solution.py:527
  66.5 15.9 %collective-permute-start.10 = (bf16[64,1024]{1,0:T(8,128)(2,1)S(1)}, bf16[64,1024]{1,0:T(8,128)(2,1)S(1)}, u32[]{:S(2)}, u32[]{:S(2)}) collective-permute-start(bf16[64,1024]{1,0:T(8,128)(2,1)S(1)} %get-tuple-element.42), channel_id=1, source_target_pairs={{0,8},{2,10},{4,12},{6,14},{8,0},{10,2},{12,4},{14,6},{1,9},{3,11}... | collective-permute-start | bytes 393224 | tf_op jit(solution)/shard_map/ppermute | solution.py:527
  68.8 13.5 %collective-permute-start.11 = (bf16[64,1024]{1,0:T(8,128)(2,1)S(1)}, bf16[64,1024]{1,0:T(8,128)(2,1)S(1)}, u32[]{:S(2)}, u32[]{:S(2)}) collective-permute-start(bf16[64,1024]{1,0:T(8,128)(2,1)S(1)} %get-tuple-element.43), channel_id=1, source_target_pairs={{0,12},{2,14},{4,8},{6,10},{8,4},{10,6},{12,0},{14,2},{1,13},{3,15... | collective-permute-start | bytes 393224 | tf_op jit(solution)/shard_map/ppermute | solution.py:527
  68.9 7.4 %collective-permute-start.14 = (f32[64,256]{1,0:T(8,128)S(1)}, f32[64,256]{1,0:T(8,128)S(1)}, u32[]{:S(2)}, u32[]{:S(2)}) collective-permute-start(f32[64,256]{1,0:T(8,128)S(1)} %collective-permute-done.6.pay2_ref), channel_id=1, source_target_pairs={{0,2},{2,0},{4,6},{6,4},{8,10},{10,8},{12,14},{14,12},{1,3},{3,1},... | collective-permute-start | bytes 196616 | tf_op jit(solution)/shard_map/ppermute | solution.py:527
  70.4 5.9 %collective-permute-start.15 = (f32[64,256]{1,0:T(8,128)S(1)}, f32[64,256]{1,0:T(8,128)S(1)}, u32[]{:S(2)}, u32[]{:S(2)}) collective-permute-start(f32[64,256]{1,0:T(8,128)S(1)} %collective-permute-done.7.pay3_ref), channel_id=1, source_target_pairs={{0,2},{2,0},{4,6},{6,4},{8,10},{10,8},{12,14},{14,12},{1,3},{3,1},... | collective-permute-start | bytes 196616 | tf_op jit(solution)/shard_map/ppermute | solution.py:527
  85.6 1.3 %collective-permute-start.16 = (f32[8,2048]{1,0:T(8,128)S(1)}, f32[8,2048]{1,0:T(8,128)S(1)}, u32[]{:S(2)}, u32[]{:S(2)}) collective-permute-start(f32[8,2048]{1,0:T(8,128)S(1)} %get-tuple-element.51), channel_id=1, source_target_pairs={{0,1},{1,0},{2,3},{3,2},{4,5},{5,4},{6,7},{7,6},{8,9},{9,8},{10,11... | collective-permute-start | bytes 196616 | tf_op jit(solution)/shard_map/ppermute | solution.py:530
  86.9 4.3 %collective-permute-start.17 = (f32[8,2048]{1,0:T(8,128)S(1)}, f32[8,2048]{1,0:T(8,128)S(1)}, u32[]{:S(2)}, u32[]{:S(2)}) collective-permute-start(f32[8,2048]{1,0:T(8,128)S(1)} %add.33), channel_id=1, source_target_pairs={{0,2},{2,0},{4,6},{6,4},{8,10},{10,8},{12,14},{14,12},{1,3},{3,1},... | collective-permute-start | bytes 196616 | tf_op jit(solution)/shard_map/ppermute | solution.py:527
  91.2 5.1 %collective-permute-start.18 = (f32[8,2048]{1,0:T(8,128)S(1)}, f32[8,2048]{1,0:T(8,128)S(1)}, u32[]{:S(2)}, u32[]{:S(2)}) collective-permute-start(f32[8,2048]{1,0:T(8,128)S(1)} %add.34), channel_id=1, source_target_pairs={{0,4},{2,6},{4,0},{6,2},{8,12},{10,14},{12,8},{14,10},{1,5},{3,7},... | collective-permute-start | bytes 196616 | tf_op jit(solution)/shard_map/ppermute | solution.py:527
  96.4 5.2 %collective-permute-start.19 = (f32[8,2048]{1,0:T(8,128)S(1)}, f32[8,2048]{1,0:T(8,128)S(1)}, u32[]{:S(2)}, u32[]{:S(2)}) collective-permute-start(f32[8,2048]{1,0:T(8,128)S(1)} %add.35), channel_id=1, source_target_pairs={{0,8},{2,10},{4,12},{6,14},{8,0},{10,2},{12,4},{14,6},{1,9},{3,11}... | collective-permute-start | bytes 196616 | tf_op jit(solution)/shard_map/ppermute | solution.py:527
  101.6 1.3 %collective-permute-start.20 = (f32[8,2048]{1,0:T(8,128)S(1)}, f32[8,2048]{1,0:T(8,128)S(1)}, u32[]{:S(2)}, u32[]{:S(2)}) collective-permute-start(f32[8,2048]{1,0:T(8,128)S(1)} %add.36.mine_ref), channel_id=1, source_target_pairs={{0,1},{1,0},{2,3},{3,2},{4,5},{5,4},{6,7},{7,6},{8,9},{9,8},{10,11... | collective-permute-start | bytes 196616 | tf_op jit(solution)/shard_map/ppermute | solution.py:530

commit v7 on v6

--- a/solution.py
+++ b/solution.py
@@ -20,6 +20,7 @@
 ANY = pl.BlockSpec(memory_space=pl.ANY)
 
 STRIDE = 168
+SHARED = 48
 
 
 def params(mebibytes):
@@ -165,8 +166,8 @@
     return even.astype(BF), odd.astype(BF)
 
 
-def assemble_columns(inv_ref, inv_row, tiles_ref, put):
-    @pl.loop(0, 16)
+def assemble_columns(inv_ref, inv_row, tiles_ref, put, first_row=0, row_count=16):
+    @pl.loop(first_row, first_row + row_count)
     def _(block_row):
         for pair in range(8):
             cell = block_row * 16 + 2 * pair
@@ -179,8 +180,9 @@
 
 
 def head_kernel(
-    place_ref, tok_in_ref, gate_ref, up_ref, zone_out_ref, kind_out_ref, tok_ref, blocks_ref, sem
+    place_ref, tok_in_ref, gate_ref, up_ref, zone_out_ref, a_out_ref, b_out_ref, tok_ref, blocks_ref, sem
 ):
+    group = place_ref[1] // 2
     core = place_ref[3]
 
     @pl.when(core == 0)
@@ -195,22 +197,60 @@
     for zone in range(4):
         held = tok_ref.at[zone]
         lanes = pl.ds(2048 * zone, 2048)
-        loads.append(pltpu.make_async_copy(tok_in_ref.at[:, lanes], held, sem.at[2 + zone]))
-        stores.append(pltpu.make_async_copy(held, zone_out_ref.at[zone], sem.at[6 + zone]))
+        loads.append(pltpu.make_async_copy(tok_in_ref.at[:, lanes], held, sem.at[3 + zone]))
+        stores.append(pltpu.make_async_copy(held, zone_out_ref.at[zone], sem.at[7 + zone]))
     for load in loads:
         load.start()
     pltpu.make_async_copy(gate_ref, blocks_ref, sem.at[0]).wait()
-    kind_store = pltpu.make_async_copy(blocks_ref, kind_out_ref, sem.at[1])
-    kind_store.start()
-    for load, store in zip(loads, stores):
+    first = pl.multiple_of(SHARED * group, 16)
+    stores.append(
+        pltpu.make_async_copy(blocks_ref.at[pl.ds(first, SHARED)], a_out_ref, sem.at[1])
+    )
+    stores.append(
+        pltpu.make_async_copy(
+            blocks_ref.at[pl.ds(2 * SHARED, 160 - 2 * SHARED)], b_out_ref, sem.at[2]
+        )
+    )
+    stores[4].start()
+    stores[5].start()
+    for load, store in zip(loads, stores[:4]):
         load.wait()
         store.start()
     for store in stores:
         store.wait()
-    kind_store.wait()
 
 
 def own_kernel(
+    inv_ref, gate_ref, up_ref, weight_out_ref, tiles_ref, blocks_ref, weight_ref, in_sem, out_sem
+):
+    loads = [
+        pltpu.make_async_copy(source, blocks_ref.at[i], in_sem.at[i])
+        for i, source in enumerate((gate_ref, up_ref))
+    ]
+    for load in loads:
+        load.start()
+    clear_empty_slot(tiles_ref)
+    stores = []
+    for which in range(2):
+        loads[which].wait()
+        stage_blocks(blocks_ref.at[which], tiles_ref, 0)
+
+        def put(pair, row, piece):
+            lane = (pair % 2) * 128
+            weight_ref[4 * which + pair // 2, pl.ds(row, 32), lane : lane + 128] = piece
+
+        for half in range(2):
+            assemble_columns(inv_ref, which, tiles_ref, put, 8 * half, 8)
+            source = weight_ref.at[pl.ds(4 * which, 4), pl.ds(512 * half, 512)]
+            target = weight_out_ref.at[pl.ds(4 * which, 4), pl.ds(512 * half, 512)]
+            store = pltpu.make_async_copy(source, target, out_sem.at[2 * which + half])
+            store.start()
+            stores.append(store)
+    for store in stores:
+        store.wait()
+
+
+def payload_kernel(
     place_ref,
     inv_ref,
     gate_ref,
@@ -219,7 +259,6 @@
     sketch_ref,
     index_ref,
     value_ref,
-    weight_out_ref,
     payload_ref,
     tiles_ref,
     omega_ref,
@@ -228,7 +267,6 @@
     blocks_ref,
     weight_ref,
     in_sem,
-    out_sem,
 ):
     owner = place_ref[0]
     quarter = place_ref[1]
@@ -236,37 +274,9 @@
         pltpu.make_async_copy(source, blocks_ref.at[i], in_sem.at[i])
         for i, source in enumerate((gate_ref, up_ref, down_ref))
     ]
-    stores = [
-        pltpu.make_async_copy(
-            weight_ref.at[pl.ds(4 * i, 4)], weight_out_ref.at[pl.ds(4 * i, 4)], out_sem.at[i]
-        )
-        for i in range(2)
-    ]
     for load in loads:
         load.start()
     clear_empty_slot(tiles_ref)
-
-    for which in range(2):
-        loads[which].wait()
-        stage_blocks(blocks_ref.at[which], tiles_ref, 0)
-
-        def put(pair, row, piece):
-            lane = (pair % 2) * 128
-            weight_ref[4 * which + pair // 2, pl.ds(row, 32), lane : lane + 128] = piece
-
-        assemble_columns(inv_ref, which, tiles_ref, put)
-        stores[which].start()
-
-    loads[2].wait()
-    stage_blocks(blocks_ref.at[2], tiles_ref, 0)
-    for local_row in range(4):
-        for pair in range(8):
-            cell = (quarter * 4 + local_row) * 16 + 2 * pair
-            even, odd = assembled_pair(tiles_ref, inv_ref[2, cell], inv_ref[2, cell + 1])
-            row = local_row * BLK
-            down_dense_ref[row : row + 32, 128 * pair : 128 * (pair + 1)] = even
-            down_dense_ref[row + 32 : row + 64, 128 * pair : 128 * (pair + 1)] = odd
-    payload_ref[32:64, :] = contract_last(sketch_ref[...], down_dense_ref[...])
 
     local = index_ref[...] - owner * 1024
     inside = (local >= 0) & (local < 1024)
@@ -293,11 +303,35 @@
             split_ref[
                 16 * part_index : 16 * (part_index + 1), 128 * high : 128 * (high + 1)
             ] = part
+
     for which in range(2):
-        triple = dot(split_ref[...], weight_ref[4 * which + quarter])
+        loads[which].wait()
+        stage_blocks(blocks_ref.at[which], tiles_ref, 0)
+
+        @pl.loop(0, 16)
+        def _(block_row):
+            for pair in range(2):
+                cell = block_row * 16 + 4 * quarter + 2 * pair
+                even, odd = assembled_pair(
+                    tiles_ref, inv_ref[which, cell], inv_ref[which, cell + 1]
+                )
+                row = pl.multiple_of(block_row * BLK, BLK)
+                weight_ref[pl.ds(row, 32), 128 * pair : 128 * (pair + 1)] = even
+                weight_ref[pl.ds(row + 32, 32), 128 * pair : 128 * (pair + 1)] = odd
+
+        triple = dot(split_ref[...], weight_ref[...])
         payload_ref[16 * which : 16 * (which + 1), :] = triple[:16] + triple[16:32] + triple[32:]
-    for store in stores:
-        store.wait()
+
+    loads[2].wait()
+    stage_blocks(blocks_ref.at[2], tiles_ref, 0)
+    for local_row in range(4):
+        for pair in range(8):
+            cell = (quarter * 4 + local_row) * 16 + 2 * pair
+            even, odd = assembled_pair(tiles_ref, inv_ref[2, cell], inv_ref[2, cell + 1])
+            row = local_row * BLK
+            down_dense_ref[row : row + 32, 128 * pair : 128 * (pair + 1)] = even
+            down_dense_ref[row + 32 : row + 64, 128 * pair : 128 * (pair + 1)] = odd
+    payload_ref[32:64, :] = contract_last(sketch_ref[...], down_dense_ref[...])
 
 
 def flipped(two_bits, flip):
@@ -318,7 +352,9 @@
 def first_kernel(
     place_ref,
     inv_ref,
-    blocks_in_ref,
+    a_in_ref,
+    b_in_ref,
+    a_other_ref,
     weight_in_ref,
     tok_in_ref,
     keep_ref,
@@ -339,15 +375,23 @@
     zone = place_ref[0] // 2
     side = place_ref[2]
     core = place_ref[3]
+    group = place_ref[1] // 2
+    mine = pl.multiple_of(SHARED * group, 16)
+    other = pl.multiple_of(SHARED * (1 - group), 16)
     loads = [
-        pltpu.make_async_copy(blocks_in_ref, blocks_ref, in_sem.at[0]),
-        pltpu.make_async_copy(tok_in_ref, tok_ref, in_sem.at[1]),
-        pltpu.make_async_copy(weight_in_ref.at[pl.ds(4 * core, 4)], own_ref, in_sem.at[2]),
+        pltpu.make_async_copy(a_in_ref, blocks_ref.at[pl.ds(mine, SHARED)], in_sem.at[0]),
+        pltpu.make_async_copy(a_other_ref, blocks_ref.at[pl.ds(other, SHARED)], in_sem.at[1]),
+        pltpu.make_async_copy(
+            b_in_ref, blocks_ref.at[pl.ds(2 * SHARED, 160 - 2 * SHARED)], in_sem.at[2]
+        ),
+        pltpu.make_async_copy(tok_in_ref, tok_ref, in_sem.at[3]),
+        pltpu.make_async_copy(weight_in_ref.at[pl.ds(4 * core, 4)], own_ref, in_sem.at[4]),
     ]
     for load in loads:
         load.start()
     clear_empty_slot(tiles_ref)
-    loads[0].wait()
+    for load in loads[:3]:
+        load.wait()
     stage_blocks(blocks_ref, tiles_ref, 0)
 
     def put(pair, row, piece):
@@ -357,9 +401,9 @@
     assemble_columns(inv_ref, core, tiles_ref, put)
     near_store = pltpu.make_async_copy(near_ref, near_out_ref, near_sem)
     near_store.start()
-    loads[1].wait()
+    loads[3].wait()
     shuffle_tokens(side, tok_ref, tokens_ref)
-    loads[2].wait()
+    loads[4].wait()
     stores = []
     for chunk in range(4):
         total = dot(tokens_ref[0], own_ref[chunk]) + dot(tokens_ref[1], near_ref[chunk])
@@ -430,10 +474,6 @@
     pay1_ref,
     pay2_ref,
     pay3_ref,
-    across0_ref,
-    across1_ref,
-    across2_ref,
-    across3_ref,
     mine_ref,
     theirs_ref,
     lead_ref,
@@ -447,10 +487,8 @@
     quarter = place_ref[1]
     core = place_ref[3]
     unshuffle = unshuffle_matrix(256)
-    near_parts = (pay0_ref, pay1_ref, pay2_ref, pay3_ref)
-    across_parts = (across0_ref, across1_ref, across2_ref, across3_ref)
-    for flip in range(4):
-        pay_ref[flipped(quarter, flip)] = near_parts[flip][...] + across_parts[flip][...]
+    for flip, ref in enumerate((pay0_ref, pay1_ref, pay2_ref, pay3_ref)):
+        pay_ref[flipped(quarter, flip)] = ref[...]
     for chunk in range(4):
         cols = slice(256 * chunk, 256 * (chunk + 1))
         proj_ref[:, cols] = dot(pay_ref[chunk, 32:64, :].astype(BF), unshuffle).astype(BF)
@@ -539,23 +577,25 @@
             axis_index_groups=[[0, 2, 4, 6], [1, 3, 5, 7]],
         )
 
-    by_zone, kind = pl.pallas_call(
+    by_zone, kind_a, kind_b = pl.pallas_call(
         head_kernel,
         out_shape=(
             jax.ShapeDtypeStruct((4, 64, 2048), BF),
-            jax.ShapeDtypeStruct((160, 4096), BF),
+            jax.ShapeDtypeStruct((SHARED, 4096), BF),
+            jax.ShapeDtypeStruct((160 - 2 * SHARED, 4096), BF),
         ),
         in_specs=[SMEM, HBM, HBM, HBM],
-        out_specs=(HBM, HBM),
+        out_specs=(HBM,) * 3,
         scratch_shapes=[
             pltpu.VMEM((4, 64, 2048), BF),
             pltpu.VMEM((160, 4096), BF),
-            pltpu.SemaphoreType.DMA((10,)),
+            pltpu.SemaphoreType.DMA((11,)),
         ],
         compiler_params=params(60),
         name="head",
     )(place, tokens, gate_blocks, up_blocks)
-    near = owner_flip(kind, 1)
+    near_a = owner_flip(kind_a, 1)
+    near_b = owner_flip(kind_b, 1)
     gathered = zone_exchange(by_zone)
 
     slots = jnp.stack([gate_slot, up_slot, down_slot])
@@ -564,38 +604,46 @@
     inv = jnp.min(jnp.where(slots[:, :, None] == cells, slot_numbers, 160), axis=1)
     near_inv = owner_flip(inv, 1)
 
-    weights, payload = pl.pallas_call(
-        own_kernel,
-        out_shape=(
-            jax.ShapeDtypeStruct((8, 1024, 256), BF),
-            jax.ShapeDtypeStruct((64, 256), F32),
-        ),
+    payload = pl.pallas_call(
+        payload_kernel,
+        out_shape=jax.ShapeDtypeStruct((64, 256), F32),
         in_specs=[SMEM, SMEM] + [HBM] * 3 + [VMEM] * 3,
-        out_specs=(HBM, VMEM),
+        out_specs=VMEM,
         scratch_shapes=[
             pltpu.VMEM((32 * STRIDE, 128), F32),
             pltpu.VMEM((128, 128), F32),
             pltpu.VMEM((48, 1024), BF),
             pltpu.VMEM((256, 1024), BF),
             pltpu.VMEM((3, 160, 4096), BF),
+            pltpu.VMEM((1024, 256), BF),
+            pltpu.SemaphoreType.DMA((3,)),
+        ],
+        compiler_params=params(59.5),
+        name="probe_terms",
+    )(place, inv, gate_blocks, up_blocks, down_blocks, sketch, probe_index, probe_value)
+
+    weights = pl.pallas_call(
+        own_kernel,
+        out_shape=jax.ShapeDtypeStruct((8, 1024, 256), BF),
+        in_specs=[SMEM, HBM, HBM],
+        out_specs=HBM,
+        scratch_shapes=[
+            pltpu.VMEM((32 * STRIDE, 128), F32),
+            pltpu.VMEM((2, 160, 4096), BF),
             pltpu.VMEM((8, 1024, 256), BF),
-            pltpu.SemaphoreType.DMA((3,)),
             pltpu.SemaphoreType.DMA((2,)),
+            pltpu.SemaphoreType.DMA((4,)),
         ],
-        compiler_params=params(60),
+        compiler_params=params(59.5),
         name="own_blocks",
-    )(place, inv, gate_blocks, up_blocks, down_blocks, sketch, probe_index, probe_value)
-
-    from_zones = [owner_flip(payload, bits) for bits in (4, 6, 2)]
-    payload = payload + from_zones[0] + from_zones[1] + from_zones[2]
-    pay_parts = [
-        payload,
-        core_flip(payload),
-        lax.ppermute(payload, "groups", [(0, 1), (1, 0)]),
-        lax.ppermute(payload, ("groups", "seq"), [(i, i ^ 3) for i in range(4)]),
-    ]
-    near, near_inv, gathered, pay_parts = lax.optimization_barrier(
-        (near, near_inv, gathered, pay_parts)
+    )(inv, gate_blocks, up_blocks)
+
+    near_a, payload = lax.optimization_barrier((near_a, payload))
+    near_a_other = lax.ppermute(near_a, "groups", [(0, 1), (1, 0)])
+    for bits in (2, 4):
+        payload = payload + owner_flip(payload, bits)
+    near_inv, near_b, near_a_other, gathered, payload, weights = lax.optimization_barrier(
+        (near_inv, near_b, near_a_other, gathered, payload, weights)
     )
 
     first_keep, first_sent, near_weights = pl.pallas_call(
@@ -605,7 +653,7 @@
             jax.ShapeDtypeStruct((4, 64, 1024), BF),
             jax.ShapeDtypeStruct((4, 1024, 256), BF),
         ),
-        in_specs=[SMEM, SMEM, ANY, HBM, ANY],
+        in_specs=[SMEM, SMEM, ANY, ANY, ANY, HBM, ANY],
         out_specs=(VMEM, HBM, HBM),
         scratch_shapes=[
             pltpu.VMEM((160, 4096), BF),
@@ -616,13 +664,13 @@
             pltpu.VMEM((2, 256, 1024), BF),
             pltpu.VMEM((4, 64, 1024), BF),
             pltpu.VMEM((256, 256), F32),
-            pltpu.SemaphoreType.DMA((3,)),
+            pltpu.SemaphoreType.DMA((5,)),
             pltpu.SemaphoreType.DMA,
             pltpu.SemaphoreType.DMA((4,)),
         ],
         compiler_params=params(50),
         name="first_partial",
-    )(place, near_inv, near, weights, gathered)
+    )(place, near_inv, near_a, near_b, near_a_other, weights, gathered)
     first_back = zone_exchange(first_sent)
 
     second_keep, *second_sent = pl.pallas_call(
@@ -644,7 +692,15 @@
     )(place, core_flip(near_weights), weights, gathered)
     second_back = [owner_flip(second_sent[flip - 1], 2 * flip) for flip in (1, 2, 3)]
 
-    pay_parts = pay_parts + [owner_flip(part, 1) for part in pay_parts]
+    across = owner_flip(payload, 1)
+    second_keep, across = lax.optimization_barrier((second_keep, across))
+    payload = payload + across
+    pay_parts = [
+        payload,
+        core_flip(payload),
+        lax.ppermute(payload, "groups", [(0, 1), (1, 0)]),
+        lax.ppermute(payload, ("groups", "seq"), [(i, i ^ 3) for i in range(4)]),
+    ]
 
     first_back, weights = lax.optimization_barrier((first_back, weights))
     weights_at_hand = pl.pallas_call(
@@ -661,7 +717,7 @@
     mine, theirs = pl.pallas_call(
         middle_kernel,
         out_shape=(jax.ShapeDtypeStruct((8, 2048), F32),) * 2,
-        in_specs=[SMEM] + [VMEM] * 14,
+        in_specs=[SMEM] + [VMEM] * 10,
         out_specs=(VMEM,) * 2,
         scratch_shapes=[
             pltpu.VMEM((64, 1024), F32),

time: 106 us -> 102 us (0.962)
  waiting for transfers between devices: 37.1 us -> 27.3 us
  Pallas kernels: 31.2 us -> 37.5 us
    ppermute x15 -> x12, waiting for transfers between devices: 31.3 us -> 20 us  [owner_flip(): return lax.ppermute(value, 'fsdp', [(i, i ^ bits) for i in range(8)])]
    pallas_call x1 -> x2, Pallas kernels: 9.59 us -> 15.6 us  [the longest x1 8.07 us: pair_split(): pl.pallas_call(own_kernel, out_shape=jax.ShapeDtypeStruct((8, 1024, 256),...]
    ppermute x15 -> x12, starting transfers between devices: 22.6 us -> 20.9 us  [owner_flip(): return lax.ppermute(value, 'fsdp', [(i, i ^ bits) for i in range(8)])]
    ppermute x0 -> x1, starting transfers between devices: none -> 1.52 us  [pair_split(): near_a_other = lax.ppermute(near_a, 'groups', [(0, 1), (1, 0)])]
    all_to_all x2, waiting for transfers between devices: 3.12 us -> 4.39 us  [zone_exchange(): lax.all_to_all(value, 'fsdp', split_axis=0, concat_axis=0, tiled=True, ax...]
  transfers between devices with their start and end apart: 23 -> 21, of which waited for: 12 -> 10; matrix products, arithmetic and copies ran while one was open for 2% -> 2% of each run, Pallas kernels for 15% -> 22%
where the time goes in v7:
time: 102 us
  Pallas kernels  37.5 us (37%)
  starting transfers between devices  34.2 us (34%)
  waiting for transfers between devices  27.3 us (27%)
  other arithmetic  2.25 us (2%)
    ppermute x12, starting transfers between devices, owner_flip(): return lax.ppermute(value, 'fsdp', [(i, i ^ bits) for i in range(8)])  20.9 us
    ppermute x12, waiting for transfers between devices, owner_flip(): return lax.ppermute(value, 'fsdp', [(i, i ^ bits) for i in range(8)])  20 us
    all_to_all x2, starting transfers between devices, zone_exchange(): lax.all_to_all(value, 'fsdp', split_axis=0, concat_axis=0, tiled=True, ax...  9.94 us
    pallas_call x1, Pallas kernels, pair_split(): pl.pallas_call(own_kernel, out_shape=jax.ShapeDtypeStruct((8, 1024, 256),...  8.07 us
    pallas_call x1, Pallas kernels, pair_split(): pl.pallas_call(payload_kernel, out_shape=jax.ShapeDtypeStruct((64, 256),...  7.49 us
    pallas_call x1, Pallas kernels, pair_split(): pl.pallas_call(first_kernel, out_shape=(jax.ShapeDtypeStruct((64, 1024),...  6.23 us
    all_to_all x2, waiting for transfers between devices, zone_exchange(): lax.all_to_all(value, 'fsdp', split_axis=0, concat_axis=0, tiled=True, ax...  4.39 us
    pallas_call x1, Pallas kernels, pair_split(): pl.pallas_call(second_kernel, out_shape=(jax.ShapeDtypeStruct((64, 1024),...  4.25 us
  transfers between devices with their start and end apart: 21, of which 10 were waited for; matrix products, arithmetic and copies ran while one was open for 2% of the time, Pallas kernels for 22%

profile of v7, /device:TPU:0, one launch (start us, length us, event | category | flops | bytes accessed | tf_op | source)
XLA Modules:
  0.0 101.6 jit_solution(2350983457695417437)
XLA Ops:
  0.6 3.5 %head.1 = (bf16[4,64,2048]{2,1,0:T(8,128)(2,1)}, bf16[48,4096]{1,0:T(8,128)(2,1)}, bf16[64,4096]{1,0:T(8,128)(2,1)}) custom-call(s32[4]{0:T(128)} %pad_add_fusion.1.place_ref, bf16[64,8192]{1,0:T(8,128)(2,1)} %tok_in_ref.1, bf16[160,4096]{1,0:T(8,128)(2,1)} %gate_ref.5, bf16[160,4096]{1,0:T(8,128)(2,1)} %up_ref.5), custom_call_target="tpu_custom_call" | custom-call | tf_op jit(solution)/shard_map/head/pallas_call | solution.py:580
  4.1 6.5 %all-to-all-start = ((bf16[4,64,2048]{2,1,0:T(8,128)(2,1)}), bf16[4,64,2048]{2,1,0:T(8,128)(2,1)S(1)}, u32[]{:S(2)}, u32[]{:S(2)}) async-start(bf16[4,64,2048]{2,1,0:T(8,128)(2,1)} %get-tuple-element.34), calls=%async_computation | async-start | bytes 2097152 | tf_op jit(solution)/shard_map/all_to_all | solution.py:571
  10.6 1.5 %collective-permute-start.2 = (bf16[48,4096]{1,0:T(8,128)(2,1)S(1)}, bf16[48,4096]{1,0:T(8,128)(2,1)S(1)}, u32[]{:S(2)}, u32[]{:S(2)}) collective-permute-start(bf16[48,4096]{1,0:T(8,128)(2,1)S(1)} %copy-done.6), channel_id=1, source_target_pairs={{0,2},{2,0},{4,6},{6,4},{8,10},{10,8},{12,14},{14,12},{1,3},{3,1},... | collective-permute-start | bytes 1179656 | tf_op jit(solution)/shard_map/ppermute | solution.py:565
  12.6 0.7 select_reduce_fusion.inv_ref
  13.4 7.5 %probe_terms.1 = f32[64,256]{1,0:T(8,128)} custom-call(s32[4]{0:T(128)} %pad_add_fusion.1.place_ref, s32[3,256]{1,0:T(4,128)} %select_reduce_fusion.inv_ref, bf16[160,4096]{1,0:T(8,128)(2,1)} %gate_ref.5, bf16[160,4096]{1,0:T(8,128)(2,1)} %up_ref.5, bf16[160,4096]{1,0:T(8,128)(2,1)} %down_ref.1, bf16[32,1024]{1,0:T(8,128)(2,1)} %sketch_ref.1, ...), custom_call_target="tpu_custom_call" | custom-call | tf_op jit(solution)/shard_map/probe_terms/pallas_call | solution.py:607
  20.9 1.7 %collective-permute-done.2.a_in_ref = bf16[48,4096]{1,0:T(8,128)(2,1)S(1)} collective-permute-done((bf16[48,4096]{1,0:T(8,128)(2,1)S(1)}, bf16[48,4096]{1,0:T(8,128)(2,1)S(1)}, u32[]{:S(2)}, u32[]{:S(2)}) %collective-permute-start.2) | collective-permute-done | bytes 393248 | tf_op jit(solution)/shard_map/ppermute | solution.py:565
  22.6 1.5 %collective-permute-start.3 = (bf16[48,4096]{1,0:T(8,128)(2,1)S(1)}, bf16[48,4096]{1,0:T(8,128)(2,1)S(1)}, u32[]{:S(2)}, u32[]{:S(2)}) collective-permute-start(bf16[48,4096]{1,0:T(8,128)(2,1)S(1)} %collective-permute-done.2.a_in_ref), channel_id=1, source_target_pairs={{0,16},{16,0},{1,17},{17,1},{2,18},{18,2},{3,19},{19,3},{4,20},{20... | collective-permute-start | bytes 1179656 | tf_op jit(solution)/shard_map/ppermute | solution.py:642
  24.2 2.0 %collective-permute-start.4 = (f32[64,256]{1,0:T(8,128)}, f32[64,256]{1,0:T(8,128)S(1)}, u32[]{:S(2)}, u32[]{:S(2)}) collective-permute-start(f32[64,256]{1,0:T(8,128)} %probe_terms.1), channel_id=1, source_target_pairs={{0,4},{2,6},{4,0},{6,2},{8,12},{10,14},{12,8},{14,10},{1,5},{3,7},... | collective-permute-start | bytes 196616 | tf_op jit(solution)/shard_map/ppermute | solution.py:565
  26.2 3.0 %collective-permute-done.4 = f32[64,256]{1,0:T(8,128)S(1)} collective-permute-done((f32[64,256]{1,0:T(8,128)}, f32[64,256]{1,0:T(8,128)S(1)}, u32[]{:S(2)}, u32[]{:S(2)}) %collective-permute-start.4) | collective-permute-done | bytes 65568 | tf_op jit(solution)/shard_map/ppermute | solution.py:565
  29.2 0.8 add.30
  30.0 4.6 %collective-permute-start.5 = (f32[64,256]{1,0:T(8,128)S(1)}, f32[64,256]{1,0:T(8,128)S(1)}, u32[]{:S(2)}, u32[]{:S(2)}) collective-permute-start(f32[64,256]{1,0:T(8,128)S(1)} %add.30), channel_id=1, source_target_pairs={{0,8},{2,10},{4,12},{6,14},{8,0},{10,2},{12,4},{14,6},{1,9},{3,11}... | collective-permute-start | bytes 196616 | tf_op jit(solution)/shard_map/ppermute | solution.py:565
  34.6 1.5 %collective-permute-start = (s32[3,256]{1,0:T(4,128)S(1)}, s32[3,256]{1,0:T(4,128)S(1)}, u32[]{:S(2)}, u32[]{:S(2)}) collective-permute-start(s32[3,256]{1,0:T(4,128)S(1)} %copy-done.1), channel_id=1, source_target_pairs={{0,2},{2,0},{4,6},{6,4},{8,10},{10,8},{12,14},{14,12},{1,3},{3,1},... | collective-permute-start | bytes 9224 | tf_op jit(solution)/shard_map/ppermute | solution.py:565
  36.1 8.1 %own_blocks.1.weight_in_ref = bf16[8,1024,256]{2,1,0:T(8,128)(2,1)} custom-call(s32[3,256]{1,0:T(4,128)} %select_reduce_fusion.inv_ref, bf16[160,4096]{1,0:T(8,128)(2,1)} %gate_ref.5, bf16[160,4096]{1,0:T(8,128)(2,1)} %up_ref.5), custom_call_target="tpu_custom_call" | custom-call | tf_op jit(solution)/shard_map/own_blocks/pallas_call | solution.py:625
  44.2 6.2 %first_partial.1 = (f32[64,1024]{1,0:T(8,128)S(1)}, bf16[4,64,1024]{2,1,0:T(8,128)(2,1)}, bf16[4,1024,256]{2,1,0:T(8,128)(2,1)}) custom-call(s32[4]{0:T(128)S(1)} %copy-done, s32[3,256]{1,0:T(4,128)S(1)} %collective-permute-done.inv_ref, bf16[48,4096]{1,0:T(8,128)(2,1)S(1)} %collective-permute-done.2.a_in_ref, ...), custom_call_target="tpu_custom_call" | custom-call | tf_op jit(solution)/shard_map/first_partial/pallas_call | solution.py:649
  50.6 3.5 %all-to-all-start.1 = ((bf16[4,64,1024]{2,1,0:T(8,128)(2,1)}), bf16[4,64,1024]{2,1,0:T(8,128)(2,1)S(1)}, u32[]{:S(2)}, u32[]{:S(2)}) async-start(bf16[4,64,1024]{2,1,0:T(8,128)(2,1)} %get-tuple-element.42), calls=%async_computation.1 | async-start | bytes 1048576 | tf_op jit(solution)/shard_map/all_to_all | solution.py:571
  55.0 4.2 %second_partial.1 = (f32[64,1024]{1,0:T(8,128)S(1)}, bf16[64,1024]{1,0:T(8,128)(2,1)S(1)}, bf16[64,1024]{1,0:T(8,128)(2,1)S(1)}, bf16[64,1024]{1,0:T(8,128)(2,1)S(1)}) custom-call(s32[4]{0:T(128)S(1)} %copy-done, bf16[4,1024,256]{2,1,0:T(8,128)(2,1)} %collective-permute-done.6.near_in_ref, bf16[8,1024,256]{2,1,0:T(8,128)(2,1)} %own_blocks.1.weight_in_ref, ...), custom_call_target="tpu_custom_call" | custom-call | tf_op jit(solution)/shard_map/second_partial/pallas_call | solution.py:676
  59.3 1.6 %collective-permute-start.8 = (bf16[64,1024]{1,0:T(8,128)(2,1)S(1)}, bf16[64,1024]{1,0:T(8,128)(2,1)S(1)}, u32[]{:S(2)}, u32[]{:S(2)}) collective-permute-start(bf16[64,1024]{1,0:T(8,128)(2,1)S(1)} %get-tuple-element.48), channel_id=1, source_target_pairs={{0,4},{2,6},{4,0},{6,2},{8,12},{10,14},{12,8},{14,10},{1,5},{3,7},... | collective-permute-start | bytes 393224 | tf_op jit(solution)/shard_map/ppermute | solution.py:565
  61.0 2.4 %collective-permute-start.9 = (bf16[64,1024]{1,0:T(8,128)(2,1)S(1)}, bf16[64,1024]{1,0:T(8,128)(2,1)S(1)}, u32[]{:S(2)}, u32[]{:S(2)}) collective-permute-start(bf16[64,1024]{1,0:T(8,128)(2,1)S(1)} %get-tuple-element.49), channel_id=1, source_target_pairs={{0,8},{2,10},{4,12},{6,14},{8,0},{10,2},{12,4},{14,6},{1,9},{3,11}... | collective-permute-start | bytes 393224 | tf_op jit(solution)/shard_map/ppermute | solution.py:565
  63.9 1.5 %collective-permute-start.12 = (f32[64,256]{1,0:T(8,128)S(1)}, f32[64,256]{1,0:T(8,128)S(1)}, u32[]{:S(2)}, u32[]{:S(2)}) collective-permute-start(f32[64,256]{1,0:T(8,128)S(1)} %add.32.pay0_ref), channel_id=1, source_target_pairs={{0,16},{16,0},{1,17},{17,1},{2,18},{18,2},{3,19},{19,3},{4,20},{20... | collective-permute-start | bytes 196616 | tf_op jit(solution)/shard_map/ppermute | solution.py:701
  65.4 4.4 %all-to-all-done.1.first_ref = bf16[4,64,1024]{2,1,0:T(8,128)(2,1)S(1)} async-done(((bf16[4,64,1024]{2,1,0:T(8,128)(2,1)}), bf16[4,64,1024]{2,1,0:T(8,128)(2,1)S(1)}, u32[]{:S(2)}, u32[]{:S(2)}) %all-to-all-start.1) | async-done | bytes 524320 | tf_op jit(solution)/shard_map/all_to_all | solution.py:571
  69.8 2.2 %fetch_weights.1.weight_ref = bf16[8,1024,256]{2,1,0:T(8,128)(2,1)S(1)} custom-call(bf16[8,1024,256]{2,1,0:T(8,128)(2,1)} %own_blocks.1.weight_in_ref), custom_call_target="tpu_custom_call" | custom-call | tf_op jit(solution)/shard_map/fetch_weights/pallas_call | solution.py:706
  72.1 6.2 %collective-permute-done.9.second2_ref = bf16[64,1024]{1,0:T(8,128)(2,1)S(1)} collective-permute-done((bf16[64,1024]{1,0:T(8,128)(2,1)S(1)}, bf16[64,1024]{1,0:T(8,128)(2,1)S(1)}, u32[]{:S(2)}, u32[]{:S(2)}) %collective-permute-start.9) | collective-permute-done | bytes 131104 | tf_op jit(solution)/shard_map/ppermute | solution.py:565
  78.3 3.2 %token_sums.1 = (f32[8,2048]{1,0:T(8,128)S(1)}, f32[8,2048]{1,0:T(8,128)S(1)}) custom-call(s32[4]{0:T(128)S(1)} %copy-done, f32[64,1024]{1,0:T(8,128)S(1)} %get-tuple-element.41.first_keep_ref, bf16[4,64,1024]{2,1,0:T(8,128)(2,1)S(1)} %all-to-all-done.1.first_ref, f32[64,1024]{1,0:T(8,128)S(1)} %get-tuple-element.47.second_keep_ref, ...), custom_call_target="tpu_custom_call" | custom-call | tf_op jit(solution)/shard_map/token_sums/pallas_call | solution.py:717
  81.5 1.2 %collective-permute-done.14 = f32[8,2048]{1,0:T(8,128)S(1)} collective-permute-done((f32[8,2048]{1,0:T(8,128)S(1)}, f32[8,2048]{1,0:T(8,128)S(1)}, u32[]{:S(2)}, u32[]{:S(2)}) %collective-permute-start.14) | collective-permute-done | bytes 65568 | tf_op jit(solution)/shard_map/ppermute | solution.py:568
  82.8 0.6 collective-permute-start.15
  83.4 3.7 %collective-permute-done.15 = f32[8,2048]{1,0:T(8,128)S(1)} collective-permute-done((f32[8,2048]{1,0:T(8,128)S(1)}, f32[8,2048]{1,0:T(8,128)S(1)}, u32[]{:S(2)}, u32[]{:S(2)}) %collective-permute-start.15) | collective-permute-done | bytes 65568 | tf_op jit(solution)/shard_map/ppermute | solution.py:565
  87.1 3.0 %collective-permute-start.16 = (f32[8,2048]{1,0:T(8,128)S(1)}, f32[8,2048]{1,0:T(8,128)S(1)}, u32[]{:S(2)}, u32[]{:S(2)}) collective-permute-start(f32[8,2048]{1,0:T(8,128)S(1)} %add.34), channel_id=1, source_target_pairs={{0,4},{2,6},{4,0},{6,2},{8,12},{10,14},{12,8},{14,10},{1,5},{3,7},... | collective-permute-start | bytes 196616 | tf_op jit(solution)/shard_map/ppermute | solution.py:565
  90.1 2.2 %collective-permute-done.16 = f32[8,2048]{1,0:T(8,128)S(1)} collective-permute-done((f32[8,2048]{1,0:T(8,128)S(1)}, f32[8,2048]{1,0:T(8,128)S(1)}, u32[]{:S(2)}, u32[]{:S(2)}) %collective-permute-start.16) | collective-permute-done | bytes 65568 | tf_op jit(solution)/shard_map/ppermute | solution.py:565
  92.4 2.1 %collective-permute-start.17 = (f32[8,2048]{1,0:T(8,128)S(1)}, f32[8,2048]{1,0:T(8,128)S(1)}, u32[]{:S(2)}, u32[]{:S(2)}) collective-permute-start(f32[8,2048]{1,0:T(8,128)S(1)} %add.35), channel_id=1, source_target_pairs={{0,8},{2,10},{4,12},{6,14},{8,0},{10,2},{12,4},{14,6},{1,9},{3,11}... | collective-permute-start | bytes 196616 | tf_op jit(solution)/shard_map/ppermute | solution.py:565
  94.5 3.1 %collective-permute-done.17 = f32[8,2048]{1,0:T(8,128)S(1)} collective-permute-done((f32[8,2048]{1,0:T(8,128)S(1)}, f32[8,2048]{1,0:T(8,128)S(1)}, u32[]{:S(2)}, u32[]{:S(2)}) %collective-permute-start.17) | collective-permute-done | bytes 65568 | tf_op jit(solution)/shard_map/ppermute | solution.py:565
  97.7 1.2 %collective-permute-done.18.theirs_ref = f32[8,2048]{1,0:T(8,128)S(1)} collective-permute-done((f32[8,2048]{1,0:T(8,128)S(1)}, f32[8,2048]{1,0:T(8,128)S(1)}, u32[]{:S(2)}, u32[]{:S(2)}) %collective-permute-start.18) | collective-permute-done | bytes 65568 | tf_op jit(solution)/shard_map/ppermute | solution.py:568
  99.0 2.6 %products.1 = f32[16,1024]{1,0:T(8,128)} custom-call(s32[4]{0:T(128)S(1)} %copy-done, f32[8,2048]{1,0:T(8,128)S(1)} %add.36.mine_ref, f32[8,2048]{1,0:T(8,128)S(1)} %collective-permute-done.18.theirs_ref, bf16[8,1024,256]{2,1,0:T(8,128)(2,1)S(1)} %fetch_weights.1.weight_ref), custom_call_target="tpu_custom_call" | custom-call | tf_op jit(solution)/shard_map/products/pallas_call | solution.py:738
  (42 shorter events, 3.0 us)
Async XLA Ops:
  0.6 12.0 %copy-start.2 = (s32[160]{0:T(256)S(1)}, s32[160]{0:T(256)}, u32[]{:S(2)}) copy-start(s32[160]{0:T(256)} %param.16) | copy-start | bytes 1924
  0.6 12.0 %copy-start.3 = (s32[160]{0:T(256)S(1)}, s32[160]{0:T(256)}, u32[]{:S(2)}) copy-start(s32[160]{0:T(256)} %param.14) | copy-start | bytes 1924
  0.6 12.0 %copy-start.4 = (s32[160]{0:T(256)S(1)}, s32[160]{0:T(256)}, u32[]{:S(2)}) copy-start(s32[160]{0:T(256)} %param.12) | copy-start | bytes 1924
  4.1 6.5 %copy-start.6 = (bf16[48,4096]{1,0:T(8,128)(2,1)S(1)}, bf16[48,4096]{1,0:T(8,128)(2,1)}, u32[]{:S(2)}) copy-start(bf16[48,4096]{1,0:T(8,128)(2,1)} %get-tuple-element.32) | copy-start | bytes 1179652
  4.1 8.0 %copy-start.5 = (bf16[64,4096]{1,0:T(8,128)(2,1)S(1)}, bf16[64,4096]{1,0:T(8,128)(2,1)}, u32[]{:S(2)}) copy-start(bf16[64,4096]{1,0:T(8,128)(2,1)} %get-tuple-element.31) | copy-start | bytes 1572868
  4.1 40.1 %all-to-all-start = ((bf16[4,64,2048]{2,1,0:T(8,128)(2,1)}), bf16[4,64,2048]{2,1,0:T(8,128)(2,1)S(1)}, u32[]{:S(2)}, u32[]{:S(2)}) async-start(bf16[4,64,2048]{2,1,0:T(8,128)(2,1)} %get-tuple-element.34), calls=%async_computation | async-start | bytes 2097152 | tf_op jit(solution)/shard_map/all_to_all | solution.py:571
  10.6 12.0 %collective-permute-start.2 = (bf16[48,4096]{1,0:T(8,128)(2,1)S(1)}, bf16[48,4096]{1,0:T(8,128)(2,1)S(1)}, u32[]{:S(2)}, u32[]{:S(2)}) collective-permute-start(bf16[48,4096]{1,0:T(8,128)(2,1)S(1)} %copy-done.6), channel_id=1, source_target_pairs={{0,2},{2,0},{4,6},{6,4},{8,10},{10,8},{12,14},{14,12},{1,3},{3,1},... | collective-permute-start | bytes 1179656 | tf_op jit(solution)/shard_map/ppermute | solution.py:565
  12.1 32.1 %collective-permute-start.1 = (bf16[64,4096]{1,0:T(8,128)(2,1)S(1)}, bf16[64,4096]{1,0:T(8,128)(2,1)S(1)}, u32[]{:S(2)}, u32[]{:S(2)}) collective-permute-start(bf16[64,4096]{1,0:T(8,128)(2,1)S(1)} %copy-done.5), channel_id=1, source_target_pairs={{0,2},{2,0},{4,6},{6,4},{8,10},{10,8},{12,14},{14,12},{1,3},{3,1},... | collective-permute-start | bytes 1572872 | tf_op jit(solution)/shard_map/ppermute | solution.py:565
  13.4 21.2 %copy-start.1 = (s32[3,256]{1,0:T(4,128)S(1)}, s32[3,256]{1,0:T(4,128)}, u32[]{:S(2)}) copy-start(s32[3,256]{1,0:T(4,128)} %select_reduce_fusion.inv_ref) | copy-start | bytes 9220
  22.6 21.6 %collective-permute-start.3 = (bf16[48,4096]{1,0:T(8,128)(2,1)S(1)}, bf16[48,4096]{1,0:T(8,128)(2,1)S(1)}, u32[]{:S(2)}, u32[]{:S(2)}) collective-permute-start(bf16[48,4096]{1,0:T(8,128)(2,1)S(1)} %collective-permute-done.2.a_in_ref), channel_id=1, source_target_pairs={{0,16},{16,0},{1,17},{17,1},{2,18},{18,2},{3,19},{19,3},{4,20},{20... | collective-permute-start | bytes 1179656 | tf_op jit(solution)/shard_map/ppermute | solution.py:642
  24.2 5.0 %collective-permute-start.4 = (f32[64,256]{1,0:T(8,128)}, f32[64,256]{1,0:T(8,128)S(1)}, u32[]{:S(2)}, u32[]{:S(2)}) collective-permute-start(f32[64,256]{1,0:T(8,128)} %probe_terms.1), channel_id=1, source_target_pairs={{0,4},{2,6},{4,0},{6,2},{8,12},{10,14},{12,8},{14,10},{1,5},{3,7},... | collective-permute-start | bytes 196616 | tf_op jit(solution)/shard_map/ppermute | solution.py:565
  30.0 14.2 %copy-start = (s32[4]{0:T(128)S(1)}, s32[4]{0:T(128)}, u32[]{:S(2)}) copy-start(s32[4]{0:T(128)} %pad_add_fusion.1.place_ref) | copy-start | bytes 52
  30.0 14.1 %collective-permute-start.5 = (f32[64,256]{1,0:T(8,128)S(1)}, f32[64,256]{1,0:T(8,128)S(1)}, u32[]{:S(2)}, u32[]{:S(2)}) collective-permute-start(f32[64,256]{1,0:T(8,128)S(1)} %add.30), channel_id=1, source_target_pairs={{0,8},{2,10},{4,12},{6,14},{8,0},{10,2},{12,4},{14,6},{1,9},{3,11}... | collective-permute-start | bytes 196616 | tf_op jit(solution)/shard_map/ppermute | solution.py:565
  34.6 9.6 %collective-permute-start = (s32[3,256]{1,0:T(4,128)S(1)}, s32[3,256]{1,0:T(4,128)S(1)}, u32[]{:S(2)}, u32[]{:S(2)}) collective-permute-start(s32[3,256]{1,0:T(4,128)S(1)} %copy-done.1), channel_id=1, source_target_pairs={{0,2},{2,0},{4,6},{6,4},{8,10},{10,8},{12,14},{14,12},{1,3},{3,1},... | collective-permute-start | bytes 9224 | tf_op jit(solution)/shard_map/ppermute | solution.py:565
  50.5 4.6 %collective-permute-start.6 = (bf16[4,1024,256]{2,1,0:T(8,128)(2,1)}, bf16[4,1024,256]{2,1,0:T(8,128)(2,1)}, u32[]{:S(2)}, u32[]{:S(2)}) collective-permute-start(bf16[4,1024,256]{2,1,0:T(8,128)(2,1)} %get-tuple-element.44), channel_id=1, source_target_pairs={{0,1},{1,0},{2,3},{3,2},{4,5},{5,4},{6,7},{7,6},{8,9},{9,8},{10,11... | collective-permute-start | bytes 6291464 | tf_op jit(solution)/shard_map/ppermute | solution.py:568
  50.6 19.3 %all-to-all-start.1 = ((bf16[4,64,1024]{2,1,0:T(8,128)(2,1)}), bf16[4,64,1024]{2,1,0:T(8,128)(2,1)S(1)}, u32[]{:S(2)}, u32[]{:S(2)}) async-start(bf16[4,64,1024]{2,1,0:T(8,128)(2,1)} %get-tuple-element.42), calls=%async_computation.1 | async-start | bytes 1048576 | tf_op jit(solution)/shard_map/all_to_all | solution.py:571
  54.0 5.3 %collective-permute-start.7 = (f32[64,256]{1,0:T(8,128)S(1)}, f32[64,256]{1,0:T(8,128)S(1)}, u32[]{:S(2)}, u32[]{:S(2)}) collective-permute-start(f32[64,256]{1,0:T(8,128)S(1)} %add.31), channel_id=1, source_target_pairs={{0,2},{2,0},{4,6},{6,4},{8,10},{10,8},{12,14},{14,12},{1,3},{3,1},... | collective-permute-start | bytes 196616 | tf_op jit(solution)/shard_map/ppermute | solution.py:565
  59.3 12.8 %collective-permute-start.8 = (bf16[64,1024]{1,0:T(8,128)(2,1)S(1)}, bf16[64,1024]{1,0:T(8,128)(2,1)S(1)}, u32[]{:S(2)}, u32[]{:S(2)}) collective-permute-start(bf16[64,1024]{1,0:T(8,128)(2,1)S(1)} %get-tuple-element.48), channel_id=1, source_target_pairs={{0,4},{2,6},{4,0},{6,2},{8,12},{10,14},{12,8},{14,10},{1,5},{3,7},... | collective-permute-start | bytes 393224 | tf_op jit(solution)/shard_map/ppermute | solution.py:565
  60.9 4.5 %collective-permute-start.11 = (f32[64,256]{1,0:T(8,128)S(1)}, f32[64,256]{1,0:T(8,128)S(1)}, u32[]{:S(2)}, u32[]{:S(2)}) collective-permute-start(f32[64,256]{1,0:T(8,128)S(1)} %add.32.pay0_ref), channel_id=1, source_target_pairs={{0,1},{1,0},{2,3},{3,2},{4,5},{5,4},{6,7},{7,6},{8,9},{9,8},{10,11... | collective-permute-start | bytes 196616 | tf_op jit(solution)/shard_map/ppermute | solution.py:568
  61.0 17.3 %collective-permute-start.9 = (bf16[64,1024]{1,0:T(8,128)(2,1)S(1)}, bf16[64,1024]{1,0:T(8,128)(2,1)S(1)}, u32[]{:S(2)}, u32[]{:S(2)}) collective-permute-start(bf16[64,1024]{1,0:T(8,128)(2,1)S(1)} %get-tuple-element.49), channel_id=1, source_target_pairs={{0,8},{2,10},{4,12},{6,14},{8,0},{10,2},{12,4},{14,6},{1,9},{3,11}... | collective-permute-start | bytes 393224 | tf_op jit(solution)/shard_map/ppermute | solution.py:565
  63.4 14.8 %collective-permute-start.10 = (bf16[64,1024]{1,0:T(8,128)(2,1)S(1)}, bf16[64,1024]{1,0:T(8,128)(2,1)S(1)}, u32[]{:S(2)}, u32[]{:S(2)}) collective-permute-start(bf16[64,1024]{1,0:T(8,128)(2,1)S(1)} %get-tuple-element.50), channel_id=1, source_target_pairs={{0,12},{2,14},{4,8},{6,10},{8,4},{10,6},{12,0},{14,2},{1,13},{3,15... | collective-permute-start | bytes 393224 | tf_op jit(solution)/shard_map/ppermute | solution.py:565
  63.9 8.1 %collective-permute-start.12 = (f32[64,256]{1,0:T(8,128)S(1)}, f32[64,256]{1,0:T(8,128)S(1)}, u32[]{:S(2)}, u32[]{:S(2)}) collective-permute-start(f32[64,256]{1,0:T(8,128)S(1)} %add.32.pay0_ref), channel_id=1, source_target_pairs={{0,16},{16,0},{1,17},{17,1},{2,18},{18,2},{3,19},{19,3},{4,20},{20... | collective-permute-start | bytes 196616 | tf_op jit(solution)/shard_map/ppermute | solution.py:701
  65.4 6.6 %collective-permute-start.13 = (f32[64,256]{1,0:T(8,128)S(1)}, f32[64,256]{1,0:T(8,128)S(1)}, u32[]{:S(2)}, u32[]{:S(2)}) collective-permute-start(f32[64,256]{1,0:T(8,128)S(1)} %add.32.pay0_ref), channel_id=1, source_target_pairs={{0,17},{1,16},{16,1},{17,0},{2,19},{3,18},{18,3},{19,2},{4,21},{5,... | collective-permute-start | bytes 196616 | tf_op jit(solution)/shard_map/ppermute | solution.py:702
  81.4 1.3 %collective-permute-start.14 = (f32[8,2048]{1,0:T(8,128)S(1)}, f32[8,2048]{1,0:T(8,128)S(1)}, u32[]{:S(2)}, u32[]{:S(2)}) collective-permute-start(f32[8,2048]{1,0:T(8,128)S(1)} %get-tuple-element.55), channel_id=1, source_target_pairs={{0,1},{1,0},{2,3},{3,2},{4,5},{5,4},{6,7},{7,6},{8,9},{9,8},{10,11... | collective-permute-start | bytes 196616 | tf_op jit(solution)/shard_map/ppermute | solution.py:568
  82.8 4.3 %collective-permute-start.15 = (f32[8,2048]{1,0:T(8,128)S(1)}, f32[8,2048]{1,0:T(8,128)S(1)}, u32[]{:S(2)}, u32[]{:S(2)}) collective-permute-start(f32[8,2048]{1,0:T(8,128)S(1)} %add.33), channel_id=1, source_target_pairs={{0,2},{2,0},{4,6},{6,4},{8,10},{10,8},{12,14},{14,12},{1,3},{3,1},... | collective-permute-start | bytes 196616 | tf_op jit(solution)/shard_map/ppermute | solution.py:565
  87.1 5.3 %collective-permute-start.16 = (f32[8,2048]{1,0:T(8,128)S(1)}, f32[8,2048]{1,0:T(8,128)S(1)}, u32[]{:S(2)}, u32[]{:S(2)}) collective-permute-start(f32[8,2048]{1,0:T(8,128)S(1)} %add.34), channel_id=1, source_target_pairs={{0,4},{2,6},{4,0},{6,2},{8,12},{10,14},{12,8},{14,10},{1,5},{3,7},... | collective-permute-start | bytes 196616 | tf_op jit(solution)/shard_map/ppermute | solution.py:565
  92.4 5.2 %collective-permute-start.17 = (f32[8,2048]{1,0:T(8,128)S(1)}, f32[8,2048]{1,0:T(8,128)S(1)}, u32[]{:S(2)}, u32[]{:S(2)}) collective-permute-start(f32[8,2048]{1,0:T(8,128)S(1)} %add.35), channel_id=1, source_target_pairs={{0,8},{2,10},{4,12},{6,14},{8,0},{10,2},{12,4},{14,6},{1,9},{3,11}... | collective-permute-start | bytes 196616 | tf_op jit(solution)/shard_map/ppermute | solution.py:565
  97.6 1.3 %collective-permute-start.18 = (f32[8,2048]{1,0:T(8,128)S(1)}, f32[8,2048]{1,0:T(8,128)S(1)}, u32[]{:S(2)}, u32[]{:S(2)}) collective-permute-start(f32[8,2048]{1,0:T(8,128)S(1)} %add.36.mine_ref), channel_id=1, source_target_pairs={{0,1},{1,0},{2,3},{3,2},{4,5},{5,4},{6,7},{7,6},{8,9},{9,8},{10,11... | collective-permute-start | bytes 196616 | tf_op jit(solution)/shard_map/ppermute | solution.py:568

commit v8 on v6

--- a/solution.py
+++ b/solution.py
@@ -20,6 +20,7 @@
 ANY = pl.BlockSpec(memory_space=pl.ANY)
 
 STRIDE = 168
+SHARED = 48
 
 
 def params(mebibytes):
@@ -179,8 +180,9 @@
 
 
 def head_kernel(
-    place_ref, tok_in_ref, gate_ref, up_ref, zone_out_ref, kind_out_ref, tok_ref, blocks_ref, sem
+    place_ref, tok_in_ref, gate_ref, up_ref, zone_out_ref, a_out_ref, b_out_ref, tok_ref, blocks_ref, sem
 ):
+    group = place_ref[1] // 2
     core = place_ref[3]
 
     @pl.when(core == 0)
@@ -195,19 +197,27 @@
     for zone in range(4):
         held = tok_ref.at[zone]
         lanes = pl.ds(2048 * zone, 2048)
-        loads.append(pltpu.make_async_copy(tok_in_ref.at[:, lanes], held, sem.at[2 + zone]))
-        stores.append(pltpu.make_async_copy(held, zone_out_ref.at[zone], sem.at[6 + zone]))
+        loads.append(pltpu.make_async_copy(tok_in_ref.at[:, lanes], held, sem.at[3 + zone]))
+        stores.append(pltpu.make_async_copy(held, zone_out_ref.at[zone], sem.at[7 + zone]))
     for load in loads:
         load.start()
     pltpu.make_async_copy(gate_ref, blocks_ref, sem.at[0]).wait()
-    kind_store = pltpu.make_async_copy(blocks_ref, kind_out_ref, sem.at[1])
-    kind_store.start()
-    for load, store in zip(loads, stores):
+    first = pl.multiple_of(SHARED * group, 16)
+    stores.append(
+        pltpu.make_async_copy(blocks_ref.at[pl.ds(first, SHARED)], a_out_ref, sem.at[1])
+    )
+    stores.append(
+        pltpu.make_async_copy(
+            blocks_ref.at[pl.ds(2 * SHARED, 160 - 2 * SHARED)], b_out_ref, sem.at[2]
+        )
+    )
+    stores[4].start()
+    stores[5].start()
+    for load, store in zip(loads, stores[:4]):
         load.wait()
         store.start()
     for store in stores:
         store.wait()
-    kind_store.wait()
 
 
 def own_kernel(
@@ -318,7 +328,9 @@
 def first_kernel(
     place_ref,
     inv_ref,
-    blocks_in_ref,
+    a_in_ref,
+    b_in_ref,
+    a_other_ref,
     weight_in_ref,
     tok_in_ref,
     keep_ref,
@@ -339,15 +351,23 @@
     zone = place_ref[0] // 2
     side = place_ref[2]
     core = place_ref[3]
+    group = place_ref[1] // 2
+    mine = pl.multiple_of(SHARED * group, 16)
+    other = pl.multiple_of(SHARED * (1 - group), 16)
     loads = [
-        pltpu.make_async_copy(blocks_in_ref, blocks_ref, in_sem.at[0]),
-        pltpu.make_async_copy(tok_in_ref, tok_ref, in_sem.at[1]),
-        pltpu.make_async_copy(weight_in_ref.at[pl.ds(4 * core, 4)], own_ref, in_sem.at[2]),
+        pltpu.make_async_copy(a_in_ref, blocks_ref.at[pl.ds(mine, SHARED)], in_sem.at[0]),
+        pltpu.make_async_copy(a_other_ref, blocks_ref.at[pl.ds(other, SHARED)], in_sem.at[1]),
+        pltpu.make_async_copy(
+            b_in_ref, blocks_ref.at[pl.ds(2 * SHARED, 160 - 2 * SHARED)], in_sem.at[2]
+        ),
+        pltpu.make_async_copy(tok_in_ref, tok_ref, in_sem.at[3]),
+        pltpu.make_async_copy(weight_in_ref.at[pl.ds(4 * core, 4)], own_ref, in_sem.at[4]),
     ]
     for load in loads:
         load.start()
     clear_empty_slot(tiles_ref)
-    loads[0].wait()
+    for load in loads[:3]:
+        load.wait()
     stage_blocks(blocks_ref, tiles_ref, 0)
 
     def put(pair, row, piece):
@@ -357,9 +377,9 @@
     assemble_columns(inv_ref, core, tiles_ref, put)
     near_store = pltpu.make_async_copy(near_ref, near_out_ref, near_sem)
     near_store.start()
-    loads[1].wait()
+    loads[3].wait()
     shuffle_tokens(side, tok_ref, tokens_ref)
-    loads[2].wait()
+    loads[4].wait()
     stores = []
     for chunk in range(4):
         total = dot(tokens_ref[0], own_ref[chunk]) + dot(tokens_ref[1], near_ref[chunk])
@@ -430,10 +450,6 @@
     pay1_ref,
     pay2_ref,
     pay3_ref,
-    across0_ref,
-    across1_ref,
-    across2_ref,
-    across3_ref,
     mine_ref,
     theirs_ref,
     lead_ref,
@@ -447,10 +463,8 @@
     quarter = place_ref[1]
     core = place_ref[3]
     unshuffle = unshuffle_matrix(256)
-    near_parts = (pay0_ref, pay1_ref, pay2_ref, pay3_ref)
-    across_parts = (across0_ref, across1_ref, across2_ref, across3_ref)
-    for flip in range(4):
-        pay_ref[flipped(quarter, flip)] = near_parts[flip][...] + across_parts[flip][...]
+    for flip, ref in enumerate((pay0_ref, pay1_ref, pay2_ref, pay3_ref)):
+        pay_ref[flipped(quarter, flip)] = ref[...]
     for chunk in range(4):
         cols = slice(256 * chunk, 256 * (chunk + 1))
         proj_ref[:, cols] = dot(pay_ref[chunk, 32:64, :].astype(BF), unshuffle).astype(BF)
@@ -539,23 +553,25 @@
             axis_index_groups=[[0, 2, 4, 6], [1, 3, 5, 7]],
         )
 
-    by_zone, kind = pl.pallas_call(
+    by_zone, kind_a, kind_b = pl.pallas_call(
         head_kernel,
         out_shape=(
             jax.ShapeDtypeStruct((4, 64, 2048), BF),
-            jax.ShapeDtypeStruct((160, 4096), BF),
+            jax.ShapeDtypeStruct((SHARED, 4096), BF),
+            jax.ShapeDtypeStruct((160 - 2 * SHARED, 4096), BF),
         ),
         in_specs=[SMEM, HBM, HBM, HBM],
-        out_specs=(HBM, HBM),
+        out_specs=(HBM,) * 3,
         scratch_shapes=[
             pltpu.VMEM((4, 64, 2048), BF),
             pltpu.VMEM((160, 4096), BF),
-            pltpu.SemaphoreType.DMA((10,)),
+            pltpu.SemaphoreType.DMA((11,)),
         ],
         compiler_params=params(60),
         name="head",
     )(place, tokens, gate_blocks, up_blocks)
-    near = owner_flip(kind, 1)
+    near_a = owner_flip(kind_a, 1)
+    near_b = owner_flip(kind_b, 1)
     gathered = zone_exchange(by_zone)
 
     slots = jnp.stack([gate_slot, up_slot, down_slot])
@@ -586,16 +602,12 @@
         name="own_blocks",
     )(place, inv, gate_blocks, up_blocks, down_blocks, sketch, probe_index, probe_value)
 
-    from_zones = [owner_flip(payload, bits) for bits in (4, 6, 2)]
-    payload = payload + from_zones[0] + from_zones[1] + from_zones[2]
-    pay_parts = [
-        payload,
-        core_flip(payload),
-        lax.ppermute(payload, "groups", [(0, 1), (1, 0)]),
-        lax.ppermute(payload, ("groups", "seq"), [(i, i ^ 3) for i in range(4)]),
-    ]
-    near, near_inv, gathered, pay_parts = lax.optimization_barrier(
-        (near, near_inv, gathered, pay_parts)
+    near_a, payload = lax.optimization_barrier((near_a, payload))
+    near_a_other = lax.ppermute(near_a, "groups", [(0, 1), (1, 0)])
+    for bits in (2, 4):
+        payload = payload + owner_flip(payload, bits)
+    near_inv, near_b, near_a_other, gathered, payload = lax.optimization_barrier(
+        (near_inv, near_b, near_a_other, gathered, payload)
     )
 
     first_keep, first_sent, near_weights = pl.pallas_call(
@@ -605,7 +617,7 @@
             jax.ShapeDtypeStruct((4, 64, 1024), BF),
             jax.ShapeDtypeStruct((4, 1024, 256), BF),
         ),
-        in_specs=[SMEM, SMEM, ANY, HBM, ANY],
+        in_specs=[SMEM, SMEM, ANY, ANY, ANY, HBM, ANY],
         out_specs=(VMEM, HBM, HBM),
         scratch_shapes=[
             pltpu.VMEM((160, 4096), BF),
@@ -616,13 +628,13 @@
             pltpu.VMEM((2, 256, 1024), BF),
             pltpu.VMEM((4, 64, 1024), BF),
             pltpu.VMEM((256, 256), F32),
-            pltpu.SemaphoreType.DMA((3,)),
+            pltpu.SemaphoreType.DMA((5,)),
             pltpu.SemaphoreType.DMA,
             pltpu.SemaphoreType.DMA((4,)),
         ],
         compiler_params=params(50),
         name="first_partial",
-    )(place, near_inv, near, weights, gathered)
+    )(place, near_inv, near_a, near_b, near_a_other, weights, gathered)
     first_back = zone_exchange(first_sent)
 
     second_keep, *second_sent = pl.pallas_call(
@@ -644,7 +656,15 @@
     )(place, core_flip(near_weights), weights, gathered)
     second_back = [owner_flip(second_sent[flip - 1], 2 * flip) for flip in (1, 2, 3)]
 
-    pay_parts = pay_parts + [owner_flip(part, 1) for part in pay_parts]
+    across = owner_flip(payload, 1)
+    second_keep, across = lax.optimization_barrier((second_keep, across))
+    payload = payload + across
+    pay_parts = [
+        payload,
+        core_flip(payload),
+        lax.ppermute(payload, "groups", [(0, 1), (1, 0)]),
+        lax.ppermute(payload, ("groups", "seq"), [(i, i ^ 3) for i in range(4)]),
+    ]
 
     first_back, weights = lax.optimization_barrier((first_back, weights))
     weights_at_hand = pl.pallas_call(
@@ -661,7 +681,7 @@
     mine, theirs = pl.pallas_call(
         middle_kernel,
         out_shape=(jax.ShapeDtypeStruct((8, 2048), F32),) * 2,
-        in_specs=[SMEM] + [VMEM] * 14,
+        in_specs=[SMEM] + [VMEM] * 10,
         out_specs=(VMEM,) * 2,
         scratch_shapes=[
             pltpu.VMEM((64, 1024), F32),

time: 106 us -> 97 us (0.915)
  waiting for transfers between devices: 37.1 us -> 26.3 us
  starting transfers between devices: 34.8 us -> 36.2 us
    ppermute x15 -> x12, waiting for transfers between devices: 31.3 us -> 20 us  [owner_flip(): return lax.ppermute(value, 'fsdp', [(i, i ^ bits) for i in range(8)])]
    ppermute x0 -> x1, starting transfers between devices: none -> 1.59 us  [pair_split(): near_a_other = lax.ppermute(near_a, 'groups', [(0, 1), (1, 0)])]
    ppermute x15 -> x12, starting transfers between devices: 22.6 us -> 22.8 us  [owner_flip(): return lax.ppermute(value, 'fsdp', [(i, i ^ bits) for i in range(8)])]
  transfers between devices with their start and end apart: 23 -> 21, of which waited for: 12 -> 9; matrix products, arithmetic and copies ran while one was open for 2% -> 2% of each run, Pallas kernels for 15% -> 17%
where the time goes in v8:
time: 97 us; the launch traced here: 96.6 us
  starting transfers between devices  36.2 us (37%)
  Pallas kernels  31.5 us (32%)
  waiting for transfers between devices  26.3 us (27%)
  other arithmetic  2.3 us (2%)
    ppermute x12, starting transfers between devices, owner_flip(): return lax.ppermute(value, 'fsdp', [(i, i ^ bits) for i in range(8)])  22.8 us
    ppermute x12, waiting for transfers between devices, owner_flip(): return lax.ppermute(value, 'fsdp', [(i, i ^ bits) for i in range(8)])  20 us
    all_to_all x2, starting transfers between devices, zone_exchange(): lax.all_to_all(value, 'fsdp', split_axis=0, concat_axis=0, tiled=True, ax...  9.94 us
    pallas_call x1, Pallas kernels, pair_split(): pl.pallas_call(own_kernel, out_shape=(jax.ShapeDtypeStruct((8, 1024, 256)...  9.59 us
    pallas_call x1, Pallas kernels, pair_split(): pl.pallas_call(first_kernel, out_shape=(jax.ShapeDtypeStruct((64, 1024),...  6.23 us
    pallas_call x1, Pallas kernels, pair_split(): pl.pallas_call(second_kernel, out_shape=(jax.ShapeDtypeStruct((64, 1024),...  4.25 us
    all_to_all x2, waiting for transfers between devices, zone_exchange(): lax.all_to_all(value, 'fsdp', split_axis=0, concat_axis=0, tiled=True, ax...  3.83 us
    pallas_call x1, Pallas kernels, pair_split(): pl.pallas_call(head_kernel, out_shape=(jax.ShapeDtypeStruct((4, 64, 2048)...  3.52 us
  transfers between devices with their start and end apart: 21, of which 9 were waited for; matrix products, arithmetic and copies ran while one was open for 2% of the time, Pallas kernels for 17%

profile of v8, /device:TPU:0, one launch (start us, length us, event | category | flops | bytes accessed | tf_op | source)
XLA Modules:
  0.0 96.6 jit_solution(2675641861156159801)
XLA Ops:
  0.6 3.5 %head.1 = (bf16[4,64,2048]{2,1,0:T(8,128)(2,1)}, bf16[48,4096]{1,0:T(8,128)(2,1)}, bf16[64,4096]{1,0:T(8,128)(2,1)}) custom-call(s32[4]{0:T(128)} %pad_add_fusion.1.place_ref, bf16[64,8192]{1,0:T(8,128)(2,1)} %tok_in_ref.1, bf16[160,4096]{1,0:T(8,128)(2,1)} %gate_ref.3, bf16[160,4096]{1,0:T(8,128)(2,1)} %up_ref.3), custom_call_target="tpu_custom_call" | custom-call | tf_op jit(solution)/shard_map/head/pallas_call | solution.py:556
  4.2 6.5 %all-to-all-start = ((bf16[4,64,2048]{2,1,0:T(8,128)(2,1)}), bf16[4,64,2048]{2,1,0:T(8,128)(2,1)S(1)}, u32[]{:S(2)}, u32[]{:S(2)}) async-start(bf16[4,64,2048]{2,1,0:T(8,128)(2,1)} %get-tuple-element.36), calls=%async_computation | async-start | bytes 2097152 | tf_op jit(solution)/shard_map/all_to_all | solution.py:547
  10.7 1.5 %collective-permute-start.2 = (bf16[48,4096]{1,0:T(8,128)(2,1)S(1)}, bf16[48,4096]{1,0:T(8,128)(2,1)S(1)}, u32[]{:S(2)}, u32[]{:S(2)}) collective-permute-start(bf16[48,4096]{1,0:T(8,128)(2,1)S(1)} %copy-done.6), channel_id=1, source_target_pairs={{0,2},{2,0},{4,6},{6,4},{8,10},{10,8},{12,14},{14,12},{1,3},{3,1},... | collective-permute-start | bytes 1179656 | tf_op jit(solution)/shard_map/ppermute | solution.py:541
  12.7 0.7 select_reduce_fusion.inv_ref
  13.5 9.6 %own_blocks.1 = (bf16[8,1024,256]{2,1,0:T(8,128)(2,1)}, f32[64,256]{1,0:T(8,128)}) custom-call(s32[4]{0:T(128)} %pad_add_fusion.1.place_ref, s32[3,256]{1,0:T(4,128)} %select_reduce_fusion.inv_ref, bf16[160,4096]{1,0:T(8,128)(2,1)} %gate_ref.3, bf16[160,4096]{1,0:T(8,128)(2,1)} %up_ref.3, bf16[160,4096]{1,0:T(8,128)(2,1)} %down_ref.1, ...), custom_call_target="tpu_custom_call" | custom-call | tf_op jit(solution)/shard_map/own_blocks/pallas_call | solution.py:583
  23.1 1.6 %collective-permute-start.3 = (bf16[48,4096]{1,0:T(8,128)(2,1)S(1)}, bf16[48,4096]{1,0:T(8,128)(2,1)S(1)}, u32[]{:S(2)}, u32[]{:S(2)}) collective-permute-start(bf16[48,4096]{1,0:T(8,128)(2,1)S(1)} %collective-permute-done.2.a_in_ref), channel_id=1, source_target_pairs={{0,16},{16,0},{1,17},{17,1},{2,18},{18,2},{3,19},{19,3},{4,20},{20... | collective-permute-start | bytes 1179656 | tf_op jit(solution)/shard_map/ppermute | solution.py:606
  24.7 2.0 %collective-permute-start.4 = (f32[64,256]{1,0:T(8,128)}, f32[64,256]{1,0:T(8,128)S(1)}, u32[]{:S(2)}, u32[]{:S(2)}) collective-permute-start(f32[64,256]{1,0:T(8,128)} %get-tuple-element.37), channel_id=1, source_target_pairs={{0,4},{2,6},{4,0},{6,2},{8,12},{10,14},{12,8},{14,10},{1,5},{3,7},... | collective-permute-start | bytes 196616 | tf_op jit(solution)/shard_map/ppermute | solution.py:541
  26.7 2.5 %collective-permute-done.4 = f32[64,256]{1,0:T(8,128)S(1)} collective-permute-done((f32[64,256]{1,0:T(8,128)}, f32[64,256]{1,0:T(8,128)S(1)}, u32[]{:S(2)}, u32[]{:S(2)}) %collective-permute-start.4) | collective-permute-done | bytes 65568 | tf_op jit(solution)/shard_map/ppermute | solution.py:541
  29.2 0.9 add.30
  30.1 4.5 %collective-permute-start.5 = (f32[64,256]{1,0:T(8,128)S(1)}, f32[64,256]{1,0:T(8,128)S(1)}, u32[]{:S(2)}, u32[]{:S(2)}) collective-permute-start(f32[64,256]{1,0:T(8,128)S(1)} %add.30), channel_id=1, source_target_pairs={{0,8},{2,10},{4,12},{6,14},{8,0},{10,2},{12,4},{14,6},{1,9},{3,11}... | collective-permute-start | bytes 196616 | tf_op jit(solution)/shard_map/ppermute | solution.py:541
  34.6 1.5 %collective-permute-start = (s32[3,256]{1,0:T(4,128)S(1)}, s32[3,256]{1,0:T(4,128)S(1)}, u32[]{:S(2)}, u32[]{:S(2)}) collective-permute-start(s32[3,256]{1,0:T(4,128)S(1)} %copy-done.1), channel_id=1, source_target_pairs={{0,2},{2,0},{4,6},{6,4},{8,10},{10,8},{12,14},{14,12},{1,3},{3,1},... | collective-permute-start | bytes 9224 | tf_op jit(solution)/shard_map/ppermute | solution.py:541
  36.1 3.1 %collective-permute-done.5 = f32[64,256]{1,0:T(8,128)S(1)} collective-permute-done((f32[64,256]{1,0:T(8,128)S(1)}, f32[64,256]{1,0:T(8,128)S(1)}, u32[]{:S(2)}, u32[]{:S(2)}) %collective-permute-start.5) | collective-permute-done | bytes 65568 | tf_op jit(solution)/shard_map/ppermute | solution.py:541
  39.3 6.2 %first_partial.1 = (f32[64,1024]{1,0:T(8,128)S(1)}, bf16[4,64,1024]{2,1,0:T(8,128)(2,1)}, bf16[4,1024,256]{2,1,0:T(8,128)(2,1)}) custom-call(s32[4]{0:T(128)S(1)} %copy-done, s32[3,256]{1,0:T(4,128)S(1)} %collective-permute-done.inv_ref, bf16[48,4096]{1,0:T(8,128)(2,1)S(1)} %collective-permute-done.2.a_in_ref, ...), custom_call_target="tpu_custom_call" | custom-call | tf_op jit(solution)/shard_map/first_partial/pallas_call | solution.py:613
  45.6 3.5 %all-to-all-start.1 = ((bf16[4,64,1024]{2,1,0:T(8,128)(2,1)}), bf16[4,64,1024]{2,1,0:T(8,128)(2,1)S(1)}, u32[]{:S(2)}, u32[]{:S(2)}) async-start(bf16[4,64,1024]{2,1,0:T(8,128)(2,1)} %get-tuple-element.44), calls=%async_computation.1 | async-start | bytes 1048576 | tf_op jit(solution)/shard_map/all_to_all | solution.py:547
  49.1 1.6 %collective-permute-start.7 = (f32[64,256]{1,0:T(8,128)S(1)}, f32[64,256]{1,0:T(8,128)S(1)}, u32[]{:S(2)}, u32[]{:S(2)}) collective-permute-start(f32[64,256]{1,0:T(8,128)S(1)} %add.31), channel_id=1, source_target_pairs={{0,2},{2,0},{4,6},{6,4},{8,10},{10,8},{12,14},{14,12},{1,3},{3,1},... | collective-permute-start | bytes 196616 | tf_op jit(solution)/shard_map/ppermute | solution.py:541
  50.6 4.2 %second_partial.1 = (f32[64,1024]{1,0:T(8,128)S(1)}, bf16[64,1024]{1,0:T(8,128)(2,1)S(1)}, bf16[64,1024]{1,0:T(8,128)(2,1)S(1)}, bf16[64,1024]{1,0:T(8,128)(2,1)S(1)}) custom-call(s32[4]{0:T(128)S(1)} %copy-done, bf16[4,1024,256]{2,1,0:T(8,128)(2,1)} %collective-permute-done.6.near_in_ref, bf16[8,1024,256]{2,1,0:T(8,128)(2,1)} %get-tuple-element.54.weight_in_ref, ...), custom_call_target="tpu_custom_call" | custom-call | tf_op jit(solution)/shard_map/second_partial/pallas_call | solution.py:640
  54.9 2.0 %collective-permute-start.8 = (bf16[64,1024]{1,0:T(8,128)(2,1)S(1)}, bf16[64,1024]{1,0:T(8,128)(2,1)S(1)}, u32[]{:S(2)}, u32[]{:S(2)}) collective-permute-start(bf16[64,1024]{1,0:T(8,128)(2,1)S(1)} %get-tuple-element.50), channel_id=1, source_target_pairs={{0,4},{2,6},{4,0},{6,2},{8,12},{10,14},{12,8},{14,10},{1,5},{3,7},... | collective-permute-start | bytes 393224 | tf_op jit(solution)/shard_map/ppermute | solution.py:541
  57.0 2.4 %collective-permute-start.9 = (bf16[64,1024]{1,0:T(8,128)(2,1)S(1)}, bf16[64,1024]{1,0:T(8,128)(2,1)S(1)}, u32[]{:S(2)}, u32[]{:S(2)}) collective-permute-start(bf16[64,1024]{1,0:T(8,128)(2,1)S(1)} %get-tuple-element.51), channel_id=1, source_target_pairs={{0,8},{2,10},{4,12},{6,14},{8,0},{10,2},{12,4},{14,6},{1,9},{3,11}... | collective-permute-start | bytes 393224 | tf_op jit(solution)/shard_map/ppermute | solution.py:541
  59.5 1.5 %collective-permute-start.12 = (f32[64,256]{1,0:T(8,128)S(1)}, f32[64,256]{1,0:T(8,128)S(1)}, u32[]{:S(2)}, u32[]{:S(2)}) collective-permute-start(f32[64,256]{1,0:T(8,128)S(1)} %add.32.pay0_ref), channel_id=1, source_target_pairs={{0,16},{16,0},{1,17},{17,1},{2,18},{18,2},{3,19},{19,3},{4,20},{20... | collective-permute-start | bytes 196616 | tf_op jit(solution)/shard_map/ppermute | solution.py:665
  61.0 3.8 %all-to-all-done.1.first_ref = bf16[4,64,1024]{2,1,0:T(8,128)(2,1)S(1)} async-done(((bf16[4,64,1024]{2,1,0:T(8,128)(2,1)}), bf16[4,64,1024]{2,1,0:T(8,128)(2,1)S(1)}, u32[]{:S(2)}, u32[]{:S(2)}) %all-to-all-start.1) | async-done | bytes 524320 | tf_op jit(solution)/shard_map/all_to_all | solution.py:547
  64.9 2.2 %fetch_weights.1.weight_ref = bf16[8,1024,256]{2,1,0:T(8,128)(2,1)S(1)} custom-call(bf16[8,1024,256]{2,1,0:T(8,128)(2,1)} %get-tuple-element.54.weight_in_ref), custom_call_target="tpu_custom_call" | custom-call | tf_op jit(solution)/shard_map/fetch_weights/pallas_call | solution.py:670
  67.1 6.2 %collective-permute-done.9.second2_ref = bf16[64,1024]{1,0:T(8,128)(2,1)S(1)} collective-permute-done((bf16[64,1024]{1,0:T(8,128)(2,1)S(1)}, bf16[64,1024]{1,0:T(8,128)(2,1)S(1)}, u32[]{:S(2)}, u32[]{:S(2)}) %collective-permute-start.9) | collective-permute-done | bytes 131104 | tf_op jit(solution)/shard_map/ppermute | solution.py:541
  73.3 3.2 %token_sums.1 = (f32[8,2048]{1,0:T(8,128)S(1)}, f32[8,2048]{1,0:T(8,128)S(1)}) custom-call(s32[4]{0:T(128)S(1)} %copy-done, f32[64,1024]{1,0:T(8,128)S(1)} %get-tuple-element.43.first_keep_ref, bf16[4,64,1024]{2,1,0:T(8,128)(2,1)S(1)} %all-to-all-done.1.first_ref, f32[64,1024]{1,0:T(8,128)S(1)} %get-tuple-element.49.second_keep_ref, ...), custom_call_target="tpu_custom_call" | custom-call | tf_op jit(solution)/shard_map/token_sums/pallas_call | solution.py:681
  76.5 1.2 %collective-permute-done.14 = f32[8,2048]{1,0:T(8,128)S(1)} collective-permute-done((f32[8,2048]{1,0:T(8,128)S(1)}, f32[8,2048]{1,0:T(8,128)S(1)}, u32[]{:S(2)}, u32[]{:S(2)}) %collective-permute-start.14) | collective-permute-done | bytes 65568 | tf_op jit(solution)/shard_map/ppermute | solution.py:544
  77.8 1.6 %collective-permute-start.15 = (f32[8,2048]{1,0:T(8,128)S(1)}, f32[8,2048]{1,0:T(8,128)S(1)}, u32[]{:S(2)}, u32[]{:S(2)}) collective-permute-start(f32[8,2048]{1,0:T(8,128)S(1)} %add.33), channel_id=1, source_target_pairs={{0,2},{2,0},{4,6},{6,4},{8,10},{10,8},{12,14},{14,12},{1,3},{3,1},... | collective-permute-start | bytes 196616 | tf_op jit(solution)/shard_map/ppermute | solution.py:541
  79.3 2.8 %collective-permute-done.15 = f32[8,2048]{1,0:T(8,128)S(1)} collective-permute-done((f32[8,2048]{1,0:T(8,128)S(1)}, f32[8,2048]{1,0:T(8,128)S(1)}, u32[]{:S(2)}, u32[]{:S(2)}) %collective-permute-start.15) | collective-permute-done | bytes 65568 | tf_op jit(solution)/shard_map/ppermute | solution.py:541
  82.1 3.0 %collective-permute-start.16 = (f32[8,2048]{1,0:T(8,128)S(1)}, f32[8,2048]{1,0:T(8,128)S(1)}, u32[]{:S(2)}, u32[]{:S(2)}) collective-permute-start(f32[8,2048]{1,0:T(8,128)S(1)} %add.34), channel_id=1, source_target_pairs={{0,4},{2,6},{4,0},{6,2},{8,12},{10,14},{12,8},{14,10},{1,5},{3,7},... | collective-permute-start | bytes 196616 | tf_op jit(solution)/shard_map/ppermute | solution.py:541
  85.2 2.2 %collective-permute-done.16 = f32[8,2048]{1,0:T(8,128)S(1)} collective-permute-done((f32[8,2048]{1,0:T(8,128)S(1)}, f32[8,2048]{1,0:T(8,128)S(1)}, u32[]{:S(2)}, u32[]{:S(2)}) %collective-permute-start.16) | collective-permute-done | bytes 65568 | tf_op jit(solution)/shard_map/ppermute | solution.py:541
  87.4 2.1 %collective-permute-start.17 = (f32[8,2048]{1,0:T(8,128)S(1)}, f32[8,2048]{1,0:T(8,128)S(1)}, u32[]{:S(2)}, u32[]{:S(2)}) collective-permute-start(f32[8,2048]{1,0:T(8,128)S(1)} %add.35), channel_id=1, source_target_pairs={{0,8},{2,10},{4,12},{6,14},{8,0},{10,2},{12,4},{14,6},{1,9},{3,11}... | collective-permute-start | bytes 196616 | tf_op jit(solution)/shard_map/ppermute | solution.py:541
  89.5 3.1 %collective-permute-done.17 = f32[8,2048]{1,0:T(8,128)S(1)} collective-permute-done((f32[8,2048]{1,0:T(8,128)S(1)}, f32[8,2048]{1,0:T(8,128)S(1)}, u32[]{:S(2)}, u32[]{:S(2)}) %collective-permute-start.17) | collective-permute-done | bytes 65568 | tf_op jit(solution)/shard_map/ppermute | solution.py:541
  92.7 1.2 %collective-permute-done.18.theirs_ref = f32[8,2048]{1,0:T(8,128)S(1)} collective-permute-done((f32[8,2048]{1,0:T(8,128)S(1)}, f32[8,2048]{1,0:T(8,128)S(1)}, u32[]{:S(2)}, u32[]{:S(2)}) %collective-permute-start.18) | collective-permute-done | bytes 65568 | tf_op jit(solution)/shard_map/ppermute | solution.py:544
  94.0 2.6 %products.1 = f32[16,1024]{1,0:T(8,128)} custom-call(s32[4]{0:T(128)S(1)} %copy-done, f32[8,2048]{1,0:T(8,128)S(1)} %add.36.mine_ref, f32[8,2048]{1,0:T(8,128)S(1)} %collective-permute-done.18.theirs_ref, bf16[8,1024,256]{2,1,0:T(8,128)(2,1)S(1)} %fetch_weights.1.weight_ref), custom_call_target="tpu_custom_call" | custom-call | tf_op jit(solution)/shard_map/products/pallas_call | solution.py:702
  (41 shorter events, 1.7 us)
Async XLA Ops:
  0.6 12.1 %copy-start.2 = (s32[160]{0:T(256)S(1)}, s32[160]{0:T(256)}, u32[]{:S(2)}) copy-start(s32[160]{0:T(256)} %param.16) | copy-start | bytes 1924
  0.6 12.1 %copy-start.3 = (s32[160]{0:T(256)S(1)}, s32[160]{0:T(256)}, u32[]{:S(2)}) copy-start(s32[160]{0:T(256)} %param.14) | copy-start | bytes 1924
  0.6 12.1 %copy-start.4 = (s32[160]{0:T(256)S(1)}, s32[160]{0:T(256)}, u32[]{:S(2)}) copy-start(s32[160]{0:T(256)} %param.12) | copy-start | bytes 1924
  4.2 6.5 %copy-start.6 = (bf16[48,4096]{1,0:T(8,128)(2,1)S(1)}, bf16[48,4096]{1,0:T(8,128)(2,1)}, u32[]{:S(2)}) copy-start(bf16[48,4096]{1,0:T(8,128)(2,1)} %get-tuple-element.33) | copy-start | bytes 1179652
  4.2 8.0 %copy-start.5 = (bf16[64,4096]{1,0:T(8,128)(2,1)S(1)}, bf16[64,4096]{1,0:T(8,128)(2,1)}, u32[]{:S(2)}) copy-start(bf16[64,4096]{1,0:T(8,128)(2,1)} %get-tuple-element.32) | copy-start | bytes 1572868
  4.2 35.0 %all-to-all-start = ((bf16[4,64,2048]{2,1,0:T(8,128)(2,1)}), bf16[4,64,2048]{2,1,0:T(8,128)(2,1)S(1)}, u32[]{:S(2)}, u32[]{:S(2)}) async-start(bf16[4,64,2048]{2,1,0:T(8,128)(2,1)} %get-tuple-element.36), calls=%async_computation | async-start | bytes 2097152 | tf_op jit(solution)/shard_map/all_to_all | solution.py:547
  10.7 12.4 %collective-permute-start.2 = (bf16[48,4096]{1,0:T(8,128)(2,1)S(1)}, bf16[48,4096]{1,0:T(8,128)(2,1)S(1)}, u32[]{:S(2)}, u32[]{:S(2)}) collective-permute-start(bf16[48,4096]{1,0:T(8,128)(2,1)S(1)} %copy-done.6), channel_id=1, source_target_pairs={{0,2},{2,0},{4,6},{6,4},{8,10},{10,8},{12,14},{14,12},{1,3},{3,1},... | collective-permute-start | bytes 1179656 | tf_op jit(solution)/shard_map/ppermute | solution.py:541
  12.2 27.1 %collective-permute-start.1 = (bf16[64,4096]{1,0:T(8,128)(2,1)S(1)}, bf16[64,4096]{1,0:T(8,128)(2,1)S(1)}, u32[]{:S(2)}, u32[]{:S(2)}) collective-permute-start(bf16[64,4096]{1,0:T(8,128)(2,1)S(1)} %copy-done.5), channel_id=1, source_target_pairs={{0,2},{2,0},{4,6},{6,4},{8,10},{10,8},{12,14},{14,12},{1,3},{3,1},... | collective-permute-start | bytes 1572872 | tf_op jit(solution)/shard_map/ppermute | solution.py:541
  13.5 21.1 %copy-start.1 = (s32[3,256]{1,0:T(4,128)S(1)}, s32[3,256]{1,0:T(4,128)}, u32[]{:S(2)}) copy-start(s32[3,256]{1,0:T(4,128)} %select_reduce_fusion.inv_ref) | copy-start | bytes 9220
  13.5 25.8 %copy-start = (s32[4]{0:T(128)S(1)}, s32[4]{0:T(128)}, u32[]{:S(2)}) copy-start(s32[4]{0:T(128)} %pad_add_fusion.1.place_ref) | copy-start | bytes 52
  23.1 16.2 %collective-permute-start.3 = (bf16[48,4096]{1,0:T(8,128)(2,1)S(1)}, bf16[48,4096]{1,0:T(8,128)(2,1)S(1)}, u32[]{:S(2)}, u32[]{:S(2)}) collective-permute-start(bf16[48,4096]{1,0:T(8,128)(2,1)S(1)} %collective-permute-done.2.a_in_ref), channel_id=1, source_target_pairs={{0,16},{16,0},{1,17},{17,1},{2,18},{18,2},{3,19},{19,3},{4,20},{20... | collective-permute-start | bytes 1179656 | tf_op jit(solution)/shard_map/ppermute | solution.py:606
  24.7 4.6 %collective-permute-start.4 = (f32[64,256]{1,0:T(8,128)}, f32[64,256]{1,0:T(8,128)S(1)}, u32[]{:S(2)}, u32[]{:S(2)}) collective-permute-start(f32[64,256]{1,0:T(8,128)} %get-tuple-element.37), channel_id=1, source_target_pairs={{0,4},{2,6},{4,0},{6,2},{8,12},{10,14},{12,8},{14,10},{1,5},{3,7},... | collective-permute-start | bytes 196616 | tf_op jit(solution)/shard_map/ppermute | solution.py:541
  30.1 9.1 %collective-permute-start.5 = (f32[64,256]{1,0:T(8,128)S(1)}, f32[64,256]{1,0:T(8,128)S(1)}, u32[]{:S(2)}, u32[]{:S(2)}) collective-permute-start(f32[64,256]{1,0:T(8,128)S(1)} %add.30), channel_id=1, source_target_pairs={{0,8},{2,10},{4,12},{6,14},{8,0},{10,2},{12,4},{14,6},{1,9},{3,11}... | collective-permute-start | bytes 196616 | tf_op jit(solution)/shard_map/ppermute | solution.py:541
  34.6 4.6 %collective-permute-start = (s32[3,256]{1,0:T(4,128)S(1)}, s32[3,256]{1,0:T(4,128)S(1)}, u32[]{:S(2)}, u32[]{:S(2)}) collective-permute-start(s32[3,256]{1,0:T(4,128)S(1)} %copy-done.1), channel_id=1, source_target_pairs={{0,2},{2,0},{4,6},{6,4},{8,10},{10,8},{12,14},{14,12},{1,3},{3,1},... | collective-permute-start | bytes 9224 | tf_op jit(solution)/shard_map/ppermute | solution.py:541
  45.5 5.1 %collective-permute-start.6 = (bf16[4,1024,256]{2,1,0:T(8,128)(2,1)}, bf16[4,1024,256]{2,1,0:T(8,128)(2,1)}, u32[]{:S(2)}, u32[]{:S(2)}) collective-permute-start(bf16[4,1024,256]{2,1,0:T(8,128)(2,1)} %get-tuple-element.46), channel_id=1, source_target_pairs={{0,1},{1,0},{2,3},{3,2},{4,5},{5,4},{6,7},{7,6},{8,9},{9,8},{10,11... | collective-permute-start | bytes 6291464 | tf_op jit(solution)/shard_map/ppermute | solution.py:544
  45.6 19.3 %all-to-all-start.1 = ((bf16[4,64,1024]{2,1,0:T(8,128)(2,1)}), bf16[4,64,1024]{2,1,0:T(8,128)(2,1)S(1)}, u32[]{:S(2)}, u32[]{:S(2)}) async-start(bf16[4,64,1024]{2,1,0:T(8,128)(2,1)} %get-tuple-element.44), calls=%async_computation.1 | async-start | bytes 1048576 | tf_op jit(solution)/shard_map/all_to_all | solution.py:547
  49.1 5.8 %collective-permute-start.7 = (f32[64,256]{1,0:T(8,128)S(1)}, f32[64,256]{1,0:T(8,128)S(1)}, u32[]{:S(2)}, u32[]{:S(2)}) collective-permute-start(f32[64,256]{1,0:T(8,128)S(1)} %add.31), channel_id=1, source_target_pairs={{0,2},{2,0},{4,6},{6,4},{8,10},{10,8},{12,14},{14,12},{1,3},{3,1},... | collective-permute-start | bytes 196616 | tf_op jit(solution)/shard_map/ppermute | solution.py:541
  54.9 12.2 %collective-permute-start.8 = (bf16[64,1024]{1,0:T(8,128)(2,1)S(1)}, bf16[64,1024]{1,0:T(8,128)(2,1)S(1)}, u32[]{:S(2)}, u32[]{:S(2)}) collective-permute-start(bf16[64,1024]{1,0:T(8,128)(2,1)S(1)} %get-tuple-element.50), channel_id=1, source_target_pairs={{0,4},{2,6},{4,0},{6,2},{8,12},{10,14},{12,8},{14,10},{1,5},{3,7},... | collective-permute-start | bytes 393224 | tf_op jit(solution)/shard_map/ppermute | solution.py:541
  56.9 4.1 %collective-permute-start.11 = (f32[64,256]{1,0:T(8,128)S(1)}, f32[64,256]{1,0:T(8,128)S(1)}, u32[]{:S(2)}, u32[]{:S(2)}) collective-permute-start(f32[64,256]{1,0:T(8,128)S(1)} %add.32.pay0_ref), channel_id=1, source_target_pairs={{0,1},{1,0},{2,3},{3,2},{4,5},{5,4},{6,7},{7,6},{8,9},{9,8},{10,11... | collective-permute-start | bytes 196616 | tf_op jit(solution)/shard_map/ppermute | solution.py:544
  57.0 16.3 %collective-permute-start.9 = (bf16[64,1024]{1,0:T(8,128)(2,1)S(1)}, bf16[64,1024]{1,0:T(8,128)(2,1)S(1)}, u32[]{:S(2)}, u32[]{:S(2)}) collective-permute-start(bf16[64,1024]{1,0:T(8,128)(2,1)S(1)} %get-tuple-element.51), channel_id=1, source_target_pairs={{0,8},{2,10},{4,12},{6,14},{8,0},{10,2},{12,4},{14,6},{1,9},{3,11}... | collective-permute-start | bytes 393224 | tf_op jit(solution)/shard_map/ppermute | solution.py:541
  59.4 13.9 %collective-permute-start.10 = (bf16[64,1024]{1,0:T(8,128)(2,1)S(1)}, bf16[64,1024]{1,0:T(8,128)(2,1)S(1)}, u32[]{:S(2)}, u32[]{:S(2)}) collective-permute-start(bf16[64,1024]{1,0:T(8,128)(2,1)S(1)} %get-tuple-element.52), channel_id=1, source_target_pairs={{0,12},{2,14},{4,8},{6,10},{8,4},{10,6},{12,0},{14,2},{1,13},{3,15... | collective-permute-start | bytes 393224 | tf_op jit(solution)/shard_map/ppermute | solution.py:541
  59.5 7.6 %collective-permute-start.12 = (f32[64,256]{1,0:T(8,128)S(1)}, f32[64,256]{1,0:T(8,128)S(1)}, u32[]{:S(2)}, u32[]{:S(2)}) collective-permute-start(f32[64,256]{1,0:T(8,128)S(1)} %add.32.pay0_ref), channel_id=1, source_target_pairs={{0,16},{16,0},{1,17},{17,1},{2,18},{18,2},{3,19},{19,3},{4,20},{20... | collective-permute-start | bytes 196616 | tf_op jit(solution)/shard_map/ppermute | solution.py:665
  61.0 6.0 %collective-permute-start.13 = (f32[64,256]{1,0:T(8,128)S(1)}, f32[64,256]{1,0:T(8,128)S(1)}, u32[]{:S(2)}, u32[]{:S(2)}) collective-permute-start(f32[64,256]{1,0:T(8,128)S(1)} %add.32.pay0_ref), channel_id=1, source_target_pairs={{0,17},{1,16},{16,1},{17,0},{2,19},{3,18},{18,3},{19,2},{4,21},{5,... | collective-permute-start | bytes 196616 | tf_op jit(solution)/shard_map/ppermute | solution.py:666
  76.5 1.3 %collective-permute-start.14 = (f32[8,2048]{1,0:T(8,128)S(1)}, f32[8,2048]{1,0:T(8,128)S(1)}, u32[]{:S(2)}, u32[]{:S(2)}) collective-permute-start(f32[8,2048]{1,0:T(8,128)S(1)} %get-tuple-element.57), channel_id=1, source_target_pairs={{0,1},{1,0},{2,3},{3,2},{4,5},{5,4},{6,7},{7,6},{8,9},{9,8},{10,11... | collective-permute-start | bytes 196616 | tf_op jit(solution)/shard_map/ppermute | solution.py:544
  77.8 4.3 %collective-permute-start.15 = (f32[8,2048]{1,0:T(8,128)S(1)}, f32[8,2048]{1,0:T(8,128)S(1)}, u32[]{:S(2)}, u32[]{:S(2)}) collective-permute-start(f32[8,2048]{1,0:T(8,128)S(1)} %add.33), channel_id=1, source_target_pairs={{0,2},{2,0},{4,6},{6,4},{8,10},{10,8},{12,14},{14,12},{1,3},{3,1},... | collective-permute-start | bytes 196616 | tf_op jit(solution)/shard_map/ppermute | solution.py:541
  82.1 5.3 %collective-permute-start.16 = (f32[8,2048]{1,0:T(8,128)S(1)}, f32[8,2048]{1,0:T(8,128)S(1)}, u32[]{:S(2)}, u32[]{:S(2)}) collective-permute-start(f32[8,2048]{1,0:T(8,128)S(1)} %add.34), channel_id=1, source_target_pairs={{0,4},{2,6},{4,0},{6,2},{8,12},{10,14},{12,8},{14,10},{1,5},{3,7},... | collective-permute-start | bytes 196616 | tf_op jit(solution)/shard_map/ppermute | solution.py:541
  87.4 5.2 %collective-permute-start.17 = (f32[8,2048]{1,0:T(8,128)S(1)}, f32[8,2048]{1,0:T(8,128)S(1)}, u32[]{:S(2)}, u32[]{:S(2)}) collective-permute-start(f32[8,2048]{1,0:T(8,128)S(1)} %add.35), channel_id=1, source_target_pairs={{0,8},{2,10},{4,12},{6,14},{8,0},{10,2},{12,4},{14,6},{1,9},{3,11}... | collective-permute-start | bytes 196616 | tf_op jit(solution)/shard_map/ppermute | solution.py:541
  92.7 1.3 %collective-permute-start.18 = (f32[8,2048]{1,0:T(8,128)S(1)}, f32[8,2048]{1,0:T(8,128)S(1)}, u32[]{:S(2)}, u32[]{:S(2)}) collective-permute-start(f32[8,2048]{1,0:T(8,128)S(1)} %add.36.mine_ref), channel_id=1, source_target_pairs={{0,1},{1,0},{2,3},{3,2},{4,5},{5,4},{6,7},{7,6},{8,9},{9,8},{10,11... | collective-permute-start | bytes 196616 | tf_op jit(solution)/shard_map/ppermute | solution.py:544

commit v9 on v8

--- a/solution.py
+++ b/solution.py
@@ -141,7 +141,7 @@
 
 
 def stage_blocks(blocks_ref, tiles_ref, first_slot):
-    @pl.loop(0, blocks_ref.shape[0] // 16)
+    @pl.loop(0, blocks_ref.shape[0] // 16, unroll=2)
     def _(step):
         row = pl.multiple_of(step * 16, 16)
         target = pl.multiple_of(first_slot + row, 16)
@@ -166,8 +166,8 @@
     return even.astype(BF), odd.astype(BF)
 
 
-def assemble_columns(inv_ref, inv_row, tiles_ref, put):
-    @pl.loop(0, 16)
+def assemble_columns(inv_ref, inv_row, tiles_ref, put, first_row=0, row_count=16):
+    @pl.loop(first_row, first_row + row_count, unroll=4)
     def _(block_row):
         for pair in range(8):
             cell = block_row * 16 + 2 * pair
@@ -292,10 +292,8 @@
             high_iota == high_part[probe : probe + 1, :], values[probe : probe + 1, :], 0.0
         )
         one_hot = jnp.where(low_iota == low_part[probe : probe + 1, :], 1.0, 0.0).astype(BF)
-        total = None
-        for part in split3(picked):
-            term = contract_last(part, one_hot)
-            total = term if total is None else total + term
+        terms = contract_last(jnp.concatenate(split3(picked), axis=0), one_hot)
+        total = terms[:8] + terms[8:16] + terms[16:]
         omega_ref[8 * probe : 8 * (probe + 1), :] = total
     for high in range(8):
         piece = omega_ref[pl.ds(high, 16, stride=8), :]
@@ -325,32 +323,19 @@
         )
 
 
-def first_kernel(
+def near_kernel(
     place_ref,
     inv_ref,
     a_in_ref,
     b_in_ref,
     a_other_ref,
-    weight_in_ref,
-    tok_in_ref,
-    keep_ref,
-    sent_out_ref,
     near_out_ref,
     blocks_ref,
     tiles_ref,
     near_ref,
-    own_ref,
-    tok_ref,
-    tokens_ref,
-    sent_ref,
-    total_ref,
     in_sem,
-    near_sem,
-    sent_sem,
+    out_sem,
 ):
-    zone = place_ref[0] // 2
-    side = place_ref[2]
-    core = place_ref[3]
     group = place_ref[1] // 2
     mine = pl.multiple_of(SHARED * group, 16)
     other = pl.multiple_of(SHARED * (1 - group), 16)
@@ -360,13 +345,11 @@
         pltpu.make_async_copy(
             b_in_ref, blocks_ref.at[pl.ds(2 * SHARED, 160 - 2 * SHARED)], in_sem.at[2]
         ),
-        pltpu.make_async_copy(tok_in_ref, tok_ref, in_sem.at[3]),
-        pltpu.make_async_copy(weight_in_ref.at[pl.ds(4 * core, 4)], own_ref, in_sem.at[4]),
     ]
     for load in loads:
         load.start()
     clear_empty_slot(tiles_ref)
-    for load in loads[:3]:
+    for load in loads:
         load.wait()
     stage_blocks(blocks_ref, tiles_ref, 0)
 
@@ -374,52 +357,31 @@
         lane = (pair % 2) * 128
         near_ref[pair // 2, pl.ds(row, 32), lane : lane + 128] = piece
 
-    assemble_columns(inv_ref, core, tiles_ref, put)
-    near_store = pltpu.make_async_copy(near_ref, near_out_ref, near_sem)
-    near_store.start()
-    loads[3].wait()
-    shuffle_tokens(side, tok_ref, tokens_ref)
-    loads[4].wait()
     stores = []
-    for chunk in range(4):
-        total = dot(tokens_ref[0], own_ref[chunk]) + dot(tokens_ref[1], near_ref[chunk])
-        cols = slice(256 * chunk, 256 * (chunk + 1))
-        total_ref[...] = total
-        keep_ref[:, cols] = total_ref[pl.ds(pl.multiple_of(64 * zone, 64), 64), :]
-        sent_ref[:, :, cols] = total.astype(BF).reshape(4, 64, 256)
-        lanes = pl.ds(256 * chunk, 256)
+    for part in range(2):
+        assemble_columns(inv_ref, place_ref[3], tiles_ref, put, 8 * part, 8)
+        rows = pl.ds(512 * part, 512)
         store = pltpu.make_async_copy(
-            sent_ref.at[:, :, lanes], sent_out_ref.at[:, :, lanes], sent_sem.at[chunk]
+            near_ref.at[:, rows], near_out_ref.at[:, rows], out_sem.at[part]
         )
         store.start()
         stores.append(store)
     for store in stores:
         store.wait()
-    near_store.wait()
-
-
-def second_kernel(
-    place_ref,
-    near_in_ref,
-    weight_in_ref,
-    tok_in_ref,
-    keep_ref,
-    out1_ref,
-    out2_ref,
-    out3_ref,
-    near_ref,
-    own_ref,
-    tok_ref,
-    tokens_ref,
-    total_ref,
-    in_sem,
+
+
+def partial_kernel(
+    first, place_ref, near_in_ref, weight_in_ref, tok_in_ref, keep_ref, *rest
 ):
+    outs, scratch = (rest[:1], rest[1:]) if first else (rest[:3], rest[3:])
+    near_ref, own_ref, tok_ref, tokens_ref, total_ref, in_sem = scratch[:6]
     zone = place_ref[0] // 2
     side = place_ref[2]
     core = place_ref[3]
+    kind = core if first else 1 - core
     loads = [
         pltpu.make_async_copy(tok_in_ref, tok_ref, in_sem.at[0]),
-        pltpu.make_async_copy(weight_in_ref.at[pl.ds(4 - 4 * core, 4)], own_ref, in_sem.at[1]),
+        pltpu.make_async_copy(weight_in_ref.at[pl.ds(4 * kind, 4)], own_ref, in_sem.at[1]),
         pltpu.make_async_copy(near_in_ref, near_ref, in_sem.at[2]),
     ]
     for load in loads:
@@ -428,14 +390,27 @@
     shuffle_tokens(side, tok_ref, tokens_ref)
     loads[1].wait()
     loads[2].wait()
+    stores = []
     for chunk in range(4):
         total = dot(tokens_ref[0], own_ref[chunk]) + dot(tokens_ref[1], near_ref[chunk])
         cols = slice(256 * chunk, 256 * (chunk + 1))
         total_ref[...] = total
         keep_ref[:, cols] = total_ref[pl.ds(pl.multiple_of(64 * zone, 64), 64), :]
-        for flip, ref in enumerate((out1_ref, out2_ref, out3_ref), 1):
-            row = pl.multiple_of(64 * flipped(zone, flip), 64)
-            ref[:, cols] = total_ref[pl.ds(row, 64), :].astype(BF)
+        if first:
+            sent_ref, sent_sem = scratch[6:]
+            sent_ref[:, :, cols] = total.astype(BF).reshape(4, 64, 256)
+            lanes = pl.ds(256 * chunk, 256)
+            store = pltpu.make_async_copy(
+                sent_ref.at[:, :, lanes], outs[0].at[:, :, lanes], sent_sem.at[chunk]
+            )
+            store.start()
+            stores.append(store)
+        else:
+            for flip, ref in enumerate(outs, 1):
+                row = pl.multiple_of(64 * flipped(zone, flip), 64)
+                ref[:, cols] = total_ref[pl.ds(row, 64), :].astype(BF)
+    for store in stores:
+        store.wait()
 
 
 def middle_kernel(
@@ -604,41 +579,56 @@
 
     near_a, payload = lax.optimization_barrier((near_a, payload))
     near_a_other = lax.ppermute(near_a, "groups", [(0, 1), (1, 0)])
-    for bits in (2, 4):
-        payload = payload + owner_flip(payload, bits)
+    payload = payload + owner_flip(payload, 2)
+    from_far = owner_flip(payload, 4)
     near_inv, near_b, near_a_other, gathered, payload = lax.optimization_barrier(
         (near_inv, near_b, near_a_other, gathered, payload)
     )
 
-    first_keep, first_sent, near_weights = pl.pallas_call(
-        first_kernel,
-        out_shape=(
-            jax.ShapeDtypeStruct((64, 1024), F32),
-            jax.ShapeDtypeStruct((4, 64, 1024), BF),
-            jax.ShapeDtypeStruct((4, 1024, 256), BF),
-        ),
-        in_specs=[SMEM, SMEM, ANY, ANY, ANY, HBM, ANY],
-        out_specs=(VMEM, HBM, HBM),
+    near_weights = pl.pallas_call(
+        near_kernel,
+        out_shape=jax.ShapeDtypeStruct((4, 1024, 256), BF),
+        in_specs=[SMEM, SMEM, ANY, ANY, ANY],
+        out_specs=HBM,
         scratch_shapes=[
             pltpu.VMEM((160, 4096), BF),
             pltpu.VMEM((32 * STRIDE, 128), F32),
             pltpu.VMEM((4, 1024, 256), BF),
+            pltpu.SemaphoreType.DMA((3,)),
+            pltpu.SemaphoreType.DMA((2,)),
+        ],
+        compiler_params=params(59.5),
+        name="near_blocks",
+    )(place, near_inv, near_a, near_b, near_a_other)
+
+    near_weights, from_far = lax.optimization_barrier((near_weights, from_far))
+    payload = payload + from_far
+
+    first_keep, first_sent = pl.pallas_call(
+        functools.partial(partial_kernel, True),
+        out_shape=(
+            jax.ShapeDtypeStruct((64, 1024), F32),
+            jax.ShapeDtypeStruct((4, 64, 1024), BF),
+        ),
+        in_specs=[SMEM, ANY, HBM, ANY],
+        out_specs=(VMEM, HBM),
+        scratch_shapes=[
+            pltpu.VMEM((4, 1024, 256), BF),
             pltpu.VMEM((4, 1024, 256), BF),
             pltpu.VMEM((4, 64, 2048), BF),
             pltpu.VMEM((2, 256, 1024), BF),
+            pltpu.VMEM((256, 256), F32),
+            pltpu.SemaphoreType.DMA((3,)),
             pltpu.VMEM((4, 64, 1024), BF),
-            pltpu.VMEM((256, 256), F32),
-            pltpu.SemaphoreType.DMA((5,)),
-            pltpu.SemaphoreType.DMA,
             pltpu.SemaphoreType.DMA((4,)),
         ],
-        compiler_params=params(50),
+        compiler_params=params(59.5),
         name="first_partial",
-    )(place, near_inv, near_a, near_b, near_a_other, weights, gathered)
+    )(place, near_weights, weights, gathered)
     first_back = zone_exchange(first_sent)
 
     second_keep, *second_sent = pl.pallas_call(
-        second_kernel,
+        functools.partial(partial_kernel, False),
         out_shape=(jax.ShapeDtypeStruct((64, 1024), F32),)
         + (jax.ShapeDtypeStruct((64, 1024), BF),) * 3,
         in_specs=[SMEM, ANY, HBM, ANY],
@@ -696,8 +686,9 @@
     )(place, first_keep, first_back, second_keep, *second_back, *pay_parts)
 
     sums = mine + core_flip(theirs)
-    for bits in (1, 2, 4):
-        sums = sums + owner_flip(sums, bits)
+    x_part, z_part, xz_part = [owner_flip(sums, bits) for bits in (1, 2, 3)]
+    sums = (sums + x_part) + (z_part + xz_part)
+    sums = sums + owner_flip(sums, 4)
 
     return pl.pallas_call(
         product_kernel,

time: 97 us -> 101 us (1.041)
  Pallas kernels: 31.5 us -> 33.5 us
  local copies, waits for them, and re-layouts: 0.03 us -> 2.02 us
    pallas_call x2 -> x3, Pallas kernels: 10.5 us -> 14.5 us  [the longest x1 6.1 us: pair_split(): pl.pallas_call(functools.partial(partial_kernel, True), out_shape=(jax.Sh...]
    pallas_call x1, Pallas kernels: 9.59 us -> 7.56 us  [pair_split(): pl.pallas_call(own_kernel, out_shape=(jax.ShapeDtypeStruct((8, 1024, 256)...]
    unnamed x14 -> x28, local copies, waits for them, and re-layouts: 0.03 us -> 2.02 us
    ppermute x1, starting transfers between devices: 0.01 us -> 1.46 us  [pair_split(): lax.ppermute(payload, ('groups', 'seq'), [(i, i ^ 3) for i in range(4)])]
    ppermute x1, starting transfers between devices: 1.52 us -> 0.51 us  [pair_split(): lax.ppermute(payload, 'groups', [(0, 1), (1, 0)])]
    ppermute x12 -> x13, waiting for transfers between devices: 20 us -> 19.9 us  [owner_flip(): return lax.ppermute(value, 'fsdp', [(i, i ^ bits) for i in range(8)])]
    ppermute x12 -> x13, starting transfers between devices: 22.8 us -> 22.8 us  [owner_flip(): return lax.ppermute(value, 'fsdp', [(i, i ^ bits) for i in range(8)])]
  transfers between devices with their start and end apart: 21 -> 22, of which waited for: 9 -> 11; matrix products, arithmetic and copies ran while one was open for 2% -> 2% of each run, Pallas kernels for 17% -> 24%
where the time goes in v9:
time: 101 us; the launch traced here: 100 us
  starting transfers between devices  36.4 us (36%)
  Pallas kernels  33.5 us (33%)
  waiting for transfers between devices  25.7 us (25%)
  other arithmetic  2.25 us (2%)
  local copies, waits for them, and re-layouts  2.02 us (2%)
    ppermute x13, starting transfers between devices, owner_flip(): return lax.ppermute(value, 'fsdp', [(i, i ^ bits) for i in range(8)])  22.8 us
    ppermute x13, waiting for transfers between devices, owner_flip(): return lax.ppermute(value, 'fsdp', [(i, i ^ bits) for i in range(8)])  19.9 us
    all_to_all x2, starting transfers between devices, zone_exchange(): lax.all_to_all(value, 'fsdp', split_axis=0, concat_axis=0, tiled=True, ax...  9.94 us
    pallas_call x1, Pallas kernels, pair_split(): pl.pallas_call(own_kernel, out_shape=(jax.ShapeDtypeStruct((8, 1024, 256)...  7.56 us
    pallas_call x1, Pallas kernels, pair_split(): pl.pallas_call(functools.partial(partial_kernel, True), out_shape=(jax.Sh...  6.1 us
    pallas_call x1, Pallas kernels, pair_split(): pl.pallas_call(near_kernel, out_shape=jax.ShapeDtypeStruct((4, 1024, 256)...  4.76 us
    pallas_call x1, Pallas kernels, pair_split(): pl.pallas_call(functools.partial(partial_kernel, False), out_shape=(jax.S...  3.61 us
    pallas_call x1, Pallas kernels, pair_split(): pl.pallas_call(head_kernel, out_shape=(jax.ShapeDtypeStruct((4, 64, 2048)...  3.52 us
  transfers between devices with their start and end apart: 22, of which 11 were waited for; matrix products, arithmetic and copies ran while one was open for 2% of the time, Pallas kernels for 24%

profile of v9, /device:TPU:0, one launch (start us, length us, event | category | flops | bytes accessed | tf_op | source)
XLA Modules:
  0.0 100.1 jit_solution(18386384219087989757)
XLA Ops:
  0.6 3.5 %head.1 = (bf16[4,64,2048]{2,1,0:T(8,128)(2,1)}, bf16[48,4096]{1,0:T(8,128)(2,1)}, bf16[64,4096]{1,0:T(8,128)(2,1)}) custom-call(s32[4]{0:T(128)} %pad_add_fusion.1.place_ref, bf16[64,8192]{1,0:T(8,128)(2,1)} %tok_in_ref.1, bf16[160,4096]{1,0:T(8,128)(2,1)} %gate_ref.3, bf16[160,4096]{1,0:T(8,128)(2,1)} %up_ref.3), custom_call_target="tpu_custom_call" | custom-call | tf_op jit(solution)/shard_map/head/pallas_call | solution.py:531
  4.1 6.5 %all-to-all-start = ((bf16[4,64,2048]{2,1,0:T(8,128)(2,1)}), bf16[4,64,2048]{2,1,0:T(8,128)(2,1)S(1)}, u32[]{:S(2)}, u32[]{:S(2)}) async-start(bf16[4,64,2048]{2,1,0:T(8,128)(2,1)} %get-tuple-element.37), calls=%async_computation | async-start | bytes 2097152 | tf_op jit(solution)/shard_map/all_to_all | solution.py:522
  10.6 1.5 %collective-permute-start.2 = (bf16[48,4096]{1,0:T(8,128)(2,1)S(1)}, bf16[48,4096]{1,0:T(8,128)(2,1)S(1)}, u32[]{:S(2)}, u32[]{:S(2)}) collective-permute-start(bf16[48,4096]{1,0:T(8,128)(2,1)S(1)} %copy-done.13), channel_id=1, source_target_pairs={{0,2},{2,0},{4,6},{6,4},{8,10},{10,8},{12,14},{14,12},{1,3},{3,1},... | collective-permute-start | bytes 1179656 | tf_op jit(solution)/shard_map/ppermute | solution.py:516
  13.4 7.6 %own_blocks.1 = (bf16[8,1024,256]{2,1,0:T(8,128)(2,1)}, f32[64,256]{1,0:T(8,128)}) custom-call(s32[4]{0:T(128)} %pad_add_fusion.1.place_ref, s32[3,256]{1,0:T(4,128)} %select_reduce_fusion.inv_ref, bf16[160,4096]{1,0:T(8,128)(2,1)} %gate_ref.3, bf16[160,4096]{1,0:T(8,128)(2,1)} %up_ref.3, bf16[160,4096]{1,0:T(8,128)(2,1)} %down_ref.1, ...), custom_call_target="tpu_custom_call" | custom-call | tf_op jit(solution)/shard_map/own_blocks/pallas_call | solution.py:558
  21.0 1.7 %collective-permute-done.2.a_in_ref = bf16[48,4096]{1,0:T(8,128)(2,1)S(1)} collective-permute-done((bf16[48,4096]{1,0:T(8,128)(2,1)S(1)}, bf16[48,4096]{1,0:T(8,128)(2,1)S(1)}, u32[]{:S(2)}, u32[]{:S(2)}) %collective-permute-start.2) | collective-permute-done | bytes 393248 | tf_op jit(solution)/shard_map/ppermute | solution.py:516
  22.7 1.5 %collective-permute-start.3 = (bf16[48,4096]{1,0:T(8,128)(2,1)S(1)}, bf16[48,4096]{1,0:T(8,128)(2,1)S(1)}, u32[]{:S(2)}, u32[]{:S(2)}) collective-permute-start(bf16[48,4096]{1,0:T(8,128)(2,1)S(1)} %collective-permute-done.2.a_in_ref), channel_id=1, source_target_pairs={{0,16},{16,0},{1,17},{17,1},{2,18},{18,2},{3,19},{19,3},{4,20},{20... | collective-permute-start | bytes 1179656 | tf_op jit(solution)/shard_map/ppermute | solution.py:581
  24.2 2.0 %collective-permute-start.4 = (f32[64,256]{1,0:T(8,128)}, f32[64,256]{1,0:T(8,128)S(1)}, u32[]{:S(2)}, u32[]{:S(2)}) collective-permute-start(f32[64,256]{1,0:T(8,128)} %get-tuple-element.38), channel_id=1, source_target_pairs={{0,4},{2,6},{4,0},{6,2},{8,12},{10,14},{12,8},{14,10},{1,5},{3,7},... | collective-permute-start | bytes 196616 | tf_op jit(solution)/shard_map/ppermute | solution.py:516
  26.2 3.0 %collective-permute-done.4 = f32[64,256]{1,0:T(8,128)S(1)} collective-permute-done((f32[64,256]{1,0:T(8,128)}, f32[64,256]{1,0:T(8,128)S(1)}, u32[]{:S(2)}, u32[]{:S(2)}) %collective-permute-start.4) | collective-permute-done | bytes 65568 | tf_op jit(solution)/shard_map/ppermute | solution.py:516
  30.0 4.6 %collective-permute-start.5 = (f32[64,256]{1,0:T(8,128)S(1)}, f32[64,256]{1,0:T(8,128)S(1)}, u32[]{:S(2)}, u32[]{:S(2)}) collective-permute-start(f32[64,256]{1,0:T(8,128)S(1)} %add.33), channel_id=1, source_target_pairs={{0,8},{2,10},{4,12},{6,14},{8,0},{10,2},{12,4},{14,6},{1,9},{3,11}... | collective-permute-start | bytes 196616 | tf_op jit(solution)/shard_map/ppermute | solution.py:516
  34.6 1.5 %collective-permute-start = (s32[3,256]{1,0:T(4,128)S(1)}, s32[3,256]{1,0:T(4,128)S(1)}, u32[]{:S(2)}, u32[]{:S(2)}) collective-permute-start(s32[3,256]{1,0:T(4,128)S(1)} %copy-done.7), channel_id=1, source_target_pairs={{0,2},{2,0},{4,6},{6,4},{8,10},{10,8},{12,14},{14,12},{1,3},{3,1},... | collective-permute-start | bytes 9224 | tf_op jit(solution)/shard_map/ppermute | solution.py:516
  36.1 2.1 %collective-permute-done.inv_ref = s32[3,256]{1,0:T(4,128)S(1)} collective-permute-done((s32[3,256]{1,0:T(4,128)S(1)}, s32[3,256]{1,0:T(4,128)S(1)}, u32[]{:S(2)}, u32[]{:S(2)}) %collective-permute-start) | collective-permute-done | bytes 3104 | tf_op jit(solution)/shard_map/ppermute | solution.py:516
  39.2 4.8 %near_blocks.1.near_in_ref = bf16[4,1024,256]{2,1,0:T(8,128)(2,1)} custom-call(s32[4]{0:T(128)} %pad_add_fusion.1.place_ref, s32[3,256]{1,0:T(4,128)} %copy-done.8, bf16[48,4096]{1,0:T(8,128)(2,1)} %copy-done.5, bf16[64,4096]{1,0:T(8,128)(2,1)} %copy-done.4, bf16[48,4096]{1,0:T(8,128)(2,1)} %copy-done.6), custom_call_target="tpu_custom_call" | custom-call | tf_op jit(solution)/shard_map/near_blocks/pallas_call | solution.py:588
  44.1 6.1 %first_partial.1 = (f32[64,1024]{1,0:T(8,128)}, bf16[4,64,1024]{2,1,0:T(8,128)(2,1)}) custom-call(s32[4]{0:T(128)} %pad_add_fusion.1.place_ref, bf16[4,1024,256]{2,1,0:T(8,128)(2,1)} %near_blocks.1.near_in_ref, bf16[8,1024,256]{2,1,0:T(8,128)(2,1)} %get-tuple-element.56.weight_in_ref, bf16[4,64,2048]{2,1,0:T(8,128)(2,1)} %copy-done), custom_call_target="tpu_custom_call" | custom-call | tf_op jit(solution)/shard_map/first_partial/pallas_call | solution.py:607
  50.2 3.5 %all-to-all-start.1 = ((bf16[4,64,1024]{2,1,0:T(8,128)(2,1)}), bf16[4,64,1024]{2,1,0:T(8,128)(2,1)S(1)}, u32[]{:S(2)}, u32[]{:S(2)}) async-start(bf16[4,64,1024]{2,1,0:T(8,128)(2,1)} %get-tuple-element.46), calls=%async_computation.1 | async-start | bytes 1048576 | tf_op jit(solution)/shard_map/all_to_all | solution.py:522
  53.7 1.5 %collective-permute-start.7 = (f32[64,256]{1,0:T(8,128)S(1)}, f32[64,256]{1,0:T(8,128)S(1)}, u32[]{:S(2)}, u32[]{:S(2)}) collective-permute-start(f32[64,256]{1,0:T(8,128)S(1)} %add.34), channel_id=1, source_target_pairs={{0,2},{2,0},{4,6},{6,4},{8,10},{10,8},{12,14},{14,12},{1,3},{3,1},... | collective-permute-start | bytes 196616 | tf_op jit(solution)/shard_map/ppermute | solution.py:516
  55.2 1.2 %copy-done.1 = bf16[4,64,2048]{2,1,0:T(8,128)(2,1)S(1)} copy-done((bf16[4,64,2048]{2,1,0:T(8,128)(2,1)S(1)}, bf16[4,64,2048]{2,1,0:T(8,128)(2,1)}, u32[]{:S(2)}) %copy-start.1) | copy-done | bytes 1048600
  56.5 3.6 %second_partial.1 = (f32[64,1024]{1,0:T(8,128)S(1)}, bf16[64,1024]{1,0:T(8,128)(2,1)S(1)}, bf16[64,1024]{1,0:T(8,128)(2,1)S(1)}, bf16[64,1024]{1,0:T(8,128)(2,1)S(1)}) custom-call(s32[4]{0:T(128)S(1)} %copy-done.3, bf16[4,1024,256]{2,1,0:T(8,128)(2,1)S(1)} %collective-permute-done.6.near_in_ref, bf16[8,1024,256]{2,1,0:T(8,128)(2,1)} %get-tuple-element.56.weight_in_ref, ...), custom_call_target="tpu_custom_call" | custom-call | tf_op jit(solution)/shard_map/second_partial/pallas_call | solution.py:630
  60.1 1.5 %collective-permute-start.13 = (f32[64,256]{1,0:T(8,128)S(1)}, f32[64,256]{1,0:T(8,128)S(1)}, u32[]{:S(2)}, u32[]{:S(2)}) collective-permute-start(f32[64,256]{1,0:T(8,128)S(1)} %add.35.pay0_ref), channel_id=1, source_target_pairs={{0,17},{1,16},{16,1},{17,0},{2,19},{3,18},{18,3},{19,2},{4,21},{5,... | collective-permute-start | bytes 196616 | tf_op jit(solution)/shard_map/ppermute | solution.py:656
  61.6 1.7 %collective-permute-start.8 = (bf16[64,1024]{1,0:T(8,128)(2,1)S(1)}, bf16[64,1024]{1,0:T(8,128)(2,1)S(1)}, u32[]{:S(2)}, u32[]{:S(2)}) collective-permute-start(bf16[64,1024]{1,0:T(8,128)(2,1)S(1)} %get-tuple-element.52), channel_id=1, source_target_pairs={{0,4},{2,6},{4,0},{6,2},{8,12},{10,14},{12,8},{14,10},{1,5},{3,7},... | collective-permute-start | bytes 393224 | tf_op jit(solution)/shard_map/ppermute | solution.py:516
  63.3 2.3 %collective-permute-start.9 = (bf16[64,1024]{1,0:T(8,128)(2,1)S(1)}, bf16[64,1024]{1,0:T(8,128)(2,1)S(1)}, u32[]{:S(2)}, u32[]{:S(2)}) collective-permute-start(bf16[64,1024]{1,0:T(8,128)(2,1)S(1)} %get-tuple-element.53), channel_id=1, source_target_pairs={{0,8},{2,10},{4,12},{6,14},{8,0},{10,2},{12,4},{14,6},{1,9},{3,11}... | collective-permute-start | bytes 393224 | tf_op jit(solution)/shard_map/ppermute | solution.py:516
  66.5 3.1 %all-to-all-done.1.first_ref = bf16[4,64,1024]{2,1,0:T(8,128)(2,1)S(1)} async-done(((bf16[4,64,1024]{2,1,0:T(8,128)(2,1)}), bf16[4,64,1024]{2,1,0:T(8,128)(2,1)S(1)}, u32[]{:S(2)}, u32[]{:S(2)}) %all-to-all-start.1) | async-done | bytes 524320 | tf_op jit(solution)/shard_map/all_to_all | solution.py:522
  69.6 2.2 %fetch_weights.1.weight_ref = bf16[8,1024,256]{2,1,0:T(8,128)(2,1)S(1)} custom-call(bf16[8,1024,256]{2,1,0:T(8,128)(2,1)} %get-tuple-element.56.weight_in_ref), custom_call_target="tpu_custom_call" | custom-call | tf_op jit(solution)/shard_map/fetch_weights/pallas_call | solution.py:660
  71.8 6.1 %collective-permute-done.9.second2_ref = bf16[64,1024]{1,0:T(8,128)(2,1)S(1)} collective-permute-done((bf16[64,1024]{1,0:T(8,128)(2,1)S(1)}, bf16[64,1024]{1,0:T(8,128)(2,1)S(1)}, u32[]{:S(2)}, u32[]{:S(2)}) %collective-permute-start.9) | collective-permute-done | bytes 131104 | tf_op jit(solution)/shard_map/ppermute | solution.py:516
  77.9 3.2 %token_sums.1 = (f32[8,2048]{1,0:T(8,128)S(1)}, f32[8,2048]{1,0:T(8,128)S(1)}) custom-call(s32[4]{0:T(128)S(1)} %copy-done.3, f32[64,1024]{1,0:T(8,128)S(1)} %copy-done.2, bf16[4,64,1024]{2,1,0:T(8,128)(2,1)S(1)} %all-to-all-done.1.first_ref, f32[64,1024]{1,0:T(8,128)S(1)} %get-tuple-element.51.second_keep_ref, ...), custom_call_target="tpu_custom_call" | custom-call | tf_op jit(solution)/shard_map/token_sums/pallas_call | solution.py:671
  81.2 1.2 %collective-permute-done.14 = f32[8,2048]{1,0:T(8,128)S(1)} collective-permute-done((f32[8,2048]{1,0:T(8,128)S(1)}, f32[8,2048]{1,0:T(8,128)S(1)}, u32[]{:S(2)}, u32[]{:S(2)}) %collective-permute-start.14) | collective-permute-done | bytes 65568 | tf_op jit(solution)/shard_map/ppermute | solution.py:519
  82.4 4.0 %collective-permute-start.17 = (f32[8,2048]{1,0:T(8,128)S(1)}, f32[8,2048]{1,0:T(8,128)S(1)}, u32[]{:S(2)}, u32[]{:S(2)}) collective-permute-start(f32[8,2048]{1,0:T(8,128)S(1)} %add.36), channel_id=1, source_target_pairs={{0,6},{2,4},{4,2},{6,0},{8,14},{10,12},{12,10},{14,8},{1,7},{3,5},... | collective-permute-start | bytes 196616 | tf_op jit(solution)/shard_map/ppermute | solution.py:516
  87.0 1.8 %collective-permute-done.17 = f32[8,2048]{1,0:T(8,128)S(1)} collective-permute-done((f32[8,2048]{1,0:T(8,128)S(1)}, f32[8,2048]{1,0:T(8,128)S(1)}, u32[]{:S(2)}, u32[]{:S(2)}) %collective-permute-start.17) | collective-permute-done | bytes 65568 | tf_op jit(solution)/shard_map/ppermute | solution.py:516
  88.8 1.9 %collective-permute-done.16 = f32[8,2048]{1,0:T(8,128)S(1)} collective-permute-done((f32[8,2048]{1,0:T(8,128)S(1)}, f32[8,2048]{1,0:T(8,128)S(1)}, u32[]{:S(2)}, u32[]{:S(2)}) %collective-permute-start.16) | collective-permute-done | bytes 65568 | tf_op jit(solution)/shard_map/ppermute | solution.py:516
  90.7 2.1 %collective-permute-start.18 = (f32[8,2048]{1,0:T(8,128)S(1)}, f32[8,2048]{1,0:T(8,128)S(1)}, u32[]{:S(2)}, u32[]{:S(2)}) collective-permute-start(f32[8,2048]{1,0:T(8,128)S(1)} %add_add_fusion), channel_id=1, source_target_pairs={{0,8},{2,10},{4,12},{6,14},{8,0},{10,2},{12,4},{14,6},{1,9},{3,11}... | collective-permute-start | bytes 196616 | tf_op jit(solution)/shard_map/ppermute | solution.py:516
  92.8 3.4 %collective-permute-done.18 = f32[8,2048]{1,0:T(8,128)S(1)} collective-permute-done((f32[8,2048]{1,0:T(8,128)S(1)}, f32[8,2048]{1,0:T(8,128)S(1)}, u32[]{:S(2)}, u32[]{:S(2)}) %collective-permute-start.18) | collective-permute-done | bytes 65568 | tf_op jit(solution)/shard_map/ppermute | solution.py:516
  96.3 1.2 %collective-permute-done.19.theirs_ref = f32[8,2048]{1,0:T(8,128)S(1)} collective-permute-done((f32[8,2048]{1,0:T(8,128)S(1)}, f32[8,2048]{1,0:T(8,128)S(1)}, u32[]{:S(2)}, u32[]{:S(2)}) %collective-permute-start.19) | collective-permute-done | bytes 65568 | tf_op jit(solution)/shard_map/ppermute | solution.py:519
  97.6 2.6 %products.1 = f32[16,1024]{1,0:T(8,128)} custom-call(s32[4]{0:T(128)S(1)} %copy-done.3, f32[8,2048]{1,0:T(8,128)S(1)} %add.40.mine_ref, f32[8,2048]{1,0:T(8,128)S(1)} %collective-permute-done.19.theirs_ref, bf16[8,1024,256]{2,1,0:T(8,128)(2,1)S(1)} %fetch_weights.1.weight_ref), custom_call_target="tpu_custom_call" | custom-call | tf_op jit(solution)/shard_map/products/pallas_call | solution.py:693
  (57 shorter events, 5.5 us)
Async XLA Ops:
  0.6 12.0 %copy-start.9 = (s32[160]{0:T(256)S(1)}, s32[160]{0:T(256)}, u32[]{:S(2)}) copy-start(s32[160]{0:T(256)} %param.16) | copy-start | bytes 1924
  0.6 12.0 %copy-start.10 = (s32[160]{0:T(256)S(1)}, s32[160]{0:T(256)}, u32[]{:S(2)}) copy-start(s32[160]{0:T(256)} %param.14) | copy-start | bytes 1924
  0.6 12.0 %copy-start.11 = (s32[160]{0:T(256)S(1)}, s32[160]{0:T(256)}, u32[]{:S(2)}) copy-start(s32[160]{0:T(256)} %param.12) | copy-start | bytes 1924
  4.1 6.5 %copy-start.13 = (bf16[48,4096]{1,0:T(8,128)(2,1)S(1)}, bf16[48,4096]{1,0:T(8,128)(2,1)}, u32[]{:S(2)}) copy-start(bf16[48,4096]{1,0:T(8,128)(2,1)} %get-tuple-element.34) | copy-start | bytes 1179652
  4.1 8.0 %copy-start.12 = (bf16[64,4096]{1,0:T(8,128)(2,1)S(1)}, bf16[64,4096]{1,0:T(8,128)(2,1)}, u32[]{:S(2)}) copy-start(bf16[64,4096]{1,0:T(8,128)(2,1)} %get-tuple-element.33) | copy-start | bytes 1572868
  4.1 34.3 %all-to-all-start = ((bf16[4,64,2048]{2,1,0:T(8,128)(2,1)}), bf16[4,64,2048]{2,1,0:T(8,128)(2,1)S(1)}, u32[]{:S(2)}, u32[]{:S(2)}) async-start(bf16[4,64,2048]{2,1,0:T(8,128)(2,1)} %get-tuple-element.37), calls=%async_computation | async-start | bytes 2097152 | tf_op jit(solution)/shard_map/all_to_all | solution.py:522
  10.6 12.0 %collective-permute-start.2 = (bf16[48,4096]{1,0:T(8,128)(2,1)S(1)}, bf16[48,4096]{1,0:T(8,128)(2,1)S(1)}, u32[]{:S(2)}, u32[]{:S(2)}) collective-permute-start(bf16[48,4096]{1,0:T(8,128)(2,1)S(1)} %copy-done.13), channel_id=1, source_target_pairs={{0,2},{2,0},{4,6},{6,4},{8,10},{10,8},{12,14},{14,12},{1,3},{3,1},... | collective-permute-start | bytes 1179656 | tf_op jit(solution)/shard_map/ppermute | solution.py:516
  12.1 26.1 %collective-permute-start.1 = (bf16[64,4096]{1,0:T(8,128)(2,1)S(1)}, bf16[64,4096]{1,0:T(8,128)(2,1)S(1)}, u32[]{:S(2)}, u32[]{:S(2)}) collective-permute-start(bf16[64,4096]{1,0:T(8,128)(2,1)S(1)} %copy-done.12), channel_id=1, source_target_pairs={{0,2},{2,0},{4,6},{6,4},{8,10},{10,8},{12,14},{14,12},{1,3},{3,1},... | collective-permute-start | bytes 1572872 | tf_op jit(solution)/shard_map/ppermute | solution.py:516
  13.4 21.2 %copy-start.7 = (s32[3,256]{1,0:T(4,128)S(1)}, s32[3,256]{1,0:T(4,128)}, u32[]{:S(2)}) copy-start(s32[3,256]{1,0:T(4,128)} %select_reduce_fusion.inv_ref) | copy-start | bytes 9220
  22.7 15.8 %copy-start.5 = (bf16[48,4096]{1,0:T(8,128)(2,1)}, bf16[48,4096]{1,0:T(8,128)(2,1)S(1)}, u32[]{:S(2)}) copy-start(bf16[48,4096]{1,0:T(8,128)(2,1)S(1)} %collective-permute-done.2.a_in_ref) | copy-start | bytes 1179652
  22.7 15.6 %collective-permute-start.3 = (bf16[48,4096]{1,0:T(8,128)(2,1)S(1)}, bf16[48,4096]{1,0:T(8,128)(2,1)S(1)}, u32[]{:S(2)}, u32[]{:S(2)}) collective-permute-start(bf16[48,4096]{1,0:T(8,128)(2,1)S(1)} %collective-permute-done.2.a_in_ref), channel_id=1, source_target_pairs={{0,16},{16,0},{1,17},{17,1},{2,18},{18,2},{3,19},{19,3},{4,20},{20... | collective-permute-start | bytes 1179656 | tf_op jit(solution)/shard_map/ppermute | solution.py:581
  24.2 5.0 %collective-permute-start.4 = (f32[64,256]{1,0:T(8,128)}, f32[64,256]{1,0:T(8,128)S(1)}, u32[]{:S(2)}, u32[]{:S(2)}) collective-permute-start(f32[64,256]{1,0:T(8,128)} %get-tuple-element.38), channel_id=1, source_target_pairs={{0,4},{2,6},{4,0},{6,2},{8,12},{10,14},{12,8},{14,10},{1,5},{3,7},... | collective-permute-start | bytes 196616 | tf_op jit(solution)/shard_map/ppermute | solution.py:516
  30.0 13.9 %collective-permute-start.5 = (f32[64,256]{1,0:T(8,128)S(1)}, f32[64,256]{1,0:T(8,128)S(1)}, u32[]{:S(2)}, u32[]{:S(2)}) collective-permute-start(f32[64,256]{1,0:T(8,128)S(1)} %add.33), channel_id=1, source_target_pairs={{0,8},{2,10},{4,12},{6,14},{8,0},{10,2},{12,4},{14,6},{1,9},{3,11}... | collective-permute-start | bytes 196616 | tf_op jit(solution)/shard_map/ppermute | solution.py:516
  34.6 3.6 %collective-permute-start = (s32[3,256]{1,0:T(4,128)S(1)}, s32[3,256]{1,0:T(4,128)S(1)}, u32[]{:S(2)}, u32[]{:S(2)}) collective-permute-start(s32[3,256]{1,0:T(4,128)S(1)} %copy-done.7), channel_id=1, source_target_pairs={{0,2},{2,0},{4,6},{6,4},{8,10},{10,8},{12,14},{14,12},{1,3},{3,1},... | collective-permute-start | bytes 9224 | tf_op jit(solution)/shard_map/ppermute | solution.py:516
  39.2 4.9 %copy-start = (bf16[4,64,2048]{2,1,0:T(8,128)(2,1)}, bf16[4,64,2048]{2,1,0:T(8,128)(2,1)S(1)}, u32[]{:S(2)}) copy-start(bf16[4,64,2048]{2,1,0:T(8,128)(2,1)S(1)} %all-to-all-done.tok_in_ref) | copy-start | bytes 3145732
  44.0 11.3 %collective-permute-start.6 = (bf16[4,1024,256]{2,1,0:T(8,128)(2,1)}, bf16[4,1024,256]{2,1,0:T(8,128)(2,1)S(1)}, u32[]{:S(2)}, u32[]{:S(2)}) collective-permute-start(bf16[4,1024,256]{2,1,0:T(8,128)(2,1)} %near_blocks.1.near_in_ref), channel_id=1, source_target_pairs={{0,1},{1,0},{2,3},{3,2},{4,5},{5,4},{6,7},{7,6},{8,9},{9,8},{10,11... | collective-permute-start | bytes 6291464 | tf_op jit(solution)/shard_map/ppermute | solution.py:519
  44.1 11.2 %copy-start.3 = (s32[4]{0:T(128)S(1)}, s32[4]{0:T(128)}, u32[]{:S(2)}) copy-start(s32[4]{0:T(128)} %pad_add_fusion.1.place_ref) | copy-start | bytes 52
  50.2 19.4 %all-to-all-start.1 = ((bf16[4,64,1024]{2,1,0:T(8,128)(2,1)}), bf16[4,64,1024]{2,1,0:T(8,128)(2,1)S(1)}, u32[]{:S(2)}, u32[]{:S(2)}) async-start(bf16[4,64,1024]{2,1,0:T(8,128)(2,1)} %get-tuple-element.46), calls=%async_computation.1 | async-start | bytes 1048576 | tf_op jit(solution)/shard_map/all_to_all | solution.py:522
  53.7 6.4 %collective-permute-start.7 = (f32[64,256]{1,0:T(8,128)S(1)}, f32[64,256]{1,0:T(8,128)S(1)}, u32[]{:S(2)}, u32[]{:S(2)}) collective-permute-start(f32[64,256]{1,0:T(8,128)S(1)} %add.34), channel_id=1, source_target_pairs={{0,2},{2,0},{4,6},{6,4},{8,10},{10,8},{12,14},{14,12},{1,3},{3,1},... | collective-permute-start | bytes 196616 | tf_op jit(solution)/shard_map/ppermute | solution.py:516
  60.1 6.4 %collective-permute-start.13 = (f32[64,256]{1,0:T(8,128)S(1)}, f32[64,256]{1,0:T(8,128)S(1)}, u32[]{:S(2)}, u32[]{:S(2)}) collective-permute-start(f32[64,256]{1,0:T(8,128)S(1)} %add.35.pay0_ref), channel_id=1, source_target_pairs={{0,17},{1,16},{16,1},{17,0},{2,19},{3,18},{18,3},{19,2},{4,21},{5,... | collective-permute-start | bytes 196616 | tf_op jit(solution)/shard_map/ppermute | solution.py:656
  61.6 10.2 %collective-permute-start.8 = (bf16[64,1024]{1,0:T(8,128)(2,1)S(1)}, bf16[64,1024]{1,0:T(8,128)(2,1)S(1)}, u32[]{:S(2)}, u32[]{:S(2)}) collective-permute-start(bf16[64,1024]{1,0:T(8,128)(2,1)S(1)} %get-tuple-element.52), channel_id=1, source_target_pairs={{0,4},{2,6},{4,0},{6,2},{8,12},{10,14},{12,8},{14,10},{1,5},{3,7},... | collective-permute-start | bytes 393224 | tf_op jit(solution)/shard_map/ppermute | solution.py:516
  63.3 14.6 %collective-permute-start.9 = (bf16[64,1024]{1,0:T(8,128)(2,1)S(1)}, bf16[64,1024]{1,0:T(8,128)(2,1)S(1)}, u32[]{:S(2)}, u32[]{:S(2)}) collective-permute-start(bf16[64,1024]{1,0:T(8,128)(2,1)S(1)} %get-tuple-element.53), channel_id=1, source_target_pairs={{0,8},{2,10},{4,12},{6,14},{8,0},{10,2},{12,4},{14,6},{1,9},{3,11}... | collective-permute-start | bytes 393224 | tf_op jit(solution)/shard_map/ppermute | solution.py:516
  65.6 12.3 %copy-start.2 = (f32[64,1024]{1,0:T(8,128)S(1)}, f32[64,1024]{1,0:T(8,128)}, u32[]{:S(2)}) copy-start(f32[64,1024]{1,0:T(8,128)} %get-tuple-element.45.first_keep_ref) | copy-start | bytes 786436
  65.6 12.3 %collective-permute-start.10 = (bf16[64,1024]{1,0:T(8,128)(2,1)S(1)}, bf16[64,1024]{1,0:T(8,128)(2,1)S(1)}, u32[]{:S(2)}, u32[]{:S(2)}) collective-permute-start(bf16[64,1024]{1,0:T(8,128)(2,1)S(1)} %get-tuple-element.54), channel_id=1, source_target_pairs={{0,12},{2,14},{4,8},{6,10},{8,4},{10,6},{12,0},{14,2},{1,13},{3,15... | collective-permute-start | bytes 393224 | tf_op jit(solution)/shard_map/ppermute | solution.py:516
  66.0 5.8 %collective-permute-start.12 = (f32[64,256]{1,0:T(8,128)S(1)}, f32[64,256]{1,0:T(8,128)S(1)}, u32[]{:S(2)}, u32[]{:S(2)}) collective-permute-start(f32[64,256]{1,0:T(8,128)S(1)} %add.35.pay0_ref), channel_id=1, source_target_pairs={{0,16},{16,0},{1,17},{17,1},{2,18},{18,2},{3,19},{19,3},{4,20},{20... | collective-permute-start | bytes 196616 | tf_op jit(solution)/shard_map/ppermute | solution.py:655
  66.5 5.3 %collective-permute-start.11 = (f32[64,256]{1,0:T(8,128)S(1)}, f32[64,256]{1,0:T(8,128)S(1)}, u32[]{:S(2)}, u32[]{:S(2)}) collective-permute-start(f32[64,256]{1,0:T(8,128)S(1)} %add.35.pay0_ref), channel_id=1, source_target_pairs={{0,1},{1,0},{2,3},{3,2},{4,5},{5,4},{6,7},{7,6},{8,9},{9,8},{10,11... | collective-permute-start | bytes 196616 | tf_op jit(solution)/shard_map/ppermute | solution.py:519
  81.1 1.3 %collective-permute-start.14 = (f32[8,2048]{1,0:T(8,128)S(1)}, f32[8,2048]{1,0:T(8,128)S(1)}, u32[]{:S(2)}, u32[]{:S(2)}) collective-permute-start(f32[8,2048]{1,0:T(8,128)S(1)} %get-tuple-element.59), channel_id=1, source_target_pairs={{0,1},{1,0},{2,3},{3,2},{4,5},{5,4},{6,7},{7,6},{8,9},{9,8},{10,11... | collective-permute-start | bytes 196616 | tf_op jit(solution)/shard_map/ppermute | solution.py:519
  82.4 6.4 %collective-permute-start.17 = (f32[8,2048]{1,0:T(8,128)S(1)}, f32[8,2048]{1,0:T(8,128)S(1)}, u32[]{:S(2)}, u32[]{:S(2)}) collective-permute-start(f32[8,2048]{1,0:T(8,128)S(1)} %add.36), channel_id=1, source_target_pairs={{0,6},{2,4},{4,2},{6,0},{8,14},{10,12},{12,10},{14,8},{1,7},{3,5},... | collective-permute-start | bytes 196616 | tf_op jit(solution)/shard_map/ppermute | solution.py:516
  86.4 4.3 %collective-permute-start.16 = (f32[8,2048]{1,0:T(8,128)S(1)}, f32[8,2048]{1,0:T(8,128)S(1)}, u32[]{:S(2)}, u32[]{:S(2)}) collective-permute-start(f32[8,2048]{1,0:T(8,128)S(1)} %add.36), channel_id=1, source_target_pairs={{0,4},{2,6},{4,0},{6,2},{8,12},{10,14},{12,8},{14,10},{1,5},{3,7},... | collective-permute-start | bytes 196616 | tf_op jit(solution)/shard_map/ppermute | solution.py:516
  86.4 4.3 %collective-permute-start.15 = (f32[8,2048]{1,0:T(8,128)S(1)}, f32[8,2048]{1,0:T(8,128)S(1)}, u32[]{:S(2)}, u32[]{:S(2)}) collective-permute-start(f32[8,2048]{1,0:T(8,128)S(1)} %add.36), channel_id=1, source_target_pairs={{0,2},{2,0},{4,6},{6,4},{8,10},{10,8},{12,14},{14,12},{1,3},{3,1},... | collective-permute-start | bytes 196616 | tf_op jit(solution)/shard_map/ppermute | solution.py:516
  90.7 5.5 %collective-permute-start.18 = (f32[8,2048]{1,0:T(8,128)S(1)}, f32[8,2048]{1,0:T(8,128)S(1)}, u32[]{:S(2)}, u32[]{:S(2)}) collective-permute-start(f32[8,2048]{1,0:T(8,128)S(1)} %add_add_fusion), channel_id=1, source_target_pairs={{0,8},{2,10},{4,12},{6,14},{8,0},{10,2},{12,4},{14,6},{1,9},{3,11}... | collective-permute-start | bytes 196616 | tf_op jit(solution)/shard_map/ppermute | solution.py:516
  96.2 1.3 %collective-permute-start.19 = (f32[8,2048]{1,0:T(8,128)S(1)}, f32[8,2048]{1,0:T(8,128)S(1)}, u32[]{:S(2)}, u32[]{:S(2)}) collective-permute-start(f32[8,2048]{1,0:T(8,128)S(1)} %add.40.mine_ref), channel_id=1, source_target_pairs={{0,1},{1,0},{2,3},{3,2},{4,5},{5,4},{6,7},{7,6},{8,9},{9,8},{10,11... | collective-permute-start | bytes 196616 | tf_op jit(solution)/shard_map/ppermute | solution.py:519
  (4 other events, 3.6 us)

commit v10 on v8

--- a/solution.py
+++ b/solution.py
@@ -141,7 +141,7 @@
 
 
 def stage_blocks(blocks_ref, tiles_ref, first_slot):
-    @pl.loop(0, blocks_ref.shape[0] // 16)
+    @pl.loop(0, blocks_ref.shape[0] // 16, unroll=2)
     def _(step):
         row = pl.multiple_of(step * 16, 16)
         target = pl.multiple_of(first_slot + row, 16)
@@ -167,7 +167,7 @@
 
 
 def assemble_columns(inv_ref, inv_row, tiles_ref, put):
-    @pl.loop(0, 16)
+    @pl.loop(0, 16, unroll=4)
     def _(block_row):
         for pair in range(8):
             cell = block_row * 16 + 2 * pair
@@ -179,9 +179,7 @@
             put(pair, row + BLK // 2, odd)
 
 
-def head_kernel(
-    place_ref, tok_in_ref, gate_ref, up_ref, zone_out_ref, a_out_ref, b_out_ref, tok_ref, blocks_ref, sem
-):
+def head_kernel(place_ref, gate_ref, up_ref, a_out_ref, b_out_ref, blocks_ref, sem):
     group = place_ref[1] // 2
     core = place_ref[3]
 
@@ -193,28 +191,15 @@
     def _():
         pltpu.make_async_copy(up_ref, blocks_ref, sem.at[0]).start()
 
-    loads, stores = [], []
-    for zone in range(4):
-        held = tok_ref.at[zone]
-        lanes = pl.ds(2048 * zone, 2048)
-        loads.append(pltpu.make_async_copy(tok_in_ref.at[:, lanes], held, sem.at[3 + zone]))
-        stores.append(pltpu.make_async_copy(held, zone_out_ref.at[zone], sem.at[7 + zone]))
-    for load in loads:
-        load.start()
     pltpu.make_async_copy(gate_ref, blocks_ref, sem.at[0]).wait()
     first = pl.multiple_of(SHARED * group, 16)
-    stores.append(
-        pltpu.make_async_copy(blocks_ref.at[pl.ds(first, SHARED)], a_out_ref, sem.at[1])
-    )
-    stores.append(
+    stores = [
+        pltpu.make_async_copy(blocks_ref.at[pl.ds(first, SHARED)], a_out_ref, sem.at[1]),
         pltpu.make_async_copy(
             blocks_ref.at[pl.ds(2 * SHARED, 160 - 2 * SHARED)], b_out_ref, sem.at[2]
-        )
-    )
-    stores[4].start()
-    stores[5].start()
-    for load, store in zip(loads, stores[:4]):
-        load.wait()
+        ),
+    ]
+    for store in stores:
         store.start()
     for store in stores:
         store.wait()
@@ -292,10 +277,8 @@
             high_iota == high_part[probe : probe + 1, :], values[probe : probe + 1, :], 0.0
         )
         one_hot = jnp.where(low_iota == low_part[probe : probe + 1, :], 1.0, 0.0).astype(BF)
-        total = None
-        for part in split3(picked):
-            term = contract_last(part, one_hot)
-            total = term if total is None else total + term
+        terms = contract_last(jnp.concatenate(split3(picked), axis=0), one_hot)
+        total = terms[:8] + terms[8:16] + terms[16:]
         omega_ref[8 * probe : 8 * (probe + 1), :] = total
     for high in range(8):
         piece = omega_ref[pl.ds(high, 16, stride=8), :]
@@ -553,23 +536,20 @@
             axis_index_groups=[[0, 2, 4, 6], [1, 3, 5, 7]],
         )
 
-    by_zone, kind_a, kind_b = pl.pallas_call(
+    by_zone = tokens.reshape(64, 4, 2048).transpose(1, 0, 2)
+    by_zone, place_now = lax.optimization_barrier((by_zone, place))
+    kind_a, kind_b = pl.pallas_call(
         head_kernel,
         out_shape=(
-            jax.ShapeDtypeStruct((4, 64, 2048), BF),
             jax.ShapeDtypeStruct((SHARED, 4096), BF),
             jax.ShapeDtypeStruct((160 - 2 * SHARED, 4096), BF),
         ),
-        in_specs=[SMEM, HBM, HBM, HBM],
-        out_specs=(HBM,) * 3,
-        scratch_shapes=[
-            pltpu.VMEM((4, 64, 2048), BF),
-            pltpu.VMEM((160, 4096), BF),
-            pltpu.SemaphoreType.DMA((11,)),
-        ],
+        in_specs=[SMEM, HBM, HBM],
+        out_specs=(HBM,) * 2,
+        scratch_shapes=[pltpu.VMEM((160, 4096), BF), pltpu.SemaphoreType.DMA((3,))],
         compiler_params=params(60),
         name="head",
-    )(place, tokens, gate_blocks, up_blocks)
+    )(place_now, gate_blocks, up_blocks)
     near_a = owner_flip(kind_a, 1)
     near_b = owner_flip(kind_b, 1)
     gathered = zone_exchange(by_zone)
@@ -696,8 +676,9 @@
     )(place, first_keep, first_back, second_keep, *second_back, *pay_parts)
 
     sums = mine + core_flip(theirs)
-    for bits in (1, 2, 4):
-        sums = sums + owner_flip(sums, bits)
+    x_part, z_part, xz_part = [owner_flip(sums, bits) for bits in (1, 2, 3)]
+    sums = (sums + x_part) + (z_part + xz_part)
+    sums = sums + owner_flip(sums, 4)
 
     return pl.pallas_call(
         product_kernel,

time: 97 us -> 97.6 us (level)
  Pallas kernels: 31.5 us -> 28.1 us
  local copies, waits for them, and re-layouts: 0.03 us -> 2.37 us
  waiting for transfers between devices: 26.3 us -> 27.9 us
    reshape x0 -> x1, local copies, waits for them, and re-layouts: none -> 2.35 us  [pair_split(): by_zone = tokens.reshape(64, 4, 2048).transpose(1, 0, 2)]
    pallas_call x1, Pallas kernels: 9.59 us -> 7.53 us  [pair_split(): pl.pallas_call(own_kernel, out_shape=(jax.ShapeDtypeStruct((8, 1024, 256)...]
    all_to_all x2, starting transfers between devices: 9.94 us -> 11.1 us  [zone_exchange(): lax.all_to_all(value, 'fsdp', split_axis=0, concat_axis=0, tiled=True, ax...]
    ppermute x12 -> x13, waiting for transfers between devices: 20 us -> 21.1 us  [owner_flip(): return lax.ppermute(value, 'fsdp', [(i, i ^ bits) for i in range(8)])]
    ppermute x12 -> x13, starting transfers between devices: 22.8 us -> 22 us  [owner_flip(): return lax.ppermute(value, 'fsdp', [(i, i ^ bits) for i in range(8)])]
  transfers between devices with their start and end apart: 21 -> 22, of which waited for: 9 -> 12; matrix products, arithmetic and copies ran while one was open for 2% -> 2% of each run, Pallas kernels for 17% -> 17%
where the time goes in v10:
time: 97.6 us; the launch traced here: 97.2 us
  starting transfers between devices  36.4 us (37%)
  Pallas kernels  28.1 us (29%)
  waiting for transfers between devices  27.9 us (29%)
  local copies, waits for them, and re-layouts  2.37 us (2%)
  other arithmetic  2.26 us (2%)
    ppermute x13, starting transfers between devices, owner_flip(): return lax.ppermute(value, 'fsdp', [(i, i ^ bits) for i in range(8)])  22 us
    ppermute x13, waiting for transfers between devices, owner_flip(): return lax.ppermute(value, 'fsdp', [(i, i ^ bits) for i in range(8)])  21.1 us
    all_to_all x2, starting transfers between devices, zone_exchange(): lax.all_to_all(value, 'fsdp', split_axis=0, concat_axis=0, tiled=True, ax...  11.1 us
    pallas_call x1, Pallas kernels, pair_split(): pl.pallas_call(own_kernel, out_shape=(jax.ShapeDtypeStruct((8, 1024, 256)...  7.53 us
    pallas_call x1, Pallas kernels, pair_split(): pl.pallas_call(first_kernel, out_shape=(jax.ShapeDtypeStruct((64, 1024),...  5.4 us
    all_to_all x2, waiting for transfers between devices, zone_exchange(): lax.all_to_all(value, 'fsdp', split_axis=0, concat_axis=0, tiled=True, ax...  4.36 us
    pallas_call x1, Pallas kernels, pair_split(): pl.pallas_call(second_kernel, out_shape=(jax.ShapeDtypeStruct((64, 1024),...  4.25 us
    pallas_call x1, Pallas kernels, pair_split(): pl.pallas_call(middle_kernel, out_shape=(jax.ShapeDtypeStruct((8, 2048),...  3.15 us
  transfers between devices with their start and end apart: 22, of which 12 were waited for; matrix products, arithmetic and copies ran while one was open for 2% of the time, Pallas kernels for 17%

profile of v10, /device:TPU:0, one launch (start us, length us, event | category | flops | bytes accessed | tf_op | source)
XLA Modules:
  0.0 97.2 jit_solution(11409432193961218962)
XLA Ops:
  0.0 2.4 %copy.15 = bf16[8,4,8,2048]{3,2,0,1:T(8,128)(2,1)} copy(bf16[8,4,8,2048]{3,2,1,0:T(8,128)(2,1)} %bitcast.14) | data formatting | bytes 2097152 | tf_op jit(solution)/shard_map/reshape | solution.py:539
  3.0 6.4 %all-to-all-start = ((bf16[4,64,2048]{2,1,0:T(8,128)(2,1)}), bf16[4,64,2048]{2,1,0:T(8,128)(2,1)S(1)}, u32[]{:S(2)}, u32[]{:S(2)}) async-start(bf16[4,64,2048]{2,1,0:T(8,128)(2,1)} %bitcast.13), calls=%async_computation | async-start | bytes 2097152 | tf_op jit(solution)/shard_map/all_to_all | solution.py:530
  9.4 2.9 %head.1 = (bf16[48,4096]{1,0:T(8,128)(2,1)}, bf16[64,4096]{1,0:T(8,128)(2,1)}) custom-call(s32[4]{0:T(128)} %pad_add_fusion.1.place_ref, bf16[160,4096]{1,0:T(8,128)(2,1)} %gate_ref.3, bf16[160,4096]{1,0:T(8,128)(2,1)} %up_ref.3), custom_call_target="tpu_custom_call" | custom-call | tf_op jit(solution)/shard_map/head/pallas_call | solution.py:541
  12.4 1.6 %collective-permute-start.2 = (bf16[48,4096]{1,0:T(8,128)(2,1)}, bf16[48,4096]{1,0:T(8,128)(2,1)S(1)}, u32[]{:S(2)}, u32[]{:S(2)}) collective-permute-start(bf16[48,4096]{1,0:T(8,128)(2,1)} %get-tuple-element.35), channel_id=1, source_target_pairs={{0,2},{2,0},{4,6},{6,4},{8,10},{10,8},{12,14},{14,12},{1,3},{3,1},... | collective-permute-start | bytes 1179656 | tf_op jit(solution)/shard_map/ppermute | solution.py:524
  15.2 7.5 %own_blocks.1 = (bf16[8,1024,256]{2,1,0:T(8,128)(2,1)}, f32[64,256]{1,0:T(8,128)}) custom-call(s32[4]{0:T(128)} %pad_add_fusion.1.place_ref, s32[3,256]{1,0:T(4,128)} %select_reduce_fusion.inv_ref, bf16[160,4096]{1,0:T(8,128)(2,1)} %gate_ref.3, bf16[160,4096]{1,0:T(8,128)(2,1)} %up_ref.3, bf16[160,4096]{1,0:T(8,128)(2,1)} %down_ref.1, ...), custom_call_target="tpu_custom_call" | custom-call | tf_op jit(solution)/shard_map/own_blocks/pallas_call | solution.py:563
  22.8 1.9 %collective-permute-done.2.a_in_ref = bf16[48,4096]{1,0:T(8,128)(2,1)S(1)} collective-permute-done((bf16[48,4096]{1,0:T(8,128)(2,1)}, bf16[48,4096]{1,0:T(8,128)(2,1)S(1)}, u32[]{:S(2)}, u32[]{:S(2)}) %collective-permute-start.2) | collective-permute-done | bytes 393248 | tf_op jit(solution)/shard_map/ppermute | solution.py:524
  24.7 1.5 %collective-permute-start.3 = (bf16[48,4096]{1,0:T(8,128)(2,1)S(1)}, bf16[48,4096]{1,0:T(8,128)(2,1)S(1)}, u32[]{:S(2)}, u32[]{:S(2)}) collective-permute-start(bf16[48,4096]{1,0:T(8,128)(2,1)S(1)} %collective-permute-done.2.a_in_ref), channel_id=1, source_target_pairs={{0,16},{16,0},{1,17},{17,1},{2,18},{18,2},{3,19},{19,3},{4,20},{20... | collective-permute-start | bytes 1179656 | tf_op jit(solution)/shard_map/ppermute | solution.py:586
  26.2 2.0 %collective-permute-start.4 = (f32[64,256]{1,0:T(8,128)}, f32[64,256]{1,0:T(8,128)S(1)}, u32[]{:S(2)}, u32[]{:S(2)}) collective-permute-start(f32[64,256]{1,0:T(8,128)} %get-tuple-element.39), channel_id=1, source_target_pairs={{0,4},{2,6},{4,0},{6,2},{8,12},{10,14},{12,8},{14,10},{1,5},{3,7},... | collective-permute-start | bytes 196616 | tf_op jit(solution)/shard_map/ppermute | solution.py:524
  28.2 2.7 %collective-permute-done.4 = f32[64,256]{1,0:T(8,128)S(1)} collective-permute-done((f32[64,256]{1,0:T(8,128)}, f32[64,256]{1,0:T(8,128)S(1)}, u32[]{:S(2)}, u32[]{:S(2)}) %collective-permute-start.4) | collective-permute-done | bytes 65568 | tf_op jit(solution)/shard_map/ppermute | solution.py:524
  31.8 4.6 %collective-permute-start.5 = (f32[64,256]{1,0:T(8,128)S(1)}, f32[64,256]{1,0:T(8,128)S(1)}, u32[]{:S(2)}, u32[]{:S(2)}) collective-permute-start(f32[64,256]{1,0:T(8,128)S(1)} %add.33), channel_id=1, source_target_pairs={{0,8},{2,10},{4,12},{6,14},{8,0},{10,2},{12,4},{14,6},{1,9},{3,11}... | collective-permute-start | bytes 196616 | tf_op jit(solution)/shard_map/ppermute | solution.py:524
  36.4 1.5 %collective-permute-start = (s32[3,256]{1,0:T(4,128)S(1)}, s32[3,256]{1,0:T(4,128)S(1)}, u32[]{:S(2)}, u32[]{:S(2)}) collective-permute-start(s32[3,256]{1,0:T(4,128)S(1)} %copy-done.1), channel_id=1, source_target_pairs={{0,2},{2,0},{4,6},{6,4},{8,10},{10,8},{12,14},{14,12},{1,3},{3,1},... | collective-permute-start | bytes 9224 | tf_op jit(solution)/shard_map/ppermute | solution.py:524
  38.6 1.4 %collective-permute-done.inv_ref = s32[3,256]{1,0:T(4,128)S(1)} collective-permute-done((s32[3,256]{1,0:T(4,128)S(1)}, s32[3,256]{1,0:T(4,128)S(1)}, u32[]{:S(2)}, u32[]{:S(2)}) %collective-permute-start) | collective-permute-done | bytes 3104 | tf_op jit(solution)/shard_map/ppermute | solution.py:524
  40.0 5.4 %first_partial.1 = (f32[64,1024]{1,0:T(8,128)S(1)}, bf16[4,64,1024]{2,1,0:T(8,128)(2,1)}, bf16[4,1024,256]{2,1,0:T(8,128)(2,1)}) custom-call(s32[4]{0:T(128)S(1)} %copy-done, s32[3,256]{1,0:T(4,128)S(1)} %collective-permute-done.inv_ref, bf16[48,4096]{1,0:T(8,128)(2,1)S(1)} %collective-permute-done.2.a_in_ref, ...), custom_call_target="tpu_custom_call" | custom-call | tf_op jit(solution)/shard_map/first_partial/pallas_call | solution.py:593
  45.5 4.7 %all-to-all-start.1 = ((bf16[4,64,1024]{2,1,0:T(8,128)(2,1)}), bf16[4,64,1024]{2,1,0:T(8,128)(2,1)S(1)}, u32[]{:S(2)}, u32[]{:S(2)}) async-start(bf16[4,64,1024]{2,1,0:T(8,128)(2,1)} %get-tuple-element.46), calls=%async_computation.1 | async-start | bytes 1048576 | tf_op jit(solution)/shard_map/all_to_all | solution.py:530
  50.2 1.5 %collective-permute-start.7 = (f32[64,256]{1,0:T(8,128)S(1)}, f32[64,256]{1,0:T(8,128)S(1)}, u32[]{:S(2)}, u32[]{:S(2)}) collective-permute-start(f32[64,256]{1,0:T(8,128)S(1)} %add.34), channel_id=1, source_target_pairs={{0,2},{2,0},{4,6},{6,4},{8,10},{10,8},{12,14},{14,12},{1,3},{3,1},... | collective-permute-start | bytes 196616 | tf_op jit(solution)/shard_map/ppermute | solution.py:524
  51.7 4.2 %second_partial.1 = (f32[64,1024]{1,0:T(8,128)S(1)}, bf16[64,1024]{1,0:T(8,128)(2,1)S(1)}, bf16[64,1024]{1,0:T(8,128)(2,1)S(1)}, bf16[64,1024]{1,0:T(8,128)(2,1)S(1)}) custom-call(s32[4]{0:T(128)S(1)} %copy-done, bf16[4,1024,256]{2,1,0:T(8,128)(2,1)} %collective-permute-done.6.near_in_ref, bf16[8,1024,256]{2,1,0:T(8,128)(2,1)} %get-tuple-element.56.weight_in_ref, ...), custom_call_target="tpu_custom_call" | custom-call | tf_op jit(solution)/shard_map/second_partial/pallas_call | solution.py:620
  55.9 2.1 %collective-permute-start.8 = (bf16[64,1024]{1,0:T(8,128)(2,1)S(1)}, bf16[64,1024]{1,0:T(8,128)(2,1)S(1)}, u32[]{:S(2)}, u32[]{:S(2)}) collective-permute-start(bf16[64,1024]{1,0:T(8,128)(2,1)S(1)} %get-tuple-element.52), channel_id=1, source_target_pairs={{0,4},{2,6},{4,0},{6,2},{8,12},{10,14},{12,8},{14,10},{1,5},{3,7},... | collective-permute-start | bytes 393224 | tf_op jit(solution)/shard_map/ppermute | solution.py:524
  58.1 2.4 %collective-permute-start.9 = (bf16[64,1024]{1,0:T(8,128)(2,1)S(1)}, bf16[64,1024]{1,0:T(8,128)(2,1)S(1)}, u32[]{:S(2)}, u32[]{:S(2)}) collective-permute-start(bf16[64,1024]{1,0:T(8,128)(2,1)S(1)} %get-tuple-element.53), channel_id=1, source_target_pairs={{0,8},{2,10},{4,12},{6,14},{8,0},{10,2},{12,4},{14,6},{1,9},{3,11}... | collective-permute-start | bytes 393224 | tf_op jit(solution)/shard_map/ppermute | solution.py:524
  60.6 1.5 %collective-permute-start.12 = (f32[64,256]{1,0:T(8,128)S(1)}, f32[64,256]{1,0:T(8,128)S(1)}, u32[]{:S(2)}, u32[]{:S(2)}) collective-permute-start(f32[64,256]{1,0:T(8,128)S(1)} %add.35.pay0_ref), channel_id=1, source_target_pairs={{0,16},{16,0},{1,17},{17,1},{2,18},{18,2},{3,19},{19,3},{4,20},{20... | collective-permute-start | bytes 196616 | tf_op jit(solution)/shard_map/ppermute | solution.py:645
  62.1 4.4 %all-to-all-done.1.first_ref = bf16[4,64,1024]{2,1,0:T(8,128)(2,1)S(1)} async-done(((bf16[4,64,1024]{2,1,0:T(8,128)(2,1)}), bf16[4,64,1024]{2,1,0:T(8,128)(2,1)S(1)}, u32[]{:S(2)}, u32[]{:S(2)}) %all-to-all-start.1) | async-done | bytes 524320 | tf_op jit(solution)/shard_map/all_to_all | solution.py:530
  66.5 2.2 %fetch_weights.1.weight_ref = bf16[8,1024,256]{2,1,0:T(8,128)(2,1)S(1)} custom-call(bf16[8,1024,256]{2,1,0:T(8,128)(2,1)} %get-tuple-element.56.weight_in_ref), custom_call_target="tpu_custom_call" | custom-call | tf_op jit(solution)/shard_map/fetch_weights/pallas_call | solution.py:650
  68.7 5.7 %collective-permute-done.9.second2_ref = bf16[64,1024]{1,0:T(8,128)(2,1)S(1)} collective-permute-done((bf16[64,1024]{1,0:T(8,128)(2,1)S(1)}, bf16[64,1024]{1,0:T(8,128)(2,1)S(1)}, u32[]{:S(2)}, u32[]{:S(2)}) %collective-permute-start.9) | collective-permute-done | bytes 131104 | tf_op jit(solution)/shard_map/ppermute | solution.py:524
  74.5 3.1 %token_sums.1 = (f32[8,2048]{1,0:T(8,128)S(1)}, f32[8,2048]{1,0:T(8,128)S(1)}) custom-call(s32[4]{0:T(128)S(1)} %copy-done, f32[64,1024]{1,0:T(8,128)S(1)} %get-tuple-element.45.first_keep_ref, bf16[4,64,1024]{2,1,0:T(8,128)(2,1)S(1)} %all-to-all-done.1.first_ref, f32[64,1024]{1,0:T(8,128)S(1)} %get-tuple-element.51.second_keep_ref, ...), custom_call_target="tpu_custom_call" | custom-call | tf_op jit(solution)/shard_map/token_sums/pallas_call | solution.py:661
  77.7 1.2 %collective-permute-done.14 = f32[8,2048]{1,0:T(8,128)S(1)} collective-permute-done((f32[8,2048]{1,0:T(8,128)S(1)}, f32[8,2048]{1,0:T(8,128)S(1)}, u32[]{:S(2)}, u32[]{:S(2)}) %collective-permute-start.14) | collective-permute-done | bytes 65568 | tf_op jit(solution)/shard_map/ppermute | solution.py:527
  78.9 2.7 %collective-permute-start.16 = (f32[8,2048]{1,0:T(8,128)S(1)}, f32[8,2048]{1,0:T(8,128)S(1)}, u32[]{:S(2)}, u32[]{:S(2)}) collective-permute-start(f32[8,2048]{1,0:T(8,128)S(1)} %add.36), channel_id=1, source_target_pairs={{0,4},{2,6},{4,0},{6,2},{8,12},{10,14},{12,8},{14,10},{1,5},{3,7},... | collective-permute-start | bytes 196616 | tf_op jit(solution)/shard_map/ppermute | solution.py:524
  81.6 1.0 %collective-permute-start.17 = (f32[8,2048]{1,0:T(8,128)S(1)}, f32[8,2048]{1,0:T(8,128)S(1)}, u32[]{:S(2)}, u32[]{:S(2)}) collective-permute-start(f32[8,2048]{1,0:T(8,128)S(1)} %add.36), channel_id=1, source_target_pairs={{0,6},{2,4},{4,2},{6,0},{8,14},{10,12},{12,10},{14,8},{1,7},{3,5},... | collective-permute-start | bytes 196616 | tf_op jit(solution)/shard_map/ppermute | solution.py:524
  84.1 2.8 %collective-permute-done.17 = f32[8,2048]{1,0:T(8,128)S(1)} collective-permute-done((f32[8,2048]{1,0:T(8,128)S(1)}, f32[8,2048]{1,0:T(8,128)S(1)}, u32[]{:S(2)}, u32[]{:S(2)}) %collective-permute-start.17) | collective-permute-done | bytes 65568 | tf_op jit(solution)/shard_map/ppermute | solution.py:524
  86.9 1.0 collective-permute-done.15
  87.8 1.4 %collective-permute-start.18 = (f32[8,2048]{1,0:T(8,128)S(1)}, f32[8,2048]{1,0:T(8,128)S(1)}, u32[]{:S(2)}, u32[]{:S(2)}) collective-permute-start(f32[8,2048]{1,0:T(8,128)S(1)} %add_add_fusion), channel_id=1, source_target_pairs={{0,8},{2,10},{4,12},{6,14},{8,0},{10,2},{12,4},{14,6},{1,9},{3,11}... | collective-permute-start | bytes 196616 | tf_op jit(solution)/shard_map/ppermute | solution.py:524
  89.3 4.0 %collective-permute-done.18 = f32[8,2048]{1,0:T(8,128)S(1)} collective-permute-done((f32[8,2048]{1,0:T(8,128)S(1)}, f32[8,2048]{1,0:T(8,128)S(1)}, u32[]{:S(2)}, u32[]{:S(2)}) %collective-permute-start.18) | collective-permute-done | bytes 65568 | tf_op jit(solution)/shard_map/ppermute | solution.py:524
  93.3 1.2 %collective-permute-done.19.theirs_ref = f32[8,2048]{1,0:T(8,128)S(1)} collective-permute-done((f32[8,2048]{1,0:T(8,128)S(1)}, f32[8,2048]{1,0:T(8,128)S(1)}, u32[]{:S(2)}, u32[]{:S(2)}) %collective-permute-start.19) | collective-permute-done | bytes 65568 | tf_op jit(solution)/shard_map/ppermute | solution.py:527
  94.6 2.6 %products.1 = f32[16,1024]{1,0:T(8,128)} custom-call(s32[4]{0:T(128)S(1)} %copy-done, f32[8,2048]{1,0:T(8,128)S(1)} %add.40.mine_ref, f32[8,2048]{1,0:T(8,128)S(1)} %collective-permute-done.19.theirs_ref, bf16[8,1024,256]{2,1,0:T(8,128)(2,1)S(1)} %fetch_weights.1.weight_ref), custom_call_target="tpu_custom_call" | custom-call | tf_op jit(solution)/shard_map/products/pallas_call | solution.py:683
  (39 shorter events, 5.4 us)
Async XLA Ops:
  3.0 11.5 %copy-start.2 = (s32[160]{0:T(256)S(1)}, s32[160]{0:T(256)}, u32[]{:S(2)}) copy-start(s32[160]{0:T(256)} %param.16) | copy-start | bytes 1924
  3.0 11.5 %copy-start.3 = (s32[160]{0:T(256)S(1)}, s32[160]{0:T(256)}, u32[]{:S(2)}) copy-start(s32[160]{0:T(256)} %param.14) | copy-start | bytes 1924
  3.0 11.5 %copy-start.4 = (s32[160]{0:T(256)S(1)}, s32[160]{0:T(256)}, u32[]{:S(2)}) copy-start(s32[160]{0:T(256)} %param.12) | copy-start | bytes 1924
  3.0 37.0 %all-to-all-start = ((bf16[4,64,2048]{2,1,0:T(8,128)(2,1)}), bf16[4,64,2048]{2,1,0:T(8,128)(2,1)S(1)}, u32[]{:S(2)}, u32[]{:S(2)}) async-start(bf16[4,64,2048]{2,1,0:T(8,128)(2,1)} %bitcast.13), calls=%async_computation | async-start | bytes 2097152 | tf_op jit(solution)/shard_map/all_to_all | solution.py:530
  12.4 12.3 %collective-permute-start.2 = (bf16[48,4096]{1,0:T(8,128)(2,1)}, bf16[48,4096]{1,0:T(8,128)(2,1)S(1)}, u32[]{:S(2)}, u32[]{:S(2)}) collective-permute-start(bf16[48,4096]{1,0:T(8,128)(2,1)} %get-tuple-element.35), channel_id=1, source_target_pairs={{0,2},{2,0},{4,6},{6,4},{8,10},{10,8},{12,14},{14,12},{1,3},{3,1},... | collective-permute-start | bytes 1179656 | tf_op jit(solution)/shard_map/ppermute | solution.py:524
  13.9 26.1 %collective-permute-start.1 = (bf16[64,4096]{1,0:T(8,128)(2,1)}, bf16[64,4096]{1,0:T(8,128)(2,1)S(1)}, u32[]{:S(2)}, u32[]{:S(2)}) collective-permute-start(bf16[64,4096]{1,0:T(8,128)(2,1)} %get-tuple-element.34), channel_id=1, source_target_pairs={{0,2},{2,0},{4,6},{6,4},{8,10},{10,8},{12,14},{14,12},{1,3},{3,1},... | collective-permute-start | bytes 1572872 | tf_op jit(solution)/shard_map/ppermute | solution.py:524
  15.2 21.2 %copy-start.1 = (s32[3,256]{1,0:T(4,128)S(1)}, s32[3,256]{1,0:T(4,128)}, u32[]{:S(2)}) copy-start(s32[3,256]{1,0:T(4,128)} %select_reduce_fusion.inv_ref) | copy-start | bytes 9220
  15.2 24.8 %copy-start = (s32[4]{0:T(128)S(1)}, s32[4]{0:T(128)}, u32[]{:S(2)}) copy-start(s32[4]{0:T(128)} %pad_add_fusion.1.place_ref) | copy-start | bytes 52
  24.7 15.3 %collective-permute-start.3 = (bf16[48,4096]{1,0:T(8,128)(2,1)S(1)}, bf16[48,4096]{1,0:T(8,128)(2,1)S(1)}, u32[]{:S(2)}, u32[]{:S(2)}) collective-permute-start(bf16[48,4096]{1,0:T(8,128)(2,1)S(1)} %collective-permute-done.2.a_in_ref), channel_id=1, source_target_pairs={{0,16},{16,0},{1,17},{17,1},{2,18},{18,2},{3,19},{19,3},{4,20},{20... | collective-permute-start | bytes 1179656 | tf_op jit(solution)/shard_map/ppermute | solution.py:586
  26.2 4.7 %collective-permute-start.4 = (f32[64,256]{1,0:T(8,128)}, f32[64,256]{1,0:T(8,128)S(1)}, u32[]{:S(2)}, u32[]{:S(2)}) collective-permute-start(f32[64,256]{1,0:T(8,128)} %get-tuple-element.39), channel_id=1, source_target_pairs={{0,4},{2,6},{4,0},{6,2},{8,12},{10,14},{12,8},{14,10},{1,5},{3,7},... | collective-permute-start | bytes 196616 | tf_op jit(solution)/shard_map/ppermute | solution.py:524
  31.8 6.8 %collective-permute-start.5 = (f32[64,256]{1,0:T(8,128)S(1)}, f32[64,256]{1,0:T(8,128)S(1)}, u32[]{:S(2)}, u32[]{:S(2)}) collective-permute-start(f32[64,256]{1,0:T(8,128)S(1)} %add.33), channel_id=1, source_target_pairs={{0,8},{2,10},{4,12},{6,14},{8,0},{10,2},{12,4},{14,6},{1,9},{3,11}... | collective-permute-start | bytes 196616 | tf_op jit(solution)/shard_map/ppermute | solution.py:524
  36.4 3.6 %collective-permute-start = (s32[3,256]{1,0:T(4,128)S(1)}, s32[3,256]{1,0:T(4,128)S(1)}, u32[]{:S(2)}, u32[]{:S(2)}) collective-permute-start(s32[3,256]{1,0:T(4,128)S(1)} %copy-done.1), channel_id=1, source_target_pairs={{0,2},{2,0},{4,6},{6,4},{8,10},{10,8},{12,14},{14,12},{1,3},{3,1},... | collective-permute-start | bytes 9224 | tf_op jit(solution)/shard_map/ppermute | solution.py:524
  45.4 6.2 %collective-permute-start.6 = (bf16[4,1024,256]{2,1,0:T(8,128)(2,1)}, bf16[4,1024,256]{2,1,0:T(8,128)(2,1)}, u32[]{:S(2)}, u32[]{:S(2)}) collective-permute-start(bf16[4,1024,256]{2,1,0:T(8,128)(2,1)} %get-tuple-element.48), channel_id=1, source_target_pairs={{0,1},{1,0},{2,3},{3,2},{4,5},{5,4},{6,7},{7,6},{8,9},{9,8},{10,11... | collective-permute-start | bytes 6291464 | tf_op jit(solution)/shard_map/ppermute | solution.py:527
  45.5 21.0 %all-to-all-start.1 = ((bf16[4,64,1024]{2,1,0:T(8,128)(2,1)}), bf16[4,64,1024]{2,1,0:T(8,128)(2,1)S(1)}, u32[]{:S(2)}, u32[]{:S(2)}) async-start(bf16[4,64,1024]{2,1,0:T(8,128)(2,1)} %get-tuple-element.46), calls=%async_computation.1 | async-start | bytes 1048576 | tf_op jit(solution)/shard_map/all_to_all | solution.py:530
  50.2 5.8 %collective-permute-start.7 = (f32[64,256]{1,0:T(8,128)S(1)}, f32[64,256]{1,0:T(8,128)S(1)}, u32[]{:S(2)}, u32[]{:S(2)}) collective-permute-start(f32[64,256]{1,0:T(8,128)S(1)} %add.34), channel_id=1, source_target_pairs={{0,2},{2,0},{4,6},{6,4},{8,10},{10,8},{12,14},{14,12},{1,3},{3,1},... | collective-permute-start | bytes 196616 | tf_op jit(solution)/shard_map/ppermute | solution.py:524
  55.9 12.8 %collective-permute-start.8 = (bf16[64,1024]{1,0:T(8,128)(2,1)S(1)}, bf16[64,1024]{1,0:T(8,128)(2,1)S(1)}, u32[]{:S(2)}, u32[]{:S(2)}) collective-permute-start(bf16[64,1024]{1,0:T(8,128)(2,1)S(1)} %get-tuple-element.52), channel_id=1, source_target_pairs={{0,4},{2,6},{4,0},{6,2},{8,12},{10,14},{12,8},{14,10},{1,5},{3,7},... | collective-permute-start | bytes 393224 | tf_op jit(solution)/shard_map/ppermute | solution.py:524
  58.0 4.1 %collective-permute-start.11 = (f32[64,256]{1,0:T(8,128)S(1)}, f32[64,256]{1,0:T(8,128)S(1)}, u32[]{:S(2)}, u32[]{:S(2)}) collective-permute-start(f32[64,256]{1,0:T(8,128)S(1)} %add.35.pay0_ref), channel_id=1, source_target_pairs={{0,1},{1,0},{2,3},{3,2},{4,5},{5,4},{6,7},{7,6},{8,9},{9,8},{10,11... | collective-permute-start | bytes 196616 | tf_op jit(solution)/shard_map/ppermute | solution.py:527
  58.1 16.3 %collective-permute-start.9 = (bf16[64,1024]{1,0:T(8,128)(2,1)S(1)}, bf16[64,1024]{1,0:T(8,128)(2,1)S(1)}, u32[]{:S(2)}, u32[]{:S(2)}) collective-permute-start(bf16[64,1024]{1,0:T(8,128)(2,1)S(1)} %get-tuple-element.53), channel_id=1, source_target_pairs={{0,8},{2,10},{4,12},{6,14},{8,0},{10,2},{12,4},{14,6},{1,9},{3,11}... | collective-permute-start | bytes 393224 | tf_op jit(solution)/shard_map/ppermute | solution.py:524
  60.5 13.9 %collective-permute-start.10 = (bf16[64,1024]{1,0:T(8,128)(2,1)S(1)}, bf16[64,1024]{1,0:T(8,128)(2,1)S(1)}, u32[]{:S(2)}, u32[]{:S(2)}) collective-permute-start(bf16[64,1024]{1,0:T(8,128)(2,1)S(1)} %get-tuple-element.54), channel_id=1, source_target_pairs={{0,12},{2,14},{4,8},{6,10},{8,4},{10,6},{12,0},{14,2},{1,13},{3,15... | collective-permute-start | bytes 393224 | tf_op jit(solution)/shard_map/ppermute | solution.py:524
  60.6 8.1 %collective-permute-start.12 = (f32[64,256]{1,0:T(8,128)S(1)}, f32[64,256]{1,0:T(8,128)S(1)}, u32[]{:S(2)}, u32[]{:S(2)}) collective-permute-start(f32[64,256]{1,0:T(8,128)S(1)} %add.35.pay0_ref), channel_id=1, source_target_pairs={{0,16},{16,0},{1,17},{17,1},{2,18},{18,2},{3,19},{19,3},{4,20},{20... | collective-permute-start | bytes 196616 | tf_op jit(solution)/shard_map/ppermute | solution.py:645
  62.1 6.6 %collective-permute-start.13 = (f32[64,256]{1,0:T(8,128)S(1)}, f32[64,256]{1,0:T(8,128)S(1)}, u32[]{:S(2)}, u32[]{:S(2)}) collective-permute-start(f32[64,256]{1,0:T(8,128)S(1)} %add.35.pay0_ref), channel_id=1, source_target_pairs={{0,17},{1,16},{16,1},{17,0},{2,19},{3,18},{18,3},{19,2},{4,21},{5,... | collective-permute-start | bytes 196616 | tf_op jit(solution)/shard_map/ppermute | solution.py:646
  77.6 1.3 %collective-permute-start.14 = (f32[8,2048]{1,0:T(8,128)S(1)}, f32[8,2048]{1,0:T(8,128)S(1)}, u32[]{:S(2)}, u32[]{:S(2)}) collective-permute-start(f32[8,2048]{1,0:T(8,128)S(1)} %get-tuple-element.59), channel_id=1, source_target_pairs={{0,1},{1,0},{2,3},{3,2},{4,5},{5,4},{6,7},{7,6},{8,9},{9,8},{10,11... | collective-permute-start | bytes 196616 | tf_op jit(solution)/shard_map/ppermute | solution.py:527
  78.9 5.1 %collective-permute-start.16 = (f32[8,2048]{1,0:T(8,128)S(1)}, f32[8,2048]{1,0:T(8,128)S(1)}, u32[]{:S(2)}, u32[]{:S(2)}) collective-permute-start(f32[8,2048]{1,0:T(8,128)S(1)} %add.36), channel_id=1, source_target_pairs={{0,4},{2,6},{4,0},{6,2},{8,12},{10,14},{12,8},{14,10},{1,5},{3,7},... | collective-permute-start | bytes 196616 | tf_op jit(solution)/shard_map/ppermute | solution.py:524
  81.6 5.2 %collective-permute-start.17 = (f32[8,2048]{1,0:T(8,128)S(1)}, f32[8,2048]{1,0:T(8,128)S(1)}, u32[]{:S(2)}, u32[]{:S(2)}) collective-permute-start(f32[8,2048]{1,0:T(8,128)S(1)} %add.36), channel_id=1, source_target_pairs={{0,6},{2,4},{4,2},{6,0},{8,14},{10,12},{12,10},{14,8},{1,7},{3,5},... | collective-permute-start | bytes 196616 | tf_op jit(solution)/shard_map/ppermute | solution.py:524
  82.7 5.2 %collective-permute-start.15 = (f32[8,2048]{1,0:T(8,128)S(1)}, f32[8,2048]{1,0:T(8,128)S(1)}, u32[]{:S(2)}, u32[]{:S(2)}) collective-permute-start(f32[8,2048]{1,0:T(8,128)S(1)} %add.36), channel_id=1, source_target_pairs={{0,2},{2,0},{4,6},{6,4},{8,10},{10,8},{12,14},{14,12},{1,3},{3,1},... | collective-permute-start | bytes 196616 | tf_op jit(solution)/shard_map/ppermute | solution.py:524
  87.8 5.4 %collective-permute-start.18 = (f32[8,2048]{1,0:T(8,128)S(1)}, f32[8,2048]{1,0:T(8,128)S(1)}, u32[]{:S(2)}, u32[]{:S(2)}) collective-permute-start(f32[8,2048]{1,0:T(8,128)S(1)} %add_add_fusion), channel_id=1, source_target_pairs={{0,8},{2,10},{4,12},{6,14},{8,0},{10,2},{12,4},{14,6},{1,9},{3,11}... | collective-permute-start | bytes 196616 | tf_op jit(solution)/shard_map/ppermute | solution.py:524
  93.2 1.3 %collective-permute-start.19 = (f32[8,2048]{1,0:T(8,128)S(1)}, f32[8,2048]{1,0:T(8,128)S(1)}, u32[]{:S(2)}, u32[]{:S(2)}) collective-permute-start(f32[8,2048]{1,0:T(8,128)S(1)} %add.40.mine_ref), channel_id=1, source_target_pairs={{0,1},{1,0},{2,3},{3,2},{4,5},{5,4},{6,7},{7,6},{8,9},{9,8},{10,11... | collective-permute-start | bytes 196616 | tf_op jit(solution)/shard_map/ppermute | solution.py:527

commit v11 on v10

--- a/solution.py
+++ b/solution.py
@@ -179,34 +179,48 @@
             put(pair, row + BLK // 2, odd)
 
 
-def head_kernel(place_ref, gate_ref, up_ref, a_out_ref, b_out_ref, blocks_ref, sem):
-    group = place_ref[1] // 2
-    core = place_ref[3]
-
-    @pl.when(core == 0)
-    def _():
-        pltpu.make_async_copy(gate_ref, blocks_ref, sem.at[0]).start()
-
-    @pl.when(core != 0)
-    def _():
-        pltpu.make_async_copy(up_ref, blocks_ref, sem.at[0]).start()
-
-    pltpu.make_async_copy(gate_ref, blocks_ref, sem.at[0]).wait()
-    first = pl.multiple_of(SHARED * group, 16)
-    stores = [
-        pltpu.make_async_copy(blocks_ref.at[pl.ds(first, SHARED)], a_out_ref, sem.at[1]),
-        pltpu.make_async_copy(
-            blocks_ref.at[pl.ds(2 * SHARED, 160 - 2 * SHARED)], b_out_ref, sem.at[2]
-        ),
-    ]
-    for store in stores:
+def position():
+    owner = lax.axis_index("fsdp")
+    core = lax.axis_index("seq")
+    return owner, 2 * lax.axis_index("groups") + core, lax.rem(owner, 2), core
+
+
+def head_kernel(
+    tok_in_ref, gate_ref, up_ref, zone_out_ref, a_out_ref, b_out_ref, tok_ref, blocks_ref, sem
+):
+    unused_owner, quarter, unused_side, core = position()
+    first = pl.multiple_of(SHARED * (quarter // 2), 16)
+    a_part = pl.ds(first, SHARED)
+    b_part = pl.ds(2 * SHARED, 160 - 2 * SHARED)
+    loads, stores = [], []
+    for zone in range(4):
+        held = tok_ref.at[zone]
+        lanes = pl.ds(2048 * zone, 2048)
+        loads.append(pltpu.make_async_copy(tok_in_ref.at[:, lanes], held, sem.at[zone]))
+        stores.append(pltpu.make_async_copy(held, zone_out_ref.at[zone], sem.at[4 + zone]))
+    for load in loads:
+        load.start()
+    for kind, source in enumerate((gate_ref, up_ref)):
+
+        @pl.when(core == kind)
+        def _():
+            pltpu.make_async_copy(source.at[a_part], blocks_ref.at[a_part], sem.at[8]).start()
+            pltpu.make_async_copy(source.at[b_part], blocks_ref.at[b_part], sem.at[9]).start()
+
+    for load, store in zip(loads, stores):
+        load.wait()
         store.start()
+    pltpu.make_async_copy(gate_ref.at[a_part], blocks_ref.at[a_part], sem.at[8]).wait()
+    stores.append(pltpu.make_async_copy(blocks_ref.at[a_part], a_out_ref, sem.at[10]))
+    stores[4].start()
+    pltpu.make_async_copy(gate_ref.at[b_part], blocks_ref.at[b_part], sem.at[9]).wait()
+    stores.append(pltpu.make_async_copy(blocks_ref.at[b_part], b_out_ref, sem.at[11]))
+    stores[5].start()
     for store in stores:
         store.wait()
 
 
 def own_kernel(
-    place_ref,
     inv_ref,
     gate_ref,
     up_ref,
@@ -225,8 +239,7 @@
     in_sem,
     out_sem,
 ):
-    owner = place_ref[0]
-    quarter = place_ref[1]
+    owner, quarter, unused_side, unused_core = position()
     loads = [
         pltpu.make_async_copy(source, blocks_ref.at[i], in_sem.at[i])
         for i, source in enumerate((gate_ref, up_ref, down_ref))
@@ -309,7 +322,6 @@
 
 
 def first_kernel(
-    place_ref,
     inv_ref,
     a_in_ref,
     b_in_ref,
@@ -331,10 +343,9 @@
     near_sem,
     sent_sem,
 ):
-    zone = place_ref[0] // 2
-    side = place_ref[2]
-    core = place_ref[3]
-    group = place_ref[1] // 2
+    owner, quarter, side, core = position()
+    zone = owner // 2
+    group = quarter // 2
     mine = pl.multiple_of(SHARED * group, 16)
     other = pl.multiple_of(SHARED * (1 - group), 16)
     loads = [
@@ -382,7 +393,6 @@
 
 
 def second_kernel(
-    place_ref,
     near_in_ref,
     weight_in_ref,
     tok_in_ref,
@@ -397,9 +407,8 @@
     total_ref,
     in_sem,
 ):
-    zone = place_ref[0] // 2
-    side = place_ref[2]
-    core = place_ref[3]
+    owner, unused_quarter, side, core = position()
+    zone = owner // 2
     loads = [
         pltpu.make_async_copy(tok_in_ref, tok_ref, in_sem.at[0]),
         pltpu.make_async_copy(weight_in_ref.at[pl.ds(4 - 4 * core, 4)], own_ref, in_sem.at[1]),
@@ -422,7 +431,6 @@
 
 
 def middle_kernel(
-    place_ref,
     first_keep_ref,
     first_ref,
     second_keep_ref,
@@ -442,9 +450,8 @@
     tangent_ref,
     rows_ref,
 ):
-    zone = place_ref[0] // 2
-    quarter = place_ref[1]
-    core = place_ref[3]
+    owner, quarter, unused_side, core = position()
+    zone = owner // 2
     unshuffle = unshuffle_matrix(256)
     for flip, ref in enumerate((pay0_ref, pay1_ref, pay2_ref, pay3_ref)):
         pay_ref[flipped(quarter, flip)] = ref[...]
@@ -487,8 +494,8 @@
     copy.wait()
 
 
-def product_kernel(place_ref, mine_ref, theirs_ref, weight_ref, out_ref, sum_ref):
-    core = place_ref[3]
+def product_kernel(mine_ref, theirs_ref, weight_ref, out_ref, sum_ref):
+    core = lax.axis_index("seq")
     sum_ref[core] = mine_ref[...]
     sum_ref[1 - core] = theirs_ref[...]
     sums = jnp.concatenate([sum_ref[0], sum_ref[1]], axis=0).astype(BF)
@@ -515,11 +522,6 @@
     probe_index,
     probe_value,
 ):
-    owner = lax.axis_index("fsdp")
-    core = lax.axis_index("seq")
-    group = lax.axis_index("groups")
-    place = jnp.stack([owner, 2 * group + core, owner % 2, core]).astype(jnp.int32)
-
     def owner_flip(value, bits):
         return lax.ppermute(value, "fsdp", [(i, i ^ bits) for i in range(8)])
 
@@ -536,20 +538,23 @@
             axis_index_groups=[[0, 2, 4, 6], [1, 3, 5, 7]],
         )
 
-    by_zone = tokens.reshape(64, 4, 2048).transpose(1, 0, 2)
-    by_zone, place_now = lax.optimization_barrier((by_zone, place))
-    kind_a, kind_b = pl.pallas_call(
+    by_zone, kind_a, kind_b = pl.pallas_call(
         head_kernel,
         out_shape=(
+            jax.ShapeDtypeStruct((4, 64, 2048), BF),
             jax.ShapeDtypeStruct((SHARED, 4096), BF),
             jax.ShapeDtypeStruct((160 - 2 * SHARED, 4096), BF),
         ),
-        in_specs=[SMEM, HBM, HBM],
-        out_specs=(HBM,) * 2,
-        scratch_shapes=[pltpu.VMEM((160, 4096), BF), pltpu.SemaphoreType.DMA((3,))],
+        in_specs=[HBM, HBM, HBM],
+        out_specs=(HBM,) * 3,
+        scratch_shapes=[
+            pltpu.VMEM((4, 64, 2048), BF),
+            pltpu.VMEM((160, 4096), BF),
+            pltpu.SemaphoreType.DMA((12,)),
+        ],
         compiler_params=params(60),
         name="head",
-    )(place_now, gate_blocks, up_blocks)
+    )(tokens, gate_blocks, up_blocks)
     near_a = owner_flip(kind_a, 1)
     near_b = owner_flip(kind_b, 1)
     gathered = zone_exchange(by_zone)
@@ -566,7 +571,7 @@
             jax.ShapeDtypeStruct((8, 1024, 256), BF),
             jax.ShapeDtypeStruct((64, 256), F32),
         ),
-        in_specs=[SMEM, SMEM] + [HBM] * 3 + [VMEM] * 3,
+        in_specs=[SMEM] + [HBM] * 3 + [VMEM] * 3,
         out_specs=(HBM, VMEM),
         scratch_shapes=[
             pltpu.VMEM((32 * STRIDE, 128), F32),
@@ -580,7 +585,7 @@
         ],
         compiler_params=params(60),
         name="own_blocks",
-    )(place, inv, gate_blocks, up_blocks, down_blocks, sketch, probe_index, probe_value)
+    )(inv, gate_blocks, up_blocks, down_blocks, sketch, probe_index, probe_value)
 
     near_a, payload = lax.optimization_barrier((near_a, payload))
     near_a_other = lax.ppermute(near_a, "groups", [(0, 1), (1, 0)])
@@ -597,7 +602,7 @@
             jax.ShapeDtypeStruct((4, 64, 1024), BF),
             jax.ShapeDtypeStruct((4, 1024, 256), BF),
         ),
-        in_specs=[SMEM, SMEM, ANY, ANY, ANY, HBM, ANY],
+        in_specs=[SMEM, ANY, ANY, ANY, HBM, ANY],
         out_specs=(VMEM, HBM, HBM),
         scratch_shapes=[
             pltpu.VMEM((160, 4096), BF),
@@ -612,16 +617,16 @@
             pltpu.SemaphoreType.DMA,
             pltpu.SemaphoreType.DMA((4,)),
         ],
-        compiler_params=params(50),
+        compiler_params=params(53),
         name="first_partial",
-    )(place, near_inv, near_a, near_b, near_a_other, weights, gathered)
+    )(near_inv, near_a, near_b, near_a_other, weights, gathered)
     first_back = zone_exchange(first_sent)
 
     second_keep, *second_sent = pl.pallas_call(
         second_kernel,
         out_shape=(jax.ShapeDtypeStruct((64, 1024), F32),)
         + (jax.ShapeDtypeStruct((64, 1024), BF),) * 3,
-        in_specs=[SMEM, ANY, HBM, ANY],
+        in_specs=[ANY, HBM, ANY],
         out_specs=(VMEM,) * 4,
         scratch_shapes=[
             pltpu.VMEM((4, 1024, 256), BF),
@@ -633,7 +638,7 @@
         ],
         compiler_params=params(50),
         name="second_partial",
-    )(place, core_flip(near_weights), weights, gathered)
+    )(core_flip(near_weights), weights, gathered)
     second_back = [owner_flip(second_sent[flip - 1], 2 * flip) for flip in (1, 2, 3)]
 
     across = owner_flip(payload, 1)
@@ -661,7 +666,7 @@
     mine, theirs = pl.pallas_call(
         middle_kernel,
         out_shape=(jax.ShapeDtypeStruct((8, 2048), F32),) * 2,
-        in_specs=[SMEM] + [VMEM] * 10,
+        in_specs=[VMEM] * 10,
         out_specs=(VMEM,) * 2,
         scratch_shapes=[
             pltpu.VMEM((64, 1024), F32),
@@ -673,7 +678,7 @@
         ],
         compiler_params=params(48),
         name="token_sums",
-    )(place, first_keep, first_back, second_keep, *second_back, *pay_parts)
+    )(first_keep, first_back, second_keep, *second_back, *pay_parts)
 
     sums = mine + core_flip(theirs)
     x_part, z_part, xz_part = [owner_flip(sums, bits) for bits in (1, 2, 3)]
@@ -683,12 +688,12 @@
     return pl.pallas_call(
         product_kernel,
         out_shape=jax.ShapeDtypeStruct((P_SIZE, 1024), F32),
-        in_specs=[SMEM, VMEM, VMEM, VMEM],
+        in_specs=[VMEM, VMEM, VMEM],
         out_specs=VMEM,
         scratch_shapes=[pltpu.VMEM((2, 8, 2048), F32)],
         compiler_params=params(30),
         name="products",
-    )(place, sums, core_flip(sums), weights_at_hand)
+    )(sums, core_flip(sums), weights_at_hand)
 
 
 def per_device(tokens, gate_blocks, *rest):

time: 97.6 us -> 95.9 us (0.983)
  Pallas kernels: 28.1 us -> 26.1 us
  starting transfers between devices: 36.4 us -> 35.4 us
    unnamed x10 -> x20, local copies, waits for them, and re-layouts: 0.02 us -> 2.49 us
    reshape x1 -> x0, local copies, waits for them, and re-layouts: 2.35 us -> none  [pair_split(): by_zone = tokens.reshape(64, 4, 2048).transpose(1, 0, 2)]
    ppermute x13, waiting for transfers between devices: 21.1 us -> 22.5 us  [owner_flip(): return lax.ppermute(value, 'fsdp', [(i, i ^ bits) for i in range(8)])]
    all_to_all x2, waiting for transfers between devices: 4.36 us -> 2.95 us  [zone_exchange(): lax.all_to_all(value, 'fsdp', split_axis=0, concat_axis=0, tiled=True, ax...]
    pallas_call x1, Pallas kernels: 4.25 us -> 3.07 us  [pair_split(): pl.pallas_call(second_kernel, out_shape=(jax.ShapeDtypeStruct((64, 1024),...]
    all_to_all x2, starting transfers between devices: 11.1 us -> 9.94 us  [zone_exchange(): lax.all_to_all(value, 'fsdp', split_axis=0, concat_axis=0, tiled=True, ax...]
  transfers between devices with their start and end apart: 22 -> 22, of which waited for: 12 -> 11; matrix products, arithmetic and copies ran while one was open for 2% -> 3% of each run, Pallas kernels for 17% -> 13%
where the time goes in v11:
time: 95.9 us; the launch traced here: 95.4 us
  starting transfers between devices  35.4 us (37%)
  waiting for transfers between devices  28 us (29%)
  Pallas kernels  26.1 us (27%)
  other arithmetic  3.12 us (3%)
  local copies, waits for them, and re-layouts  2.49 us (3%)
    ppermute x13, waiting for transfers between devices, owner_flip(): return lax.ppermute(value, 'fsdp', [(i, i ^ bits) for i in range(8)])  22.5 us
    ppermute x13, starting transfers between devices, owner_flip(): return lax.ppermute(value, 'fsdp', [(i, i ^ bits) for i in range(8)])  22.2 us
    all_to_all x2, starting transfers between devices, zone_exchange(): lax.all_to_all(value, 'fsdp', split_axis=0, concat_axis=0, tiled=True, ax...  9.94 us
    pallas_call x1, Pallas kernels, pair_split(): pl.pallas_call(own_kernel, out_shape=(jax.ShapeDtypeStruct((8, 1024, 256)...  7.54 us
    pallas_call x1, Pallas kernels, pair_split(): pl.pallas_call(first_kernel, out_shape=(jax.ShapeDtypeStruct((64, 1024),...  6.27 us
    pallas_call x1, Pallas kernels, pair_split(): pl.pallas_call(second_kernel, out_shape=(jax.ShapeDtypeStruct((64, 1024),...  3.07 us
    all_to_all x2, waiting for transfers between devices, zone_exchange(): lax.all_to_all(value, 'fsdp', split_axis=0, concat_axis=0, tiled=True, ax...  2.95 us
    pallas_call x1, Pallas kernels, pair_split(): pl.pallas_call(middle_kernel, out_shape=(jax.ShapeDtypeStruct((8, 2048),...  2.61 us
  transfers between devices with their start and end apart: 22, of which 11 were waited for; matrix products, arithmetic and copies ran while one was open for 3% of the time, Pallas kernels for 13%

profile of v11, /device:TPU:0, one launch (start us, length us, event | category | flops | bytes accessed | tf_op | source)
XLA Modules:
  0.0 95.4 jit_solution(6358707373371650899)
XLA Ops:
  0.0 2.4 %head.1 = (bf16[4,64,2048]{2,1,0:T(8,128)(2,1)}, bf16[48,4096]{1,0:T(8,128)(2,1)}, bf16[64,4096]{1,0:T(8,128)(2,1)}) custom-call(bf16[64,8192]{1,0:T(8,128)(2,1)} %tok_in_ref.1, bf16[160,4096]{1,0:T(8,128)(2,1)} %gate_ref.3, bf16[160,4096]{1,0:T(8,128)(2,1)} %up_ref.3), custom_call_target="tpu_custom_call" | custom-call | tf_op jit(solution)/shard_map/head/pallas_call | solution.py:541
  2.5 6.5 %all-to-all-start = ((bf16[4,64,2048]{2,1,0:T(8,128)(2,1)}), bf16[4,64,2048]{2,1,0:T(8,128)(2,1)S(1)}, u32[]{:S(2)}, u32[]{:S(2)}) async-start(bf16[4,64,2048]{2,1,0:T(8,128)(2,1)} %get-tuple-element.36), calls=%async_computation | async-start | bytes 2097152 | tf_op jit(solution)/shard_map/all_to_all | solution.py:532
  8.9 1.5 %collective-permute-start.2 = (bf16[48,4096]{1,0:T(8,128)(2,1)S(1)}, bf16[48,4096]{1,0:T(8,128)(2,1)S(1)}, u32[]{:S(2)}, u32[]{:S(2)}) collective-permute-start(bf16[48,4096]{1,0:T(8,128)(2,1)S(1)} %copy-done.9), channel_id=1, source_target_pairs={{0,2},{2,0},{4,6},{6,4},{8,10},{10,8},{12,14},{14,12},{1,3},{3,1},... | collective-permute-start | bytes 1179656 | tf_op jit(solution)/shard_map/ppermute | solution.py:526
  11.7 7.5 %own_blocks.1 = (bf16[8,1024,256]{2,1,0:T(8,128)(2,1)}, f32[64,256]{1,0:T(8,128)}) custom-call(s32[3,256]{1,0:T(4,128)} %select_reduce_fusion.inv_ref, bf16[160,4096]{1,0:T(8,128)(2,1)} %gate_ref.3, bf16[160,4096]{1,0:T(8,128)(2,1)} %up_ref.3, bf16[160,4096]{1,0:T(8,128)(2,1)} %down_ref.1, bf16[32,1024]{1,0:T(8,128)(2,1)} %sketch_ref.1, ...), custom_call_target="tpu_custom_call" | custom-call | tf_op jit(solution)/shard_map/own_blocks/pallas_call | solution.py:568
  19.3 1.7 %collective-permute-done.2.a_in_ref = bf16[48,4096]{1,0:T(8,128)(2,1)S(1)} collective-permute-done((bf16[48,4096]{1,0:T(8,128)(2,1)S(1)}, bf16[48,4096]{1,0:T(8,128)(2,1)S(1)}, u32[]{:S(2)}, u32[]{:S(2)}) %collective-permute-start.2) | collective-permute-done | bytes 393248 | tf_op jit(solution)/shard_map/ppermute | solution.py:526
  21.0 1.5 %collective-permute-start.3 = (bf16[48,4096]{1,0:T(8,128)(2,1)S(1)}, bf16[48,4096]{1,0:T(8,128)(2,1)S(1)}, u32[]{:S(2)}, u32[]{:S(2)}) collective-permute-start(bf16[48,4096]{1,0:T(8,128)(2,1)S(1)} %collective-permute-done.2.a_in_ref), channel_id=1, source_target_pairs={{0,16},{16,0},{1,17},{17,1},{2,18},{18,2},{3,19},{19,3},{4,20},{20... | collective-permute-start | bytes 1179656 | tf_op jit(solution)/shard_map/ppermute | solution.py:591
  22.5 2.0 %collective-permute-start.4 = (f32[64,256]{1,0:T(8,128)}, f32[64,256]{1,0:T(8,128)S(1)}, u32[]{:S(2)}, u32[]{:S(2)}) collective-permute-start(f32[64,256]{1,0:T(8,128)} %get-tuple-element.37), channel_id=1, source_target_pairs={{0,4},{2,6},{4,0},{6,2},{8,12},{10,14},{12,8},{14,10},{1,5},{3,7},... | collective-permute-start | bytes 196616 | tf_op jit(solution)/shard_map/ppermute | solution.py:526
  24.5 3.0 %collective-permute-done.4 = f32[64,256]{1,0:T(8,128)S(1)} collective-permute-done((f32[64,256]{1,0:T(8,128)}, f32[64,256]{1,0:T(8,128)S(1)}, u32[]{:S(2)}, u32[]{:S(2)}) %collective-permute-start.4) | collective-permute-done | bytes 65568 | tf_op jit(solution)/shard_map/ppermute | solution.py:526
  28.3 4.6 %collective-permute-start.5 = (f32[64,256]{1,0:T(8,128)S(1)}, f32[64,256]{1,0:T(8,128)S(1)}, u32[]{:S(2)}, u32[]{:S(2)}) collective-permute-start(f32[64,256]{1,0:T(8,128)S(1)} %add.24), channel_id=1, source_target_pairs={{0,8},{2,10},{4,12},{6,14},{8,0},{10,2},{12,4},{14,6},{1,9},{3,11}... | collective-permute-start | bytes 196616 | tf_op jit(solution)/shard_map/ppermute | solution.py:526
  32.9 1.5 %collective-permute-start = (s32[3,256]{1,0:T(4,128)S(1)}, s32[3,256]{1,0:T(4,128)S(1)}, u32[]{:S(2)}, u32[]{:S(2)}) collective-permute-start(s32[3,256]{1,0:T(4,128)S(1)} %copy-done.4), channel_id=1, source_target_pairs={{0,2},{2,0},{4,6},{6,4},{8,10},{10,8},{12,14},{14,12},{1,3},{3,1},... | collective-permute-start | bytes 9224 | tf_op jit(solution)/shard_map/ppermute | solution.py:526
  34.4 3.1 %collective-permute-done.5 = f32[64,256]{1,0:T(8,128)S(1)} collective-permute-done((f32[64,256]{1,0:T(8,128)S(1)}, f32[64,256]{1,0:T(8,128)S(1)}, u32[]{:S(2)}, u32[]{:S(2)}) %collective-permute-start.5) | collective-permute-done | bytes 65568 | tf_op jit(solution)/shard_map/ppermute | solution.py:526
  39.4 6.3 %first_partial.1 = (f32[64,1024]{1,0:T(8,128)S(1)}, bf16[4,64,1024]{2,1,0:T(8,128)(2,1)}, bf16[4,1024,256]{2,1,0:T(8,128)(2,1)}) custom-call(s32[3,256]{1,0:T(4,128)S(1)} %collective-permute-done.inv_ref, bf16[48,4096]{1,0:T(8,128)(2,1)S(1)} %collective-permute-done.2.a_in_ref, bf16[64,4096]{1,0:T(8,128)(2,1)} %copy-done.2, bf16[48,4096]{1,0:T(8,128)(2,1)} %copy-done.3, ...), custom_call_target="tpu_custom_call" | custom-call | tf_op jit(solution)/shard_map/first_partial/pallas_call | solution.py:598
  45.7 3.5 %all-to-all-start.1 = ((bf16[4,64,1024]{2,1,0:T(8,128)(2,1)}), bf16[4,64,1024]{2,1,0:T(8,128)(2,1)S(1)}, u32[]{:S(2)}, u32[]{:S(2)}) async-start(bf16[4,64,1024]{2,1,0:T(8,128)(2,1)} %get-tuple-element.44), calls=%async_computation.1 | async-start | bytes 1048576 | tf_op jit(solution)/shard_map/all_to_all | solution.py:532
  49.2 1.6 %collective-permute-start.7 = (f32[64,256]{1,0:T(8,128)}, f32[64,256]{1,0:T(8,128)S(1)}, u32[]{:S(2)}, u32[]{:S(2)}) collective-permute-start(f32[64,256]{1,0:T(8,128)} %add.25), channel_id=1, source_target_pairs={{0,2},{2,0},{4,6},{6,4},{8,10},{10,8},{12,14},{14,12},{1,3},{3,1},... | collective-permute-start | bytes 196616 | tf_op jit(solution)/shard_map/ppermute | solution.py:526
  50.8 1.2 %copy-done.1 = bf16[4,64,2048]{2,1,0:T(8,128)(2,1)S(1)} copy-done((bf16[4,64,2048]{2,1,0:T(8,128)(2,1)S(1)}, bf16[4,64,2048]{2,1,0:T(8,128)(2,1)}, u32[]{:S(2)}) %copy-start.1) | copy-done | bytes 1048600
  52.0 3.1 %second_partial.1 = (f32[64,1024]{1,0:T(8,128)S(1)}, bf16[64,1024]{1,0:T(8,128)(2,1)S(1)}, bf16[64,1024]{1,0:T(8,128)(2,1)S(1)}, bf16[64,1024]{1,0:T(8,128)(2,1)S(1)}) custom-call(bf16[4,1024,256]{2,1,0:T(8,128)(2,1)S(1)} %collective-permute-done.6.near_in_ref, bf16[8,1024,256]{2,1,0:T(8,128)(2,1)} %get-tuple-element.54.weight_in_ref, ...), custom_call_target="tpu_custom_call" | custom-call | tf_op jit(solution)/shard_map/second_partial/pallas_call | solution.py:625
  55.1 2.0 %collective-permute-start.8 = (bf16[64,1024]{1,0:T(8,128)(2,1)S(1)}, bf16[64,1024]{1,0:T(8,128)(2,1)S(1)}, u32[]{:S(2)}, u32[]{:S(2)}) collective-permute-start(bf16[64,1024]{1,0:T(8,128)(2,1)S(1)} %get-tuple-element.50), channel_id=1, source_target_pairs={{0,4},{2,6},{4,0},{6,2},{8,12},{10,14},{12,8},{14,10},{1,5},{3,7},... | collective-permute-start | bytes 393224 | tf_op jit(solution)/shard_map/ppermute | solution.py:526
  58.0 2.4 %collective-permute-start.9 = (bf16[64,1024]{1,0:T(8,128)(2,1)S(1)}, bf16[64,1024]{1,0:T(8,128)(2,1)S(1)}, u32[]{:S(2)}, u32[]{:S(2)}) collective-permute-start(bf16[64,1024]{1,0:T(8,128)(2,1)S(1)} %get-tuple-element.51), channel_id=1, source_target_pairs={{0,8},{2,10},{4,12},{6,14},{8,0},{10,2},{12,4},{14,6},{1,9},{3,11}... | collective-permute-start | bytes 393224 | tf_op jit(solution)/shard_map/ppermute | solution.py:526
  60.5 1.5 %collective-permute-start.12 = (f32[64,256]{1,0:T(8,128)S(1)}, f32[64,256]{1,0:T(8,128)S(1)}, u32[]{:S(2)}, u32[]{:S(2)}) collective-permute-start(f32[64,256]{1,0:T(8,128)S(1)} %add.26.pay0_ref), channel_id=1, source_target_pairs={{0,16},{16,0},{1,17},{17,1},{2,18},{18,2},{3,19},{19,3},{4,20},{20... | collective-permute-start | bytes 196616 | tf_op jit(solution)/shard_map/ppermute | solution.py:650
  62.1 2.9 %all-to-all-done.1.first_ref = bf16[4,64,1024]{2,1,0:T(8,128)(2,1)S(1)} async-done(((bf16[4,64,1024]{2,1,0:T(8,128)(2,1)}), bf16[4,64,1024]{2,1,0:T(8,128)(2,1)S(1)}, u32[]{:S(2)}, u32[]{:S(2)}) %all-to-all-start.1) | async-done | bytes 524320 | tf_op jit(solution)/shard_map/all_to_all | solution.py:532
  65.0 2.2 %fetch_weights.1.weight_ref = bf16[8,1024,256]{2,1,0:T(8,128)(2,1)S(1)} custom-call(bf16[8,1024,256]{2,1,0:T(8,128)(2,1)} %get-tuple-element.54.weight_in_ref), custom_call_target="tpu_custom_call" | custom-call | tf_op jit(solution)/shard_map/fetch_weights/pallas_call | solution.py:655
  67.2 6.2 %collective-permute-done.9.second2_ref = bf16[64,1024]{1,0:T(8,128)(2,1)S(1)} collective-permute-done((bf16[64,1024]{1,0:T(8,128)(2,1)S(1)}, bf16[64,1024]{1,0:T(8,128)(2,1)S(1)}, u32[]{:S(2)}, u32[]{:S(2)}) %collective-permute-start.9) | collective-permute-done | bytes 131104 | tf_op jit(solution)/shard_map/ppermute | solution.py:526
  73.4 2.6 %token_sums.1 = (f32[8,2048]{1,0:T(8,128)S(1)}, f32[8,2048]{1,0:T(8,128)S(1)}) custom-call(f32[64,1024]{1,0:T(8,128)S(1)} %get-tuple-element.43.first_keep_ref, bf16[4,64,1024]{2,1,0:T(8,128)(2,1)S(1)} %all-to-all-done.1.first_ref, f32[64,1024]{1,0:T(8,128)S(1)} %get-tuple-element.49.second_keep_ref, ...), custom_call_target="tpu_custom_call" | custom-call | tf_op jit(solution)/shard_map/token_sums/pallas_call | solution.py:666
  76.1 1.2 %collective-permute-done.14 = f32[8,2048]{1,0:T(8,128)S(1)} collective-permute-done((f32[8,2048]{1,0:T(8,128)S(1)}, f32[8,2048]{1,0:T(8,128)S(1)}, u32[]{:S(2)}, u32[]{:S(2)}) %collective-permute-start.14) | collective-permute-done | bytes 65568 | tf_op jit(solution)/shard_map/ppermute | solution.py:529
  77.4 3.0 %collective-permute-start.16 = (f32[8,2048]{1,0:T(8,128)S(1)}, f32[8,2048]{1,0:T(8,128)S(1)}, u32[]{:S(2)}, u32[]{:S(2)}) collective-permute-start(f32[8,2048]{1,0:T(8,128)S(1)} %add.27), channel_id=1, source_target_pairs={{0,4},{2,6},{4,0},{6,2},{8,12},{10,14},{12,8},{14,10},{1,5},{3,7},... | collective-permute-start | bytes 196616 | tf_op jit(solution)/shard_map/ppermute | solution.py:526
  80.4 1.0 %collective-permute-start.17 = (f32[8,2048]{1,0:T(8,128)S(1)}, f32[8,2048]{1,0:T(8,128)S(1)}, u32[]{:S(2)}, u32[]{:S(2)}) collective-permute-start(f32[8,2048]{1,0:T(8,128)S(1)} %add.27), channel_id=1, source_target_pairs={{0,6},{2,4},{4,2},{6,0},{8,14},{10,12},{12,10},{14,8},{1,7},{3,5},... | collective-permute-start | bytes 196616 | tf_op jit(solution)/shard_map/ppermute | solution.py:526
  82.8 2.8 %collective-permute-done.17 = f32[8,2048]{1,0:T(8,128)S(1)} collective-permute-done((f32[8,2048]{1,0:T(8,128)S(1)}, f32[8,2048]{1,0:T(8,128)S(1)}, u32[]{:S(2)}, u32[]{:S(2)}) %collective-permute-start.17) | collective-permute-done | bytes 65568 | tf_op jit(solution)/shard_map/ppermute | solution.py:526
  85.6 1.0 collective-permute-done.15
  86.6 1.4 %collective-permute-start.18 = (f32[8,2048]{1,0:T(8,128)S(1)}, f32[8,2048]{1,0:T(8,128)S(1)}, u32[]{:S(2)}, u32[]{:S(2)}) collective-permute-start(f32[8,2048]{1,0:T(8,128)S(1)} %add_add_fusion), channel_id=1, source_target_pairs={{0,8},{2,10},{4,12},{6,14},{8,0},{10,2},{12,4},{14,6},{1,9},{3,11}... | collective-permute-start | bytes 196616 | tf_op jit(solution)/shard_map/ppermute | solution.py:526
  88.0 4.0 %collective-permute-done.18 = f32[8,2048]{1,0:T(8,128)S(1)} collective-permute-done((f32[8,2048]{1,0:T(8,128)S(1)}, f32[8,2048]{1,0:T(8,128)S(1)}, u32[]{:S(2)}, u32[]{:S(2)}) %collective-permute-start.18) | collective-permute-done | bytes 65568 | tf_op jit(solution)/shard_map/ppermute | solution.py:526
  92.1 1.2 %collective-permute-done.19.theirs_ref = f32[8,2048]{1,0:T(8,128)S(1)} collective-permute-done((f32[8,2048]{1,0:T(8,128)S(1)}, f32[8,2048]{1,0:T(8,128)S(1)}, u32[]{:S(2)}, u32[]{:S(2)}) %collective-permute-start.19) | collective-permute-done | bytes 65568 | tf_op jit(solution)/shard_map/ppermute | solution.py:529
  93.3 2.0 %products.1 = f32[16,1024]{1,0:T(8,128)} custom-call(f32[8,2048]{1,0:T(8,128)S(1)} %add.31.mine_ref, f32[8,2048]{1,0:T(8,128)S(1)} %collective-permute-done.19.theirs_ref, bf16[8,1024,256]{2,1,0:T(8,128)(2,1)S(1)} %fetch_weights.1.weight_ref), custom_call_target="tpu_custom_call" | custom-call | tf_op jit(solution)/shard_map/products/pallas_call | solution.py:688
  (47 shorter events, 6.7 us)
Async XLA Ops:
  0.0 10.9 %copy-start.5 = (s32[160]{0:T(256)S(1)}, s32[160]{0:T(256)}, u32[]{:S(2)}) copy-start(s32[160]{0:T(256)} %param.16) | copy-start | bytes 1924
  0.0 10.9 %copy-start.6 = (s32[160]{0:T(256)S(1)}, s32[160]{0:T(256)}, u32[]{:S(2)}) copy-start(s32[160]{0:T(256)} %param.14) | copy-start | bytes 1924
  0.0 10.9 %copy-start.7 = (s32[160]{0:T(256)S(1)}, s32[160]{0:T(256)}, u32[]{:S(2)}) copy-start(s32[160]{0:T(256)} %param.12) | copy-start | bytes 1924
  2.4 6.5 %copy-start.9 = (bf16[48,4096]{1,0:T(8,128)(2,1)S(1)}, bf16[48,4096]{1,0:T(8,128)(2,1)}, u32[]{:S(2)}) copy-start(bf16[48,4096]{1,0:T(8,128)(2,1)} %get-tuple-element.33) | copy-start | bytes 1179652
  2.4 8.0 %copy-start.8 = (bf16[64,4096]{1,0:T(8,128)(2,1)S(1)}, bf16[64,4096]{1,0:T(8,128)(2,1)}, u32[]{:S(2)}) copy-start(bf16[64,4096]{1,0:T(8,128)(2,1)} %get-tuple-element.32) | copy-start | bytes 1572868
  2.5 35.7 %all-to-all-start = ((bf16[4,64,2048]{2,1,0:T(8,128)(2,1)}), bf16[4,64,2048]{2,1,0:T(8,128)(2,1)S(1)}, u32[]{:S(2)}, u32[]{:S(2)}) async-start(bf16[4,64,2048]{2,1,0:T(8,128)(2,1)} %get-tuple-element.36), calls=%async_computation | async-start | bytes 2097152 | tf_op jit(solution)/shard_map/all_to_all | solution.py:532
  8.9 12.0 %collective-permute-start.2 = (bf16[48,4096]{1,0:T(8,128)(2,1)S(1)}, bf16[48,4096]{1,0:T(8,128)(2,1)S(1)}, u32[]{:S(2)}, u32[]{:S(2)}) collective-permute-start(bf16[48,4096]{1,0:T(8,128)(2,1)S(1)} %copy-done.9), channel_id=1, source_target_pairs={{0,2},{2,0},{4,6},{6,4},{8,10},{10,8},{12,14},{14,12},{1,3},{3,1},... | collective-permute-start | bytes 1179656 | tf_op jit(solution)/shard_map/ppermute | solution.py:526
  10.4 27.7 %collective-permute-start.1 = (bf16[64,4096]{1,0:T(8,128)(2,1)S(1)}, bf16[64,4096]{1,0:T(8,128)(2,1)S(1)}, u32[]{:S(2)}, u32[]{:S(2)}) collective-permute-start(bf16[64,4096]{1,0:T(8,128)(2,1)S(1)} %copy-done.8), channel_id=1, source_target_pairs={{0,2},{2,0},{4,6},{6,4},{8,10},{10,8},{12,14},{14,12},{1,3},{3,1},... | collective-permute-start | bytes 1572872 | tf_op jit(solution)/shard_map/ppermute | solution.py:526
  11.7 21.2 %copy-start.4 = (s32[3,256]{1,0:T(4,128)S(1)}, s32[3,256]{1,0:T(4,128)}, u32[]{:S(2)}) copy-start(s32[3,256]{1,0:T(4,128)} %select_reduce_fusion.inv_ref) | copy-start | bytes 9220
  21.0 17.1 %collective-permute-start.3 = (bf16[48,4096]{1,0:T(8,128)(2,1)S(1)}, bf16[48,4096]{1,0:T(8,128)(2,1)S(1)}, u32[]{:S(2)}, u32[]{:S(2)}) collective-permute-start(bf16[48,4096]{1,0:T(8,128)(2,1)S(1)} %collective-permute-done.2.a_in_ref), channel_id=1, source_target_pairs={{0,16},{16,0},{1,17},{17,1},{2,18},{18,2},{3,19},{19,3},{4,20},{20... | collective-permute-start | bytes 1179656 | tf_op jit(solution)/shard_map/ppermute | solution.py:591
  22.5 5.0 %collective-permute-start.4 = (f32[64,256]{1,0:T(8,128)}, f32[64,256]{1,0:T(8,128)S(1)}, u32[]{:S(2)}, u32[]{:S(2)}) collective-permute-start(f32[64,256]{1,0:T(8,128)} %get-tuple-element.37), channel_id=1, source_target_pairs={{0,4},{2,6},{4,0},{6,2},{8,12},{10,14},{12,8},{14,10},{1,5},{3,7},... | collective-permute-start | bytes 196616 | tf_op jit(solution)/shard_map/ppermute | solution.py:526
  28.3 9.1 %collective-permute-start.5 = (f32[64,256]{1,0:T(8,128)S(1)}, f32[64,256]{1,0:T(8,128)S(1)}, u32[]{:S(2)}, u32[]{:S(2)}) collective-permute-start(f32[64,256]{1,0:T(8,128)S(1)} %add.24), channel_id=1, source_target_pairs={{0,8},{2,10},{4,12},{6,14},{8,0},{10,2},{12,4},{14,6},{1,9},{3,11}... | collective-permute-start | bytes 196616 | tf_op jit(solution)/shard_map/ppermute | solution.py:526
  32.9 5.2 %collective-permute-start = (s32[3,256]{1,0:T(4,128)S(1)}, s32[3,256]{1,0:T(4,128)S(1)}, u32[]{:S(2)}, u32[]{:S(2)}) collective-permute-start(s32[3,256]{1,0:T(4,128)S(1)} %copy-done.4), channel_id=1, source_target_pairs={{0,2},{2,0},{4,6},{6,4},{8,10},{10,8},{12,14},{14,12},{1,3},{3,1},... | collective-permute-start | bytes 9224 | tf_op jit(solution)/shard_map/ppermute | solution.py:526
  38.1 0.8 copy-start.2
  38.1 1.0 %copy-start.3 = (bf16[48,4096]{1,0:T(8,128)(2,1)}, bf16[48,4096]{1,0:T(8,128)(2,1)S(1)}, u32[]{:S(2)}) copy-start(bf16[48,4096]{1,0:T(8,128)(2,1)S(1)} %collective-permute-done.3.a_other_ref) | copy-start | bytes 1179652
  38.1 1.2 %copy-start = (bf16[4,64,2048]{2,1,0:T(8,128)(2,1)}, bf16[4,64,2048]{2,1,0:T(8,128)(2,1)S(1)}, u32[]{:S(2)}) copy-start(bf16[4,64,2048]{2,1,0:T(8,128)(2,1)S(1)} %all-to-all-done.tok_in_ref) | copy-start | bytes 3145732
  45.7 5.1 %collective-permute-start.6 = (bf16[4,1024,256]{2,1,0:T(8,128)(2,1)}, bf16[4,1024,256]{2,1,0:T(8,128)(2,1)S(1)}, u32[]{:S(2)}, u32[]{:S(2)}) collective-permute-start(bf16[4,1024,256]{2,1,0:T(8,128)(2,1)} %get-tuple-element.46), channel_id=1, source_target_pairs={{0,1},{1,0},{2,3},{3,2},{4,5},{5,4},{6,7},{7,6},{8,9},{9,8},{10,11... | collective-permute-start | bytes 6291464 | tf_op jit(solution)/shard_map/ppermute | solution.py:529
  45.7 19.3 %all-to-all-start.1 = ((bf16[4,64,1024]{2,1,0:T(8,128)(2,1)}), bf16[4,64,1024]{2,1,0:T(8,128)(2,1)S(1)}, u32[]{:S(2)}, u32[]{:S(2)}) async-start(bf16[4,64,1024]{2,1,0:T(8,128)(2,1)} %get-tuple-element.44), calls=%async_computation.1 | async-start | bytes 1048576 | tf_op jit(solution)/shard_map/all_to_all | solution.py:532
  49.2 5.9 %collective-permute-start.7 = (f32[64,256]{1,0:T(8,128)}, f32[64,256]{1,0:T(8,128)S(1)}, u32[]{:S(2)}, u32[]{:S(2)}) collective-permute-start(f32[64,256]{1,0:T(8,128)} %add.25), channel_id=1, source_target_pairs={{0,2},{2,0},{4,6},{6,4},{8,10},{10,8},{12,14},{14,12},{1,3},{3,1},... | collective-permute-start | bytes 196616 | tf_op jit(solution)/shard_map/ppermute | solution.py:526
  50.8 1.2 %copy-start.1 = (bf16[4,64,2048]{2,1,0:T(8,128)(2,1)S(1)}, bf16[4,64,2048]{2,1,0:T(8,128)(2,1)}, u32[]{:S(2)}) copy-start(bf16[4,64,2048]{2,1,0:T(8,128)(2,1)} %copy-done) | copy-start | bytes 3145732
  55.1 12.1 %collective-permute-start.8 = (bf16[64,1024]{1,0:T(8,128)(2,1)S(1)}, bf16[64,1024]{1,0:T(8,128)(2,1)S(1)}, u32[]{:S(2)}, u32[]{:S(2)}) collective-permute-start(bf16[64,1024]{1,0:T(8,128)(2,1)S(1)} %get-tuple-element.50), channel_id=1, source_target_pairs={{0,4},{2,6},{4,0},{6,2},{8,12},{10,14},{12,8},{14,10},{1,5},{3,7},... | collective-permute-start | bytes 393224 | tf_op jit(solution)/shard_map/ppermute | solution.py:526
  57.9 4.1 %collective-permute-start.11 = (f32[64,256]{1,0:T(8,128)S(1)}, f32[64,256]{1,0:T(8,128)S(1)}, u32[]{:S(2)}, u32[]{:S(2)}) collective-permute-start(f32[64,256]{1,0:T(8,128)S(1)} %add.26.pay0_ref), channel_id=1, source_target_pairs={{0,1},{1,0},{2,3},{3,2},{4,5},{5,4},{6,7},{7,6},{8,9},{9,8},{10,11... | collective-permute-start | bytes 196616 | tf_op jit(solution)/shard_map/ppermute | solution.py:529
  58.0 15.4 %collective-permute-start.9 = (bf16[64,1024]{1,0:T(8,128)(2,1)S(1)}, bf16[64,1024]{1,0:T(8,128)(2,1)S(1)}, u32[]{:S(2)}, u32[]{:S(2)}) collective-permute-start(bf16[64,1024]{1,0:T(8,128)(2,1)S(1)} %get-tuple-element.51), channel_id=1, source_target_pairs={{0,8},{2,10},{4,12},{6,14},{8,0},{10,2},{12,4},{14,6},{1,9},{3,11}... | collective-permute-start | bytes 393224 | tf_op jit(solution)/shard_map/ppermute | solution.py:526
  60.4 13.0 %collective-permute-start.10 = (bf16[64,1024]{1,0:T(8,128)(2,1)S(1)}, bf16[64,1024]{1,0:T(8,128)(2,1)S(1)}, u32[]{:S(2)}, u32[]{:S(2)}) collective-permute-start(bf16[64,1024]{1,0:T(8,128)(2,1)S(1)} %get-tuple-element.52), channel_id=1, source_target_pairs={{0,12},{2,14},{4,8},{6,10},{8,4},{10,6},{12,0},{14,2},{1,13},{3,15... | collective-permute-start | bytes 393224 | tf_op jit(solution)/shard_map/ppermute | solution.py:526
  60.5 6.7 %collective-permute-start.12 = (f32[64,256]{1,0:T(8,128)S(1)}, f32[64,256]{1,0:T(8,128)S(1)}, u32[]{:S(2)}, u32[]{:S(2)}) collective-permute-start(f32[64,256]{1,0:T(8,128)S(1)} %add.26.pay0_ref), channel_id=1, source_target_pairs={{0,16},{16,0},{1,17},{17,1},{2,18},{18,2},{3,19},{19,3},{4,20},{20... | collective-permute-start | bytes 196616 | tf_op jit(solution)/shard_map/ppermute | solution.py:650
  62.1 5.2 %collective-permute-start.13 = (f32[64,256]{1,0:T(8,128)S(1)}, f32[64,256]{1,0:T(8,128)S(1)}, u32[]{:S(2)}, u32[]{:S(2)}) collective-permute-start(f32[64,256]{1,0:T(8,128)S(1)} %add.26.pay0_ref), channel_id=1, source_target_pairs={{0,17},{1,16},{16,1},{17,0},{2,19},{3,18},{18,3},{19,2},{4,21},{5,... | collective-permute-start | bytes 196616 | tf_op jit(solution)/shard_map/ppermute | solution.py:651
  76.1 1.3 %collective-permute-start.14 = (f32[8,2048]{1,0:T(8,128)S(1)}, f32[8,2048]{1,0:T(8,128)S(1)}, u32[]{:S(2)}, u32[]{:S(2)}) collective-permute-start(f32[8,2048]{1,0:T(8,128)S(1)} %get-tuple-element.57), channel_id=1, source_target_pairs={{0,1},{1,0},{2,3},{3,2},{4,5},{5,4},{6,7},{7,6},{8,9},{9,8},{10,11... | collective-permute-start | bytes 196616 | tf_op jit(solution)/shard_map/ppermute | solution.py:529
  77.4 5.4 %collective-permute-start.16 = (f32[8,2048]{1,0:T(8,128)S(1)}, f32[8,2048]{1,0:T(8,128)S(1)}, u32[]{:S(2)}, u32[]{:S(2)}) collective-permute-start(f32[8,2048]{1,0:T(8,128)S(1)} %add.27), channel_id=1, source_target_pairs={{0,4},{2,6},{4,0},{6,2},{8,12},{10,14},{12,8},{14,10},{1,5},{3,7},... | collective-permute-start | bytes 196616 | tf_op jit(solution)/shard_map/ppermute | solution.py:526
  80.4 5.2 %collective-permute-start.17 = (f32[8,2048]{1,0:T(8,128)S(1)}, f32[8,2048]{1,0:T(8,128)S(1)}, u32[]{:S(2)}, u32[]{:S(2)}) collective-permute-start(f32[8,2048]{1,0:T(8,128)S(1)} %add.27), channel_id=1, source_target_pairs={{0,6},{2,4},{4,2},{6,0},{8,14},{10,12},{12,10},{14,8},{1,7},{3,5},... | collective-permute-start | bytes 196616 | tf_op jit(solution)/shard_map/ppermute | solution.py:526
  81.4 5.2 %collective-permute-start.15 = (f32[8,2048]{1,0:T(8,128)S(1)}, f32[8,2048]{1,0:T(8,128)S(1)}, u32[]{:S(2)}, u32[]{:S(2)}) collective-permute-start(f32[8,2048]{1,0:T(8,128)S(1)} %add.27), channel_id=1, source_target_pairs={{0,2},{2,0},{4,6},{6,4},{8,10},{10,8},{12,14},{14,12},{1,3},{3,1},... | collective-permute-start | bytes 196616 | tf_op jit(solution)/shard_map/ppermute | solution.py:526
  86.6 5.4 %collective-permute-start.18 = (f32[8,2048]{1,0:T(8,128)S(1)}, f32[8,2048]{1,0:T(8,128)S(1)}, u32[]{:S(2)}, u32[]{:S(2)}) collective-permute-start(f32[8,2048]{1,0:T(8,128)S(1)} %add_add_fusion), channel_id=1, source_target_pairs={{0,8},{2,10},{4,12},{6,14},{8,0},{10,2},{12,4},{14,6},{1,9},{3,11}... | collective-permute-start | bytes 196616 | tf_op jit(solution)/shard_map/ppermute | solution.py:526
  92.0 1.3 %collective-permute-start.19 = (f32[8,2048]{1,0:T(8,128)S(1)}, f32[8,2048]{1,0:T(8,128)S(1)}, u32[]{:S(2)}, u32[]{:S(2)}) collective-permute-start(f32[8,2048]{1,0:T(8,128)S(1)} %add.31.mine_ref), channel_id=1, source_target_pairs={{0,1},{1,0},{2,3},{3,2},{4,5},{5,4},{6,7},{7,6},{8,9},{9,8},{10,11... | collective-permute-start | bytes 196616 | tf_op jit(solution)/shard_map/ppermute | solution.py:529

commit v12 on v11

--- a/solution.py
+++ b/solution.py
@@ -331,6 +331,7 @@
     keep_ref,
     sent_out_ref,
     near_out_ref,
+    tokens_out_ref,
     blocks_ref,
     tiles_ref,
     near_ref,
@@ -369,10 +370,12 @@
         near_ref[pair // 2, pl.ds(row, 32), lane : lane + 128] = piece
 
     assemble_columns(inv_ref, core, tiles_ref, put)
-    near_store = pltpu.make_async_copy(near_ref, near_out_ref, near_sem)
+    near_store = pltpu.make_async_copy(near_ref, near_out_ref, near_sem.at[0])
     near_store.start()
     loads[3].wait()
     shuffle_tokens(side, tok_ref, tokens_ref)
+    tokens_store = pltpu.make_async_copy(tokens_ref, tokens_out_ref, near_sem.at[1])
+    tokens_store.start()
     loads[4].wait()
     stores = []
     for chunk in range(4):
@@ -390,36 +393,34 @@
     for store in stores:
         store.wait()
     near_store.wait()
+    tokens_store.wait()
 
 
 def second_kernel(
     near_in_ref,
     weight_in_ref,
-    tok_in_ref,
+    tokens_in_ref,
     keep_ref,
     out1_ref,
     out2_ref,
     out3_ref,
     near_ref,
     own_ref,
-    tok_ref,
     tokens_ref,
     total_ref,
     in_sem,
 ):
-    owner, unused_quarter, side, core = position()
+    owner, unused_quarter, unused_side, core = position()
     zone = owner // 2
     loads = [
-        pltpu.make_async_copy(tok_in_ref, tok_ref, in_sem.at[0]),
+        pltpu.make_async_copy(tokens_in_ref, tokens_ref, in_sem.at[0]),
         pltpu.make_async_copy(weight_in_ref.at[pl.ds(4 - 4 * core, 4)], own_ref, in_sem.at[1]),
         pltpu.make_async_copy(near_in_ref, near_ref, in_sem.at[2]),
     ]
     for load in loads:
         load.start()
-    loads[0].wait()
-    shuffle_tokens(side, tok_ref, tokens_ref)
-    loads[1].wait()
-    loads[2].wait()
+    for load in loads:
+        load.wait()
     for chunk in range(4):
         total = dot(tokens_ref[0], own_ref[chunk]) + dot(tokens_ref[1], near_ref[chunk])
         cols = slice(256 * chunk, 256 * (chunk + 1))
@@ -595,15 +596,16 @@
         (near_inv, near_b, near_a_other, gathered, payload)
     )
 
-    first_keep, first_sent, near_weights = pl.pallas_call(
+    first_keep, first_sent, near_weights, shuffled_tokens = pl.pallas_call(
         first_kernel,
         out_shape=(
             jax.ShapeDtypeStruct((64, 1024), F32),
             jax.ShapeDtypeStruct((4, 64, 1024), BF),
             jax.ShapeDtypeStruct((4, 1024, 256), BF),
+            jax.ShapeDtypeStruct((2, 256, 1024), BF),
         ),
         in_specs=[SMEM, ANY, ANY, ANY, HBM, ANY],
-        out_specs=(VMEM, HBM, HBM),
+        out_specs=(VMEM, HBM, HBM, HBM),
         scratch_shapes=[
             pltpu.VMEM((160, 4096), BF),
             pltpu.VMEM((32 * STRIDE, 128), F32),
@@ -614,10 +616,10 @@
             pltpu.VMEM((4, 64, 1024), BF),
             pltpu.VMEM((256, 256), F32),
             pltpu.SemaphoreType.DMA((5,)),
-            pltpu.SemaphoreType.DMA,
+            pltpu.SemaphoreType.DMA((2,)),
             pltpu.SemaphoreType.DMA((4,)),
         ],
-        compiler_params=params(53),
+        compiler_params=params(46),
         name="first_partial",
     )(near_inv, near_a, near_b, near_a_other, weights, gathered)
     first_back = zone_exchange(first_sent)
@@ -631,14 +633,13 @@
         scratch_shapes=[
             pltpu.VMEM((4, 1024, 256), BF),
             pltpu.VMEM((4, 1024, 256), BF),
-            pltpu.VMEM((4, 64, 2048), BF),
             pltpu.VMEM((2, 256, 1024), BF),
             pltpu.VMEM((256, 256), F32),
             pltpu.SemaphoreType.DMA((3,)),
         ],
-        compiler_params=params(50),
+        compiler_params=params(56),
         name="second_partial",
-    )(core_flip(near_weights), weights, gathered)
+    )(core_flip(near_weights), weights, shuffled_tokens)
     second_back = [owner_flip(second_sent[flip - 1], 2 * flip) for flip in (1, 2, 3)]
 
     across = owner_flip(payload, 1)

time: 95.9 us -> 94.1 us (0.981)
  other arithmetic: 3.12 us -> 1.65 us
  local copies, waits for them, and re-layouts: 2.49 us -> 1.05 us
  Pallas kernels: 26.1 us -> 27.1 us
    pallas_call x1, Pallas kernels: 3.07 us -> 4.78 us  [pair_split(): pl.pallas_call(second_kernel, out_shape=(jax.ShapeDtypeStruct((64, 1024),...]
    unnamed x20 -> x16, local copies, waits for them, and re-layouts: 2.49 us -> 1.05 us
  transfers between devices with their start and end apart: 22 -> 22, of which waited for: 11 -> 11; matrix products, arithmetic and copies ran while one was open for 3% -> 2% of each run, Pallas kernels for 13% -> 15%
where the time goes in v12:
time: 94.1 us; the launch traced here: 93.7 us
  starting transfers between devices  35.4 us (38%)
  waiting for transfers between devices  28.3 us (30%)
  Pallas kernels  27.1 us (29%)
  other arithmetic  1.65 us (2%)
  local copies, waits for them, and re-layouts  1.05 us (1%)
    ppermute x13, waiting for transfers between devices, owner_flip(): return lax.ppermute(value, 'fsdp', [(i, i ^ bits) for i in range(8)])  22.5 us
    ppermute x13, starting transfers between devices, owner_flip(): return lax.ppermute(value, 'fsdp', [(i, i ^ bits) for i in range(8)])  22.2 us
    all_to_all x2, starting transfers between devices, zone_exchange(): lax.all_to_all(value, 'fsdp', split_axis=0, concat_axis=0, tiled=True, ax...  9.93 us
    pallas_call x1, Pallas kernels, pair_split(): pl.pallas_call(own_kernel, out_shape=(jax.ShapeDtypeStruct((8, 1024, 256)...  7.55 us
    pallas_call x1, Pallas kernels, pair_split(): pl.pallas_call(first_kernel, out_shape=(jax.ShapeDtypeStruct((64, 1024),...  5.46 us
    pallas_call x1, Pallas kernels, pair_split(): pl.pallas_call(second_kernel, out_shape=(jax.ShapeDtypeStruct((64, 1024),...  4.78 us
    all_to_all x2, waiting for transfers between devices, zone_exchange(): lax.all_to_all(value, 'fsdp', split_axis=0, concat_axis=0, tiled=True, ax...  3.3 us
    pallas_call x1, Pallas kernels, pair_split(): pl.pallas_call(middle_kernel, out_shape=(jax.ShapeDtypeStruct((8, 2048),...  2.61 us
  transfers between devices with their start and end apart: 22, of which 11 were waited for; matrix products, arithmetic and copies ran while one was open for 2% of the time, Pallas kernels for 15%

profile of v12, /device:TPU:0, one launch (start us, length us, event | category | flops | bytes accessed | tf_op | source)
XLA Modules:
  0.0 93.7 jit_solution(15904649073423055007)
XLA Ops:
  0.0 2.4 %head.1 = (bf16[4,64,2048]{2,1,0:T(8,128)(2,1)}, bf16[48,4096]{1,0:T(8,128)(2,1)}, bf16[64,4096]{1,0:T(8,128)(2,1)}) custom-call(bf16[64,8192]{1,0:T(8,128)(2,1)} %tok_in_ref.1, bf16[160,4096]{1,0:T(8,128)(2,1)} %gate_ref.3, bf16[160,4096]{1,0:T(8,128)(2,1)} %up_ref.3), custom_call_target="tpu_custom_call" | custom-call | tf_op jit(solution)/shard_map/head/pallas_call | solution.py:542
  2.5 6.5 %all-to-all-start = ((bf16[4,64,2048]{2,1,0:T(8,128)(2,1)}), bf16[4,64,2048]{2,1,0:T(8,128)(2,1)S(1)}, u32[]{:S(2)}, u32[]{:S(2)}) async-start(bf16[4,64,2048]{2,1,0:T(8,128)(2,1)} %get-tuple-element.37), calls=%async_computation | async-start | bytes 2097152 | tf_op jit(solution)/shard_map/all_to_all | solution.py:533
  8.9 1.5 %collective-permute-start.2 = (bf16[48,4096]{1,0:T(8,128)(2,1)S(1)}, bf16[48,4096]{1,0:T(8,128)(2,1)S(1)}, u32[]{:S(2)}, u32[]{:S(2)}) collective-permute-start(bf16[48,4096]{1,0:T(8,128)(2,1)S(1)} %copy-done.7), channel_id=1, source_target_pairs={{0,2},{2,0},{4,6},{6,4},{8,10},{10,8},{12,14},{14,12},{1,3},{3,1},... | collective-permute-start | bytes 1179656 | tf_op jit(solution)/shard_map/ppermute | solution.py:527
  11.7 7.5 %own_blocks.1 = (bf16[8,1024,256]{2,1,0:T(8,128)(2,1)}, f32[64,256]{1,0:T(8,128)}) custom-call(s32[3,256]{1,0:T(4,128)} %select_reduce_fusion.inv_ref, bf16[160,4096]{1,0:T(8,128)(2,1)} %gate_ref.3, bf16[160,4096]{1,0:T(8,128)(2,1)} %up_ref.3, bf16[160,4096]{1,0:T(8,128)(2,1)} %down_ref.1, bf16[32,1024]{1,0:T(8,128)(2,1)} %sketch_ref.1, ...), custom_call_target="tpu_custom_call" | custom-call | tf_op jit(solution)/shard_map/own_blocks/pallas_call | solution.py:569
  19.3 1.7 %collective-permute-done.2.a_in_ref = bf16[48,4096]{1,0:T(8,128)(2,1)S(1)} collective-permute-done((bf16[48,4096]{1,0:T(8,128)(2,1)S(1)}, bf16[48,4096]{1,0:T(8,128)(2,1)S(1)}, u32[]{:S(2)}, u32[]{:S(2)}) %collective-permute-start.2) | collective-permute-done | bytes 393248 | tf_op jit(solution)/shard_map/ppermute | solution.py:527
  21.0 1.5 %collective-permute-start.3 = (bf16[48,4096]{1,0:T(8,128)(2,1)S(1)}, bf16[48,4096]{1,0:T(8,128)(2,1)S(1)}, u32[]{:S(2)}, u32[]{:S(2)}) collective-permute-start(bf16[48,4096]{1,0:T(8,128)(2,1)S(1)} %collective-permute-done.2.a_in_ref), channel_id=1, source_target_pairs={{0,16},{16,0},{1,17},{17,1},{2,18},{18,2},{3,19},{19,3},{4,20},{20... | collective-permute-start | bytes 1179656 | tf_op jit(solution)/shard_map/ppermute | solution.py:592
  22.5 2.0 %collective-permute-start.4 = (f32[64,256]{1,0:T(8,128)}, f32[64,256]{1,0:T(8,128)S(1)}, u32[]{:S(2)}, u32[]{:S(2)}) collective-permute-start(f32[64,256]{1,0:T(8,128)} %get-tuple-element.38), channel_id=1, source_target_pairs={{0,4},{2,6},{4,0},{6,2},{8,12},{10,14},{12,8},{14,10},{1,5},{3,7},... | collective-permute-start | bytes 196616 | tf_op jit(solution)/shard_map/ppermute | solution.py:527
  24.5 3.0 %collective-permute-done.4 = f32[64,256]{1,0:T(8,128)S(1)} collective-permute-done((f32[64,256]{1,0:T(8,128)}, f32[64,256]{1,0:T(8,128)S(1)}, u32[]{:S(2)}, u32[]{:S(2)}) %collective-permute-start.4) | collective-permute-done | bytes 65568 | tf_op jit(solution)/shard_map/ppermute | solution.py:527
  28.3 4.6 %collective-permute-start.5 = (f32[64,256]{1,0:T(8,128)S(1)}, f32[64,256]{1,0:T(8,128)S(1)}, u32[]{:S(2)}, u32[]{:S(2)}) collective-permute-start(f32[64,256]{1,0:T(8,128)S(1)} %add.24), channel_id=1, source_target_pairs={{0,8},{2,10},{4,12},{6,14},{8,0},{10,2},{12,4},{14,6},{1,9},{3,11}... | collective-permute-start | bytes 196616 | tf_op jit(solution)/shard_map/ppermute | solution.py:527
  32.9 1.5 %collective-permute-start = (s32[3,256]{1,0:T(4,128)S(1)}, s32[3,256]{1,0:T(4,128)S(1)}, u32[]{:S(2)}, u32[]{:S(2)}) collective-permute-start(s32[3,256]{1,0:T(4,128)S(1)} %copy-done.2), channel_id=1, source_target_pairs={{0,2},{2,0},{4,6},{6,4},{8,10},{10,8},{12,14},{14,12},{1,3},{3,1},... | collective-permute-start | bytes 9224 | tf_op jit(solution)/shard_map/ppermute | solution.py:527
  34.4 3.1 %collective-permute-done.5 = f32[64,256]{1,0:T(8,128)S(1)} collective-permute-done((f32[64,256]{1,0:T(8,128)S(1)}, f32[64,256]{1,0:T(8,128)S(1)}, u32[]{:S(2)}, u32[]{:S(2)}) %collective-permute-start.5) | collective-permute-done | bytes 65568 | tf_op jit(solution)/shard_map/ppermute | solution.py:527
  37.5 5.5 %first_partial.1 = (f32[64,1024]{1,0:T(8,128)S(1)}, bf16[4,64,1024]{2,1,0:T(8,128)(2,1)}, bf16[4,1024,256]{2,1,0:T(8,128)(2,1)}, bf16[2,256,1024]{2,1,0:T(8,128)(2,1)S(1)}) custom-call(s32[3,256]{1,0:T(4,128)S(1)} %collective-permute-done.inv_ref, bf16[48,4096]{1,0:T(8,128)(2,1)S(1)} %collective-permute-done.2.a_in_ref, ...), custom_call_target="tpu_custom_call" | custom-call | tf_op jit(solution)/shard_map/first_partial/pallas_call | solution.py:599
  43.0 1.0 %copy-done = bf16[2,256,1024]{2,1,0:T(8,128)(2,1)} copy-done((bf16[2,256,1024]{2,1,0:T(8,128)(2,1)}, bf16[2,256,1024]{2,1,0:T(8,128)(2,1)S(1)}, u32[]{:S(2)}) %copy-start) | copy-done | bytes 1048600
  44.0 3.5 %all-to-all-start.1 = ((bf16[4,64,1024]{2,1,0:T(8,128)(2,1)}), bf16[4,64,1024]{2,1,0:T(8,128)(2,1)S(1)}, u32[]{:S(2)}, u32[]{:S(2)}) async-start(bf16[4,64,1024]{2,1,0:T(8,128)(2,1)} %get-tuple-element.45), calls=%async_computation.1 | async-start | bytes 1048576 | tf_op jit(solution)/shard_map/all_to_all | solution.py:533
  47.5 1.6 %collective-permute-start.7 = (f32[64,256]{1,0:T(8,128)S(1)}, f32[64,256]{1,0:T(8,128)S(1)}, u32[]{:S(2)}, u32[]{:S(2)}) collective-permute-start(f32[64,256]{1,0:T(8,128)S(1)} %add.25), channel_id=1, source_target_pairs={{0,2},{2,0},{4,6},{6,4},{8,10},{10,8},{12,14},{14,12},{1,3},{3,1},... | collective-permute-start | bytes 196616 | tf_op jit(solution)/shard_map/ppermute | solution.py:527
  49.0 4.8 %second_partial.1 = (f32[64,1024]{1,0:T(8,128)}, bf16[64,1024]{1,0:T(8,128)(2,1)}, bf16[64,1024]{1,0:T(8,128)(2,1)}, bf16[64,1024]{1,0:T(8,128)(2,1)}) custom-call(bf16[4,1024,256]{2,1,0:T(8,128)(2,1)} %collective-permute-done.6.near_in_ref, bf16[8,1024,256]{2,1,0:T(8,128)(2,1)} %get-tuple-element.56.weight_in_ref, bf16[2,256,1024]{2,1,0:T(8,128)(2,1)} %copy-done), custom_call_target="tpu_custom_call" | custom-call | tf_op jit(solution)/shard_map/second_partial/pallas_call | solution.py:627
  53.8 2.0 %collective-permute-start.8 = (bf16[64,1024]{1,0:T(8,128)(2,1)}, bf16[64,1024]{1,0:T(8,128)(2,1)S(1)}, u32[]{:S(2)}, u32[]{:S(2)}) collective-permute-start(bf16[64,1024]{1,0:T(8,128)(2,1)} %get-tuple-element.52), channel_id=1, source_target_pairs={{0,4},{2,6},{4,0},{6,2},{8,12},{10,14},{12,8},{14,10},{1,5},{3,7},... | collective-permute-start | bytes 393224 | tf_op jit(solution)/shard_map/ppermute | solution.py:527
  55.9 2.4 %collective-permute-start.9 = (bf16[64,1024]{1,0:T(8,128)(2,1)}, bf16[64,1024]{1,0:T(8,128)(2,1)S(1)}, u32[]{:S(2)}, u32[]{:S(2)}) collective-permute-start(bf16[64,1024]{1,0:T(8,128)(2,1)} %get-tuple-element.53), channel_id=1, source_target_pairs={{0,8},{2,10},{4,12},{6,14},{8,0},{10,2},{12,4},{14,6},{1,9},{3,11}... | collective-permute-start | bytes 393224 | tf_op jit(solution)/shard_map/ppermute | solution.py:527
  58.5 1.5 %collective-permute-start.12 = (f32[64,256]{1,0:T(8,128)S(1)}, f32[64,256]{1,0:T(8,128)S(1)}, u32[]{:S(2)}, u32[]{:S(2)}) collective-permute-start(f32[64,256]{1,0:T(8,128)S(1)} %add.26.pay0_ref), channel_id=1, source_target_pairs={{0,16},{16,0},{1,17},{17,1},{2,18},{18,2},{3,19},{19,3},{4,20},{20... | collective-permute-start | bytes 196616 | tf_op jit(solution)/shard_map/ppermute | solution.py:651
  60.0 3.3 %all-to-all-done.1.first_ref = bf16[4,64,1024]{2,1,0:T(8,128)(2,1)S(1)} async-done(((bf16[4,64,1024]{2,1,0:T(8,128)(2,1)}), bf16[4,64,1024]{2,1,0:T(8,128)(2,1)S(1)}, u32[]{:S(2)}, u32[]{:S(2)}) %all-to-all-start.1) | async-done | bytes 524320 | tf_op jit(solution)/shard_map/all_to_all | solution.py:533
  63.3 2.2 %fetch_weights.1.weight_ref = bf16[8,1024,256]{2,1,0:T(8,128)(2,1)S(1)} custom-call(bf16[8,1024,256]{2,1,0:T(8,128)(2,1)} %get-tuple-element.56.weight_in_ref), custom_call_target="tpu_custom_call" | custom-call | tf_op jit(solution)/shard_map/fetch_weights/pallas_call | solution.py:656
  65.5 6.2 %collective-permute-done.9.second2_ref = bf16[64,1024]{1,0:T(8,128)(2,1)S(1)} collective-permute-done((bf16[64,1024]{1,0:T(8,128)(2,1)}, bf16[64,1024]{1,0:T(8,128)(2,1)S(1)}, u32[]{:S(2)}, u32[]{:S(2)}) %collective-permute-start.9) | collective-permute-done | bytes 131104 | tf_op jit(solution)/shard_map/ppermute | solution.py:527
  71.7 2.6 %token_sums.1 = (f32[8,2048]{1,0:T(8,128)S(1)}, f32[8,2048]{1,0:T(8,128)S(1)}) custom-call(f32[64,1024]{1,0:T(8,128)S(1)} %get-tuple-element.44.first_keep_ref, bf16[4,64,1024]{2,1,0:T(8,128)(2,1)S(1)} %all-to-all-done.1.first_ref, f32[64,1024]{1,0:T(8,128)S(1)} %copy-done.1, bf16[64,1024]{1,0:T(8,128)(2,1)S(1)} %collective-permute-done.8.second1_ref, ...), custom_call_target="tpu_custom_call" | custom-call | tf_op jit(solution)/shard_map/token_sums/pallas_call | solution.py:667
  74.4 1.2 %collective-permute-done.14 = f32[8,2048]{1,0:T(8,128)S(1)} collective-permute-done((f32[8,2048]{1,0:T(8,128)S(1)}, f32[8,2048]{1,0:T(8,128)S(1)}, u32[]{:S(2)}, u32[]{:S(2)}) %collective-permute-start.14) | collective-permute-done | bytes 65568 | tf_op jit(solution)/shard_map/ppermute | solution.py:530
  75.7 3.0 %collective-permute-start.16 = (f32[8,2048]{1,0:T(8,128)S(1)}, f32[8,2048]{1,0:T(8,128)S(1)}, u32[]{:S(2)}, u32[]{:S(2)}) collective-permute-start(f32[8,2048]{1,0:T(8,128)S(1)} %add.27), channel_id=1, source_target_pairs={{0,4},{2,6},{4,0},{6,2},{8,12},{10,14},{12,8},{14,10},{1,5},{3,7},... | collective-permute-start | bytes 196616 | tf_op jit(solution)/shard_map/ppermute | solution.py:527
  78.7 1.0 %collective-permute-start.17 = (f32[8,2048]{1,0:T(8,128)S(1)}, f32[8,2048]{1,0:T(8,128)S(1)}, u32[]{:S(2)}, u32[]{:S(2)}) collective-permute-start(f32[8,2048]{1,0:T(8,128)S(1)} %add.27), channel_id=1, source_target_pairs={{0,6},{2,4},{4,2},{6,0},{8,14},{10,12},{12,10},{14,8},{1,7},{3,5},... | collective-permute-start | bytes 196616 | tf_op jit(solution)/shard_map/ppermute | solution.py:527
  81.1 2.8 %collective-permute-done.17 = f32[8,2048]{1,0:T(8,128)S(1)} collective-permute-done((f32[8,2048]{1,0:T(8,128)S(1)}, f32[8,2048]{1,0:T(8,128)S(1)}, u32[]{:S(2)}, u32[]{:S(2)}) %collective-permute-start.17) | collective-permute-done | bytes 65568 | tf_op jit(solution)/shard_map/ppermute | solution.py:527
  83.9 1.0 %collective-permute-done.15 = f32[8,2048]{1,0:T(8,128)S(1)} collective-permute-done((f32[8,2048]{1,0:T(8,128)S(1)}, f32[8,2048]{1,0:T(8,128)S(1)}, u32[]{:S(2)}, u32[]{:S(2)}) %collective-permute-start.15) | collective-permute-done | bytes 65568 | tf_op jit(solution)/shard_map/ppermute | solution.py:527
  84.9 1.5 %collective-permute-start.18 = (f32[8,2048]{1,0:T(8,128)S(1)}, f32[8,2048]{1,0:T(8,128)S(1)}, u32[]{:S(2)}, u32[]{:S(2)}) collective-permute-start(f32[8,2048]{1,0:T(8,128)S(1)} %add_add_fusion), channel_id=1, source_target_pairs={{0,8},{2,10},{4,12},{6,14},{8,0},{10,2},{12,4},{14,6},{1,9},{3,11}... | collective-permute-start | bytes 196616 | tf_op jit(solution)/shard_map/ppermute | solution.py:527
  86.4 3.9 %collective-permute-done.18 = f32[8,2048]{1,0:T(8,128)S(1)} collective-permute-done((f32[8,2048]{1,0:T(8,128)S(1)}, f32[8,2048]{1,0:T(8,128)S(1)}, u32[]{:S(2)}, u32[]{:S(2)}) %collective-permute-start.18) | collective-permute-done | bytes 65568 | tf_op jit(solution)/shard_map/ppermute | solution.py:527
  90.4 1.2 %collective-permute-done.19.theirs_ref = f32[8,2048]{1,0:T(8,128)S(1)} collective-permute-done((f32[8,2048]{1,0:T(8,128)S(1)}, f32[8,2048]{1,0:T(8,128)S(1)}, u32[]{:S(2)}, u32[]{:S(2)}) %collective-permute-start.19) | collective-permute-done | bytes 65568 | tf_op jit(solution)/shard_map/ppermute | solution.py:530
  91.6 2.0 %products.1 = f32[16,1024]{1,0:T(8,128)} custom-call(f32[8,2048]{1,0:T(8,128)S(1)} %add.31.mine_ref, f32[8,2048]{1,0:T(8,128)S(1)} %collective-permute-done.19.theirs_ref, bf16[8,1024,256]{2,1,0:T(8,128)(2,1)S(1)} %fetch_weights.1.weight_ref), custom_call_target="tpu_custom_call" | custom-call | tf_op jit(solution)/shard_map/products/pallas_call | solution.py:689
  (43 shorter events, 4.0 us)
Async XLA Ops:
  0.0 10.9 %copy-start.3 = (s32[160]{0:T(256)S(1)}, s32[160]{0:T(256)}, u32[]{:S(2)}) copy-start(s32[160]{0:T(256)} %param.16) | copy-start | bytes 1924
  0.0 10.9 %copy-start.4 = (s32[160]{0:T(256)S(1)}, s32[160]{0:T(256)}, u32[]{:S(2)}) copy-start(s32[160]{0:T(256)} %param.14) | copy-start | bytes 1924
  0.0 10.9 %copy-start.5 = (s32[160]{0:T(256)S(1)}, s32[160]{0:T(256)}, u32[]{:S(2)}) copy-start(s32[160]{0:T(256)} %param.12) | copy-start | bytes 1924
  2.4 6.5 %copy-start.7 = (bf16[48,4096]{1,0:T(8,128)(2,1)S(1)}, bf16[48,4096]{1,0:T(8,128)(2,1)}, u32[]{:S(2)}) copy-start(bf16[48,4096]{1,0:T(8,128)(2,1)} %get-tuple-element.34) | copy-start | bytes 1179652
  2.4 8.0 %copy-start.6 = (bf16[64,4096]{1,0:T(8,128)(2,1)S(1)}, bf16[64,4096]{1,0:T(8,128)(2,1)}, u32[]{:S(2)}) copy-start(bf16[64,4096]{1,0:T(8,128)(2,1)} %get-tuple-element.33) | copy-start | bytes 1572868
  2.5 35.0 %all-to-all-start = ((bf16[4,64,2048]{2,1,0:T(8,128)(2,1)}), bf16[4,64,2048]{2,1,0:T(8,128)(2,1)S(1)}, u32[]{:S(2)}, u32[]{:S(2)}) async-start(bf16[4,64,2048]{2,1,0:T(8,128)(2,1)} %get-tuple-element.37), calls=%async_computation | async-start | bytes 2097152 | tf_op jit(solution)/shard_map/all_to_all | solution.py:533
  8.9 12.0 %collective-permute-start.2 = (bf16[48,4096]{1,0:T(8,128)(2,1)S(1)}, bf16[48,4096]{1,0:T(8,128)(2,1)S(1)}, u32[]{:S(2)}, u32[]{:S(2)}) collective-permute-start(bf16[48,4096]{1,0:T(8,128)(2,1)S(1)} %copy-done.7), channel_id=1, source_target_pairs={{0,2},{2,0},{4,6},{6,4},{8,10},{10,8},{12,14},{14,12},{1,3},{3,1},... | collective-permute-start | bytes 1179656 | tf_op jit(solution)/shard_map/ppermute | solution.py:527
  10.4 27.1 %collective-permute-start.1 = (bf16[64,4096]{1,0:T(8,128)(2,1)S(1)}, bf16[64,4096]{1,0:T(8,128)(2,1)S(1)}, u32[]{:S(2)}, u32[]{:S(2)}) collective-permute-start(bf16[64,4096]{1,0:T(8,128)(2,1)S(1)} %copy-done.6), channel_id=1, source_target_pairs={{0,2},{2,0},{4,6},{6,4},{8,10},{10,8},{12,14},{14,12},{1,3},{3,1},... | collective-permute-start | bytes 1572872 | tf_op jit(solution)/shard_map/ppermute | solution.py:527
  11.7 21.2 %copy-start.2 = (s32[3,256]{1,0:T(4,128)S(1)}, s32[3,256]{1,0:T(4,128)}, u32[]{:S(2)}) copy-start(s32[3,256]{1,0:T(4,128)} %select_reduce_fusion.inv_ref) | copy-start | bytes 9220
  21.0 16.5 %collective-permute-start.3 = (bf16[48,4096]{1,0:T(8,128)(2,1)S(1)}, bf16[48,4096]{1,0:T(8,128)(2,1)S(1)}, u32[]{:S(2)}, u32[]{:S(2)}) collective-permute-start(bf16[48,4096]{1,0:T(8,128)(2,1)S(1)} %collective-permute-done.2.a_in_ref), channel_id=1, source_target_pairs={{0,16},{16,0},{1,17},{17,1},{2,18},{18,2},{3,19},{19,3},{4,20},{20... | collective-permute-start | bytes 1179656 | tf_op jit(solution)/shard_map/ppermute | solution.py:592
  22.5 5.0 %collective-permute-start.4 = (f32[64,256]{1,0:T(8,128)}, f32[64,256]{1,0:T(8,128)S(1)}, u32[]{:S(2)}, u32[]{:S(2)}) collective-permute-start(f32[64,256]{1,0:T(8,128)} %get-tuple-element.38), channel_id=1, source_target_pairs={{0,4},{2,6},{4,0},{6,2},{8,12},{10,14},{12,8},{14,10},{1,5},{3,7},... | collective-permute-start | bytes 196616 | tf_op jit(solution)/shard_map/ppermute | solution.py:527
  28.3 9.1 %collective-permute-start.5 = (f32[64,256]{1,0:T(8,128)S(1)}, f32[64,256]{1,0:T(8,128)S(1)}, u32[]{:S(2)}, u32[]{:S(2)}) collective-permute-start(f32[64,256]{1,0:T(8,128)S(1)} %add.24), channel_id=1, source_target_pairs={{0,8},{2,10},{4,12},{6,14},{8,0},{10,2},{12,4},{14,6},{1,9},{3,11}... | collective-permute-start | bytes 196616 | tf_op jit(solution)/shard_map/ppermute | solution.py:527
  32.9 4.6 %collective-permute-start = (s32[3,256]{1,0:T(4,128)S(1)}, s32[3,256]{1,0:T(4,128)S(1)}, u32[]{:S(2)}, u32[]{:S(2)}) collective-permute-start(s32[3,256]{1,0:T(4,128)S(1)} %copy-done.2), channel_id=1, source_target_pairs={{0,2},{2,0},{4,6},{6,4},{8,10},{10,8},{12,14},{14,12},{1,3},{3,1},... | collective-permute-start | bytes 9224 | tf_op jit(solution)/shard_map/ppermute | solution.py:527
  43.0 1.0 %copy-start = (bf16[2,256,1024]{2,1,0:T(8,128)(2,1)}, bf16[2,256,1024]{2,1,0:T(8,128)(2,1)S(1)}, u32[]{:S(2)}) copy-start(bf16[2,256,1024]{2,1,0:T(8,128)(2,1)S(1)} %get-tuple-element.48.tokens_in_ref) | copy-start | bytes 3145732
  44.0 5.0 %collective-permute-start.6 = (bf16[4,1024,256]{2,1,0:T(8,128)(2,1)}, bf16[4,1024,256]{2,1,0:T(8,128)(2,1)}, u32[]{:S(2)}, u32[]{:S(2)}) collective-permute-start(bf16[4,1024,256]{2,1,0:T(8,128)(2,1)} %get-tuple-element.47), channel_id=1, source_target_pairs={{0,1},{1,0},{2,3},{3,2},{4,5},{5,4},{6,7},{7,6},{8,9},{9,8},{10,11... | collective-permute-start | bytes 6291464 | tf_op jit(solution)/shard_map/ppermute | solution.py:530
  44.0 19.3 %all-to-all-start.1 = ((bf16[4,64,1024]{2,1,0:T(8,128)(2,1)}), bf16[4,64,1024]{2,1,0:T(8,128)(2,1)S(1)}, u32[]{:S(2)}, u32[]{:S(2)}) async-start(bf16[4,64,1024]{2,1,0:T(8,128)(2,1)} %get-tuple-element.45), calls=%async_computation.1 | async-start | bytes 1048576 | tf_op jit(solution)/shard_map/all_to_all | solution.py:533
  47.5 6.3 %collective-permute-start.7 = (f32[64,256]{1,0:T(8,128)S(1)}, f32[64,256]{1,0:T(8,128)S(1)}, u32[]{:S(2)}, u32[]{:S(2)}) collective-permute-start(f32[64,256]{1,0:T(8,128)S(1)} %add.25), channel_id=1, source_target_pairs={{0,2},{2,0},{4,6},{6,4},{8,10},{10,8},{12,14},{14,12},{1,3},{3,1},... | collective-permute-start | bytes 196616 | tf_op jit(solution)/shard_map/ppermute | solution.py:527
  53.8 11.7 %collective-permute-start.8 = (bf16[64,1024]{1,0:T(8,128)(2,1)}, bf16[64,1024]{1,0:T(8,128)(2,1)S(1)}, u32[]{:S(2)}, u32[]{:S(2)}) collective-permute-start(bf16[64,1024]{1,0:T(8,128)(2,1)} %get-tuple-element.52), channel_id=1, source_target_pairs={{0,4},{2,6},{4,0},{6,2},{8,12},{10,14},{12,8},{14,10},{1,5},{3,7},... | collective-permute-start | bytes 393224 | tf_op jit(solution)/shard_map/ppermute | solution.py:527
  55.8 4.1 %collective-permute-start.11 = (f32[64,256]{1,0:T(8,128)S(1)}, f32[64,256]{1,0:T(8,128)S(1)}, u32[]{:S(2)}, u32[]{:S(2)}) collective-permute-start(f32[64,256]{1,0:T(8,128)S(1)} %add.26.pay0_ref), channel_id=1, source_target_pairs={{0,1},{1,0},{2,3},{3,2},{4,5},{5,4},{6,7},{7,6},{8,9},{9,8},{10,11... | collective-permute-start | bytes 196616 | tf_op jit(solution)/shard_map/ppermute | solution.py:530
  55.9 15.8 %collective-permute-start.9 = (bf16[64,1024]{1,0:T(8,128)(2,1)}, bf16[64,1024]{1,0:T(8,128)(2,1)S(1)}, u32[]{:S(2)}, u32[]{:S(2)}) collective-permute-start(bf16[64,1024]{1,0:T(8,128)(2,1)} %get-tuple-element.53), channel_id=1, source_target_pairs={{0,8},{2,10},{4,12},{6,14},{8,0},{10,2},{12,4},{14,6},{1,9},{3,11}... | collective-permute-start | bytes 393224 | tf_op jit(solution)/shard_map/ppermute | solution.py:527
  58.3 13.4 %copy-start.1 = (f32[64,1024]{1,0:T(8,128)S(1)}, f32[64,1024]{1,0:T(8,128)}, u32[]{:S(2)}) copy-start(f32[64,1024]{1,0:T(8,128)} %get-tuple-element.51.second_keep_ref) | copy-start | bytes 786436
  58.3 13.4 %collective-permute-start.10 = (bf16[64,1024]{1,0:T(8,128)(2,1)}, bf16[64,1024]{1,0:T(8,128)(2,1)S(1)}, u32[]{:S(2)}, u32[]{:S(2)}) collective-permute-start(bf16[64,1024]{1,0:T(8,128)(2,1)} %get-tuple-element.54), channel_id=1, source_target_pairs={{0,12},{2,14},{4,8},{6,10},{8,4},{10,6},{12,0},{14,2},{1,13},{3,15... | collective-permute-start | bytes 393224 | tf_op jit(solution)/shard_map/ppermute | solution.py:527
  58.5 7.0 %collective-permute-start.12 = (f32[64,256]{1,0:T(8,128)S(1)}, f32[64,256]{1,0:T(8,128)S(1)}, u32[]{:S(2)}, u32[]{:S(2)}) collective-permute-start(f32[64,256]{1,0:T(8,128)S(1)} %add.26.pay0_ref), channel_id=1, source_target_pairs={{0,16},{16,0},{1,17},{17,1},{2,18},{18,2},{3,19},{19,3},{4,20},{20... | collective-permute-start | bytes 196616 | tf_op jit(solution)/shard_map/ppermute | solution.py:651
  60.0 5.5 %collective-permute-start.13 = (f32[64,256]{1,0:T(8,128)S(1)}, f32[64,256]{1,0:T(8,128)S(1)}, u32[]{:S(2)}, u32[]{:S(2)}) collective-permute-start(f32[64,256]{1,0:T(8,128)S(1)} %add.26.pay0_ref), channel_id=1, source_target_pairs={{0,17},{1,16},{16,1},{17,0},{2,19},{3,18},{18,3},{19,2},{4,21},{5,... | collective-permute-start | bytes 196616 | tf_op jit(solution)/shard_map/ppermute | solution.py:652
  74.3 1.3 %collective-permute-start.14 = (f32[8,2048]{1,0:T(8,128)S(1)}, f32[8,2048]{1,0:T(8,128)S(1)}, u32[]{:S(2)}, u32[]{:S(2)}) collective-permute-start(f32[8,2048]{1,0:T(8,128)S(1)} %get-tuple-element.59), channel_id=1, source_target_pairs={{0,1},{1,0},{2,3},{3,2},{4,5},{5,4},{6,7},{7,6},{8,9},{9,8},{10,11... | collective-permute-start | bytes 196616 | tf_op jit(solution)/shard_map/ppermute | solution.py:530
  75.7 5.5 %collective-permute-start.16 = (f32[8,2048]{1,0:T(8,128)S(1)}, f32[8,2048]{1,0:T(8,128)S(1)}, u32[]{:S(2)}, u32[]{:S(2)}) collective-permute-start(f32[8,2048]{1,0:T(8,128)S(1)} %add.27), channel_id=1, source_target_pairs={{0,4},{2,6},{4,0},{6,2},{8,12},{10,14},{12,8},{14,10},{1,5},{3,7},... | collective-permute-start | bytes 196616 | tf_op jit(solution)/shard_map/ppermute | solution.py:527
  78.7 5.2 %collective-permute-start.17 = (f32[8,2048]{1,0:T(8,128)S(1)}, f32[8,2048]{1,0:T(8,128)S(1)}, u32[]{:S(2)}, u32[]{:S(2)}) collective-permute-start(f32[8,2048]{1,0:T(8,128)S(1)} %add.27), channel_id=1, source_target_pairs={{0,6},{2,4},{4,2},{6,0},{8,14},{10,12},{12,10},{14,8},{1,7},{3,5},... | collective-permute-start | bytes 196616 | tf_op jit(solution)/shard_map/ppermute | solution.py:527
  79.7 5.2 %collective-permute-start.15 = (f32[8,2048]{1,0:T(8,128)S(1)}, f32[8,2048]{1,0:T(8,128)S(1)}, u32[]{:S(2)}, u32[]{:S(2)}) collective-permute-start(f32[8,2048]{1,0:T(8,128)S(1)} %add.27), channel_id=1, source_target_pairs={{0,2},{2,0},{4,6},{6,4},{8,10},{10,8},{12,14},{14,12},{1,3},{3,1},... | collective-permute-start | bytes 196616 | tf_op jit(solution)/shard_map/ppermute | solution.py:527
  84.9 5.4 %collective-permute-start.18 = (f32[8,2048]{1,0:T(8,128)S(1)}, f32[8,2048]{1,0:T(8,128)S(1)}, u32[]{:S(2)}, u32[]{:S(2)}) collective-permute-start(f32[8,2048]{1,0:T(8,128)S(1)} %add_add_fusion), channel_id=1, source_target_pairs={{0,8},{2,10},{4,12},{6,14},{8,0},{10,2},{12,4},{14,6},{1,9},{3,11}... | collective-permute-start | bytes 196616 | tf_op jit(solution)/shard_map/ppermute | solution.py:527
  90.3 1.3 %collective-permute-start.19 = (f32[8,2048]{1,0:T(8,128)S(1)}, f32[8,2048]{1,0:T(8,128)S(1)}, u32[]{:S(2)}, u32[]{:S(2)}) collective-permute-start(f32[8,2048]{1,0:T(8,128)S(1)} %add.31.mine_ref), channel_id=1, source_target_pairs={{0,1},{1,0},{2,3},{3,2},{4,5},{5,4},{6,7},{7,6},{8,9},{9,8},{10,11... | collective-permute-start | bytes 196616 | tf_op jit(solution)/shard_map/ppermute | solution.py:530

commit v13 on v12

--- a/solution.py
+++ b/solution.py
@@ -499,7 +499,7 @@
     core = lax.axis_index("seq")
     sum_ref[core] = mine_ref[...]
     sum_ref[1 - core] = theirs_ref[...]
-    sums = jnp.concatenate([sum_ref[0], sum_ref[1]], axis=0).astype(BF)
+    sums = jnp.concatenate([sum_ref[0], sum_ref[1]], axis=0)
     total = None
     for chunk in range(8):
         term = contract_last(sums[:, 256 * chunk : 256 * (chunk + 1)], weight_ref[chunk])
@@ -602,7 +602,7 @@
             jax.ShapeDtypeStruct((64, 1024), F32),
             jax.ShapeDtypeStruct((4, 64, 1024), BF),
             jax.ShapeDtypeStruct((4, 1024, 256), BF),
-            jax.ShapeDtypeStruct((2, 256, 1024), BF),
+            pltpu.HBM((2, 256, 1024), BF),
         ),
         in_specs=[SMEM, ANY, ANY, ANY, HBM, ANY],
         out_specs=(VMEM, HBM, HBM, HBM),
@@ -682,16 +682,18 @@
     )(first_keep, first_back, second_keep, *second_back, *pay_parts)
 
     sums = mine + core_flip(theirs)
-    x_part, z_part, xz_part = [owner_flip(sums, bits) for bits in (1, 2, 3)]
+    x_part, z_part, xz_part = [
+        owner_flip(sums.astype(BF), bits).astype(F32) for bits in (1, 2, 3)
+    ]
     sums = (sums + x_part) + (z_part + xz_part)
-    sums = sums + owner_flip(sums, 4)
+    sums = (sums + owner_flip(sums.astype(BF), 4).astype(F32)).astype(BF)
 
     return pl.pallas_call(
         product_kernel,
         out_shape=jax.ShapeDtypeStruct((P_SIZE, 1024), F32),
         in_specs=[VMEM, VMEM, VMEM],
         out_specs=VMEM,
-        scratch_shapes=[pltpu.VMEM((2, 8, 2048), F32)],
+        scratch_shapes=[pltpu.VMEM((2, 8, 2048), BF)],
         compiler_params=params(30),
         name="products",
     )(sums, core_flip(sums), weights_at_hand)

time: 94.1 us -> 91.2 us (0.969)
  waiting for transfers between devices: 28.3 us -> 25.7 us
  local copies, waits for them, and re-layouts: 1.05 us -> 0.03 us
    ppermute x13, waiting for transfers between devices: 22.5 us -> 19.9 us  [owner_flip(): return lax.ppermute(value, 'fsdp', [(i, i ^ bits) for i in range(8)])]
    unnamed x16 -> x14, local copies, waits for them, and re-layouts: 1.05 us -> 0.03 us
  transfers between devices with their start and end apart: 22 -> 22, of which waited for: 11 -> 10; matrix products, arithmetic and copies ran while one was open for 2% -> 2% of each run, Pallas kernels for 15% -> 16%
where the time goes in v13:
time: 91.2 us; the launch traced here: 90.8 us
  starting transfers between devices  36.2 us (40%)
  Pallas kernels  27 us (30%)
  waiting for transfers between devices  25.7 us (28%)
  other arithmetic  1.67 us (2%)
    ppermute x13, starting transfers between devices, owner_flip(): return lax.ppermute(value, 'fsdp', [(i, i ^ bits) for i in range(8)])  22.9 us
    ppermute x13, waiting for transfers between devices, owner_flip(): return lax.ppermute(value, 'fsdp', [(i, i ^ bits) for i in range(8)])  19.9 us
    all_to_all x2, starting transfers between devices, zone_exchange(): lax.all_to_all(value, 'fsdp', split_axis=0, concat_axis=0, tiled=True, ax...  9.94 us
    pallas_call x1, Pallas kernels, pair_split(): pl.pallas_call(own_kernel, out_shape=(jax.ShapeDtypeStruct((8, 1024, 256)...  7.56 us
    pallas_call x1, Pallas kernels, pair_split(): pl.pallas_call(first_kernel, out_shape=(jax.ShapeDtypeStruct((64, 1024),...  5.39 us
    pallas_call x1, Pallas kernels, pair_split(): pl.pallas_call(second_kernel, out_shape=(jax.ShapeDtypeStruct((64, 1024),...  4.78 us
    all_to_all x2, waiting for transfers between devices, zone_exchange(): lax.all_to_all(value, 'fsdp', split_axis=0, concat_axis=0, tiled=True, ax...  3.3 us
    pallas_call x1, Pallas kernels, pair_split(): pl.pallas_call(middle_kernel, out_shape=(jax.ShapeDtypeStruct((8, 2048),...  2.61 us
  transfers between devices with their start and end apart: 22, of which 10 were waited for; matrix products, arithmetic and copies ran while one was open for 2% of the time, Pallas kernels for 16%

profile of v13, /device:TPU:0, one launch (start us, length us, event | category | flops | bytes accessed | tf_op | source)
XLA Modules:
  0.0 90.8 jit_solution(9710896102108175594)
XLA Ops:
  0.0 2.4 %head.1 = (bf16[4,64,2048]{2,1,0:T(8,128)(2,1)}, bf16[48,4096]{1,0:T(8,128)(2,1)}, bf16[64,4096]{1,0:T(8,128)(2,1)}) custom-call(bf16[64,8192]{1,0:T(8,128)(2,1)} %tok_in_ref.1, bf16[160,4096]{1,0:T(8,128)(2,1)} %gate_ref.3, bf16[160,4096]{1,0:T(8,128)(2,1)} %up_ref.3), custom_call_target="tpu_custom_call" | custom-call | tf_op jit(solution)/shard_map/head/pallas_call | solution.py:542
  2.5 6.5 %all-to-all-start = ((bf16[4,64,2048]{2,1,0:T(8,128)(2,1)}), bf16[4,64,2048]{2,1,0:T(8,128)(2,1)S(1)}, u32[]{:S(2)}, u32[]{:S(2)}) async-start(bf16[4,64,2048]{2,1,0:T(8,128)(2,1)} %get-tuple-element.37), calls=%async_computation | async-start | bytes 2097152 | tf_op jit(solution)/shard_map/all_to_all | solution.py:533
  8.9 1.5 %collective-permute-start.2 = (bf16[48,4096]{1,0:T(8,128)(2,1)S(1)}, bf16[48,4096]{1,0:T(8,128)(2,1)S(1)}, u32[]{:S(2)}, u32[]{:S(2)}) collective-permute-start(bf16[48,4096]{1,0:T(8,128)(2,1)S(1)} %copy-done.6), channel_id=1, source_target_pairs={{0,2},{2,0},{4,6},{6,4},{8,10},{10,8},{12,14},{14,12},{1,3},{3,1},... | collective-permute-start | bytes 1179656 | tf_op jit(solution)/shard_map/ppermute | solution.py:527
  11.0 0.7 select_reduce_fusion.inv_ref
  11.7 7.6 %own_blocks.1 = (bf16[8,1024,256]{2,1,0:T(8,128)(2,1)}, f32[64,256]{1,0:T(8,128)}) custom-call(s32[3,256]{1,0:T(4,128)} %select_reduce_fusion.inv_ref, bf16[160,4096]{1,0:T(8,128)(2,1)} %gate_ref.3, bf16[160,4096]{1,0:T(8,128)(2,1)} %up_ref.3, bf16[160,4096]{1,0:T(8,128)(2,1)} %down_ref.1, bf16[32,1024]{1,0:T(8,128)(2,1)} %sketch_ref.1, ...), custom_call_target="tpu_custom_call" | custom-call | tf_op jit(solution)/shard_map/own_blocks/pallas_call | solution.py:569
  19.3 1.7 %collective-permute-done.2.a_in_ref = bf16[48,4096]{1,0:T(8,128)(2,1)S(1)} collective-permute-done((bf16[48,4096]{1,0:T(8,128)(2,1)S(1)}, bf16[48,4096]{1,0:T(8,128)(2,1)S(1)}, u32[]{:S(2)}, u32[]{:S(2)}) %collective-permute-start.2) | collective-permute-done | bytes 393248 | tf_op jit(solution)/shard_map/ppermute | solution.py:527
  21.0 1.5 %collective-permute-start.3 = (bf16[48,4096]{1,0:T(8,128)(2,1)S(1)}, bf16[48,4096]{1,0:T(8,128)(2,1)S(1)}, u32[]{:S(2)}, u32[]{:S(2)}) collective-permute-start(bf16[48,4096]{1,0:T(8,128)(2,1)S(1)} %collective-permute-done.2.a_in_ref), channel_id=1, source_target_pairs={{0,16},{16,0},{1,17},{17,1},{2,18},{18,2},{3,19},{19,3},{4,20},{20... | collective-permute-start | bytes 1179656 | tf_op jit(solution)/shard_map/ppermute | solution.py:592
  22.5 2.0 %collective-permute-start.4 = (f32[64,256]{1,0:T(8,128)}, f32[64,256]{1,0:T(8,128)S(1)}, u32[]{:S(2)}, u32[]{:S(2)}) collective-permute-start(f32[64,256]{1,0:T(8,128)} %get-tuple-element.38), channel_id=1, source_target_pairs={{0,4},{2,6},{4,0},{6,2},{8,12},{10,14},{12,8},{14,10},{1,5},{3,7},... | collective-permute-start | bytes 196616 | tf_op jit(solution)/shard_map/ppermute | solution.py:527
  24.5 3.0 %collective-permute-done.4 = f32[64,256]{1,0:T(8,128)S(1)} collective-permute-done((f32[64,256]{1,0:T(8,128)}, f32[64,256]{1,0:T(8,128)S(1)}, u32[]{:S(2)}, u32[]{:S(2)}) %collective-permute-start.4) | collective-permute-done | bytes 65568 | tf_op jit(solution)/shard_map/ppermute | solution.py:527
  27.5 0.8 add.24
  28.3 4.6 %collective-permute-start.5 = (f32[64,256]{1,0:T(8,128)S(1)}, f32[64,256]{1,0:T(8,128)S(1)}, u32[]{:S(2)}, u32[]{:S(2)}) collective-permute-start(f32[64,256]{1,0:T(8,128)S(1)} %add.24), channel_id=1, source_target_pairs={{0,8},{2,10},{4,12},{6,14},{8,0},{10,2},{12,4},{14,6},{1,9},{3,11}... | collective-permute-start | bytes 196616 | tf_op jit(solution)/shard_map/ppermute | solution.py:527
  32.9 1.5 %collective-permute-start = (s32[3,256]{1,0:T(4,128)S(1)}, s32[3,256]{1,0:T(4,128)S(1)}, u32[]{:S(2)}, u32[]{:S(2)}) collective-permute-start(s32[3,256]{1,0:T(4,128)S(1)} %copy-done.1), channel_id=1, source_target_pairs={{0,2},{2,0},{4,6},{6,4},{8,10},{10,8},{12,14},{14,12},{1,3},{3,1},... | collective-permute-start | bytes 9224 | tf_op jit(solution)/shard_map/ppermute | solution.py:527
  34.4 3.1 %collective-permute-done.5 = f32[64,256]{1,0:T(8,128)S(1)} collective-permute-done((f32[64,256]{1,0:T(8,128)S(1)}, f32[64,256]{1,0:T(8,128)S(1)}, u32[]{:S(2)}, u32[]{:S(2)}) %collective-permute-start.5) | collective-permute-done | bytes 65568 | tf_op jit(solution)/shard_map/ppermute | solution.py:527
  37.5 5.4 %first_partial.1 = (f32[64,1024]{1,0:T(8,128)S(1)}, bf16[4,64,1024]{2,1,0:T(8,128)(2,1)}, bf16[4,1024,256]{2,1,0:T(8,128)(2,1)}, bf16[2,256,1024]{2,1,0:T(8,128)(2,1)}) custom-call(s32[3,256]{1,0:T(4,128)S(1)} %collective-permute-done.inv_ref, bf16[48,4096]{1,0:T(8,128)(2,1)S(1)} %collective-permute-done.2.a_in_ref, ...), custom_call_target="tpu_custom_call" | custom-call | tf_op jit(solution)/shard_map/first_partial/pallas_call | solution.py:599
  43.0 3.5 %all-to-all-start.1 = ((bf16[4,64,1024]{2,1,0:T(8,128)(2,1)}), bf16[4,64,1024]{2,1,0:T(8,128)(2,1)S(1)}, u32[]{:S(2)}, u32[]{:S(2)}) async-start(bf16[4,64,1024]{2,1,0:T(8,128)(2,1)} %get-tuple-element.45), calls=%async_computation.1 | async-start | bytes 1048576 | tf_op jit(solution)/shard_map/all_to_all | solution.py:533
  46.5 1.6 %collective-permute-start.7 = (f32[64,256]{1,0:T(8,128)S(1)}, f32[64,256]{1,0:T(8,128)S(1)}, u32[]{:S(2)}, u32[]{:S(2)}) collective-permute-start(f32[64,256]{1,0:T(8,128)S(1)} %add.25), channel_id=1, source_target_pairs={{0,2},{2,0},{4,6},{6,4},{8,10},{10,8},{12,14},{14,12},{1,3},{3,1},... | collective-permute-start | bytes 196616 | tf_op jit(solution)/shard_map/ppermute | solution.py:527
  48.0 4.8 %second_partial.1 = (f32[64,1024]{1,0:T(8,128)}, bf16[64,1024]{1,0:T(8,128)(2,1)}, bf16[64,1024]{1,0:T(8,128)(2,1)}, bf16[64,1024]{1,0:T(8,128)(2,1)}) custom-call(bf16[4,1024,256]{2,1,0:T(8,128)(2,1)} %collective-permute-done.6.near_in_ref, bf16[8,1024,256]{2,1,0:T(8,128)(2,1)} %get-tuple-element.56.weight_in_ref, ...), custom_call_target="tpu_custom_call" | custom-call | tf_op jit(solution)/shard_map/second_partial/pallas_call | solution.py:627
  52.8 2.0 %collective-permute-start.8 = (bf16[64,1024]{1,0:T(8,128)(2,1)}, bf16[64,1024]{1,0:T(8,128)(2,1)S(1)}, u32[]{:S(2)}, u32[]{:S(2)}) collective-permute-start(bf16[64,1024]{1,0:T(8,128)(2,1)} %get-tuple-element.52), channel_id=1, source_target_pairs={{0,4},{2,6},{4,0},{6,2},{8,12},{10,14},{12,8},{14,10},{1,5},{3,7},... | collective-permute-start | bytes 393224 | tf_op jit(solution)/shard_map/ppermute | solution.py:527
  54.9 2.4 %collective-permute-start.9 = (bf16[64,1024]{1,0:T(8,128)(2,1)}, bf16[64,1024]{1,0:T(8,128)(2,1)S(1)}, u32[]{:S(2)}, u32[]{:S(2)}) collective-permute-start(bf16[64,1024]{1,0:T(8,128)(2,1)} %get-tuple-element.53), channel_id=1, source_target_pairs={{0,8},{2,10},{4,12},{6,14},{8,0},{10,2},{12,4},{14,6},{1,9},{3,11}... | collective-permute-start | bytes 393224 | tf_op jit(solution)/shard_map/ppermute | solution.py:527
  57.4 1.5 %collective-permute-start.12 = (f32[64,256]{1,0:T(8,128)S(1)}, f32[64,256]{1,0:T(8,128)S(1)}, u32[]{:S(2)}, u32[]{:S(2)}) collective-permute-start(f32[64,256]{1,0:T(8,128)S(1)} %add.26.pay0_ref), channel_id=1, source_target_pairs={{0,16},{16,0},{1,17},{17,1},{2,18},{18,2},{3,19},{19,3},{4,20},{20... | collective-permute-start | bytes 196616 | tf_op jit(solution)/shard_map/ppermute | solution.py:651
  59.0 3.3 %all-to-all-done.1.first_ref = bf16[4,64,1024]{2,1,0:T(8,128)(2,1)S(1)} async-done(((bf16[4,64,1024]{2,1,0:T(8,128)(2,1)}), bf16[4,64,1024]{2,1,0:T(8,128)(2,1)S(1)}, u32[]{:S(2)}, u32[]{:S(2)}) %all-to-all-start.1) | async-done | bytes 524320 | tf_op jit(solution)/shard_map/all_to_all | solution.py:533
  62.3 2.2 %fetch_weights.1.weight_ref = bf16[8,1024,256]{2,1,0:T(8,128)(2,1)S(1)} custom-call(bf16[8,1024,256]{2,1,0:T(8,128)(2,1)} %get-tuple-element.56.weight_in_ref), custom_call_target="tpu_custom_call" | custom-call | tf_op jit(solution)/shard_map/fetch_weights/pallas_call | solution.py:656
  64.5 6.2 %collective-permute-done.9.second2_ref = bf16[64,1024]{1,0:T(8,128)(2,1)S(1)} collective-permute-done((bf16[64,1024]{1,0:T(8,128)(2,1)}, bf16[64,1024]{1,0:T(8,128)(2,1)S(1)}, u32[]{:S(2)}, u32[]{:S(2)}) %collective-permute-start.9) | collective-permute-done | bytes 131104 | tf_op jit(solution)/shard_map/ppermute | solution.py:527
  70.7 2.6 %token_sums.1 = (f32[8,2048]{1,0:T(8,128)S(1)}, f32[8,2048]{1,0:T(8,128)S(1)}) custom-call(f32[64,1024]{1,0:T(8,128)S(1)} %get-tuple-element.44.first_keep_ref, bf16[4,64,1024]{2,1,0:T(8,128)(2,1)S(1)} %all-to-all-done.1.first_ref, f32[64,1024]{1,0:T(8,128)S(1)} %copy-done, bf16[64,1024]{1,0:T(8,128)(2,1)S(1)} %collective-permute-done.8.second1_ref, ...), custom_call_target="tpu_custom_call" | custom-call | tf_op jit(solution)/shard_map/token_sums/pallas_call | solution.py:667
  73.4 1.2 %collective-permute-done.14 = f32[8,2048]{1,0:T(8,128)S(1)} collective-permute-done((f32[8,2048]{1,0:T(8,128)S(1)}, f32[8,2048]{1,0:T(8,128)S(1)}, u32[]{:S(2)}, u32[]{:S(2)}) %collective-permute-start.14) | collective-permute-done | bytes 65568 | tf_op jit(solution)/shard_map/ppermute | solution.py:530
  74.6 4.0 %collective-permute-start.17 = (bf16[8,2048]{1,0:T(8,128)(2,1)S(1)}, bf16[8,2048]{1,0:T(8,128)(2,1)S(1)}, u32[]{:S(2)}, u32[]{:S(2)}) collective-permute-start(bf16[8,2048]{1,0:T(8,128)(2,1)S(1)} %get-tuple-element.61), channel_id=1, source_target_pairs={{0,6},{2,4},{4,2},{6,0},{8,14},{10,12},{12,10},{14,8},{1,7},{3,5},... | collective-permute-start | bytes 98312 | tf_op jit(solution)/shard_map/ppermute | solution.py:527
  79.2 1.3 %collective-permute-done.17 = bf16[8,2048]{1,0:T(8,128)(2,1)S(1)} collective-permute-done((bf16[8,2048]{1,0:T(8,128)(2,1)S(1)}, bf16[8,2048]{1,0:T(8,128)(2,1)S(1)}, u32[]{:S(2)}, u32[]{:S(2)}) %collective-permute-start.17) | collective-permute-done | bytes 32800 | tf_op jit(solution)/shard_map/ppermute | solution.py:527
  80.5 2.0 %collective-permute-done.16 = bf16[8,2048]{1,0:T(8,128)(2,1)S(1)} collective-permute-done((bf16[8,2048]{1,0:T(8,128)(2,1)S(1)}, bf16[8,2048]{1,0:T(8,128)(2,1)S(1)}, u32[]{:S(2)}, u32[]{:S(2)}) %collective-permute-start.16) | collective-permute-done | bytes 32800 | tf_op jit(solution)/shard_map/ppermute | solution.py:527
  82.5 2.1 %collective-permute-start.18 = (bf16[8,2048]{1,0:T(8,128)(2,1)S(1)}, bf16[8,2048]{1,0:T(8,128)(2,1)S(1)}, u32[]{:S(2)}, u32[]{:S(2)}) collective-permute-start(bf16[8,2048]{1,0:T(8,128)(2,1)S(1)} %fusion), channel_id=1, source_target_pairs={{0,8},{2,10},{4,12},{6,14},{8,0},{10,2},{12,4},{14,6},{1,9},{3,11}... | collective-permute-start | bytes 98312 | tf_op jit(solution)/shard_map/ppermute | solution.py:527
  84.7 2.8 %collective-permute-done.18 = bf16[8,2048]{1,0:T(8,128)(2,1)S(1)} collective-permute-done((bf16[8,2048]{1,0:T(8,128)(2,1)S(1)}, bf16[8,2048]{1,0:T(8,128)(2,1)S(1)}, u32[]{:S(2)}, u32[]{:S(2)}) %collective-permute-start.18) | collective-permute-done | bytes 32800 | tf_op jit(solution)/shard_map/ppermute | solution.py:527
  87.5 1.2 %collective-permute-done.19.theirs_ref = bf16[8,2048]{1,0:T(8,128)(2,1)S(1)} collective-permute-done((bf16[8,2048]{1,0:T(8,128)(2,1)S(1)}, bf16[8,2048]{1,0:T(8,128)(2,1)S(1)}, u32[]{:S(2)}, u32[]{:S(2)}) %collective-permute-start.19) | collective-permute-done | bytes 32800 | tf_op jit(solution)/shard_map/ppermute | solution.py:530
  88.7 2.1 %products.1 = f32[16,1024]{1,0:T(8,128)} custom-call(bf16[8,2048]{1,0:T(8,128)(2,1)S(1)} %add_convert_fusion.mine_ref, bf16[8,2048]{1,0:T(8,128)(2,1)S(1)} %collective-permute-done.19.theirs_ref, bf16[8,1024,256]{2,1,0:T(8,128)(2,1)S(1)} %fetch_weights.1.weight_ref), custom_call_target="tpu_custom_call" | custom-call | tf_op jit(solution)/shard_map/products/pallas_call | solution.py:691
  (41 shorter events, 1.7 us)
Async XLA Ops:
  0.0 10.9 %copy-start.2 = (s32[160]{0:T(256)S(1)}, s32[160]{0:T(256)}, u32[]{:S(2)}) copy-start(s32[160]{0:T(256)} %param.16) | copy-start | bytes 1924
  0.0 10.9 %copy-start.3 = (s32[160]{0:T(256)S(1)}, s32[160]{0:T(256)}, u32[]{:S(2)}) copy-start(s32[160]{0:T(256)} %param.14) | copy-start | bytes 1924
  0.0 10.9 %copy-start.4 = (s32[160]{0:T(256)S(1)}, s32[160]{0:T(256)}, u32[]{:S(2)}) copy-start(s32[160]{0:T(256)} %param.12) | copy-start | bytes 1924
  2.4 6.5 %copy-start.6 = (bf16[48,4096]{1,0:T(8,128)(2,1)S(1)}, bf16[48,4096]{1,0:T(8,128)(2,1)}, u32[]{:S(2)}) copy-start(bf16[48,4096]{1,0:T(8,128)(2,1)} %get-tuple-element.34) | copy-start | bytes 1179652
  2.4 8.0 %copy-start.5 = (bf16[64,4096]{1,0:T(8,128)(2,1)S(1)}, bf16[64,4096]{1,0:T(8,128)(2,1)}, u32[]{:S(2)}) copy-start(bf16[64,4096]{1,0:T(8,128)(2,1)} %get-tuple-element.33) | copy-start | bytes 1572868
  2.5 35.0 %all-to-all-start = ((bf16[4,64,2048]{2,1,0:T(8,128)(2,1)}), bf16[4,64,2048]{2,1,0:T(8,128)(2,1)S(1)}, u32[]{:S(2)}, u32[]{:S(2)}) async-start(bf16[4,64,2048]{2,1,0:T(8,128)(2,1)} %get-tuple-element.37), calls=%async_computation | async-start | bytes 2097152 | tf_op jit(solution)/shard_map/all_to_all | solution.py:533
  8.9 12.0 %collective-permute-start.2 = (bf16[48,4096]{1,0:T(8,128)(2,1)S(1)}, bf16[48,4096]{1,0:T(8,128)(2,1)S(1)}, u32[]{:S(2)}, u32[]{:S(2)}) collective-permute-start(bf16[48,4096]{1,0:T(8,128)(2,1)S(1)} %copy-done.6), channel_id=1, source_target_pairs={{0,2},{2,0},{4,6},{6,4},{8,10},{10,8},{12,14},{14,12},{1,3},{3,1},... | collective-permute-start | bytes 1179656 | tf_op jit(solution)/shard_map/ppermute | solution.py:527
  10.4 27.1 %collective-permute-start.1 = (bf16[64,4096]{1,0:T(8,128)(2,1)S(1)}, bf16[64,4096]{1,0:T(8,128)(2,1)S(1)}, u32[]{:S(2)}, u32[]{:S(2)}) collective-permute-start(bf16[64,4096]{1,0:T(8,128)(2,1)S(1)} %copy-done.5), channel_id=1, source_target_pairs={{0,2},{2,0},{4,6},{6,4},{8,10},{10,8},{12,14},{14,12},{1,3},{3,1},... | collective-permute-start | bytes 1572872 | tf_op jit(solution)/shard_map/ppermute | solution.py:527
  11.7 21.2 %copy-start.1 = (s32[3,256]{1,0:T(4,128)S(1)}, s32[3,256]{1,0:T(4,128)}, u32[]{:S(2)}) copy-start(s32[3,256]{1,0:T(4,128)} %select_reduce_fusion.inv_ref) | copy-start | bytes 9220
  21.0 16.5 %collective-permute-start.3 = (bf16[48,4096]{1,0:T(8,128)(2,1)S(1)}, bf16[48,4096]{1,0:T(8,128)(2,1)S(1)}, u32[]{:S(2)}, u32[]{:S(2)}) collective-permute-start(bf16[48,4096]{1,0:T(8,128)(2,1)S(1)} %collective-permute-done.2.a_in_ref), channel_id=1, source_target_pairs={{0,16},{16,0},{1,17},{17,1},{2,18},{18,2},{3,19},{19,3},{4,20},{20... | collective-permute-start | bytes 1179656 | tf_op jit(solution)/shard_map/ppermute | solution.py:592
  22.5 5.0 %collective-permute-start.4 = (f32[64,256]{1,0:T(8,128)}, f32[64,256]{1,0:T(8,128)S(1)}, u32[]{:S(2)}, u32[]{:S(2)}) collective-permute-start(f32[64,256]{1,0:T(8,128)} %get-tuple-element.38), channel_id=1, source_target_pairs={{0,4},{2,6},{4,0},{6,2},{8,12},{10,14},{12,8},{14,10},{1,5},{3,7},... | collective-permute-start | bytes 196616 | tf_op jit(solution)/shard_map/ppermute | solution.py:527
  28.3 9.1 %collective-permute-start.5 = (f32[64,256]{1,0:T(8,128)S(1)}, f32[64,256]{1,0:T(8,128)S(1)}, u32[]{:S(2)}, u32[]{:S(2)}) collective-permute-start(f32[64,256]{1,0:T(8,128)S(1)} %add.24), channel_id=1, source_target_pairs={{0,8},{2,10},{4,12},{6,14},{8,0},{10,2},{12,4},{14,6},{1,9},{3,11}... | collective-permute-start | bytes 196616 | tf_op jit(solution)/shard_map/ppermute | solution.py:527
  32.9 4.6 %collective-permute-start = (s32[3,256]{1,0:T(4,128)S(1)}, s32[3,256]{1,0:T(4,128)S(1)}, u32[]{:S(2)}, u32[]{:S(2)}) collective-permute-start(s32[3,256]{1,0:T(4,128)S(1)} %copy-done.1), channel_id=1, source_target_pairs={{0,2},{2,0},{4,6},{6,4},{8,10},{10,8},{12,14},{14,12},{1,3},{3,1},... | collective-permute-start | bytes 9224 | tf_op jit(solution)/shard_map/ppermute | solution.py:527
  42.9 5.1 %collective-permute-start.6 = (bf16[4,1024,256]{2,1,0:T(8,128)(2,1)}, bf16[4,1024,256]{2,1,0:T(8,128)(2,1)}, u32[]{:S(2)}, u32[]{:S(2)}) collective-permute-start(bf16[4,1024,256]{2,1,0:T(8,128)(2,1)} %get-tuple-element.47), channel_id=1, source_target_pairs={{0,1},{1,0},{2,3},{3,2},{4,5},{5,4},{6,7},{7,6},{8,9},{9,8},{10,11... | collective-permute-start | bytes 6291464 | tf_op jit(solution)/shard_map/ppermute | solution.py:530
  43.0 19.3 %all-to-all-start.1 = ((bf16[4,64,1024]{2,1,0:T(8,128)(2,1)}), bf16[4,64,1024]{2,1,0:T(8,128)(2,1)S(1)}, u32[]{:S(2)}, u32[]{:S(2)}) async-start(bf16[4,64,1024]{2,1,0:T(8,128)(2,1)} %get-tuple-element.45), calls=%async_computation.1 | async-start | bytes 1048576 | tf_op jit(solution)/shard_map/all_to_all | solution.py:533
  46.5 6.3 %collective-permute-start.7 = (f32[64,256]{1,0:T(8,128)S(1)}, f32[64,256]{1,0:T(8,128)S(1)}, u32[]{:S(2)}, u32[]{:S(2)}) collective-permute-start(f32[64,256]{1,0:T(8,128)S(1)} %add.25), channel_id=1, source_target_pairs={{0,2},{2,0},{4,6},{6,4},{8,10},{10,8},{12,14},{14,12},{1,3},{3,1},... | collective-permute-start | bytes 196616 | tf_op jit(solution)/shard_map/ppermute | solution.py:527
  52.8 11.7 %collective-permute-start.8 = (bf16[64,1024]{1,0:T(8,128)(2,1)}, bf16[64,1024]{1,0:T(8,128)(2,1)S(1)}, u32[]{:S(2)}, u32[]{:S(2)}) collective-permute-start(bf16[64,1024]{1,0:T(8,128)(2,1)} %get-tuple-element.52), channel_id=1, source_target_pairs={{0,4},{2,6},{4,0},{6,2},{8,12},{10,14},{12,8},{14,10},{1,5},{3,7},... | collective-permute-start | bytes 393224 | tf_op jit(solution)/shard_map/ppermute | solution.py:527
  54.8 4.1 %collective-permute-start.11 = (f32[64,256]{1,0:T(8,128)S(1)}, f32[64,256]{1,0:T(8,128)S(1)}, u32[]{:S(2)}, u32[]{:S(2)}) collective-permute-start(f32[64,256]{1,0:T(8,128)S(1)} %add.26.pay0_ref), channel_id=1, source_target_pairs={{0,1},{1,0},{2,3},{3,2},{4,5},{5,4},{6,7},{7,6},{8,9},{9,8},{10,11... | collective-permute-start | bytes 196616 | tf_op jit(solution)/shard_map/ppermute | solution.py:530
  54.9 15.8 %collective-permute-start.9 = (bf16[64,1024]{1,0:T(8,128)(2,1)}, bf16[64,1024]{1,0:T(8,128)(2,1)S(1)}, u32[]{:S(2)}, u32[]{:S(2)}) collective-permute-start(bf16[64,1024]{1,0:T(8,128)(2,1)} %get-tuple-element.53), channel_id=1, source_target_pairs={{0,8},{2,10},{4,12},{6,14},{8,0},{10,2},{12,4},{14,6},{1,9},{3,11}... | collective-permute-start | bytes 393224 | tf_op jit(solution)/shard_map/ppermute | solution.py:527
  57.3 13.4 %copy-start = (f32[64,1024]{1,0:T(8,128)S(1)}, f32[64,1024]{1,0:T(8,128)}, u32[]{:S(2)}) copy-start(f32[64,1024]{1,0:T(8,128)} %get-tuple-element.51.second_keep_ref) | copy-start | bytes 786436
  57.3 13.4 %collective-permute-start.10 = (bf16[64,1024]{1,0:T(8,128)(2,1)}, bf16[64,1024]{1,0:T(8,128)(2,1)S(1)}, u32[]{:S(2)}, u32[]{:S(2)}) collective-permute-start(bf16[64,1024]{1,0:T(8,128)(2,1)} %get-tuple-element.54), channel_id=1, source_target_pairs={{0,12},{2,14},{4,8},{6,10},{8,4},{10,6},{12,0},{14,2},{1,13},{3,15... | collective-permute-start | bytes 393224 | tf_op jit(solution)/shard_map/ppermute | solution.py:527
  57.4 7.0 %collective-permute-start.12 = (f32[64,256]{1,0:T(8,128)S(1)}, f32[64,256]{1,0:T(8,128)S(1)}, u32[]{:S(2)}, u32[]{:S(2)}) collective-permute-start(f32[64,256]{1,0:T(8,128)S(1)} %add.26.pay0_ref), channel_id=1, source_target_pairs={{0,16},{16,0},{1,17},{17,1},{2,18},{18,2},{3,19},{19,3},{4,20},{20... | collective-permute-start | bytes 196616 | tf_op jit(solution)/shard_map/ppermute | solution.py:651
  59.0 5.5 %collective-permute-start.13 = (f32[64,256]{1,0:T(8,128)S(1)}, f32[64,256]{1,0:T(8,128)S(1)}, u32[]{:S(2)}, u32[]{:S(2)}) collective-permute-start(f32[64,256]{1,0:T(8,128)S(1)} %add.26.pay0_ref), channel_id=1, source_target_pairs={{0,17},{1,16},{16,1},{17,0},{2,19},{3,18},{18,3},{19,2},{4,21},{5,... | collective-permute-start | bytes 196616 | tf_op jit(solution)/shard_map/ppermute | solution.py:652
  73.3 1.3 %collective-permute-start.14 = (f32[8,2048]{1,0:T(8,128)S(1)}, f32[8,2048]{1,0:T(8,128)S(1)}, u32[]{:S(2)}, u32[]{:S(2)}) collective-permute-start(f32[8,2048]{1,0:T(8,128)S(1)} %get-tuple-element.59), channel_id=1, source_target_pairs={{0,1},{1,0},{2,3},{3,2},{4,5},{5,4},{6,7},{7,6},{8,9},{9,8},{10,11... | collective-permute-start | bytes 196616 | tf_op jit(solution)/shard_map/ppermute | solution.py:530
  74.6 5.9 %collective-permute-start.17 = (bf16[8,2048]{1,0:T(8,128)(2,1)S(1)}, bf16[8,2048]{1,0:T(8,128)(2,1)S(1)}, u32[]{:S(2)}, u32[]{:S(2)}) collective-permute-start(bf16[8,2048]{1,0:T(8,128)(2,1)S(1)} %get-tuple-element.61), channel_id=1, source_target_pairs={{0,6},{2,4},{4,2},{6,0},{8,14},{10,12},{12,10},{14,8},{1,7},{3,5},... | collective-permute-start | bytes 98312 | tf_op jit(solution)/shard_map/ppermute | solution.py:527
  78.6 3.9 %collective-permute-start.16 = (bf16[8,2048]{1,0:T(8,128)(2,1)S(1)}, bf16[8,2048]{1,0:T(8,128)(2,1)S(1)}, u32[]{:S(2)}, u32[]{:S(2)}) collective-permute-start(bf16[8,2048]{1,0:T(8,128)(2,1)S(1)} %get-tuple-element.61), channel_id=1, source_target_pairs={{0,4},{2,6},{4,0},{6,2},{8,12},{10,14},{12,8},{14,10},{1,5},{3,7},... | collective-permute-start | bytes 98312 | tf_op jit(solution)/shard_map/ppermute | solution.py:527
  78.6 3.9 %collective-permute-start.15 = (bf16[8,2048]{1,0:T(8,128)(2,1)S(1)}, bf16[8,2048]{1,0:T(8,128)(2,1)S(1)}, u32[]{:S(2)}, u32[]{:S(2)}) collective-permute-start(bf16[8,2048]{1,0:T(8,128)(2,1)S(1)} %get-tuple-element.61), channel_id=1, source_target_pairs={{0,2},{2,0},{4,6},{6,4},{8,10},{10,8},{12,14},{14,12},{1,3},{3,1},... | collective-permute-start | bytes 98312 | tf_op jit(solution)/shard_map/ppermute | solution.py:527
  82.5 4.9 %collective-permute-start.18 = (bf16[8,2048]{1,0:T(8,128)(2,1)S(1)}, bf16[8,2048]{1,0:T(8,128)(2,1)S(1)}, u32[]{:S(2)}, u32[]{:S(2)}) collective-permute-start(bf16[8,2048]{1,0:T(8,128)(2,1)S(1)} %fusion), channel_id=1, source_target_pairs={{0,8},{2,10},{4,12},{6,14},{8,0},{10,2},{12,4},{14,6},{1,9},{3,11}... | collective-permute-start | bytes 98312 | tf_op jit(solution)/shard_map/ppermute | solution.py:527
  87.4 1.3 %collective-permute-start.19 = (bf16[8,2048]{1,0:T(8,128)(2,1)S(1)}, bf16[8,2048]{1,0:T(8,128)(2,1)S(1)}, u32[]{:S(2)}, u32[]{:S(2)}) collective-permute-start(bf16[8,2048]{1,0:T(8,128)(2,1)S(1)} %add_convert_fusion.mine_ref), channel_id=1, source_target_pairs={{0,1},{1,0},{2,3},{3,2},{4,5},{5,4},{6,7},{7,6},{8,9},{9,8},{10,11... | collective-permute-start | bytes 98312 | tf_op jit(solution)/shard_map/ppermute | solution.py:530

commit v14 on v13

--- a/solution.py
+++ b/solution.py
@@ -361,28 +361,36 @@
     for load in loads:
         load.start()
     clear_empty_slot(tiles_ref)
-    for load in loads[:3]:
-        load.wait()
-    stage_blocks(blocks_ref, tiles_ref, 0)
-
-    def put(pair, row, piece):
-        lane = (pair % 2) * 128
-        near_ref[pair // 2, pl.ds(row, 32), lane : lane + 128] = piece
-
-    assemble_columns(inv_ref, core, tiles_ref, put)
-    near_store = pltpu.make_async_copy(near_ref, near_out_ref, near_sem.at[0])
-    near_store.start()
     loads[3].wait()
     shuffle_tokens(side, tok_ref, tokens_ref)
     tokens_store = pltpu.make_async_copy(tokens_ref, tokens_out_ref, near_sem.at[1])
     tokens_store.start()
+    for load in loads[:3]:
+        load.wait()
+    stage_blocks(blocks_ref, tiles_ref, 0)
     loads[4].wait()
+
+    @pl.loop(0, 4)
+    def _(step):
+        total_ref[step] = dot(tokens_ref[0], own_ref[step])
+        for inner in range(4):
+            block_row = 4 * step + inner
+            for pair in range(8):
+                cell = block_row * 16 + 2 * pair
+                even, odd = assembled_pair(tiles_ref, inv_ref[core, cell], inv_ref[core, cell + 1])
+                row = pl.multiple_of(block_row * BLK, BLK)
+                cols = slice((pair % 2) * 128, (pair % 2) * 128 + 128)
+                near_ref[pair // 2, pl.ds(row, 32), cols] = even
+                near_ref[pair // 2, pl.ds(row + 32, 32), cols] = odd
+
+    near_store = pltpu.make_async_copy(near_ref, near_out_ref, near_sem.at[0])
+    near_store.start()
     stores = []
     for chunk in range(4):
-        total = dot(tokens_ref[0], own_ref[chunk]) + dot(tokens_ref[1], near_ref[chunk])
+        total = total_ref[chunk] + dot(tokens_ref[1], near_ref[chunk])
         cols = slice(256 * chunk, 256 * (chunk + 1))
-        total_ref[...] = total
-        keep_ref[:, cols] = total_ref[pl.ds(pl.multiple_of(64 * zone, 64), 64), :]
+        total_ref[chunk] = total
+        keep_ref[:, cols] = total_ref[chunk, pl.ds(pl.multiple_of(64 * zone, 64), 64), :]
         sent_ref[:, :, cols] = total.astype(BF).reshape(4, 64, 256)
         lanes = pl.ds(256 * chunk, 256)
         store = pltpu.make_async_copy(
@@ -614,7 +622,7 @@
             pltpu.VMEM((4, 64, 2048), BF),
             pltpu.VMEM((2, 256, 1024), BF),
             pltpu.VMEM((4, 64, 1024), BF),
-            pltpu.VMEM((256, 256), F32),
+            pltpu.VMEM((4, 256, 256), F32),
             pltpu.SemaphoreType.DMA((5,)),
             pltpu.SemaphoreType.DMA((2,)),
             pltpu.SemaphoreType.DMA((4,)),
@@ -682,11 +690,9 @@
     )(first_keep, first_back, second_keep, *second_back, *pay_parts)
 
     sums = mine + core_flip(theirs)
-    x_part, z_part, xz_part = [
-        owner_flip(sums.astype(BF), bits).astype(F32) for bits in (1, 2, 3)
-    ]
-    sums = (sums + x_part) + (z_part + xz_part)
-    sums = (sums + owner_flip(sums.astype(BF), 4).astype(F32)).astype(BF)
+    sums = sums + owner_flip(sums.astype(BF), 1).astype(F32)
+    parts = [owner_flip(sums.astype(BF), bits).astype(F32) for bits in (2, 4, 6)]
+    sums = ((sums + parts[0]) + (parts[1] + parts[2])).astype(BF)
 
     return pl.pallas_call(
         product_kernel,

time: 91.2 us -> 92.7 us (1.016)
  Pallas kernels: 27 us -> 28.8 us
    pallas_call x1, Pallas kernels: 5.39 us -> 7.24 us  [pair_split(): pl.pallas_call(first_kernel, out_shape=(jax.ShapeDtypeStruct((64, 1024),...]
  transfers between devices with their start and end apart: 22 -> 22, of which waited for: 10 -> 11; matrix products, arithmetic and copies ran while one was open for 2% -> 2% of each run, Pallas kernels for 16% -> 16%
where the time goes in v14:
time: 92.7 us; the launch traced here: 92.2 us
  starting transfers between devices  35.5 us (38%)
  Pallas kernels  28.8 us (31%)
  waiting for transfers between devices  26 us (28%)
  other arithmetic  1.66 us (2%)
    ppermute x13, starting transfers between devices, owner_flip(): return lax.ppermute(value, 'fsdp', [(i, i ^ bits) for i in range(8)])  22.2 us
    ppermute x13, waiting for transfers between devices, owner_flip(): return lax.ppermute(value, 'fsdp', [(i, i ^ bits) for i in range(8)])  20.3 us
    all_to_all x2, starting transfers between devices, zone_exchange(): lax.all_to_all(value, 'fsdp', split_axis=0, concat_axis=0, tiled=True, ax...  9.94 us
    pallas_call x1, Pallas kernels, pair_split(): pl.pallas_call(own_kernel, out_shape=(jax.ShapeDtypeStruct((8, 1024, 256)...  7.56 us
    pallas_call x1, Pallas kernels, pair_split(): pl.pallas_call(first_kernel, out_shape=(jax.ShapeDtypeStruct((64, 1024),...  7.24 us
    pallas_call x1, Pallas kernels, pair_split(): pl.pallas_call(second_kernel, out_shape=(jax.ShapeDtypeStruct((64, 1024),...  4.78 us
    all_to_all x2, waiting for transfers between devices, zone_exchange(): lax.all_to_all(value, 'fsdp', split_axis=0, concat_axis=0, tiled=True, ax...  3.31 us
    pallas_call x1, Pallas kernels, pair_split(): pl.pallas_call(middle_kernel, out_shape=(jax.ShapeDtypeStruct((8, 2048),...  2.61 us
  transfers between devices with their start and end apart: 22, of which 11 were waited for; matrix products, arithmetic and copies ran while one was open for 2% of the time, Pallas kernels for 16%

profile of v14, /device:TPU:0, one launch (start us, length us, event | category | flops | bytes accessed | tf_op | source)
XLA Modules:
  0.0 92.2 jit_solution(8113791007321868342)
XLA Ops:
  0.0 2.4 %head.1 = (bf16[4,64,2048]{2,1,0:T(8,128)(2,1)}, bf16[48,4096]{1,0:T(8,128)(2,1)}, bf16[64,4096]{1,0:T(8,128)(2,1)}) custom-call(bf16[64,8192]{1,0:T(8,128)(2,1)} %tok_in_ref.1, bf16[160,4096]{1,0:T(8,128)(2,1)} %gate_ref.3, bf16[160,4096]{1,0:T(8,128)(2,1)} %up_ref.3), custom_call_target="tpu_custom_call" | custom-call | tf_op jit(solution)/shard_map/head/pallas_call | solution.py:550
  2.5 6.5 %all-to-all-start = ((bf16[4,64,2048]{2,1,0:T(8,128)(2,1)}), bf16[4,64,2048]{2,1,0:T(8,128)(2,1)S(1)}, u32[]{:S(2)}, u32[]{:S(2)}) async-start(bf16[4,64,2048]{2,1,0:T(8,128)(2,1)} %get-tuple-element.37), calls=%async_computation | async-start | bytes 2097152 | tf_op jit(solution)/shard_map/all_to_all | solution.py:541
  8.9 1.5 %collective-permute-start.2 = (bf16[48,4096]{1,0:T(8,128)(2,1)S(1)}, bf16[48,4096]{1,0:T(8,128)(2,1)S(1)}, u32[]{:S(2)}, u32[]{:S(2)}) collective-permute-start(bf16[48,4096]{1,0:T(8,128)(2,1)S(1)} %copy-done.6), channel_id=1, source_target_pairs={{0,2},{2,0},{4,6},{6,4},{8,10},{10,8},{12,14},{14,12},{1,3},{3,1},... | collective-permute-start | bytes 1179656 | tf_op jit(solution)/shard_map/ppermute | solution.py:535
  11.7 7.6 %own_blocks.1 = (bf16[8,1024,256]{2,1,0:T(8,128)(2,1)}, f32[64,256]{1,0:T(8,128)}) custom-call(s32[3,256]{1,0:T(4,128)} %select_reduce_fusion.inv_ref, bf16[160,4096]{1,0:T(8,128)(2,1)} %gate_ref.3, bf16[160,4096]{1,0:T(8,128)(2,1)} %up_ref.3, bf16[160,4096]{1,0:T(8,128)(2,1)} %down_ref.1, bf16[32,1024]{1,0:T(8,128)(2,1)} %sketch_ref.1, ...), custom_call_target="tpu_custom_call" | custom-call | tf_op jit(solution)/shard_map/own_blocks/pallas_call | solution.py:577
  19.3 1.7 %collective-permute-done.2.a_in_ref = bf16[48,4096]{1,0:T(8,128)(2,1)S(1)} collective-permute-done((bf16[48,4096]{1,0:T(8,128)(2,1)S(1)}, bf16[48,4096]{1,0:T(8,128)(2,1)S(1)}, u32[]{:S(2)}, u32[]{:S(2)}) %collective-permute-start.2) | collective-permute-done | bytes 393248 | tf_op jit(solution)/shard_map/ppermute | solution.py:535
  21.0 1.5 %collective-permute-start.3 = (bf16[48,4096]{1,0:T(8,128)(2,1)S(1)}, bf16[48,4096]{1,0:T(8,128)(2,1)S(1)}, u32[]{:S(2)}, u32[]{:S(2)}) collective-permute-start(bf16[48,4096]{1,0:T(8,128)(2,1)S(1)} %collective-permute-done.2.a_in_ref), channel_id=1, source_target_pairs={{0,16},{16,0},{1,17},{17,1},{2,18},{18,2},{3,19},{19,3},{4,20},{20... | collective-permute-start | bytes 1179656 | tf_op jit(solution)/shard_map/ppermute | solution.py:600
  22.5 2.0 %collective-permute-start.4 = (f32[64,256]{1,0:T(8,128)}, f32[64,256]{1,0:T(8,128)S(1)}, u32[]{:S(2)}, u32[]{:S(2)}) collective-permute-start(f32[64,256]{1,0:T(8,128)} %get-tuple-element.38), channel_id=1, source_target_pairs={{0,4},{2,6},{4,0},{6,2},{8,12},{10,14},{12,8},{14,10},{1,5},{3,7},... | collective-permute-start | bytes 196616 | tf_op jit(solution)/shard_map/ppermute | solution.py:535
  24.5 3.0 %collective-permute-done.4 = f32[64,256]{1,0:T(8,128)S(1)} collective-permute-done((f32[64,256]{1,0:T(8,128)}, f32[64,256]{1,0:T(8,128)S(1)}, u32[]{:S(2)}, u32[]{:S(2)}) %collective-permute-start.4) | collective-permute-done | bytes 65568 | tf_op jit(solution)/shard_map/ppermute | solution.py:535
  27.5 0.8 add.24
  28.3 4.6 %collective-permute-start.5 = (f32[64,256]{1,0:T(8,128)S(1)}, f32[64,256]{1,0:T(8,128)S(1)}, u32[]{:S(2)}, u32[]{:S(2)}) collective-permute-start(f32[64,256]{1,0:T(8,128)S(1)} %add.24), channel_id=1, source_target_pairs={{0,8},{2,10},{4,12},{6,14},{8,0},{10,2},{12,4},{14,6},{1,9},{3,11}... | collective-permute-start | bytes 196616 | tf_op jit(solution)/shard_map/ppermute | solution.py:535
  32.9 1.5 %collective-permute-start = (s32[3,256]{1,0:T(4,128)S(1)}, s32[3,256]{1,0:T(4,128)S(1)}, u32[]{:S(2)}, u32[]{:S(2)}) collective-permute-start(s32[3,256]{1,0:T(4,128)S(1)} %copy-done.1), channel_id=1, source_target_pairs={{0,2},{2,0},{4,6},{6,4},{8,10},{10,8},{12,14},{14,12},{1,3},{3,1},... | collective-permute-start | bytes 9224 | tf_op jit(solution)/shard_map/ppermute | solution.py:535
  34.4 3.1 %collective-permute-done.5 = f32[64,256]{1,0:T(8,128)S(1)} collective-permute-done((f32[64,256]{1,0:T(8,128)S(1)}, f32[64,256]{1,0:T(8,128)S(1)}, u32[]{:S(2)}, u32[]{:S(2)}) %collective-permute-start.5) | collective-permute-done | bytes 65568 | tf_op jit(solution)/shard_map/ppermute | solution.py:535
  37.5 7.2 %first_partial.1 = (f32[64,1024]{1,0:T(8,128)S(1)}, bf16[4,64,1024]{2,1,0:T(8,128)(2,1)}, bf16[4,1024,256]{2,1,0:T(8,128)(2,1)}, bf16[2,256,1024]{2,1,0:T(8,128)(2,1)}) custom-call(s32[3,256]{1,0:T(4,128)S(1)} %collective-permute-done.inv_ref, bf16[48,4096]{1,0:T(8,128)(2,1)S(1)} %collective-permute-done.2.a_in_ref, ...), custom_call_target="tpu_custom_call" | custom-call | tf_op jit(solution)/shard_map/first_partial/pallas_call | solution.py:607
  44.8 3.5 %all-to-all-start.1 = ((bf16[4,64,1024]{2,1,0:T(8,128)(2,1)}), bf16[4,64,1024]{2,1,0:T(8,128)(2,1)S(1)}, u32[]{:S(2)}, u32[]{:S(2)}) async-start(bf16[4,64,1024]{2,1,0:T(8,128)(2,1)} %get-tuple-element.45), calls=%async_computation.1 | async-start | bytes 1048576 | tf_op jit(solution)/shard_map/all_to_all | solution.py:541
  48.3 1.5 %collective-permute-start.7 = (f32[64,256]{1,0:T(8,128)S(1)}, f32[64,256]{1,0:T(8,128)S(1)}, u32[]{:S(2)}, u32[]{:S(2)}) collective-permute-start(f32[64,256]{1,0:T(8,128)S(1)} %add.25), channel_id=1, source_target_pairs={{0,2},{2,0},{4,6},{6,4},{8,10},{10,8},{12,14},{14,12},{1,3},{3,1},... | collective-permute-start | bytes 196616 | tf_op jit(solution)/shard_map/ppermute | solution.py:535
  49.9 4.8 %second_partial.1 = (f32[64,1024]{1,0:T(8,128)}, bf16[64,1024]{1,0:T(8,128)(2,1)}, bf16[64,1024]{1,0:T(8,128)(2,1)}, bf16[64,1024]{1,0:T(8,128)(2,1)}) custom-call(bf16[4,1024,256]{2,1,0:T(8,128)(2,1)} %collective-permute-done.6.near_in_ref, bf16[8,1024,256]{2,1,0:T(8,128)(2,1)} %get-tuple-element.56.weight_in_ref, ...), custom_call_target="tpu_custom_call" | custom-call | tf_op jit(solution)/shard_map/second_partial/pallas_call | solution.py:635
  54.7 2.0 %collective-permute-start.8 = (bf16[64,1024]{1,0:T(8,128)(2,1)}, bf16[64,1024]{1,0:T(8,128)(2,1)S(1)}, u32[]{:S(2)}, u32[]{:S(2)}) collective-permute-start(bf16[64,1024]{1,0:T(8,128)(2,1)} %get-tuple-element.52), channel_id=1, source_target_pairs={{0,4},{2,6},{4,0},{6,2},{8,12},{10,14},{12,8},{14,10},{1,5},{3,7},... | collective-permute-start | bytes 393224 | tf_op jit(solution)/shard_map/ppermute | solution.py:535
  56.7 2.4 %collective-permute-start.9 = (bf16[64,1024]{1,0:T(8,128)(2,1)}, bf16[64,1024]{1,0:T(8,128)(2,1)S(1)}, u32[]{:S(2)}, u32[]{:S(2)}) collective-permute-start(bf16[64,1024]{1,0:T(8,128)(2,1)} %get-tuple-element.53), channel_id=1, source_target_pairs={{0,8},{2,10},{4,12},{6,14},{8,0},{10,2},{12,4},{14,6},{1,9},{3,11}... | collective-permute-start | bytes 393224 | tf_op jit(solution)/shard_map/ppermute | solution.py:535
  59.3 1.5 %collective-permute-start.12 = (f32[64,256]{1,0:T(8,128)S(1)}, f32[64,256]{1,0:T(8,128)S(1)}, u32[]{:S(2)}, u32[]{:S(2)}) collective-permute-start(f32[64,256]{1,0:T(8,128)S(1)} %add.26.pay0_ref), channel_id=1, source_target_pairs={{0,16},{16,0},{1,17},{17,1},{2,18},{18,2},{3,19},{19,3},{4,20},{20... | collective-permute-start | bytes 196616 | tf_op jit(solution)/shard_map/ppermute | solution.py:659
  60.8 3.3 %all-to-all-done.1.first_ref = bf16[4,64,1024]{2,1,0:T(8,128)(2,1)S(1)} async-done(((bf16[4,64,1024]{2,1,0:T(8,128)(2,1)}), bf16[4,64,1024]{2,1,0:T(8,128)(2,1)S(1)}, u32[]{:S(2)}, u32[]{:S(2)}) %all-to-all-start.1) | async-done | bytes 524320 | tf_op jit(solution)/shard_map/all_to_all | solution.py:541
  64.1 2.2 %fetch_weights.1.weight_ref = bf16[8,1024,256]{2,1,0:T(8,128)(2,1)S(1)} custom-call(bf16[8,1024,256]{2,1,0:T(8,128)(2,1)} %get-tuple-element.56.weight_in_ref), custom_call_target="tpu_custom_call" | custom-call | tf_op jit(solution)/shard_map/fetch_weights/pallas_call | solution.py:664
  66.3 6.2 %collective-permute-done.9.second2_ref = bf16[64,1024]{1,0:T(8,128)(2,1)S(1)} collective-permute-done((bf16[64,1024]{1,0:T(8,128)(2,1)}, bf16[64,1024]{1,0:T(8,128)(2,1)S(1)}, u32[]{:S(2)}, u32[]{:S(2)}) %collective-permute-start.9) | collective-permute-done | bytes 131104 | tf_op jit(solution)/shard_map/ppermute | solution.py:535
  72.5 2.6 %token_sums.1 = (f32[8,2048]{1,0:T(8,128)S(1)}, f32[8,2048]{1,0:T(8,128)S(1)}) custom-call(f32[64,1024]{1,0:T(8,128)S(1)} %get-tuple-element.44.first_keep_ref, bf16[4,64,1024]{2,1,0:T(8,128)(2,1)S(1)} %all-to-all-done.1.first_ref, f32[64,1024]{1,0:T(8,128)S(1)} %copy-done, bf16[64,1024]{1,0:T(8,128)(2,1)S(1)} %collective-permute-done.8.second1_ref, ...), custom_call_target="tpu_custom_call" | custom-call | tf_op jit(solution)/shard_map/token_sums/pallas_call | solution.py:675
  75.2 1.2 %collective-permute-done.14 = f32[8,2048]{1,0:T(8,128)S(1)} collective-permute-done((f32[8,2048]{1,0:T(8,128)S(1)}, f32[8,2048]{1,0:T(8,128)S(1)}, u32[]{:S(2)}, u32[]{:S(2)}) %collective-permute-start.14) | collective-permute-done | bytes 65568 | tf_op jit(solution)/shard_map/ppermute | solution.py:538
  76.5 1.5 %collective-permute-start.15 = (bf16[8,2048]{1,0:T(8,128)(2,1)S(1)}, bf16[8,2048]{1,0:T(8,128)(2,1)S(1)}, u32[]{:S(2)}, u32[]{:S(2)}) collective-permute-start(bf16[8,2048]{1,0:T(8,128)(2,1)S(1)} %get-tuple-element.61), channel_id=1, source_target_pairs={{0,2},{2,0},{4,6},{6,4},{8,10},{10,8},{12,14},{14,12},{1,3},{3,1},... | collective-permute-start | bytes 98312 | tf_op jit(solution)/shard_map/ppermute | solution.py:535
  78.0 2.4 %collective-permute-done.15 = bf16[8,2048]{1,0:T(8,128)(2,1)S(1)} collective-permute-done((bf16[8,2048]{1,0:T(8,128)(2,1)S(1)}, bf16[8,2048]{1,0:T(8,128)(2,1)S(1)}, u32[]{:S(2)}, u32[]{:S(2)}) %collective-permute-start.15) | collective-permute-done | bytes 32800 | tf_op jit(solution)/shard_map/ppermute | solution.py:535
  80.5 1.6 %collective-permute-start.18 = (bf16[8,2048]{1,0:T(8,128)(2,1)S(1)}, bf16[8,2048]{1,0:T(8,128)(2,1)S(1)}, u32[]{:S(2)}, u32[]{:S(2)}) collective-permute-start(bf16[8,2048]{1,0:T(8,128)(2,1)S(1)} %fusion), channel_id=1, source_target_pairs={{0,12},{2,14},{4,8},{6,10},{8,4},{10,6},{12,0},{14,2},{1,13},{3,15... | collective-permute-start | bytes 98312 | tf_op jit(solution)/shard_map/ppermute | solution.py:535
  82.1 2.9 %collective-permute-start.17 = (bf16[8,2048]{1,0:T(8,128)(2,1)S(1)}, bf16[8,2048]{1,0:T(8,128)(2,1)S(1)}, u32[]{:S(2)}, u32[]{:S(2)}) collective-permute-start(bf16[8,2048]{1,0:T(8,128)(2,1)S(1)} %fusion), channel_id=1, source_target_pairs={{0,8},{2,10},{4,12},{6,14},{8,0},{10,2},{12,4},{14,6},{1,9},{3,11}... | collective-permute-start | bytes 98312 | tf_op jit(solution)/shard_map/ppermute | solution.py:535
  85.0 1.6 %collective-permute-done.18 = bf16[8,2048]{1,0:T(8,128)(2,1)S(1)} collective-permute-done((bf16[8,2048]{1,0:T(8,128)(2,1)S(1)}, bf16[8,2048]{1,0:T(8,128)(2,1)S(1)}, u32[]{:S(2)}, u32[]{:S(2)}) %collective-permute-start.18) | collective-permute-done | bytes 32800 | tf_op jit(solution)/shard_map/ppermute | solution.py:535
  87.3 1.6 %collective-permute-done.16 = bf16[8,2048]{1,0:T(8,128)(2,1)S(1)} collective-permute-done((bf16[8,2048]{1,0:T(8,128)(2,1)S(1)}, bf16[8,2048]{1,0:T(8,128)(2,1)S(1)}, u32[]{:S(2)}, u32[]{:S(2)}) %collective-permute-start.16) | collective-permute-done | bytes 32800 | tf_op jit(solution)/shard_map/ppermute | solution.py:535
  89.0 1.2 %collective-permute-done.19.theirs_ref = bf16[8,2048]{1,0:T(8,128)(2,1)S(1)} collective-permute-done((bf16[8,2048]{1,0:T(8,128)(2,1)S(1)}, bf16[8,2048]{1,0:T(8,128)(2,1)S(1)}, u32[]{:S(2)}, u32[]{:S(2)}) %collective-permute-start.19) | collective-permute-done | bytes 32800 | tf_op jit(solution)/shard_map/ppermute | solution.py:538
  90.2 2.1 %products.1 = f32[16,1024]{1,0:T(8,128)} custom-call(bf16[8,2048]{1,0:T(8,128)(2,1)S(1)} %add_convert_fusion.mine_ref, bf16[8,2048]{1,0:T(8,128)(2,1)S(1)} %collective-permute-done.19.theirs_ref, bf16[8,1024,256]{2,1,0:T(8,128)(2,1)S(1)} %fetch_weights.1.weight_ref), custom_call_target="tpu_custom_call" | custom-call | tf_op jit(solution)/shard_map/products/pallas_call | solution.py:697
  (41 shorter events, 2.4 us)
Async XLA Ops:
  0.0 10.9 %copy-start.2 = (s32[160]{0:T(256)S(1)}, s32[160]{0:T(256)}, u32[]{:S(2)}) copy-start(s32[160]{0:T(256)} %param.16) | copy-start | bytes 1924
  0.0 10.9 %copy-start.3 = (s32[160]{0:T(256)S(1)}, s32[160]{0:T(256)}, u32[]{:S(2)}) copy-start(s32[160]{0:T(256)} %param.14) | copy-start | bytes 1924
  0.0 10.9 %copy-start.4 = (s32[160]{0:T(256)S(1)}, s32[160]{0:T(256)}, u32[]{:S(2)}) copy-start(s32[160]{0:T(256)} %param.12) | copy-start | bytes 1924
  2.4 6.5 %copy-start.6 = (bf16[48,4096]{1,0:T(8,128)(2,1)S(1)}, bf16[48,4096]{1,0:T(8,128)(2,1)}, u32[]{:S(2)}) copy-start(bf16[48,4096]{1,0:T(8,128)(2,1)} %get-tuple-element.34) | copy-start | bytes 1179652
  2.4 8.0 %copy-start.5 = (bf16[64,4096]{1,0:T(8,128)(2,1)S(1)}, bf16[64,4096]{1,0:T(8,128)(2,1)}, u32[]{:S(2)}) copy-start(bf16[64,4096]{1,0:T(8,128)(2,1)} %get-tuple-element.33) | copy-start | bytes 1572868
  2.5 35.0 %all-to-all-start = ((bf16[4,64,2048]{2,1,0:T(8,128)(2,1)}), bf16[4,64,2048]{2,1,0:T(8,128)(2,1)S(1)}, u32[]{:S(2)}, u32[]{:S(2)}) async-start(bf16[4,64,2048]{2,1,0:T(8,128)(2,1)} %get-tuple-element.37), calls=%async_computation | async-start | bytes 2097152 | tf_op jit(solution)/shard_map/all_to_all | solution.py:541
  8.9 12.0 %collective-permute-start.2 = (bf16[48,4096]{1,0:T(8,128)(2,1)S(1)}, bf16[48,4096]{1,0:T(8,128)(2,1)S(1)}, u32[]{:S(2)}, u32[]{:S(2)}) collective-permute-start(bf16[48,4096]{1,0:T(8,128)(2,1)S(1)} %copy-done.6), channel_id=1, source_target_pairs={{0,2},{2,0},{4,6},{6,4},{8,10},{10,8},{12,14},{14,12},{1,3},{3,1},... | collective-permute-start | bytes 1179656 | tf_op jit(solution)/shard_map/ppermute | solution.py:535
  10.4 27.1 %collective-permute-start.1 = (bf16[64,4096]{1,0:T(8,128)(2,1)S(1)}, bf16[64,4096]{1,0:T(8,128)(2,1)S(1)}, u32[]{:S(2)}, u32[]{:S(2)}) collective-permute-start(bf16[64,4096]{1,0:T(8,128)(2,1)S(1)} %copy-done.5), channel_id=1, source_target_pairs={{0,2},{2,0},{4,6},{6,4},{8,10},{10,8},{12,14},{14,12},{1,3},{3,1},... | collective-permute-start | bytes 1572872 | tf_op jit(solution)/shard_map/ppermute | solution.py:535
  11.7 21.2 %copy-start.1 = (s32[3,256]{1,0:T(4,128)S(1)}, s32[3,256]{1,0:T(4,128)}, u32[]{:S(2)}) copy-start(s32[3,256]{1,0:T(4,128)} %select_reduce_fusion.inv_ref) | copy-start | bytes 9220
  21.0 16.5 %collective-permute-start.3 = (bf16[48,4096]{1,0:T(8,128)(2,1)S(1)}, bf16[48,4096]{1,0:T(8,128)(2,1)S(1)}, u32[]{:S(2)}, u32[]{:S(2)}) collective-permute-start(bf16[48,4096]{1,0:T(8,128)(2,1)S(1)} %collective-permute-done.2.a_in_ref), channel_id=1, source_target_pairs={{0,16},{16,0},{1,17},{17,1},{2,18},{18,2},{3,19},{19,3},{4,20},{20... | collective-permute-start | bytes 1179656 | tf_op jit(solution)/shard_map/ppermute | solution.py:600
  22.5 5.0 %collective-permute-start.4 = (f32[64,256]{1,0:T(8,128)}, f32[64,256]{1,0:T(8,128)S(1)}, u32[]{:S(2)}, u32[]{:S(2)}) collective-permute-start(f32[64,256]{1,0:T(8,128)} %get-tuple-element.38), channel_id=1, source_target_pairs={{0,4},{2,6},{4,0},{6,2},{8,12},{10,14},{12,8},{14,10},{1,5},{3,7},... | collective-permute-start | bytes 196616 | tf_op jit(solution)/shard_map/ppermute | solution.py:535
  28.3 9.1 %collective-permute-start.5 = (f32[64,256]{1,0:T(8,128)S(1)}, f32[64,256]{1,0:T(8,128)S(1)}, u32[]{:S(2)}, u32[]{:S(2)}) collective-permute-start(f32[64,256]{1,0:T(8,128)S(1)} %add.24), channel_id=1, source_target_pairs={{0,8},{2,10},{4,12},{6,14},{8,0},{10,2},{12,4},{14,6},{1,9},{3,11}... | collective-permute-start | bytes 196616 | tf_op jit(solution)/shard_map/ppermute | solution.py:535
  32.9 4.6 %collective-permute-start = (s32[3,256]{1,0:T(4,128)S(1)}, s32[3,256]{1,0:T(4,128)S(1)}, u32[]{:S(2)}, u32[]{:S(2)}) collective-permute-start(s32[3,256]{1,0:T(4,128)S(1)} %copy-done.1), channel_id=1, source_target_pairs={{0,2},{2,0},{4,6},{6,4},{8,10},{10,8},{12,14},{14,12},{1,3},{3,1},... | collective-permute-start | bytes 9224 | tf_op jit(solution)/shard_map/ppermute | solution.py:535
  44.8 5.1 %collective-permute-start.6 = (bf16[4,1024,256]{2,1,0:T(8,128)(2,1)}, bf16[4,1024,256]{2,1,0:T(8,128)(2,1)}, u32[]{:S(2)}, u32[]{:S(2)}) collective-permute-start(bf16[4,1024,256]{2,1,0:T(8,128)(2,1)} %get-tuple-element.47), channel_id=1, source_target_pairs={{0,1},{1,0},{2,3},{3,2},{4,5},{5,4},{6,7},{7,6},{8,9},{9,8},{10,11... | collective-permute-start | bytes 6291464 | tf_op jit(solution)/shard_map/ppermute | solution.py:538
  44.8 19.3 %all-to-all-start.1 = ((bf16[4,64,1024]{2,1,0:T(8,128)(2,1)}), bf16[4,64,1024]{2,1,0:T(8,128)(2,1)S(1)}, u32[]{:S(2)}, u32[]{:S(2)}) async-start(bf16[4,64,1024]{2,1,0:T(8,128)(2,1)} %get-tuple-element.45), calls=%async_computation.1 | async-start | bytes 1048576 | tf_op jit(solution)/shard_map/all_to_all | solution.py:541
  48.3 6.3 %collective-permute-start.7 = (f32[64,256]{1,0:T(8,128)S(1)}, f32[64,256]{1,0:T(8,128)S(1)}, u32[]{:S(2)}, u32[]{:S(2)}) collective-permute-start(f32[64,256]{1,0:T(8,128)S(1)} %add.25), channel_id=1, source_target_pairs={{0,2},{2,0},{4,6},{6,4},{8,10},{10,8},{12,14},{14,12},{1,3},{3,1},... | collective-permute-start | bytes 196616 | tf_op jit(solution)/shard_map/ppermute | solution.py:535
  54.7 11.7 %collective-permute-start.8 = (bf16[64,1024]{1,0:T(8,128)(2,1)}, bf16[64,1024]{1,0:T(8,128)(2,1)S(1)}, u32[]{:S(2)}, u32[]{:S(2)}) collective-permute-start(bf16[64,1024]{1,0:T(8,128)(2,1)} %get-tuple-element.52), channel_id=1, source_target_pairs={{0,4},{2,6},{4,0},{6,2},{8,12},{10,14},{12,8},{14,10},{1,5},{3,7},... | collective-permute-start | bytes 393224 | tf_op jit(solution)/shard_map/ppermute | solution.py:535
  56.7 4.1 %collective-permute-start.11 = (f32[64,256]{1,0:T(8,128)S(1)}, f32[64,256]{1,0:T(8,128)S(1)}, u32[]{:S(2)}, u32[]{:S(2)}) collective-permute-start(f32[64,256]{1,0:T(8,128)S(1)} %add.26.pay0_ref), channel_id=1, source_target_pairs={{0,1},{1,0},{2,3},{3,2},{4,5},{5,4},{6,7},{7,6},{8,9},{9,8},{10,11... | collective-permute-start | bytes 196616 | tf_op jit(solution)/shard_map/ppermute | solution.py:538
  56.7 15.8 %collective-permute-start.9 = (bf16[64,1024]{1,0:T(8,128)(2,1)}, bf16[64,1024]{1,0:T(8,128)(2,1)S(1)}, u32[]{:S(2)}, u32[]{:S(2)}) collective-permute-start(bf16[64,1024]{1,0:T(8,128)(2,1)} %get-tuple-element.53), channel_id=1, source_target_pairs={{0,8},{2,10},{4,12},{6,14},{8,0},{10,2},{12,4},{14,6},{1,9},{3,11}... | collective-permute-start | bytes 393224 | tf_op jit(solution)/shard_map/ppermute | solution.py:535
  59.2 13.4 %copy-start = (f32[64,1024]{1,0:T(8,128)S(1)}, f32[64,1024]{1,0:T(8,128)}, u32[]{:S(2)}) copy-start(f32[64,1024]{1,0:T(8,128)} %get-tuple-element.51.second_keep_ref) | copy-start | bytes 786436
  59.2 13.4 %collective-permute-start.10 = (bf16[64,1024]{1,0:T(8,128)(2,1)}, bf16[64,1024]{1,0:T(8,128)(2,1)S(1)}, u32[]{:S(2)}, u32[]{:S(2)}) collective-permute-start(bf16[64,1024]{1,0:T(8,128)(2,1)} %get-tuple-element.54), channel_id=1, source_target_pairs={{0,12},{2,14},{4,8},{6,10},{8,4},{10,6},{12,0},{14,2},{1,13},{3,15... | collective-permute-start | bytes 393224 | tf_op jit(solution)/shard_map/ppermute | solution.py:535
  59.3 7.0 %collective-permute-start.12 = (f32[64,256]{1,0:T(8,128)S(1)}, f32[64,256]{1,0:T(8,128)S(1)}, u32[]{:S(2)}, u32[]{:S(2)}) collective-permute-start(f32[64,256]{1,0:T(8,128)S(1)} %add.26.pay0_ref), channel_id=1, source_target_pairs={{0,16},{16,0},{1,17},{17,1},{2,18},{18,2},{3,19},{19,3},{4,20},{20... | collective-permute-start | bytes 196616 | tf_op jit(solution)/shard_map/ppermute | solution.py:659
  60.8 5.5 %collective-permute-start.13 = (f32[64,256]{1,0:T(8,128)S(1)}, f32[64,256]{1,0:T(8,128)S(1)}, u32[]{:S(2)}, u32[]{:S(2)}) collective-permute-start(f32[64,256]{1,0:T(8,128)S(1)} %add.26.pay0_ref), channel_id=1, source_target_pairs={{0,17},{1,16},{16,1},{17,0},{2,19},{3,18},{18,3},{19,2},{4,21},{5,... | collective-permute-start | bytes 196616 | tf_op jit(solution)/shard_map/ppermute | solution.py:660
  75.2 1.3 %collective-permute-start.14 = (f32[8,2048]{1,0:T(8,128)S(1)}, f32[8,2048]{1,0:T(8,128)S(1)}, u32[]{:S(2)}, u32[]{:S(2)}) collective-permute-start(f32[8,2048]{1,0:T(8,128)S(1)} %get-tuple-element.59), channel_id=1, source_target_pairs={{0,1},{1,0},{2,3},{3,2},{4,5},{5,4},{6,7},{7,6},{8,9},{9,8},{10,11... | collective-permute-start | bytes 196616 | tf_op jit(solution)/shard_map/ppermute | solution.py:538
  76.5 4.0 %collective-permute-start.15 = (bf16[8,2048]{1,0:T(8,128)(2,1)S(1)}, bf16[8,2048]{1,0:T(8,128)(2,1)S(1)}, u32[]{:S(2)}, u32[]{:S(2)}) collective-permute-start(bf16[8,2048]{1,0:T(8,128)(2,1)S(1)} %get-tuple-element.61), channel_id=1, source_target_pairs={{0,2},{2,0},{4,6},{6,4},{8,10},{10,8},{12,14},{14,12},{1,3},{3,1},... | collective-permute-start | bytes 98312 | tf_op jit(solution)/shard_map/ppermute | solution.py:535
  80.5 6.1 %collective-permute-start.18 = (bf16[8,2048]{1,0:T(8,128)(2,1)S(1)}, bf16[8,2048]{1,0:T(8,128)(2,1)S(1)}, u32[]{:S(2)}, u32[]{:S(2)}) collective-permute-start(bf16[8,2048]{1,0:T(8,128)(2,1)S(1)} %fusion), channel_id=1, source_target_pairs={{0,12},{2,14},{4,8},{6,10},{8,4},{10,6},{12,0},{14,2},{1,13},{3,15... | collective-permute-start | bytes 98312 | tf_op jit(solution)/shard_map/ppermute | solution.py:535
  82.1 5.2 %collective-permute-start.17 = (bf16[8,2048]{1,0:T(8,128)(2,1)S(1)}, bf16[8,2048]{1,0:T(8,128)(2,1)S(1)}, u32[]{:S(2)}, u32[]{:S(2)}) collective-permute-start(bf16[8,2048]{1,0:T(8,128)(2,1)S(1)} %fusion), channel_id=1, source_target_pairs={{0,8},{2,10},{4,12},{6,14},{8,0},{10,2},{12,4},{14,6},{1,9},{3,11}... | collective-permute-start | bytes 98312 | tf_op jit(solution)/shard_map/ppermute | solution.py:535
  85.0 3.9 %collective-permute-start.16 = (bf16[8,2048]{1,0:T(8,128)(2,1)S(1)}, bf16[8,2048]{1,0:T(8,128)(2,1)S(1)}, u32[]{:S(2)}, u32[]{:S(2)}) collective-permute-start(bf16[8,2048]{1,0:T(8,128)(2,1)S(1)} %fusion), channel_id=1, source_target_pairs={{0,4},{2,6},{4,0},{6,2},{8,12},{10,14},{12,8},{14,10},{1,5},{3,7},... | collective-permute-start | bytes 98312 | tf_op jit(solution)/shard_map/ppermute | solution.py:535
  88.9 1.3 %collective-permute-start.19 = (bf16[8,2048]{1,0:T(8,128)(2,1)S(1)}, bf16[8,2048]{1,0:T(8,128)(2,1)S(1)}, u32[]{:S(2)}, u32[]{:S(2)}) collective-permute-start(bf16[8,2048]{1,0:T(8,128)(2,1)S(1)} %add_convert_fusion.mine_ref), channel_id=1, source_target_pairs={{0,1},{1,0},{2,3},{3,2},{4,5},{5,4},{6,7},{7,6},{8,9},{9,8},{10,11... | collective-permute-start | bytes 98312 | tf_op jit(solution)/shard_map/ppermute | solution.py:538

commit v15 on v13

--- a/solution.py
+++ b/solution.py
@@ -412,16 +412,22 @@
 ):
     owner, unused_quarter, unused_side, core = position()
     zone = owner // 2
-    loads = [
-        pltpu.make_async_copy(tokens_in_ref, tokens_ref, in_sem.at[0]),
-        pltpu.make_async_copy(weight_in_ref.at[pl.ds(4 - 4 * core, 4)], own_ref, in_sem.at[1]),
-        pltpu.make_async_copy(near_in_ref, near_ref, in_sem.at[2]),
-    ]
-    for load in loads:
-        load.start()
-    for load in loads:
-        load.wait()
+    token_load = pltpu.make_async_copy(tokens_in_ref, tokens_ref, in_sem.at[0])
+    token_load.start()
+    loads = []
     for chunk in range(4):
+        source = weight_in_ref.at[4 - 4 * core + chunk]
+        own_load = pltpu.make_async_copy(source, own_ref.at[chunk], in_sem.at[1 + chunk])
+        near_load = pltpu.make_async_copy(
+            near_in_ref.at[chunk], near_ref.at[chunk], in_sem.at[5 + chunk]
+        )
+        own_load.start()
+        near_load.start()
+        loads.append((own_load, near_load))
+    token_load.wait()
+    for chunk in range(4):
+        for load in loads[chunk]:
+            load.wait()
         total = dot(tokens_ref[0], own_ref[chunk]) + dot(tokens_ref[1], near_ref[chunk])
         cols = slice(256 * chunk, 256 * (chunk + 1))
         total_ref[...] = total
@@ -635,12 +641,12 @@
             pltpu.VMEM((4, 1024, 256), BF),
             pltpu.VMEM((2, 256, 1024), BF),
             pltpu.VMEM((256, 256), F32),
-            pltpu.SemaphoreType.DMA((3,)),
+            pltpu.SemaphoreType.DMA((9,)),
         ],
         compiler_params=params(56),
         name="second_partial",
     )(core_flip(near_weights), weights, shuffled_tokens)
-    second_back = [owner_flip(second_sent[flip - 1], 2 * flip) for flip in (1, 2, 3)]
+    second_back = [owner_flip(second_sent[flip - 1], 2 * flip) for flip in (2, 3, 1)]
 
     across = owner_flip(payload, 1)
     second_keep, across = lax.optimization_barrier((second_keep, across))

time: 91.2 us -> 91.2 us (level)
    ppermute x13, waiting for transfers between devices: 19.9 us -> 14.6 us  [owner_flip(): return lax.ppermute(value, 'fsdp', [(i, i ^ bits) for i in range(8)])]
    all_to_all x2, waiting for transfers between devices: 3.3 us -> 8.5 us  [zone_exchange(): lax.all_to_all(value, 'fsdp', split_axis=0, concat_axis=0, tiled=True, ax...]
  transfers between devices with their start and end apart: 22 -> 22, of which waited for: 10 -> 11; matrix products, arithmetic and copies ran while one was open for 2% -> 2% of each run, Pallas kernels for 16% -> 17%
where the time goes in v15:
time: 91.2 us; the launch traced here: 90.8 us
  starting transfers between devices  35.8 us (39%)
  Pallas kernels  27.5 us (30%)
  waiting for transfers between devices  25.5 us (28%)
  other arithmetic  1.67 us (2%)
    ppermute x13, starting transfers between devices, owner_flip(): return lax.ppermute(value, 'fsdp', [(i, i ^ bits) for i in range(8)])  22.5 us
    ppermute x13, waiting for transfers between devices, owner_flip(): return lax.ppermute(value, 'fsdp', [(i, i ^ bits) for i in range(8)])  14.6 us
    all_to_all x2, starting transfers between devices, zone_exchange(): lax.all_to_all(value, 'fsdp', split_axis=0, concat_axis=0, tiled=True, ax...  9.94 us
    all_to_all x2, waiting for transfers between devices, zone_exchange(): lax.all_to_all(value, 'fsdp', split_axis=0, concat_axis=0, tiled=True, ax...  8.5 us
    pallas_call x1, Pallas kernels, pair_split(): pl.pallas_call(own_kernel, out_shape=(jax.ShapeDtypeStruct((8, 1024, 256)...  7.55 us
    pallas_call x1, Pallas kernels, pair_split(): pl.pallas_call(first_kernel, out_shape=(jax.ShapeDtypeStruct((64, 1024),...  5.39 us
    pallas_call x1, Pallas kernels, pair_split(): pl.pallas_call(second_kernel, out_shape=(jax.ShapeDtypeStruct((64, 1024),...  5.32 us
    pallas_call x1, Pallas kernels, pair_split(): pl.pallas_call(middle_kernel, out_shape=(jax.ShapeDtypeStruct((8, 2048),...  2.61 us
  transfers between devices with their start and end apart: 22, of which 11 were waited for; matrix products, arithmetic and copies ran while one was open for 2% of the time, Pallas kernels for 17%

profile of v15, /device:TPU:0, one launch (start us, length us, event | category | flops | bytes accessed | tf_op | source)
XLA Modules:
  0.0 90.8 jit_solution(178103202072002594)
XLA Ops:
  0.0 2.4 %head.1 = (bf16[4,64,2048]{2,1,0:T(8,128)(2,1)}, bf16[48,4096]{1,0:T(8,128)(2,1)}, bf16[64,4096]{1,0:T(8,128)(2,1)}) custom-call(bf16[64,8192]{1,0:T(8,128)(2,1)} %tok_in_ref.1, bf16[160,4096]{1,0:T(8,128)(2,1)} %gate_ref.3, bf16[160,4096]{1,0:T(8,128)(2,1)} %up_ref.3), custom_call_target="tpu_custom_call" | custom-call | tf_op jit(solution)/shard_map/head/pallas_call | solution.py:548
  2.5 6.5 %all-to-all-start = ((bf16[4,64,2048]{2,1,0:T(8,128)(2,1)}), bf16[4,64,2048]{2,1,0:T(8,128)(2,1)S(1)}, u32[]{:S(2)}, u32[]{:S(2)}) async-start(bf16[4,64,2048]{2,1,0:T(8,128)(2,1)} %get-tuple-element.37), calls=%async_computation | async-start | bytes 2097152 | tf_op jit(solution)/shard_map/all_to_all | solution.py:539
  8.9 1.5 %collective-permute-start.2 = (bf16[48,4096]{1,0:T(8,128)(2,1)S(1)}, bf16[48,4096]{1,0:T(8,128)(2,1)S(1)}, u32[]{:S(2)}, u32[]{:S(2)}) collective-permute-start(bf16[48,4096]{1,0:T(8,128)(2,1)S(1)} %copy-done.6), channel_id=1, source_target_pairs={{0,2},{2,0},{4,6},{6,4},{8,10},{10,8},{12,14},{14,12},{1,3},{3,1},... | collective-permute-start | bytes 1179656 | tf_op jit(solution)/shard_map/ppermute | solution.py:533
  11.0 0.7 select_reduce_fusion.inv_ref
  11.7 7.5 %own_blocks.1 = (bf16[8,1024,256]{2,1,0:T(8,128)(2,1)}, f32[64,256]{1,0:T(8,128)}) custom-call(s32[3,256]{1,0:T(4,128)} %select_reduce_fusion.inv_ref, bf16[160,4096]{1,0:T(8,128)(2,1)} %gate_ref.3, bf16[160,4096]{1,0:T(8,128)(2,1)} %up_ref.3, bf16[160,4096]{1,0:T(8,128)(2,1)} %down_ref.1, bf16[32,1024]{1,0:T(8,128)(2,1)} %sketch_ref.1, ...), custom_call_target="tpu_custom_call" | custom-call | tf_op jit(solution)/shard_map/own_blocks/pallas_call | solution.py:575
  19.3 1.7 %collective-permute-done.2.a_in_ref = bf16[48,4096]{1,0:T(8,128)(2,1)S(1)} collective-permute-done((bf16[48,4096]{1,0:T(8,128)(2,1)S(1)}, bf16[48,4096]{1,0:T(8,128)(2,1)S(1)}, u32[]{:S(2)}, u32[]{:S(2)}) %collective-permute-start.2) | collective-permute-done | bytes 393248 | tf_op jit(solution)/shard_map/ppermute | solution.py:533
  21.0 1.5 %collective-permute-start.3 = (bf16[48,4096]{1,0:T(8,128)(2,1)S(1)}, bf16[48,4096]{1,0:T(8,128)(2,1)S(1)}, u32[]{:S(2)}, u32[]{:S(2)}) collective-permute-start(bf16[48,4096]{1,0:T(8,128)(2,1)S(1)} %collective-permute-done.2.a_in_ref), channel_id=1, source_target_pairs={{0,16},{16,0},{1,17},{17,1},{2,18},{18,2},{3,19},{19,3},{4,20},{20... | collective-permute-start | bytes 1179656 | tf_op jit(solution)/shard_map/ppermute | solution.py:598
  22.5 2.0 %collective-permute-start.4 = (f32[64,256]{1,0:T(8,128)}, f32[64,256]{1,0:T(8,128)S(1)}, u32[]{:S(2)}, u32[]{:S(2)}) collective-permute-start(f32[64,256]{1,0:T(8,128)} %get-tuple-element.38), channel_id=1, source_target_pairs={{0,4},{2,6},{4,0},{6,2},{8,12},{10,14},{12,8},{14,10},{1,5},{3,7},... | collective-permute-start | bytes 196616 | tf_op jit(solution)/shard_map/ppermute | solution.py:533
  24.5 3.0 %collective-permute-done.4 = f32[64,256]{1,0:T(8,128)S(1)} collective-permute-done((f32[64,256]{1,0:T(8,128)}, f32[64,256]{1,0:T(8,128)S(1)}, u32[]{:S(2)}, u32[]{:S(2)}) %collective-permute-start.4) | collective-permute-done | bytes 65568 | tf_op jit(solution)/shard_map/ppermute | solution.py:533
  27.5 0.8 add.24
  28.3 4.6 %collective-permute-start.5 = (f32[64,256]{1,0:T(8,128)S(1)}, f32[64,256]{1,0:T(8,128)S(1)}, u32[]{:S(2)}, u32[]{:S(2)}) collective-permute-start(f32[64,256]{1,0:T(8,128)S(1)} %add.24), channel_id=1, source_target_pairs={{0,8},{2,10},{4,12},{6,14},{8,0},{10,2},{12,4},{14,6},{1,9},{3,11}... | collective-permute-start | bytes 196616 | tf_op jit(solution)/shard_map/ppermute | solution.py:533
  32.9 1.5 %collective-permute-start = (s32[3,256]{1,0:T(4,128)S(1)}, s32[3,256]{1,0:T(4,128)S(1)}, u32[]{:S(2)}, u32[]{:S(2)}) collective-permute-start(s32[3,256]{1,0:T(4,128)S(1)} %copy-done.1), channel_id=1, source_target_pairs={{0,2},{2,0},{4,6},{6,4},{8,10},{10,8},{12,14},{14,12},{1,3},{3,1},... | collective-permute-start | bytes 9224 | tf_op jit(solution)/shard_map/ppermute | solution.py:533
  34.4 3.1 %collective-permute-done.5 = f32[64,256]{1,0:T(8,128)S(1)} collective-permute-done((f32[64,256]{1,0:T(8,128)S(1)}, f32[64,256]{1,0:T(8,128)S(1)}, u32[]{:S(2)}, u32[]{:S(2)}) %collective-permute-start.5) | collective-permute-done | bytes 65568 | tf_op jit(solution)/shard_map/ppermute | solution.py:533
  37.5 5.4 %first_partial.1 = (f32[64,1024]{1,0:T(8,128)S(1)}, bf16[4,64,1024]{2,1,0:T(8,128)(2,1)}, bf16[4,1024,256]{2,1,0:T(8,128)(2,1)}, bf16[2,256,1024]{2,1,0:T(8,128)(2,1)}) custom-call(s32[3,256]{1,0:T(4,128)S(1)} %collective-permute-done.inv_ref, bf16[48,4096]{1,0:T(8,128)(2,1)S(1)} %collective-permute-done.2.a_in_ref, ...), custom_call_target="tpu_custom_call" | custom-call | tf_op jit(solution)/shard_map/first_partial/pallas_call | solution.py:605
  43.0 3.5 %all-to-all-start.1 = ((bf16[4,64,1024]{2,1,0:T(8,128)(2,1)}), bf16[4,64,1024]{2,1,0:T(8,128)(2,1)S(1)}, u32[]{:S(2)}, u32[]{:S(2)}) async-start(bf16[4,64,1024]{2,1,0:T(8,128)(2,1)} %get-tuple-element.45), calls=%async_computation.1 | async-start | bytes 1048576 | tf_op jit(solution)/shard_map/all_to_all | solution.py:539
  46.5 1.6 %collective-permute-start.7 = (f32[64,256]{1,0:T(8,128)S(1)}, f32[64,256]{1,0:T(8,128)S(1)}, u32[]{:S(2)}, u32[]{:S(2)}) collective-permute-start(f32[64,256]{1,0:T(8,128)S(1)} %add.25), channel_id=1, source_target_pairs={{0,2},{2,0},{4,6},{6,4},{8,10},{10,8},{12,14},{14,12},{1,3},{3,1},... | collective-permute-start | bytes 196616 | tf_op jit(solution)/shard_map/ppermute | solution.py:533
  48.0 5.3 %second_partial.1 = (f32[64,1024]{1,0:T(8,128)}, bf16[64,1024]{1,0:T(8,128)(2,1)}, bf16[64,1024]{1,0:T(8,128)(2,1)}, bf16[64,1024]{1,0:T(8,128)(2,1)}) custom-call(bf16[4,1024,256]{2,1,0:T(8,128)(2,1)} %collective-permute-done.6.near_in_ref, bf16[8,1024,256]{2,1,0:T(8,128)(2,1)} %get-tuple-element.56.weight_in_ref, ...), custom_call_target="tpu_custom_call" | custom-call | tf_op jit(solution)/shard_map/second_partial/pallas_call | solution.py:633
  53.4 2.9 %collective-permute-start.8 = (bf16[64,1024]{1,0:T(8,128)(2,1)}, bf16[64,1024]{1,0:T(8,128)(2,1)S(1)}, u32[]{:S(2)}, u32[]{:S(2)}) collective-permute-start(bf16[64,1024]{1,0:T(8,128)(2,1)} %get-tuple-element.52), channel_id=1, source_target_pairs={{0,8},{2,10},{4,12},{6,14},{8,0},{10,2},{12,4},{14,6},{1,9},{3,11}... | collective-permute-start | bytes 393224 | tf_op jit(solution)/shard_map/ppermute | solution.py:533
  56.4 1.5 %collective-permute-start.9 = (bf16[64,1024]{1,0:T(8,128)(2,1)}, bf16[64,1024]{1,0:T(8,128)(2,1)S(1)}, u32[]{:S(2)}, u32[]{:S(2)}) collective-permute-start(bf16[64,1024]{1,0:T(8,128)(2,1)} %get-tuple-element.53), channel_id=1, source_target_pairs={{0,12},{2,14},{4,8},{6,10},{8,4},{10,6},{12,0},{14,2},{1,13},{3,15... | collective-permute-start | bytes 393224 | tf_op jit(solution)/shard_map/ppermute | solution.py:533
  58.0 1.5 %collective-permute-start.12 = (f32[64,256]{1,0:T(8,128)S(1)}, f32[64,256]{1,0:T(8,128)S(1)}, u32[]{:S(2)}, u32[]{:S(2)}) collective-permute-start(f32[64,256]{1,0:T(8,128)S(1)} %add.26.pay0_ref), channel_id=1, source_target_pairs={{0,16},{16,0},{1,17},{17,1},{2,18},{18,2},{3,19},{19,3},{4,20},{20... | collective-permute-start | bytes 196616 | tf_op jit(solution)/shard_map/ppermute | solution.py:657
  59.5 8.5 %all-to-all-done.1.first_ref = bf16[4,64,1024]{2,1,0:T(8,128)(2,1)S(1)} async-done(((bf16[4,64,1024]{2,1,0:T(8,128)(2,1)}), bf16[4,64,1024]{2,1,0:T(8,128)(2,1)S(1)}, u32[]{:S(2)}, u32[]{:S(2)}) %all-to-all-start.1) | async-done | bytes 524320 | tf_op jit(solution)/shard_map/all_to_all | solution.py:539
  68.0 2.2 %fetch_weights.1.weight_ref = bf16[8,1024,256]{2,1,0:T(8,128)(2,1)S(1)} custom-call(bf16[8,1024,256]{2,1,0:T(8,128)(2,1)} %get-tuple-element.56.weight_in_ref), custom_call_target="tpu_custom_call" | custom-call | tf_op jit(solution)/shard_map/fetch_weights/pallas_call | solution.py:662
  71.0 2.6 %token_sums.1 = (f32[8,2048]{1,0:T(8,128)S(1)}, f32[8,2048]{1,0:T(8,128)S(1)}) custom-call(f32[64,1024]{1,0:T(8,128)S(1)} %get-tuple-element.44.first_keep_ref, bf16[4,64,1024]{2,1,0:T(8,128)(2,1)S(1)} %all-to-all-done.1.first_ref, f32[64,1024]{1,0:T(8,128)S(1)} %copy-done, bf16[64,1024]{1,0:T(8,128)(2,1)S(1)} %collective-permute-done.8.second1_ref, ...), custom_call_target="tpu_custom_call" | custom-call | tf_op jit(solution)/shard_map/token_sums/pallas_call | solution.py:673
  73.7 1.2 %collective-permute-done.14 = f32[8,2048]{1,0:T(8,128)S(1)} collective-permute-done((f32[8,2048]{1,0:T(8,128)S(1)}, f32[8,2048]{1,0:T(8,128)S(1)}, u32[]{:S(2)}, u32[]{:S(2)}) %collective-permute-start.14) | collective-permute-done | bytes 65568 | tf_op jit(solution)/shard_map/ppermute | solution.py:536
  75.0 3.6 %collective-permute-start.17 = (bf16[8,2048]{1,0:T(8,128)(2,1)S(1)}, bf16[8,2048]{1,0:T(8,128)(2,1)S(1)}, u32[]{:S(2)}, u32[]{:S(2)}) collective-permute-start(bf16[8,2048]{1,0:T(8,128)(2,1)S(1)} %get-tuple-element.61), channel_id=1, source_target_pairs={{0,6},{2,4},{4,2},{6,0},{8,14},{10,12},{12,10},{14,8},{1,7},{3,5},... | collective-permute-start | bytes 98312 | tf_op jit(solution)/shard_map/ppermute | solution.py:533
  78.6 0.6 collective-permute-start.15
  79.2 1.3 %collective-permute-done.17 = bf16[8,2048]{1,0:T(8,128)(2,1)S(1)} collective-permute-done((bf16[8,2048]{1,0:T(8,128)(2,1)S(1)}, bf16[8,2048]{1,0:T(8,128)(2,1)S(1)}, u32[]{:S(2)}, u32[]{:S(2)}) %collective-permute-start.17) | collective-permute-done | bytes 32800 | tf_op jit(solution)/shard_map/ppermute | solution.py:533
  80.5 2.0 %collective-permute-done.16 = bf16[8,2048]{1,0:T(8,128)(2,1)S(1)} collective-permute-done((bf16[8,2048]{1,0:T(8,128)(2,1)S(1)}, bf16[8,2048]{1,0:T(8,128)(2,1)S(1)}, u32[]{:S(2)}, u32[]{:S(2)}) %collective-permute-start.16) | collective-permute-done | bytes 32800 | tf_op jit(solution)/shard_map/ppermute | solution.py:533
  82.5 2.1 %collective-permute-start.18 = (bf16[8,2048]{1,0:T(8,128)(2,1)S(1)}, bf16[8,2048]{1,0:T(8,128)(2,1)S(1)}, u32[]{:S(2)}, u32[]{:S(2)}) collective-permute-start(bf16[8,2048]{1,0:T(8,128)(2,1)S(1)} %fusion), channel_id=1, source_target_pairs={{0,8},{2,10},{4,12},{6,14},{8,0},{10,2},{12,4},{14,6},{1,9},{3,11}... | collective-permute-start | bytes 98312 | tf_op jit(solution)/shard_map/ppermute | solution.py:533
  84.7 2.7 %collective-permute-done.18 = bf16[8,2048]{1,0:T(8,128)(2,1)S(1)} collective-permute-done((bf16[8,2048]{1,0:T(8,128)(2,1)S(1)}, bf16[8,2048]{1,0:T(8,128)(2,1)S(1)}, u32[]{:S(2)}, u32[]{:S(2)}) %collective-permute-start.18) | collective-permute-done | bytes 32800 | tf_op jit(solution)/shard_map/ppermute | solution.py:533
  87.5 1.2 %collective-permute-done.19.theirs_ref = bf16[8,2048]{1,0:T(8,128)(2,1)S(1)} collective-permute-done((bf16[8,2048]{1,0:T(8,128)(2,1)S(1)}, bf16[8,2048]{1,0:T(8,128)(2,1)S(1)}, u32[]{:S(2)}, u32[]{:S(2)}) %collective-permute-start.19) | collective-permute-done | bytes 32800 | tf_op jit(solution)/shard_map/ppermute | solution.py:536
  88.7 2.1 %products.1 = f32[16,1024]{1,0:T(8,128)} custom-call(bf16[8,2048]{1,0:T(8,128)(2,1)S(1)} %add_convert_fusion.mine_ref, bf16[8,2048]{1,0:T(8,128)(2,1)S(1)} %collective-permute-done.19.theirs_ref, bf16[8,1024,256]{2,1,0:T(8,128)(2,1)S(1)} %fetch_weights.1.weight_ref), custom_call_target="tpu_custom_call" | custom-call | tf_op jit(solution)/shard_map/products/pallas_call | solution.py:697
  (41 shorter events, 1.9 us)
Async XLA Ops:
  0.0 10.9 %copy-start.2 = (s32[160]{0:T(256)S(1)}, s32[160]{0:T(256)}, u32[]{:S(2)}) copy-start(s32[160]{0:T(256)} %param.16) | copy-start | bytes 1924
  0.0 10.9 %copy-start.3 = (s32[160]{0:T(256)S(1)}, s32[160]{0:T(256)}, u32[]{:S(2)}) copy-start(s32[160]{0:T(256)} %param.14) | copy-start | bytes 1924
  0.0 10.9 %copy-start.4 = (s32[160]{0:T(256)S(1)}, s32[160]{0:T(256)}, u32[]{:S(2)}) copy-start(s32[160]{0:T(256)} %param.12) | copy-start | bytes 1924
  2.4 6.5 %copy-start.6 = (bf16[48,4096]{1,0:T(8,128)(2,1)S(1)}, bf16[48,4096]{1,0:T(8,128)(2,1)}, u32[]{:S(2)}) copy-start(bf16[48,4096]{1,0:T(8,128)(2,1)} %get-tuple-element.34) | copy-start | bytes 1179652
  2.4 8.0 %copy-start.5 = (bf16[64,4096]{1,0:T(8,128)(2,1)S(1)}, bf16[64,4096]{1,0:T(8,128)(2,1)}, u32[]{:S(2)}) copy-start(bf16[64,4096]{1,0:T(8,128)(2,1)} %get-tuple-element.33) | copy-start | bytes 1572868
  2.5 35.0 %all-to-all-start = ((bf16[4,64,2048]{2,1,0:T(8,128)(2,1)}), bf16[4,64,2048]{2,1,0:T(8,128)(2,1)S(1)}, u32[]{:S(2)}, u32[]{:S(2)}) async-start(bf16[4,64,2048]{2,1,0:T(8,128)(2,1)} %get-tuple-element.37), calls=%async_computation | async-start | bytes 2097152 | tf_op jit(solution)/shard_map/all_to_all | solution.py:539
  8.9 12.0 %collective-permute-start.2 = (bf16[48,4096]{1,0:T(8,128)(2,1)S(1)}, bf16[48,4096]{1,0:T(8,128)(2,1)S(1)}, u32[]{:S(2)}, u32[]{:S(2)}) collective-permute-start(bf16[48,4096]{1,0:T(8,128)(2,1)S(1)} %copy-done.6), channel_id=1, source_target_pairs={{0,2},{2,0},{4,6},{6,4},{8,10},{10,8},{12,14},{14,12},{1,3},{3,1},... | collective-permute-start | bytes 1179656 | tf_op jit(solution)/shard_map/ppermute | solution.py:533
  10.4 27.1 %collective-permute-start.1 = (bf16[64,4096]{1,0:T(8,128)(2,1)S(1)}, bf16[64,4096]{1,0:T(8,128)(2,1)S(1)}, u32[]{:S(2)}, u32[]{:S(2)}) collective-permute-start(bf16[64,4096]{1,0:T(8,128)(2,1)S(1)} %copy-done.5), channel_id=1, source_target_pairs={{0,2},{2,0},{4,6},{6,4},{8,10},{10,8},{12,14},{14,12},{1,3},{3,1},... | collective-permute-start | bytes 1572872 | tf_op jit(solution)/shard_map/ppermute | solution.py:533
  11.7 21.2 %copy-start.1 = (s32[3,256]{1,0:T(4,128)S(1)}, s32[3,256]{1,0:T(4,128)}, u32[]{:S(2)}) copy-start(s32[3,256]{1,0:T(4,128)} %select_reduce_fusion.inv_ref) | copy-start | bytes 9220
  21.0 16.5 %collective-permute-start.3 = (bf16[48,4096]{1,0:T(8,128)(2,1)S(1)}, bf16[48,4096]{1,0:T(8,128)(2,1)S(1)}, u32[]{:S(2)}, u32[]{:S(2)}) collective-permute-start(bf16[48,4096]{1,0:T(8,128)(2,1)S(1)} %collective-permute-done.2.a_in_ref), channel_id=1, source_target_pairs={{0,16},{16,0},{1,17},{17,1},{2,18},{18,2},{3,19},{19,3},{4,20},{20... | collective-permute-start | bytes 1179656 | tf_op jit(solution)/shard_map/ppermute | solution.py:598
  22.5 5.0 %collective-permute-start.4 = (f32[64,256]{1,0:T(8,128)}, f32[64,256]{1,0:T(8,128)S(1)}, u32[]{:S(2)}, u32[]{:S(2)}) collective-permute-start(f32[64,256]{1,0:T(8,128)} %get-tuple-element.38), channel_id=1, source_target_pairs={{0,4},{2,6},{4,0},{6,2},{8,12},{10,14},{12,8},{14,10},{1,5},{3,7},... | collective-permute-start | bytes 196616 | tf_op jit(solution)/shard_map/ppermute | solution.py:533
  28.3 9.1 %collective-permute-start.5 = (f32[64,256]{1,0:T(8,128)S(1)}, f32[64,256]{1,0:T(8,128)S(1)}, u32[]{:S(2)}, u32[]{:S(2)}) collective-permute-start(f32[64,256]{1,0:T(8,128)S(1)} %add.24), channel_id=1, source_target_pairs={{0,8},{2,10},{4,12},{6,14},{8,0},{10,2},{12,4},{14,6},{1,9},{3,11}... | collective-permute-start | bytes 196616 | tf_op jit(solution)/shard_map/ppermute | solution.py:533
  32.9 4.6 %collective-permute-start = (s32[3,256]{1,0:T(4,128)S(1)}, s32[3,256]{1,0:T(4,128)S(1)}, u32[]{:S(2)}, u32[]{:S(2)}) collective-permute-start(s32[3,256]{1,0:T(4,128)S(1)} %copy-done.1), channel_id=1, source_target_pairs={{0,2},{2,0},{4,6},{6,4},{8,10},{10,8},{12,14},{14,12},{1,3},{3,1},... | collective-permute-start | bytes 9224 | tf_op jit(solution)/shard_map/ppermute | solution.py:533
  42.9 5.1 %collective-permute-start.6 = (bf16[4,1024,256]{2,1,0:T(8,128)(2,1)}, bf16[4,1024,256]{2,1,0:T(8,128)(2,1)}, u32[]{:S(2)}, u32[]{:S(2)}) collective-permute-start(bf16[4,1024,256]{2,1,0:T(8,128)(2,1)} %get-tuple-element.47), channel_id=1, source_target_pairs={{0,1},{1,0},{2,3},{3,2},{4,5},{5,4},{6,7},{7,6},{8,9},{9,8},{10,11... | collective-permute-start | bytes 6291464 | tf_op jit(solution)/shard_map/ppermute | solution.py:536
  43.0 25.0 %all-to-all-start.1 = ((bf16[4,64,1024]{2,1,0:T(8,128)(2,1)}), bf16[4,64,1024]{2,1,0:T(8,128)(2,1)S(1)}, u32[]{:S(2)}, u32[]{:S(2)}) async-start(bf16[4,64,1024]{2,1,0:T(8,128)(2,1)} %get-tuple-element.45), calls=%async_computation.1 | async-start | bytes 1048576 | tf_op jit(solution)/shard_map/all_to_all | solution.py:539
  46.5 6.9 %collective-permute-start.7 = (f32[64,256]{1,0:T(8,128)S(1)}, f32[64,256]{1,0:T(8,128)S(1)}, u32[]{:S(2)}, u32[]{:S(2)}) collective-permute-start(f32[64,256]{1,0:T(8,128)S(1)} %add.25), channel_id=1, source_target_pairs={{0,2},{2,0},{4,6},{6,4},{8,10},{10,8},{12,14},{14,12},{1,3},{3,1},... | collective-permute-start | bytes 196616 | tf_op jit(solution)/shard_map/ppermute | solution.py:533
  53.4 17.4 %collective-permute-start.8 = (bf16[64,1024]{1,0:T(8,128)(2,1)}, bf16[64,1024]{1,0:T(8,128)(2,1)S(1)}, u32[]{:S(2)}, u32[]{:S(2)}) collective-permute-start(bf16[64,1024]{1,0:T(8,128)(2,1)} %get-tuple-element.52), channel_id=1, source_target_pairs={{0,8},{2,10},{4,12},{6,14},{8,0},{10,2},{12,4},{14,6},{1,9},{3,11}... | collective-permute-start | bytes 393224 | tf_op jit(solution)/shard_map/ppermute | solution.py:533
  56.3 3.2 %collective-permute-start.11 = (f32[64,256]{1,0:T(8,128)S(1)}, f32[64,256]{1,0:T(8,128)S(1)}, u32[]{:S(2)}, u32[]{:S(2)}) collective-permute-start(f32[64,256]{1,0:T(8,128)S(1)} %add.26.pay0_ref), channel_id=1, source_target_pairs={{0,1},{1,0},{2,3},{3,2},{4,5},{5,4},{6,7},{7,6},{8,9},{9,8},{10,11... | collective-permute-start | bytes 196616 | tf_op jit(solution)/shard_map/ppermute | solution.py:536
  56.4 14.4 %collective-permute-start.9 = (bf16[64,1024]{1,0:T(8,128)(2,1)}, bf16[64,1024]{1,0:T(8,128)(2,1)S(1)}, u32[]{:S(2)}, u32[]{:S(2)}) collective-permute-start(bf16[64,1024]{1,0:T(8,128)(2,1)} %get-tuple-element.53), channel_id=1, source_target_pairs={{0,12},{2,14},{4,8},{6,10},{8,4},{10,6},{12,0},{14,2},{1,13},{3,15... | collective-permute-start | bytes 393224 | tf_op jit(solution)/shard_map/ppermute | solution.py:533
  57.9 13.2 %copy-start = (f32[64,1024]{1,0:T(8,128)S(1)}, f32[64,1024]{1,0:T(8,128)}, u32[]{:S(2)}) copy-start(f32[64,1024]{1,0:T(8,128)} %get-tuple-element.51.second_keep_ref) | copy-start | bytes 786436
  57.9 13.2 %collective-permute-start.10 = (bf16[64,1024]{1,0:T(8,128)(2,1)}, bf16[64,1024]{1,0:T(8,128)(2,1)S(1)}, u32[]{:S(2)}, u32[]{:S(2)}) collective-permute-start(bf16[64,1024]{1,0:T(8,128)(2,1)} %get-tuple-element.54), channel_id=1, source_target_pairs={{0,4},{2,6},{4,0},{6,2},{8,12},{10,14},{12,8},{14,10},{1,5},{3,7},... | collective-permute-start | bytes 393224 | tf_op jit(solution)/shard_map/ppermute | solution.py:533
  58.0 12.2 %collective-permute-start.12 = (f32[64,256]{1,0:T(8,128)S(1)}, f32[64,256]{1,0:T(8,128)S(1)}, u32[]{:S(2)}, u32[]{:S(2)}) collective-permute-start(f32[64,256]{1,0:T(8,128)S(1)} %add.26.pay0_ref), channel_id=1, source_target_pairs={{0,16},{16,0},{1,17},{17,1},{2,18},{18,2},{3,19},{19,3},{4,20},{20... | collective-permute-start | bytes 196616 | tf_op jit(solution)/shard_map/ppermute | solution.py:657
  59.5 10.7 %collective-permute-start.13 = (f32[64,256]{1,0:T(8,128)S(1)}, f32[64,256]{1,0:T(8,128)S(1)}, u32[]{:S(2)}, u32[]{:S(2)}) collective-permute-start(f32[64,256]{1,0:T(8,128)S(1)} %add.26.pay0_ref), channel_id=1, source_target_pairs={{0,17},{1,16},{16,1},{17,0},{2,19},{3,18},{18,3},{19,2},{4,21},{5,... | collective-permute-start | bytes 196616 | tf_op jit(solution)/shard_map/ppermute | solution.py:658
  73.6 1.3 %collective-permute-start.14 = (f32[8,2048]{1,0:T(8,128)S(1)}, f32[8,2048]{1,0:T(8,128)S(1)}, u32[]{:S(2)}, u32[]{:S(2)}) collective-permute-start(f32[8,2048]{1,0:T(8,128)S(1)} %get-tuple-element.59), channel_id=1, source_target_pairs={{0,1},{1,0},{2,3},{3,2},{4,5},{5,4},{6,7},{7,6},{8,9},{9,8},{10,11... | collective-permute-start | bytes 196616 | tf_op jit(solution)/shard_map/ppermute | solution.py:536
  75.0 5.5 %collective-permute-start.17 = (bf16[8,2048]{1,0:T(8,128)(2,1)S(1)}, bf16[8,2048]{1,0:T(8,128)(2,1)S(1)}, u32[]{:S(2)}, u32[]{:S(2)}) collective-permute-start(bf16[8,2048]{1,0:T(8,128)(2,1)S(1)} %get-tuple-element.61), channel_id=1, source_target_pairs={{0,6},{2,4},{4,2},{6,0},{8,14},{10,12},{12,10},{14,8},{1,7},{3,5},... | collective-permute-start | bytes 98312 | tf_op jit(solution)/shard_map/ppermute | solution.py:533
  78.6 3.9 %collective-permute-start.16 = (bf16[8,2048]{1,0:T(8,128)(2,1)S(1)}, bf16[8,2048]{1,0:T(8,128)(2,1)S(1)}, u32[]{:S(2)}, u32[]{:S(2)}) collective-permute-start(bf16[8,2048]{1,0:T(8,128)(2,1)S(1)} %get-tuple-element.61), channel_id=1, source_target_pairs={{0,4},{2,6},{4,0},{6,2},{8,12},{10,14},{12,8},{14,10},{1,5},{3,7},... | collective-permute-start | bytes 98312 | tf_op jit(solution)/shard_map/ppermute | solution.py:533
  78.6 3.9 %collective-permute-start.15 = (bf16[8,2048]{1,0:T(8,128)(2,1)S(1)}, bf16[8,2048]{1,0:T(8,128)(2,1)S(1)}, u32[]{:S(2)}, u32[]{:S(2)}) collective-permute-start(bf16[8,2048]{1,0:T(8,128)(2,1)S(1)} %get-tuple-element.61), channel_id=1, source_target_pairs={{0,2},{2,0},{4,6},{6,4},{8,10},{10,8},{12,14},{14,12},{1,3},{3,1},... | collective-permute-start | bytes 98312 | tf_op jit(solution)/shard_map/ppermute | solution.py:533
  82.5 4.9 %collective-permute-start.18 = (bf16[8,2048]{1,0:T(8,128)(2,1)S(1)}, bf16[8,2048]{1,0:T(8,128)(2,1)S(1)}, u32[]{:S(2)}, u32[]{:S(2)}) collective-permute-start(bf16[8,2048]{1,0:T(8,128)(2,1)S(1)} %fusion), channel_id=1, source_target_pairs={{0,8},{2,10},{4,12},{6,14},{8,0},{10,2},{12,4},{14,6},{1,9},{3,11}... | collective-permute-start | bytes 98312 | tf_op jit(solution)/shard_map/ppermute | solution.py:533
  87.4 1.3 %collective-permute-start.19 = (bf16[8,2048]{1,0:T(8,128)(2,1)S(1)}, bf16[8,2048]{1,0:T(8,128)(2,1)S(1)}, u32[]{:S(2)}, u32[]{:S(2)}) collective-permute-start(bf16[8,2048]{1,0:T(8,128)(2,1)S(1)} %add_convert_fusion.mine_ref), channel_id=1, source_target_pairs={{0,1},{1,0},{2,3},{3,2},{4,5},{5,4},{6,7},{7,6},{8,9},{9,8},{10,11... | collective-permute-start | bytes 98312 | tf_op jit(solution)/shard_map/ppermute | solution.py:536

commit v16 on v13

--- a/solution.py
+++ b/solution.py
@@ -332,11 +332,9 @@
     sent_out_ref,
     near_out_ref,
     tokens_out_ref,
-    blocks_ref,
     tiles_ref,
     near_ref,
     own_ref,
-    tok_ref,
     tokens_ref,
     sent_ref,
     total_ref,
@@ -347,23 +345,12 @@
     owner, quarter, side, core = position()
     zone = owner // 2
     group = quarter // 2
-    mine = pl.multiple_of(SHARED * group, 16)
-    other = pl.multiple_of(SHARED * (1 - group), 16)
-    loads = [
-        pltpu.make_async_copy(a_in_ref, blocks_ref.at[pl.ds(mine, SHARED)], in_sem.at[0]),
-        pltpu.make_async_copy(a_other_ref, blocks_ref.at[pl.ds(other, SHARED)], in_sem.at[1]),
-        pltpu.make_async_copy(
-            b_in_ref, blocks_ref.at[pl.ds(2 * SHARED, 160 - 2 * SHARED)], in_sem.at[2]
-        ),
-        pltpu.make_async_copy(tok_in_ref, tok_ref, in_sem.at[3]),
-        pltpu.make_async_copy(weight_in_ref.at[pl.ds(4 * core, 4)], own_ref, in_sem.at[4]),
-    ]
-    for load in loads:
-        load.start()
+    load = pltpu.make_async_copy(weight_in_ref.at[pl.ds(4 * core, 4)], own_ref, in_sem)
+    load.start()
     clear_empty_slot(tiles_ref)
-    for load in loads[:3]:
-        load.wait()
-    stage_blocks(blocks_ref, tiles_ref, 0)
+    stage_blocks(a_in_ref, tiles_ref, SHARED * group)
+    stage_blocks(a_other_ref, tiles_ref, SHARED * (1 - group))
+    stage_blocks(b_in_ref, tiles_ref, 2 * SHARED)
 
     def put(pair, row, piece):
         lane = (pair % 2) * 128
@@ -372,11 +359,10 @@
     assemble_columns(inv_ref, core, tiles_ref, put)
     near_store = pltpu.make_async_copy(near_ref, near_out_ref, near_sem.at[0])
     near_store.start()
-    loads[3].wait()
-    shuffle_tokens(side, tok_ref, tokens_ref)
+    shuffle_tokens(side, tok_in_ref, tokens_ref)
     tokens_store = pltpu.make_async_copy(tokens_ref, tokens_out_ref, near_sem.at[1])
     tokens_store.start()
-    loads[4].wait()
+    load.wait()
     stores = []
     for chunk in range(4):
         total = dot(tokens_ref[0], own_ref[chunk]) + dot(tokens_ref[1], near_ref[chunk])
@@ -575,8 +561,8 @@
         in_specs=[SMEM] + [HBM] * 3 + [VMEM] * 3,
         out_specs=(HBM, VMEM),
         scratch_shapes=[
-            pltpu.VMEM((32 * STRIDE, 128), F32),
-            pltpu.VMEM((128, 128), F32),
+            pltpu.VMEM((33 * STRIDE, 128), F32),
+            pltpu.VMEM((136, 128), F32),
             pltpu.VMEM((48, 1024), BF),
             pltpu.VMEM((256, 1024), BF),
             pltpu.VMEM((3, 160, 4096), BF),
@@ -604,18 +590,16 @@
             jax.ShapeDtypeStruct((4, 1024, 256), BF),
             pltpu.HBM((2, 256, 1024), BF),
         ),
-        in_specs=[SMEM, ANY, ANY, ANY, HBM, ANY],
+        in_specs=[SMEM, VMEM, VMEM, VMEM, HBM, VMEM],
         out_specs=(VMEM, HBM, HBM, HBM),
         scratch_shapes=[
-            pltpu.VMEM((160, 4096), BF),
-            pltpu.VMEM((32 * STRIDE, 128), F32),
+            pltpu.VMEM((33 * STRIDE, 128), F32),
             pltpu.VMEM((4, 1024, 256), BF),
             pltpu.VMEM((4, 1024, 256), BF),
-            pltpu.VMEM((4, 64, 2048), BF),
             pltpu.VMEM((2, 256, 1024), BF),
             pltpu.VMEM((4, 64, 1024), BF),
             pltpu.VMEM((256, 256), F32),
-            pltpu.SemaphoreType.DMA((5,)),
+            pltpu.SemaphoreType.DMA,
             pltpu.SemaphoreType.DMA((2,)),
             pltpu.SemaphoreType.DMA((4,)),
         ],

time: 91.2 us -> 90.6 us (level)
  no operation moved by 1% of the time
where the time goes in v16:
time: 90.6 us; the launch traced here: 90.2 us
  starting transfers between devices  36.2 us (40%)
  Pallas kernels  26.4 us (29%)
  waiting for transfers between devices  25.7 us (28%)
  other arithmetic  1.67 us (2%)
    ppermute x13, starting transfers between devices, owner_flip(): return lax.ppermute(value, 'fsdp', [(i, i ^ bits) for i in range(8)])  22.9 us
    ppermute x13, waiting for transfers between devices, owner_flip(): return lax.ppermute(value, 'fsdp', [(i, i ^ bits) for i in range(8)])  19.9 us
    all_to_all x2, starting transfers between devices, zone_exchange(): lax.all_to_all(value, 'fsdp', split_axis=0, concat_axis=0, tiled=True, ax...  9.94 us
    pallas_call x1, Pallas kernels, pair_split(): pl.pallas_call(own_kernel, out_shape=(jax.ShapeDtypeStruct((8, 1024, 256)...  7.55 us
    pallas_call x1, Pallas kernels, pair_split(): pl.pallas_call(first_kernel, out_shape=(jax.ShapeDtypeStruct((64, 1024),...  4.85 us
    pallas_call x1, Pallas kernels, pair_split(): pl.pallas_call(second_kernel, out_shape=(jax.ShapeDtypeStruct((64, 1024),...  4.78 us
    all_to_all x2, waiting for transfers between devices, zone_exchange(): lax.all_to_all(value, 'fsdp', split_axis=0, concat_axis=0, tiled=True, ax...  3.3 us
    pallas_call x1, Pallas kernels, pair_split(): pl.pallas_call(middle_kernel, out_shape=(jax.ShapeDtypeStruct((8, 2048),...  2.61 us
  transfers between devices with their start and end apart: 22, of which 10 were waited for; matrix products, arithmetic and copies ran while one was open for 2% of the time, Pallas kernels for 16%

profile of v16, /device:TPU:0, one launch (start us, length us, event | category | flops | bytes accessed | tf_op | source)
XLA Modules:
  0.0 90.2 jit_solution(630197822904915082)
XLA Ops:
  0.0 2.4 %head.1 = (bf16[4,64,2048]{2,1,0:T(8,128)(2,1)}, bf16[48,4096]{1,0:T(8,128)(2,1)}, bf16[64,4096]{1,0:T(8,128)(2,1)}) custom-call(bf16[64,8192]{1,0:T(8,128)(2,1)} %tok_in_ref.1, bf16[160,4096]{1,0:T(8,128)(2,1)} %gate_ref.3, bf16[160,4096]{1,0:T(8,128)(2,1)} %up_ref.3), custom_call_target="tpu_custom_call" | custom-call | tf_op jit(solution)/shard_map/head/pallas_call | solution.py:528
  2.5 6.5 %all-to-all-start = ((bf16[4,64,2048]{2,1,0:T(8,128)(2,1)}), bf16[4,64,2048]{2,1,0:T(8,128)(2,1)S(1)}, u32[]{:S(2)}, u32[]{:S(2)}) async-start(bf16[4,64,2048]{2,1,0:T(8,128)(2,1)} %get-tuple-element.37), calls=%async_computation | async-start | bytes 2097152 | tf_op jit(solution)/shard_map/all_to_all | solution.py:519
  8.9 1.5 %collective-permute-start.2 = (bf16[48,4096]{1,0:T(8,128)(2,1)S(1)}, bf16[48,4096]{1,0:T(8,128)(2,1)S(1)}, u32[]{:S(2)}, u32[]{:S(2)}) collective-permute-start(bf16[48,4096]{1,0:T(8,128)(2,1)S(1)} %copy-done.6), channel_id=1, source_target_pairs={{0,2},{2,0},{4,6},{6,4},{8,10},{10,8},{12,14},{14,12},{1,3},{3,1},... | collective-permute-start | bytes 1179656 | tf_op jit(solution)/shard_map/ppermute | solution.py:513
  11.0 0.7 select_reduce_fusion.inv_ref
  11.7 7.5 %own_blocks.1 = (bf16[8,1024,256]{2,1,0:T(8,128)(2,1)}, f32[64,256]{1,0:T(8,128)}) custom-call(s32[3,256]{1,0:T(4,128)} %select_reduce_fusion.inv_ref, bf16[160,4096]{1,0:T(8,128)(2,1)} %gate_ref.3, bf16[160,4096]{1,0:T(8,128)(2,1)} %up_ref.3, bf16[160,4096]{1,0:T(8,128)(2,1)} %down_ref.1, bf16[32,1024]{1,0:T(8,128)(2,1)} %sketch_ref.1, ...), custom_call_target="tpu_custom_call" | custom-call | tf_op jit(solution)/shard_map/own_blocks/pallas_call | solution.py:555
  19.3 1.7 %collective-permute-done.2.a_in_ref = bf16[48,4096]{1,0:T(8,128)(2,1)S(1)} collective-permute-done((bf16[48,4096]{1,0:T(8,128)(2,1)S(1)}, bf16[48,4096]{1,0:T(8,128)(2,1)S(1)}, u32[]{:S(2)}, u32[]{:S(2)}) %collective-permute-start.2) | collective-permute-done | bytes 393248 | tf_op jit(solution)/shard_map/ppermute | solution.py:513
  21.0 1.5 %collective-permute-start.3 = (bf16[48,4096]{1,0:T(8,128)(2,1)S(1)}, bf16[48,4096]{1,0:T(8,128)(2,1)S(1)}, u32[]{:S(2)}, u32[]{:S(2)}) collective-permute-start(bf16[48,4096]{1,0:T(8,128)(2,1)S(1)} %collective-permute-done.2.a_in_ref), channel_id=1, source_target_pairs={{0,16},{16,0},{1,17},{17,1},{2,18},{18,2},{3,19},{19,3},{4,20},{20... | collective-permute-start | bytes 1179656 | tf_op jit(solution)/shard_map/ppermute | solution.py:578
  22.5 2.0 %collective-permute-start.4 = (f32[64,256]{1,0:T(8,128)}, f32[64,256]{1,0:T(8,128)S(1)}, u32[]{:S(2)}, u32[]{:S(2)}) collective-permute-start(f32[64,256]{1,0:T(8,128)} %get-tuple-element.38), channel_id=1, source_target_pairs={{0,4},{2,6},{4,0},{6,2},{8,12},{10,14},{12,8},{14,10},{1,5},{3,7},... | collective-permute-start | bytes 196616 | tf_op jit(solution)/shard_map/ppermute | solution.py:513
  24.5 3.0 %collective-permute-done.4 = f32[64,256]{1,0:T(8,128)S(1)} collective-permute-done((f32[64,256]{1,0:T(8,128)}, f32[64,256]{1,0:T(8,128)S(1)}, u32[]{:S(2)}, u32[]{:S(2)}) %collective-permute-start.4) | collective-permute-done | bytes 65568 | tf_op jit(solution)/shard_map/ppermute | solution.py:513
  27.5 0.8 add.24
  28.3 4.6 %collective-permute-start.5 = (f32[64,256]{1,0:T(8,128)S(1)}, f32[64,256]{1,0:T(8,128)S(1)}, u32[]{:S(2)}, u32[]{:S(2)}) collective-permute-start(f32[64,256]{1,0:T(8,128)S(1)} %add.24), channel_id=1, source_target_pairs={{0,8},{2,10},{4,12},{6,14},{8,0},{10,2},{12,4},{14,6},{1,9},{3,11}... | collective-permute-start | bytes 196616 | tf_op jit(solution)/shard_map/ppermute | solution.py:513
  32.9 1.5 %collective-permute-start = (s32[3,256]{1,0:T(4,128)S(1)}, s32[3,256]{1,0:T(4,128)S(1)}, u32[]{:S(2)}, u32[]{:S(2)}) collective-permute-start(s32[3,256]{1,0:T(4,128)S(1)} %copy-done.1), channel_id=1, source_target_pairs={{0,2},{2,0},{4,6},{6,4},{8,10},{10,8},{12,14},{14,12},{1,3},{3,1},... | collective-permute-start | bytes 9224 | tf_op jit(solution)/shard_map/ppermute | solution.py:513
  34.4 3.1 %collective-permute-done.5 = f32[64,256]{1,0:T(8,128)S(1)} collective-permute-done((f32[64,256]{1,0:T(8,128)S(1)}, f32[64,256]{1,0:T(8,128)S(1)}, u32[]{:S(2)}, u32[]{:S(2)}) %collective-permute-start.5) | collective-permute-done | bytes 65568 | tf_op jit(solution)/shard_map/ppermute | solution.py:513
  37.5 4.8 %first_partial.1 = (f32[64,1024]{1,0:T(8,128)S(1)}, bf16[4,64,1024]{2,1,0:T(8,128)(2,1)}, bf16[4,1024,256]{2,1,0:T(8,128)(2,1)}, bf16[2,256,1024]{2,1,0:T(8,128)(2,1)}) custom-call(s32[3,256]{1,0:T(4,128)S(1)} %collective-permute-done.inv_ref, bf16[48,4096]{1,0:T(8,128)(2,1)S(1)} %collective-permute-done.2.a_in_ref, ...), custom_call_target="tpu_custom_call" | custom-call | tf_op jit(solution)/shard_map/first_partial/pallas_call | solution.py:585
  42.4 3.5 %all-to-all-start.1 = ((bf16[4,64,1024]{2,1,0:T(8,128)(2,1)}), bf16[4,64,1024]{2,1,0:T(8,128)(2,1)S(1)}, u32[]{:S(2)}, u32[]{:S(2)}) async-start(bf16[4,64,1024]{2,1,0:T(8,128)(2,1)} %get-tuple-element.45), calls=%async_computation.1 | async-start | bytes 1048576 | tf_op jit(solution)/shard_map/all_to_all | solution.py:519
  45.9 1.6 %collective-permute-start.7 = (f32[64,256]{1,0:T(8,128)S(1)}, f32[64,256]{1,0:T(8,128)S(1)}, u32[]{:S(2)}, u32[]{:S(2)}) collective-permute-start(f32[64,256]{1,0:T(8,128)S(1)} %add.25), channel_id=1, source_target_pairs={{0,2},{2,0},{4,6},{6,4},{8,10},{10,8},{12,14},{14,12},{1,3},{3,1},... | collective-permute-start | bytes 196616 | tf_op jit(solution)/shard_map/ppermute | solution.py:513
  47.5 4.8 %second_partial.1 = (f32[64,1024]{1,0:T(8,128)}, bf16[64,1024]{1,0:T(8,128)(2,1)}, bf16[64,1024]{1,0:T(8,128)(2,1)}, bf16[64,1024]{1,0:T(8,128)(2,1)}) custom-call(bf16[4,1024,256]{2,1,0:T(8,128)(2,1)} %collective-permute-done.6.near_in_ref, bf16[8,1024,256]{2,1,0:T(8,128)(2,1)} %get-tuple-element.56.weight_in_ref, ...), custom_call_target="tpu_custom_call" | custom-call | tf_op jit(solution)/shard_map/second_partial/pallas_call | solution.py:611
  52.3 2.0 %collective-permute-start.8 = (bf16[64,1024]{1,0:T(8,128)(2,1)}, bf16[64,1024]{1,0:T(8,128)(2,1)S(1)}, u32[]{:S(2)}, u32[]{:S(2)}) collective-permute-start(bf16[64,1024]{1,0:T(8,128)(2,1)} %get-tuple-element.52), channel_id=1, source_target_pairs={{0,4},{2,6},{4,0},{6,2},{8,12},{10,14},{12,8},{14,10},{1,5},{3,7},... | collective-permute-start | bytes 393224 | tf_op jit(solution)/shard_map/ppermute | solution.py:513
  54.4 2.4 %collective-permute-start.9 = (bf16[64,1024]{1,0:T(8,128)(2,1)}, bf16[64,1024]{1,0:T(8,128)(2,1)S(1)}, u32[]{:S(2)}, u32[]{:S(2)}) collective-permute-start(bf16[64,1024]{1,0:T(8,128)(2,1)} %get-tuple-element.53), channel_id=1, source_target_pairs={{0,8},{2,10},{4,12},{6,14},{8,0},{10,2},{12,4},{14,6},{1,9},{3,11}... | collective-permute-start | bytes 393224 | tf_op jit(solution)/shard_map/ppermute | solution.py:513
  56.9 1.5 %collective-permute-start.12 = (f32[64,256]{1,0:T(8,128)S(1)}, f32[64,256]{1,0:T(8,128)S(1)}, u32[]{:S(2)}, u32[]{:S(2)}) collective-permute-start(f32[64,256]{1,0:T(8,128)S(1)} %add.26.pay0_ref), channel_id=1, source_target_pairs={{0,16},{16,0},{1,17},{17,1},{2,18},{18,2},{3,19},{19,3},{4,20},{20... | collective-permute-start | bytes 196616 | tf_op jit(solution)/shard_map/ppermute | solution.py:635
  58.4 3.3 %all-to-all-done.1.first_ref = bf16[4,64,1024]{2,1,0:T(8,128)(2,1)S(1)} async-done(((bf16[4,64,1024]{2,1,0:T(8,128)(2,1)}), bf16[4,64,1024]{2,1,0:T(8,128)(2,1)S(1)}, u32[]{:S(2)}, u32[]{:S(2)}) %all-to-all-start.1) | async-done | bytes 524320 | tf_op jit(solution)/shard_map/all_to_all | solution.py:519
  61.7 2.2 %fetch_weights.1.weight_ref = bf16[8,1024,256]{2,1,0:T(8,128)(2,1)S(1)} custom-call(bf16[8,1024,256]{2,1,0:T(8,128)(2,1)} %get-tuple-element.56.weight_in_ref), custom_call_target="tpu_custom_call" | custom-call | tf_op jit(solution)/shard_map/fetch_weights/pallas_call | solution.py:640
  64.0 6.2 %collective-permute-done.9.second2_ref = bf16[64,1024]{1,0:T(8,128)(2,1)S(1)} collective-permute-done((bf16[64,1024]{1,0:T(8,128)(2,1)}, bf16[64,1024]{1,0:T(8,128)(2,1)S(1)}, u32[]{:S(2)}, u32[]{:S(2)}) %collective-permute-start.9) | collective-permute-done | bytes 131104 | tf_op jit(solution)/shard_map/ppermute | solution.py:513
  70.2 2.6 %token_sums.1 = (f32[8,2048]{1,0:T(8,128)S(1)}, f32[8,2048]{1,0:T(8,128)S(1)}) custom-call(f32[64,1024]{1,0:T(8,128)S(1)} %get-tuple-element.44.first_keep_ref, bf16[4,64,1024]{2,1,0:T(8,128)(2,1)S(1)} %all-to-all-done.1.first_ref, f32[64,1024]{1,0:T(8,128)S(1)} %copy-done, bf16[64,1024]{1,0:T(8,128)(2,1)S(1)} %collective-permute-done.8.second1_ref, ...), custom_call_target="tpu_custom_call" | custom-call | tf_op jit(solution)/shard_map/token_sums/pallas_call | solution.py:651
  72.8 1.2 %collective-permute-done.14 = f32[8,2048]{1,0:T(8,128)S(1)} collective-permute-done((f32[8,2048]{1,0:T(8,128)S(1)}, f32[8,2048]{1,0:T(8,128)S(1)}, u32[]{:S(2)}, u32[]{:S(2)}) %collective-permute-start.14) | collective-permute-done | bytes 65568 | tf_op jit(solution)/shard_map/ppermute | solution.py:516
  74.1 4.0 %collective-permute-start.17 = (bf16[8,2048]{1,0:T(8,128)(2,1)S(1)}, bf16[8,2048]{1,0:T(8,128)(2,1)S(1)}, u32[]{:S(2)}, u32[]{:S(2)}) collective-permute-start(bf16[8,2048]{1,0:T(8,128)(2,1)S(1)} %get-tuple-element.61), channel_id=1, source_target_pairs={{0,6},{2,4},{4,2},{6,0},{8,14},{10,12},{12,10},{14,8},{1,7},{3,5},... | collective-permute-start | bytes 98312 | tf_op jit(solution)/shard_map/ppermute | solution.py:513
  78.7 1.3 %collective-permute-done.17 = bf16[8,2048]{1,0:T(8,128)(2,1)S(1)} collective-permute-done((bf16[8,2048]{1,0:T(8,128)(2,1)S(1)}, bf16[8,2048]{1,0:T(8,128)(2,1)S(1)}, u32[]{:S(2)}, u32[]{:S(2)}) %collective-permute-start.17) | collective-permute-done | bytes 32800 | tf_op jit(solution)/shard_map/ppermute | solution.py:513
  79.9 2.0 %collective-permute-done.16 = bf16[8,2048]{1,0:T(8,128)(2,1)S(1)} collective-permute-done((bf16[8,2048]{1,0:T(8,128)(2,1)S(1)}, bf16[8,2048]{1,0:T(8,128)(2,1)S(1)}, u32[]{:S(2)}, u32[]{:S(2)}) %collective-permute-start.16) | collective-permute-done | bytes 32800 | tf_op jit(solution)/shard_map/ppermute | solution.py:513
  82.0 2.1 %collective-permute-start.18 = (bf16[8,2048]{1,0:T(8,128)(2,1)S(1)}, bf16[8,2048]{1,0:T(8,128)(2,1)S(1)}, u32[]{:S(2)}, u32[]{:S(2)}) collective-permute-start(bf16[8,2048]{1,0:T(8,128)(2,1)S(1)} %fusion), channel_id=1, source_target_pairs={{0,8},{2,10},{4,12},{6,14},{8,0},{10,2},{12,4},{14,6},{1,9},{3,11}... | collective-permute-start | bytes 98312 | tf_op jit(solution)/shard_map/ppermute | solution.py:513
  84.1 2.8 %collective-permute-done.18 = bf16[8,2048]{1,0:T(8,128)(2,1)S(1)} collective-permute-done((bf16[8,2048]{1,0:T(8,128)(2,1)S(1)}, bf16[8,2048]{1,0:T(8,128)(2,1)S(1)}, u32[]{:S(2)}, u32[]{:S(2)}) %collective-permute-start.18) | collective-permute-done | bytes 32800 | tf_op jit(solution)/shard_map/ppermute | solution.py:513
  87.0 1.2 %collective-permute-done.19.theirs_ref = bf16[8,2048]{1,0:T(8,128)(2,1)S(1)} collective-permute-done((bf16[8,2048]{1,0:T(8,128)(2,1)S(1)}, bf16[8,2048]{1,0:T(8,128)(2,1)S(1)}, u32[]{:S(2)}, u32[]{:S(2)}) %collective-permute-start.19) | collective-permute-done | bytes 32800 | tf_op jit(solution)/shard_map/ppermute | solution.py:516
  88.2 2.1 %products.1 = f32[16,1024]{1,0:T(8,128)} custom-call(bf16[8,2048]{1,0:T(8,128)(2,1)S(1)} %add_convert_fusion.mine_ref, bf16[8,2048]{1,0:T(8,128)(2,1)S(1)} %collective-permute-done.19.theirs_ref, bf16[8,1024,256]{2,1,0:T(8,128)(2,1)S(1)} %fetch_weights.1.weight_ref), custom_call_target="tpu_custom_call" | custom-call | tf_op jit(solution)/shard_map/products/pallas_call | solution.py:675
  (41 shorter events, 1.7 us)
Async XLA Ops:
  0.0 10.9 %copy-start.2 = (s32[160]{0:T(256)S(1)}, s32[160]{0:T(256)}, u32[]{:S(2)}) copy-start(s32[160]{0:T(256)} %param.16) | copy-start | bytes 1924
  0.0 10.9 %copy-start.3 = (s32[160]{0:T(256)S(1)}, s32[160]{0:T(256)}, u32[]{:S(2)}) copy-start(s32[160]{0:T(256)} %param.14) | copy-start | bytes 1924
  0.0 10.9 %copy-start.4 = (s32[160]{0:T(256)S(1)}, s32[160]{0:T(256)}, u32[]{:S(2)}) copy-start(s32[160]{0:T(256)} %param.12) | copy-start | bytes 1924
  2.4 6.5 %copy-start.6 = (bf16[48,4096]{1,0:T(8,128)(2,1)S(1)}, bf16[48,4096]{1,0:T(8,128)(2,1)}, u32[]{:S(2)}) copy-start(bf16[48,4096]{1,0:T(8,128)(2,1)} %get-tuple-element.34) | copy-start | bytes 1179652
  2.4 8.0 %copy-start.5 = (bf16[64,4096]{1,0:T(8,128)(2,1)S(1)}, bf16[64,4096]{1,0:T(8,128)(2,1)}, u32[]{:S(2)}) copy-start(bf16[64,4096]{1,0:T(8,128)(2,1)} %get-tuple-element.33) | copy-start | bytes 1572868
  2.5 35.0 %all-to-all-start = ((bf16[4,64,2048]{2,1,0:T(8,128)(2,1)}), bf16[4,64,2048]{2,1,0:T(8,128)(2,1)S(1)}, u32[]{:S(2)}, u32[]{:S(2)}) async-start(bf16[4,64,2048]{2,1,0:T(8,128)(2,1)} %get-tuple-element.37), calls=%async_computation | async-start | bytes 2097152 | tf_op jit(solution)/shard_map/all_to_all | solution.py:519
  8.9 12.0 %collective-permute-start.2 = (bf16[48,4096]{1,0:T(8,128)(2,1)S(1)}, bf16[48,4096]{1,0:T(8,128)(2,1)S(1)}, u32[]{:S(2)}, u32[]{:S(2)}) collective-permute-start(bf16[48,4096]{1,0:T(8,128)(2,1)S(1)} %copy-done.6), channel_id=1, source_target_pairs={{0,2},{2,0},{4,6},{6,4},{8,10},{10,8},{12,14},{14,12},{1,3},{3,1},... | collective-permute-start | bytes 1179656 | tf_op jit(solution)/shard_map/ppermute | solution.py:513
  10.4 27.1 %collective-permute-start.1 = (bf16[64,4096]{1,0:T(8,128)(2,1)S(1)}, bf16[64,4096]{1,0:T(8,128)(2,1)S(1)}, u32[]{:S(2)}, u32[]{:S(2)}) collective-permute-start(bf16[64,4096]{1,0:T(8,128)(2,1)S(1)} %copy-done.5), channel_id=1, source_target_pairs={{0,2},{2,0},{4,6},{6,4},{8,10},{10,8},{12,14},{14,12},{1,3},{3,1},... | collective-permute-start | bytes 1572872 | tf_op jit(solution)/shard_map/ppermute | solution.py:513
  11.7 21.2 %copy-start.1 = (s32[3,256]{1,0:T(4,128)S(1)}, s32[3,256]{1,0:T(4,128)}, u32[]{:S(2)}) copy-start(s32[3,256]{1,0:T(4,128)} %select_reduce_fusion.inv_ref) | copy-start | bytes 9220
  21.0 16.5 %collective-permute-start.3 = (bf16[48,4096]{1,0:T(8,128)(2,1)S(1)}, bf16[48,4096]{1,0:T(8,128)(2,1)S(1)}, u32[]{:S(2)}, u32[]{:S(2)}) collective-permute-start(bf16[48,4096]{1,0:T(8,128)(2,1)S(1)} %collective-permute-done.2.a_in_ref), channel_id=1, source_target_pairs={{0,16},{16,0},{1,17},{17,1},{2,18},{18,2},{3,19},{19,3},{4,20},{20... | collective-permute-start | bytes 1179656 | tf_op jit(solution)/shard_map/ppermute | solution.py:578
  22.5 5.0 %collective-permute-start.4 = (f32[64,256]{1,0:T(8,128)}, f32[64,256]{1,0:T(8,128)S(1)}, u32[]{:S(2)}, u32[]{:S(2)}) collective-permute-start(f32[64,256]{1,0:T(8,128)} %get-tuple-element.38), channel_id=1, source_target_pairs={{0,4},{2,6},{4,0},{6,2},{8,12},{10,14},{12,8},{14,10},{1,5},{3,7},... | collective-permute-start | bytes 196616 | tf_op jit(solution)/shard_map/ppermute | solution.py:513
  28.3 9.1 %collective-permute-start.5 = (f32[64,256]{1,0:T(8,128)S(1)}, f32[64,256]{1,0:T(8,128)S(1)}, u32[]{:S(2)}, u32[]{:S(2)}) collective-permute-start(f32[64,256]{1,0:T(8,128)S(1)} %add.24), channel_id=1, source_target_pairs={{0,8},{2,10},{4,12},{6,14},{8,0},{10,2},{12,4},{14,6},{1,9},{3,11}... | collective-permute-start | bytes 196616 | tf_op jit(solution)/shard_map/ppermute | solution.py:513
  32.9 4.6 %collective-permute-start = (s32[3,256]{1,0:T(4,128)S(1)}, s32[3,256]{1,0:T(4,128)S(1)}, u32[]{:S(2)}, u32[]{:S(2)}) collective-permute-start(s32[3,256]{1,0:T(4,128)S(1)} %copy-done.1), channel_id=1, source_target_pairs={{0,2},{2,0},{4,6},{6,4},{8,10},{10,8},{12,14},{14,12},{1,3},{3,1},... | collective-permute-start | bytes 9224 | tf_op jit(solution)/shard_map/ppermute | solution.py:513
  42.4 5.1 %collective-permute-start.6 = (bf16[4,1024,256]{2,1,0:T(8,128)(2,1)}, bf16[4,1024,256]{2,1,0:T(8,128)(2,1)}, u32[]{:S(2)}, u32[]{:S(2)}) collective-permute-start(bf16[4,1024,256]{2,1,0:T(8,128)(2,1)} %get-tuple-element.47), channel_id=1, source_target_pairs={{0,1},{1,0},{2,3},{3,2},{4,5},{5,4},{6,7},{7,6},{8,9},{9,8},{10,11... | collective-permute-start | bytes 6291464 | tf_op jit(solution)/shard_map/ppermute | solution.py:516
  42.4 19.3 %all-to-all-start.1 = ((bf16[4,64,1024]{2,1,0:T(8,128)(2,1)}), bf16[4,64,1024]{2,1,0:T(8,128)(2,1)S(1)}, u32[]{:S(2)}, u32[]{:S(2)}) async-start(bf16[4,64,1024]{2,1,0:T(8,128)(2,1)} %get-tuple-element.45), calls=%async_computation.1 | async-start | bytes 1048576 | tf_op jit(solution)/shard_map/all_to_all | solution.py:519
  45.9 6.3 %collective-permute-start.7 = (f32[64,256]{1,0:T(8,128)S(1)}, f32[64,256]{1,0:T(8,128)S(1)}, u32[]{:S(2)}, u32[]{:S(2)}) collective-permute-start(f32[64,256]{1,0:T(8,128)S(1)} %add.25), channel_id=1, source_target_pairs={{0,2},{2,0},{4,6},{6,4},{8,10},{10,8},{12,14},{14,12},{1,3},{3,1},... | collective-permute-start | bytes 196616 | tf_op jit(solution)/shard_map/ppermute | solution.py:513
  52.3 11.7 %collective-permute-start.8 = (bf16[64,1024]{1,0:T(8,128)(2,1)}, bf16[64,1024]{1,0:T(8,128)(2,1)S(1)}, u32[]{:S(2)}, u32[]{:S(2)}) collective-permute-start(bf16[64,1024]{1,0:T(8,128)(2,1)} %get-tuple-element.52), channel_id=1, source_target_pairs={{0,4},{2,6},{4,0},{6,2},{8,12},{10,14},{12,8},{14,10},{1,5},{3,7},... | collective-permute-start | bytes 393224 | tf_op jit(solution)/shard_map/ppermute | solution.py:513
  54.3 4.1 %collective-permute-start.11 = (f32[64,256]{1,0:T(8,128)S(1)}, f32[64,256]{1,0:T(8,128)S(1)}, u32[]{:S(2)}, u32[]{:S(2)}) collective-permute-start(f32[64,256]{1,0:T(8,128)S(1)} %add.26.pay0_ref), channel_id=1, source_target_pairs={{0,1},{1,0},{2,3},{3,2},{4,5},{5,4},{6,7},{7,6},{8,9},{9,8},{10,11... | collective-permute-start | bytes 196616 | tf_op jit(solution)/shard_map/ppermute | solution.py:516
  54.4 15.8 %collective-permute-start.9 = (bf16[64,1024]{1,0:T(8,128)(2,1)}, bf16[64,1024]{1,0:T(8,128)(2,1)S(1)}, u32[]{:S(2)}, u32[]{:S(2)}) collective-permute-start(bf16[64,1024]{1,0:T(8,128)(2,1)} %get-tuple-element.53), channel_id=1, source_target_pairs={{0,8},{2,10},{4,12},{6,14},{8,0},{10,2},{12,4},{14,6},{1,9},{3,11}... | collective-permute-start | bytes 393224 | tf_op jit(solution)/shard_map/ppermute | solution.py:513
  56.8 13.4 %copy-start = (f32[64,1024]{1,0:T(8,128)S(1)}, f32[64,1024]{1,0:T(8,128)}, u32[]{:S(2)}) copy-start(f32[64,1024]{1,0:T(8,128)} %get-tuple-element.51.second_keep_ref) | copy-start | bytes 786436
  56.8 13.4 %collective-permute-start.10 = (bf16[64,1024]{1,0:T(8,128)(2,1)}, bf16[64,1024]{1,0:T(8,128)(2,1)S(1)}, u32[]{:S(2)}, u32[]{:S(2)}) collective-permute-start(bf16[64,1024]{1,0:T(8,128)(2,1)} %get-tuple-element.54), channel_id=1, source_target_pairs={{0,12},{2,14},{4,8},{6,10},{8,4},{10,6},{12,0},{14,2},{1,13},{3,15... | collective-permute-start | bytes 393224 | tf_op jit(solution)/shard_map/ppermute | solution.py:513
  56.9 7.0 %collective-permute-start.12 = (f32[64,256]{1,0:T(8,128)S(1)}, f32[64,256]{1,0:T(8,128)S(1)}, u32[]{:S(2)}, u32[]{:S(2)}) collective-permute-start(f32[64,256]{1,0:T(8,128)S(1)} %add.26.pay0_ref), channel_id=1, source_target_pairs={{0,16},{16,0},{1,17},{17,1},{2,18},{18,2},{3,19},{19,3},{4,20},{20... | collective-permute-start | bytes 196616 | tf_op jit(solution)/shard_map/ppermute | solution.py:635
  58.4 5.5 %collective-permute-start.13 = (f32[64,256]{1,0:T(8,128)S(1)}, f32[64,256]{1,0:T(8,128)S(1)}, u32[]{:S(2)}, u32[]{:S(2)}) collective-permute-start(f32[64,256]{1,0:T(8,128)S(1)} %add.26.pay0_ref), channel_id=1, source_target_pairs={{0,17},{1,16},{16,1},{17,0},{2,19},{3,18},{18,3},{19,2},{4,21},{5,... | collective-permute-start | bytes 196616 | tf_op jit(solution)/shard_map/ppermute | solution.py:636
  72.8 1.3 %collective-permute-start.14 = (f32[8,2048]{1,0:T(8,128)S(1)}, f32[8,2048]{1,0:T(8,128)S(1)}, u32[]{:S(2)}, u32[]{:S(2)}) collective-permute-start(f32[8,2048]{1,0:T(8,128)S(1)} %get-tuple-element.59), channel_id=1, source_target_pairs={{0,1},{1,0},{2,3},{3,2},{4,5},{5,4},{6,7},{7,6},{8,9},{9,8},{10,11... | collective-permute-start | bytes 196616 | tf_op jit(solution)/shard_map/ppermute | solution.py:516
  74.1 5.9 %collective-permute-start.17 = (bf16[8,2048]{1,0:T(8,128)(2,1)S(1)}, bf16[8,2048]{1,0:T(8,128)(2,1)S(1)}, u32[]{:S(2)}, u32[]{:S(2)}) collective-permute-start(bf16[8,2048]{1,0:T(8,128)(2,1)S(1)} %get-tuple-element.61), channel_id=1, source_target_pairs={{0,6},{2,4},{4,2},{6,0},{8,14},{10,12},{12,10},{14,8},{1,7},{3,5},... | collective-permute-start | bytes 98312 | tf_op jit(solution)/shard_map/ppermute | solution.py:513
  78.1 3.9 %collective-permute-start.16 = (bf16[8,2048]{1,0:T(8,128)(2,1)S(1)}, bf16[8,2048]{1,0:T(8,128)(2,1)S(1)}, u32[]{:S(2)}, u32[]{:S(2)}) collective-permute-start(bf16[8,2048]{1,0:T(8,128)(2,1)S(1)} %get-tuple-element.61), channel_id=1, source_target_pairs={{0,4},{2,6},{4,0},{6,2},{8,12},{10,14},{12,8},{14,10},{1,5},{3,7},... | collective-permute-start | bytes 98312 | tf_op jit(solution)/shard_map/ppermute | solution.py:513
  78.1 3.9 %collective-permute-start.15 = (bf16[8,2048]{1,0:T(8,128)(2,1)S(1)}, bf16[8,2048]{1,0:T(8,128)(2,1)S(1)}, u32[]{:S(2)}, u32[]{:S(2)}) collective-permute-start(bf16[8,2048]{1,0:T(8,128)(2,1)S(1)} %get-tuple-element.61), channel_id=1, source_target_pairs={{0,2},{2,0},{4,6},{6,4},{8,10},{10,8},{12,14},{14,12},{1,3},{3,1},... | collective-permute-start | bytes 98312 | tf_op jit(solution)/shard_map/ppermute | solution.py:513
  82.0 4.9 %collective-permute-start.18 = (bf16[8,2048]{1,0:T(8,128)(2,1)S(1)}, bf16[8,2048]{1,0:T(8,128)(2,1)S(1)}, u32[]{:S(2)}, u32[]{:S(2)}) collective-permute-start(bf16[8,2048]{1,0:T(8,128)(2,1)S(1)} %fusion), channel_id=1, source_target_pairs={{0,8},{2,10},{4,12},{6,14},{8,0},{10,2},{12,4},{14,6},{1,9},{3,11}... | collective-permute-start | bytes 98312 | tf_op jit(solution)/shard_map/ppermute | solution.py:513
  86.9 1.3 %collective-permute-start.19 = (bf16[8,2048]{1,0:T(8,128)(2,1)S(1)}, bf16[8,2048]{1,0:T(8,128)(2,1)S(1)}, u32[]{:S(2)}, u32[]{:S(2)}) collective-permute-start(bf16[8,2048]{1,0:T(8,128)(2,1)S(1)} %add_convert_fusion.mine_ref), channel_id=1, source_target_pairs={{0,1},{1,0},{2,3},{3,2},{4,5},{5,4},{6,7},{7,6},{8,9},{9,8},{10,11... | collective-permute-start | bytes 98312 | tf_op jit(solution)/shard_map/ppermute | solution.py:516

commit v17 on v16

--- a/solution.py
+++ b/solution.py
@@ -167,7 +167,7 @@
 
 
 def assemble_columns(inv_ref, inv_row, tiles_ref, put):
-    @pl.loop(0, 16, unroll=4)
+    @pl.loop(0, 16, unroll=8)
     def _(block_row):
         for pair in range(8):
             cell = block_row * 16 + 2 * pair
@@ -666,11 +666,9 @@
     )(first_keep, first_back, second_keep, *second_back, *pay_parts)
 
     sums = mine + core_flip(theirs)
-    x_part, z_part, xz_part = [
-        owner_flip(sums.astype(BF), bits).astype(F32) for bits in (1, 2, 3)
-    ]
-    sums = (sums + x_part) + (z_part + xz_part)
-    sums = (sums + owner_flip(sums.astype(BF), 4).astype(F32)).astype(BF)
+    sums = sums + owner_flip(sums.astype(BF), 1).astype(F32)
+    parts = [owner_flip(sums.astype(BF), bits).astype(F32) for bits in (2, 4, 6)]
+    sums = ((sums + parts[0]) + (parts[1] + parts[2])).astype(BF)
 
     return pl.pallas_call(
         product_kernel,

time: 90.6 us -> 90.2 us (level)
  transfers between devices with their start and end apart: 22 -> 22, of which waited for: 10 -> 11; matrix products, arithmetic and copies ran while one was open for 2% -> 2% of each run, Pallas kernels for 16% -> 16%
where the time goes in v17:
time: 90.2 us; the launch traced here: 89.8 us
  starting transfers between devices  35.5 us (39%)
  Pallas kernels  26.2 us (29%)
  waiting for transfers between devices  26.2 us (29%)
  other arithmetic  1.66 us (2%)
    ppermute x13, starting transfers between devices, owner_flip(): return lax.ppermute(value, 'fsdp', [(i, i ^ bits) for i in range(8)])  22.2 us
    ppermute x13, waiting for transfers between devices, owner_flip(): return lax.ppermute(value, 'fsdp', [(i, i ^ bits) for i in range(8)])  20.4 us
    all_to_all x2, starting transfers between devices, zone_exchange(): lax.all_to_all(value, 'fsdp', split_axis=0, concat_axis=0, tiled=True, ax...  9.94 us
    pallas_call x1, Pallas kernels, pair_split(): pl.pallas_call(own_kernel, out_shape=(jax.ShapeDtypeStruct((8, 1024, 256)...  7.37 us
    pallas_call x1, Pallas kernels, pair_split(): pl.pallas_call(first_kernel, out_shape=(jax.ShapeDtypeStruct((64, 1024),...  4.78 us
    pallas_call x1, Pallas kernels, pair_split(): pl.pallas_call(second_kernel, out_shape=(jax.ShapeDtypeStruct((64, 1024),...  4.78 us
    all_to_all x2, waiting for transfers between devices, zone_exchange(): lax.all_to_all(value, 'fsdp', split_axis=0, concat_axis=0, tiled=True, ax...  3.3 us
    pallas_call x1, Pallas kernels, pair_split(): pl.pallas_call(middle_kernel, out_shape=(jax.ShapeDtypeStruct((8, 2048),...  2.61 us
  transfers between devices with their start and end apart: 22, of which 11 were waited for; matrix products, arithmetic and copies ran while one was open for 2% of the time, Pallas kernels for 16%

profile of v17, /device:TPU:0, one launch (start us, length us, event | category | flops | bytes accessed | tf_op | source)
XLA Modules:
  0.0 89.8 jit_solution(15737791975483767001)
XLA Ops:
  0.0 2.4 %head.1 = (bf16[4,64,2048]{2,1,0:T(8,128)(2,1)}, bf16[48,4096]{1,0:T(8,128)(2,1)}, bf16[64,4096]{1,0:T(8,128)(2,1)}) custom-call(bf16[64,8192]{1,0:T(8,128)(2,1)} %tok_in_ref.1, bf16[160,4096]{1,0:T(8,128)(2,1)} %gate_ref.3, bf16[160,4096]{1,0:T(8,128)(2,1)} %up_ref.3), custom_call_target="tpu_custom_call" | custom-call | tf_op jit(solution)/shard_map/head/pallas_call | solution.py:528
  2.5 6.5 %all-to-all-start = ((bf16[4,64,2048]{2,1,0:T(8,128)(2,1)}), bf16[4,64,2048]{2,1,0:T(8,128)(2,1)S(1)}, u32[]{:S(2)}, u32[]{:S(2)}) async-start(bf16[4,64,2048]{2,1,0:T(8,128)(2,1)} %get-tuple-element.37), calls=%async_computation | async-start | bytes 2097152 | tf_op jit(solution)/shard_map/all_to_all | solution.py:519
  8.9 1.5 %collective-permute-start.2 = (bf16[48,4096]{1,0:T(8,128)(2,1)S(1)}, bf16[48,4096]{1,0:T(8,128)(2,1)S(1)}, u32[]{:S(2)}, u32[]{:S(2)}) collective-permute-start(bf16[48,4096]{1,0:T(8,128)(2,1)S(1)} %copy-done.6), channel_id=1, source_target_pairs={{0,2},{2,0},{4,6},{6,4},{8,10},{10,8},{12,14},{14,12},{1,3},{3,1},... | collective-permute-start | bytes 1179656 | tf_op jit(solution)/shard_map/ppermute | solution.py:513
  11.7 7.4 %own_blocks.1 = (bf16[8,1024,256]{2,1,0:T(8,128)(2,1)}, f32[64,256]{1,0:T(8,128)}) custom-call(s32[3,256]{1,0:T(4,128)} %select_reduce_fusion.inv_ref, bf16[160,4096]{1,0:T(8,128)(2,1)} %gate_ref.3, bf16[160,4096]{1,0:T(8,128)(2,1)} %up_ref.3, bf16[160,4096]{1,0:T(8,128)(2,1)} %down_ref.1, bf16[32,1024]{1,0:T(8,128)(2,1)} %sketch_ref.1, ...), custom_call_target="tpu_custom_call" | custom-call | tf_op jit(solution)/shard_map/own_blocks/pallas_call | solution.py:555
  19.1 1.9 %collective-permute-done.2.a_in_ref = bf16[48,4096]{1,0:T(8,128)(2,1)S(1)} collective-permute-done((bf16[48,4096]{1,0:T(8,128)(2,1)S(1)}, bf16[48,4096]{1,0:T(8,128)(2,1)S(1)}, u32[]{:S(2)}, u32[]{:S(2)}) %collective-permute-start.2) | collective-permute-done | bytes 393248 | tf_op jit(solution)/shard_map/ppermute | solution.py:513
  21.0 1.5 %collective-permute-start.3 = (bf16[48,4096]{1,0:T(8,128)(2,1)S(1)}, bf16[48,4096]{1,0:T(8,128)(2,1)S(1)}, u32[]{:S(2)}, u32[]{:S(2)}) collective-permute-start(bf16[48,4096]{1,0:T(8,128)(2,1)S(1)} %collective-permute-done.2.a_in_ref), channel_id=1, source_target_pairs={{0,16},{16,0},{1,17},{17,1},{2,18},{18,2},{3,19},{19,3},{4,20},{20... | collective-permute-start | bytes 1179656 | tf_op jit(solution)/shard_map/ppermute | solution.py:578
  22.5 2.0 %collective-permute-start.4 = (f32[64,256]{1,0:T(8,128)}, f32[64,256]{1,0:T(8,128)S(1)}, u32[]{:S(2)}, u32[]{:S(2)}) collective-permute-start(f32[64,256]{1,0:T(8,128)} %get-tuple-element.38), channel_id=1, source_target_pairs={{0,4},{2,6},{4,0},{6,2},{8,12},{10,14},{12,8},{14,10},{1,5},{3,7},... | collective-permute-start | bytes 196616 | tf_op jit(solution)/shard_map/ppermute | solution.py:513
  24.5 3.0 %collective-permute-done.4 = f32[64,256]{1,0:T(8,128)S(1)} collective-permute-done((f32[64,256]{1,0:T(8,128)}, f32[64,256]{1,0:T(8,128)S(1)}, u32[]{:S(2)}, u32[]{:S(2)}) %collective-permute-start.4) | collective-permute-done | bytes 65568 | tf_op jit(solution)/shard_map/ppermute | solution.py:513
  27.5 0.8 add.24
  28.3 4.6 %collective-permute-start.5 = (f32[64,256]{1,0:T(8,128)S(1)}, f32[64,256]{1,0:T(8,128)S(1)}, u32[]{:S(2)}, u32[]{:S(2)}) collective-permute-start(f32[64,256]{1,0:T(8,128)S(1)} %add.24), channel_id=1, source_target_pairs={{0,8},{2,10},{4,12},{6,14},{8,0},{10,2},{12,4},{14,6},{1,9},{3,11}... | collective-permute-start | bytes 196616 | tf_op jit(solution)/shard_map/ppermute | solution.py:513
  32.9 1.5 %collective-permute-start = (s32[3,256]{1,0:T(4,128)S(1)}, s32[3,256]{1,0:T(4,128)S(1)}, u32[]{:S(2)}, u32[]{:S(2)}) collective-permute-start(s32[3,256]{1,0:T(4,128)S(1)} %copy-done.1), channel_id=1, source_target_pairs={{0,2},{2,0},{4,6},{6,4},{8,10},{10,8},{12,14},{14,12},{1,3},{3,1},... | collective-permute-start | bytes 9224 | tf_op jit(solution)/shard_map/ppermute | solution.py:513
  34.4 3.1 %collective-permute-done.5 = f32[64,256]{1,0:T(8,128)S(1)} collective-permute-done((f32[64,256]{1,0:T(8,128)S(1)}, f32[64,256]{1,0:T(8,128)S(1)}, u32[]{:S(2)}, u32[]{:S(2)}) %collective-permute-start.5) | collective-permute-done | bytes 65568 | tf_op jit(solution)/shard_map/ppermute | solution.py:513
  37.5 4.8 %first_partial.1 = (f32[64,1024]{1,0:T(8,128)S(1)}, bf16[4,64,1024]{2,1,0:T(8,128)(2,1)}, bf16[4,1024,256]{2,1,0:T(8,128)(2,1)}, bf16[2,256,1024]{2,1,0:T(8,128)(2,1)}) custom-call(s32[3,256]{1,0:T(4,128)S(1)} %collective-permute-done.inv_ref, bf16[48,4096]{1,0:T(8,128)(2,1)S(1)} %collective-permute-done.2.a_in_ref, ...), custom_call_target="tpu_custom_call" | custom-call | tf_op jit(solution)/shard_map/first_partial/pallas_call | solution.py:585
  42.4 3.5 %all-to-all-start.1 = ((bf16[4,64,1024]{2,1,0:T(8,128)(2,1)}), bf16[4,64,1024]{2,1,0:T(8,128)(2,1)S(1)}, u32[]{:S(2)}, u32[]{:S(2)}) async-start(bf16[4,64,1024]{2,1,0:T(8,128)(2,1)} %get-tuple-element.45), calls=%async_computation.1 | async-start | bytes 1048576 | tf_op jit(solution)/shard_map/all_to_all | solution.py:519
  45.9 1.6 %collective-permute-start.7 = (f32[64,256]{1,0:T(8,128)S(1)}, f32[64,256]{1,0:T(8,128)S(1)}, u32[]{:S(2)}, u32[]{:S(2)}) collective-permute-start(f32[64,256]{1,0:T(8,128)S(1)} %add.25), channel_id=1, source_target_pairs={{0,2},{2,0},{4,6},{6,4},{8,10},{10,8},{12,14},{14,12},{1,3},{3,1},... | collective-permute-start | bytes 196616 | tf_op jit(solution)/shard_map/ppermute | solution.py:513
  47.4 4.8 %second_partial.1 = (f32[64,1024]{1,0:T(8,128)}, bf16[64,1024]{1,0:T(8,128)(2,1)}, bf16[64,1024]{1,0:T(8,128)(2,1)}, bf16[64,1024]{1,0:T(8,128)(2,1)}) custom-call(bf16[4,1024,256]{2,1,0:T(8,128)(2,1)} %collective-permute-done.6.near_in_ref, bf16[8,1024,256]{2,1,0:T(8,128)(2,1)} %get-tuple-element.56.weight_in_ref, ...), custom_call_target="tpu_custom_call" | custom-call | tf_op jit(solution)/shard_map/second_partial/pallas_call | solution.py:611
  52.2 2.0 %collective-permute-start.8 = (bf16[64,1024]{1,0:T(8,128)(2,1)}, bf16[64,1024]{1,0:T(8,128)(2,1)S(1)}, u32[]{:S(2)}, u32[]{:S(2)}) collective-permute-start(bf16[64,1024]{1,0:T(8,128)(2,1)} %get-tuple-element.52), channel_id=1, source_target_pairs={{0,4},{2,6},{4,0},{6,2},{8,12},{10,14},{12,8},{14,10},{1,5},{3,7},... | collective-permute-start | bytes 393224 | tf_op jit(solution)/shard_map/ppermute | solution.py:513
  54.3 2.4 %collective-permute-start.9 = (bf16[64,1024]{1,0:T(8,128)(2,1)}, bf16[64,1024]{1,0:T(8,128)(2,1)S(1)}, u32[]{:S(2)}, u32[]{:S(2)}) collective-permute-start(bf16[64,1024]{1,0:T(8,128)(2,1)} %get-tuple-element.53), channel_id=1, source_target_pairs={{0,8},{2,10},{4,12},{6,14},{8,0},{10,2},{12,4},{14,6},{1,9},{3,11}... | collective-permute-start | bytes 393224 | tf_op jit(solution)/shard_map/ppermute | solution.py:513
  56.8 1.5 %collective-permute-start.12 = (f32[64,256]{1,0:T(8,128)S(1)}, f32[64,256]{1,0:T(8,128)S(1)}, u32[]{:S(2)}, u32[]{:S(2)}) collective-permute-start(f32[64,256]{1,0:T(8,128)S(1)} %add.26.pay0_ref), channel_id=1, source_target_pairs={{0,16},{16,0},{1,17},{17,1},{2,18},{18,2},{3,19},{19,3},{4,20},{20... | collective-permute-start | bytes 196616 | tf_op jit(solution)/shard_map/ppermute | solution.py:635
  58.4 3.3 %all-to-all-done.1.first_ref = bf16[4,64,1024]{2,1,0:T(8,128)(2,1)S(1)} async-done(((bf16[4,64,1024]{2,1,0:T(8,128)(2,1)}), bf16[4,64,1024]{2,1,0:T(8,128)(2,1)S(1)}, u32[]{:S(2)}, u32[]{:S(2)}) %all-to-all-start.1) | async-done | bytes 524320 | tf_op jit(solution)/shard_map/all_to_all | solution.py:519
  61.6 2.2 %fetch_weights.1.weight_ref = bf16[8,1024,256]{2,1,0:T(8,128)(2,1)S(1)} custom-call(bf16[8,1024,256]{2,1,0:T(8,128)(2,1)} %get-tuple-element.56.weight_in_ref), custom_call_target="tpu_custom_call" | custom-call | tf_op jit(solution)/shard_map/fetch_weights/pallas_call | solution.py:640
  63.9 6.2 %collective-permute-done.9.second2_ref = bf16[64,1024]{1,0:T(8,128)(2,1)S(1)} collective-permute-done((bf16[64,1024]{1,0:T(8,128)(2,1)}, bf16[64,1024]{1,0:T(8,128)(2,1)S(1)}, u32[]{:S(2)}, u32[]{:S(2)}) %collective-permute-start.9) | collective-permute-done | bytes 131104 | tf_op jit(solution)/shard_map/ppermute | solution.py:513
  70.1 2.6 %token_sums.1 = (f32[8,2048]{1,0:T(8,128)S(1)}, f32[8,2048]{1,0:T(8,128)S(1)}) custom-call(f32[64,1024]{1,0:T(8,128)S(1)} %get-tuple-element.44.first_keep_ref, bf16[4,64,1024]{2,1,0:T(8,128)(2,1)S(1)} %all-to-all-done.1.first_ref, f32[64,1024]{1,0:T(8,128)S(1)} %copy-done, bf16[64,1024]{1,0:T(8,128)(2,1)S(1)} %collective-permute-done.8.second1_ref, ...), custom_call_target="tpu_custom_call" | custom-call | tf_op jit(solution)/shard_map/token_sums/pallas_call | solution.py:651
  72.8 1.2 %collective-permute-done.14 = f32[8,2048]{1,0:T(8,128)S(1)} collective-permute-done((f32[8,2048]{1,0:T(8,128)S(1)}, f32[8,2048]{1,0:T(8,128)S(1)}, u32[]{:S(2)}, u32[]{:S(2)}) %collective-permute-start.14) | collective-permute-done | bytes 65568 | tf_op jit(solution)/shard_map/ppermute | solution.py:516
  74.0 1.6 %collective-permute-start.15 = (bf16[8,2048]{1,0:T(8,128)(2,1)S(1)}, bf16[8,2048]{1,0:T(8,128)(2,1)S(1)}, u32[]{:S(2)}, u32[]{:S(2)}) collective-permute-start(bf16[8,2048]{1,0:T(8,128)(2,1)S(1)} %get-tuple-element.61), channel_id=1, source_target_pairs={{0,2},{2,0},{4,6},{6,4},{8,10},{10,8},{12,14},{14,12},{1,3},{3,1},... | collective-permute-start | bytes 98312 | tf_op jit(solution)/shard_map/ppermute | solution.py:513
  75.6 2.4 %collective-permute-done.15 = bf16[8,2048]{1,0:T(8,128)(2,1)S(1)} collective-permute-done((bf16[8,2048]{1,0:T(8,128)(2,1)S(1)}, bf16[8,2048]{1,0:T(8,128)(2,1)S(1)}, u32[]{:S(2)}, u32[]{:S(2)}) %collective-permute-start.15) | collective-permute-done | bytes 32800 | tf_op jit(solution)/shard_map/ppermute | solution.py:513
  78.0 1.6 %collective-permute-start.18 = (bf16[8,2048]{1,0:T(8,128)(2,1)S(1)}, bf16[8,2048]{1,0:T(8,128)(2,1)S(1)}, u32[]{:S(2)}, u32[]{:S(2)}) collective-permute-start(bf16[8,2048]{1,0:T(8,128)(2,1)S(1)} %fusion), channel_id=1, source_target_pairs={{0,12},{2,14},{4,8},{6,10},{8,4},{10,6},{12,0},{14,2},{1,13},{3,15... | collective-permute-start | bytes 98312 | tf_op jit(solution)/shard_map/ppermute | solution.py:513
  79.6 2.9 %collective-permute-start.17 = (bf16[8,2048]{1,0:T(8,128)(2,1)S(1)}, bf16[8,2048]{1,0:T(8,128)(2,1)S(1)}, u32[]{:S(2)}, u32[]{:S(2)}) collective-permute-start(bf16[8,2048]{1,0:T(8,128)(2,1)S(1)} %fusion), channel_id=1, source_target_pairs={{0,8},{2,10},{4,12},{6,14},{8,0},{10,2},{12,4},{14,6},{1,9},{3,11}... | collective-permute-start | bytes 98312 | tf_op jit(solution)/shard_map/ppermute | solution.py:513
  82.5 1.6 %collective-permute-done.18 = bf16[8,2048]{1,0:T(8,128)(2,1)S(1)} collective-permute-done((bf16[8,2048]{1,0:T(8,128)(2,1)S(1)}, bf16[8,2048]{1,0:T(8,128)(2,1)S(1)}, u32[]{:S(2)}, u32[]{:S(2)}) %collective-permute-start.18) | collective-permute-done | bytes 32800 | tf_op jit(solution)/shard_map/ppermute | solution.py:513
  84.8 1.6 %collective-permute-done.16 = bf16[8,2048]{1,0:T(8,128)(2,1)S(1)} collective-permute-done((bf16[8,2048]{1,0:T(8,128)(2,1)S(1)}, bf16[8,2048]{1,0:T(8,128)(2,1)S(1)}, u32[]{:S(2)}, u32[]{:S(2)}) %collective-permute-start.16) | collective-permute-done | bytes 32800 | tf_op jit(solution)/shard_map/ppermute | solution.py:513
  86.5 1.2 %collective-permute-done.19.theirs_ref = bf16[8,2048]{1,0:T(8,128)(2,1)S(1)} collective-permute-done((bf16[8,2048]{1,0:T(8,128)(2,1)S(1)}, bf16[8,2048]{1,0:T(8,128)(2,1)S(1)}, u32[]{:S(2)}, u32[]{:S(2)}) %collective-permute-start.19) | collective-permute-done | bytes 32800 | tf_op jit(solution)/shard_map/ppermute | solution.py:516
  87.7 2.1 %products.1 = f32[16,1024]{1,0:T(8,128)} custom-call(bf16[8,2048]{1,0:T(8,128)(2,1)S(1)} %add_convert_fusion.mine_ref, bf16[8,2048]{1,0:T(8,128)(2,1)S(1)} %collective-permute-done.19.theirs_ref, bf16[8,1024,256]{2,1,0:T(8,128)(2,1)S(1)} %fetch_weights.1.weight_ref), custom_call_target="tpu_custom_call" | custom-call | tf_op jit(solution)/shard_map/products/pallas_call | solution.py:673
  (41 shorter events, 2.4 us)
Async XLA Ops:
  0.0 10.9 %copy-start.2 = (s32[160]{0:T(256)S(1)}, s32[160]{0:T(256)}, u32[]{:S(2)}) copy-start(s32[160]{0:T(256)} %param.16) | copy-start | bytes 1924
  0.0 10.9 %copy-start.3 = (s32[160]{0:T(256)S(1)}, s32[160]{0:T(256)}, u32[]{:S(2)}) copy-start(s32[160]{0:T(256)} %param.14) | copy-start | bytes 1924
  0.0 10.9 %copy-start.4 = (s32[160]{0:T(256)S(1)}, s32[160]{0:T(256)}, u32[]{:S(2)}) copy-start(s32[160]{0:T(256)} %param.12) | copy-start | bytes 1924
  2.4 6.5 %copy-start.6 = (bf16[48,4096]{1,0:T(8,128)(2,1)S(1)}, bf16[48,4096]{1,0:T(8,128)(2,1)}, u32[]{:S(2)}) copy-start(bf16[48,4096]{1,0:T(8,128)(2,1)} %get-tuple-element.34) | copy-start | bytes 1179652
  2.4 8.0 %copy-start.5 = (bf16[64,4096]{1,0:T(8,128)(2,1)S(1)}, bf16[64,4096]{1,0:T(8,128)(2,1)}, u32[]{:S(2)}) copy-start(bf16[64,4096]{1,0:T(8,128)(2,1)} %get-tuple-element.33) | copy-start | bytes 1572868
  2.5 35.0 %all-to-all-start = ((bf16[4,64,2048]{2,1,0:T(8,128)(2,1)}), bf16[4,64,2048]{2,1,0:T(8,128)(2,1)S(1)}, u32[]{:S(2)}, u32[]{:S(2)}) async-start(bf16[4,64,2048]{2,1,0:T(8,128)(2,1)} %get-tuple-element.37), calls=%async_computation | async-start | bytes 2097152 | tf_op jit(solution)/shard_map/all_to_all | solution.py:519
  8.9 12.0 %collective-permute-start.2 = (bf16[48,4096]{1,0:T(8,128)(2,1)S(1)}, bf16[48,4096]{1,0:T(8,128)(2,1)S(1)}, u32[]{:S(2)}, u32[]{:S(2)}) collective-permute-start(bf16[48,4096]{1,0:T(8,128)(2,1)S(1)} %copy-done.6), channel_id=1, source_target_pairs={{0,2},{2,0},{4,6},{6,4},{8,10},{10,8},{12,14},{14,12},{1,3},{3,1},... | collective-permute-start | bytes 1179656 | tf_op jit(solution)/shard_map/ppermute | solution.py:513
  10.4 27.1 %collective-permute-start.1 = (bf16[64,4096]{1,0:T(8,128)(2,1)S(1)}, bf16[64,4096]{1,0:T(8,128)(2,1)S(1)}, u32[]{:S(2)}, u32[]{:S(2)}) collective-permute-start(bf16[64,4096]{1,0:T(8,128)(2,1)S(1)} %copy-done.5), channel_id=1, source_target_pairs={{0,2},{2,0},{4,6},{6,4},{8,10},{10,8},{12,14},{14,12},{1,3},{3,1},... | collective-permute-start | bytes 1572872 | tf_op jit(solution)/shard_map/ppermute | solution.py:513
  11.7 21.2 %copy-start.1 = (s32[3,256]{1,0:T(4,128)S(1)}, s32[3,256]{1,0:T(4,128)}, u32[]{:S(2)}) copy-start(s32[3,256]{1,0:T(4,128)} %select_reduce_fusion.inv_ref) | copy-start | bytes 9220
  21.0 16.5 %collective-permute-start.3 = (bf16[48,4096]{1,0:T(8,128)(2,1)S(1)}, bf16[48,4096]{1,0:T(8,128)(2,1)S(1)}, u32[]{:S(2)}, u32[]{:S(2)}) collective-permute-start(bf16[48,4096]{1,0:T(8,128)(2,1)S(1)} %collective-permute-done.2.a_in_ref), channel_id=1, source_target_pairs={{0,16},{16,0},{1,17},{17,1},{2,18},{18,2},{3,19},{19,3},{4,20},{20... | collective-permute-start | bytes 1179656 | tf_op jit(solution)/shard_map/ppermute | solution.py:578
  22.5 5.0 %collective-permute-start.4 = (f32[64,256]{1,0:T(8,128)}, f32[64,256]{1,0:T(8,128)S(1)}, u32[]{:S(2)}, u32[]{:S(2)}) collective-permute-start(f32[64,256]{1,0:T(8,128)} %get-tuple-element.38), channel_id=1, source_target_pairs={{0,4},{2,6},{4,0},{6,2},{8,12},{10,14},{12,8},{14,10},{1,5},{3,7},... | collective-permute-start | bytes 196616 | tf_op jit(solution)/shard_map/ppermute | solution.py:513
  28.3 9.1 %collective-permute-start.5 = (f32[64,256]{1,0:T(8,128)S(1)}, f32[64,256]{1,0:T(8,128)S(1)}, u32[]{:S(2)}, u32[]{:S(2)}) collective-permute-start(f32[64,256]{1,0:T(8,128)S(1)} %add.24), channel_id=1, source_target_pairs={{0,8},{2,10},{4,12},{6,14},{8,0},{10,2},{12,4},{14,6},{1,9},{3,11}... | collective-permute-start | bytes 196616 | tf_op jit(solution)/shard_map/ppermute | solution.py:513
  32.9 4.6 %collective-permute-start = (s32[3,256]{1,0:T(4,128)S(1)}, s32[3,256]{1,0:T(4,128)S(1)}, u32[]{:S(2)}, u32[]{:S(2)}) collective-permute-start(s32[3,256]{1,0:T(4,128)S(1)} %copy-done.1), channel_id=1, source_target_pairs={{0,2},{2,0},{4,6},{6,4},{8,10},{10,8},{12,14},{14,12},{1,3},{3,1},... | collective-permute-start | bytes 9224 | tf_op jit(solution)/shard_map/ppermute | solution.py:513
  42.3 5.1 %collective-permute-start.6 = (bf16[4,1024,256]{2,1,0:T(8,128)(2,1)}, bf16[4,1024,256]{2,1,0:T(8,128)(2,1)}, u32[]{:S(2)}, u32[]{:S(2)}) collective-permute-start(bf16[4,1024,256]{2,1,0:T(8,128)(2,1)} %get-tuple-element.47), channel_id=1, source_target_pairs={{0,1},{1,0},{2,3},{3,2},{4,5},{5,4},{6,7},{7,6},{8,9},{9,8},{10,11... | collective-permute-start | bytes 6291464 | tf_op jit(solution)/shard_map/ppermute | solution.py:516
  42.4 19.3 %all-to-all-start.1 = ((bf16[4,64,1024]{2,1,0:T(8,128)(2,1)}), bf16[4,64,1024]{2,1,0:T(8,128)(2,1)S(1)}, u32[]{:S(2)}, u32[]{:S(2)}) async-start(bf16[4,64,1024]{2,1,0:T(8,128)(2,1)} %get-tuple-element.45), calls=%async_computation.1 | async-start | bytes 1048576 | tf_op jit(solution)/shard_map/all_to_all | solution.py:519
  45.9 6.3 %collective-permute-start.7 = (f32[64,256]{1,0:T(8,128)S(1)}, f32[64,256]{1,0:T(8,128)S(1)}, u32[]{:S(2)}, u32[]{:S(2)}) collective-permute-start(f32[64,256]{1,0:T(8,128)S(1)} %add.25), channel_id=1, source_target_pairs={{0,2},{2,0},{4,6},{6,4},{8,10},{10,8},{12,14},{14,12},{1,3},{3,1},... | collective-permute-start | bytes 196616 | tf_op jit(solution)/shard_map/ppermute | solution.py:513
  52.2 11.7 %collective-permute-start.8 = (bf16[64,1024]{1,0:T(8,128)(2,1)}, bf16[64,1024]{1,0:T(8,128)(2,1)S(1)}, u32[]{:S(2)}, u32[]{:S(2)}) collective-permute-start(bf16[64,1024]{1,0:T(8,128)(2,1)} %get-tuple-element.52), channel_id=1, source_target_pairs={{0,4},{2,6},{4,0},{6,2},{8,12},{10,14},{12,8},{14,10},{1,5},{3,7},... | collective-permute-start | bytes 393224 | tf_op jit(solution)/shard_map/ppermute | solution.py:513
  54.2 4.1 %collective-permute-start.11 = (f32[64,256]{1,0:T(8,128)S(1)}, f32[64,256]{1,0:T(8,128)S(1)}, u32[]{:S(2)}, u32[]{:S(2)}) collective-permute-start(f32[64,256]{1,0:T(8,128)S(1)} %add.26.pay0_ref), channel_id=1, source_target_pairs={{0,1},{1,0},{2,3},{3,2},{4,5},{5,4},{6,7},{7,6},{8,9},{9,8},{10,11... | collective-permute-start | bytes 196616 | tf_op jit(solution)/shard_map/ppermute | solution.py:516
  54.3 15.8 %collective-permute-start.9 = (bf16[64,1024]{1,0:T(8,128)(2,1)}, bf16[64,1024]{1,0:T(8,128)(2,1)S(1)}, u32[]{:S(2)}, u32[]{:S(2)}) collective-permute-start(bf16[64,1024]{1,0:T(8,128)(2,1)} %get-tuple-element.53), channel_id=1, source_target_pairs={{0,8},{2,10},{4,12},{6,14},{8,0},{10,2},{12,4},{14,6},{1,9},{3,11}... | collective-permute-start | bytes 393224 | tf_op jit(solution)/shard_map/ppermute | solution.py:513
  56.7 13.4 %copy-start = (f32[64,1024]{1,0:T(8,128)S(1)}, f32[64,1024]{1,0:T(8,128)}, u32[]{:S(2)}) copy-start(f32[64,1024]{1,0:T(8,128)} %get-tuple-element.51.second_keep_ref) | copy-start | bytes 786436
  56.7 13.4 %collective-permute-start.10 = (bf16[64,1024]{1,0:T(8,128)(2,1)}, bf16[64,1024]{1,0:T(8,128)(2,1)S(1)}, u32[]{:S(2)}, u32[]{:S(2)}) collective-permute-start(bf16[64,1024]{1,0:T(8,128)(2,1)} %get-tuple-element.54), channel_id=1, source_target_pairs={{0,12},{2,14},{4,8},{6,10},{8,4},{10,6},{12,0},{14,2},{1,13},{3,15... | collective-permute-start | bytes 393224 | tf_op jit(solution)/shard_map/ppermute | solution.py:513
  56.8 7.0 %collective-permute-start.12 = (f32[64,256]{1,0:T(8,128)S(1)}, f32[64,256]{1,0:T(8,128)S(1)}, u32[]{:S(2)}, u32[]{:S(2)}) collective-permute-start(f32[64,256]{1,0:T(8,128)S(1)} %add.26.pay0_ref), channel_id=1, source_target_pairs={{0,16},{16,0},{1,17},{17,1},{2,18},{18,2},{3,19},{19,3},{4,20},{20... | collective-permute-start | bytes 196616 | tf_op jit(solution)/shard_map/ppermute | solution.py:635
  58.4 5.5 %collective-permute-start.13 = (f32[64,256]{1,0:T(8,128)S(1)}, f32[64,256]{1,0:T(8,128)S(1)}, u32[]{:S(2)}, u32[]{:S(2)}) collective-permute-start(f32[64,256]{1,0:T(8,128)S(1)} %add.26.pay0_ref), channel_id=1, source_target_pairs={{0,17},{1,16},{16,1},{17,0},{2,19},{3,18},{18,3},{19,2},{4,21},{5,... | collective-permute-start | bytes 196616 | tf_op jit(solution)/shard_map/ppermute | solution.py:636
  72.7 1.3 %collective-permute-start.14 = (f32[8,2048]{1,0:T(8,128)S(1)}, f32[8,2048]{1,0:T(8,128)S(1)}, u32[]{:S(2)}, u32[]{:S(2)}) collective-permute-start(f32[8,2048]{1,0:T(8,128)S(1)} %get-tuple-element.59), channel_id=1, source_target_pairs={{0,1},{1,0},{2,3},{3,2},{4,5},{5,4},{6,7},{7,6},{8,9},{9,8},{10,11... | collective-permute-start | bytes 196616 | tf_op jit(solution)/shard_map/ppermute | solution.py:516
  74.0 4.0 %collective-permute-start.15 = (bf16[8,2048]{1,0:T(8,128)(2,1)S(1)}, bf16[8,2048]{1,0:T(8,128)(2,1)S(1)}, u32[]{:S(2)}, u32[]{:S(2)}) collective-permute-start(bf16[8,2048]{1,0:T(8,128)(2,1)S(1)} %get-tuple-element.61), channel_id=1, source_target_pairs={{0,2},{2,0},{4,6},{6,4},{8,10},{10,8},{12,14},{14,12},{1,3},{3,1},... | collective-permute-start | bytes 98312 | tf_op jit(solution)/shard_map/ppermute | solution.py:513
  78.0 6.1 %collective-permute-start.18 = (bf16[8,2048]{1,0:T(8,128)(2,1)S(1)}, bf16[8,2048]{1,0:T(8,128)(2,1)S(1)}, u32[]{:S(2)}, u32[]{:S(2)}) collective-permute-start(bf16[8,2048]{1,0:T(8,128)(2,1)S(1)} %fusion), channel_id=1, source_target_pairs={{0,12},{2,14},{4,8},{6,10},{8,4},{10,6},{12,0},{14,2},{1,13},{3,15... | collective-permute-start | bytes 98312 | tf_op jit(solution)/shard_map/ppermute | solution.py:513
  79.6 5.2 %collective-permute-start.17 = (bf16[8,2048]{1,0:T(8,128)(2,1)S(1)}, bf16[8,2048]{1,0:T(8,128)(2,1)S(1)}, u32[]{:S(2)}, u32[]{:S(2)}) collective-permute-start(bf16[8,2048]{1,0:T(8,128)(2,1)S(1)} %fusion), channel_id=1, source_target_pairs={{0,8},{2,10},{4,12},{6,14},{8,0},{10,2},{12,4},{14,6},{1,9},{3,11}... | collective-permute-start | bytes 98312 | tf_op jit(solution)/shard_map/ppermute | solution.py:513
  82.5 3.9 %collective-permute-start.16 = (bf16[8,2048]{1,0:T(8,128)(2,1)S(1)}, bf16[8,2048]{1,0:T(8,128)(2,1)S(1)}, u32[]{:S(2)}, u32[]{:S(2)}) collective-permute-start(bf16[8,2048]{1,0:T(8,128)(2,1)S(1)} %fusion), channel_id=1, source_target_pairs={{0,4},{2,6},{4,0},{6,2},{8,12},{10,14},{12,8},{14,10},{1,5},{3,7},... | collective-permute-start | bytes 98312 | tf_op jit(solution)/shard_map/ppermute | solution.py:513
  86.5 1.3 %collective-permute-start.19 = (bf16[8,2048]{1,0:T(8,128)(2,1)S(1)}, bf16[8,2048]{1,0:T(8,128)(2,1)S(1)}, u32[]{:S(2)}, u32[]{:S(2)}) collective-permute-start(bf16[8,2048]{1,0:T(8,128)(2,1)S(1)} %add_convert_fusion.mine_ref), channel_id=1, source_target_pairs={{0,1},{1,0},{2,3},{3,2},{4,5},{5,4},{6,7},{7,6},{8,9},{9,8},{10,11... | collective-permute-start | bytes 98312 | tf_op jit(solution)/shard_map/ppermute | solution.py:516

commit v18 on v17

--- a/solution.py
+++ b/solution.py
@@ -667,7 +667,7 @@
 
     sums = mine + core_flip(theirs)
     sums = sums + owner_flip(sums.astype(BF), 1).astype(F32)
-    parts = [owner_flip(sums.astype(BF), bits).astype(F32) for bits in (2, 4, 6)]
+    parts = [owner_flip(sums.astype(BF), bits).astype(F32) for bits in (4, 6, 2)]
     sums = ((sums + parts[0]) + (parts[1] + parts[2])).astype(BF)
 
     return pl.pallas_call(

time: 90.2 us -> 91.2 us (1.011)
    ppermute x13, waiting for transfers between devices: 20.4 us -> 21.4 us  [owner_flip(): return lax.ppermute(value, 'fsdp', [(i, i ^ bits) for i in range(8)])]
where the time goes in v18:
time: 91.2 us; the launch traced here: 90.8 us
  starting transfers between devices  35.6 us (39%)
  waiting for transfers between devices  27.1 us (30%)
  Pallas kernels  26.2 us (29%)
  other arithmetic  1.66 us (2%)
    ppermute x13, starting transfers between devices, owner_flip(): return lax.ppermute(value, 'fsdp', [(i, i ^ bits) for i in range(8)])  22.3 us
    ppermute x13, waiting for transfers between devices, owner_flip(): return lax.ppermute(value, 'fsdp', [(i, i ^ bits) for i in range(8)])  21.4 us
    all_to_all x2, starting transfers between devices, zone_exchange(): lax.all_to_all(value, 'fsdp', split_axis=0, concat_axis=0, tiled=True, ax...  9.94 us
    pallas_call x1, Pallas kernels, pair_split(): pl.pallas_call(own_kernel, out_shape=(jax.ShapeDtypeStruct((8, 1024, 256)...  7.37 us
    pallas_call x1, Pallas kernels, pair_split(): pl.pallas_call(first_kernel, out_shape=(jax.ShapeDtypeStruct((64, 1024),...  4.78 us
    pallas_call x1, Pallas kernels, pair_split(): pl.pallas_call(second_kernel, out_shape=(jax.ShapeDtypeStruct((64, 1024),...  4.78 us
    all_to_all x2, waiting for transfers between devices, zone_exchange(): lax.all_to_all(value, 'fsdp', split_axis=0, concat_axis=0, tiled=True, ax...  3.3 us
    pallas_call x1, Pallas kernels, pair_split(): pl.pallas_call(middle_kernel, out_shape=(jax.ShapeDtypeStruct((8, 2048),...  2.61 us
  transfers between devices with their start and end apart: 22, of which 11 were waited for; matrix products, arithmetic and copies ran while one was open for 2% of the time, Pallas kernels for 16%

profile of v18, /device:TPU:0, one launch (start us, length us, event | category | flops | bytes accessed | tf_op | source)
XLA Modules:
  0.0 90.8 jit_solution(10818201802075992641)
XLA Ops:
  0.0 2.4 %head.1 = (bf16[4,64,2048]{2,1,0:T(8,128)(2,1)}, bf16[48,4096]{1,0:T(8,128)(2,1)}, bf16[64,4096]{1,0:T(8,128)(2,1)}) custom-call(bf16[64,8192]{1,0:T(8,128)(2,1)} %tok_in_ref.1, bf16[160,4096]{1,0:T(8,128)(2,1)} %gate_ref.3, bf16[160,4096]{1,0:T(8,128)(2,1)} %up_ref.3), custom_call_target="tpu_custom_call" | custom-call | tf_op jit(solution)/shard_map/head/pallas_call | solution.py:528
  2.5 6.5 %all-to-all-start = ((bf16[4,64,2048]{2,1,0:T(8,128)(2,1)}), bf16[4,64,2048]{2,1,0:T(8,128)(2,1)S(1)}, u32[]{:S(2)}, u32[]{:S(2)}) async-start(bf16[4,64,2048]{2,1,0:T(8,128)(2,1)} %get-tuple-element.37), calls=%async_computation | async-start | bytes 2097152 | tf_op jit(solution)/shard_map/all_to_all | solution.py:519
  8.9 1.5 %collective-permute-start.2 = (bf16[48,4096]{1,0:T(8,128)(2,1)S(1)}, bf16[48,4096]{1,0:T(8,128)(2,1)S(1)}, u32[]{:S(2)}, u32[]{:S(2)}) collective-permute-start(bf16[48,4096]{1,0:T(8,128)(2,1)S(1)} %copy-done.6), channel_id=1, source_target_pairs={{0,2},{2,0},{4,6},{6,4},{8,10},{10,8},{12,14},{14,12},{1,3},{3,1},... | collective-permute-start | bytes 1179656 | tf_op jit(solution)/shard_map/ppermute | solution.py:513
  11.0 0.7 select_reduce_fusion.inv_ref
  11.7 7.4 %own_blocks.1 = (bf16[8,1024,256]{2,1,0:T(8,128)(2,1)}, f32[64,256]{1,0:T(8,128)}) custom-call(s32[3,256]{1,0:T(4,128)} %select_reduce_fusion.inv_ref, bf16[160,4096]{1,0:T(8,128)(2,1)} %gate_ref.3, bf16[160,4096]{1,0:T(8,128)(2,1)} %up_ref.3, bf16[160,4096]{1,0:T(8,128)(2,1)} %down_ref.1, bf16[32,1024]{1,0:T(8,128)(2,1)} %sketch_ref.1, ...), custom_call_target="tpu_custom_call" | custom-call | tf_op jit(solution)/shard_map/own_blocks/pallas_call | solution.py:555
  19.1 1.9 %collective-permute-done.2.a_in_ref = bf16[48,4096]{1,0:T(8,128)(2,1)S(1)} collective-permute-done((bf16[48,4096]{1,0:T(8,128)(2,1)S(1)}, bf16[48,4096]{1,0:T(8,128)(2,1)S(1)}, u32[]{:S(2)}, u32[]{:S(2)}) %collective-permute-start.2) | collective-permute-done | bytes 393248 | tf_op jit(solution)/shard_map/ppermute | solution.py:513
  21.0 1.5 %collective-permute-start.3 = (bf16[48,4096]{1,0:T(8,128)(2,1)S(1)}, bf16[48,4096]{1,0:T(8,128)(2,1)S(1)}, u32[]{:S(2)}, u32[]{:S(2)}) collective-permute-start(bf16[48,4096]{1,0:T(8,128)(2,1)S(1)} %collective-permute-done.2.a_in_ref), channel_id=1, source_target_pairs={{0,16},{16,0},{1,17},{17,1},{2,18},{18,2},{3,19},{19,3},{4,20},{20... | collective-permute-start | bytes 1179656 | tf_op jit(solution)/shard_map/ppermute | solution.py:578
  22.5 2.0 %collective-permute-start.4 = (f32[64,256]{1,0:T(8,128)}, f32[64,256]{1,0:T(8,128)S(1)}, u32[]{:S(2)}, u32[]{:S(2)}) collective-permute-start(f32[64,256]{1,0:T(8,128)} %get-tuple-element.38), channel_id=1, source_target_pairs={{0,4},{2,6},{4,0},{6,2},{8,12},{10,14},{12,8},{14,10},{1,5},{3,7},... | collective-permute-start | bytes 196616 | tf_op jit(solution)/shard_map/ppermute | solution.py:513
  24.5 3.0 %collective-permute-done.4 = f32[64,256]{1,0:T(8,128)S(1)} collective-permute-done((f32[64,256]{1,0:T(8,128)}, f32[64,256]{1,0:T(8,128)S(1)}, u32[]{:S(2)}, u32[]{:S(2)}) %collective-permute-start.4) | collective-permute-done | bytes 65568 | tf_op jit(solution)/shard_map/ppermute | solution.py:513
  27.5 0.8 add.24
  28.3 4.6 %collective-permute-start.5 = (f32[64,256]{1,0:T(8,128)S(1)}, f32[64,256]{1,0:T(8,128)S(1)}, u32[]{:S(2)}, u32[]{:S(2)}) collective-permute-start(f32[64,256]{1,0:T(8,128)S(1)} %add.24), channel_id=1, source_target_pairs={{0,8},{2,10},{4,12},{6,14},{8,0},{10,2},{12,4},{14,6},{1,9},{3,11}... | collective-permute-start | bytes 196616 | tf_op jit(solution)/shard_map/ppermute | solution.py:513
  32.9 1.5 %collective-permute-start = (s32[3,256]{1,0:T(4,128)S(1)}, s32[3,256]{1,0:T(4,128)S(1)}, u32[]{:S(2)}, u32[]{:S(2)}) collective-permute-start(s32[3,256]{1,0:T(4,128)S(1)} %copy-done.1), channel_id=1, source_target_pairs={{0,2},{2,0},{4,6},{6,4},{8,10},{10,8},{12,14},{14,12},{1,3},{3,1},... | collective-permute-start | bytes 9224 | tf_op jit(solution)/shard_map/ppermute | solution.py:513
  34.4 3.1 %collective-permute-done.5 = f32[64,256]{1,0:T(8,128)S(1)} collective-permute-done((f32[64,256]{1,0:T(8,128)S(1)}, f32[64,256]{1,0:T(8,128)S(1)}, u32[]{:S(2)}, u32[]{:S(2)}) %collective-permute-start.5) | collective-permute-done | bytes 65568 | tf_op jit(solution)/shard_map/ppermute | solution.py:513
  37.5 4.8 %first_partial.1 = (f32[64,1024]{1,0:T(8,128)S(1)}, bf16[4,64,1024]{2,1,0:T(8,128)(2,1)}, bf16[4,1024,256]{2,1,0:T(8,128)(2,1)}, bf16[2,256,1024]{2,1,0:T(8,128)(2,1)}) custom-call(s32[3,256]{1,0:T(4,128)S(1)} %collective-permute-done.inv_ref, bf16[48,4096]{1,0:T(8,128)(2,1)S(1)} %collective-permute-done.2.a_in_ref, ...), custom_call_target="tpu_custom_call" | custom-call | tf_op jit(solution)/shard_map/first_partial/pallas_call | solution.py:585
  42.4 3.5 %all-to-all-start.1 = ((bf16[4,64,1024]{2,1,0:T(8,128)(2,1)}), bf16[4,64,1024]{2,1,0:T(8,128)(2,1)S(1)}, u32[]{:S(2)}, u32[]{:S(2)}) async-start(bf16[4,64,1024]{2,1,0:T(8,128)(2,1)} %get-tuple-element.45), calls=%async_computation.1 | async-start | bytes 1048576 | tf_op jit(solution)/shard_map/all_to_all | solution.py:519
  45.9 1.6 %collective-permute-start.7 = (f32[64,256]{1,0:T(8,128)S(1)}, f32[64,256]{1,0:T(8,128)S(1)}, u32[]{:S(2)}, u32[]{:S(2)}) collective-permute-start(f32[64,256]{1,0:T(8,128)S(1)} %add.25), channel_id=1, source_target_pairs={{0,2},{2,0},{4,6},{6,4},{8,10},{10,8},{12,14},{14,12},{1,3},{3,1},... | collective-permute-start | bytes 196616 | tf_op jit(solution)/shard_map/ppermute | solution.py:513
  47.4 4.8 %second_partial.1 = (f32[64,1024]{1,0:T(8,128)}, bf16[64,1024]{1,0:T(8,128)(2,1)}, bf16[64,1024]{1,0:T(8,128)(2,1)}, bf16[64,1024]{1,0:T(8,128)(2,1)}) custom-call(bf16[4,1024,256]{2,1,0:T(8,128)(2,1)} %collective-permute-done.6.near_in_ref, bf16[8,1024,256]{2,1,0:T(8,128)(2,1)} %get-tuple-element.56.weight_in_ref, ...), custom_call_target="tpu_custom_call" | custom-call | tf_op jit(solution)/shard_map/second_partial/pallas_call | solution.py:611
  52.2 2.0 %collective-permute-start.8 = (bf16[64,1024]{1,0:T(8,128)(2,1)}, bf16[64,1024]{1,0:T(8,128)(2,1)S(1)}, u32[]{:S(2)}, u32[]{:S(2)}) collective-permute-start(bf16[64,1024]{1,0:T(8,128)(2,1)} %get-tuple-element.52), channel_id=1, source_target_pairs={{0,4},{2,6},{4,0},{6,2},{8,12},{10,14},{12,8},{14,10},{1,5},{3,7},... | collective-permute-start | bytes 393224 | tf_op jit(solution)/shard_map/ppermute | solution.py:513
  54.3 2.4 %collective-permute-start.9 = (bf16[64,1024]{1,0:T(8,128)(2,1)}, bf16[64,1024]{1,0:T(8,128)(2,1)S(1)}, u32[]{:S(2)}, u32[]{:S(2)}) collective-permute-start(bf16[64,1024]{1,0:T(8,128)(2,1)} %get-tuple-element.53), channel_id=1, source_target_pairs={{0,8},{2,10},{4,12},{6,14},{8,0},{10,2},{12,4},{14,6},{1,9},{3,11}... | collective-permute-start | bytes 393224 | tf_op jit(solution)/shard_map/ppermute | solution.py:513
  56.8 1.5 %collective-permute-start.12 = (f32[64,256]{1,0:T(8,128)S(1)}, f32[64,256]{1,0:T(8,128)S(1)}, u32[]{:S(2)}, u32[]{:S(2)}) collective-permute-start(f32[64,256]{1,0:T(8,128)S(1)} %add.26.pay0_ref), channel_id=1, source_target_pairs={{0,16},{16,0},{1,17},{17,1},{2,18},{18,2},{3,19},{19,3},{4,20},{20... | collective-permute-start | bytes 196616 | tf_op jit(solution)/shard_map/ppermute | solution.py:635
  58.4 3.3 %all-to-all-done.1.first_ref = bf16[4,64,1024]{2,1,0:T(8,128)(2,1)S(1)} async-done(((bf16[4,64,1024]{2,1,0:T(8,128)(2,1)}), bf16[4,64,1024]{2,1,0:T(8,128)(2,1)S(1)}, u32[]{:S(2)}, u32[]{:S(2)}) %all-to-all-start.1) | async-done | bytes 524320 | tf_op jit(solution)/shard_map/all_to_all | solution.py:519
  61.6 2.2 %fetch_weights.1.weight_ref = bf16[8,1024,256]{2,1,0:T(8,128)(2,1)S(1)} custom-call(bf16[8,1024,256]{2,1,0:T(8,128)(2,1)} %get-tuple-element.56.weight_in_ref), custom_call_target="tpu_custom_call" | custom-call | tf_op jit(solution)/shard_map/fetch_weights/pallas_call | solution.py:640
  63.9 6.2 %collective-permute-done.9.second2_ref = bf16[64,1024]{1,0:T(8,128)(2,1)S(1)} collective-permute-done((bf16[64,1024]{1,0:T(8,128)(2,1)}, bf16[64,1024]{1,0:T(8,128)(2,1)S(1)}, u32[]{:S(2)}, u32[]{:S(2)}) %collective-permute-start.9) | collective-permute-done | bytes 131104 | tf_op jit(solution)/shard_map/ppermute | solution.py:513
  70.1 2.6 %token_sums.1 = (f32[8,2048]{1,0:T(8,128)S(1)}, f32[8,2048]{1,0:T(8,128)S(1)}) custom-call(f32[64,1024]{1,0:T(8,128)S(1)} %get-tuple-element.44.first_keep_ref, bf16[4,64,1024]{2,1,0:T(8,128)(2,1)S(1)} %all-to-all-done.1.first_ref, f32[64,1024]{1,0:T(8,128)S(1)} %copy-done, bf16[64,1024]{1,0:T(8,128)(2,1)S(1)} %collective-permute-done.8.second1_ref, ...), custom_call_target="tpu_custom_call" | custom-call | tf_op jit(solution)/shard_map/token_sums/pallas_call | solution.py:651
  72.8 1.2 %collective-permute-done.14 = f32[8,2048]{1,0:T(8,128)S(1)} collective-permute-done((f32[8,2048]{1,0:T(8,128)S(1)}, f32[8,2048]{1,0:T(8,128)S(1)}, u32[]{:S(2)}, u32[]{:S(2)}) %collective-permute-start.14) | collective-permute-done | bytes 65568 | tf_op jit(solution)/shard_map/ppermute | solution.py:516
  74.0 1.6 %collective-permute-start.15 = (bf16[8,2048]{1,0:T(8,128)(2,1)S(1)}, bf16[8,2048]{1,0:T(8,128)(2,1)S(1)}, u32[]{:S(2)}, u32[]{:S(2)}) collective-permute-start(bf16[8,2048]{1,0:T(8,128)(2,1)S(1)} %get-tuple-element.61), channel_id=1, source_target_pairs={{0,2},{2,0},{4,6},{6,4},{8,10},{10,8},{12,14},{14,12},{1,3},{3,1},... | collective-permute-start | bytes 98312 | tf_op jit(solution)/shard_map/ppermute | solution.py:513
  75.6 2.4 %collective-permute-done.15 = bf16[8,2048]{1,0:T(8,128)(2,1)S(1)} collective-permute-done((bf16[8,2048]{1,0:T(8,128)(2,1)S(1)}, bf16[8,2048]{1,0:T(8,128)(2,1)S(1)}, u32[]{:S(2)}, u32[]{:S(2)}) %collective-permute-start.15) | collective-permute-done | bytes 32800 | tf_op jit(solution)/shard_map/ppermute | solution.py:513
  78.0 3.0 %collective-permute-start.18 = (bf16[8,2048]{1,0:T(8,128)(2,1)S(1)}, bf16[8,2048]{1,0:T(8,128)(2,1)S(1)}, u32[]{:S(2)}, u32[]{:S(2)}) collective-permute-start(bf16[8,2048]{1,0:T(8,128)(2,1)S(1)} %fusion), channel_id=1, source_target_pairs={{0,4},{2,6},{4,0},{6,2},{8,12},{10,14},{12,8},{14,10},{1,5},{3,7},... | collective-permute-start | bytes 98312 | tf_op jit(solution)/shard_map/ppermute | solution.py:513
  81.0 1.5 %collective-permute-start.17 = (bf16[8,2048]{1,0:T(8,128)(2,1)S(1)}, bf16[8,2048]{1,0:T(8,128)(2,1)S(1)}, u32[]{:S(2)}, u32[]{:S(2)}) collective-permute-start(bf16[8,2048]{1,0:T(8,128)(2,1)S(1)} %fusion), channel_id=1, source_target_pairs={{0,12},{2,14},{4,8},{6,10},{8,4},{10,6},{12,0},{14,2},{1,13},{3,15... | collective-permute-start | bytes 98312 | tf_op jit(solution)/shard_map/ppermute | solution.py:513
  82.9 3.8 %collective-permute-done.17 = bf16[8,2048]{1,0:T(8,128)(2,1)S(1)} collective-permute-done((bf16[8,2048]{1,0:T(8,128)(2,1)S(1)}, bf16[8,2048]{1,0:T(8,128)(2,1)S(1)}, u32[]{:S(2)}, u32[]{:S(2)}) %collective-permute-start.17) | collective-permute-done | bytes 32800 | tf_op jit(solution)/shard_map/ppermute | solution.py:513
  87.6 1.2 %collective-permute-done.19.theirs_ref = bf16[8,2048]{1,0:T(8,128)(2,1)S(1)} collective-permute-done((bf16[8,2048]{1,0:T(8,128)(2,1)S(1)}, bf16[8,2048]{1,0:T(8,128)(2,1)S(1)}, u32[]{:S(2)}, u32[]{:S(2)}) %collective-permute-start.19) | collective-permute-done | bytes 32800 | tf_op jit(solution)/shard_map/ppermute | solution.py:516
  88.8 2.1 %products.1 = f32[16,1024]{1,0:T(8,128)} custom-call(bf16[8,2048]{1,0:T(8,128)(2,1)S(1)} %add_convert_fusion.mine_ref, bf16[8,2048]{1,0:T(8,128)(2,1)S(1)} %collective-permute-done.19.theirs_ref, bf16[8,1024,256]{2,1,0:T(8,128)(2,1)S(1)} %fetch_weights.1.weight_ref), custom_call_target="tpu_custom_call" | custom-call | tf_op jit(solution)/shard_map/products/pallas_call | solution.py:673
  (41 shorter events, 2.1 us)
Async XLA Ops:
  0.0 10.9 %copy-start.2 = (s32[160]{0:T(256)S(1)}, s32[160]{0:T(256)}, u32[]{:S(2)}) copy-start(s32[160]{0:T(256)} %param.16) | copy-start | bytes 1924
  0.0 10.9 %copy-start.3 = (s32[160]{0:T(256)S(1)}, s32[160]{0:T(256)}, u32[]{:S(2)}) copy-start(s32[160]{0:T(256)} %param.14) | copy-start | bytes 1924
  0.0 10.9 %copy-start.4 = (s32[160]{0:T(256)S(1)}, s32[160]{0:T(256)}, u32[]{:S(2)}) copy-start(s32[160]{0:T(256)} %param.12) | copy-start | bytes 1924
  2.4 6.5 %copy-start.6 = (bf16[48,4096]{1,0:T(8,128)(2,1)S(1)}, bf16[48,4096]{1,0:T(8,128)(2,1)}, u32[]{:S(2)}) copy-start(bf16[48,4096]{1,0:T(8,128)(2,1)} %get-tuple-element.34) | copy-start | bytes 1179652
  2.4 8.0 %copy-start.5 = (bf16[64,4096]{1,0:T(8,128)(2,1)S(1)}, bf16[64,4096]{1,0:T(8,128)(2,1)}, u32[]{:S(2)}) copy-start(bf16[64,4096]{1,0:T(8,128)(2,1)} %get-tuple-element.33) | copy-start | bytes 1572868
  2.5 35.0 %all-to-all-start = ((bf16[4,64,2048]{2,1,0:T(8,128)(2,1)}), bf16[4,64,2048]{2,1,0:T(8,128)(2,1)S(1)}, u32[]{:S(2)}, u32[]{:S(2)}) async-start(bf16[4,64,2048]{2,1,0:T(8,128)(2,1)} %get-tuple-element.37), calls=%async_computation | async-start | bytes 2097152 | tf_op jit(solution)/shard_map/all_to_all | solution.py:519
  8.9 12.0 %collective-permute-start.2 = (bf16[48,4096]{1,0:T(8,128)(2,1)S(1)}, bf16[48,4096]{1,0:T(8,128)(2,1)S(1)}, u32[]{:S(2)}, u32[]{:S(2)}) collective-permute-start(bf16[48,4096]{1,0:T(8,128)(2,1)S(1)} %copy-done.6), channel_id=1, source_target_pairs={{0,2},{2,0},{4,6},{6,4},{8,10},{10,8},{12,14},{14,12},{1,3},{3,1},... | collective-permute-start | bytes 1179656 | tf_op jit(solution)/shard_map/ppermute | solution.py:513
  10.4 27.1 %collective-permute-start.1 = (bf16[64,4096]{1,0:T(8,128)(2,1)S(1)}, bf16[64,4096]{1,0:T(8,128)(2,1)S(1)}, u32[]{:S(2)}, u32[]{:S(2)}) collective-permute-start(bf16[64,4096]{1,0:T(8,128)(2,1)S(1)} %copy-done.5), channel_id=1, source_target_pairs={{0,2},{2,0},{4,6},{6,4},{8,10},{10,8},{12,14},{14,12},{1,3},{3,1},... | collective-permute-start | bytes 1572872 | tf_op jit(solution)/shard_map/ppermute | solution.py:513
  11.7 21.2 %copy-start.1 = (s32[3,256]{1,0:T(4,128)S(1)}, s32[3,256]{1,0:T(4,128)}, u32[]{:S(2)}) copy-start(s32[3,256]{1,0:T(4,128)} %select_reduce_fusion.inv_ref) | copy-start | bytes 9220
  21.0 16.5 %collective-permute-start.3 = (bf16[48,4096]{1,0:T(8,128)(2,1)S(1)}, bf16[48,4096]{1,0:T(8,128)(2,1)S(1)}, u32[]{:S(2)}, u32[]{:S(2)}) collective-permute-start(bf16[48,4096]{1,0:T(8,128)(2,1)S(1)} %collective-permute-done.2.a_in_ref), channel_id=1, source_target_pairs={{0,16},{16,0},{1,17},{17,1},{2,18},{18,2},{3,19},{19,3},{4,20},{20... | collective-permute-start | bytes 1179656 | tf_op jit(solution)/shard_map/ppermute | solution.py:578
  22.5 5.0 %collective-permute-start.4 = (f32[64,256]{1,0:T(8,128)}, f32[64,256]{1,0:T(8,128)S(1)}, u32[]{:S(2)}, u32[]{:S(2)}) collective-permute-start(f32[64,256]{1,0:T(8,128)} %get-tuple-element.38), channel_id=1, source_target_pairs={{0,4},{2,6},{4,0},{6,2},{8,12},{10,14},{12,8},{14,10},{1,5},{3,7},... | collective-permute-start | bytes 196616 | tf_op jit(solution)/shard_map/ppermute | solution.py:513
  28.3 9.1 %collective-permute-start.5 = (f32[64,256]{1,0:T(8,128)S(1)}, f32[64,256]{1,0:T(8,128)S(1)}, u32[]{:S(2)}, u32[]{:S(2)}) collective-permute-start(f32[64,256]{1,0:T(8,128)S(1)} %add.24), channel_id=1, source_target_pairs={{0,8},{2,10},{4,12},{6,14},{8,0},{10,2},{12,4},{14,6},{1,9},{3,11}... | collective-permute-start | bytes 196616 | tf_op jit(solution)/shard_map/ppermute | solution.py:513
  32.9 4.6 %collective-permute-start = (s32[3,256]{1,0:T(4,128)S(1)}, s32[3,256]{1,0:T(4,128)S(1)}, u32[]{:S(2)}, u32[]{:S(2)}) collective-permute-start(s32[3,256]{1,0:T(4,128)S(1)} %copy-done.1), channel_id=1, source_target_pairs={{0,2},{2,0},{4,6},{6,4},{8,10},{10,8},{12,14},{14,12},{1,3},{3,1},... | collective-permute-start | bytes 9224 | tf_op jit(solution)/shard_map/ppermute | solution.py:513
  42.3 5.1 %collective-permute-start.6 = (bf16[4,1024,256]{2,1,0:T(8,128)(2,1)}, bf16[4,1024,256]{2,1,0:T(8,128)(2,1)}, u32[]{:S(2)}, u32[]{:S(2)}) collective-permute-start(bf16[4,1024,256]{2,1,0:T(8,128)(2,1)} %get-tuple-element.47), channel_id=1, source_target_pairs={{0,1},{1,0},{2,3},{3,2},{4,5},{5,4},{6,7},{7,6},{8,9},{9,8},{10,11... | collective-permute-start | bytes 6291464 | tf_op jit(solution)/shard_map/ppermute | solution.py:516
  42.4 19.3 %all-to-all-start.1 = ((bf16[4,64,1024]{2,1,0:T(8,128)(2,1)}), bf16[4,64,1024]{2,1,0:T(8,128)(2,1)S(1)}, u32[]{:S(2)}, u32[]{:S(2)}) async-start(bf16[4,64,1024]{2,1,0:T(8,128)(2,1)} %get-tuple-element.45), calls=%async_computation.1 | async-start | bytes 1048576 | tf_op jit(solution)/shard_map/all_to_all | solution.py:519
  45.9 6.3 %collective-permute-start.7 = (f32[64,256]{1,0:T(8,128)S(1)}, f32[64,256]{1,0:T(8,128)S(1)}, u32[]{:S(2)}, u32[]{:S(2)}) collective-permute-start(f32[64,256]{1,0:T(8,128)S(1)} %add.25), channel_id=1, source_target_pairs={{0,2},{2,0},{4,6},{6,4},{8,10},{10,8},{12,14},{14,12},{1,3},{3,1},... | collective-permute-start | bytes 196616 | tf_op jit(solution)/shard_map/ppermute | solution.py:513
  52.2 11.7 %collective-permute-start.8 = (bf16[64,1024]{1,0:T(8,128)(2,1)}, bf16[64,1024]{1,0:T(8,128)(2,1)S(1)}, u32[]{:S(2)}, u32[]{:S(2)}) collective-permute-start(bf16[64,1024]{1,0:T(8,128)(2,1)} %get-tuple-element.52), channel_id=1, source_target_pairs={{0,4},{2,6},{4,0},{6,2},{8,12},{10,14},{12,8},{14,10},{1,5},{3,7},... | collective-permute-start | bytes 393224 | tf_op jit(solution)/shard_map/ppermute | solution.py:513
  54.2 4.1 %collective-permute-start.11 = (f32[64,256]{1,0:T(8,128)S(1)}, f32[64,256]{1,0:T(8,128)S(1)}, u32[]{:S(2)}, u32[]{:S(2)}) collective-permute-start(f32[64,256]{1,0:T(8,128)S(1)} %add.26.pay0_ref), channel_id=1, source_target_pairs={{0,1},{1,0},{2,3},{3,2},{4,5},{5,4},{6,7},{7,6},{8,9},{9,8},{10,11... | collective-permute-start | bytes 196616 | tf_op jit(solution)/shard_map/ppermute | solution.py:516
  54.3 15.8 %collective-permute-start.9 = (bf16[64,1024]{1,0:T(8,128)(2,1)}, bf16[64,1024]{1,0:T(8,128)(2,1)S(1)}, u32[]{:S(2)}, u32[]{:S(2)}) collective-permute-start(bf16[64,1024]{1,0:T(8,128)(2,1)} %get-tuple-element.53), channel_id=1, source_target_pairs={{0,8},{2,10},{4,12},{6,14},{8,0},{10,2},{12,4},{14,6},{1,9},{3,11}... | collective-permute-start | bytes 393224 | tf_op jit(solution)/shard_map/ppermute | solution.py:513
  56.7 13.4 %copy-start = (f32[64,1024]{1,0:T(8,128)S(1)}, f32[64,1024]{1,0:T(8,128)}, u32[]{:S(2)}) copy-start(f32[64,1024]{1,0:T(8,128)} %get-tuple-element.51.second_keep_ref) | copy-start | bytes 786436
  56.7 13.4 %collective-permute-start.10 = (bf16[64,1024]{1,0:T(8,128)(2,1)}, bf16[64,1024]{1,0:T(8,128)(2,1)S(1)}, u32[]{:S(2)}, u32[]{:S(2)}) collective-permute-start(bf16[64,1024]{1,0:T(8,128)(2,1)} %get-tuple-element.54), channel_id=1, source_target_pairs={{0,12},{2,14},{4,8},{6,10},{8,4},{10,6},{12,0},{14,2},{1,13},{3,15... | collective-permute-start | bytes 393224 | tf_op jit(solution)/shard_map/ppermute | solution.py:513
  56.8 7.0 %collective-permute-start.12 = (f32[64,256]{1,0:T(8,128)S(1)}, f32[64,256]{1,0:T(8,128)S(1)}, u32[]{:S(2)}, u32[]{:S(2)}) collective-permute-start(f32[64,256]{1,0:T(8,128)S(1)} %add.26.pay0_ref), channel_id=1, source_target_pairs={{0,16},{16,0},{1,17},{17,1},{2,18},{18,2},{3,19},{19,3},{4,20},{20... | collective-permute-start | bytes 196616 | tf_op jit(solution)/shard_map/ppermute | solution.py:635
  58.3 5.5 %collective-permute-start.13 = (f32[64,256]{1,0:T(8,128)S(1)}, f32[64,256]{1,0:T(8,128)S(1)}, u32[]{:S(2)}, u32[]{:S(2)}) collective-permute-start(f32[64,256]{1,0:T(8,128)S(1)} %add.26.pay0_ref), channel_id=1, source_target_pairs={{0,17},{1,16},{16,1},{17,0},{2,19},{3,18},{18,3},{19,2},{4,21},{5,... | collective-permute-start | bytes 196616 | tf_op jit(solution)/shard_map/ppermute | solution.py:636
  72.7 1.3 %collective-permute-start.14 = (f32[8,2048]{1,0:T(8,128)S(1)}, f32[8,2048]{1,0:T(8,128)S(1)}, u32[]{:S(2)}, u32[]{:S(2)}) collective-permute-start(f32[8,2048]{1,0:T(8,128)S(1)} %get-tuple-element.59), channel_id=1, source_target_pairs={{0,1},{1,0},{2,3},{3,2},{4,5},{5,4},{6,7},{7,6},{8,9},{9,8},{10,11... | collective-permute-start | bytes 196616 | tf_op jit(solution)/shard_map/ppermute | solution.py:516
  74.0 4.0 %collective-permute-start.15 = (bf16[8,2048]{1,0:T(8,128)(2,1)S(1)}, bf16[8,2048]{1,0:T(8,128)(2,1)S(1)}, u32[]{:S(2)}, u32[]{:S(2)}) collective-permute-start(bf16[8,2048]{1,0:T(8,128)(2,1)S(1)} %get-tuple-element.61), channel_id=1, source_target_pairs={{0,2},{2,0},{4,6},{6,4},{8,10},{10,8},{12,14},{14,12},{1,3},{3,1},... | collective-permute-start | bytes 98312 | tf_op jit(solution)/shard_map/ppermute | solution.py:513
  78.0 4.9 %collective-permute-start.18 = (bf16[8,2048]{1,0:T(8,128)(2,1)S(1)}, bf16[8,2048]{1,0:T(8,128)(2,1)S(1)}, u32[]{:S(2)}, u32[]{:S(2)}) collective-permute-start(bf16[8,2048]{1,0:T(8,128)(2,1)S(1)} %fusion), channel_id=1, source_target_pairs={{0,4},{2,6},{4,0},{6,2},{8,12},{10,14},{12,8},{14,10},{1,5},{3,7},... | collective-permute-start | bytes 98312 | tf_op jit(solution)/shard_map/ppermute | solution.py:513
  81.0 5.7 %collective-permute-start.17 = (bf16[8,2048]{1,0:T(8,128)(2,1)S(1)}, bf16[8,2048]{1,0:T(8,128)(2,1)S(1)}, u32[]{:S(2)}, u32[]{:S(2)}) collective-permute-start(bf16[8,2048]{1,0:T(8,128)(2,1)S(1)} %fusion), channel_id=1, source_target_pairs={{0,12},{2,14},{4,8},{6,10},{8,4},{10,6},{12,0},{14,2},{1,13},{3,15... | collective-permute-start | bytes 98312 | tf_op jit(solution)/shard_map/ppermute | solution.py:513
  82.6 4.9 %collective-permute-start.16 = (bf16[8,2048]{1,0:T(8,128)(2,1)S(1)}, bf16[8,2048]{1,0:T(8,128)(2,1)S(1)}, u32[]{:S(2)}, u32[]{:S(2)}) collective-permute-start(bf16[8,2048]{1,0:T(8,128)(2,1)S(1)} %fusion), channel_id=1, source_target_pairs={{0,8},{2,10},{4,12},{6,14},{8,0},{10,2},{12,4},{14,6},{1,9},{3,11}... | collective-permute-start | bytes 98312 | tf_op jit(solution)/shard_map/ppermute | solution.py:513
  87.5 1.3 %collective-permute-start.19 = (bf16[8,2048]{1,0:T(8,128)(2,1)S(1)}, bf16[8,2048]{1,0:T(8,128)(2,1)S(1)}, u32[]{:S(2)}, u32[]{:S(2)}) collective-permute-start(bf16[8,2048]{1,0:T(8,128)(2,1)S(1)} %add_convert_fusion.mine_ref), channel_id=1, source_target_pairs={{0,1},{1,0},{2,3},{3,2},{4,5},{5,4},{6,7},{7,6},{8,9},{9,8},{10,11... | collective-permute-start | bytes 98312 | tf_op jit(solution)/shard_map/ppermute | solution.py:516
